TPU v7x, 128 devices: a whole 4x4x4 slice. The times are simulated.
128 devices in a mesh: row: 16 (over z, x_lo, core), col: 8 (over y, x_hi).
Axes of the slice: x: 4 (x_hi: 2, x_lo: 2; x = x_hi * 2 + x_lo), y: 4, z: 4, core: 2. Of those that a mesh axis runs over, the one named last changes fastest.
Arguments:
- stored: float32 [16, 16, 8, 2, 128, 128], P('col', 'row'), may hold values from -1.2 to 1.2
- tile_rows: int32 [16, 8], replicated, may hold values from 0 to 63, as said below
- offsets: int32 [16, 16, 2], replicated, may hold values from 0 to 63, as said below
- kept_rows: int32 [16, 16, 32], P('col', 'row'), may hold values from 0 to 63, as said below
- kept_cols: int32 [16, 16, 32], P('col', 'row'), may hold values from 0 to 63, as said below
- kept_count: int32 [16, 16], P('col', 'row'), may hold values from 8 to 32, as said below
Outputs:
- kept_blocks: float32 [16, 16, 32, 128, 128], P('col', 'row')
Inputs may be any that keep to these rules, and one draw needn't show every extreme that they name: Every list is increasing and is the set of block rows a with (a AND m) equal to one value of the grid row, for one bit mask m with log2(8) bits set, the same for all grid rows; the tiles of grid column Y have their occupied block columns in tile_rows[Y]. A XOR offsets[X, Y, r] lies in tile_rows[Y] for every a in tile_rows[X]. `kept_rows`: within a tile the kept (row, column) pairs are distinct; rows lie in tile_rows[I] and columns in tile_rows[J], also in slots past the count. `kept_cols`: paired with kept_rows slot by slot. `kept_count`: tiles whose grid row and column differ by at most one, cyclically, keep 32 blocks.
All inputs are finite; a program needn't handle non-finite values.
Results may differ from a plain program's by a relative error of at most 0.0003.
Values sent between devices are 32-bit elements; how exact they have to be, the bound alone decides.
A program may use at most 192 MiB of HBM per device.

v0:
```python
import jax
import jax.numpy as jnp
from jax import lax
from jax.sharding import PartitionSpec as P


def from_behind(value, axis, steps):
    count = lax.axis_size(axis)
    pairs = [(source, (source + steps) % count) for source in range(count)]
    return lax.ppermute(value, axis, pairs)


def rank_in(row_list, lookup_keys):
    positions = jnp.arange(row_list.shape[0], dtype=jnp.int32)
    matches = row_list == lookup_keys[..., None]
    return jnp.sum(jnp.where(matches, positions, 0), -1)


def tile_cols(tile_rows, offsets, tile_x, tile_y):
    offsets_both = jnp.concatenate([offsets[tile_x, tile_y], offsets[tile_y, tile_x]])
    return jnp.bitwise_xor(tile_rows[tile_x][:, None], offsets_both[None, :])


def assemble(own_half, mirror, tile_rows, offsets, tile_x, tile_y):
    half_slots = own_half.shape[1]
    mirror_rows = jnp.bitwise_xor(tile_rows[tile_x][:, None], offsets[tile_y, tile_x][None, :])
    position = rank_in(tile_rows[tile_y], mirror_rows)
    picked = mirror[position, jnp.arange(half_slots, dtype=jnp.int32)[None, :]]
    return jnp.concatenate([own_half, jnp.swapaxes(picked, -1, -2)], 1)


def lane_terms(vals_a, vals_b, cols_a, cols_b, rows_i, rows_k, want_rows, want_cols, live_count):
    kept_slots = want_rows.shape[0]
    block_size = vals_a.shape[-1]
    is_live = jnp.arange(kept_slots, dtype=jnp.int32) < live_count
    position = rank_in(rows_k, cols_a)
    summed = jnp.zeros((kept_slots, block_size * block_size), jnp.float32)
    for slot in range(vals_a.shape[1]):
        picked = vals_b[position[:, slot]]
        picked_cols = cols_b[position[:, slot]]
        products = jnp.einsum(
            "eij,ebjk->ebik", vals_a[:, slot], picked, precision=lax.Precision.HIGHEST
        )
        weights = (
            (rows_i[None, :, None] == want_rows[:, None, None])
            & (picked_cols[None] == want_cols[:, None, None])
            & is_live[:, None, None]
        ).astype(jnp.float32)
        summed = summed + jnp.dot(
            weights.reshape(kept_slots, -1),
            products.reshape(-1, block_size * block_size),
            precision=lax.Precision.HIGHEST,
        )
    return summed.reshape(kept_slots, block_size, block_size)


def rotate_tiles(tiles, amount, bit_count, lane_count):
    for bit in range(bit_count):
        stride = 1 << bit
        sender = tiles if stride >= lane_count else tiles[:stride]
        arrived = from_behind(sender, "col", -max(1, stride // lane_count))
        if stride >= lane_count:
            candidate = arrived
        else:
            candidate = jnp.concatenate([tiles[stride:], arrived], 0)
        tiles = jnp.where(amount >> bit & 1 == 1, candidate, tiles)
    return tiles


def local(stored, tile_rows, offsets, kept_rows, kept_cols, kept_count):
    lane_count = stored.shape[0]
    active = stored.shape[2]
    half_slots = stored.shape[3]
    block_size = stored.shape[-1]
    slot_count = 2 * half_slots
    grid_size = lax.axis_size("row")
    col_count = lax.axis_size("col")
    row_id = lax.axis_index("row")
    col_id = lax.axis_index("col")
    lane_ids = col_id * lane_count + jnp.arange(lane_count, dtype=jnp.int32)
    own_half = stored[:, 0]
    entry_count = active * half_slots
    piece = entry_count // col_count
    routed = own_half
    routed = lax.all_to_all(
        lax.all_to_all(routed, "col", split_axis=1, concat_axis=0, tiled=True),
        "row",
        split_axis=0,
        concat_axis=0,
        tiled=True,
    )
    routed = routed.reshape(col_count, lane_count, 1, piece, block_size, block_size)
    routed = lax.all_to_all(routed, "col", split_axis=0, concat_axis=2, tiled=True)
    mirror = routed.reshape(lane_count, active, half_slots, block_size, block_size)
    full_tiles = jax.vmap(assemble, in_axes=(0, 0, None, None, 0, None))(
        own_half, mirror, tile_rows, offsets, lane_ids, row_id
    )
    tile_entries = active * slot_count
    left_piece = tile_entries // grid_size
    spread = full_tiles.reshape(lane_count, grid_size, left_piece, block_size, block_size)
    spread = lax.all_to_all(spread, "row", split_axis=1, concat_axis=1, tiled=True)
    first_tile = (jnp.arange(grid_size, dtype=jnp.int32)[None, :] + lane_ids[:, None]) % grid_size
    pick_now = jnp.take_along_axis(spread, first_tile[:, :, None, None, None], axis=1)
    pick_next = jnp.take_along_axis(
        spread, ((first_tile + 1) % grid_size)[:, :, None, None, None], axis=1
    )
    paired = jnp.stack([pick_now, pick_next], 2)
    paired = lax.all_to_all(paired, "row", split_axis=1, concat_axis=3, tiled=True)
    left_pair = paired.reshape(lane_count, 2, active, slot_count, block_size, block_size)
    bit_count = (grid_size - 1).bit_length()
    right_now = rotate_tiles(full_tiles, row_id, bit_count, lane_count)
    right_next = rotate_tiles(right_now, 1, 1, lane_count)
    right_pair = jnp.stack([right_now, right_next], 1)
    results = []
    for lane_index in range(lane_count):
        tile_i = lane_ids[lane_index]
        summed = jnp.zeros((kept_rows.shape[-1], block_size, block_size), jnp.float32)
        for step_index in range(2):
            tile_k = (tile_i + row_id + step_index) % grid_size
            summed = summed + lane_terms(
                left_pair[lane_index, step_index],
                right_pair[lane_index, step_index],
                tile_cols(tile_rows, offsets, tile_i, tile_k),
                tile_cols(tile_rows, offsets, tile_k, row_id),
                tile_rows[tile_i],
                tile_rows[tile_k],
                kept_rows[lane_index, 0],
                kept_cols[lane_index, 0],
                kept_count[lane_index, 0],
            )
        results.append(summed)
    return jnp.stack(results)[:, None]


def solution(mesh):
    in_specs = (
        P("col", "row", None, None, None, None),
        P(),
        P(),
        P("col", "row", None),
        P("col", "row", None),
        P("col", "row"),
    )
    out_specs = P("col", "row", None, None, None)
    return jax.shard_map(local, mesh=mesh, in_specs=in_specs, out_specs=out_specs, check_vma=False)
```

profile of v0, /device:TPU:42, one launch (start us, length us, event | category | flops | bytes accessed | tf_op | source)
XLA Modules:
  0.0 757.8 jit_solution(17229895904587869810)
XLA Ops:
  1.7 33.1 %all_to_all.58 = f32[2,8,2,128,128]{4,3,2,0,1:T(8,128)S(1)} all-to-all(f32[2,8,2,128,128]{4,3,2,0,1:T(8,128)S(1)} %bitcast.388), channel_id=1, replica_groups=mesh['row'=16,'col'=8] {'col'}, dimensions={1} | all-to-all | bytes 4194304 | tf_op jit(solution)/shard_map/all_to_all | solution.py:86
  34.8 30.5 %all_to_all.59 = f32[16,1,2,128,128]{4,3,2,1,0:T(8,128)} all-to-all(f32[16,1,2,128,128]{4,3,2,1,0:T(8,128)S(1)} %bitcast.423), channel_id=1, replica_groups=mesh['row'=16,'col'=8] {'row'}, dimensions={0} | all-to-all | bytes 4194304 | tf_op jit(solution)/shard_map/all_to_all | solution.py:85
  65.3 6.2 all-to-all-start.2
  79.5 20.2 %all-to-all-done.2 = f32[8,2,1,2,128,128]{5,4,3,1,2,0:T(8,128)} async-done(((f32[8,2,1,2,128,128]{5,4,3,1,2,0:T(8,128)}), f32[8,2,1,2,128,128]{5,4,3,1,2,0:T(8,128)}, u32[]{:S(2)}, u32[]{:S(2)}) %all-to-all-start.2) | async-done | bytes 2097184 | tf_op jit(solution)/shard_map/all_to_all | solution.py:93
  99.7 3.1 copy.350
  102.8 3.6 gather_fusion.34
  109.3 3.9 fusion.4
  115.3 47.3 %collective-permute-done = f32[1,8,4,128,128]{4,3,2,0,1:T(8,128)} collective-permute-done((f32[1,8,4,128,128]{4,3,2,0,1:T(8,128)}, f32[1,8,4,128,128]{4,3,2,0,1:T(8,128)}, u32[]{:S(2)}, u32[]{:S(2)}) %collective-permute-start) | collective-permute-done | bytes 2097184 | tf_op jit(solution)/shard_map/ppermute | solution.py:10
  162.5 5.9 pad_maximum_fusion.1
  171.0 4.8 all-to-all-start.3
  179.4 43.9 %all-to-all-done.3 = f32[2,16,2,128,128]{4,3,2,0,1:T(8,128)} async-done(((f32[2,16,2,128,128]{4,3,2,0,1:T(8,128)}), f32[2,16,2,128,128]{4,3,2,0,1:T(8,128)}, u32[]{:S(2)}, u32[]{:S(2)}) %all-to-all-start.3) | async-done | bytes 4194336 | tf_op jit(solution)/shard_map/all_to_all | solution.py:101
  223.3 5.0 gather_fusion.36
  228.2 5.0 gather_fusion.35
  236.0 79.3 %collective-permute-done.1 = f32[2,8,4,128,128]{4,3,2,0,1:T(8,128)} collective-permute-done((f32[2,8,4,128,128]{4,3,2,0,1:T(8,128)}, f32[2,8,4,128,128]{4,3,2,0,1:T(8,128)}, u32[]{:S(2)}, u32[]{:S(2)}) %collective-permute-start.1) | collective-permute-done | bytes 4194336 | tf_op jit(solution)/shard_map/ppermute | solution.py:10
  315.4 5.1 broadcast_select_fusion
  321.5 3.8 pad_maximum_fusion
  325.3 6.1 all-to-all-start.4
  337.5 75.4 %collective-permute-done.2 = f32[2,8,4,128,128]{4,3,2,0,1:T(8,128)} collective-permute-done((f32[2,8,4,128,128]{4,3,2,0,1:T(8,128)}, f32[2,8,4,128,128]{4,3,2,0,1:T(8,128)}, u32[]{:S(2)}, u32[]{:S(2)}) %collective-permute-start.2) | collective-permute-done | bytes 4194336 | tf_op jit(solution)/shard_map/ppermute | solution.py:10
  412.9 5.3 broadcast_select_fusion.1
  418.2 4.0 collective-permute-start.3
  429.9 4.0 copy.175
  440.9 71.1 %collective-permute-done.3 = f32[2,8,4,128,128]{4,3,2,0,1:T(8,128)} collective-permute-done((f32[2,8,4,128,128]{4,3,2,0,1:T(8,128)}, f32[2,8,4,128,128]{4,3,2,0,1:T(8,128)}, u32[]{:S(2)}, u32[]{:S(2)}) %collective-permute-start.3) | collective-permute-done | bytes 4194336 | tf_op jit(solution)/shard_map/ppermute | solution.py:10
  523.8 3.6 gather_fusion.3
  527.5 3.6 gather_fusion.5
  531.0 3.6 gather_fusion.7
  534.6 3.6 gather_fusion.9
  548.4 6.4 convolution_bitcast_fusion.11
  554.8 3.5 copy.187
  558.2 6.3 convolution_bitcast_fusion.10
  567.5 6.3 convolution_bitcast_fusion.9
  576.8 6.4 convolution_bitcast_fusion.15
  583.2 3.1 copy.178
  586.3 6.4 convolution_bitcast_fusion.14
  595.6 6.4 convolution_bitcast_fusion.13
  604.9 6.4 convolution_bitcast_fusion.12
  614.2 6.4 convolution_bitcast_fusion.8
  620.6 3.4 copy.193
  647.9 5.9 convolution_bitcast_fusion.4
  656.9 6.4 convolution_bitcast_fusion.5
  666.2 6.4 convolution_bitcast_fusion.6
  675.6 6.4 convolution_bitcast_fusion.7
  682.0 3.3 copy.196
  685.3 4.1 fusion.21
  694.5 3.9 convolution_add_fusion.3
  706.5 6.6 convolution_bitcast_fusion
  716.1 6.3 convolution_bitcast_fusion.1
  725.4 6.4 convolution_bitcast_fusion.2
  734.7 6.4 convolution_bitcast_fusion.3
  (190 shorter events, 147.3 us)
Async XLA Ops:
  65.3 10.7 %copy-start.22 = (s32[16,16,2]{1,2,0:T(2,128)S(1)}, s32[16,16,2]{1,2,0:T(2,128)}, u32[]{:S(2)}) copy-start(s32[16,16,2]{1,2,0:T(2,128)} %param.10) | copy-start | bytes 6148
  65.3 10.9 %copy-start.21 = (s32[16,8]{0,1:T(8,128)S(1)}, s32[16,8]{0,1:T(8,128)}, u32[]{:S(2)}) copy-start(s32[16,8]{0,1:T(8,128)} %param.9) | copy-start | bytes 1540
  65.3 34.3 %all-to-all-start.2 = ((f32[8,2,1,2,128,128]{5,4,3,1,2,0:T(8,128)}), f32[8,2,1,2,128,128]{5,4,3,1,2,0:T(8,128)}, u32[]{:S(2)}, u32[]{:S(2)}) async-start(f32[8,2,1,2,128,128]{5,4,3,1,2,0:T(8,128)} %bitcast.420), calls=%async_computation.2 | async-start | bytes 4194304 | tf_op jit(solution)/shard_map/all_to_all | solution.py:93
  113.3 49.3 %collective-permute-start = (f32[1,8,4,128,128]{4,3,2,0,1:T(8,128)}, f32[1,8,4,128,128]{4,3,2,0,1:T(8,128)}, u32[]{:S(2)}, u32[]{:S(2)}) collective-permute-start(f32[1,8,4,128,128]{4,3,2,0,1:T(8,128)} %get-tuple-element.39), channel_id=1, source_target_pairs={{0,7},{1,0},{2,1},{3,2},{4,3},{5,4},{6,5},{7,6},{8,15},{9,8},{10,9... | collective-permute-start | bytes 6291464 | tf_op jit(solution)/shard_map/ppermute | solution.py:10
  171.0 52.3 %all-to-all-start.3 = ((f32[2,16,2,128,128]{4,3,2,0,1:T(8,128)}), f32[2,16,2,128,128]{4,3,2,0,1:T(8,128)}, u32[]{:S(2)}, u32[]{:S(2)}) async-start(f32[2,16,2,128,128]{4,3,2,0,1:T(8,128)} %copy.171), calls=%async_computation.3 | async-start | bytes 8388608 | tf_op jit(solution)/shard_map/all_to_all | solution.py:101
  175.8 139.5 %collective-permute-start.1 = (f32[2,8,4,128,128]{4,3,2,0,1:T(8,128)}, f32[2,8,4,128,128]{4,3,2,0,1:T(8,128)}, u32[]{:S(2)}, u32[]{:S(2)}) collective-permute-start(f32[2,8,4,128,128]{4,3,2,0,1:T(8,128)} %get-tuple-element.37), channel_id=1, source_target_pairs={{0,7},{1,0},{2,1},{3,2},{4,3},{5,4},{6,5},{7,6},{8,15},{9,8},{10,9... | collective-permute-start | bytes 12582920 | tf_op jit(solution)/shard_map/ppermute | solution.py:10
  233.2 82.2 %copy-start = (f32[2,8,4,128,128]{4,3,2,0,1:T(8,128)S(1)}, f32[2,8,4,128,128]{4,3,2,0,1:T(8,128)}, u32[]{:S(2)}) copy-start(f32[2,8,4,128,128]{4,3,2,0,1:T(8,128)} %get-tuple-element.37) | copy-start | bytes 12582916
  315.4 5.7 copy-start.1
  320.5 92.4 %collective-permute-start.2 = (f32[2,8,4,128,128]{4,3,2,0,1:T(8,128)}, f32[2,8,4,128,128]{4,3,2,0,1:T(8,128)}, u32[]{:S(2)}, u32[]{:S(2)}) collective-permute-start(f32[2,8,4,128,128]{4,3,2,0,1:T(8,128)} %broadcast_select_fusion), channel_id=1, source_target_pairs={{0,6},{1,7},{2,0},{3,1},{4,2},{5,3},{6,4},{7,5},{8,14},{9,15},{10,... | collective-permute-start | bytes 12582920 | tf_op jit(solution)/shard_map/ppermute | solution.py:10
  325.3 104.6 %all-to-all-start.4 = ((f32[2,16,2,2,128,128]{5,4,3,2,0,1:T(8,128)}), f32[2,16,2,2,128,128]{5,4,3,2,0,1:T(8,128)}, u32[]{:S(2)}, u32[]{:S(2)}) async-start(f32[2,16,2,2,128,128]{5,4,3,2,0,1:T(8,128)} %pad_maximum_fusion), calls=%async_computation.4 | async-start | bytes 16777216 | tf_op jit(solution)/shard_map/all_to_all | solution.py:108
  337.5 90.2 %copy-start.23 = (s32[2,1]{0,1:T(1,128)S(1)}, s32[2,1]{0,1:T(1,128)}, u32[]{:S(2)}) copy-start(s32[2,1]{0,1:T(1,128)} %param.13) | copy-start | bytes 28
  337.5 92.0 %copy-start.24 = (s32[2,1,32]{2,1,0:T(1,128)S(1)}, s32[2,1,32]{2,1,0:T(1,128)}, u32[]{:S(2)}) copy-start(s32[2,1,32]{2,1,0:T(1,128)} %param.11) | copy-start | bytes 772
  337.5 92.0 %copy-start.25 = (s32[2,1,32]{2,1,0:T(1,128)S(1)}, s32[2,1,32]{2,1,0:T(1,128)}, u32[]{:S(2)}) copy-start(s32[2,1,32]{2,1,0:T(1,128)} %param.12) | copy-start | bytes 772
  418.2 93.8 %collective-permute-start.3 = (f32[2,8,4,128,128]{4,3,2,0,1:T(8,128)}, f32[2,8,4,128,128]{4,3,2,0,1:T(8,128)}, u32[]{:S(2)}, u32[]{:S(2)}) collective-permute-start(f32[2,8,4,128,128]{4,3,2,0,1:T(8,128)} %broadcast_select_fusion.1), channel_id=1, source_target_pairs={{0,4},{1,5},{2,6},{3,7},{4,0},{5,1},{6,2},{7,3},{8,12},{9,13},{10,... | collective-permute-start | bytes 12582920 | tf_op jit(solution)/shard_map/ppermute | solution.py:10
  554.8 3.5 copy-start.3
  620.6 3.4 copy-start.4
  624.1 2.5 copy-start.5
  626.6 2.5 copy-start.8
  629.1 2.6 copy-start.9
  631.6 2.6 copy-start.10
  634.2 2.7 copy-start.11
  637.0 2.6 copy-start.12
  639.5 2.6 copy-start.13
  644.8 3.1 copy-start.6
  646.5 51.9 %collective-permute-start.4 = (f32[1,8,4,128,128]{4,3,2,0,1:T(8,128)}, f32[1,8,4,128,128]{4,3,2,0,1:T(8,128)S(1)}, u32[]{:S(2)}, u32[]{:S(2)}) collective-permute-start(f32[1,8,4,128,128]{4,3,2,0,1:T(8,128)} %get-tuple-element.35), channel_id=1, source_target_pairs={{0,7},{1,0},{2,1},{3,2},{4,3},{5,4},{6,5},{7,6},{8,15},{9,8},{10,9... | collective-permute-start | bytes 6291464 | tf_op jit(solution)/shard_map/ppermute | solution.py:10
  685.3 4.1 copy-start.18
  689.4 2.6 copy-start.16
  692.0 2.6 copy-start.15
  713.1 3.0 copy-start.2
  743.2 2.5 copy-start.19
  745.7 2.6 copy-start.17
  748.4 2.6 copy-start.14
  748.4 2.6 copy-start.20
  753.6 1.6 copy-start.7
where the time goes:
time: 771 us; the launch traced here: 758 us
  waiting for transfers between devices  337 us (44%)
  matrix products  146 us (19%)
  local copies, waits for them, and re-layouts  140 us (18%)
  blocking collectives  63.6 us (8%)
  other arithmetic  36.6 us (5%)
  starting transfers between devices  28.2 us (4%)
    ppermute x5, waiting for transfers between devices, from_behind(): return lax.ppermute(value, axis, pairs)  273 us
    dot_general x16, matrix products, lane_terms(): jnp.einsum('eij,ebjk->ebik', vals_a[:, slot], picked, precision=lax.Preci...  102 us
    transpose x16, local copies, waits for them, and re-layouts, lane_terms(): jnp.einsum('eij,ebjk->ebik', vals_a[:, slot], picked, precision=lax.Preci...  47.8 us
    dot_general x16, matrix products, lane_terms(): jnp.dot(weights.reshape(kept_slots, -1), products.reshape(-1, block_size...  43.9 us
    all_to_all x1, waiting for transfers between devices, local(): lax.all_to_all(spread, 'row', split_axis=1, concat_axis=1, tiled=True)  43.9 us
    gather x16, local copies, waits for them, and re-layouts, lane_terms(): picked = vals_b[position[:, slot]]  38.6 us
    all_to_all x1, blocking collectives, local(): lax.all_to_all(routed, 'col', split_axis=1, concat_axis=0, tiled=True)  33.1 us
    all_to_all x1, blocking collectives, local(): lax.all_to_all(lax.all_to_all(routed, 'col', split_axis=1, concat_axis=0,...  30.5 us
  transfers between devices with their start and end apart: 8, of which 6 were waited for; matrix products, arithmetic and copies ran while one was open for 13% of the time, Pallas kernels for 0%

commit v1 on v0

v1 whole, which is shorter than its diff:
```python
import jax
import jax.numpy as jnp
import numpy as np
from jax import lax
from jax.experimental import pallas as pl
from jax.experimental.pallas import tpu as pltpu
from jax.sharding import PartitionSpec as P

MESH = pl.DeviceIdType.MESH
CHUNKS = 4
SLOTS = 16
SENDS = [
    [32, 5, 8, 408576, 525313, 525345, 525377, 525409, 656898, 407553, 408608, 656930, 657410, 656962, 657442, 656994, 787971, 407585, 788003, 657474, 408640, 788035, 788067, 407617, 919044, 657506, 919076, 408672, 919108, 407649, 919140, 1865731, 1865763, 1865795, 1865827],
    [36, 4, 9, 655360, 786433, 655392, 786465, 655424, 786497, 655456, 786529, 276480, 918018, 276512, 818178, 1558530, 918050, 788995, 918082, 818210, 918114, 789027, 1558562, 276544, 1558594, 789059, 818242, 789091, 276576, 932865, 818274, 932897, 1558626, 1557505, 932929, 932961, 1557537, 1557569, 1557601],
    [52, 8, 14, 263169, 281090, 281122, 281154, 624640, 802816, 309763, 281186, 263201, 624672, 263233, 263265, 309795, 393216, 393248, 624704, 393280, 309827, 1314308, 802848, 393312, 1314340, 624736, 1314372, 309859, 1314404, 2066949, 802880, 701444, 2067974, 802912, 701476, 2066981, 1576455, 2068006, 701508, 2067013, 1576487, 1721348, 1852423, 1576519, 1721380, 701540, 2068038, 1576551, 2067045, 1852455, 1721412, 2068070, 1852487, 1721444, 1852519],
    [80, 9, 14, 494592, 1050624, 279553, 1181697, 1050656, 1181729, 1050688, 1181761, 1050720, 1181793, 494624, 279585, 1313283, 494656, 699909, 279617, 494688, 279649, 1313315, 699941, 756737, 1313347, 673284, 673316, 756769, 1313379, 673348, 699973, 673380, 933893, 1065478, 1343493, 756801, 1066498, 1343525, 933925, 756833, 1065510, 804868, 1343557, 1066530, 1805315, 835079, 933957, 835111, 804900, 1869320, 830472, 1065542, 831016, 1066562, 804932, 831048, 700005, 933989, 1805347, 804964, 1868840, 835143, 1065574, 1049601, 831080, 1066594, 1616902, 1049633, 1747970, 1868872, 1049665, 1805379, 835175, 1616934, 1049697, 1748002, 1343589, 1805411, 1616966, 1868904, 1748034, 1616998, 1748066],
    [56, 10, 14, 658432, 612867, 1184771, 790018, 658464, 1185315, 1185347, 790050, 1150976, 658496, 612387, 1185379, 1544193, 612419, 1675266, 1151008, 790082, 658528, 1544225, 612451, 1675298, 790114, 1151040, 526337, 526369, 1544257, 526401, 1675330, 1563140, 526433, 1151072, 1676805, 1563172, 1823238, 1676837, 1562119, 1676869, 1693192, 1544289, 1823270, 1563204, 1675362, 1562151, 1676901, 1693224, 1709577, 1709609, 1823302, 1562183, 1709641, 1563236, 1693256, 1709673, 1823334, 1562215, 1693288],
    [52, 9, 14, 294912, 1314816, 365569, 1445889, 1314848, 1445921, 1314880, 1445953, 1314912, 1445985, 365601, 294944, 365633, 365665, 558594, 530950, 558626, 294976, 558658, 295008, 1300995, 558690, 793093, 1344515, 1694212, 530982, 557060, 793125, 531014, 1301027, 1344547, 793157, 531046, 557604, 1693732, 1345091, 1824263, 557636, 1300547, 793189, 1708552, 1345123, 1693764, 557668, 1708584, 1824295, 1708616, 1300579, 1708648, 1693796, 1824327, 1824359],
    [40, 8, 14, 464896, 397313, 464928, 397345, 464960, 397377, 464992, 397409, 1315840, 1989122, 1315872, 925189, 925221, 1645060, 1646086, 794115, 1360901, 794147, 1315904, 794179, 925253, 1645092, 1315936, 1646118, 794211, 1858055, 925285, 1989154, 1858087, 1360933, 1645124, 1646150, 1858119, 1360965, 1645156, 1989186, 1646182, 1858151, 1360997, 1989218],
    [48, 6, 14, 311296, 1054720, 1185793, 1054752, 1185825, 1054784, 1185857, 1054816, 1185889, 465921, 713729, 984578, 465953, 713761, 1446913, 465985, 713793, 459267, 466017, 713825, 1317381, 311328, 311360, 459299, 1317413, 810500, 1383424, 1317445, 810532, 311392, 459331, 1514498, 1446945, 1317477, 810564, 1383456, 459363, 810596, 1515042, 1446977, 1383488, 1515074, 984098, 984130, 1383520, 1447009, 1515106, 984162],
    [44, 7, 14, 466944, 466976, 467008, 467040, 715268, 926724, 927268, 927300, 861185, 714788, 927332, 1434115, 975362, 714820, 1238533, 1189382, 661505, 661537, 975394, 714852, 1238565, 661569, 975426, 1189414, 1238597, 661601, 975458, 1189446, 2025478, 1238629, 1317890, 2025510, 1189478, 1317922, 861217, 2025542, 861249, 1434147, 2025574, 861281, 1317954, 1434179, 1317986, 1434211],
    [44, 7, 14, 925696, 269313, 1056769, 925728, 1056801, 925760, 1056833, 925792, 1056865, 453122, 269345, 453154, 269377, 453186, 269409, 582656, 453218, 582688, 582720, 1830403, 582752, 1108484, 1319430, 860161, 797189, 1830435, 1108516, 1319462, 797221, 1108548, 797253, 1108580, 1319494, 797285, 1319526, 2024454, 1830467, 2024486, 860193, 2024518, 1830499, 860225, 860257, 2024550],
    [36, 7, 14, 271360, 271392, 271424, 271456, 532481, 532513, 667141, 532545, 536067, 532577, 667173, 667205, 1206788, 536099, 1337858, 962054, 536131, 1484800, 536163, 1484832, 1206820, 962086, 1484864, 667237, 1337890, 962118, 1206852, 1337922, 1484896, 1206884, 962150, 1152005, 1152037, 1337954, 1152069, 1152101],
    [40, 4, 14, 927744, 306177, 1058817, 927776, 1058849, 927808, 1058881, 927840, 1058913, 306209, 947715, 1190402, 947747, 1190434, 947779, 1190466, 306241, 625667, 1190498, 306273, 625699, 437248, 437280, 1057793, 437312, 625731, 437344, 947811, 1057825, 1019907, 625763, 1057857, 1485826, 1057889, 1485858, 1019939, 1485890, 1019971, 1020003, 1485922],
    [52, 6, 14, 360448, 438273, 665601, 1601536, 360480, 438305, 686594, 930818, 360512, 665633, 438337, 360544, 438369, 686626, 930850, 1093632, 665665, 686658, 930882, 686690, 930914, 1225219, 1357316, 1995780, 1093664, 1601568, 1225251, 1996324, 1473029, 1324037, 665697, 1356836, 1473061, 1324069, 1093696, 1601600, 1715203, 1225283, 1473093, 1324101, 1357380, 1995844, 1093728, 1715235, 1601632, 1225315, 1715267, 1357412, 1473125, 1324133, 1715299, 1995876],
    [52, 7, 14, 798720, 404481, 929793, 798752, 929825, 798784, 929857, 798816, 929889, 293378, 404513, 1454598, 293410, 404545, 1454630, 293442, 404577, 293474, 556547, 1340416, 753664, 556579, 963585, 540164, 556611, 540196, 540228, 556643, 1210885, 1340448, 963617, 1342468, 1210917, 540260, 753696, 1342500, 1340480, 963649, 1210949, 753728, 1062917, 1342532, 753760, 1342564, 1210981, 963681, 1062949, 1454662, 1062981, 1454694, 1063013, 1340512],
    [24, 4, 12, 275456, 275488, 671234, 275520, 275552, 802307, 274433, 671266, 274465, 274497, 802339, 274529, 671298, 802371, 1164290, 671330, 1426435, 802403, 1164322, 1426467, 1164354, 1426499, 1164386, 1426531],
    [28, 5, 9, 538624, 669697, 538656, 669729, 538688, 669761, 538720, 669793, 406529, 801282, 406561, 801314, 377856, 801346, 377888, 406593, 801378, 377920, 932356, 377952, 406625, 932388, 932420, 1163779, 932452, 1163811, 1163843, 1163875],
    [60, 10, 12, 262144, 396289, 396321, 1328642, 262176, 1328674, 396353, 1328706, 685056, 262208, 1328738, 396385, 685088, 262240, 685120, 1444357, 1445380, 685152, 946691, 1397255, 1444389, 1560578, 1208321, 1445412, 1528328, 946723, 1397287, 1208353, 1528360, 1560610, 946755, 1444421, 1397319, 1208385, 1706505, 1590281, 1528392, 1560642, 946787, 1820672, 1706537, 1590313, 1208417, 1445444, 1472006, 1820704, 1560674, 1397351, 1472038, 1820736, 1706569, 1590345, 1444453, 1820768, 1528424, 1472070, 1445476, 1706601, 1590377, 1472102],
    [64, 10, 15, 291841, 1458697, 395779, 394241, 291873, 291905, 675332, 395811, 291937, 554498, 394273, 774663, 395843, 774695, 554530, 394305, 395875, 513541, 554562, 1574921, 675364, 513573, 394337, 1327622, 513605, 554594, 1327654, 675396, 513637, 1429510, 1327686, 1707012, 675428, 1034240, 1327718, 524288, 1429542, 1034272, 774727, 1660424, 524320, 524352, 1707044, 1034304, 774759, 1660456, 524384, 1429574, 1034336, 1575465, 1458217, 1429606, 1460227, 1707076, 1660488, 1575497, 1458249, 1460259, 1460291, 1460323, 1660520, 1575529, 1458281, 1707108],
    [56, 7, 12, 293888, 293920, 293952, 1068547, 935426, 293984, 1199620, 1427456, 1068579, 935458, 454659, 1199652, 586756, 1068611, 1211393, 1821697, 1427488, 1211425, 1821729, 1199684, 1068643, 935490, 1427520, 1330694, 2054147, 1199716, 935522, 1196033, 1211457, 1821761, 1461765, 1330726, 1196065, 1461797, 454691, 1330758, 1427552, 2054179, 586788, 1461829, 1330790, 1461861, 1196097, 1211489, 1633283, 454723, 586820, 2054211, 1633315, 1821793, 1196129, 454755, 1633347, 586852, 2054243, 1633379],
    [68, 8, 12, 1197056, 379905, 1329670, 379937, 676354, 1067010, 379969, 380001, 1198597, 938500, 1428480, 949248, 936451, 1067554, 675874, 439301, 936483, 938532, 1067586, 949280, 1198629, 675906, 936515, 1428512, 439333, 936547, 938564, 1067618, 1198661, 675938, 439365, 1198693, 938596, 1329702, 1329734, 439397, 1870852, 1329766, 1870884, 1428544, 949312, 832518, 1197088, 962563, 949344, 832550, 1197120, 962595, 1428576, 832582, 1473537, 1764871, 2069510, 1870916, 1197152, 1473569, 962627, 2069542, 1764903, 832614, 1473601, 2069574, 1473633, 1764935, 962659, 1870948, 2069606, 1764967],
    [52, 9, 16, 410624, 410656, 1036288, 410688, 1036320, 920577, 1036352, 410720, 920609, 1036384, 1415688, 803841, 298498, 803873, 298530, 528899, 803905, 298562, 1201670, 528931, 803937, 298594, 1201702, 528963, 1547266, 1201734, 920641, 1201766, 1677829, 920673, 528995, 1940999, 2072068, 1413120, 1415720, 1413152, 1547298, 1677861, 1941031, 2072100, 1413184, 1415752, 1413216, 1547330, 1677893, 1941063, 2072132, 1415784, 1547362, 1677925, 1941095, 2072164],
    [52, 9, 16, 805888, 381953, 541697, 381985, 615939, 384514, 382017, 615971, 267266, 541729, 382049, 616003, 384546, 1331719, 267298, 541761, 267842, 384066, 1200645, 541793, 267874, 384098, 616035, 1200677, 805920, 805952, 805984, 1202692, 1200709, 1333251, 1202724, 1333283, 1331751, 1200741, 1202756, 1593864, 1331783, 1926662, 1331815, 1333315, 1202788, 1593896, 1333347, 1926694, 1593928, 1926726, 2000901, 2000933, 1593960, 2000965, 2000997, 1926758],
    [40, 7, 16, 411648, 542721, 411680, 708101, 542753, 1069056, 1203716, 411712, 1203748, 808451, 708133, 1069088, 1203780, 542785, 808483, 411744, 839170, 708165, 1069120, 1680386, 1680930, 838690, 542817, 1203812, 1680962, 838722, 808515, 708197, 1069152, 839266, 1680482, 808547, 2018308, 1332742, 1332774, 2018340, 1332806, 2018372, 1332838, 2018404],
    [64, 9, 16, 613376, 282625, 282657, 482818, 680453, 282689, 282721, 482850, 676864, 940547, 940579, 482882, 676896, 482914, 680485, 1127942, 614916, 1071108, 613408, 1071652, 940611, 614436, 613440, 614980, 1071172, 940643, 676928, 936961, 936993, 1127974, 1071716, 613472, 937025, 614500, 937057, 676960, 1755139, 1128006, 1886210, 1128038, 680517, 1793025, 680549, 1755171, 1886242, 1597959, 1793057, 1755203, 1597991, 729091, 1886274, 1726984, 1598023, 729123, 1793089, 1727016, 1598055, 729155, 1727048, 1755235, 1727080, 729187, 1886306, 1793121],
    [44, 7, 16, 352256, 352288, 352320, 545792, 545824, 545856, 545888, 352352, 806913, 1205763, 806945, 1205795, 806977, 1022979, 1205827, 483329, 807009, 1205859, 1581570, 1681924, 1023011, 483361, 1023043, 1712132, 1023075, 483393, 1682950, 483425, 1681956, 1581602, 1682982, 1712164, 1401349, 1581634, 1681988, 1712196, 1401381, 1683014, 1682020, 1581666, 1712228, 1401413, 1683046, 1401445],
    [52, 9, 16, 414721, 942597, 629251, 414753, 402946, 942629, 414785, 289284, 402978, 414817, 289316, 416768, 1813506, 289348, 416800, 629283, 629315, 289380, 1204744, 942661, 942693, 403010, 629347, 1073670, 403042, 1599491, 1204776, 416832, 1896456, 416864, 1073702, 1862151, 1599523, 1862183, 1204808, 1073734, 1371142, 1073766, 1371174, 1599555, 1813538, 1896488, 1204840, 1371206, 1813570, 1862215, 1599587, 1371238, 1896520, 1813602, 1862247, 1896552],
    [40, 5, 16, 285696, 285728, 285760, 993281, 1338883, 285792, 993313, 546817, 644099, 570884, 644643, 1338403, 570916, 546849, 993345, 890370, 546881, 890402, 1338947, 644163, 1335296, 644707, 1338467, 1467396, 570948, 1335328, 890434, 546913, 890466, 570980, 1894400, 993377, 1467428, 1894432, 1335360, 1467460, 1894464, 1335392, 1894496, 1467492],
    [60, 10, 16, 680960, 715776, 680992, 773635, 555524, 425477, 1075720, 846849, 2012168, 555556, 681024, 425509, 681056, 555588, 715808, 904710, 425541, 846881, 555620, 773667, 425573, 715840, 1466369, 813575, 813607, 846913, 1075752, 813639, 1466401, 1334273, 904742, 1438210, 715872, 1438242, 813671, 1334305, 846945, 1438274, 1334337, 1438306, 1468937, 1075784, 1882121, 773699, 1882665, 1468457, 904774, 2012200, 1075816, 1334369, 773731, 1466433, 1469001, 1466465, 904806, 1469033, 1882185, 2012232, 1882217, 2012264],
    [76, 12, 16, 418816, 512514, 506371, 418848, 643588, 512546, 506403, 716800, 418880, 847873, 506435, 716832, 418912, 643620, 847905, 506467, 716864, 417793, 417825, 847937, 507397, 1486848, 716896, 417857, 507429, 847969, 417889, 1716227, 507461, 1488898, 512578, 1078791, 643652, 1585670, 512610, 1209865, 507493, 1078823, 965636, 643684, 1486880, 1751560, 1209897, 1585702, 1228298, 1078855, 1488930, 1716259, 1209929, 965668, 1078887, 1751592, 1486912, 1209961, 1691658, 1228330, 1488962, 1603083, 1585734, 1716291, 965700, 1691690, 1603115, 1751624, 1228362, 1486944, 1488994, 1603147, 1585766, 1691722, 965732, 1716323, 1603179, 1751656, 1228394, 1691754],
    [36, 7, 16, 308224, 324609, 308256, 549889, 324641, 308288, 324673, 376323, 308320, 549921, 324705, 424450, 376355, 424482, 549953, 424514, 376387, 424546, 549985, 1604100, 376419, 1735173, 1717251, 1604132, 1735205, 1717283, 1604164, 1735237, 1995270, 1717315, 1604196, 1735269, 1995302, 1995334, 1717347, 1995366],
    [32, 6, 15, 420864, 290816, 419841, 510466, 290848, 510498, 420896, 510530, 290880, 419873, 510562, 511493, 420928, 290912, 419905, 511525, 420960, 1077764, 419937, 1077796, 511557, 1619969, 1077828, 511589, 1620001, 1691139, 1077860, 1691171, 1691203, 1620033, 1691235, 1620065],
    [48, 10, 12, 642048, 552961, 814081, 552993, 814113, 553025, 817670, 903684, 948743, 553057, 672258, 1341961, 814145, 817702, 903716, 948775, 1339907, 672290, 1341993, 814177, 642080, 903748, 1339939, 1079816, 672322, 642112, 1079848, 817734, 1339971, 903780, 672354, 948807, 642144, 1342025, 1079880, 817766, 1340003, 948839, 1470464, 1079912, 816645, 1342057, 1470496, 816677, 1470528, 816709, 1470560, 816741],
    [44, 7, 12, 266240, 698369, 567810, 266272, 266304, 567842, 266336, 698401, 698433, 567874, 567906, 698465, 1476099, 1607172, 1476131, 572419, 457732, 1607204, 572451, 1476163, 457764, 572483, 1607236, 1053697, 573027, 1475683, 457796, 1053729, 1607268, 1359365, 1053761, 1490438, 457828, 1359397, 1053793, 2011136, 2011168, 1490470, 2011200, 1359429, 2011232, 1490502, 1359461, 1490534],
    [64, 11, 15, 307201, 307233, 307265, 821763, 307297, 719364, 364544, 821795, 719396, 821827, 660994, 1214468, 719428, 364576, 457221, 1214500, 588294, 821859, 661026, 457253, 661058, 1214532, 364608, 950793, 588326, 457285, 661090, 364640, 1081866, 588358, 1215076, 457317, 659457, 1099271, 950825, 659489, 588390, 831488, 441353, 718948, 659521, 326666, 1081898, 441385, 950857, 326698, 1099303, 831520, 659553, 441417, 1081930, 441961, 950377, 326730, 831552, 1184264, 1099335, 1081962, 1184296, 326762, 831584, 1184328, 1099367, 1184360],
    [44, 9, 16, 264192, 264224, 444931, 264256, 444963, 264288, 444995, 496641, 440320, 445027, 496673, 496705, 2028034, 440352, 1022468, 496737, 2028066, 689156, 1022500, 820741, 440384, 689188, 1022532, 820773, 2028098, 689220, 1740295, 440416, 820805, 689764, 1740327, 820837, 1022052, 1740359, 1740391, 1284614, 1284646, 2017800, 1284678, 1284710, 2017832, 2017864, 2017896, 2028130],
    [60, 11, 16, 310272, 310304, 310336, 310368, 527361, 527393, 571393, 527425, 527457, 1608198, 1503746, 571425, 1608230, 1503778, 1182720, 1503810, 1182752, 1477124, 571457, 1477156, 1182784, 456195, 1345539, 1182816, 456227, 1345571, 456259, 1345603, 571489, 456291, 1477188, 1345635, 1856007, 1857032, 1987081, 1477220, 1988106, 1856039, 1887749, 1857064, 1987113, 1608262, 2043914, 2044458, 1987626, 1608294, 1887781, 1856071, 1857096, 2044490, 1987145, 1987658, 1887813, 1503842, 1887845, 1856103, 1857128, 2044522, 1987177, 1987690],
    [52, 8, 12, 790528, 1086981, 955908, 601602, 601634, 955940, 1052673, 601666, 955972, 1087013, 601698, 956004, 790560, 1087045, 1087077, 425985, 953859, 1052705, 426017, 1349126, 1349158, 1215490, 748550, 1349190, 1346564, 790592, 953891, 426049, 748582, 1052737, 1349222, 1215522, 1346596, 790624, 953923, 426081, 748614, 1215554, 1480199, 1346628, 688128, 953955, 1052769, 748646, 688160, 1215586, 1480231, 1346660, 1480263, 688192, 1480295, 688224],
    [44, 7, 12, 1085954, 921600, 1085986, 1743364, 1347588, 1086018, 922625, 1213440, 1743396, 1347620, 1086050, 1217027, 1743428, 1347652, 1217059, 921632, 1217091, 1213472, 1217123, 1348196, 1084418, 922657, 1213504, 921664, 1084450, 922689, 1213536, 1479174, 1084482, 1479206, 921696, 819201, 1084514, 1479238, 819233, 922721, 1479270, 2005509, 819265, 2005541, 2005573, 819297, 1742948, 2005605],
    [40, 7, 16, 559104, 398337, 1234434, 1481730, 559136, 692740, 559168, 398369, 559200, 398401, 1482274, 710149, 398433, 1482306, 1482338, 692772, 1233954, 2075139, 692804, 1233986, 692836, 1234018, 1576960, 1627654, 2075171, 710181, 1217542, 1576992, 1627686, 1217574, 710213, 1218118, 710245, 1218150, 1577024, 1627206, 1577056, 1627238, 2075203, 2075235],
    [68, 11, 16, 629760, 690177, 760833, 317954, 629792, 690209, 760865, 316931, 317986, 629824, 316963, 318018, 690241, 760897, 316995, 629856, 317027, 318050, 690273, 760929, 2020874, 1945092, 841222, 1945124, 429056, 429088, 429120, 1577985, 429152, 1945156, 841254, 1088005, 1088037, 1088069, 841286, 1578017, 1088101, 841318, 2020906, 1219079, 1774088, 1757192, 1875976, 1889801, 1480713, 1219111, 1757736, 1876008, 1219143, 1773608, 1889833, 1480745, 1219175, 1578049, 2020938, 1757768, 1876040, 1889865, 1480777, 1578081, 1757800, 1876072, 1773640, 1945188, 1889897, 1480809, 1773672, 2020970],
    [52, 8, 16, 430080, 1024000, 631298, 430112, 631330, 433667, 433699, 430144, 631362, 433731, 631394, 1615364, 433763, 1615396, 430176, 1615428, 1615460, 1024032, 1024064, 952321, 603137, 603169, 952353, 603201, 603233, 952385, 1024096, 952417, 1725441, 2023942, 908292, 1613319, 1417217, 1250821, 1417249, 908324, 1613351, 1250853, 1725473, 1417281, 908356, 2023974, 1250885, 1417313, 908388, 1250917, 1613383, 1725505, 2024006, 1613415, 1725537, 2024038],
    [64, 12, 16, 732160, 732192, 300033, 300065, 595458, 893953, 300097, 961032, 514565, 1092105, 595490, 732224, 645638, 1090051, 961064, 595522, 1090083, 893985, 1092137, 732256, 300129, 1614346, 595554, 1090115, 431104, 1505803, 1744907, 1090147, 431136, 514597, 961096, 431168, 645670, 431200, 514629, 894017, 1092169, 988676, 645702, 1614378, 988708, 514661, 1745451, 988740, 894049, 645734, 988772, 987655, 2028554, 1614410, 1505323, 987687, 1745483, 961128, 987719, 1505355, 987751, 1092201, 2028586, 1614442, 1505899, 1745003, 2028618, 2028650],
    [52, 10, 16, 563200, 2053637, 1223685, 1093124, 1093156, 600064, 697858, 1922052, 1224229, 1224261, 828931, 702983, 1093188, 704008, 600096, 563232, 697890, 600128, 563264, 828963, 703015, 563296, 697922, 704040, 828995, 1093220, 697954, 1355270, 829027, 703047, 1224293, 1355302, 823297, 600160, 823329, 1355334, 823361, 1452553, 704072, 1452585, 1355366, 823393, 1922084, 2053157, 703079, 1452617, 704104, 1922116, 2053189, 1452649, 1922148, 2053221],
    [48, 8, 16, 323074, 323106, 1356293, 323138, 323170, 708608, 1356325, 708640, 610819, 610851, 1354244, 610883, 1354276, 1356357, 708672, 825345, 1354308, 708704, 825377, 1354340, 610915, 825409, 1125377, 825441, 1880582, 1125409, 957440, 1096708, 1880614, 1125441, 957472, 1125473, 1502727, 1649664, 957504, 1880646, 1649696, 957536, 1649728, 1502759, 1096740, 1649760, 1356389, 1502791, 1880678, 1096772, 1502823, 1096804],
    [48, 8, 16, 368640, 301057, 368672, 265730, 368704, 265762, 368736, 265794, 265826, 403972, 301089, 301121, 301153, 404004, 995328, 404036, 404068, 1241088, 1634821, 1126401, 1025025, 995360, 1750534, 1126433, 1025057, 1241120, 1881607, 995392, 1025089, 1126465, 1634853, 1750566, 995424, 1025121, 1241152, 1881639, 1126497, 1918467, 1750598, 1634885, 1881671, 1241184, 1918499, 1750630, 1918531, 1881703, 1634917, 1918563],
    [44, 7, 16, 303105, 303137, 303169, 303201, 472065, 472097, 472129, 472161, 435200, 759298, 435232, 435264, 759330, 435296, 945154, 965123, 724992, 945186, 759362, 725024, 945218, 1242112, 725056, 759394, 725088, 1897988, 1618437, 945250, 965155, 1749510, 965187, 965219, 1618469, 1242144, 1749542, 1898020, 1618501, 1242176, 1749574, 1898052, 1618533, 1749606, 1242208, 1898084],
    [28, 6, 15, 325633, 305152, 325665, 325697, 305184, 325729, 849920, 1095170, 305216, 1488387, 1619460, 1243653, 305248, 1095202, 1488419, 1619492, 1095234, 849952, 1488451, 1243685, 849984, 1619524, 1243717, 1095266, 1488483, 850016, 1619556, 1243749],
    [40, 7, 12, 775168, 279042, 833538, 279074, 833570, 436225, 279106, 833602, 279138, 833634, 436257, 775200, 850945, 436289, 1113605, 436321, 829440, 829472, 850977, 1358342, 829504, 1358374, 775232, 1096195, 829536, 775264, 1113637, 1227268, 1096227, 1227300, 851009, 1358406, 1096259, 1113669, 1227332, 1096291, 1227364, 1358438, 851041, 1113701],
    [44, 7, 12, 451584, 451616, 451648, 451680, 596993, 837123, 719875, 597025, 597057, 837155, 597089, 837187, 968196, 968228, 968260, 837219, 968292, 1710597, 1580550, 1710629, 1237506, 719907, 1368065, 1237538, 1368097, 1580582, 1237570, 1710661, 719939, 1368129, 1237602, 1368161, 719971, 1580614, 1375237, 1710693, 1506310, 1375269, 1580646, 1506342, 1375301, 1506374, 1375333, 1506406],
    [44, 6, 15, 295937, 295969, 296001, 296033, 707074, 707106, 967171, 1098244, 707138, 967203, 588804, 967235, 1098276, 998403, 967267, 874496, 975873, 874528, 874560, 975905, 998435, 874592, 1098308, 707170, 975937, 1082368, 1082400, 1447940, 1098340, 975969, 1082432, 1447972, 998467, 1082464, 998499, 588836, 1448004, 588868, 1448036, 588900, 1893893, 1893925, 1893957, 1893989],
    [68, 10, 16, 281600, 296960, 321537, 296992, 321569, 1232386, 297024, 321601, 1232418, 297056, 321633, 1232450, 1232482, 281632, 865797, 846342, 281664, 865829, 846374, 619522, 281696, 619554, 846406, 865861, 619586, 619618, 1869825, 1492487, 809475, 846438, 1754632, 1923072, 1661953, 1885705, 865893, 809507, 1869857, 1492519, 991748, 1923104, 809539, 1661985, 1754664, 1885737, 809571, 1895424, 1869889, 1923136, 991780, 1662017, 1492551, 1072132, 1895456, 1754696, 1072164, 1072708, 1885769, 1923168, 1072740, 1895488, 991300, 1662049, 1869921, 1492583, 991332, 1895520, 1754728, 1885801],
    [60, 9, 16, 543745, 416258, 416290, 416322, 733701, 1361925, 578051, 578083, 584705, 543777, 578115, 578147, 543809, 1362469, 733221, 584737, 543841, 730114, 548356, 1624584, 1493510, 584769, 730146, 548388, 1773063, 416354, 733765, 1361989, 584801, 548420, 1493542, 548452, 1624616, 673792, 585728, 1493574, 730178, 673824, 1362533, 1773095, 1924097, 673856, 1493606, 730210, 673888, 585760, 733285, 1389574, 1389606, 1924129, 1773127, 585792, 1624648, 1389638, 1924161, 1389670, 1773159, 1624680, 585824, 1924193],
    [64, 9, 16, 427008, 323585, 564739, 323617, 323649, 564771, 413696, 427040, 1350150, 323681, 413728, 562690, 432644, 413760, 432676, 427072, 413792, 564803, 544769, 1625091, 432708, 544801, 564835, 427104, 544833, 432740, 544865, 562722, 562754, 1625123, 562786, 1009157, 1758727, 717824, 1625155, 1874951, 1009189, 1465347, 2006536, 1009221, 1350182, 1465379, 1536003, 1009253, 1625187, 1758759, 717856, 1874983, 2006568, 1465411, 1350214, 1536035, 1465443, 1758791, 717888, 1536067, 1875015, 2006600, 1350246, 1536099, 1758823, 717920, 1875047, 2006632],
    [52, 9, 16, 283649, 283681, 529408, 1612295, 283713, 529440, 283745, 1626632, 751107, 529472, 751139, 1233412, 529504, 1495558, 1233444, 956420, 1233476, 1233508, 1873928, 956452, 751171, 878596, 956484, 956516, 1235461, 1495590, 751203, 1235493, 1495622, 849410, 1612327, 1235525, 1495654, 1235557, 878628, 1612359, 1667078, 849442, 878660, 1874472, 1626152, 1667110, 878692, 1874504, 1626184, 1626728, 1667142, 849474, 1612391, 1667174, 1874024, 849506],
    [44, 6, 12, 515073, 448002, 973826, 515105, 448034, 1105411, 973858, 974402, 442369, 515137, 1105443, 974434, 447554, 1105475, 442401, 515169, 447586, 1105507, 442433, 1236484, 1824768, 1236516, 442465, 704512, 1775620, 1236548, 778243, 778275, 1824800, 704544, 1236580, 1775652, 1367557, 778307, 1367589, 1367621, 1824832, 704576, 1775684, 1367653, 778339, 704608, 1824864, 1775716],
    [40, 7, 12, 973315, 646660, 1496067, 973347, 574464, 842242, 646692, 842274, 574496, 842306, 842338, 973379, 973411, 574528, 646724, 646756, 1496099, 1104389, 1366534, 574560, 1366566, 1694720, 1104421, 1825793, 1104453, 835585, 1104485, 1694752, 1825825, 1496131, 835617, 1366598, 1496163, 1366630, 1694784, 1825857, 835649, 835681, 1694816, 1825889],
    [60, 11, 16, 647168, 312320, 312352, 647200, 312384, 312416, 443393, 443425, 443457, 647232, 443489, 859651, 1491463, 647264, 1369606, 859683, 1369638, 910850, 1369670, 910882, 859715, 1369702, 1360392, 1491495, 1360424, 859747, 923648, 910914, 923680, 923712, 1360456, 923744, 1631753, 1491527, 910946, 2007557, 1171972, 1762826, 1711105, 1631785, 1826817, 1172004, 1762858, 2007589, 1631817, 1360488, 1711137, 1826849, 1762890, 1491559, 2007621, 1631849, 1172036, 1711169, 1762922, 1826881, 2007653, 1172068, 1711201, 1826913],
    [52, 10, 16, 584195, 517121, 304642, 584227, 304674, 858628, 584259, 517153, 304706, 584291, 531457, 304738, 1229318, 284672, 531489, 284704, 517185, 531521, 1229350, 284736, 531553, 858660, 284768, 1230345, 977413, 517217, 858692, 977445, 977477, 858724, 977509, 1370118, 1501703, 1499656, 1370150, 1230377, 1244168, 1499688, 1501735, 1370694, 1228870, 1499720, 1244200, 1501767, 1499752, 1230409, 1244232, 1370726, 1228902, 1501799, 1230441, 1244264],
    [76, 12, 16, 486400, 313345, 486432, 1109506, 313377, 481795, 1109538, 313409, 792068, 939010, 1109570, 313441, 481827, 1362944, 1109602, 481859, 1362976, 486464, 481891, 1474564, 1363008, 1475108, 486496, 744965, 791588, 792132, 1270278, 951815, 744997, 951847, 951879, 745029, 1363040, 951911, 1223176, 745061, 792164, 1240585, 1223208, 1212938, 1792004, 1240617, 939042, 1212970, 1595392, 1400331, 1223240, 1240649, 939074, 1792036, 939106, 1989633, 1213002, 1240681, 1400363, 1270310, 1595424, 1943553, 1792068, 1989665, 1474628, 1270342, 1595456, 1400395, 1223272, 1213034, 1792100, 1989697, 1595488, 1400427, 1943585, 1989729, 1474660, 1270374, 1943617, 1943649],
    [44, 8, 16, 446465, 446497, 743938, 446529, 1632771, 743970, 446561, 578560, 1737731, 744002, 970246, 1138694, 979460, 1632803, 578592, 1737763, 744034, 578624, 970278, 578656, 1632835, 876037, 1632867, 979492, 876069, 970310, 979524, 979556, 1763847, 876101, 1763879, 876133, 1138726, 970342, 1763911, 1534977, 1763943, 1535009, 1737795, 1138758, 1535041, 1737827, 1138790, 1535073],
    [48, 5, 16, 971776, 980482, 980514, 487424, 980546, 487456, 980578, 487488, 487520, 1273857, 1273889, 631808, 560130, 1273921, 560162, 1273953, 631840, 502785, 502817, 631872, 560194, 631904, 970753, 502849, 502881, 1635844, 1497088, 971808, 560226, 1739267, 1497120, 970785, 971840, 2070532, 1635876, 1497152, 2070564, 1497184, 970817, 1739299, 971872, 1635908, 1739331, 2070596, 970849, 1739363, 1635940, 2070628],
    [40, 7, 16, 357377, 340993, 357409, 341025, 357441, 341057, 357473, 341089, 318464, 318496, 318528, 1372676, 318560, 734208, 734240, 734272, 1226242, 1110531, 1226274, 1110563, 1110595, 1110627, 734304, 1899013, 2045446, 1939460, 1372708, 1226306, 1939492, 1899045, 1226338, 1372740, 2045478, 1939524, 1899077, 1372772, 2045510, 1939556, 1899109, 2045542],
    [40, 6, 15, 342017, 342049, 342081, 342113, 565762, 565794, 565826, 565858, 581632, 581664, 581696, 581728, 579584, 579616, 1111555, 1504772, 579648, 1783808, 1766917, 579680, 1111587, 1504804, 710657, 1766949, 710689, 1111619, 710721, 1783840, 1504836, 710753, 1766981, 1432576, 1111651, 1432608, 1432640, 1783872, 1504868, 1432672, 1767013, 1783904],
    [36, 6, 12, 580609, 580641, 343041, 343073, 343105, 343137, 1636868, 1767941, 580673, 580705, 843776, 843808, 843840, 843872, 777216, 1112578, 1892353, 1374723, 777248, 1112610, 1374755, 777280, 1636900, 1892385, 1767973, 1112642, 777312, 1374787, 1636932, 1768005, 1892417, 1112674, 1374819, 1636964, 1768037, 1892449],
    [32, 5, 12, 335872, 335904, 335936, 335968, 727041, 1115650, 727073, 1115682, 727105, 1115714, 728579, 795649, 1115746, 605186, 605218, 728611, 795681, 727137, 728643, 1776640, 605250, 728675, 605282, 1508868, 795713, 1776672, 1508900, 795745, 1508932, 1776704, 1508964, 1776736],
    [52, 8, 15, 334849, 334881, 334913, 334945, 336896, 663553, 706055, 336928, 663585, 336960, 663617, 336992, 663649, 1006083, 599041, 599073, 794627, 1623040, 1006115, 1006147, 852485, 1006179, 1114630, 752130, 752162, 599105, 752194, 794659, 852517, 1772036, 599137, 1114662, 2033666, 752226, 794691, 852549, 1772068, 1623072, 1114694, 2033698, 794723, 706087, 706119, 852581, 1114726, 1623104, 706151, 1772100, 2033730, 1772132, 2033762, 1623136],
    [40, 6, 16, 428032, 428064, 428096, 428128, 477698, 477730, 1598979, 1379331, 477762, 1531904, 477794, 598016, 1531936, 575489, 1531968, 575521, 1532000, 575553, 575585, 1379875, 598048, 598080, 1598499, 598112, 1639940, 1379907, 1771013, 1639972, 1771045, 1386496, 1598531, 1386528, 1379939, 1640004, 1386560, 1771077, 1386592, 1640036, 1771109, 1598563],
    [56, 9, 16, 314369, 488962, 854018, 314401, 488994, 854050, 314433, 489026, 854082, 314465, 1477632, 489058, 854114, 1608705, 1477664, 1608737, 1477696, 1608769, 1477728, 1116679, 1608801, 1729543, 882180, 731136, 1511941, 1730087, 1116199, 882212, 731168, 882244, 731200, 882276, 1658371, 731232, 2060806, 1551364, 1511973, 1116743, 1658403, 1512005, 1551396, 1551428, 1729607, 1658435, 1512037, 1551460, 1116775, 1509896, 1509928, 2060838, 1509960, 1658467, 1509992, 1729639, 2060870, 2060902],
    [48, 8, 16, 299008, 299040, 299072, 299104, 1091078, 602627, 958467, 593410, 602659, 1091110, 593442, 593474, 1353220, 593506, 602691, 862209, 1091142, 602723, 1650688, 862241, 958499, 1353252, 862273, 1548288, 958531, 1353284, 1548320, 862305, 1644039, 1091174, 824321, 1644071, 824353, 1154565, 1548352, 1644103, 1154597, 1650720, 1644135, 958563, 1154629, 1548384, 824385, 1353316, 1154661, 1650752, 824417, 1650784],
    [60, 10, 16, 339968, 470017, 340000, 470049, 340032, 470081, 1463296, 340064, 1351173, 1027587, 1118211, 1222152, 827906, 1251844, 1118755, 470113, 1118787, 1222184, 1118819, 1484294, 827938, 1251876, 1027107, 1222216, 1027139, 1484326, 1249799, 827970, 1249831, 1251908, 1679360, 1800199, 1249863, 1251940, 1351205, 1811457, 1249895, 1484358, 1380873, 1679392, 1027171, 1351237, 1811489, 1380905, 1800231, 1222248, 1679424, 828002, 1380937, 1463328, 1811521, 1800263, 1380969, 1463360, 1679456, 1811553, 1484390, 1463392, 1800295, 1351269],
    [60, 11, 16, 473088, 268288, 677889, 268320, 333314, 473120, 268352, 333346, 268384, 333378, 473152, 333410, 1661443, 990725, 1121798, 473184, 677921, 990757, 844803, 990789, 1381895, 1245190, 845347, 1512968, 677953, 1660963, 845379, 1121830, 845411, 990821, 1381927, 1121862, 1513000, 677985, 1660995, 1121894, 1107460, 1245222, 1107492, 1381959, 1252874, 1513032, 1107524, 1523209, 1245254, 1252906, 1661027, 1252938, 1107556, 1252970, 1381991, 1302528, 1513064, 1523241, 1302560, 1245286, 1523273, 1302592, 1302624, 1523305],
    [48, 7, 16, 648193, 735233, 735265, 1055744, 648225, 735297, 663044, 1269251, 1187330, 648257, 735329, 1448961, 1513990, 1055776, 663076, 663108, 474112, 1187362, 1269283, 663140, 474144, 648289, 474176, 1514022, 474208, 1448993, 1106437, 1514054, 1106469, 1269315, 1391622, 1106501, 1514086, 1106533, 1055808, 1269347, 1391654, 1695744, 1187394, 1695776, 1391686, 1449025, 1055840, 1695808, 1187426, 1449057, 1391718, 1695840],
    [44, 8, 12, 401408, 270850, 270882, 270914, 400899, 270946, 327681, 400931, 401440, 327713, 400963, 401472, 327745, 400995, 401504, 327777, 1123844, 1449985, 1254918, 1827841, 1450017, 1123876, 1123908, 1123940, 1450049, 1129472, 1517063, 1129504, 1827873, 1450081, 1129536, 1517095, 1129568, 1385989, 1827905, 1254950, 1386021, 1254982, 1386053, 1517127, 1255014, 1386085, 1517159, 1827937],
    [48, 7, 12, 469507, 1253379, 1253923, 1122818, 1253955, 1122850, 1122882, 469027, 1122914, 1187840, 1516038, 469059, 867328, 1384964, 1319937, 867360, 1384996, 1187872, 469603, 1253475, 867392, 1319969, 399362, 399394, 1187904, 1507329, 399426, 1780229, 399458, 1385028, 867424, 1385060, 1320001, 1260545, 1187936, 1507361, 1260577, 1320033, 1260609, 1780261, 1507393, 1516070, 1516102, 1260641, 1780293, 1516134, 1780325, 1507425],
    [48, 8, 16, 370688, 370720, 370752, 1083907, 370784, 691714, 878087, 649217, 691746, 878119, 616964, 691778, 649249, 878151, 649281, 649313, 1083939, 992258, 616996, 617028, 752641, 1083971, 992290, 2057734, 1518598, 992322, 992866, 1519142, 752673, 745989, 1387525, 1519174, 1084003, 617060, 746021, 1387557, 746053, 1387589, 752705, 746085, 1387621, 878183, 1519206, 691298, 2057254, 752737, 2057286, 2057318],
    [64, 10, 16, 330752, 328705, 1124869, 330784, 484867, 328737, 1124901, 330816, 484899, 328769, 330848, 484931, 328801, 1925639, 764928, 484963, 1664005, 1124933, 1795593, 896001, 2056708, 1124965, 764960, 1255942, 1925671, 896033, 1664037, 695810, 1795625, 695842, 1255974, 1519623, 695874, 1781769, 2056740, 764992, 695906, 1256006, 1256038, 896065, 1519655, 765024, 1781801, 896097, 748040, 2001926, 1925703, 748072, 1519687, 1664069, 1795657, 1781833, 2001958, 748104, 2056772, 748136, 2001990, 1925735, 1519719, 1664101, 1782377, 2002022, 1795177, 2056804],
    [44, 6, 16, 356352, 373761, 1521154, 356384, 373793, 1521186, 356416, 373825, 1521218, 356448, 373857, 1521250, 371712, 1652229, 371744, 822274, 822306, 371776, 371808, 1652261, 1351680, 1652293, 1552384, 1552416, 1351712, 1765892, 1552448, 1929731, 1552480, 1765924, 1652325, 822338, 1351744, 1929763, 822370, 1942533, 1351776, 1942565, 1765956, 1942597, 1929795, 1942629, 1765988, 1929827],
    [64, 11, 16, 331777, 331809, 331841, 331873, 370178, 463872, 370210, 463904, 370242, 370274, 463936, 897025, 463968, 1522182, 897057, 1373699, 897089, 864772, 969224, 1652744, 1482752, 864804, 1522214, 1100295, 1745921, 864836, 1522246, 897121, 864868, 1231369, 1156613, 969256, 1482784, 1373731, 1156645, 1745953, 1652776, 1100327, 1156677, 1231401, 969288, 1652808, 1389066, 1156709, 1100359, 1389098, 2072583, 1231433, 1482816, 1373763, 2072615, 1745985, 1522278, 1389130, 969320, 2072647, 1482848, 1100391, 1746017, 1373795, 1389162, 2072679, 1231465, 1652840],
    [36, 7, 15, 333824, 358401, 333856, 358433, 333888, 358465, 333920, 358497, 1120772, 386562, 996867, 386594, 620544, 1120804, 386626, 1259013, 386658, 996899, 1120836, 620576, 1259045, 996931, 620608, 1259077, 1120868, 996963, 620640, 1259109, 1907206, 1931268, 1931300, 1907238, 1931332, 1907270, 1931364, 1907302],
    [60, 10, 12, 319488, 359425, 989185, 319520, 359457, 319552, 359489, 319584, 359521, 989217, 1391111, 1128964, 989249, 1260038, 1128996, 1391143, 1260070, 573955, 997379, 573987, 997411, 721926, 574019, 997443, 1260102, 574051, 997475, 1434630, 1129028, 989281, 1391175, 721958, 1129060, 1382400, 1434662, 721990, 1260134, 1382432, 1382464, 1391207, 1382496, 1697289, 1908226, 1434694, 722022, 1697321, 2039301, 1908258, 1697353, 1376776, 2039333, 1908290, 1376808, 1376840, 1376872, 1434726, 2039365, 1908322, 1697385, 2039397],
    [36, 7, 12, 349184, 273409, 273441, 349216, 273473, 273505, 349248, 1191427, 721412, 983040, 349280, 721444, 1191459, 1000965, 983072, 1000997, 1394182, 721476, 1134593, 1191491, 1134625, 1394214, 983104, 1001029, 1733122, 721508, 1134657, 1134689, 1394246, 1733154, 983136, 1191523, 1733186, 1001061, 1394278, 1733218],
    [32, 7, 15, 459776, 459808, 611329, 1133058, 459840, 611361, 459872, 611393, 1377281, 1246724, 611425, 1395203, 1131013, 1133090, 1395235, 1131045, 1133122, 1246756, 1395267, 1393158, 1133154, 1377313, 1131077, 1395299, 1393190, 1246788, 1377345, 1131109, 1393222, 1246820, 1377377, 1393254],
    [52, 8, 16, 390658, 871426, 390690, 871458, 758276, 390722, 871490, 837632, 350209, 390754, 871522, 1247232, 350241, 837664, 1132037, 350273, 1378305, 350305, 837696, 700931, 1787398, 1247264, 700963, 758308, 1132069, 700995, 837728, 1787430, 1378337, 701027, 985607, 758340, 985639, 941056, 985671, 758372, 2055168, 941088, 1132101, 1247296, 941120, 1378369, 2055200, 1787462, 941152, 1132133, 985703, 1247328, 2055232, 1378401, 1787494, 2055264],
    [32, 6, 16, 351233, 351265, 351297, 351329, 576512, 576544, 1641473, 1510915, 1510947, 576576, 1526274, 1657348, 576608, 1788421, 1526306, 1494017, 1494049, 1657380, 1641505, 1494081, 1788453, 1526338, 1494113, 1657412, 1510979, 1788485, 1526370, 1657444, 1641537, 1788517, 1511011, 1641569],
    [56, 9, 16, 315392, 353280, 315424, 1398279, 315456, 338945, 856578, 353312, 315488, 1398311, 338977, 353344, 1398343, 1363969, 339009, 353376, 339041, 1364001, 856610, 568835, 1267204, 568867, 1267236, 1364033, 856642, 568899, 1267268, 1265157, 568931, 1910784, 1265189, 1267300, 1364065, 876545, 999428, 769542, 999460, 769574, 999492, 769606, 1529352, 769638, 856674, 999524, 1529384, 1398375, 1910816, 876577, 1265221, 1529416, 1529448, 876609, 1265253, 876641, 1910848, 1910880],
    [48, 9, 16, 1137154, 1268228, 1266183, 606725, 1119747, 1137186, 1268260, 1364993, 607750, 606757, 1119779, 1266215, 607782, 1137218, 1365025, 606789, 1268292, 607814, 1365057, 1119811, 1459720, 1911809, 1266247, 606821, 1137250, 2009095, 1459752, 617473, 607846, 617505, 1266279, 617537, 1268324, 617569, 1459784, 879616, 1459816, 879648, 1365089, 1119843, 1911841, 879680, 2009127, 879712, 1911873, 2009159, 1911905, 2009191],
    [56, 10, 16, 445440, 445472, 534024, 445504, 1102849, 742915, 454148, 873989, 354304, 742947, 354336, 445536, 1007106, 874021, 354368, 1007138, 742979, 354400, 1007170, 454180, 874053, 1007202, 485377, 1138183, 665097, 812034, 485409, 743011, 485441, 454212, 874085, 485473, 534056, 454244, 1138215, 665129, 534088, 1138247, 812066, 1138279, 665161, 1239558, 534120, 1464320, 812098, 1239590, 812130, 1239622, 665193, 1239654, 1464352, 1464384, 1102881, 1464416, 1102913, 1102945],
    [52, 7, 16, 1011712, 355329, 679426, 355361, 355393, 355425, 1100800, 679458, 1011744, 1399301, 1008131, 1530374, 1011776, 1399333, 1100832, 679490, 978436, 1640451, 1530406, 1399365, 1902598, 679522, 1901573, 978468, 1530438, 1399397, 978500, 1530470, 1727488, 1008163, 1858561, 978532, 1640483, 1901605, 1902630, 1727520, 1011808, 1008195, 1858593, 1901637, 1100864, 1640515, 1727552, 1902662, 1858625, 1901669, 1727584, 1100896, 1008227, 1858657, 1640547, 1902694],
    [64, 11, 16, 1012736, 468482, 468514, 880641, 468546, 548864, 548896, 1781256, 1012768, 548928, 880673, 1530888, 468578, 1012800, 863747, 1140228, 1649159, 2042377, 1140260, 863779, 1140292, 1697792, 1517572, 1402374, 880705, 863811, 548960, 863843, 1140324, 1697824, 1781288, 1697856, 1012832, 1070597, 1517604, 1697888, 1530920, 2043402, 880737, 1649191, 2026506, 1517636, 1070629, 2042409, 1402406, 2027050, 2042922, 1649223, 1531464, 1402438, 1780808, 1070661, 2042441, 1402470, 1517668, 2027082, 2042954, 1649255, 1531496, 1070693, 1780840, 2042473, 2027114, 2042986],
    [36, 8, 16, 1042432, 287745, 287777, 338436, 1042464, 287809, 338468, 287841, 338500, 1143809, 1663494, 561667, 1663526, 1141250, 1141282, 1663558, 561699, 561731, 338532, 561763, 1143841, 1042496, 1888773, 1042528, 1141314, 1141346, 1794567, 1143873, 1888805, 1794599, 1794631, 1663590, 1143905, 1794663, 1888837, 1888869],
    [44, 7, 12, 780288, 781313, 1011202, 780320, 1011234, 747012, 1011266, 1011298, 1142275, 781345, 780352, 1142307, 1142339, 781377, 780384, 1142371, 1404422, 1145857, 781409, 747044, 747076, 1145889, 747108, 1145921, 1533445, 1272837, 1404454, 1273381, 1798146, 1532965, 1145953, 1404486, 1408000, 1273413, 1798178, 1408032, 1532997, 1273445, 1408064, 1404518, 1798210, 1408096, 1533029, 1798242],
    [60, 7, 12, 490497, 619011, 1009667, 1010211, 750082, 490529, 1756162, 618531, 490561, 1756706, 1010243, 1714176, 749602, 1756738, 490593, 1714208, 1010275, 1714240, 618563, 1014784, 749634, 618595, 750178, 1436672, 1272324, 1014816, 1272356, 1567745, 1270788, 693252, 1272388, 1403397, 693284, 1270820, 1272420, 1403429, 1436704, 1014848, 1270852, 1534470, 693316, 1270884, 1567777, 1534502, 1436736, 693348, 954374, 1567809, 1403461, 1436768, 1014880, 1534534, 1567841, 1403493, 954406, 954438, 1534566, 954470, 1756258, 1714272],
    [56, 8, 16, 389120, 1550855, 1668103, 389152, 389184, 1419780, 839684, 389216, 724482, 1537542, 1044481, 2076165, 1257987, 1044513, 1419812, 724514, 1537574, 738305, 2076197, 738337, 1044545, 1668647, 1550375, 1044577, 1419844, 1668679, 724546, 811014, 1101829, 811046, 1537606, 738369, 839716, 1550407, 811078, 2076229, 724578, 738401, 1258019, 1101861, 1537638, 839748, 1668711, 811110, 1419876, 1550439, 1258051, 1101893, 1117190, 1117222, 839780, 1258083, 1117254, 1117286, 1102437, 2075749],
    [56, 10, 16, 345089, 450050, 450082, 1143299, 345121, 1143331, 1014279, 1143363, 345153, 1143395, 765952, 914433, 591879, 345185, 723464, 914465, 1783301, 450114, 1405444, 450146, 1405476, 765984, 1405508, 1144840, 1405540, 592423, 347136, 766016, 723496, 914497, 766048, 347168, 914529, 1013799, 1144872, 592455, 347200, 1013831, 1336838, 1145416, 723016, 347232, 1336870, 1014375, 591975, 1145448, 723048, 1783333, 1336902, 1336934, 1783365, 1783397, 2035209, 2035241, 2035273, 2035305],
    [36, 7, 15, 346113, 346145, 346177, 346209, 519168, 519200, 1406467, 519232, 519264, 590851, 650754, 1406499, 590883, 650786, 1406531, 650818, 590915, 650850, 1406563, 590947, 1993729, 1305092, 1799685, 1305124, 1799717, 1993761, 1993793, 1305156, 1799749, 1920518, 1799781, 1305188, 1920550, 1920582, 1993825, 1920614],
    [72, 11, 12, 1003520, 388097, 475651, 388129, 388161, 1005060, 1003552, 388193, 1003584, 475683, 1005092, 475715, 475747, 1174018, 1276421, 1174050, 1005124, 1174082, 1407494, 852997, 1174114, 869895, 1538055, 1876994, 1669640, 1005156, 1276453, 589830, 868360, 1877026, 1407526, 912384, 853029, 869927, 1538087, 589862, 912416, 868904, 1669160, 1276485, 1877058, 1003616, 853061, 1407558, 869959, 1538119, 589894, 868936, 1669192, 1788929, 1276517, 912448, 853093, 1407590, 2051593, 589926, 869991, 1538151, 1788961, 912480, 868968, 1669224, 1524234, 2051625, 1788993, 1877090, 1524266, 2051657, 1524298, 1789025, 1524330, 2051689],
    [40, 7, 12, 495616, 363520, 799745, 363552, 799777, 363584, 495648, 363616, 755713, 888322, 888354, 755745, 888386, 1148420, 495680, 669187, 1672710, 755777, 1148452, 1148484, 888418, 1148516, 669219, 755809, 495712, 669251, 1672742, 1280517, 1280549, 669283, 1672774, 1937410, 1937442, 1672806, 1280581, 799809, 1937474, 799841, 1280613, 1937506],
    [52, 8, 15, 1016322, 626689, 1016354, 391684, 538115, 1016386, 391716, 538147, 569344, 1016418, 391748, 569376, 569408, 391780, 1018881, 569440, 522757, 626721, 1018913, 522789, 538179, 1524736, 1278471, 522821, 538211, 1569794, 626753, 1018945, 522853, 668166, 1278503, 668198, 1524768, 1569826, 626785, 1018977, 668230, 888832, 1278535, 888864, 888896, 1424386, 1524800, 888928, 1569858, 1278567, 1424418, 668262, 1424450, 1524832, 1569890, 1424482],
    [48, 10, 16, 329728, 608257, 329760, 624130, 329792, 624162, 329824, 624194, 759808, 624226, 1412613, 608289, 759840, 755203, 608321, 755235, 1412645, 755267, 759872, 608353, 755299, 1690116, 759904, 1412677, 1803782, 1733637, 1934855, 1690148, 1412709, 1803814, 1733669, 1934887, 1690180, 1674761, 1543688, 1674793, 1803846, 1543720, 1934919, 1690212, 1543752, 1803878, 1674825, 1934951, 1543784, 1733701, 1674857, 1733733],
    [52, 9, 16, 366593, 410115, 366625, 410147, 366657, 410179, 366689, 410211, 461825, 344578, 890880, 461857, 344610, 461889, 344642, 890912, 461921, 344674, 1248256, 1262086, 1059846, 1248288, 1263108, 1248320, 890944, 1248352, 1584647, 1060390, 1560069, 1655815, 1261606, 890976, 1263140, 1560101, 1584679, 1060422, 1655847, 1261638, 1560133, 1263172, 1584711, 1935880, 1935912, 1060454, 1560165, 1655879, 1261670, 1935944, 1263204, 1935976, 1584743, 1655911],
    [48, 8, 16, 462848, 367616, 367648, 593921, 367680, 367712, 1283589, 406019, 1076229, 497665, 462880, 537092, 497697, 406051, 593953, 497729, 497761, 462912, 537124, 593985, 1810432, 1541639, 406083, 462944, 1076773, 1283109, 1810464, 594017, 1810496, 1283653, 537156, 1541671, 1076293, 920066, 406115, 1283685, 1541703, 1545734, 537188, 1545766, 1076325, 920098, 1545798, 1541735, 1545830, 920130, 920162, 1810528],
    [60, 9, 16, 499713, 499745, 551428, 499777, 551460, 499809, 892928, 413187, 892960, 413219, 1546758, 413251, 892992, 413283, 1809409, 1282565, 478214, 1546790, 478246, 893024, 1809441, 1282597, 551492, 1809473, 1136130, 1136162, 1282629, 551524, 1136194, 1001991, 1051650, 1002023, 1282661, 1051682, 1002055, 1051714, 478790, 1052258, 1002087, 1774593, 1135714, 478822, 1219584, 2050053, 1546310, 1774625, 1219616, 2069000, 2050085, 2069032, 1774657, 1219648, 1774689, 2069064, 2050117, 1546342, 2069096, 1809505, 2050149, 1219680],
    [48, 8, 16, 501760, 501792, 628226, 501824, 628258, 501856, 943621, 1285635, 761857, 1416710, 694272, 1285667, 1074182, 1285699, 761889, 943653, 1416742, 1285731, 761921, 1074214, 761953, 1462791, 628290, 943685, 1416774, 694304, 628322, 1021444, 1021476, 1416806, 1021508, 694336, 1021540, 1074246, 1414149, 694368, 1414181, 1414213, 943717, 1414245, 1462823, 1431559, 1074278, 1431591, 1462855, 1431623, 1432167, 1462375],
    [52, 9, 16, 302081, 1724932, 1594885, 302113, 726531, 302145, 1724964, 726563, 632833, 302177, 1563653, 1594917, 632865, 632897, 726595, 826368, 632929, 1153543, 726627, 763904, 826400, 1153575, 1153607, 1153639, 763936, 826432, 763968, 764000, 826464, 1903623, 1089030, 1089062, 1903655, 2019842, 1808904, 1089094, 1808936, 1563685, 2019874, 1724996, 1903687, 1808968, 1089126, 1564229, 1594437, 1809000, 2019906, 1725028, 1564261, 1594469, 1903719, 2019938],
    [48, 8, 16, 1026049, 696321, 994823, 634880, 434691, 499204, 434723, 499236, 434755, 892418, 634912, 434787, 499268, 1418758, 499300, 1287685, 1418790, 634944, 1287717, 892450, 1418822, 994855, 1287749, 1287781, 892482, 1418854, 711685, 892514, 634976, 994887, 711717, 711749, 696353, 1026081, 696385, 1912838, 711781, 1913861, 994919, 1026113, 696417, 1912870, 1913893, 1026145, 1912902, 1913925, 1912934, 1913957],
    [44, 9, 16, 635904, 766977, 635936, 767009, 895490, 1256966, 471555, 635968, 471587, 471619, 1256998, 471651, 767041, 636000, 1158145, 767073, 895522, 1596933, 1155591, 1158177, 1286664, 895554, 1257030, 1155623, 1596965, 1286696, 1155655, 1596997, 1257062, 1286728, 1155687, 1158209, 1286760, 895586, 2008065, 1597029, 2008097, 1158241, 1812996, 2008129, 1813028, 1813060, 1813092, 2008161],
    [44, 8, 16, 636928, 272384, 503809, 518658, 272416, 1420807, 518690, 636960, 272448, 518722, 272480, 286722, 518754, 501251, 636992, 2061319, 286754, 501283, 501315, 286786, 501347, 637024, 503841, 286818, 503873, 503905, 1289733, 1549828, 1549860, 1549892, 1289765, 1420839, 1289797, 1549924, 1289829, 2061351, 1420871, 1744390, 1420903, 2061383, 1744422, 1744454, 1744486, 2061415],
    [60, 9, 16, 899073, 899105, 1288711, 1930247, 899137, 797696, 928769, 899169, 1729029, 1713670, 637952, 1860098, 1157635, 1698822, 1860614, 637984, 797728, 1157667, 1991172, 638016, 928801, 1729061, 1288743, 1713702, 638048, 1992200, 1157699, 1860130, 1288775, 1157731, 1930279, 797760, 1731585, 1860646, 1991204, 928833, 1713734, 797792, 1992232, 1729093, 1698854, 1860162, 1288807, 1731617, 928865, 1930311, 1698886, 1860678, 1731649, 1991236, 1699430, 1992264, 1731681, 1729125, 1860194, 1713254, 1930343, 1860710, 1991268, 1992296],
    [68, 7, 12, 1060864, 1031168, 1160707, 1293313, 634372, 1323009, 1031200, 1422853, 1293345, 1029634, 634404, 1029666, 1060896, 855044, 1029698, 622593, 1323041, 1553926, 1160739, 1029730, 1422885, 1160771, 1553958, 1060928, 622625, 1553990, 1031232, 609283, 622657, 1160803, 1422917, 855076, 1323073, 622689, 1730565, 1422949, 1220612, 1554022, 1409024, 609315, 1293377, 1060960, 634436, 855108, 609347, 634468, 1992707, 1323105, 1220644, 609379, 1220676, 1730597, 1220708, 1031264, 855140, 1409056, 1992739, 1730629, 1904644, 1409088, 1992771, 1730661, 1904676, 1409120, 1293409, 1904708, 1992803, 1904740],
    [60, 7, 12, 361472, 1028610, 1191936, 361504, 1159683, 361536, 1028642, 1290756, 361568, 1555457, 1061889, 1159715, 1028674, 739331, 1421829, 1159747, 1028706, 460802, 1159779, 739363, 1290788, 1421861, 739395, 1191968, 986116, 1290820, 739427, 1274885, 1061921, 460834, 1421893, 1555489, 1192000, 986148, 1290852, 1061953, 1421925, 460866, 1863174, 1192032, 986180, 1274917, 460898, 1061985, 1555521, 1863206, 1540097, 986212, 1540129, 1863238, 1274949, 2035717, 1274981, 1540161, 1863270, 2035749, 1540193, 1555553, 2035781, 2035813],
    [48, 10, 15, 362496, 392193, 651780, 362528, 392225, 362560, 521734, 392257, 651812, 362592, 392289, 521766, 372740, 372772, 651844, 535042, 372804, 1291270, 521798, 373348, 651364, 1291302, 521830, 887299, 535074, 1616391, 1291334, 535106, 1291366, 1878537, 535138, 740869, 887331, 887363, 1453576, 740901, 1616423, 887395, 1453608, 740933, 1453640, 740965, 1878569, 1453672, 1616455, 1878601, 1616487, 1878633],
    [68, 12, 12, 783360, 1686025, 1192961, 783392, 493569, 783424, 1686057, 493601, 493633, 493665, 1554950, 1192993, 1307140, 1423364, 783456, 1018370, 1307172, 1423396, 1321990, 1307204, 1423428, 1018402, 1554982, 1307236, 1193025, 2010632, 1423460, 1831431, 1686089, 1018434, 1322022, 1700873, 1832459, 1018466, 1879557, 1831463, 1148928, 1322566, 1554502, 1700905, 1150467, 1879589, 1148960, 1817098, 1832491, 1150499, 1831495, 1148992, 1193057, 1700937, 1150531, 1817130, 1149024, 1832523, 1555046, 1322086, 1831527, 1150563, 1817162, 2010664, 1879621, 1701481, 1685609, 1817194, 1832555, 2010696, 1879653, 2010728],
    [40, 7, 9, 508928, 640001, 508960, 640033, 508992, 640065, 509024, 640097, 771587, 641024, 902661, 277505, 641056, 277537, 771619, 277569, 641088, 277601, 641120, 1194498, 1325059, 771651, 902693, 1064452, 1194530, 771683, 902725, 1033734, 1325091, 1033766, 1064484, 902757, 1194562, 1033798, 1325123, 1064516, 1194594, 1033830, 1325155, 1064548],
    [12, 3, 12, 378881, 378913, 378945, 378977, 772096, 772128, 1032706, 772160, 1032738, 1032770, 772192, 1032802],
    [64, 8, 14, 380928, 551936, 1035264, 1166337, 1035296, 1166369, 1035328, 1166401, 1035360, 1166433, 1263616, 380960, 493058, 380992, 493090, 381024, 493122, 770563, 493154, 687105, 492036, 551968, 886277, 1297413, 1263648, 492068, 552000, 886309, 1297445, 492100, 552032, 886341, 1297477, 492132, 1804289, 687137, 886373, 1297509, 687169, 1146883, 770595, 1263680, 687201, 1080839, 1410566, 1080871, 1146915, 770627, 1263712, 1804321, 1410598, 1146947, 1080903, 1804353, 1410630, 1147491, 1080935, 770147, 1410662, 1804385, 1295366, 1295398, 1295430, 1295462],
    [52, 7, 14, 1296900, 683009, 1919493, 1002496, 1133569, 541186, 905216, 683041, 1165827, 541218, 541250, 1002528, 683073, 1165859, 1673220, 1133601, 541282, 683105, 1396230, 1919525, 1936385, 1296932, 1278979, 1165891, 1673252, 1002560, 905248, 1133633, 1296964, 1279011, 1396262, 1165923, 1207296, 1002592, 1936417, 1673284, 1133665, 1279043, 1296996, 1207328, 905280, 1919557, 1936449, 1279075, 1396294, 1207360, 905312, 1673316, 1919589, 1207392, 1396326, 1936481],
    [40, 7, 14, 348160, 1168384, 1299457, 1168416, 1299489, 1168448, 1299521, 1168480, 1299553, 1542659, 348192, 1281540, 348224, 1411586, 1542691, 1806853, 348256, 1431046, 776192, 1281572, 479233, 1411618, 479265, 1806885, 479297, 1411650, 479329, 1411682, 1542723, 1281604, 776224, 1542755, 1281636, 1431078, 776256, 776288, 1806917, 1431110, 1431142, 1806949],
    [44, 8, 14, 382976, 1298949, 383008, 480257, 383040, 383072, 480289, 1807874, 1527300, 1167364, 480321, 1167908, 480353, 1298981, 1938947, 1807906, 1167940, 907265, 1167972, 1789957, 1938979, 1526820, 1807938, 1659398, 907297, 1791495, 1659430, 907329, 1789989, 1299013, 1299045, 1791527, 907361, 1526852, 1659462, 1790021, 1939011, 1791559, 1659494, 1807970, 1790053, 1791591, 1526884, 1939043],
    [44, 5, 14, 385024, 1039360, 1170433, 1039392, 1170465, 1039424, 1170497, 1039456, 1170529, 1302018, 595969, 857090, 1302050, 1302082, 385056, 1302114, 596001, 385088, 857122, 596033, 385120, 596065, 857154, 906755, 842752, 1037828, 906787, 857186, 842784, 1037860, 1642499, 906819, 2036740, 1642531, 1037892, 906851, 2036772, 1037924, 1642563, 842816, 842848, 2036804, 1642595, 2036836],
    [40, 7, 14, 516097, 448512, 516129, 448544, 448576, 516161, 448608, 516193, 1038853, 1678850, 1906182, 1169414, 1579523, 1038885, 1565188, 1906214, 1169446, 1678882, 1038917, 1579555, 1906246, 1169478, 1678914, 2037765, 1038949, 1565220, 1498113, 1170022, 1579587, 1498145, 1678946, 1905766, 1579619, 1565252, 1498177, 2037797, 1498209, 2037829, 1565284, 2037861],
    [60, 6, 14, 1041408, 1172481, 1041440, 1172513, 1041472, 1172545, 1041504, 1172577, 604160, 450561, 604192, 604224, 450593, 604256, 450625, 866818, 450657, 1942020, 712704, 712736, 712768, 736771, 866850, 1566720, 712800, 980994, 1630210, 1566752, 736803, 866882, 1761283, 1566784, 736835, 866914, 982019, 1304069, 1566816, 736867, 1942052, 1304101, 1630242, 981026, 1761315, 1914885, 982051, 1942084, 1304133, 1630274, 981058, 1761347, 1914917, 982083, 981090, 1304165, 982115, 1942116, 1630306, 1914949, 1761379, 1914981],
    [32, 7, 14, 387072, 320513, 387104, 320545, 387136, 320577, 387168, 320609, 763396, 911361, 911393, 911425, 763428, 909826, 763460, 909858, 2074115, 909890, 909922, 911457, 1040902, 1040934, 763492, 1500677, 1500709, 1040966, 2074147, 1500741, 2074179, 1040998, 1500773, 2074211],
    [60, 10, 14, 944128, 1043456, 1174529, 1043488, 1174561, 1043520, 1174593, 1043552, 1174625, 1306114, 621569, 489987, 1306146, 490019, 1306178, 1306210, 913408, 621601, 490051, 566274, 566306, 913440, 621633, 490083, 944160, 913472, 621665, 566338, 884231, 566370, 944192, 913504, 779784, 779816, 884263, 1451524, 779848, 779880, 1582087, 944224, 1566217, 884295, 1321477, 1451556, 1566249, 1582119, 884327, 1321509, 1451588, 1566281, 1582151, 1451620, 1321541, 1582183, 1321573, 1539590, 1566313, 1539622, 1539654, 1539686],
    [48, 7, 14, 520192, 290306, 520224, 290338, 520256, 290370, 520288, 290402, 682499, 782339, 1469440, 1175553, 782883, 1600513, 682019, 1436164, 1175585, 1436196, 782915, 1469472, 1436228, 1600545, 1436260, 682051, 1175617, 782947, 959492, 1469504, 959524, 1600577, 1175649, 682083, 959556, 1829382, 959588, 1829414, 1469536, 1746950, 1583621, 1600609, 1746982, 1829446, 1583653, 1829478, 1747014, 1583685, 1583717, 1747046],
    [84, 11, 14, 421888, 1176576, 1307649, 1176608, 1307681, 1176640, 1307713, 1176672, 1307745, 505346, 374786, 1439235, 505378, 374818, 1439267, 421920, 505410, 374850, 1439299, 505442, 374882, 1439331, 421952, 870916, 768003, 741893, 768035, 421984, 870948, 768067, 741925, 768099, 684033, 1030149, 870980, 684065, 900615, 684097, 871012, 684129, 741957, 1292806, 1162760, 1030181, 737801, 741989, 900647, 882694, 737833, 872970, 1292838, 873002, 1276936, 1162792, 1030213, 873034, 900679, 873066, 737865, 882726, 1292870, 1177600, 1162824, 1030245, 1921030, 1276968, 900711, 737897, 882758, 2052104, 1277000, 1921062, 883302, 1292390, 1277544, 1162344, 1177632, 1177664, 2052136, 1921094, 1177696, 2052168, 1921126, 2052200],
    [48, 8, 14, 523264, 1700357, 422913, 1569282, 1569314, 476675, 422945, 1569346, 1569378, 422977, 1700389, 523296, 476707, 423009, 1700421, 523328, 476739, 523360, 1161734, 898054, 815620, 898598, 815652, 476771, 898630, 815684, 1700453, 815716, 1161254, 898662, 1863685, 654337, 654369, 654401, 1161286, 1865223, 654433, 1863717, 1865255, 1161318, 1863749, 1865287, 1947650, 1947682, 1863781, 1865319, 1947714, 1947746],
    [28, 4, 9, 785408, 916481, 785440, 916513, 785472, 916545, 785504, 916577, 376832, 507905, 376864, 507937, 376896, 652802, 652834, 1048067, 652866, 1048099, 652898, 1048131, 507969, 376928, 1048163, 508001, 1045507, 1045539, 1045571, 1045603],
    [44, 5, 8, 1456128, 653312, 653344, 653376, 653408, 784898, 915971, 784930, 784962, 638977, 784994, 1455106, 1586179, 639009, 916003, 916035, 1016834, 884739, 916067, 639041, 1016866, 884771, 1455138, 1047044, 639073, 1016898, 901120, 1586211, 1047076, 884803, 1047108, 1455170, 901152, 1016930, 1047140, 884835, 1586243, 901184, 1455202, 1586275, 901216, 1456160, 1456192, 1456224],
]
ROLES = [
    [0, 0, 5, 1, 6, 6, 7, 4, 0, 0, 1, 5, 2, 3],
    [0, 4, 6, 5, 2, 7, 8, 3, 1, 1, 7, 2, 3, 8],
    [0, 5, 8, 10, 9, 6, 4, 7, 11, 11, 13, 12, 2, 3],
    [0, 3, 5, 6, 10, 12, 8, 2, 11, 11, 9, 7, 4, 13],
    [0, 2, 10, 13, 11, 5, 3, 9, 6, 6, 8, 7, 4, 12],
    [0, 8, 10, 6, 9, 13, 11, 5, 7, 7, 4, 3, 2, 12],
    [0, 4, 8, 10, 9, 6, 5, 3, 13, 13, 12, 11, 2, 7],
    [0, 5, 3, 10, 7, 6, 2, 9, 12, 12, 8, 13, 11, 4],
    [0, 2, 7, 10, 8, 5, 4, 6, 3, 3, 11, 9, 13, 12],
    [0, 6, 2, 4, 7, 9, 8, 5, 10, 10, 12, 11, 3, 13],
    [0, 11, 7, 9, 8, 6, 5, 3, 10, 10, 12, 13, 2, 4],
    [0, 2, 8, 13, 5, 4, 3, 12, 9, 9, 6, 10, 7, 11],
    [0, 3, 6, 11, 7, 4, 2, 5, 8, 8, 10, 9, 13, 12],
    [0, 6, 2, 5, 7, 10, 3, 4, 8, 8, 12, 11, 13, 9],
    [0, 8, 4, 6, 5, 7, 3, 2, 9, 9, 10, 11, 0, 8],
    [0, 2, 3, 3, 6, 5, 7, 7, 8, 8, 0, 2, 1, 4],
    [5, 5, 11, 9, 4, 4, 10, 2, 0, 6, 1, 3, 8, 7],
    [9, 12, 3, 7, 6, 10, 4, 5, 1, 2, 14, 13, 8, 11],
    [11, 2, 10, 7, 9, 6, 4, 5, 2, 11, 7, 10, 8, 3],
    [6, 3, 8, 2, 9, 11, 7, 4, 10, 5, 11, 9, 4, 7],
    [8, 5, 9, 10, 2, 7, 6, 12, 3, 11, 4, 13, 15, 14],
    [5, 7, 4, 10, 9, 8, 3, 6, 2, 12, 11, 13, 15, 14],
    [9, 6, 7, 13, 10, 3, 4, 8, 15, 14, 5, 2, 11, 12],
    [3, 8, 2, 7, 9, 4, 10, 5, 12, 6, 13, 15, 14, 11],
    [10, 12, 7, 8, 11, 5, 3, 9, 4, 2, 6, 13, 15, 14],
    [5, 6, 3, 7, 9, 8, 4, 11, 2, 14, 13, 12, 15, 10],
    [12, 14, 6, 8, 2, 4, 3, 11, 10, 9, 15, 13, 7, 5],
    [7, 8, 3, 4, 10, 9, 6, 5, 13, 14, 11, 15, 12, 2],
    [2, 8, 11, 15, 4, 10, 9, 7, 3, 6, 5, 14, 12, 13],
    [12, 6, 5, 11, 9, 8, 2, 4, 3, 14, 10, 13, 7, 15],
    [13, 14, 8, 6, 3, 12, 10, 7, 2, 9, 5, 11, 0, 4],
    [8, 6, 2, 2, 9, 7, 11, 11, 4, 10, 0, 5, 1, 3],
    [5, 5, 7, 3, 6, 6, 8, 4, 0, 10, 1, 2, 11, 9],
    [9, 11, 5, 3, 10, 12, 6, 4, 1, 14, 8, 13, 2, 7],
    [4, 6, 10, 11, 5, 9, 7, 12, 2, 13, 14, 15, 3, 8],
    [3, 4, 7, 9, 13, 6, 8, 10, 14, 2, 11, 15, 12, 5],
    [3, 2, 9, 11, 8, 4, 6, 7, 2, 3, 11, 9, 10, 5],
    [3, 6, 8, 4, 10, 11, 9, 5, 7, 2, 11, 10, 5, 9],
    [4, 13, 9, 8, 6, 15, 2, 11, 3, 10, 14, 7, 5, 12],
    [7, 5, 8, 12, 11, 9, 10, 3, 15, 4, 6, 14, 2, 13],
    [14, 7, 8, 12, 2, 3, 4, 13, 9, 10, 5, 11, 15, 6],
    [3, 10, 5, 8, 12, 11, 6, 9, 15, 13, 4, 7, 2, 14],
    [2, 7, 6, 10, 3, 8, 5, 4, 14, 12, 15, 13, 11, 9],
    [10, 4, 12, 5, 9, 8, 13, 6, 15, 14, 3, 11, 2, 7],
    [15, 10, 6, 12, 2, 14, 7, 13, 8, 9, 3, 4, 11, 5],
    [13, 5, 11, 8, 14, 6, 12, 3, 7, 10, 2, 15, 9, 4],
    [3, 2, 6, 10, 4, 7, 9, 8, 11, 13, 12, 14, 0, 5],
    [2, 6, 10, 10, 4, 3, 11, 11, 7, 9, 0, 8, 1, 5],
    [5, 5, 8, 3, 6, 6, 7, 4, 0, 9, 1, 2, 11, 10],
    [4, 6, 2, 13, 3, 7, 11, 14, 1, 8, 12, 10, 9, 5],
    [5, 8, 11, 10, 7, 9, 2, 12, 3, 15, 4, 13, 6, 14],
    [6, 5, 10, 3, 9, 8, 12, 13, 2, 14, 4, 15, 11, 7],
    [6, 4, 9, 12, 3, 8, 7, 11, 2, 14, 10, 5, 15, 13],
    [4, 8, 7, 5, 13, 6, 11, 3, 10, 12, 14, 9, 2, 15],
    [11, 9, 6, 8, 7, 2, 5, 3, 9, 11, 8, 6, 10, 4],
    [2, 5, 9, 6, 10, 8, 4, 11, 7, 3, 8, 10, 11, 4],
    [4, 12, 6, 11, 14, 13, 10, 9, 5, 15, 3, 2, 8, 7],
    [10, 8, 3, 6, 13, 12, 7, 5, 2, 11, 4, 15, 14, 9],
    [4, 10, 9, 12, 11, 7, 2, 13, 3, 8, 5, 15, 14, 6],
    [9, 3, 14, 12, 8, 7, 4, 13, 2, 11, 5, 10, 6, 15],
    [15, 3, 4, 10, 7, 11, 2, 8, 5, 12, 6, 14, 9, 13],
    [12, 4, 5, 8, 7, 3, 13, 11, 2, 14, 9, 15, 10, 6],
    [14, 3, 10, 8, 5, 4, 13, 12, 6, 9, 2, 11, 0, 7],
    [3, 2, 10, 10, 5, 4, 11, 11, 6, 8, 0, 9, 1, 7],
    [10, 10, 6, 2, 11, 11, 8, 4, 0, 3, 1, 9, 7, 5],
    [5, 8, 4, 12, 6, 11, 2, 13, 1, 7, 3, 14, 10, 9],
    [13, 4, 6, 11, 15, 5, 3, 8, 9, 12, 10, 14, 2, 7],
    [2, 8, 5, 6, 10, 7, 4, 15, 12, 13, 9, 14, 3, 11],
    [11, 14, 8, 10, 2, 15, 7, 9, 3, 13, 4, 5, 6, 12],
    [3, 9, 2, 11, 12, 7, 10, 4, 13, 5, 6, 14, 8, 15],
    [2, 8, 10, 11, 7, 9, 5, 6, 14, 13, 4, 15, 3, 12],
    [9, 6, 13, 5, 7, 8, 2, 11, 15, 14, 10, 4, 3, 12],
    [2, 3, 8, 11, 10, 6, 7, 5, 3, 2, 11, 8, 9, 4],
    [2, 6, 8, 3, 11, 10, 5, 7, 9, 4, 10, 11, 7, 5],
    [10, 3, 5, 9, 13, 2, 6, 8, 12, 15, 7, 11, 4, 14],
    [10, 6, 4, 7, 11, 5, 3, 9, 13, 15, 12, 2, 8, 14],
    [12, 11, 2, 6, 15, 13, 5, 10, 7, 4, 8, 14, 9, 3],
    [11, 4, 7, 6, 12, 10, 9, 8, 3, 15, 5, 14, 2, 13],
    [3, 11, 7, 10, 5, 12, 8, 9, 13, 6, 2, 14, 0, 4],
    [3, 7, 8, 8, 4, 6, 9, 9, 2, 5, 0, 10, 1, 11],
    [11, 11, 10, 6, 3, 3, 8, 5, 0, 4, 1, 7, 2, 9],
    [6, 10, 8, 13, 5, 7, 2, 3, 1, 4, 11, 14, 12, 9],
    [5, 6, 11, 12, 8, 10, 2, 13, 3, 7, 4, 15, 9, 14],
    [2, 4, 9, 14, 6, 5, 13, 15, 12, 3, 7, 11, 8, 10],
    [5, 14, 7, 9, 6, 15, 8, 4, 2, 12, 3, 13, 10, 11],
    [10, 7, 2, 5, 11, 9, 4, 6, 3, 13, 14, 15, 8, 12],
    [8, 3, 7, 10, 9, 5, 2, 11, 12, 13, 4, 6, 15, 14],
    [8, 5, 15, 3, 7, 6, 2, 11, 9, 10, 4, 12, 13, 14],
    [9, 7, 4, 12, 10, 8, 6, 13, 2, 11, 3, 5, 14, 15],
    [8, 6, 2, 5, 10, 7, 9, 11, 4, 14, 12, 15, 13, 3],
    [8, 4, 11, 10, 9, 5, 3, 6, 4, 8, 10, 11, 7, 2],
    [6, 5, 7, 3, 8, 10, 2, 11, 9, 4, 10, 8, 11, 2],
    [13, 4, 7, 10, 5, 11, 6, 8, 3, 14, 9, 12, 2, 15],
    [12, 4, 7, 10, 11, 3, 8, 13, 2, 5, 14, 15, 6, 9],
    [7, 3, 10, 9, 8, 5, 12, 11, 4, 14, 2, 13, 0, 6],
    [6, 5, 10, 10, 8, 7, 3, 3, 2, 11, 0, 4, 1, 9],
    [10, 10, 7, 4, 11, 11, 9, 6, 0, 2, 1, 5, 3, 8],
    [2, 8, 4, 13, 7, 12, 5, 14, 1, 11, 6, 9, 3, 10],
    [2, 6, 8, 14, 3, 7, 5, 9, 10, 11, 13, 12, 4, 15],
    [11, 8, 2, 6, 10, 12, 7, 4, 14, 9, 3, 13, 5, 15],
    [3, 14, 6, 15, 4, 7, 5, 9, 8, 12, 11, 2, 10, 13],
    [11, 8, 10, 7, 9, 5, 4, 6, 2, 12, 15, 3, 13, 14],
    [5, 4, 6, 8, 2, 11, 3, 13, 10, 12, 14, 15, 7, 9],
    [10, 7, 2, 6, 9, 8, 13, 3, 11, 14, 4, 15, 5, 12],
    [13, 2, 6, 8, 3, 4, 5, 9, 7, 11, 10, 12, 14, 15],
    [10, 7, 3, 4, 9, 8, 11, 2, 6, 13, 12, 14, 15, 5],
    [3, 13, 5, 8, 4, 6, 7, 9, 10, 15, 14, 11, 2, 12],
    [9, 3, 4, 2, 10, 7, 8, 11, 14, 15, 5, 12, 6, 13],
    [4, 11, 9, 7, 10, 6, 3, 5, 11, 4, 7, 9, 8, 2],
    [4, 2, 7, 3, 8, 10, 9, 6, 11, 5, 10, 8, 6, 9],
    [4, 2, 10, 11, 6, 8, 12, 13, 7, 9, 14, 5, 0, 3],
    [4, 6, 7, 7, 9, 10, 11, 11, 5, 8, 0, 3, 1, 2],
    [2, 2, 6, 3, 4, 4, 1, 7, 0, 5, 1, 7, 8, 8],
    [7, 5, 3, 6, 4, 2, 1, 9, 1, 9, 8, 10, 11, 11],
    [4, 3, 5, 8, 2, 6, 1, 9, 12, 13, 11, 7, 10, 10],
    [9, 3, 7, 5, 8, 4, 1, 6, 11, 12, 10, 13, 2, 2],
    [2, 3, 6, 8, 12, 4, 1, 9, 7, 5, 10, 11, 13, 13],
    [10, 4, 8, 6, 9, 5, 1, 7, 2, 3, 11, 12, 13, 13],
    [5, 3, 2, 8, 6, 4, 1, 7, 10, 11, 9, 12, 13, 13],
    [9, 6, 7, 10, 8, 5, 1, 4, 11, 2, 12, 3, 13, 13],
    [2, 8, 5, 6, 3, 11, 1, 7, 4, 9, 13, 12, 10, 10],
    [9, 2, 7, 11, 8, 6, 1, 5, 3, 4, 10, 13, 12, 12],
    [11, 9, 2, 10, 6, 8, 1, 13, 3, 12, 4, 7, 5, 5],
    [9, 4, 7, 3, 8, 6, 1, 2, 12, 13, 10, 5, 11, 11],
    [6, 5, 3, 11, 8, 10, 1, 12, 2, 4, 7, 9, 13, 13],
    [10, 2, 8, 4, 9, 5, 1, 7, 6, 3, 11, 12, 13, 13],
    [8, 2, 6, 5, 7, 3, 1, 4, 2, 8, 5, 6, 0, 0],
    [3, 2, 5, 5, 6, 0, 1, 1, 7, 4, 0, 6, 1, 1],
]


def fill_table(tbl, me, lo, hi):
    if hi - lo == 1:
        head = SENDS[lo]
        for place, word in enumerate(head):
            tbl[place] = jnp.int32(word)
        return
    mid = (lo + hi) // 2
    lax.cond(
        me < mid,
        lambda: fill_table(tbl, me, lo, mid),
        lambda: fill_table(tbl, me, mid, hi),
    )


def spread_kernel(stored_ref, slots_ref, tbl, own_sem, send_sem, recv_sem):
    rows_per = stored_ref.shape[2] // CHUNKS
    row_count = lax.axis_size("row")
    me = lax.axis_index("col") * row_count + lax.axis_index("row")
    fill_table(tbl, me, 0, len(SENDS))
    own = [
        pltpu.make_async_copy(stored_ref.at[lane, 0], slots_ref.at[lane], own_sem.at[lane])
        for lane in range(2)
    ]
    for copy in own:
        copy.start()

    def hop(source, target, slot, chunk, place):
        return pltpu.make_async_remote_copy(
            src_ref=source,
            dst_ref=slots_ref.at[slot, pl.ds(chunk * rows_per, rows_per)],
            send_sem=send_sem.at[place],
            recv_sem=recv_sem.at[slot, chunk],
            device_id={"col": target // row_count, "row": lax.rem(target, row_count)},
            device_id_type=MESH,
        )

    def arrival(slot, chunk):
        piece = slots_ref.at[slot, pl.ds(chunk * rows_per, rows_per)]
        hop(piece, me, slot, chunk, 0).wait_recv()

    sends = tbl[0]

    @pl.loop(0, sends)
    def _(place):
        word = tbl[3 + place]
        slot = word & 31
        chunk = (word >> 5) & 15
        target = (word >> 10) & 127
        landing = word >> 17

        @pl.when(((word >> 9) & 1) == 1)
        def _():
            arrival(slot, chunk)

        @pl.when(slot < 2)
        def _():
            piece = stored_ref.at[slot, 0, pl.ds(chunk * rows_per, rows_per)]
            hop(piece, target, landing, chunk, place).start()

        @pl.when(slot >= 2)
        def _():
            piece = slots_ref.at[slot, pl.ds(chunk * rows_per, rows_per)]
            hop(piece, target, landing, chunk, place).start()

    @pl.loop(tbl[1], tbl[2])
    def _(slot):
        for chunk in range(CHUNKS):
            arrival(slot, chunk)

    @pl.loop(0, sends)
    def _(place):
        piece = slots_ref.at[0, pl.ds(0, rows_per)]
        hop(piece, me, 0, 0, place).wait_send()

    for copy in own:
        copy.wait()


def spread(stored):
    return pl.pallas_call(
        spread_kernel,
        out_shape=jax.ShapeDtypeStruct((SLOTS,) + stored.shape[2:], jnp.float32),
        in_specs=[pl.BlockSpec(memory_space=pl.ANY)],
        out_specs=pl.BlockSpec(memory_space=pl.ANY),
        scratch_shapes=[
            pltpu.SMEM((max(len(entry) for entry in SENDS),), jnp.int32),
            pltpu.SemaphoreType.DMA((2,)),
            pltpu.SemaphoreType.DMA((max(entry[0] for entry in SENDS),)),
            pltpu.SemaphoreType.DMA((SLOTS, CHUNKS)),
        ],
        compiler_params=pltpu.CompilerParams(has_side_effects=True),
        name="spread",
    )(stored)


def rank_in(row_list, lookup_keys):
    positions = jnp.arange(row_list.shape[0], dtype=jnp.int32)
    matches = row_list == lookup_keys[..., None]
    return jnp.sum(jnp.where(matches, positions, 0), -1)


def tile_cols(tile_rows, offsets, tile_x, tile_y):
    offsets_both = jnp.concatenate([offsets[tile_x, tile_y], offsets[tile_y, tile_x]])
    return jnp.bitwise_xor(tile_rows[tile_x][:, None], offsets_both[None, :])


def assemble(own_half, mirror, tile_rows, offsets, tile_x, tile_y):
    half_slots = own_half.shape[1]
    mirror_rows = jnp.bitwise_xor(tile_rows[tile_x][:, None], offsets[tile_y, tile_x][None, :])
    position = rank_in(tile_rows[tile_y], mirror_rows)
    picked = mirror[position, jnp.arange(half_slots, dtype=jnp.int32)[None, :]]
    return jnp.concatenate([own_half, jnp.swapaxes(picked, -1, -2)], 1)


def lane_terms(vals_a, vals_b, cols_a, cols_b, rows_i, rows_k, want_rows, want_cols, live_count):
    kept_slots = want_rows.shape[0]
    block_size = vals_a.shape[-1]
    is_live = jnp.arange(kept_slots, dtype=jnp.int32) < live_count
    position = rank_in(rows_k, cols_a)
    summed = jnp.zeros((kept_slots, block_size * block_size), jnp.float32)
    for slot in range(vals_a.shape[1]):
        picked = vals_b[position[:, slot]]
        picked_cols = cols_b[position[:, slot]]
        products = jnp.einsum(
            "eij,ebjk->ebik", vals_a[:, slot], picked, precision=lax.Precision.HIGHEST
        )
        weights = (
            (rows_i[None, :, None] == want_rows[:, None, None])
            & (picked_cols[None] == want_cols[:, None, None])
            & is_live[:, None, None]
        ).astype(jnp.float32)
        summed = summed + jnp.dot(
            weights.reshape(kept_slots, -1),
            products.reshape(-1, block_size * block_size),
            precision=lax.Precision.HIGHEST,
        )
    return summed.reshape(kept_slots, block_size, block_size)


def local(stored, tile_rows, offsets, kept_rows, kept_cols, kept_count):
    grid_size = lax.axis_size("row")
    row_id = lax.axis_index("row")
    col_id = lax.axis_index("col")
    me = col_id * grid_size + row_id
    lane_count = stored.shape[0]
    slots = spread(stored)
    roles = jnp.asarray(np.array(ROLES, np.int32))[me]
    results = []
    for lane in range(lane_count):
        tile_i = col_id * lane_count + lane
        summed = jnp.zeros((kept_rows.shape[-1],) + stored.shape[-2:], jnp.float32)
        for step in range(2):
            tile_k = (tile_i + row_id + step) % grid_size
            left = 2 * (2 * lane + step)
            right = 8 + 2 * (lane + step)
            vals_a = assemble(slots[roles[left]], slots[roles[left + 1]], tile_rows, offsets, tile_i, tile_k)
            vals_b = assemble(slots[roles[right]], slots[roles[right + 1]], tile_rows, offsets, tile_k, row_id)
            summed = summed + lane_terms(
                vals_a, vals_b,
                tile_cols(tile_rows, offsets, tile_i, tile_k),
                tile_cols(tile_rows, offsets, tile_k, row_id),
                tile_rows[tile_i], tile_rows[tile_k],
                kept_rows[lane, 0], kept_cols[lane, 0], kept_count[lane, 0],
            )
        results.append(summed)
    return jnp.stack(results)[:, None]


def solution(mesh):
    in_specs = (
        P("col", "row", None, None, None, None),
        P(),
        P(),
        P("col", "row", None),
        P("col", "row", None),
        P("col", "row"),
    )
    out_specs = P("col", "row", None, None, None)
    return jax.shard_map(local, mesh=mesh, in_specs=in_specs, out_specs=out_specs, check_vma=False)
```

time: 771 us -> 587 us (0.76)
  waiting for transfers between devices: 337 us -> 0 us
  Pallas kernels: 0 us -> 199 us
  blocking collectives: 63.6 us -> 0 us
  starting transfers between devices: 28.2 us -> 0 us
  matrix products: 146 us -> 172 us
  local copies, waits for them, and re-layouts: 140 us -> 162 us
  between operations: 6.18 us -> 27.3 us
  other arithmetic: 36.6 us -> 16.6 us
    ppermute x5 -> x0, waiting for transfers between devices: 273 us -> none  [from_behind(): return lax.ppermute(value, axis, pairs)]
    pallas_call x0 -> x1, Pallas kernels: none -> 199 us  [spread(): pl.pallas_call(spread_kernel, out_shape=jax.ShapeDtypeStruct((SLOTS,) + s...]
    all_to_all x3 -> x0, waiting for transfers between devices: 64.1 us -> none  [the longest x1 43.9 us: local(): lax.all_to_all(spread, 'row', split_axis=1, concat_axis=1, tiled=True)]
    all_to_all x2 -> x0, blocking collectives: 63.6 us -> none  [the longest x1 33.1 us: local(): lax.all_to_all(routed, 'col', split_axis=1, concat_axis=0, tiled=True)]
    gather x4 -> x16, local copies, waits for them, and re-layouts: 6.69 us -> 36.3 us  [assemble(): picked = mirror[position, jnp.arange(half_slots, dtype=jnp.int32)[None, :]]]
    dot_general x16, matrix products: 43.9 us -> 68.7 us  [lane_terms(): jnp.dot(weights.reshape(kept_slots, -1), products.reshape(-1, block_size...]
    all_to_all x3 -> x0, starting transfers between devices: 17.2 us -> none  [the longest x1 6.22 us: local(): lax.all_to_all(routed, 'col', split_axis=0, concat_axis=2, tiled=True)]
    select_n x3 -> x0, other arithmetic: 13.4 us -> none  [rotate_tiles(): tiles = jnp.where(amount >> bit & 1 == 1, candidate, tiles)]
  transfers between devices with their start and end apart: 8 -> 0, of which waited for: 6 -> 0; matrix products, arithmetic and copies ran while one was open for 13% -> 0% of each run, Pallas kernels for 0% -> 0%
where the time goes in v1:
time: 587 us; the launch traced here: 577 us
  Pallas kernels  199 us (34%)
  matrix products  172 us (29%)
  local copies, waits for them, and re-layouts  162 us (28%)
  between operations  27.3 us (5%)
  other arithmetic  16.6 us (3%)
    pallas_call x1, Pallas kernels, spread(): pl.pallas_call(spread_kernel, out_shape=jax.ShapeDtypeStruct((SLOTS,) + s...  199 us
    dot_general x16, matrix products, lane_terms(): jnp.einsum('eij,ebjk->ebik', vals_a[:, slot], picked, precision=lax.Preci...  103 us
    dot_general x16, matrix products, lane_terms(): jnp.dot(weights.reshape(kept_slots, -1), products.reshape(-1, block_size...  68.7 us
    gather x16, local copies, waits for them, and re-layouts, lane_terms(): picked = vals_b[position[:, slot]]  51.4 us
    transpose x16, local copies, waits for them, and re-layouts, lane_terms(): jnp.einsum('eij,ebjk->ebik', vals_a[:, slot], picked, precision=lax.Preci...  48.4 us
    gather x16, local copies, waits for them, and re-layouts, assemble(): picked = mirror[position, jnp.arange(half_slots, dtype=jnp.int32)[None, :]]  36.3 us

profile of v1, /device:TPU:42, one launch (start us, length us, event | category | flops | bytes accessed | tf_op | source)
XLA Modules:
  0.0 576.8 jit_solution(11604811373522974441)
XLA Ops:
  27.7 198.9 %spread.1 = f32[16,8,2,128,128]{4,3,2,1,0:T(8,128)} custom-call(f32[2,1,8,2,128,128]{5,4,3,2,1,0:T(8,128)} %stored_ref.1), custom_call_target="tpu_custom_call" | custom-call | tf_op jit(solution)/shard_map/spread/pallas_call | solution.py:353
  226.6 9.9 %dynamic-slice_bitcast_fusion.6 = (f32[8,2,128,128]{3,2,1,0:T(8,128)}, f32[8,2,128,128]{3,2,1,0:T(8,128)}, f32[8,2,128,128]{3,2,1,0:T(8,128)}, f32[8,2,128,128]{...) fusion(f32[16,8,2,128,128]{4,3,2,1,0:T(8,128)} %spread.1, ...), kind=kLoop, calls=%fused_computation.119 | loop fusion | bytes 29360184 | tf_op jit(solution)/shard_map/squeeze | solution.py:429
  242.3 3.7 pad_maximum_fusion.1
  246.5 3.6 gather_fusion.12
  250.1 6.4 %convolution_bitcast_fusion.11 = f32[8,4,128,128]{2,3,1,0:T(8,128)} fusion(f32[8,4,128,128]{3,2,1,0:T(8,128)} %gather_fusion.12, f32[8,2,128,128]{3,2,1,0:T(8,128)} %get-tuple-element.39), kind=kOutput, calls=%fused_computation.108 | convolution fusion | flops 805306368 | bytes 4718592 | tf_op jit(solution)/shard_map/eij,ebjk->ebik/dot_general | solution.py:397
  256.5 3.1 copy.90
  266.0 5.3 fusion.26
  271.3 3.6 gather_fusion.14
  274.8 6.4 %convolution_bitcast_fusion.10 = f32[8,4,128,128]{2,3,1,0:T(8,128)} fusion(f32[8,4,128,128]{3,2,1,0:T(8,128)} %gather_fusion.14, f32[8,2,128,128]{3,2,1,0:T(8,128)} %get-tuple-element.39), kind=kOutput, calls=%fused_computation.107 | convolution fusion | flops 805306368 | bytes 4718592 | tf_op jit(solution)/shard_map/eij,ebjk->ebik/dot_general | solution.py:397
  284.4 5.9 %convolution_add_fusion.8 = f32[32,16384]{1,0:T(8,128)} fusion(f32[32,16384]{1,0:T(8,128)} %fusion.26, pred[32,32]{0,1:T(8,128)(4,1)S(1)} %bitcast.469, f32[4,8,128,128]{3,2,1,0:T(8,128)} %bitcast.430), kind=kOutput, calls=%fused_computation.50 | convolution fusion | flops 201850880 | bytes 6292480 | tf_op jit(solution)/shard_map/dot_general | solution.py:405
  290.3 3.6 gather_fusion.16
  299.4 6.4 %convolution_bitcast_fusion.9 = f32[8,4,128,128]{2,3,1,0:T(8,128)} fusion(f32[8,4,128,128]{3,2,1,0:T(8,128)} %gather_fusion.16, f32[8,2,128,128]{3,2,0,1:T(8,128)} %bitcast.436), kind=kOutput, calls=%fused_computation.106 | convolution fusion | flops 805306368 | bytes 4718592 | tf_op jit(solution)/shard_map/eij,ebjk->ebik/dot_general | solution.py:397
  305.8 3.2 copy.97
  309.0 5.9 %convolution_add_fusion.7 = f32[32,16384]{1,0:T(8,128)} fusion(f32[32,16384]{1,0:T(8,128)} %convolution_add_fusion.8, pred[32,32]{0,1:T(8,128)(4,1)S(1)} %bitcast.468, f32[4,8,128,128]{3,2,1,0:T(8,128)} %bitcast.431), kind=kOutput, calls=%fused_computation.49 | convolution fusion | flops 201850880 | bytes 6292480 | tf_op jit(solution)/shard_map/dot_general | solution.py:405
  320.5 3.1 pad_maximum_fusion.2
  323.6 3.6 gather_fusion.2
  327.2 6.4 %convolution_bitcast_fusion.15 = f32[8,4,128,128]{2,3,1,0:T(8,128)} fusion(f32[8,4,128,128]{3,2,1,0:T(8,128)} %gather_fusion.2, f32[8,2,128,128]{3,2,1,0:T(8,128)} %get-tuple-element.43), kind=kOutput, calls=%fused_computation.112 | convolution fusion | flops 805306368 | bytes 4718592 | tf_op jit(solution)/shard_map/eij,ebjk->ebik/dot_general | solution.py:397
  333.6 3.2 copy.76
  336.8 5.2 fusion.35
  342.0 3.7 gather_fusion.4
  345.7 6.4 %convolution_bitcast_fusion.14 = f32[8,4,128,128]{2,3,1,0:T(8,128)} fusion(f32[8,4,128,128]{3,2,1,0:T(8,128)} %gather_fusion.4, f32[8,2,128,128]{3,2,1,0:T(8,128)} %get-tuple-element.43), kind=kOutput, calls=%fused_computation.111 | convolution fusion | flops 805306368 | bytes 4718592 | tf_op jit(solution)/shard_map/eij,ebjk->ebik/dot_general | solution.py:397
  352.1 3.5 copy.79
  355.6 5.9 %convolution_add_fusion.11 = f32[32,16384]{1,0:T(8,128)} fusion(f32[32,16384]{1,0:T(8,128)} %fusion.35, pred[32,32]{0,1:T(8,128)(4,1)S(1)} %bitcast.464, f32[4,8,128,128]{3,2,1,0:T(8,128)} %bitcast.432), kind=kOutput, calls=%fused_computation.53 | convolution fusion | flops 201850880 | bytes 6292480 | tf_op jit(solution)/shard_map/dot_general | solution.py:405
  361.5 3.6 gather_fusion.6
  370.9 6.5 %convolution_bitcast_fusion.13 = f32[8,4,128,128]{2,3,1,0:T(8,128)} fusion(f32[8,4,128,128]{3,2,1,0:T(8,128)} %gather_fusion.6, f32[8,2,128,128]{3,2,0,1:T(8,128)} %bitcast.439), kind=kOutput, calls=%fused_computation.110 | convolution fusion | flops 805306368 | bytes 4718592 | tf_op jit(solution)/shard_map/eij,ebjk->ebik/dot_general | solution.py:397
  380.5 5.9 %convolution_add_fusion.10 = f32[32,16384]{1,0:T(8,128)} fusion(f32[32,16384]{1,0:T(8,128)} %convolution_add_fusion.11, pred[32,32]{0,1:T(8,128)(4,1)S(1)} %bitcast.463, f32[4,8,128,128]{3,2,1,0:T(8,128)} %bitcast.433), kind=kOutput, calls=%fused_computation.52 | convolution fusion | flops 201850880 | bytes 6292480 | tf_op jit(solution)/shard_map/dot_general | solution.py:405
  386.3 3.6 gather_fusion.9
  390.0 6.4 %convolution_bitcast_fusion.12 = f32[8,4,128,128]{2,3,1,0:T(8,128)} fusion(f32[8,4,128,128]{3,2,1,0:T(8,128)} %gather_fusion.9, f32[8,2,128,128]{3,2,0,1:T(8,128)} %bitcast.440), kind=kOutput, calls=%fused_computation.109 | convolution fusion | flops 805306368 | bytes 4718592 | tf_op jit(solution)/shard_map/eij,ebjk->ebik/dot_general | solution.py:397
  399.3 5.9 %convolution_add_fusion.9 = f32[32,16384]{1,0:T(8,128)} fusion(f32[32,16384]{1,0:T(8,128)} %convolution_add_fusion.10, pred[32,32]{0,1:T(8,128)(4,1)S(1)} %bitcast.462, f32[4,8,128,128]{3,2,1,0:T(8,128)} %bitcast.434), kind=kOutput, calls=%fused_computation.51 | convolution fusion | flops 201850880 | bytes 6292480 | tf_op jit(solution)/shard_map/dot_general | solution.py:405
  405.2 3.6 gather_fusion.19
  408.8 6.4 %convolution_bitcast_fusion.8 = f32[8,4,128,128]{2,3,1,0:T(8,128)} fusion(f32[8,4,128,128]{3,2,1,0:T(8,128)} %gather_fusion.19, f32[8,2,128,128]{3,2,0,1:T(8,128)} %bitcast.437), kind=kOutput, calls=%fused_computation.105 | convolution fusion | flops 805306368 | bytes 4718592 | tf_op jit(solution)/shard_map/eij,ebjk->ebik/dot_general | solution.py:397
  415.2 3.1 copy.99
  418.4 5.4 fusion.38
  434.6 3.6 gather_fusion.39
  444.1 6.4 %convolution_bitcast_fusion = f32[8,4,128,128]{2,3,1,0:T(8,128)} fusion(f32[8,4,128,128]{3,2,1,0:T(8,128)} %gather_fusion.39, f32[8,2,128,128]{3,2,0,1:T(8,128)} %bitcast.441), kind=kOutput, calls=%fused_computation.97 | convolution fusion | flops 805306368 | bytes 4718592 | tf_op jit(solution)/shard_map/eij,ebjk->ebik/dot_general | solution.py:397
  453.4 3.6 gather_fusion.36
  457.0 6.4 %convolution_bitcast_fusion.1 = f32[8,4,128,128]{2,3,1,0:T(8,128)} fusion(f32[8,4,128,128]{3,2,1,0:T(8,128)} %gather_fusion.36, f32[8,2,128,128]{3,2,0,1:T(8,128)} %bitcast.442), kind=kOutput, calls=%fused_computation.98 | convolution fusion | flops 805306368 | bytes 4718592 | tf_op jit(solution)/shard_map/eij,ebjk->ebik/dot_general | solution.py:397
  463.5 3.3 copy.125
  466.8 3.6 gather_fusion.34
  470.4 6.5 %convolution_bitcast_fusion.2 = f32[8,4,128,128]{2,3,1,0:T(8,128)} fusion(f32[8,4,128,128]{3,2,1,0:T(8,128)} %gather_fusion.34, f32[8,2,128,128]{3,2,1,0:T(8,128)} %get-tuple-element.34), kind=kOutput, calls=%fused_computation.99 | convolution fusion | flops 805306368 | bytes 4718592 | tf_op jit(solution)/shard_map/eij,ebjk->ebik/dot_general | solution.py:397
  479.8 3.7 gather_fusion.32
  483.5 6.4 %convolution_bitcast_fusion.3 = f32[8,4,128,128]{2,3,1,0:T(8,128)} fusion(f32[8,4,128,128]{3,2,1,0:T(8,128)} %gather_fusion.32, f32[8,2,128,128]{3,2,1,0:T(8,128)} %get-tuple-element.34), kind=kOutput, calls=%fused_computation.100 | convolution fusion | flops 805306368 | bytes 4718592 | tf_op jit(solution)/shard_map/eij,ebjk->ebik/dot_general | solution.py:397
  498.5 4.1 fusion.8
  505.2 3.9 convolution_add_fusion.1
  516.7 6.5 %convolution_bitcast_fusion.4 = f32[8,4,128,128]{2,3,1,0:T(8,128)} fusion(f32[8,4,128,128]{3,2,1,0:T(8,128)} %gather_fusion.29, f32[8,2,128,128]{3,2,0,1:T(8,128)} %bitcast.443), kind=kOutput, calls=%fused_computation.101 | convolution fusion | flops 805306368 | bytes 4718592 | tf_op jit(solution)/shard_map/eij,ebjk->ebik/dot_general | solution.py:397
  528.3 6.4 %convolution_bitcast_fusion.5 = f32[8,4,128,128]{2,3,1,0:T(8,128)} fusion(f32[8,4,128,128]{3,2,1,0:T(8,128)} %gather_fusion.26, f32[8,2,128,128]{3,2,0,1:T(8,128)} %bitcast.444), kind=kOutput, calls=%fused_computation.102 | convolution fusion | flops 805306368 | bytes 4718592 | tf_op jit(solution)/shard_map/eij,ebjk->ebik/dot_general | solution.py:397
  539.6 6.4 %convolution_bitcast_fusion.6 = f32[8,4,128,128]{2,3,1,0:T(8,128)} fusion(f32[8,4,128,128]{3,2,1,0:T(8,128)} %gather_fusion.24, f32[8,2,128,128]{3,2,1,0:T(8,128)S(1)} %get-tuple-element.38), kind=kOutput, calls=%fused_computation.103 | convolution fusion | flops 805306368 | bytes 4718592 | tf_op jit(solution)/shard_map/eij,ebjk->ebik/dot_general | solution.py:397
  550.9 6.4 %convolution_bitcast_fusion.7 = f32[8,4,128,128]{2,3,1,0:T(8,128)} fusion(f32[8,4,128,128]{3,2,1,0:T(8,128)} %gather_fusion.22, f32[8,2,128,128]{3,2,1,0:T(8,128)S(1)} %get-tuple-element.38), kind=kOutput, calls=%fused_computation.104 | convolution fusion | flops 805306368 | bytes 4718592 | tf_op jit(solution)/shard_map/eij,ebjk->ebik/dot_general | solution.py:397
  (161 shorter events, 114.9 us)
Async XLA Ops:
  226.6 9.9 %copy-start.8 = (s32[16,8]{0,1:T(8,128)S(1)}, s32[16,8]{0,1:T(8,128)}, u32[]{:S(2)}) copy-start(s32[16,8]{0,1:T(8,128)} %param.8) | copy-start | bytes 1540
  226.6 10.2 %copy-start.9 = (s32[16,16,2]{1,2,0:T(2,128)S(1)}, s32[16,16,2]{1,2,0:T(2,128)}, u32[]{:S(2)}) copy-start(s32[16,16,2]{1,2,0:T(2,128)} %param.9) | copy-start | bytes 6148
  256.5 7.9 %copy-start.11 = (s32[2,1,32]{2,1,0:T(1,128)S(1)}, s32[2,1,32]{2,1,0:T(1,128)}, u32[]{:S(2)}) copy-start(s32[2,1,32]{2,1,0:T(1,128)} %param.10) | copy-start | bytes 772
  256.5 8.0 %copy-start.10 = (s32[2,1]{0,1:T(1,128)S(1)}, s32[2,1]{0,1:T(1,128)}, u32[]{:S(2)}) copy-start(s32[2,1]{0,1:T(1,128)} %param.12) | copy-start | bytes 28
  256.5 9.3 %copy-start.12 = (s32[2,1,32]{2,1,0:T(1,128)S(1)}, s32[2,1,32]{2,1,0:T(1,128)}, u32[]{:S(2)}) copy-start(s32[2,1,32]{2,1,0:T(1,128)} %param.11) | copy-start | bytes 772
  498.5 4.1 copy-start.3
  502.7 2.6 copy-start.2
  559.5 2.5 copy-start.6
  562.0 2.6 copy-start.5
  564.6 2.6 copy-start.4
  567.2 2.6 copy-start.1
  567.2 2.6 copy-start.7
  572.5 1.6 copy-start

commit v2 on v0

v2 whole, which is shorter than its diff:
```python
import jax
import jax.numpy as jnp
import numpy as np
from jax import lax
from jax.experimental import pallas as pl
from jax.experimental.pallas import tpu as pltpu
from jax.sharding import PartitionSpec as P

MESH = pl.DeviceIdType.MESH
CHUNKS = 2
SLOTS = 21
SENDS = [
    [32, 12, 16, 539648, 1442817, 1442849, 427523, 527363, 361986, 362018, 790020, 427555, 527395, 1574408, 790052, 2070025, 1213958, 1022469, 1213990, 1022501, 1016327, 801793, 1016359, 1574440, 1329161, 539680, 1147402, 1704970, 1329705, 1705514, 801825, 1146922, 2197003, 2069545, 2197035],
    [32, 11, 14, 1572864, 1703937, 1572896, 1703969, 886275, 948741, 886307, 1821701, 1966600, 1868295, 1323526, 1835014, 948773, 932865, 1323558, 1835046, 852484, 1868327, 1410054, 1821733, 1966632, 852516, 932897, 1476105, 931840, 1410086, 1476137, 2000394, 1444354, 931872, 2000426, 1444386],
    [32, 12, 18, 278528, 1673216, 278560, 1969672, 412162, 409091, 1804804, 409123, 412194, 560645, 787457, 1838598, 1083911, 787489, 560677, 1310720, 1673248, 1908233, 1310752, 1838630, 1983496, 1969704, 1083943, 1804836, 2114566, 1983528, 1871370, 1908265, 1150475, 2114598, 1150507, 1871402],
    [36, 12, 17, 1574912, 656385, 1705985, 1574944, 1706017, 1543168, 1674241, 411140, 675331, 437766, 542213, 411172, 2067976, 1837064, 670210, 675363, 656417, 670242, 437798, 542245, 1064960, 1064992, 2066953, 1327623, 1837608, 1543200, 1327655, 1740298, 1674273, 2113542, 1117707, 2066985, 1117739, 2067496, 2113574, 1740330],
    [30, 12, 20, 364544, 1483777, 1050625, 364576, 400900, 524802, 400932, 524834, 630275, 1282049, 630307, 794117, 794149, 2330626, 1282081, 983559, 1938954, 1206792, 1050657, 983591, 1483809, 1206824, 1059337, 2330658, 2349579, 1059369, 1938986, 2349611, 1449478, 1449510],
    [42, 13, 15, 532480, 1576960, 393217, 1708033, 1576992, 1708065, 557570, 557602, 393249, 758275, 532512, 1839620, 758307, 786436, 1839652, 951299, 1676289, 786468, 951331, 918528, 1970695, 918560, 924165, 1970727, 1055238, 1807882, 1181193, 1562633, 1606152, 1676321, 1181225, 1562665, 924197, 1312267, 1807914, 1055270, 1312299, 2494988, 1606184, 2495020, 1380358, 1380390],
    [20, 9, 17, 267264, 267296, 529409, 529441, 547330, 547362, 564740, 1187334, 564772, 1360902, 1185283, 1187366, 1185315, 1693189, 2300423, 1360934, 2170376, 1693221, 2300455, 2170408],
    [34, 8, 15, 272384, 1185792, 465921, 1316865, 1185824, 1316897, 272416, 465953, 1201666, 728579, 1201698, 1335299, 728611, 657410, 1065984, 657442, 1579527, 583174, 1181702, 1448453, 941572, 583206, 1448485, 941604, 1645568, 1335331, 1677317, 1066016, 1446913, 1579559, 1446945, 1181734, 1645600, 1677349],
    [34, 11, 20, 528384, 698884, 528416, 890376, 1451526, 799234, 535554, 696326, 536098, 682499, 698916, 1123329, 798754, 682531, 792577, 696870, 1451046, 1183752, 1615370, 1324042, 1184296, 792609, 889896, 1841671, 1123361, 1580549, 1842697, 1615402, 1324074, 2301952, 1841703, 2301984, 1580581, 1842729],
    [28, 10, 16, 322560, 1449984, 499713, 1581057, 1450016, 1581089, 435715, 322592, 659457, 435747, 659489, 525826, 921600, 499745, 921632, 525858, 2368008, 666118, 1516036, 2484745, 2236935, 1811973, 666150, 1516068, 2236967, 1812005, 2368040, 2484777],
    [20, 9, 16, 436224, 276481, 276513, 1319936, 436256, 1319968, 1862147, 1237506, 1617413, 1237538, 1289732, 1289764, 2386438, 1617445, 1715719, 1862179, 2386470, 1977864, 1715751, 1977896],
    [36, 12, 17, 1189888, 402433, 1320961, 1189920, 1320993, 402465, 806912, 408066, 1223680, 408098, 811523, 806944, 801285, 1354753, 801317, 2125322, 1153540, 811555, 1223712, 1354785, 2256391, 1974792, 1728520, 1153572, 1974824, 1728552, 1583625, 2141707, 1583657, 2256900, 2258438, 2125354, 2256932, 2141739, 2258470, 2256423],
    [32, 11, 17, 1748992, 273408, 360448, 1056769, 273440, 360480, 308739, 1882626, 308771, 1880065, 1056801, 1455624, 1188359, 2142726, 1424900, 1017353, 1586185, 1188391, 1424932, 1455656, 1080842, 1017385, 1586217, 1442309, 1749024, 1080874, 1442341, 1880097, 2258953, 2258985, 2142758, 1882658],
    [36, 11, 18, 293888, 1454080, 262145, 1585153, 1454112, 1585185, 293920, 262177, 1342978, 394242, 1343010, 817669, 2012161, 394274, 1716739, 788998, 949251, 917504, 817701, 1716771, 917536, 949283, 789030, 2143753, 671239, 671271, 2012193, 2029066, 1866759, 1980936, 2143785, 2112004, 1866791, 2029098, 1980968, 2112036],
    [18, 8, 17, 795138, 668672, 1864195, 795170, 668704, 554502, 554534, 1191937, 835077, 1864227, 1191969, 835109, 2109956, 2109988, 1820167, 1195015, 1195559, 1819687],
    [24, 9, 11, 1062912, 275457, 1193985, 1062944, 1194017, 1458692, 377856, 275489, 1849864, 377888, 571907, 571939, 1456646, 1847810, 1328647, 1458724, 1280006, 1847842, 1587717, 1280550, 1456166, 1587749, 1328679, 1849896],
    [40, 14, 18, 816128, 526336, 1721861, 1048576, 638976, 423426, 639008, 806406, 1051649, 573956, 526368, 806438, 1721893, 573988, 663043, 423458, 979463, 663075, 1048608, 816160, 1051681, 1819147, 1968652, 979495, 1822725, 1855492, 1339912, 2183690, 1819179, 1787401, 1470465, 1339944, 2183722, 2100749, 1822757, 1968684, 1470497, 1787433, 1855524, 2100781],
    [38, 13, 17, 507904, 263169, 507936, 395778, 263201, 395810, 1078273, 905733, 1884680, 808451, 1049600, 644612, 808483, 1330180, 644644, 905765, 1365510, 1199623, 1365542, 1049632, 1078305, 1558026, 2099723, 1982475, 1199655, 1851913, 2230796, 2244620, 1330212, 2115586, 1851945, 1884712, 1558058, 2115618, 2099755, 1982507, 2230828, 2244652],
    [34, 12, 17, 1589248, 424961, 424993, 1077764, 1461252, 1604608, 673283, 646658, 646690, 642565, 1461796, 642597, 871942, 673315, 969223, 1820672, 1592840, 969255, 1952769, 1077284, 1592872, 1723915, 871974, 1854986, 1604640, 1723947, 1590273, 2149897, 1855018, 1820704, 1589280, 1952801, 2149929, 1590305],
    [34, 11, 16, 510976, 511008, 1591810, 1591842, 577027, 1735681, 655362, 676356, 577059, 818694, 1722374, 655394, 676388, 1722918, 804357, 818214, 804389, 1985034, 1315846, 2279943, 1459200, 2083841, 1853961, 1315878, 1720321, 1735713, 1853993, 2182664, 2279975, 1985066, 1459232, 2083873, 2182696, 1720353],
    [36, 11, 18, 279552, 279584, 265217, 348674, 513026, 265249, 348706, 872966, 513058, 774144, 809475, 872998, 775684, 933892, 892421, 934436, 892453, 1167880, 809507, 774176, 1314314, 1463306, 775204, 1332745, 1197057, 1167912, 1332777, 1691649, 1314346, 1463338, 1197089, 1446407, 2201607, 1691681, 1446439, 2201639],
    [24, 9, 18, 381953, 398850, 802816, 381985, 398882, 802848, 907780, 1707009, 1462791, 907812, 1071619, 934913, 1462823, 1071651, 934945, 1707041, 2184710, 2000903, 1333765, 1593864, 1333797, 1593896, 2184742, 2000935],
    [32, 11, 17, 542721, 413186, 544768, 1203715, 413218, 544800, 542753, 1203747, 936452, 839174, 936484, 664582, 839206, 1460224, 1231368, 664614, 1075200, 1460256, 1231400, 2232839, 1075232, 1232394, 1724423, 2232871, 1725957, 1232426, 2103817, 1724455, 2578432, 1725989, 2578464, 2103849],
    [26, 9, 17, 482304, 282625, 1464836, 282657, 420354, 482336, 420386, 1595909, 939008, 936964, 533508, 1464868, 1595941, 1204739, 533540, 1204771, 939040, 936996, 1070598, 1070630, 1985537, 1858056, 1985569, 1858088, 1493511, 1493543],
    [28, 11, 19, 414720, 483328, 414752, 502274, 483360, 502306, 582147, 909828, 1157640, 582179, 909860, 1025541, 685575, 1331201, 1726469, 685607, 1499657, 1157672, 1308166, 1400833, 1025573, 1331233, 1726501, 1308198, 1400865, 1499689, 2155018, 2155050],
    [28, 10, 16, 547840, 289282, 615425, 289314, 547872, 676865, 1023491, 1466371, 946692, 1466915, 1599492, 676897, 615457, 1023011, 1597958, 946724, 1599524, 1597990, 1209864, 1859592, 1993223, 1991177, 1445381, 1993255, 1209896, 1859624, 1445413, 1991209],
    [30, 10, 20, 286720, 423937, 286752, 415745, 926212, 366082, 415777, 366114, 423969, 584195, 1334272, 926244, 681478, 805381, 584227, 681510, 805413, 1763328, 1334304, 1210372, 1601031, 1763360, 2086916, 1601063, 1210404, 1895944, 2086948, 1895976, 1467913, 1467945],
    [38, 10, 19, 781313, 584704, 649731, 1337347, 293378, 548865, 649763, 1337379, 293410, 781345, 548897, 584736, 1465345, 812032, 1174022, 1468422, 1198081, 796167, 812064, 1174054, 1633281, 1193480, 1730568, 1468454, 1465377, 1198113, 1731112, 1208837, 1633313, 796199, 1205769, 1193000, 2127877, 1208869, 1205801, 2127909, 1845764, 1845796],
    [40, 13, 18, 287744, 287776, 643587, 637442, 585728, 1340932, 418817, 667650, 637474, 585760, 418849, 667682, 900613, 1340964, 849415, 687622, 900645, 1619971, 980488, 643619, 1182724, 687654, 1182756, 849447, 1752070, 2332680, 980520, 1896449, 2275849, 1996298, 1620003, 2127371, 1490444, 1996330, 2332712, 1896481, 2127403, 1490476, 2275881, 1752102],
    [22, 10, 18, 325632, 324609, 325664, 324641, 1473027, 1733122, 1196548, 1406469, 1733154, 1196580, 1866246, 943105, 1406501, 1852935, 1997320, 943137, 1473059, 1866278, 1852967, 1997352, 2290185, 2290217],
    [30, 10, 18, 421888, 420865, 274433, 420897, 274465, 1338368, 421920, 622082, 622114, 1338400, 1061380, 1141251, 947719, 1474053, 1061412, 1474085, 1068033, 1296902, 947751, 1141283, 1296934, 1068065, 1506825, 1062408, 1297408, 1506857, 1062440, 1297440, 2018307, 2018339],
    [24, 10, 15, 379905, 552960, 1341955, 379937, 673792, 1341987, 673824, 552992, 1469441, 292356, 701958, 292388, 1732101, 1469473, 1603074, 701990, 1732133, 1604104, 1734151, 1735177, 1603106, 1604136, 1735209, 1734183],
    [38, 13, 18, 266240, 1353729, 266272, 430595, 443906, 313860, 430627, 443938, 313892, 660997, 1351174, 1613827, 661029, 1249284, 966152, 853511, 1613859, 1228298, 966184, 1349129, 853543, 1353761, 1349161, 851468, 1868812, 1577985, 1228330, 1578017, 1351206, 1249316, 2263563, 851500, 1868844, 2535424, 2001929, 2263595, 2535456, 2001961],
    [34, 13, 16, 458752, 307201, 458784, 1737220, 307233, 831488, 962564, 562690, 831520, 1737252, 719368, 562722, 792070, 591365, 962596, 1477127, 591397, 1085961, 850442, 792102, 570375, 1477159, 1085993, 719400, 1314817, 570407, 850474, 1314849, 1487363, 1487395, 2261516, 2130443, 2130475, 2261548],
    [24, 9, 18, 264192, 309248, 264224, 1082883, 331266, 309280, 1179649, 331298, 1345029, 593412, 1082915, 593444, 1345061, 1216006, 1379847, 1179681, 1216038, 1379879, 1738248, 1738280, 2249734, 1094657, 1094689, 2249766],
    [26, 9, 16, 671744, 440321, 658433, 671776, 658465, 440353, 1575936, 441344, 2159109, 1575968, 441376, 1739268, 1101314, 1608198, 1200643, 1608230, 1200675, 1739300, 1101346, 2249224, 1870343, 1111046, 1870375, 1111078, 2159141, 2249256],
    [34, 11, 17, 397313, 1347079, 397345, 1480194, 2101248, 594435, 1612803, 1480226, 594467, 1477634, 957957, 1612835, 1611270, 988676, 1081344, 988708, 1743369, 957989, 1240584, 1081376, 1611302, 1240616, 1643525, 2185224, 2101280, 1347111, 1606657, 1643557, 1743401, 2185256, 1873418, 1606689, 1477666, 1873450],
    [30, 11, 15, 558080, 843266, 1478658, 558112, 1610245, 1479202, 1119747, 875012, 922628, 875044, 922660, 1741318, 1610277, 2363392, 842786, 1343489, 1119779, 1709057, 1744392, 1872391, 2267657, 1741350, 1343521, 2003466, 1872423, 2363424, 2003498, 1709089, 1744424, 2267689],
    [24, 11, 19, 428032, 366592, 366624, 300546, 841219, 300578, 399361, 399393, 428064, 823813, 925190, 841251, 1252872, 824836, 990727, 823845, 990759, 824868, 925222, 1742346, 1252904, 1742378, 2150921, 2150953],
    [36, 12, 16, 690177, 712195, 690209, 1874442, 535042, 1234438, 822272, 535074, 961028, 840197, 712227, 1416192, 822304, 961060, 1234470, 1612297, 1547265, 840229, 1481224, 2019337, 1840129, 1481256, 1416224, 2020362, 2136587, 1612329, 2151943, 1547297, 1840161, 1874474, 2282507, 2019369, 2136619, 2020394, 2151975, 2282539],
    [24, 9, 20, 954368, 269313, 269345, 431618, 1745922, 700416, 431650, 1745954, 692740, 846341, 700448, 826886, 846373, 1024001, 692772, 826918, 954400, 1024033, 981507, 981539, 1223176, 1223208, 1748487, 1748519],
    [36, 13, 19, 438273, 438305, 1712642, 454147, 601088, 1712674, 595460, 454179, 601120, 439813, 595492, 561670, 439845, 561702, 1092103, 950274, 987656, 1351688, 950306, 1092135, 2269708, 1483274, 955392, 987688, 1351720, 1355782, 1485321, 1483306, 955424, 1355814, 964107, 1636361, 1485353, 964139, 2269740, 1636393],
    [38, 13, 18, 301056, 860161, 301088, 697858, 1486346, 962053, 697890, 694273, 828932, 828964, 1108483, 731136, 1103366, 1092614, 694305, 962085, 731168, 1103398, 1092646, 860193, 970757, 1745415, 1363975, 970789, 1108515, 1893900, 1714697, 1745447, 1359368, 1486378, 1364007, 1714729, 1893932, 1359400, 2315274, 2013707, 2315306, 2013739],
    [22, 7, 18, 338945, 338977, 1664000, 1251843, 1846789, 1219584, 1780736, 1780768, 1349633, 1189378, 1191428, 1251875, 1219616, 1349665, 1191460, 1664032, 1189410, 1878534, 1846821, 1620998, 1878566, 1621030],
    [38, 12, 21, 1650688, 425984, 457728, 426016, 457760, 396802, 471555, 396834, 471587, 819201, 1226246, 864773, 762881, 799750, 704007, 1781761, 1226278, 864805, 762913, 819233, 704039, 2073603, 799782, 1650720, 958984, 1212419, 1781793, 1915396, 959016, 1212451, 1375754, 1375786, 928265, 2010635, 928297, 2073635, 2010667, 1915428],
    [24, 9, 18, 1242112, 565249, 588801, 588833, 798210, 588291, 565281, 798242, 1618437, 1090560, 588323, 1782785, 1751558, 1090592, 1112580, 1618469, 1112612, 1242144, 1782817, 2273799, 1751590, 2404872, 2273831, 2404904],
    [18, 8, 18, 305152, 303105, 305184, 454657, 303137, 1619458, 454689, 1750531, 1357316, 1357348, 1619490, 998917, 2667015, 1750563, 998949, 1128966, 1128998, 2667047],
    [24, 11, 14, 567297, 567329, 1106434, 829440, 1096195, 829472, 604676, 1227269, 1096227, 661509, 1358342, 662053, 604708, 1226789, 1358374, 1106466, 2216455, 1489416, 1489448, 1955337, 1637898, 2216487, 1637930, 1955369],
    [24, 10, 17, 409601, 710146, 688128, 451584, 409633, 451616, 688160, 559620, 710178, 848390, 714245, 559652, 848422, 1100291, 1100323, 2272775, 714277, 1492489, 1363464, 1106945, 1492521, 1106977, 1363496, 2272807],
    [28, 9, 15, 295936, 295968, 1360386, 1360418, 825859, 820225, 820257, 838148, 825891, 1710599, 1490951, 838180, 1491495, 1972226, 975873, 1710119, 1362437, 2146824, 1362469, 975905, 1113090, 1711112, 1113122, 1972258, 2146856, 1711144, 2024966, 2024998],
    [30, 12, 19, 326656, 318465, 1214465, 326688, 318497, 1214497, 705026, 705058, 678403, 678435, 1067008, 2054144, 1067040, 1623559, 1105412, 1475081, 1236485, 1072648, 1475113, 1072680, 1521158, 1105444, 1728010, 2054176, 1521190, 1728042, 1236517, 1754635, 1623591, 1754667],
    [34, 11, 17, 281600, 281632, 489986, 543745, 490018, 1624579, 543777, 581124, 1624611, 1755653, 581156, 977921, 1012741, 1013285, 1104392, 1277446, 2017286, 1755173, 977953, 2120706, 1277478, 2017318, 2322436, 1622535, 2186241, 1622567, 1104424, 1609225, 1609257, 2186273, 2120738, 2411018, 2411050, 2322468],
    [32, 11, 17, 319488, 319520, 1494530, 455681, 455713, 563715, 937984, 1627657, 563747, 1494562, 1069057, 956932, 938016, 956964, 1069089, 1089029, 1496582, 1791495, 1089061, 2005001, 1858562, 1496614, 1875464, 2421258, 1791527, 1627689, 2006018, 2005033, 1858594, 1875496, 2421290, 2006050],
    [28, 11, 18, 283649, 283681, 302594, 1495042, 545792, 302626, 1495074, 842245, 545824, 580100, 1626627, 1626659, 580132, 1135112, 842277, 1135144, 1218055, 1368586, 1497606, 2053130, 1218087, 1368618, 2398211, 1497638, 2160137, 2053162, 2398243, 2160169],
    [30, 10, 16, 550912, 312321, 613891, 1629187, 312353, 448002, 550944, 613923, 1760774, 448034, 1629219, 1217028, 1137157, 1825793, 1086470, 1137189, 1760806, 1217060, 1989128, 2015232, 1086502, 1594376, 1825825, 1348103, 1891849, 1989160, 1348135, 2015264, 1594408, 1891881],
    [38, 12, 15, 321537, 434176, 810498, 321569, 434208, 777731, 790529, 1370114, 790561, 777763, 578052, 1366533, 810530, 578084, 967680, 967712, 2087937, 1366565, 1757702, 1268736, 1268768, 1628680, 1370146, 1759753, 2317314, 1889285, 1757734, 1890826, 1628712, 2317346, 1759785, 2087969, 1889317, 2021899, 1900039, 1890858, 1900071, 2021931],
    [34, 12, 19, 516096, 587266, 574464, 516128, 587298, 1088003, 574496, 572932, 702981, 1369606, 1302529, 572964, 703013, 2056715, 1631753, 834055, 1302561, 2157579, 1369638, 2029572, 1088035, 1631785, 1879562, 1098753, 910856, 834087, 910888, 1911819, 2158123, 1879594, 1098785, 2056235, 2029604, 1911851],
    [26, 10, 16, 386049, 566786, 1317889, 566818, 453123, 386081, 453155, 679936, 679968, 705537, 2025989, 705569, 1761798, 1097728, 2270729, 1097760, 2157063, 2026021, 1761830, 2157095, 1885700, 2417160, 1317921, 1885732, 2417192, 2270761],
    [36, 13, 17, 486400, 486432, 720386, 707585, 2027019, 2316803, 720418, 1008132, 1762821, 1138182, 1764874, 707617, 1058313, 1008164, 1661448, 2252804, 1138214, 1090055, 1090087, 2119680, 1887232, 1058345, 1762853, 1764906, 1989633, 1844231, 2027051, 2119712, 1887264, 1661480, 1989665, 2316835, 2420236, 1844263, 2252836, 2420268],
    [28, 11, 19, 314369, 1500674, 314401, 1400324, 878592, 1232896, 711171, 945670, 814597, 711203, 814629, 878624, 945702, 1500706, 1207816, 1894921, 1400356, 2552327, 1207848, 1894953, 1232928, 1797121, 1797153, 1892874, 2531338, 1892906, 2531370, 2552359],
    [28, 12, 20, 356352, 316417, 356384, 316449, 541186, 578560, 1374723, 541218, 578592, 1404929, 2011652, 1404961, 2122249, 965130, 1374755, 1373704, 1630726, 2384395, 2011684, 1373736, 1630758, 1888773, 2122281, 2132487, 1888805, 965162, 2132519, 2384427],
    [30, 9, 17, 474112, 311297, 297474, 311329, 297506, 575488, 488449, 474144, 1634819, 488481, 1505796, 919556, 1634851, 1336837, 952325, 1765895, 575520, 1336869, 1881090, 952357, 920100, 2274822, 1765927, 953347, 1881122, 953379, 1505316, 2028040, 2274854, 2028072],
    [26, 9, 17, 448512, 569345, 569377, 1488386, 448544, 785409, 785441, 689667, 715778, 706561, 689699, 716322, 1487906, 1504773, 1432068, 1432100, 706593, 1635846, 1244679, 1713155, 1244711, 1897992, 1504805, 1635878, 1713187, 1898024],
    [22, 9, 15, 280576, 324098, 280608, 449537, 324130, 717315, 449569, 717347, 843776, 1502210, 843808, 970245, 1766916, 1502242, 970277, 1899014, 1767943, 1766948, 2161160, 1767975, 1899046, 2161192],
    [20, 9, 16, 598016, 334848, 334880, 346626, 346658, 598048, 724993, 725025, 1920517, 2462211, 1381892, 1920549, 1382919, 1381924, 1257990, 1382951, 2462243, 1902088, 1258022, 1902120],
    [28, 9, 15, 294912, 294944, 1376771, 463362, 602112, 929793, 596993, 463394, 597025, 602144, 929825, 867331, 1376803, 723460, 1507845, 723492, 1254401, 867363, 735750, 1769478, 1507877, 735782, 1769510, 1254433, 2165255, 2427400, 2165287, 2427432],
    [28, 9, 19, 444416, 442369, 1274370, 444448, 442401, 600064, 837124, 1345536, 600096, 2181122, 1638919, 1345568, 837156, 858113, 1293829, 1657350, 858145, 1293861, 1508872, 1753095, 1638951, 1657382, 1513987, 1274402, 1753127, 1514019, 2181154, 1508904],
    [26, 9, 17, 297985, 1142785, 298017, 429056, 605184, 429088, 605216, 2051586, 1284098, 1247749, 1142817, 1284642, 1247781, 1640967, 1509894, 1948677, 2051106, 1509926, 1799683, 1948709, 1903112, 1640999, 2464260, 1903144, 1799715, 2464292],
    [30, 11, 20, 368640, 368672, 466945, 693249, 466977, 350723, 762372, 350755, 762404, 859653, 693281, 1222150, 859685, 2437634, 1222182, 2447881, 2134016, 1546759, 926725, 2138632, 1546791, 926757, 2037769, 2134048, 2138664, 2038313, 2579978, 2447401, 2580010, 2437666],
    [44, 15, 18, 340992, 299009, 341024, 470017, 299041, 1245698, 470049, 1245730, 960003, 727556, 960035, 727588, 1151496, 2306049, 1122822, 1169927, 2334720, 1122854, 989701, 1169959, 1151528, 1385997, 2297869, 989733, 2036235, 1511946, 1511978, 2400267, 1942028, 2464780, 1942060, 1517070, 2428942, 2036267, 2431497, 2334752, 1386029, 2297901, 2400299, 1517102, 2428974, 2464812, 2306081, 2431529],
    [26, 12, 19, 268288, 342016, 413697, 268320, 342048, 2037250, 413729, 2168323, 2037282, 1171972, 2168355, 1510920, 1172004, 1384966, 1387015, 1383946, 1510952, 2052617, 2052649, 1515019, 1384998, 1387047, 1383978, 1785349, 1515051, 1785381],
    [30, 10, 17, 337920, 744963, 475650, 531457, 779265, 337952, 592388, 531489, 744995, 475682, 592420, 985605, 869379, 985637, 1055744, 1776134, 1944071, 869411, 1055776, 1615878, 1907208, 1776166, 779297, 1392137, 1907240, 1944103, 1522696, 1615910, 1392169, 1522728],
    [38, 12, 18, 332800, 343040, 459777, 332832, 343072, 664068, 1221122, 1843200, 1221154, 459809, 1648133, 1404422, 664100, 2073095, 1648165, 1125383, 1156617, 1642498, 1353224, 1125927, 2105345, 1353256, 1770501, 1843232, 1388035, 1156649, 1388067, 1910283, 1404454, 1642530, 2105377, 2041354, 1910315, 2072615, 2075650, 2041386, 1770533, 2075682],
    [30, 12, 16, 304128, 271361, 354305, 304160, 271393, 1026562, 732675, 354337, 732707, 1909256, 1026594, 1403396, 1646596, 1778181, 1647140, 2171401, 2040327, 1402916, 2139658, 1778213, 2172933, 1909288, 2435590, 2040359, 2171433, 2172965, 2401803, 2435622, 2139690, 2401835],
    [30, 11, 19, 306177, 306209, 473089, 614915, 473121, 614947, 736770, 1779208, 599556, 736802, 1771523, 599588, 1288192, 1010181, 1650182, 1288224, 1747465, 1010213, 1650214, 1158146, 1158178, 2034183, 1779240, 2187270, 1784330, 1771555, 2034215, 1747497, 2187302, 1784362],
    [32, 12, 17, 371713, 749058, 371745, 749090, 1271299, 1518084, 764928, 1518116, 764960, 747013, 1120775, 747045, 1139208, 1120807, 1139240, 568841, 1084934, 1780234, 1271331, 2057220, 1780266, 568873, 1911307, 1942531, 1911339, 2449414, 1084966, 2188298, 1942563, 2057252, 2449446, 2188330],
    [24, 11, 19, 372736, 335872, 372768, 335904, 468483, 468515, 898049, 991750, 863746, 1253893, 863778, 898081, 1094151, 991782, 1094183, 1253925, 992772, 1914378, 2454024, 992804, 1654281, 1914410, 1654313, 2454056],
    [38, 13, 16, 359425, 1520130, 589824, 359457, 1520162, 893444, 619520, 589856, 619552, 827907, 893476, 827939, 821250, 1159169, 1287686, 821282, 1407493, 1159201, 1522185, 1287718, 1904641, 1407525, 1913351, 2007040, 1913383, 1549834, 2008065, 1904673, 1367560, 1260043, 1549866, 2007072, 1260075, 2175500, 2008097, 2175532, 1522217, 1367592],
    [18, 6, 16, 333824, 487425, 603650, 487457, 751616, 333856, 603682, 751648, 722435, 722467, 1402373, 1260549, 1539075, 1402405, 1260581, 1539107, 2169348, 2169380],
    [26, 9, 14, 460800, 310272, 460832, 310304, 464897, 638466, 638498, 464929, 866821, 997894, 862724, 866853, 1408001, 1238017, 862756, 997926, 1408033, 1390083, 1390115, 1391112, 1777159, 1958918, 1777191, 1391144, 1238049, 1958950],
    [20, 8, 16, 836099, 1900544, 520706, 742400, 520738, 836131, 742432, 873473, 873505, 967172, 1394181, 967204, 1525254, 2296327, 1900576, 1394213, 1568772, 1525286, 1568804, 2296359],
    [26, 10, 17, 328704, 480257, 328736, 1133058, 480289, 1377281, 1131012, 1264131, 1131044, 1919493, 1116681, 2312712, 1262087, 1133090, 1452039, 1264163, 1230342, 1262119, 1230374, 1452071, 1919525, 1860617, 1116713, 2312744, 1377313, 1860649],
    [22, 7, 20, 285696, 1014785, 285728, 481281, 481313, 1886208, 1038850, 1378305, 1038882, 2055168, 1886240, 1014817, 737795, 2055200, 1378337, 2032134, 2148868, 737827, 1393157, 2148900, 1393189, 2032166],
    [38, 12, 18, 880640, 351233, 445954, 351265, 479748, 678912, 445986, 479780, 678944, 880672, 2574859, 1537026, 876037, 1625088, 876069, 1756161, 2165761, 1395206, 1246729, 1625120, 1421832, 1787912, 1305604, 1537058, 1756193, 1305636, 1399303, 1395238, 1421864, 1787944, 1399335, 1246761, 2443786, 2144771, 2443818, 2165793, 2144803, 2574891],
    [36, 12, 19, 446464, 344579, 446496, 344611, 1529350, 1529382, 1008640, 708609, 606727, 1007108, 1270282, 1659914, 708641, 606759, 1007140, 1102345, 1429513, 1532929, 1531394, 1102377, 1008672, 1660458, 1531426, 1429545, 1269802, 1916934, 1037832, 1532961, 830981, 1037864, 2041856, 1824267, 2041888, 1916966, 1824299, 831013],
    [30, 11, 18, 352256, 352288, 743939, 484353, 464386, 464418, 1645060, 876548, 743971, 971777, 484385, 1790471, 1006085, 971809, 1645092, 876580, 1006117, 1255431, 1256966, 1658886, 1256998, 1658918, 1790503, 2048522, 1758728, 1255463, 1758760, 2180617, 2048554, 2180649],
    [40, 13, 20, 284672, 317441, 284704, 317473, 748037, 616962, 1793026, 1014276, 1924611, 616994, 1793058, 857092, 1924643, 748069, 857636, 1013796, 1142279, 1267208, 1775115, 1142311, 870924, 1397772, 1774089, 1272326, 1639432, 1272358, 1527817, 1774121, 1534976, 1267240, 1533953, 1775147, 1535008, 1527849, 1533985, 870956, 1397804, 1639464, 2445834, 2445866],
    [36, 13, 20, 347136, 355329, 315393, 347168, 355361, 315425, 715269, 596484, 417282, 1501699, 1923594, 417314, 1432580, 596516, 1432612, 1004038, 715301, 1265160, 1792008, 1004070, 1792552, 608775, 999434, 1695241, 1264680, 1923626, 1695273, 1501731, 608807, 1596416, 1906188, 999466, 2289163, 1596448, 1906220, 2289195],
    [26, 11, 19, 1073152, 617986, 1649157, 1795077, 618018, 881664, 1274881, 610820, 881696, 610852, 993799, 1795621, 845318, 730627, 1648677, 1073184, 1274913, 993831, 730659, 1987080, 1519114, 1519146, 845350, 2009609, 1987112, 2009641],
    [32, 13, 17, 911360, 357377, 357409, 1124870, 911392, 1925644, 880131, 2173955, 880163, 861700, 1532424, 1857033, 2304008, 861732, 1561093, 1136130, 1124902, 1794571, 1532456, 1136162, 1435146, 2320903, 2320935, 1561125, 2042891, 1794603, 1925676, 1435178, 2304040, 1857065, 2042923, 2173987],
    [30, 12, 19, 490497, 1828354, 912385, 490529, 847365, 1666566, 1239556, 912417, 726531, 726563, 1140232, 1435648, 847397, 1666598, 1435680, 1140264, 1239588, 1926663, 1875971, 1801216, 2318858, 1928715, 1876003, 1926695, 1632777, 1801248, 1928747, 1632809, 2318890, 1828386],
    [38, 12, 15, 337411, 1665027, 353797, 1796101, 337443, 1144832, 1043457, 1927684, 1665059, 1796645, 1145857, 1005063, 1927716, 353317, 2189834, 972804, 1012226, 1043489, 2058758, 1144864, 2058790, 1698313, 977416, 1012258, 1145889, 977448, 1005095, 1960960, 1698345, 972836, 2060291, 1371145, 2451979, 1960992, 2189866, 1371177, 2452011, 2060323],
    [28, 10, 20, 345088, 505857, 745990, 505889, 878088, 345120, 733698, 2035204, 1372681, 1241092, 1669635, 746022, 607233, 733730, 782336, 607265, 1266181, 782368, 1266213, 1961985, 878120, 1669667, 1962017, 1241636, 1945095, 2034724, 1372713, 1945127],
    [36, 12, 16, 358914, 390145, 476161, 718341, 358946, 390177, 517636, 476193, 517668, 724489, 1667081, 718373, 2337291, 1929227, 2075143, 1536007, 865795, 1263112, 1798666, 1133568, 724521, 1536551, 1667113, 865827, 986122, 1798698, 1503241, 1929771, 1133600, 986154, 1263144, 1931782, 2074663, 1931814, 2336811, 1503273],
    [42, 15, 18, 388096, 914433, 750083, 388128, 457218, 750115, 1932808, 457250, 485892, 2092034, 1243655, 485924, 1144326, 1437196, 1273349, 1144358, 1000456, 1932840, 1993729, 1243687, 914465, 1003017, 984587, 1273381, 1000488, 1003049, 1668107, 984619, 1437228, 1662477, 2092066, 1930762, 1115662, 1395713, 1662509, 1668139, 1115694, 1395745, 1993761, 2313216, 2313248, 1930794],
    [32, 14, 16, 609281, 751106, 650240, 2062851, 609313, 477187, 2062883, 1011206, 650272, 740868, 751138, 740900, 2193925, 477219, 1768972, 2193957, 1109511, 739848, 1389065, 1011238, 1567242, 1109543, 1567274, 2325003, 1114117, 739880, 1786381, 2325035, 1389097, 1786413, 1769004, 1114149],
    [24, 9, 14, 495616, 495106, 495648, 1541636, 406529, 495138, 1672709, 1544194, 1541668, 406561, 1803782, 1672741, 1149447, 1803814, 1544226, 1411073, 1952264, 1149479, 2110470, 1952296, 1411105, 2110502, 2460163, 2460195],
    [36, 11, 17, 887809, 405505, 405537, 364034, 626688, 995845, 364066, 626720, 903686, 1998853, 920581, 897539, 995877, 920613, 1937410, 903718, 931332, 897571, 887841, 1409545, 904711, 1224704, 2068481, 904743, 1224736, 931364, 1998885, 1937442, 1917952, 1409577, 1979912, 2083338, 2068513, 1979944, 2083370, 1917984],
    [28, 11, 20, 497664, 329728, 327681, 329760, 1046019, 327713, 497696, 493058, 493090, 854532, 1148421, 854564, 1934339, 1641991, 1046051, 1148453, 1805832, 855558, 1934371, 855590, 1936906, 1689097, 1642023, 1805864, 1991686, 1936938, 1689129, 1991718],
    [26, 9, 17, 759809, 1524227, 1772544, 667138, 2049542, 1903617, 759841, 667170, 691716, 1542661, 720897, 1176581, 691748, 1415168, 1542693, 720929, 1415200, 1176613, 1524259, 1772576, 1903649, 2329095, 2329127, 2215432, 2049574, 2215464],
    [28, 9, 20, 331776, 367616, 270851, 367648, 1118726, 755202, 270883, 331808, 760833, 1283588, 2166785, 1283620, 755234, 1564165, 1318913, 760865, 1039880, 1678341, 1564197, 1679360, 1512967, 1678373, 1679392, 1118758, 1039912, 1318945, 1512999, 2166817],
    [30, 9, 17, 373761, 373793, 1675782, 631808, 891394, 635395, 1053188, 1166342, 891426, 635427, 2298881, 631840, 1053220, 1940481, 1035781, 1413125, 1810433, 1035813, 1413157, 1481728, 1166886, 1675302, 1940513, 1810465, 2334215, 2200072, 2334247, 2200104, 1481760, 2298913],
    [34, 13, 19, 432128, 628227, 514562, 1248772, 550405, 763905, 514594, 432160, 763937, 625158, 628259, 894976, 550437, 625190, 1545737, 895008, 783879, 783911, 1414149, 1074698, 1809418, 1248804, 1414181, 1545769, 1425928, 2072075, 1074730, 1809450, 2072107, 2039308, 1425960, 2198536, 2198568, 2039340],
    [34, 12, 19, 370689, 433153, 370721, 626179, 1808901, 1939975, 530946, 433185, 2086404, 530978, 695296, 626211, 1806857, 1419264, 695328, 1808933, 1017863, 1940007, 1219080, 1292292, 1419296, 1292836, 1017895, 1806889, 1219112, 1313286, 2118154, 1957387, 2118667, 1957419, 1313318, 2118186, 2085924, 2118699],
    [26, 10, 19, 502784, 888832, 340482, 502816, 340514, 633857, 729603, 633889, 1019905, 729635, 908804, 888864, 1568262, 1019937, 996871, 908836, 1682952, 1021445, 996903, 2108937, 1021477, 1568294, 2076672, 1682984, 2076704, 2108969],
    [36, 13, 16, 504833, 504865, 766976, 1548804, 813056, 767008, 1417733, 2043908, 813088, 766466, 896001, 766498, 896033, 1417765, 1028611, 1126918, 1548836, 1813000, 1028643, 1126950, 1029639, 2206217, 1876993, 1029671, 1291786, 1813032, 1291818, 1877025, 2204171, 2206249, 2560001, 2204203, 2043940, 2466316, 2560033, 2466348],
    [30, 11, 19, 403456, 374785, 374817, 469507, 768000, 469539, 768032, 370178, 1154567, 403488, 370210, 894470, 1584644, 894502, 1423877, 1154599, 1305097, 1059849, 1551882, 1305129, 1059881, 1584676, 1551914, 1423909, 1960456, 1960488, 2191370, 1680389, 1680421, 2191402],
    [34, 11, 17, 519682, 404995, 628739, 521217, 519714, 405027, 628771, 521249, 1550852, 928769, 942597, 699392, 1550884, 942629, 1162240, 928801, 1162272, 1434120, 1582082, 1681929, 1434152, 1686532, 1681961, 1582114, 1598983, 699424, 1947649, 2468362, 1686564, 1730054, 1947681, 2468394, 1599015, 1730086],
    [34, 11, 16, 506880, 391682, 506912, 391714, 401923, 1422339, 401955, 1422371, 753665, 833028, 734725, 753697, 734757, 1555457, 1978369, 1553928, 1685001, 1259015, 1155080, 833060, 1816074, 2242054, 1553960, 1685033, 1155112, 2254858, 1671168, 1555489, 1978401, 1259047, 2255402, 1815594, 1671200, 2242086],
    [32, 10, 15, 536576, 536608, 472578, 1552899, 622592, 472610, 461827, 1552931, 899588, 1683973, 1815046, 899620, 622624, 1684005, 461859, 1815078, 1817601, 1717249, 886790, 1946120, 886822, 1653257, 1946152, 1802241, 1717281, 1652231, 1817633, 1652263, 1802273, 2044937, 1653289, 2044969],
    [38, 15, 20, 493568, 538624, 633347, 2079747, 504322, 633379, 2079779, 504354, 389637, 538656, 1322502, 389669, 1047553, 493600, 1047585, 1290245, 2046472, 1718795, 1127946, 797191, 1290277, 1097225, 2095104, 1097257, 1127978, 797223, 2095136, 1947150, 2271756, 1718827, 2140685, 1322534, 1947182, 2591236, 2140717, 2591268, 2046504, 2271788],
    [40, 15, 17, 654337, 278019, 1699843, 363010, 278051, 1699875, 363042, 756736, 654369, 755713, 1827332, 1325573, 913928, 2078728, 756768, 1027593, 1832458, 2209802, 755745, 1325605, 2603531, 1027625, 913960, 2078760, 2210346, 1453575, 1963019, 2094605, 2207246, 1831978, 2603563, 1963051, 1019398, 1827364, 1019430, 1453607, 2094637, 2061836, 2207278, 2061868],
    [30, 11, 15, 1033216, 1164289, 1033248, 1164321, 1063937, 769538, 815622, 769570, 1281541, 772096, 772128, 815654, 1165827, 1132039, 1412102, 1165859, 1281573, 1559044, 1412134, 1559076, 1132071, 1295881, 1437701, 1295913, 1655306, 1437733, 1063969, 1655338, 1326600, 1326632],
    [16, 7, 14, 378880, 641025, 378912, 1556994, 641057, 1557026, 738820, 1554947, 1687555, 1688099, 1950214, 738852, 1935877, 1554467, 1935909, 1950246],
    [36, 10, 16, 382976, 1428480, 522241, 491521, 1559553, 1428512, 1559585, 653826, 1690626, 383008, 491553, 624132, 522273, 2065410, 653858, 1690658, 1001472, 624164, 509443, 885255, 509475, 1278469, 1001504, 915976, 885287, 916008, 1079301, 1278501, 1540617, 1294345, 1079333, 1540649, 1294377, 1426950, 2065442, 1426982],
    [28, 10, 17, 478208, 512001, 381442, 478240, 1657858, 381474, 512033, 1179139, 1788929, 1179171, 1427972, 1657890, 1428004, 944128, 1300480, 1163781, 1656328, 944160, 1300512, 1788961, 1163813, 1690118, 1526279, 1690150, 1526311, 2050569, 2050601, 1656360],
    [30, 12, 17, 1299456, 1430529, 1299488, 1430561, 901635, 770562, 770594, 741377, 776192, 901667, 1285638, 776224, 741409, 2203144, 1921024, 1562119, 1285670, 771593, 1562151, 1814026, 1921056, 771625, 2198020, 1988107, 2593285, 2203176, 2198052, 2593317, 1814058, 1988139],
    [20, 9, 16, 515072, 349185, 497154, 349217, 499203, 515104, 497186, 499235, 2071045, 1955841, 1955873, 2071077, 1922566, 1954311, 1922598, 2201092, 2085384, 1954343, 2085416, 2201124],
    [36, 12, 18, 518144, 1170432, 1301505, 1170464, 1301537, 518176, 611329, 1054214, 683522, 1670145, 611361, 1042951, 683554, 856581, 940547, 1397252, 1042983, 856613, 1268234, 1054246, 1298434, 940579, 1268266, 1397284, 1298466, 906760, 1152007, 1234944, 1309195, 906792, 1152039, 1309227, 1168905, 1670177, 1168937, 1234976],
    [22, 8, 16, 385025, 612867, 1693699, 385057, 780288, 1527298, 1825284, 1040901, 612899, 780320, 1693731, 1825316, 1040933, 973825, 2218503, 1202694, 1250308, 1250340, 973857, 1202726, 2218535, 1527330],
    [34, 11, 15, 387072, 1041408, 1172481, 1041440, 1172513, 387104, 631299, 418308, 451074, 418340, 451106, 631331, 713223, 1161733, 1303557, 994822, 1662982, 1304101, 994854, 713255, 975368, 1121281, 975400, 1161253, 2023424, 1121313, 1129993, 1176074, 2285569, 1663014, 1176106, 1130025, 2023456, 2285601],
    [16, 7, 15, 320513, 320545, 501250, 501282, 1418757, 1174528, 1565188, 1174560, 1565220, 1828865, 1418789, 1420803, 1696262, 1828897, 1696294, 1420835],
    [40, 15, 19, 1698816, 1309697, 1829889, 1698848, 1829921, 647683, 523778, 647715, 523810, 778757, 753158, 778789, 753190, 1309729, 1076743, 1440768, 759304, 1036804, 1076775, 1440800, 759336, 1036836, 1538569, 1538601, 1566220, 2516992, 2063885, 1697291, 2499086, 1976842, 2063917, 1975302, 1566252, 2499118, 1498117, 2517024, 1697323, 1975334, 1976874, 1498149],
    [36, 12, 16, 651264, 384000, 289793, 2448901, 384032, 289825, 645636, 2091012, 552454, 916995, 917027, 645668, 2091044, 552486, 651296, 1530378, 2353162, 2124290, 1047048, 2222088, 1958411, 1286663, 1863177, 1047080, 2222120, 1177602, 1530410, 2353194, 1178146, 1286695, 2386944, 2123810, 1958443, 1863209, 2448933, 2386976],
    [36, 12, 16, 290816, 1438720, 1569793, 1438752, 1569825, 1701380, 290848, 684033, 2340868, 684065, 1031683, 640514, 1031715, 1030661, 1701412, 1964032, 1160197, 1030693, 640546, 868870, 2340900, 1964064, 1160229, 868902, 1686023, 1602058, 1229320, 1686055, 1229352, 1817097, 1602090, 2314249, 1817129, 2211339, 2211371, 2314281],
    [28, 10, 16, 392192, 375809, 1831430, 392224, 375841, 636418, 2471942, 636450, 1995271, 784385, 1032707, 1472004, 784417, 2126344, 2093064, 1110533, 1864705, 1032739, 1472036, 1110565, 2472486, 1830950, 1995303, 2126376, 2093096, 1864737, 2585097, 2585129],
    [24, 10, 16, 376832, 1571840, 1702913, 1571872, 1702945, 376864, 556547, 619010, 555524, 509953, 619042, 556579, 509985, 555556, 1834501, 1834533, 1211910, 1211942, 1800711, 1800743, 1307144, 982537, 1307176, 982569],
    [36, 11, 14, 1439744, 1439776, 1702404, 884233, 1571330, 621059, 1571362, 621091, 883206, 652292, 1702436, 1034242, 537600, 686600, 883238, 1833479, 652324, 537632, 773121, 686632, 1278983, 1833511, 1034274, 902144, 884265, 648709, 1276426, 773153, 648741, 1848327, 1276458, 1279015, 1044490, 1044522, 1848359, 902176],
]
ROLES = [
    [0, 0, 12, 1, 13, 13, 14, 15, 0, 0, 1, 12, 8, 10],
    [0, 11, 13, 12, 6, 8, 5, 2, 1, 1, 8, 6, 2, 5],
    [0, 4, 12, 14, 13, 11, 8, 6, 15, 15, 17, 16, 2, 3],
    [0, 8, 7, 6, 15, 14, 4, 3, 16, 16, 12, 2, 5, 13],
    [0, 2, 12, 19, 13, 10, 14, 15, 16, 16, 3, 18, 11, 17],
    [0, 12, 2, 5, 4, 7, 11, 6, 13, 13, 8, 9, 3, 14],
    [0, 7, 9, 11, 10, 8, 6, 12, 14, 14, 15, 13, 2, 16],
    [0, 5, 3, 12, 9, 7, 6, 14, 11, 11, 8, 13, 4, 10],
    [0, 5, 11, 17, 12, 9, 6, 18, 14, 14, 16, 13, 19, 15],
    [0, 7, 10, 14, 11, 8, 3, 6, 2, 2, 15, 9, 13, 12],
    [0, 13, 9, 12, 10, 5, 8, 7, 15, 15, 14, 11, 3, 6],
    [0, 9, 2, 4, 15, 13, 5, 6, 16, 16, 14, 12, 7, 10],
    [0, 6, 11, 13, 12, 3, 9, 8, 14, 14, 15, 4, 5, 16],
    [0, 3, 5, 8, 12, 11, 2, 7, 13, 13, 16, 14, 17, 15],
    [0, 15, 8, 14, 9, 12, 11, 7, 10, 10, 13, 16, 0, 15],
    [0, 8, 4, 4, 6, 9, 7, 7, 10, 10, 0, 8, 1, 5],
    [12, 12, 15, 17, 13, 13, 14, 5, 0, 2, 1, 8, 16, 10],
    [11, 12, 2, 5, 9, 13, 7, 4, 1, 14, 16, 15, 6, 3],
    [16, 3, 13, 10, 14, 15, 4, 12, 3, 16, 10, 13, 8, 11],
    [6, 14, 13, 12, 11, 2, 15, 4, 10, 9, 2, 11, 4, 15],
    [4, 14, 11, 12, 2, 5, 10, 9, 7, 13, 8, 16, 17, 15],
    [7, 8, 3, 13, 11, 10, 5, 12, 2, 16, 17, 9, 14, 15],
    [8, 5, 11, 14, 10, 15, 3, 12, 4, 9, 6, 13, 2, 16],
    [4, 8, 10, 2, 9, 5, 11, 3, 7, 13, 12, 15, 14, 16],
    [2, 17, 12, 15, 4, 9, 11, 14, 8, 13, 18, 7, 6, 16],
    [6, 9, 2, 11, 3, 8, 7, 4, 12, 14, 5, 15, 13, 10],
    [2, 9, 11, 13, 15, 12, 10, 7, 14, 18, 5, 17, 19, 16],
    [6, 8, 10, 5, 3, 12, 11, 13, 17, 16, 18, 15, 2, 14],
    [3, 9, 4, 13, 12, 6, 11, 10, 2, 15, 5, 16, 14, 17],
    [10, 2, 6, 3, 16, 15, 8, 7, 14, 11, 12, 13, 4, 17],
    [14, 11, 13, 12, 15, 7, 10, 5, 6, 8, 17, 4, 0, 16],
    [9, 8, 12, 12, 3, 11, 13, 13, 10, 14, 0, 4, 1, 5],
    [8, 8, 13, 17, 10, 10, 16, 12, 0, 15, 1, 14, 5, 4],
    [4, 12, 8, 13, 11, 14, 10, 7, 1, 3, 2, 9, 6, 15],
    [3, 8, 12, 14, 5, 11, 13, 6, 4, 16, 9, 15, 10, 17],
    [6, 7, 10, 8, 4, 9, 15, 11, 14, 5, 3, 13, 2, 12],
    [7, 16, 14, 12, 15, 2, 6, 10, 16, 7, 12, 14, 13, 11],
    [7, 5, 2, 6, 12, 14, 13, 9, 11, 10, 14, 12, 9, 13],
    [2, 4, 12, 11, 10, 17, 14, 16, 7, 9, 18, 15, 3, 13],
    [9, 8, 12, 4, 10, 11, 7, 6, 15, 14, 5, 2, 3, 13],
    [12, 13, 10, 17, 4, 6, 2, 11, 16, 9, 18, 15, 14, 19],
    [8, 12, 5, 9, 13, 10, 6, 7, 14, 15, 18, 16, 4, 17],
    [2, 11, 6, 14, 4, 8, 10, 5, 17, 16, 13, 15, 3, 9],
    [8, 6, 3, 13, 11, 7, 14, 15, 17, 16, 9, 4, 10, 12],
    [19, 8, 6, 17, 2, 11, 18, 12, 13, 16, 14, 9, 15, 20],
    [9, 7, 12, 10, 8, 5, 13, 6, 15, 2, 11, 16, 14, 17],
    [2, 4, 8, 10, 3, 13, 11, 9, 12, 17, 14, 16, 0, 15],
    [3, 6, 7, 7, 8, 5, 9, 9, 11, 13, 0, 12, 1, 10],
    [15, 15, 11, 10, 12, 12, 16, 9, 0, 5, 1, 14, 6, 13],
    [7, 2, 4, 12, 8, 11, 5, 13, 1, 9, 3, 10, 6, 14],
    [6, 7, 18, 15, 10, 11, 13, 12, 3, 9, 8, 17, 14, 16],
    [10, 6, 14, 4, 5, 3, 2, 11, 8, 9, 12, 15, 13, 16],
    [16, 4, 9, 12, 8, 2, 11, 6, 3, 13, 5, 15, 10, 14],
    [12, 3, 4, 6, 2, 11, 5, 14, 7, 13, 17, 15, 9, 16],
    [4, 11, 12, 14, 6, 10, 13, 15, 11, 4, 14, 12, 9, 3],
    [8, 10, 12, 14, 9, 11, 3, 7, 5, 13, 11, 9, 7, 3],
    [7, 4, 6, 13, 5, 3, 18, 9, 15, 14, 17, 8, 16, 12],
    [10, 6, 3, 5, 8, 12, 7, 13, 2, 9, 11, 14, 4, 15],
    [3, 15, 12, 14, 16, 5, 10, 11, 8, 7, 6, 9, 13, 4],
    [18, 9, 11, 14, 13, 15, 7, 17, 3, 6, 4, 8, 12, 16],
    [2, 7, 8, 13, 19, 16, 12, 15, 4, 10, 14, 17, 5, 18],
    [10, 7, 4, 11, 3, 8, 14, 12, 2, 6, 9, 15, 13, 16],
    [11, 5, 14, 13, 8, 6, 16, 7, 4, 12, 10, 9, 0, 15],
    [6, 7, 11, 11, 8, 9, 5, 5, 10, 12, 0, 13, 1, 14],
    [9, 9, 13, 10, 6, 6, 11, 8, 0, 12, 1, 7, 14, 15],
    [6, 3, 7, 8, 5, 14, 11, 4, 1, 13, 2, 9, 10, 12],
    [16, 18, 12, 9, 8, 5, 11, 14, 15, 13, 10, 17, 2, 6],
    [7, 5, 15, 9, 6, 8, 10, 3, 16, 11, 13, 12, 14, 2],
    [12, 8, 11, 15, 14, 19, 17, 18, 2, 4, 16, 7, 6, 13],
    [10, 11, 15, 5, 13, 14, 16, 4, 17, 12, 6, 8, 3, 7],
    [2, 7, 11, 14, 3, 5, 13, 10, 16, 4, 12, 18, 15, 17],
    [11, 8, 2, 5, 6, 10, 4, 14, 9, 13, 12, 15, 3, 16],
    [4, 17, 15, 14, 16, 5, 10, 11, 17, 4, 14, 15, 13, 12],
    [7, 8, 4, 5, 15, 14, 13, 6, 12, 9, 14, 15, 6, 13],
    [4, 16, 6, 14, 8, 18, 13, 11, 3, 7, 17, 12, 5, 15],
    [12, 11, 6, 8, 10, 4, 3, 5, 7, 14, 13, 15, 2, 16],
    [2, 6, 11, 14, 17, 3, 10, 16, 12, 18, 13, 15, 5, 8],
    [2, 7, 4, 11, 14, 12, 15, 9, 13, 3, 10, 8, 6, 5],
    [2, 9, 6, 10, 12, 11, 7, 5, 8, 4, 14, 15, 0, 13],
    [5, 8, 2, 2, 6, 9, 12, 12, 7, 10, 0, 11, 1, 13],
    [13, 13, 9, 5, 10, 10, 8, 6, 0, 15, 1, 14, 12, 11],
    [7, 10, 2, 5, 4, 11, 3, 8, 1, 16, 14, 12, 15, 13],
    [8, 14, 13, 10, 9, 17, 18, 19, 16, 12, 2, 11, 7, 15],
    [8, 6, 17, 7, 10, 11, 4, 5, 14, 15, 3, 16, 13, 12],
    [17, 18, 10, 13, 3, 7, 12, 6, 14, 11, 5, 8, 16, 15],
    [12, 7, 5, 10, 6, 11, 3, 9, 2, 14, 13, 17, 16, 15],
    [7, 12, 2, 13, 5, 8, 3, 14, 18, 17, 16, 6, 19, 15],
    [13, 8, 15, 7, 14, 10, 2, 18, 5, 19, 3, 17, 11, 16],
    [7, 4, 5, 11, 15, 12, 13, 14, 3, 17, 10, 16, 8, 18],
    [13, 8, 7, 14, 11, 12, 3, 2, 4, 6, 15, 16, 5, 9],
    [17, 7, 14, 16, 15, 13, 11, 6, 7, 17, 16, 14, 12, 18],
    [4, 10, 11, 3, 14, 12, 2, 13, 5, 6, 12, 14, 13, 2],
    [17, 15, 14, 11, 7, 5, 12, 13, 2, 18, 10, 16, 4, 19],
    [11, 7, 6, 12, 9, 10, 2, 8, 3, 14, 4, 15, 5, 13],
    [14, 11, 16, 17, 2, 6, 15, 8, 5, 4, 12, 13, 0, 9],
    [5, 11, 13, 13, 3, 14, 8, 8, 10, 15, 0, 6, 1, 4],
    [12, 12, 4, 5, 13, 13, 10, 6, 0, 2, 1, 7, 9, 11],
    [11, 12, 14, 16, 9, 13, 8, 3, 1, 2, 15, 7, 4, 6],
    [3, 19, 11, 17, 5, 2, 10, 8, 14, 16, 18, 15, 12, 13],
    [5, 7, 16, 3, 14, 13, 6, 2, 10, 9, 11, 15, 12, 8],
    [3, 11, 4, 12, 15, 14, 16, 10, 2, 17, 9, 18, 19, 13],
    [9, 6, 4, 2, 8, 5, 10, 11, 12, 14, 13, 15, 3, 16],
    [3, 6, 10, 14, 5, 9, 13, 11, 15, 18, 17, 7, 2, 16],
    [13, 7, 2, 17, 5, 15, 14, 18, 3, 6, 10, 16, 11, 12],
    [12, 5, 11, 10, 13, 14, 18, 16, 15, 2, 7, 17, 4, 6],
    [4, 5, 6, 8, 12, 11, 2, 9, 15, 14, 7, 13, 3, 10],
    [6, 13, 10, 12, 2, 16, 11, 18, 7, 14, 15, 17, 9, 8],
    [11, 9, 3, 15, 4, 10, 6, 12, 13, 14, 5, 16, 2, 7],
    [15, 2, 12, 13, 11, 8, 3, 10, 2, 15, 13, 12, 14, 9],
    [5, 6, 12, 8, 10, 13, 14, 4, 11, 3, 13, 10, 4, 14],
    [5, 7, 15, 3, 14, 6, 19, 16, 13, 12, 18, 17, 0, 4],
    [8, 15, 3, 3, 11, 10, 13, 13, 7, 16, 0, 6, 1, 2],
    [2, 2, 14, 12, 8, 8, 1, 11, 0, 9, 1, 11, 13, 13],
    [6, 3, 7, 9, 8, 2, 1, 10, 1, 10, 13, 12, 11, 11],
    [5, 9, 2, 12, 4, 6, 1, 10, 14, 11, 15, 8, 13, 13],
    [12, 6, 10, 9, 11, 4, 1, 2, 13, 16, 3, 14, 15, 15],
    [9, 4, 15, 7, 3, 2, 1, 14, 5, 6, 12, 13, 16, 16],
    [8, 11, 9, 13, 10, 7, 1, 6, 2, 4, 12, 15, 14, 14],
    [5, 10, 12, 16, 14, 8, 1, 13, 3, 17, 11, 6, 15, 15],
    [3, 7, 8, 10, 9, 4, 1, 5, 14, 11, 12, 13, 15, 15],
    [4, 8, 5, 11, 2, 7, 1, 12, 3, 14, 9, 10, 13, 13],
    [9, 4, 7, 11, 8, 6, 1, 12, 2, 5, 10, 14, 13, 13],
    [2, 12, 16, 17, 13, 11, 1, 15, 9, 14, 18, 6, 10, 10],
    [8, 10, 12, 2, 13, 4, 1, 9, 3, 15, 14, 6, 7, 7],
    [7, 9, 4, 13, 11, 3, 1, 15, 5, 2, 14, 6, 12, 12],
    [12, 6, 10, 7, 11, 8, 1, 4, 2, 3, 13, 14, 15, 15],
    [14, 15, 11, 13, 5, 12, 1, 10, 15, 14, 13, 11, 0, 0],
    [2, 7, 11, 11, 12, 0, 1, 1, 4, 13, 0, 12, 1, 1],
]


def fill_table(tbl, me, lo, hi):
    if hi - lo == 1:
        head = SENDS[lo]
        for place, word in enumerate(head):
            tbl[place] = jnp.int32(word)
        return
    mid = (lo + hi) // 2
    lax.cond(
        me < mid,
        lambda: fill_table(tbl, me, lo, mid),
        lambda: fill_table(tbl, me, mid, hi),
    )


def spread_kernel(stored_ref, slots_ref, tbl, own_sem, send_sem, recv_sem):
    rows_per = stored_ref.shape[2] // CHUNKS
    row_count = lax.axis_size("row")
    me = lax.axis_index("col") * row_count + lax.axis_index("row")
    fill_table(tbl, me, 0, len(SENDS))
    own = [
        pltpu.make_async_copy(stored_ref.at[lane, 0], slots_ref.at[lane], own_sem.at[lane])
        for lane in range(2)
    ]
    for copy in own:
        copy.start()

    def hop(source, target, slot, chunk, place):
        return pltpu.make_async_remote_copy(
            src_ref=source,
            dst_ref=slots_ref.at[slot, pl.ds(chunk * rows_per, rows_per)],
            send_sem=send_sem.at[place],
            recv_sem=recv_sem.at[slot, chunk],
            device_id={"col": target // row_count, "row": lax.rem(target, row_count)},
            device_id_type=MESH,
        )

    def arrival(slot, chunk):
        piece = slots_ref.at[slot, pl.ds(chunk * rows_per, rows_per)]
        hop(piece, me, slot, chunk, 0).wait_recv()

    sends = tbl[0]

    @pl.loop(0, sends)
    def _(place):
        word = tbl[3 + place]
        slot = word & 31
        chunk = (word >> 5) & 15
        target = (word >> 10) & 127
        landing = word >> 17

        @pl.when(((word >> 9) & 1) == 1)
        def _():
            arrival(slot, chunk)

        @pl.when(slot < 2)
        def _():
            piece = stored_ref.at[slot, 0, pl.ds(chunk * rows_per, rows_per)]
            hop(piece, target, landing, chunk, place).start()

        @pl.when(slot >= 2)
        def _():
            piece = slots_ref.at[slot, pl.ds(chunk * rows_per, rows_per)]
            hop(piece, target, landing, chunk, place).start()

    @pl.loop(tbl[1], tbl[2])
    def _(slot):
        for chunk in range(CHUNKS):
            arrival(slot, chunk)

    @pl.loop(0, sends)
    def _(place):
        piece = slots_ref.at[0, pl.ds(0, rows_per)]
        hop(piece, me, 0, 0, place).wait_send()

    for copy in own:
        copy.wait()


def spread(stored):
    return pl.pallas_call(
        spread_kernel,
        out_shape=jax.ShapeDtypeStruct((SLOTS,) + stored.shape[2:], jnp.float32),
        in_specs=[pl.BlockSpec(memory_space=pl.ANY)],
        out_specs=pl.BlockSpec(memory_space=pl.ANY),
        scratch_shapes=[
            pltpu.SMEM((max(len(entry) for entry in SENDS),), jnp.int32),
            pltpu.SemaphoreType.DMA((2,)),
            pltpu.SemaphoreType.DMA((max(entry[0] for entry in SENDS),)),
            pltpu.SemaphoreType.DMA((SLOTS, CHUNKS)),
        ],
        compiler_params=pltpu.CompilerParams(has_side_effects=True),
        name="spread",
    )(stored)


def split(value):
    high = value.astype(jnp.bfloat16)
    return high, (value - high.astype(jnp.float32)).astype(jnp.bfloat16)


def multiply_kernel(
    slots_ref, roles_ref, rows_ref, offs_ref, krow_ref, kcol_ref, kcnt_ref, out_ref,
    raw, left, right, done, in_sem, out_sem,
):
    grid = lax.axis_size("row")
    tile_j = lax.axis_index("row")
    col_id = lax.axis_index("col")
    me = col_id * grid + tile_j
    tiles = raw.shape[0]
    active = raw.shape[1]
    half = raw.shape[2]
    block = raw.shape[-1]
    kept = krow_ref.shape[-1]

    def load(place):
        return pltpu.make_async_copy(
            slots_ref.at[roles_ref[me, place]], raw.at[place], in_sem.at[place]
        )

    for place in range(tiles):
        load(place).start()

    first = rows_ref[0, 0]
    bits = [rows_ref[0, 1] ^ first, rows_ref[0, 2] ^ first, rows_ref[0, 4] ^ first]

    def rank(value):
        return sum(
            jnp.where((value & bit) != 0, jnp.int32(1 << place), jnp.int32(0))
            for place, bit in enumerate(bits)
        )

    def shifts(tile_x, tile_y):
        both = ((tile_x, tile_y), (tile_y, tile_x))
        return [rank(offs_ref[x, y, slot]) for x, y in both for slot in range(half)]

    tile_is = [col_id * 2 + lane for lane in range(2)]
    tile_ks = [lax.rem(tile_is[0] + tile_j + place, grid) for place in range(3)]
    left_shifts = [
        [shifts(tile_is[lane], tile_ks[lane + step]) for step in range(2)] for lane in range(2)
    ]

    for place in range(3):
        load(8 + 2 * place).wait()
        load(9 + 2 * place).wait()
        own, mirror = raw.at[8 + 2 * place], raw.at[9 + 2 * place]
        moves = shifts(tile_ks[place], tile_j)

        @pl.loop(0, active)
        def _(row):
            for slot in range(half):
                mirror[row, slot] = mirror[row, slot].T

        def entry(slot, row):
            if slot < half:
                return own.at[row, slot]
            return mirror.at[row ^ moves[slot], slot - half]

        alive = []
        for slot in range(2 * half):
            same = [moves[slot] == moves[before] for before in range(slot)]
            taken = jnp.bool_(False)
            for before in range(slot):
                join = same[before] & alive[before] & jnp.logical_not(taken)
                taken = taken | same[before]

                @pl.when(join)
                def _():
                    @pl.loop(0, active)
                    def _(row):
                        into = entry(before, row)
                        into[...] = into[...] + entry(slot, row)[...]

            alive.append(jnp.logical_not(taken))

        for shift in range(active):
            used = moves[0] == shift
            for slot in range(1, 2 * half):
                used = used | (moves[slot] == shift)

            @pl.when(jnp.logical_not(used))
            def _():
                @pl.loop(0, active)
                def _(row):
                    right[place, row, row ^ shift] = jnp.zeros((block, 2 * block), jnp.bfloat16)

        for slot in range(2 * half):
            @pl.when(alive[slot])
            def _():
                @pl.loop(0, active)
                def _(row):
                    high, low = split(entry(slot, row)[...])
                    column = row ^ moves[slot]
                    right[place, row, column, :, :block] = high
                    right[place, row, column, :, block:] = low

    for place in range(4):
        load(2 * place).wait()
        load(2 * place + 1).wait()

        @pl.loop(0, active)
        def _(row):
            for slot in range(half):
                high, low = split(raw[2 * place, row, slot])
                left[place, row, slot, :block] = high
                left[place, row, slot, block:] = low
                high, low = split(raw[2 * place + 1, row, slot].T)
                left[place, row, half + slot, :block] = high
                left[place, row, half + slot, block:] = low

    for lane in range(2):
        count = kcnt_ref[lane, 0]

        @pl.loop(0, kept)
        def _(item):
            @pl.when(item < count)
            def _():
                row = rank(krow_ref[lane, 0, item])
                column = rank(kcol_ref[lane, 0, item])
                lefts, rights = [], []
                for step in range(2):
                    for slot in range(2 * half):
                        middle = row ^ left_shifts[lane][step][slot]
                        source = row if slot < half else middle
                        lefts.append(left[2 * lane + step, source, slot])
                        rights.append(right[lane + step, middle, column])
                total = jnp.dot(
                    jnp.concatenate(lefts, 1),
                    jnp.concatenate(rights, 0),
                    preferred_element_type=jnp.float32,
                )
                total = total[:block] + total[block:]
                done[lane, item] = total[:, :block] + total[:, block:]

            @pl.when(item >= count)
            def _():
                done[lane, item] = jnp.zeros((block, block), jnp.float32)

        pltpu.make_async_copy(done.at[lane], out_ref.at[lane, 0], out_sem.at[lane]).start()

    for lane in range(2):
        pltpu.make_async_copy(done.at[lane], out_ref.at[lane, 0], out_sem.at[lane]).wait()


def multiply(slots, roles, tile_rows, offsets, kept_rows, kept_cols, kept_count):
    block = slots.shape[-1]
    active, half = slots.shape[1:3]
    lanes, _, kept = kept_rows.shape
    tiles = roles.shape[-1]
    smem = pl.BlockSpec(memory_space=pltpu.SMEM)
    return pl.pallas_call(
        multiply_kernel,
        out_shape=jax.ShapeDtypeStruct((lanes, 1, kept, block, block), jnp.float32),
        in_specs=[pl.BlockSpec(memory_space=pl.ANY)] + [smem] * 6,
        out_specs=pl.BlockSpec(memory_space=pl.ANY),
        scratch_shapes=[
            pltpu.VMEM((tiles, active, half, block, block), jnp.float32),
            pltpu.VMEM((4, active, 2 * half, 2 * block, block), jnp.bfloat16),
            pltpu.VMEM((3, active, active, block, 2 * block), jnp.bfloat16),
            pltpu.VMEM((lanes, kept, block, block), jnp.float32),
            pltpu.SemaphoreType.DMA((tiles,)),
            pltpu.SemaphoreType.DMA((lanes,)),
        ],
        compiler_params=pltpu.CompilerParams(vmem_limit_bytes=56 << 20),
        name="multiply",
    )(slots, roles, tile_rows, offsets, kept_rows, kept_cols, kept_count)


def local(stored, tile_rows, offsets, kept_rows, kept_cols, kept_count):
    slots = spread(stored)
    roles = jnp.asarray(np.array(ROLES, np.int32))
    return multiply(slots, roles, tile_rows, offsets, kept_rows, kept_cols, kept_count)


def solution(mesh):
    in_specs = (
        P("col", "row", None, None, None, None),
        P(),
        P(),
        P("col", "row", None),
        P("col", "row", None),
        P("col", "row"),
    )
    out_specs = P("col", "row", None, None, None)
    return jax.shard_map(local, mesh=mesh, in_specs=in_specs, out_specs=out_specs, check_vma=False)
```

time: 771 us -> 211 us (0.27)
  the two profiles are of different devices: /device:TPU:42 before, /device:TPU:45 now
where the time goes in v2:
time: 211 us
  Pallas kernels  207 us (98%)
  local copies, waits for them, and re-layouts  4.18 us (2%)
    pallas_call x1, Pallas kernels, spread(): pl.pallas_call(spread_kernel, out_shape=jax.ShapeDtypeStruct((SLOTS,) + s...  171 us
    pallas_call x1, Pallas kernels, multiply(): pl.pallas_call(multiply_kernel, out_shape=jax.ShapeDtypeStruct((lanes, 1,...  36.1 us

profile of v2, /device:TPU:45, one launch (start us, length us, event | category | flops | bytes accessed | tf_op | source)
XLA Modules:
  0.0 210.8 jit_solution(10877499858299964455)
XLA Ops:
  0.0 1.3 copy.10.kcnt_ref
  1.3 1.3 copy.8.rows_ref
  2.7 1.5 copy.9.offs_ref
  4.2 170.5 %spread.1.slots_ref = f32[21,8,2,128,128]{4,3,2,1,0:T(8,128)} custom-call(f32[2,1,8,2,128,128]{5,4,3,2,1,0:T(8,128)} %stored_ref.1), custom_call_target="tpu_custom_call" | custom-call | tf_op jit(solution)/shard_map/spread/pallas_call | solution.py:353
  174.7 36.1 %multiply.1 = f32[2,1,32,128,128]{4,3,2,1,0:T(8,128)} custom-call(f32[21,8,2,128,128]{4,3,2,1,0:T(8,128)} %spread.1.slots_ref, s32[128,14]{1,0:T(8,128)} %constant.2.clone.roles_ref, s32[16,8]{1,0:T(8,128)} %copy.8.rows_ref, s32[16,16,2]{2,1,0:T(8,128)} %copy.9.offs_ref, s32[2,1,32]{2,1,0:T(1,128)} %krow_ref.1, s32[2,1,32]{2,1,0:T(1,128)} %kcol_ref.1, ...), custom_call_target="tpu_custom_call" | custom-call | tf_op jit(solution)/shard_map/multiply/pallas_call | solution.py:523

commit v3 on v0

v3 whole, which is shorter than its diff:
```python
import jax
import jax.numpy as jnp
import numpy as np
from jax import lax
from jax.experimental import pallas as pl
from jax.experimental.pallas import tpu as pltpu
from jax.sharding import PartitionSpec as P

MESH = pl.DeviceIdType.MESH
CHUNKS = 4
SLOTS = 32
SENDS = [
    [2242561, 1187840, 1187904, 1187968, 1188032, 270337, 270401, 1851906, 270465, 2242625, 270529, 688648, 1450505, 1982473, 2242689, 688712, 1450569, 2244616, 2242753, 688776, 1450633, 1982537, 662026, 688840, 1450697, 2244680, 662090, 2523661, 1982601, 2523725, 2244744, 1982665, 3160592, 2523789, 2244808, 3160656, 958993, 1851970, 3160720, 2916883, 2236435, 1852034, 3160784, 2523853, 2237011, 1852098, 1456660, 2916435, 2237075, 3031564, 1456724, 2916499, 926214, 3031628, 662154, 2917075, 2236627, 3031692, 1456788, 1344018, 3031756, 662218, 959057, 1327630, 1456852, 1344082, 1327694, 2628118, 959121, 1327758, 2759192, 1344146, 1057287, 1327822, 2628182, 959185, 926278, 1720847, 2759256, 1344210, 1057351, 1720911, 2628246, 1737237, 926342, 1720975, 2759320, 1745431, 1057415, 1721039, 2628310, 1737301, 926406, 1729035, 2759384, 1745495, 1057479, 1729099, 1737365, 1729163, 1745559, 1729227, 1737429, 1745623],
    [2326529, 262144, 262208, 262272, 262336, 393217, 393281, 1992201, 393345, 2326593, 393409, 1992265, 2326657, 535051, 524804, 1992329, 2326721, 535115, 2516493, 2851330, 2501134, 2516557, 2851394, 2501198, 2516621, 2851458, 2501262, 655877, 1966608, 2516685, 2851522, 2501326, 524868, 1992393, 2334724, 2763279, 524932, 2376708, 1966672, 2334788, 655941, 2763343, 524996, 3040272, 2334852, 656005, 2763407, 1966736, 2376772, 2334916, 656069, 535179, 3040336, 3375113, 2763471, 1966800, 2376836, 2728460, 535243, 3040400, 2859530, 1051154, 2376900, 3375177, 1051218, 3040464, 2728524, 1051282, 1066513, 2859594, 1051346, 1459731, 3375241, 1313300, 1066577, 2728588, 1321494, 1459795, 2859658, 1313364, 1066641, 3375305, 1321558, 1459859, 2728652, 1313428, 1066705, 2859722, 1321622, 1459923, 1810965, 1313492, 1811029, 1321686, 1811093, 1811157],
    [2258944, 2237440, 1859585, 1859649, 1859713, 1859777, 1990656, 1990720, 1990784, 2237504, 2513410, 1990848, 2513474, 534019, 2646542, 2513538, 534083, 287247, 2513602, 795663, 2408976, 418321, 2775043, 787473, 2409040, 287311, 549394, 2259008, 795727, 713236, 418385, 680455, 2775107, 787537, 2409104, 287375, 549458, 2259072, 795791, 2802197, 3039253, 418449, 2775683, 787601, 2802261, 3039317, 287439, 549522, 2259136, 795855, 942614, 2802325, 3039381, 418513, 2775747, 787665, 2802389, 3039445, 2646606, 549586, 3299342, 2237568, 2646670, 3430931, 533635, 2646734, 3299406, 2237632, 1098263, 3430995, 533699, 942678, 1098327, 680519, 3299470, 1180690, 942742, 2409168, 680583, 3431059, 1180754, 1098391, 680647, 3299534, 1180818, 942806, 3457560, 1335818, 3431123, 1180882, 3457624, 1335882, 1341447, 1582090, 3457688, 1335946, 1604102, 1844246, 3457752, 1336010, 1341511, 1582154, 1098455, 1597965, 1604166, 1844310, 713300, 1598029, 1341575, 1582218, 713364, 1598093, 1604230, 1844374, 713428, 1598157, 1341639, 1582282, 1604294, 1844438],
    [401409, 278528, 278592, 278656, 278720, 409601, 409665, 409729, 533006, 409793, 2640401, 541200, 1712144, 672274, 2902547, 541264, 1712208, 639508, 672338, 2902611, 541328, 1712272, 672402, 2902675, 541392, 1712336, 672466, 2902739, 533070, 2220565, 1064981, 533134, 3303942, 2220629, 1065045, 533198, 3304006, 2220693, 1065109, 2490902, 3304070, 2220757, 1065173, 2490966, 3304134, 2867735, 2491030, 2640465, 2744840, 786959, 2640529, 2744904, 2491094, 2640593, 2744968, 2499081, 1460762, 2745032, 2499145, 1075736, 3129881, 2499209, 1591835, 3129945, 2499273, 1460826, 2867799, 917522, 1591899, 3130009, 787023, 1075800, 2867863, 917586, 1460890, 3130073, 787087, 1075864, 2867927, 917650, 1591963, 639572, 787151, 1460954, 639636, 917714, 1075928, 639700, 401473, 1592027, 1557020, 401537, 1557084, 401601, 1557148, 1557212],
    [301056, 1884160, 1900545, 1875968, 2007041, 1876032, 2007105, 1876096, 2007169, 1876160, 2015746, 563201, 1900609, 2007233, 1884224, 2687491, 2406916, 2015810, 2687555, 2406980, 1884288, 1900673, 2407044, 2015874, 2687619, 834055, 1884352, 1900737, 834119, 2015938, 2687683, 834183, 2671119, 834247, 3080720, 2671183, 2407108, 3080784, 1095683, 2671247, 3080848, 2531860, 2671311, 1350149, 2826770, 301120, 844309, 3080912, 2531924, 975374, 1358358, 2826834, 563265, 967185, 2826898, 2531988, 1095747, 1229335, 2826962, 844373, 1350213, 3342356, 2532052, 975438, 1358422, 3342420, 1221130, 301184, 967249, 3342484, 563329, 1229399, 3342548, 1221194, 844437, 1095811, 1647123, 975502, 1350277, 1647187, 1221258, 1358486, 967313, 1647251, 301248, 1229463, 1647315, 1221322, 844501, 563393, 1095875, 975566, 1350341, 967377, 1358550, 1229527],
    [1179649, 294912, 294976, 295040, 295104, 425985, 426049, 426113, 1179713, 426177, 2394640, 1179777, 2394704, 1179841, 2402819, 2680337, 819716, 1974798, 2787332, 2811410, 819780, 2105871, 2787396, 2680401, 819844, 1974862, 2787460, 2811474, 819908, 2105935, 2787524, 2680465, 1974926, 2402883, 2811538, 2105999, 2402947, 2680529, 1974990, 2394768, 3065350, 2106063, 1212935, 2403011, 3065414, 2368005, 3065478, 2394832, 2368069, 3065542, 3312148, 2368133, 2811602, 3189269, 2368197, 1631763, 3312212, 2629632, 1631827, 3189333, 2892290, 1754646, 3312276, 2629696, 1212999, 1754710, 3189397, 2892354, 1754774, 3312340, 2629760, 1213063, 1631891, 3189461, 2892418, 1754838, 2629824, 1213127, 1631955, 2892482],
    [1892352, 1892416, 1892480, 1892544, 2023425, 2023489, 2546178, 2187266, 2023553, 2023617, 2532878, 2547726, 2546242, 2187330, 2926095, 2546306, 2187394, 2532942, 2547790, 2546370, 2187458, 2679313, 3187729, 2679377, 2842639, 719376, 3187793, 2548366, 2843215, 719440, 2679441, 3187857, 2679505, 2843279, 3187921, 2548430, 3104782, 2532494, 2843343, 719504, 2532558, 3104846, 973331, 2925647, 3104910, 1235476, 2925711, 3104974, 1112599, 2925775, 1008146, 1628694, 951319, 1139221, 973395, 1213976, 1008210, 1235540, 959504, 1139285, 1106440, 1112663, 1222169, 1008274, 1106504, 1628758, 951383, 1139349, 973459, 1214040, 1008338, 1106568, 1235604, 959568, 1139413, 2021914, 1222233, 2021978, 951959, 1112215, 1214104, 2022042, 959632, 1106632, 1628822, 1222297, 973523, 952023, 1235668, 1214168, 1112279, 960208, 719056, 1222361, 2022106, 1628886],
    [2418688, 303105, 2252801, 311297, 311361, 311425, 311489, 442368, 442432, 442496, 434702, 2514958, 2418752, 442560, 2515534, 2418816, 565775, 2146834, 2515598, 2418880, 565839, 2146898, 2515662, 565903, 322064, 573954, 565967, 2777617, 322128, 574018, 434254, 2777681, 584212, 574082, 705045, 434318, 2777745, 3336213, 705109, 434382, 2777809, 322192, 574146, 2146962, 2540054, 2252865, 2654723, 322256, 2147026, 2933271, 303169, 2252929, 3983896, 2540118, 2252993, 2654787, 3983960, 705173, 303233, 3432470, 3984024, 2933335, 3563543, 2654851, 3984088, 705237, 836121, 303297, 3432534, 3336277, 2540182, 836185, 3563607, 3336341, 2654915, 2933399, 836249, 3432598, 3336405, 2924569, 2540246, 836313, 3563671, 2924633, 584276, 2933463, 3432662, 2924697, 1755674, 1360393, 3563735, 2924761, 1755738, 1360457, 1466899, 1482770, 584340, 1360521, 1466963, 1613845, 1755802, 1360585, 1467027, 1482834, 584404, 1467091, 1613909, 1755866, 1482898, 1613973, 1482962, 1614037],
    [2308096, 1916929, 1908737, 1908801, 1908865, 1908929, 2039808, 2039872, 2458114, 2039936, 2308160, 1916993, 2040000, 2458178, 2308224, 1917057, 2458242, 2308288, 2441745, 2564628, 2458306, 1917121, 2701845, 2564692, 3113490, 2441809, 858640, 3113554, 737301, 2701909, 2564756, 2204174, 2441873, 866835, 2204238, 737365, 2701973, 2564820, 3113618, 2441937, 858704, 2204302, 737429, 2702037, 2204366, 737493, 866899, 3113682, 858768, 746007, 2596884, 866963, 746071, 1253912, 2596948, 3356696, 746135, 1253976, 2597012, 3356760, 746199, 1254040, 2597076, 1270287, 3356824, 1254104, 3356888, 1393174, 1270351, 1653273, 1653337, 1663514, 1653401, 1393238, 858832, 1663578, 1270415, 867027, 1653465, 1393302, 1663642, 1270479, 1393366, 1663706],
    [2557953, 1867777, 327680, 327744, 327808, 327872, 458753, 458817, 458881, 2558017, 1867841, 458945, 2844177, 2163216, 2558081, 2269200, 2844241, 2425347, 2556434, 2558145, 2400274, 2974723, 590340, 2163280, 2697730, 2269264, 3105796, 2425411, 2556498, 2828288, 2400338, 2974787, 590404, 2163344, 2828352, 2269328, 3105860, 2556562, 2697794, 2400402, 2844305, 2425475, 2163408, 2828416, 2269392, 2974851, 590468, 2556626, 2828480, 2400466, 3105924, 2785807, 2697858, 2844369, 2425539, 2785871, 3090958, 2974915, 590532, 2785935, 3091022, 3105988, 1867905, 2697922, 1795605, 2785999, 3091086, 1795669, 3091150, 1867969, 1795733, 3475987, 1795797, 3607060, 1507851, 1656342, 3476051, 1507915, 1918487, 3607124, 1507979, 1656406, 3476115, 1508043, 1918551, 3607188, 1656470, 1638924, 3476179, 1918615, 1638988, 3607252, 1656534, 1639052, 1918679, 1639116],
    [1925120, 2056193, 1925184, 2056257, 1925248, 2056321, 1925312, 2056385, 1950222, 2557455, 352271, 2318350, 1950286, 2318414, 1950350, 2318478, 2712081, 2849298, 2211857, 2950675, 483346, 3212306, 1950414, 2980372, 2318542, 2605584, 3111445, 2950739, 483922, 3212370, 2980436, 614917, 3111509, 2950803, 483986, 3212434, 2980500, 614981, 3111573, 2950867, 484050, 3212498, 2980564, 615045, 3111637, 3737111, 352847, 615109, 2212433, 2711633, 2848850, 3737175, 2212497, 2711697, 2848914, 2557007, 352911, 2212561, 2711761, 2848978, 3737239, 2605648, 3373590, 2557071, 352975, 2605712, 3373654, 3737303, 2605776, 3373718, 2557135, 3367451, 3504155, 1771033, 3367515, 3504219, 2033178, 3367579, 3504283, 1771097, 3367643, 3504347, 2033242, 3373782, 1771161, 2062872, 2033306, 2062936, 1771225, 2063000, 2033370, 2063064],
    [354304, 335873, 344064, 475137, 344128, 475201, 344192, 475265, 344256, 467470, 354368, 475329, 354432, 598543, 320017, 606738, 467534, 354496, 320081, 606802, 2968080, 598607, 320145, 2968144, 335937, 582164, 467598, 2968208, 320209, 2968272, 598671, 870933, 336001, 606866, 870997, 467662, 868886, 606930, 871061, 598735, 868950, 871125, 336065, 869014, 1010199, 3211795, 869078, 1263630, 3211859, 1131032, 1262085, 582228, 1402881, 3211923, 1131096, 1262149, 582292, 1010263, 3211987, 1131160, 1262213, 582356, 1263694, 2957334, 1131224, 1262277, 1402945, 3088402, 1010327, 2957398, 1263758, 3088466, 1524235, 1491481, 1403009, 2957462, 1524299, 1491545, 1010391, 3088530, 1524363, 1491609, 1263822, 2957526, 1524427, 1491673, 1403073, 3088594, 1761818, 1777688, 1761882, 1777752, 1761946, 1777816, 1762010, 1777880],
    [2070528, 1941504, 2072577, 1941568, 2072641, 1941632, 2072705, 1311234, 1687554, 1941696, 2070592, 2072769, 369168, 1311298, 2081297, 2332688, 500243, 1843730, 2081361, 2070656, 500307, 1843794, 2081425, 2070720, 500371, 1843858, 2081489, 2341390, 500435, 1843922, 1958415, 2472468, 762375, 1687618, 2097171, 2341454, 762439, 2097235, 1958479, 2472532, 762503, 1688194, 2097299, 2341518, 762567, 2097363, 1958543, 2472596, 1155608, 369232, 1688258, 2621447, 2332752, 1155672, 369296, 2621511, 1958607, 2332816, 1155736, 369360, 1310850, 647701, 2332880, 1155800, 2621575, 778264, 2341582, 1310914, 647765, 2472660, 2621639, 778328, 2884119, 647829, 3146243, 778392, 2884183, 647893, 3146307, 778456, 909849, 2884247, 3146371, 1294870, 909913, 2884311, 3146435, 1294934, 909977, 1294998, 910041, 1295062],
    [370689, 2089985, 2031617, 360448, 360512, 360576, 360640, 491521, 491585, 491649, 494094, 2293774, 2090049, 491713, 625167, 2818063, 2090113, 494158, 2293838, 2090177, 771587, 625231, 2818127, 2294414, 370753, 1041922, 493710, 771651, 2818703, 2294478, 771715, 624783, 2818767, 370817, 1033733, 1026576, 2031681, 1033797, 1304081, 1026640, 2031745, 493774, 1304145, 2031809, 1304209, 1026704, 1376786, 1304273, 1026768, 1376850, 624847, 1041986, 1376914, 1409556, 1411603, 1033861, 1376978, 1540629, 1042050, 1673236, 771779, 1550357, 1409620, 1411667, 1033925, 1540693, 1042114, 1673300, 1550421, 1409684, 1411731, 1671691, 1540757, 1673364, 1671755, 1550485, 1671819, 1409748, 1411795, 1671883, 1540821, 370881, 1802765, 1673428, 1802829, 1550549, 1802893, 1802957],
    [1302528, 1302592, 1302656, 1302720, 1433601, 1433665, 2459138, 1433729, 1433793, 2349571, 2459202, 2349635, 2459266, 803341, 2349699, 385551, 2459330, 2506767, 2349763, 385615, 2852366, 516612, 2506831, 385679, 2852430, 2506895, 2873872, 385743, 2852494, 2506959, 2852558, 3136018, 2900497, 2351122, 3376660, 3136082, 3170835, 2351186, 3376724, 803405, 3376788, 3136146, 2351250, 1287692, 803469, 3376852, 3136210, 2900561, 2351314, 1418773, 2900625, 2873936, 1287756, 803533, 2874000, 1287820, 2900689, 2874064, 1287884, 3170899, 1440278, 1549847, 3170963, 1549911, 1440342, 3171027, 1418837, 1549975, 1440406, 1418901, 1440470, 1550039, 1418965, 516676, 516740, 516804],
    [2195457, 376832, 376896, 376960, 377024, 507905, 507969, 508033, 2589193, 508097, 2589257, 2589321, 2589385, 2869772, 1016330, 2869836, 1016394, 2869900, 1016458, 2869964, 2974223, 1016522, 903694, 2974287, 2195521, 2877968, 2974351, 2195585, 2878032, 2974415, 2195649, 2878096, 999954, 1286667, 2878160, 877075, 1278477, 649748, 1286731, 649812, 901636, 877139, 1278541, 1427985, 1163781, 1286795, 649876, 1401366, 901700, 1278605, 649940, 1000018, 1163845, 1286859, 1401430, 911893, 901764, 1278669, 1428049, 1000082, 1163909, 903758, 877203, 901828, 1401494, 911957, 1163973, 1428113, 1000146, 903822, 877267, 1425927, 1401558, 912021, 1425991, 1428177, 1426055, 903886, 1426119, 912085],
    [1448960, 1975296, 1975360, 1975424, 1975488, 2106369, 2106433, 1852940, 2106497, 1449024, 2106561, 681486, 1449088, 2795023, 681550, 1449152, 2795087, 681614, 531984, 2655761, 664593, 681678, 532048, 2655825, 664657, 1853004, 532112, 2655889, 664721, 1853068, 532176, 2795151, 1058323, 1853132, 1973267, 2655953, 664785, 1058387, 2508301, 1973331, 2795215, 1058451, 2508365, 1973395, 3319302, 1058515, 2508429, 1973459, 3319366, 2508493, 2366999, 3319430, 935442, 2367063, 3319494, 935506, 2367127, 1082902, 935570, 1082966, 935634, 2367191, 1083030, 1083094, 1328665, 3022345, 1319945, 1451033, 1877524, 1328729, 3022409, 1320009, 1451097, 1877588, 1328793, 3022473, 1320073, 1451161, 1877652, 1328857, 3022537, 1320137, 1451225, 1877716, 1056282, 1738264, 1056346, 1869333, 1056410, 1738328, 1056474, 1869397, 1738392, 1869461, 1738456, 1869525],
    [369665, 1573888, 1573952, 1574016, 1574080, 1704961, 1705025, 2384399, 1705089, 369729, 1705153, 263697, 2384463, 394754, 369793, 263761, 2384527, 525842, 369857, 656899, 2384591, 2729491, 525906, 934416, 2729555, 2895366, 394818, 811527, 2360327, 2729619, 656963, 811591, 2360391, 2729683, 919060, 2895430, 2360967, 811143, 2982929, 536085, 2361031, 811207, 3507716, 919124, 2895494, 1050121, 1073161, 3638287, 919188, 536149, 1050185, 1073225, 2982993, 919252, 2895558, 525970, 1073801, 1049737, 3507780, 3288598, 394882, 1073865, 1049801, 3638351, 3419671, 263825, 934480, 657027, 2983057, 3419735, 526034, 934544, 3507844, 3419799, 263889, 934608, 394946, 3638415, 3419863, 657091, 1196050, 2983121, 3550744, 1458178, 3507908, 3288662, 1589251, 3638479, 3550808, 1196114, 1680404, 3288726, 1458242, 1942544, 3550872, 1589315, 1680468, 3288790, 1196178, 1942608, 3550936, 1458306, 1680532, 536213, 1589379, 1942672, 536277, 1196242, 1680596, 1458370, 1942736, 1589443],
    [285696, 1598464, 1729537, 1598528, 1729601, 1598592, 1729665, 1442316, 1598656, 556033, 1729729, 419330, 1442380, 687629, 2254350, 419394, 1442444, 678926, 812548, 1442508, 818188, 714255, 812612, 663566, 285760, 419458, 687693, 812676, 556097, 664142, 2253902, 419522, 678990, 664206, 2253966, 1107472, 818252, 664270, 2254030, 714319, 679054, 795155, 714383, 1334802, 795219, 714447, 1211411, 795283, 3204625, 1334866, 795347, 3204689, 1211475, 943623, 3204753, 1334930, 943687, 3204817, 285824, 943751, 1623573, 812740, 687757, 943815, 1107536, 1211539, 1205768, 1623637, 1336841, 556161, 1467915, 1107600, 1336905, 818316, 1205832, 1623701, 1336969, 1334994, 1467979, 1107664, 1337033, 679118, 1205896, 1623765, 285888, 1468043, 1893908, 687821, 1205960, 2024982, 1211603, 1468107, 1893972, 556225, 2025046, 818380, 1894036, 2025110, 1894100, 2025174],
    [271360, 377856, 1590273, 1590337, 1590401, 1590465, 1721344, 1721408, 1721472, 2369036, 517645, 1721536, 2387470, 402445, 517709, 2387534, 411140, 2369100, 517773, 673285, 2649093, 411204, 271424, 779792, 673349, 2780164, 411268, 910865, 402509, 673413, 804371, 2649157, 411332, 2491411, 2868754, 673477, 804435, 2780228, 2491475, 2868818, 804499, 2649221, 2491539, 2868882, 804563, 2780292, 2491603, 2868946, 2649285, 910929, 2369164, 2780356, 910993, 271488, 2387598, 911057, 402573, 2387662, 2369228, 779856, 1068564, 271552, 779920, 1330710, 403149, 779984, 1207832, 3409423, 517325, 1338901, 3409487, 377920, 1068628, 3409551, 377984, 1330774, 3409615, 378048, 1207896, 1713687, 1434636, 1338965, 1442817, 1565697, 1068692, 1713751, 1434700, 1330838, 1442881, 1565761, 1207960, 1713815, 1434764, 1339029, 1442945, 1565825, 1068756, 1713879, 1434828, 1330902, 1443009, 1565889, 1208024, 1339093],
    [302080, 2139136, 2139200, 2139264, 2139328, 2270209, 2270273, 2270337, 2145808, 2270401, 312850, 2426370, 572945, 312914, 2426434, 302144, 312978, 2426498, 2145872, 313042, 2426562, 573009, 2942483, 304147, 302208, 992789, 2934275, 566806, 697879, 2530836, 3343896, 3073046, 304723, 2530900, 2942035, 566870, 697943, 2145936, 992853, 3073110, 304787, 573073, 3343960, 2942099, 566934, 698007, 2530964, 984601, 3073174, 304851, 302272, 992917, 3073750, 566486, 698071, 2146000, 3344024, 2942163, 573137, 1377819, 3195927, 2531028, 992981, 2934339, 3194372, 828936, 3344088, 3195991, 3324951, 829000, 984665, 2934403, 1353226, 1484316, 3194436, 829064, 1377883, 3196055, 1353290, 1484380, 3325015, 829128, 984729, 2934467, 1353354, 1484444, 3194500, 1377947, 3196119, 1353418, 1484508, 3325079, 984793, 1885722, 3194564, 1378011, 2016284, 3325143, 1885786, 1743873, 2016348, 1743937, 1885850, 1744001, 2016412, 1744065, 1885914, 2016476],
    [1836032, 2130944, 2262017, 2131008, 2262081, 2131072, 2262145, 2286096, 2131136, 1836096, 2262209, 427538, 2286160, 1836160, 427602, 2286224, 1836224, 2797075, 427666, 2286288, 926721, 3059222, 427730, 2810389, 926785, 3182100, 689687, 2810453, 926849, 3452440, 820739, 2940951, 926913, 3452504, 689751, 3072018, 1189393, 3452568, 820803, 2941015, 1189457, 3452632, 689815, 2810517, 1189521, 2797139, 820867, 3072082, 1189585, 3182164, 689879, 2810581, 3023875, 3714585, 820931, 2941079, 3023939, 3059286, 3072146, 3024003, 3714649, 2941143, 3024067, 2797203, 3072210, 3277840, 3059350, 1237530, 3277904, 3714713, 1237594, 3277968, 3182228, 1237658, 3278032, 2797267, 1237722, 1311763, 1607182, 3059414, 1311827, 1607246, 3714777, 1499675, 1311891, 1607310, 3182292, 1499739, 1311955, 1607374, 1499803, 1499867],
    [2581504, 1998849, 2155521, 2155585, 2155649, 2155713, 2286592, 2286656, 2285072, 2286720, 2581568, 1998913, 2286784, 2285136, 2581632, 1998977, 2285200, 2581696, 1999041, 583170, 2549267, 2285264, 2573314, 2261522, 583234, 2549331, 2678289, 2573378, 696852, 583298, 2549395, 2678353, 2573442, 2261586, 583362, 2549459, 2678417, 845315, 2573506, 2261650, 845379, 2678481, 3097620, 2261714, 845443, 712214, 3367953, 1081366, 845507, 842772, 696916, 3097684, 1104914, 696980, 3097748, 842836, 697044, 3097812, 1236503, 3368017, 1236567, 3368081, 1104978, 3368145, 1236631, 3359763, 1090072, 1375256, 3359827, 1081942, 711766, 3359891, 1090136, 1762828, 1375320, 3359955, 1082006, 711830, 2057749, 1090200, 1762892, 842900, 2057813, 1082070, 1105042, 2057877, 1090264, 1762956, 1375384, 2057941, 1236695, 1763020, 711894, 842964, 1105106, 1375448],
    [287745, 295937, 1887233, 2147329, 2147393, 2147457, 2147521, 2278400, 2278464, 2278528, 550416, 296001, 1887297, 2278592, 550480, 296065, 1887361, 550544, 296129, 1887425, 3057169, 550608, 323090, 435200, 2647556, 323154, 3057233, 2909699, 445971, 435264, 2647620, 446035, 837142, 3057297, 3337238, 2909763, 435328, 2647684, 323218, 968215, 3057361, 3171351, 446099, 837206, 1099272, 435392, 3337302, 2909827, 968279, 3171415, 3573253, 446163, 837270, 3337366, 2647748, 3573317, 968343, 3171479, 3573381, 323282, 968407, 1361432, 2909891, 3573445, 3337942, 836822, 1361496, 3171543, 1091092, 1361560, 1197073, 1615381, 1361624, 1197137, 1745944, 1197201, 1091156, 1099336, 1197265, 1615445, 287809, 1746008, 1099400, 287873, 1091220, 287937, 1615509, 1099464, 1746072, 1091284, 1615573, 1746136],
    [2171904, 2171968, 2172032, 2172096, 2302977, 2303041, 2303105, 2303169, 607760, 336912, 597521, 2598418, 878099, 730644, 2440707, 2598482, 2835972, 2440771, 2598546, 2966548, 597585, 869909, 2598610, 861718, 2440835, 1017368, 869973, 990743, 870037, 3245078, 861782, 2440899, 1123865, 1017432, 2836036, 990807, 2967124, 3245142, 861846, 730196, 3087898, 337488, 1017496, 2836100, 3087962, 337552, 1123929, 2967188, 3245206, 861910, 730260, 3088026, 337616, 1017560, 2836164, 3088090, 1262617, 3245270, 730836, 1252891, 1123993, 2966740, 3777561, 1383965, 3777625, 1525276, 1252955, 607312, 3777689, 1384029, 1124057, 1262681, 3777753, 990871, 1525340, 1253019, 878163, 597649, 607376, 1384093, 1262745, 990935, 1525404, 1253083, 878227, 597713, 870101, 1384157, 607440, 1262809, 1525468, 878291],
    [2393088, 2567169, 2829840, 2393152, 2179601, 329234, 2295315, 2393216, 2960402, 2310163, 2819587, 2295379, 2829904, 2393280, 2703363, 722436, 2295443, 2524176, 2829968, 2834436, 2819651, 2295507, 329298, 2917377, 2960466, 2703427, 722500, 3081749, 2524240, 2830032, 2834500, 2819715, 3081813, 329362, 2917441, 2960530, 2703491, 722564, 3081877, 2524304, 3485204, 853511, 2834564, 2819779, 3081941, 329426, 2917505, 2960594, 2703555, 722628, 2524368, 2567233, 2834628, 2917569, 3485268, 853575, 2310227, 2567297, 3441685, 2310291, 3441749, 3485332, 2310355, 1115658, 2567361, 3441813, 853639, 2179665, 1246731, 3441877, 3485396, 2179729, 1115722, 1344529, 3746833, 2179793, 1246795, 1344593, 3746897, 853703, 3620885, 1115786, 1344657, 3746961, 3620949, 1246859, 1344721, 3747025, 3621013, 1115850, 3476487, 3621077, 1246923, 3476551, 3498518, 3476615, 3498582, 3476679, 3498646, 3498710, 1786391, 1786455, 1786519, 1786583],
    [2186240, 1958913, 2188288, 2188352, 2188416, 2188480, 2319361, 2319425, 2319489, 2186304, 1958977, 2319553, 2186368, 1959041, 615939, 1959105, 2325507, 2949650, 616003, 2606608, 2325571, 1009157, 2448389, 2606672, 2695700, 1139732, 1009221, 2579987, 2606736, 852501, 1140308, 1009285, 2580051, 2606800, 2695252, 1140372, 616067, 2325635, 2695316, 1140436, 1009349, 2448453, 2695380, 2614807, 616131, 2325699, 991766, 2580115, 2614871, 852565, 2448517, 2614935, 2949714, 2580179, 2614999, 2949778, 2448581, 2949842, 3112465, 1516056, 3112529, 1516120, 3112593, 1516184, 2876953, 3112657, 1516248, 2877017, 2186432, 991830, 2877081, 852629, 2877145, 991894, 852693, 991958],
    [355328, 320513, 2434049, 2180097, 2180161, 2180225, 2180289, 452112, 459792, 355392, 2311699, 452176, 459856, 355456, 2311763, 452240, 355520, 2434113, 2311827, 2575379, 459920, 452304, 2311891, 2575443, 443921, 2434177, 2715158, 459984, 443985, 2977303, 444049, 2434241, 2715222, 3474449, 444113, 2977367, 3474513, 1238546, 2575507, 3474577, 1369620, 2715286, 3474641, 320577, 1000986, 2977431, 1385472, 1238610, 2575571, 1369684, 1517080, 2715350, 1385536, 320641, 2977495, 1238674, 1517144, 1394189, 1001050, 1527321, 1385600, 1369748, 1394253, 1527385, 320705, 1517208, 1394317, 1001114, 1527449, 1385664, 1238738, 1394381, 1001178, 1527513, 1369812, 1517272, 1788944, 1909786, 1797121, 2041365, 2049551, 1789008, 1909850, 2049615, 1797185, 2041429, 2049679, 1789072, 1909914, 2049743, 1797249, 2041493, 1789136, 1909978, 1797313, 2041557],
    [2204672, 2335745, 2204736, 2335809, 2204800, 2335873, 2221584, 2204864, 2335937, 501265, 2221648, 2098706, 2211330, 501329, 2221712, 2098770, 2211394, 501393, 2221776, 2098834, 2211458, 501457, 2737169, 2098898, 2473492, 2860548, 2737233, 2762261, 2604036, 2860612, 2737297, 2762325, 2604100, 2860676, 2737361, 2762389, 2604164, 2860740, 1164819, 2893319, 2604228, 763414, 1295382, 894487, 3016217, 2211522, 1025562, 1557530, 894551, 3016281, 2473556, 1156635, 1688603, 894615, 3016345, 2473620, 763478, 1295446, 894679, 3154967, 2473684, 1025626, 1557594, 3016409, 3382808, 1156699, 1688667, 2893383, 3382872, 763542, 1164883, 3155031, 3382936, 1025690, 1295510, 2893447, 3383000, 1156763, 1557658, 3155095, 763606, 1688731, 2893511, 1025754, 1164947, 3155159, 1156827, 1295574, 2762453, 1811979, 1557722, 1812043, 1688795, 1812107, 1165011, 1812171],
    [2163713, 2329601, 2196480, 2196544, 2196608, 2196672, 468496, 2329665, 1819138, 2589698, 362002, 599569, 2329729, 1695762, 2590274, 362066, 468560, 2329793, 1695826, 2590338, 362130, 363536, 599633, 1695890, 2590402, 362194, 363600, 468624, 1695954, 363664, 599697, 2474517, 468688, 363728, 2474581, 3517971, 599761, 1818690, 3518035, 2163777, 2474645, 3518099, 2163841, 1818754, 3518163, 2163905, 2474709, 887825, 1254934, 1818818, 887889, 1648152, 2875930, 1279002, 887953, 1779225, 2875994, 1279066, 888017, 1254998, 2998787, 1410587, 1648216, 3910683, 2876058, 1279130, 1779289, 1551900, 2998851, 1410651, 1255062, 3910747, 2876122, 1279194, 1648280, 1551964, 2998915, 1410715, 1779353, 3910811, 2998979, 1410779, 1255126, 3910875, 1040916, 1672716, 1648344, 1552028, 1040980, 1803790, 1779417, 1552092, 1041044, 1672780, 1041108, 1803854, 1171991, 1672844, 1934863, 1172055, 1803918, 1934927, 1172119, 1672908, 1934991, 1172183, 1803982, 1935055],
    [1432576, 1860609, 2064385, 1696768, 1827841, 1696832, 1827905, 1696896, 1827969, 1696960, 1695247, 1860673, 2064449, 1828033, 386562, 1695311, 1860737, 2064513, 1695375, 1860801, 2064577, 1695439, 2227730, 2778643, 2227794, 893460, 2778707, 2227858, 893524, 2778771, 1173013, 2227922, 3244053, 2778835, 1173077, 2481680, 3244117, 2639383, 1173141, 2620945, 3244181, 2639447, 1173205, 1432640, 3244245, 2639511, 2481744, 1417750, 2639575, 2621009, 1417814, 1432704, 893588, 2481808, 893652, 2621073, 1432768, 1417878, 2481872, 1417942, 386626, 2621137, 1548813, 386690, 1548877, 386754, 1548941, 1549005, 1679886, 1679950, 1680014, 1680078],
    [2466817, 484353, 2081792, 2081856, 2081920, 2081984, 2212865, 2212929, 2212993, 476685, 2466881, 2213057, 2608654, 476749, 2466945, 2739728, 509443, 738320, 2467009, 2739792, 509507, 738384, 624140, 640529, 2739856, 509571, 738448, 624204, 640593, 2739920, 624268, 476813, 519698, 902662, 738512, 624332, 519762, 3114511, 476877, 2608718, 3114575, 1401868, 519826, 3114639, 1532945, 519890, 3114703, 1664516, 2608782, 1426953, 902726, 1401932, 3515396, 2608846, 1427017, 902790, 484417, 3515972, 640657, 912915, 1427081, 902854, 1132052, 3646481, 912979, 1427145, 1132116, 3516036, 640721, 913043, 3646545, 1533009, 913107, 1664068, 3516100, 509635, 1401996, 3646609, 484481, 3646673, 1560085, 1132180, 1541637, 1560149, 1533073, 1541701, 1560213, 1541765, 1664132, 1560277, 1402060, 1541829, 2073600, 484545, 2073664, 1132244, 2073728, 1533137, 2073792, 1664196],
    [1048576, 2377729, 1976320, 1976384, 1976448, 1976512, 2001420, 1048640, 2377793, 2001484, 1048704, 2779650, 2001548, 1048768, 543246, 2001612, 1835533, 543310, 2533906, 1835597, 543374, 666131, 2533970, 1835661, 543438, 666195, 2534034, 1835725, 2779714, 2534098, 2228225, 2779778, 3058193, 2779842, 2359315, 3058257, 2228289, 2377857, 3058321, 2377921, 2359379, 928277, 666259, 3058385, 2228353, 1198612, 928341, 666323, 3181071, 2359443, 1198676, 928405, 3181135, 2228417, 1198740, 928469, 3181199, 2359507, 1198804, 3181263, 2752533, 1468950, 1190408, 3574288, 1469014, 3015174, 1190472, 3574352, 2752597, 1853975, 1190536, 3574416, 3015238, 1854039, 1190600, 3574480, 2752661, 1993240, 3015302, 1993304, 2752725, 1469078, 3015366, 1854103, 1993368, 1469142, 1854167, 1993432],
    [2240512, 362497, 1574913, 1574977, 1575041, 1575105, 1705984, 1706048, 1706112, 2240576, 362561, 1706176, 2240640, 362625, 395778, 2240704, 2721794, 2518531, 395842, 2721858, 2764803, 544273, 395906, 2721922, 2765379, 2903570, 395970, 2721986, 397843, 544337, 362689, 2765443, 2903634, 3254799, 2896404, 2903698, 3254863, 2896468, 544401, 526854, 3254927, 657941, 2896532, 2903762, 526918, 3254991, 658005, 2896596, 544465, 526982, 3377158, 658069, 2518083, 2765507, 527046, 3377222, 397907, 2518147, 920072, 3377286, 658133, 2518211, 397971, 920136, 3377350, 3697672, 398035, 920200, 1542144, 3697736, 1192471, 920264, 1935888, 3697800, 1182232, 3639320, 3697864, 1192535, 1182296, 3639384, 1854998, 1192599, 1182360, 3639448, 1855062, 1192663, 1182424, 3639512, 1855126, 1542208, 1855190, 1935952, 1986073, 1542272, 1986137, 1936016, 1986201, 1542336, 1986265, 1936080, 2066453, 2066517, 2066581, 2066645],
    [2121728, 2123777, 2123841, 2123905, 2123969, 2254848, 2254912, 1838608, 2254976, 2121792, 2255040, 2681362, 1838672, 2121856, 2681426, 1838736, 2121920, 3197459, 1838800, 2376209, 2910742, 3197523, 265238, 2908161, 2910806, 3197587, 265302, 2376273, 2910870, 3197651, 265366, 2908225, 2910934, 3721751, 265430, 2376337, 3721815, 2625028, 2908289, 3721879, 2625092, 2376401, 3721943, 527896, 2908353, 2681490, 527960, 1204240, 2681554, 528024, 1204304, 1239573, 813577, 528088, 1204368, 1239637, 813641, 2625156, 1204432, 1501722, 813705, 2625220, 944650, 3162116, 1501786, 813769, 1052185, 944714, 3162180, 1239701, 944778, 1584660, 3162244, 1501850, 944842, 1052249, 3162308, 1862157, 1239765, 1584724, 1862221, 1501914, 1052313, 1862285, 1584788, 1862349, 1052377, 1584852],
    [1959937, 2115585, 2115649, 2115713, 2115777, 2246656, 2246720, 2107920, 2246784, 1960001, 2246848, 281107, 403986, 411666, 2222609, 412242, 2370050, 2222673, 3043860, 2770964, 412306, 403538, 2222737, 2904597, 2771540, 412370, 2370114, 1960065, 3043412, 2771604, 674327, 403602, 3131415, 3043476, 2771668, 674391, 2370178, 3131479, 3437059, 674455, 403666, 3131543, 3437123, 674519, 2370242, 3131607, 2904661, 805381, 2754583, 3655685, 2904725, 936474, 805445, 2754647, 3655749, 2904789, 805509, 2754711, 3655813, 936538, 3437187, 805573, 2754775, 3655877, 936602, 3043540, 2107984, 3140121, 936666, 3437251, 281171, 2108048, 3140185, 3559958, 281235, 2108112, 3140249, 3560022, 281299, 3287059, 3140313, 3560086, 3287123, 2222801, 3560150, 3287187, 1960129, 3830296, 3287251, 1042432, 3830360, 1714202, 1042496, 3830424, 1714266, 1042560, 3830488, 1714330, 1042624, 1714394, 1566741, 1566805, 1566869, 1566933],
    [557056, 1615873, 1615937, 1616001, 1616065, 1746944, 1747008, 1747072, 557120, 1747136, 2673166, 557184, 2009616, 2935301, 436740, 950799, 2009680, 3065860, 436804, 950863, 2009744, 2935365, 950927, 723476, 2009808, 3065924, 950991, 2796053, 2959381, 567814, 707090, 557248, 2796117, 2959445, 2673230, 827408, 2796181, 2959509, 707154, 436868, 827472, 2796245, 2959573, 567878, 3065988, 436932, 827536, 723540, 567942, 3066052, 827600, 723604, 2935429, 3047953, 723668, 2935493, 3048017, 568006, 3344919, 2673294, 3048081, 3344983, 1362456, 3048145, 3345047, 1362520, 1475084, 3345111, 1362584, 1605633, 1649178, 707218, 1352205, 1649242, 1362648, 1475148, 1649306, 2673358, 1605697, 1649370, 707282, 1352269, 3738139, 1894931, 1485322, 1475212, 3738203, 2026006, 1485386, 1605761, 3738267, 1894995, 1485450, 1352333, 3738331, 2026070, 1485514, 1475276, 2042393, 1895059, 1605825, 2042457, 2026134, 1352397, 2042521, 1895123, 2042585, 2026198],
    [2404352, 264193, 1607680, 1738753, 1607744, 1738817, 1607808, 1738881, 1607872, 2404416, 272908, 1738945, 2420238, 297474, 428046, 2404480, 272972, 2404544, 273036, 2525712, 273100, 438288, 2944529, 2656273, 264257, 3060242, 2944593, 2525776, 2656337, 264321, 438352, 2944657, 2656401, 264385, 3191316, 2944721, 2656465, 796672, 3191380, 585238, 796736, 3191444, 585302, 796800, 3191508, 2420302, 428110, 796864, 1094163, 2420366, 2525840, 428174, 1059343, 1094227, 585366, 1059407, 1094291, 585430, 2525904, 1059471, 1094355, 952838, 1059535, 1085975, 297538, 3156493, 1083912, 1086039, 1109528, 952902, 3156557, 1083976, 1086103, 297602, 3156621, 1084040, 1086167, 1109592, 952966, 3156685, 1084104, 438416, 297666, 1443858, 1214985, 438480, 1109656, 953030, 428750, 1845781, 1215049, 3452949, 2419918, 1477130, 1444434, 1215113, 3059794, 1109720, 1477194, 1845845, 1215177, 3453013, 1477258, 1444498, 3059858, 1477322, 1845909, 3453077, 1444562, 3059922, 1845973, 3453141],
    [2156545, 2156609, 2156673, 2156737, 2287616, 2287680, 2417168, 2287744, 2287808, 2417232, 2574867, 306690, 451090, 2574931, 306754, 451154, 2943510, 485909, 691715, 451218, 3074583, 3099161, 452633, 691779, 451282, 2943574, 3230232, 699930, 2417296, 3074647, 3230296, 699994, 2417360, 715269, 3099225, 452697, 830469, 3064337, 1002012, 691843, 3194902, 715333, 1002076, 453273, 830533, 3325975, 3074711, 1002140, 700058, 977438, 3064401, 3074775, 453337, 1002204, 1215518, 977502, 3194966, 2943638, 3098777, 1215582, 977566, 3326039, 1108488, 2943702, 3098841, 1215646, 977630, 3064465, 1108552, 2574995, 1215710, 1108616, 3195030, 1370634, 3230360, 1477640, 1108680, 3326103, 1370698, 2575059, 1747978, 3064529, 1370762, 3230424, 1477704, 3195094, 715397, 3885595, 1748042, 3326167, 1370826, 3885659, 1477768, 1753620, 3885723, 306818, 1630749, 715461, 3885787, 1748106, 1753684, 485973, 830597, 1630813, 486037, 691907, 1753748, 486101, 1477832, 1630877, 306882, 1753812, 1748170, 1630941, 830661, 700122],
    [2385921, 2148353, 2148417, 2148481, 2148545, 2279424, 2279488, 2132496, 2279552, 2385985, 2279616, 2421265, 2542098, 2132560, 313875, 2386049, 2421329, 2542162, 2132624, 313939, 2386113, 2804244, 2421393, 2542226, 2132688, 444949, 3041297, 2804308, 2421457, 2542290, 821269, 445013, 3041361, 2936852, 3459586, 2926594, 445077, 3041425, 2936916, 3459650, 2926658, 3041489, 848408, 821333, 681984, 848472, 821397, 682048, 838150, 848536, 3459714, 2926722, 682112, 848600, 3459778, 2926786, 314003, 682176, 838214, 1241106, 969242, 445141, 821461, 3295250, 1372697, 969306, 314067, 698387, 3295314, 2804372, 2936980, 838278, 969370, 960538, 3295378, 2804436, 2937044, 838342, 969434, 698451, 3295442, 1241170, 960602, 1337878, 1372761, 698515, 1600023, 1241234, 960666, 1337942, 1888795, 698579, 1600087, 1888859, 960730, 1338006, 1888923, 1600151, 1372825, 1338070, 1241298, 1600215, 1372889, 1888987],
    [2467840, 2170881, 2172928, 2172992, 2173056, 2173120, 2467904, 2433552, 2312721, 2566675, 2467968, 2170945, 2844691, 2566739, 2468032, 2433616, 2844755, 2566803, 2983937, 2171009, 2844819, 2566867, 2984001, 2433680, 2844883, 469507, 2984065, 2171073, 2312785, 469571, 2984129, 2433744, 2312849, 469635, 3115542, 983570, 2312913, 469699, 3246096, 1114644, 3115606, 983634, 3246160, 1114708, 879127, 3246224, 1122840, 3754008, 3115670, 1122904, 3754072, 3246288, 983698, 3754648, 3516949, 1114772, 1124889, 1525785, 3115734, 1122456, 1124953, 1525849, 3648006, 983762, 1125017, 1525913, 3517013, 1114836, 1125081, 3754712, 3648070, 1122520, 1525977, 3517077, 1796634, 3648134, 1927707, 3517141, 1796698, 3648198, 1770012, 879191, 1770076, 1927771, 1770140, 1796762, 1770204, 879255, 1927835, 1796826, 879319, 1927899],
    [305152, 1773569, 2164737, 2164801, 2164865, 2164929, 2295808, 2295872, 2295936, 690704, 1773633, 2296000, 330257, 1773697, 2140177, 330321, 690768, 1773761, 330385, 2568208, 2140241, 2820610, 330449, 2568272, 2664450, 2820674, 880148, 2951188, 2568848, 2664514, 2820738, 2846229, 2568912, 2664578, 2820802, 2846293, 2664642, 2961938, 854532, 880212, 2951252, 690320, 3223556, 854596, 2846357, 2140305, 3223620, 854660, 2846421, 690384, 3223684, 854724, 880276, 2951316, 2140369, 3223748, 1265174, 829441, 2962002, 1265238, 305216, 2962066, 880340, 2951380, 829505, 2962130, 1265302, 1380883, 305280, 3493384, 1380947, 829569, 3493448, 1381011, 305344, 3493512, 1381075, 829633, 1903116, 3886092, 1389079, 1345554, 1903180, 3886156, 1389143, 1345618, 1903244, 3886220, 1389207, 1345682, 1903308, 3886284, 1389271, 1345746, 3493576, 1265366, 2051608, 2051672, 2034191, 2051736, 2034255, 2051800, 2034319, 2034383],
    [2189313, 2189377, 2189441, 2189505, 2320384, 2320448, 2320512, 2320576, 2581008, 2581072, 3091985, 2713617, 2607634, 2975762, 2581136, 470547, 3107348, 2581200, 2559509, 3107412, 2965524, 2559573, 3107476, 2965588, 2559637, 772613, 3107540, 2965652, 2714193, 2559701, 616984, 3394073, 2965716, 2714257, 2821654, 617048, 3228183, 748038, 2714321, 2821718, 3394137, 3228247, 748102, 3091537, 3631623, 3394201, 3235847, 748166, 2821782, 3631687, 3009051, 3235911, 748230, 3091601, 3631751, 2607698, 2975826, 3235975, 1141256, 2821846, 3631815, 772677, 1272348, 3236039, 1141320, 3091665, 3009115, 1272412, 3228311, 1141384, 470611, 2607762, 1272476, 2975890, 3228375, 1141448, 470675, 780811, 1531928, 1519130, 617112, 3009179, 1531992, 470739, 780875, 1532056, 1519194, 617176, 3394265, 1272540, 2976466, 1532120, 1912349, 2607314, 1654812, 1912413, 3009243, 1654876, 1912477, 1305102, 2058254, 1654940, 1519258, 1305166, 2058318, 1655004, 1912541, 772741, 2058894, 1519322, 1304718, 2058958, 780939, 772805, 1304782, 781003],
    [2549761, 2445313, 2435600, 2549825, 2445377, 346642, 2435664, 2847234, 2812433, 477715, 337939, 2847298, 2812497, 477779, 338003, 2847362, 2812561, 2837013, 477843, 338067, 2847426, 3205141, 2837077, 477907, 338131, 3205205, 2445441, 2837141, 608771, 600600, 3205269, 2445505, 2837205, 600664, 3205333, 741393, 3492377, 600728, 741457, 2549889, 3492441, 600792, 741521, 2812625, 3492505, 346706, 2435728, 741585, 2549953, 3492569, 346770, 2435792, 1099776, 3231744, 346834, 3222043, 1099840, 3231808, 3222107, 1099904, 3231872, 3222171, 1099968, 3231936, 3222235, 1397268, 3598874, 1517586, 1397332, 3598938, 1779737, 1397396, 3599002, 1517650, 1397460, 1886743, 1779801, 1790486, 1886807, 1517714, 1790550, 1886871, 1779865, 1790614, 3599066, 1517778, 1790678, 1886935, 1779929, 608835, 608899, 608963],
    [1933312, 2344960, 1968129, 2205696, 2205760, 2205824, 2205888, 2336769, 2336833, 2336897, 1933376, 2345024, 2230800, 2336961, 2730514, 2345088, 2720273, 2361362, 2730578, 2345152, 2720337, 2361426, 2730642, 1933440, 2738690, 2361490, 2730706, 641556, 2720401, 2361554, 2992662, 1933504, 2230864, 641620, 2992726, 2230928, 641684, 2720465, 2992790, 2230992, 641748, 2466325, 2992854, 2738754, 1968193, 2466389, 2738818, 1968257, 2466453, 3385880, 2738882, 1968321, 2466517, 3786774, 2885656, 3385944, 3786838, 2885720, 3386008, 3786902, 2885784, 3025431, 3786966, 3386072, 2885848, 3271187, 3025495, 3271251, 1419787, 3025559, 3271315, 1813006, 3025623, 3271379, 1559065, 1452570, 1559129, 1452634, 1559193, 1452698, 1559257, 1452762, 1419851, 1436187, 1813070, 1436251, 1419915, 1436315, 1813134, 1436379, 1419979, 1813198],
    [372737, 2304001, 1960961, 2197504, 2197568, 2197632, 2197696, 2328577, 2328641, 2328705, 2732560, 2354192, 2304065, 2328769, 2354768, 2863633, 2304129, 2863697, 1961025, 2304193, 2354832, 460800, 2863761, 460864, 2863825, 1961089, 3256850, 2354896, 460928, 3256914, 460992, 1961153, 985104, 2732112, 3009536, 3256978, 3009600, 1247763, 756230, 887320, 3082264, 2732176, 3009664, 1018375, 887384, 3082328, 3257042, 3009728, 756294, 1018439, 887448, 3082392, 2732240, 781844, 887512, 3082456, 1413654, 781908, 756358, 1018503, 1413718, 781972, 1640983, 1018567, 1413782, 782036, 1255957, 756422, 985168, 1413846, 1166874, 1806873, 1247827, 1806937, 1641047, 1429019, 372801, 1256021, 1166938, 985232, 1807001, 1429083, 372865, 1247891, 1167002, 1807065, 1641111, 1429147, 372929, 1256085, 1167066, 985296, 1429211, 1247955, 1641175, 1256149],
    [1697792, 1697856, 1697920, 1697984, 1828865, 1828929, 2731535, 1828993, 1829057, 2648593, 2731599, 2648657, 2731663, 2648721, 2731727, 2648785, 2985490, 551443, 2343444, 2484244, 2985554, 387605, 3172373, 2736644, 518148, 2985618, 387669, 3172437, 2736708, 518212, 2985682, 387733, 3172501, 2736772, 518276, 3509783, 387797, 3172565, 2482710, 518852, 3509847, 1067545, 2736324, 2484820, 3509911, 2342996, 2484884, 3509975, 1067609, 2343060, 2484948, 3649040, 1067673, 2343124, 3649104, 1329692, 3007000, 3649168, 1329756, 2482774, 3649232, 1329820, 3007064, 1420827, 1329884, 2482838, 1420891, 1731101, 3007128, 1420955, 551507, 2482902, 1421019, 1731165, 3007192, 1936922, 1731229, 1174027, 2076190, 551571, 1174091, 1936986, 1067737, 1174155, 2076254, 1731293, 1174219, 1937050, 551635, 2076318, 1937114, 2076382],
    [2451457, 2459649, 2082816, 2082880, 2082944, 2083008, 2583052, 2459713, 379406, 2583116, 2459777, 379470, 2583180, 2459841, 2355727, 510480, 501776, 2583244, 510544, 632846, 3238413, 512529, 510608, 501840, 3238477, 512593, 379534, 632910, 3238541, 501904, 3238605, 2880019, 632974, 2451521, 2880083, 2451585, 2880147, 1280532, 3524628, 2451649, 1034773, 2880211, 1157141, 3525204, 1132544, 1034837, 1157205, 1132608, 1034901, 1280084, 1132672, 913942, 1034965, 1157269, 1132736, 2355791, 1165828, 1280660, 3524756, 1296919, 1534482, 1165892, 2355855, 1288215, 3525332, 1296983, 1534546, 914006, 1288279, 1297047, 1788440, 1165956, 2355919, 1288343, 1297111, 1788504, 1166020, 1157333, 510672, 1534610, 914070, 1288407, 379598, 1788568, 501968, 1690119, 1534674, 512657, 633038, 1690183, 1788632, 512721, 1280212, 1690247, 914134, 1690311],
    [2378752, 2272256, 1967628, 2378816, 2272320, 1967692, 2272384, 2641421, 2229774, 2272448, 2641485, 2229838, 2641549, 2927617, 2229902, 2641613, 2927681, 1967756, 273937, 2378880, 2927745, 2229966, 2378944, 2927809, 1967820, 3313154, 3173388, 2754064, 274001, 3313218, 3173452, 667154, 2885139, 798211, 3313282, 3173516, 3157524, 929301, 2885203, 3313346, 3173580, 3157588, 929365, 2885267, 274065, 674834, 1084943, 929429, 2885331, 936981, 3706372, 929493, 3146772, 1060357, 1191446, 3706436, 1199126, 798275, 3146836, 1322502, 1191510, 3706500, 1592337, 667218, 2754128, 1060421, 798339, 674898, 3706564, 1191574, 3157652, 798403, 3146900, 1322566, 1191638, 937045, 1085007, 3157716, 667282, 2754192, 1060485, 274129, 1085071, 1199190, 1322630, 3146964, 1085135, 1592401, 667346, 2754256, 1060549, 1879575, 674962, 1322694, 1879639, 937109, 1879703, 1199254, 1879767, 1592465, 675026, 937173, 1199318, 1592529],
    [2468865, 1575937, 1576001, 1576065, 1576129, 1707008, 1707072, 1707136, 2468929, 1707200, 2373136, 2509329, 1969679, 2468993, 2509393, 1969743, 2100755, 2469057, 2635284, 2509457, 2854418, 2635348, 2509521, 2100819, 2854482, 2635412, 419859, 2854546, 2373200, 419923, 2100883, 2854610, 2635476, 419987, 1969807, 626197, 2373264, 3434514, 1969871, 2100947, 626261, 2373328, 420051, 626325, 2889238, 3434578, 626389, 2889302, 3434642, 1158160, 2889366, 3434706, 1158224, 2889430, 3426319, 1158288, 398873, 3426383, 1158352, 3426447, 1281560, 3426511, 1412115, 1722389, 1805847, 1722453, 1314315, 1281624, 1062427, 1722517, 1314379, 1412179, 398937, 1722581, 1314443, 1805911, 1062491, 1985050, 1314507, 1281688, 399001, 1985114, 1412243, 1062555, 1985178, 1805975, 399065, 1985242, 1281752, 1062619, 1412307, 1806039],
    [279552, 1837056, 2018304, 2124801, 2124865, 2124929, 2124993, 279616, 1837120, 2280976, 2018368, 1837184, 542225, 1837248, 542289, 2281040, 2492948, 2804756, 279680, 2493012, 2804820, 542353, 421379, 2805396, 279744, 2631683, 421443, 2018432, 2631747, 2115076, 552470, 421507, 2631811, 2281104, 2245654, 421571, 2805460, 2631875, 2115140, 552534, 2492564, 2018496, 2245718, 552598, 2492628, 2281168, 2245782, 789010, 2115204, 3198466, 552662, 789074, 2245846, 3198530, 789138, 2115268, 3198594, 789202, 542417, 3198658, 978453, 3016705, 1074192, 1076747, 3016769, 1074256, 1371667, 1076811, 1469965, 978517, 3016833, 1074320, 1076875, 1470029, 3016897, 1074384, 1371731, 1076939, 1470093, 978581, 1583639, 1470157, 1583703, 1371795, 1863182, 978645, 1583767, 1863246, 1583831, 1371859, 1863310, 1863374],
    [2108416, 2116609, 2116673, 2116737, 2116801, 2247680, 2247744, 2512400, 2247808, 2501633, 2247872, 2512464, 2108480, 380433, 2512528, 2501697, 380497, 2512592, 2108544, 380561, 2782225, 2501761, 3132948, 2782289, 2108608, 2878997, 2782353, 2501825, 3133012, 816658, 2493456, 2879061, 816722, 2493520, 3133076, 3034648, 2782929, 2493584, 2879125, 3034712, 3167256, 2493648, 3133140, 3034776, 3167320, 658966, 2879189, 3034840, 3167384, 789521, 3403283, 3167448, 659030, 3403347, 1463835, 789585, 3403411, 1594903, 659094, 3403475, 1463899, 789649, 1175068, 1594967, 659158, 1175132, 1463963, 789713, 1175196, 1595031, 1445401, 1175260, 816786, 1846810, 380113, 1464027, 1445465, 1567769, 1595095, 1846874, 1567833, 816850, 1445529, 1567897, 1846938, 1568473, 1445081, 1847002],
    [2401280, 2296832, 2141185, 2141249, 2141313, 2141377, 2149904, 2401344, 2296896, 2403858, 2682387, 2401408, 2296960, 2403922, 2682451, 2401472, 2297024, 2682515, 2428436, 558081, 2682579, 2428500, 3048977, 437781, 2149968, 2428564, 558145, 2150032, 2428628, 3049041, 568856, 2150096, 986647, 558209, 437845, 576533, 986711, 3049105, 437909, 576597, 2952729, 558273, 437973, 576661, 2952793, 3049169, 962074, 576725, 3449879, 3083290, 962138, 3329538, 3449943, 3083354, 568920, 1224200, 3329602, 2403986, 2952857, 3450519, 1355273, 962202, 3329666, 3450583, 3083418, 1355337, 2404050, 3329730, 2952921, 3704342, 1355401, 1486365, 969757, 962266, 3704406, 3083482, 1355465, 1362968, 986263, 3704470, 1486429, 969821, 1224264, 986327, 3704534, 1486493, 1363032, 1224328, 1773083, 3580946, 568984, 1486557, 969885, 1224392, 3581010, 2035228, 1363096, 1773147, 3581074, 969949, 3581138, 2035292, 1773211, 2000414, 1363672, 568536, 2035356, 2000478, 1773275, 2000542, 2035420, 2000606],
    [2370561, 2132992, 2133056, 2133120, 2133184, 2264065, 2264129, 2264193, 2370625, 2264257, 2536977, 2657297, 2370689, 2537041, 2657361, 2370753, 2537105, 3328531, 2657425, 429075, 2764304, 2537169, 576020, 2657489, 560148, 2764368, 2798612, 576084, 3051030, 560212, 2764432, 2798676, 3328595, 3051094, 429139, 2764496, 3060758, 846361, 822297, 3051158, 560788, 396824, 953882, 2798740, 3328659, 3051222, 429203, 3025946, 953946, 3060822, 846425, 822361, 560852, 3026010, 954010, 2798804, 3328723, 429267, 3026074, 954074, 3060886, 846489, 822425, 3026138, 3060950, 846553, 822489, 396888, 1086997, 1231368, 3575323, 1346568, 396952, 1619479, 1231432, 3575387, 1346632, 397016, 1349148, 575636, 3575451, 1347208, 920603, 1087061, 1230984, 3575515, 1183250, 1619543, 1493533, 1608733, 1347272, 920667, 1349212, 1493597, 1608797, 1740300, 1183314, 1087125, 2017292, 1609373, 1871390, 920731, 1619607, 1632286, 1609437, 1183378, 1349276, 1493149, 1740364, 920795, 1087189, 2017356, 1871454, 1183442, 1619671, 1632350, 1349340, 2017932, 1739916, 1632926, 1871006, 575700, 1231048, 1740492, 1493213, 1871582, 2017484, 1632478],
    [2409472, 1869825, 1633281, 1633345, 1633409, 1633473, 1764352, 1764416, 1764480, 2409536, 2263564, 1764544, 2313741, 2158095, 2409600, 2263628, 2313805, 2551313, 2672144, 1869889, 2313869, 2158159, 2409664, 2263692, 2313933, 2551377, 574995, 1869953, 617998, 3075605, 2263756, 706066, 347157, 3075669, 1870017, 976404, 347221, 3075733, 454147, 2672208, 871958, 2158223, 454211, 2672272, 872022, 2551441, 2672336, 872086, 2918916, 715780, 3075797, 575059, 872150, 2918980, 715844, 2158287, 454275, 706130, 347285, 2919044, 715908, 2551505, 976468, 347349, 2919108, 715972, 3468823, 454339, 1500183, 1403919, 1092121, 3468887, 1500247, 1534993, 1092185, 3468951, 575123, 1658392, 1092249, 3469015, 706194, 618062, 1092313, 1240582, 1500311, 1403983, 1223194, 1240646, 976532, 1535057, 1223258, 1240710, 575187, 1658456, 1223322, 1240774, 706258, 618126, 1223386, 1500375, 1404047, 976596, 1535121, 1658520, 618190, 1404111, 1535185, 1658584],
    [2290688, 2395137, 1625088, 1625152, 1625216, 1625280, 1756161, 1756225, 2256396, 1756289, 2290752, 2395201, 1756353, 2256460, 2290816, 2534927, 2412049, 2256524, 2290880, 2665489, 2543124, 2412113, 412692, 2674197, 2665553, 2814977, 2543188, 2674261, 412756, 2815041, 2534991, 2543252, 2412177, 412820, 314882, 2665617, 2815105, 2543316, 2674325, 412884, 314946, 2815169, 2535055, 2412241, 2256588, 841239, 2665681, 3304973, 972304, 2535119, 3305037, 980504, 3444246, 708100, 315010, 3305101, 980568, 3444310, 708164, 3305165, 980632, 2395265, 2674389, 806425, 980696, 3444374, 814097, 2395329, 3331590, 708228, 1461786, 3331654, 3444438, 708292, 315074, 1461850, 3331718, 3968530, 1461914, 3331782, 1617422, 1101319, 1461978, 1898003, 3976213, 1232392, 1494538, 1600533, 841303, 3968594, 1101383, 806489, 972368, 1617486, 1232456, 1494602, 814161, 1898067, 3976277, 1101447, 1600597, 841367, 3968658, 1232520, 1494666, 806553, 972432, 1617550, 1101511, 814225, 1898131, 3976341, 1232584, 1494730, 1600661, 841431, 3968722, 806617, 972496, 1617614, 814289, 1898195, 3976405, 1600725],
    [2599936, 2565121, 2173953, 2174017, 2174081, 2174145, 2565185, 2592272, 2565249, 2592336, 2565313, 2592400, 2444802, 2827264, 2592464, 2444866, 2827328, 3255812, 2444930, 601618, 2827392, 3255876, 2444994, 601682, 732691, 2827456, 3255940, 609298, 601746, 732755, 3256004, 2958352, 609362, 601810, 732819, 3640849, 2958416, 609426, 863751, 732883, 3640913, 2958480, 609490, 994836, 863815, 1125909, 2600000, 2958544, 1002517, 1256982, 1125973, 3640977, 3605508, 1133590, 994900, 1257046, 2600064, 3868166, 1395732, 1126037, 3641041, 3605572, 3100184, 1387544, 994964, 2600128, 3868230, 3100248, 1387608, 1257110, 1126101, 3771411, 3605636, 3100312, 1387672, 995028, 3771475, 3868294, 3100376, 1387736, 1257174, 3771539, 3605700, 1133654, 3771603, 3868358, 1002581, 863879, 1902105, 1945111, 1395796, 863943, 1902169, 1945175, 1133718, 1902233, 2067994, 1002645, 1902297, 2068058, 1395860, 2068122, 1133782, 1945239, 1002709, 2068186, 1395924, 1945303],
    [2526208, 2438145, 2165761, 2165825, 2165889, 2165953, 2526272, 2438209, 2443795, 2526336, 2438273, 2705940, 2526400, 2438337, 2706004, 462338, 2962966, 2788882, 2706068, 3225109, 3190288, 2706132, 724483, 3225173, 3190352, 3360789, 2963030, 2788946, 3500034, 3225237, 2789010, 3360853, 2963094, 2789074, 3360917, 1117722, 462402, 3225301, 3190416, 3622938, 2963158, 3190480, 2443859, 462466, 4002835, 1093137, 3500098, 1117786, 4002899, 1093201, 3623002, 462530, 4003475, 1093265, 2443411, 1117850, 1521175, 3836948, 3500162, 4003539, 1093329, 3623066, 1117914, 1521239, 3837012, 3360981, 724547, 3880476, 3837076, 2443475, 724611, 3880540, 3837140, 3500226, 3880604, 2002457, 3623130, 724675, 3880668, 2002521, 1919515, 1904140, 1521303, 2002585, 1919579, 1904204, 1521367, 2002649, 1919643, 1904268, 1919707, 1904332, 2050584, 2050648, 2050712, 2050776],
    [2450433, 2092033, 2190336, 2190400, 2190464, 2190528, 2092097, 2713104, 2450497, 2092161, 2092225, 2713168, 2450561, 2616336, 2616400, 2713232, 592402, 486931, 2450625, 2616464, 592466, 749076, 486995, 2617040, 3236884, 592530, 3140627, 2712784, 731669, 1011202, 749140, 3140691, 3236948, 592594, 1011266, 1142294, 650769, 3213334, 3229190, 1142358, 650833, 3213398, 3229254, 1142422, 487059, 3140755, 3213462, 3229318, 1142486, 650897, 3213526, 3229382, 749204, 650961, 3237012, 1011330, 749268, 1273353, 487123, 3140819, 3237076, 1011394, 1273417, 1387031, 1772056, 1273481, 1787417, 1666571, 1772120, 1306138, 1926683, 1666635, 1387095, 1306202, 1666699, 1911324, 1306266, 1787481, 1666763, 731733, 1822237, 1926747, 1772184, 1822301, 1928718, 1911388, 1822365, 1928782, 1787545, 731797, 1822429, 1928846, 1926811, 1387159, 1306330, 1928910, 1911452, 1273545, 1787609, 1772248, 1926875, 731861, 1911516, 1387223],
    [357376, 2305024, 2026497, 2182145, 2182209, 2182273, 2182337, 611856, 2288656, 2305088, 611920, 2288720, 339473, 611984, 593426, 2026561, 2288784, 612048, 593490, 357440, 593554, 2026625, 2288848, 357504, 593618, 357568, 2026689, 855571, 478740, 2716692, 3206658, 339537, 740886, 3109910, 3206722, 855635, 478804, 3241478, 3206786, 339601, 740950, 2716756, 3206850, 2305152, 3109974, 339665, 846867, 478868, 3241542, 846931, 855699, 741014, 2716820, 2305216, 846995, 3110038, 847571, 855251, 3231256, 478932, 3241606, 838674, 3345432, 3231320, 741078, 2716884, 838738, 3345496, 3231384, 3110102, 838802, 3345560, 3231448, 3241670, 838866, 3345624, 1405953, 1650199, 1406017, 1650263, 1406081, 1650327, 1406145, 1650391, 2043413, 2043477, 2043541, 2043605],
    [1977345, 2206720, 2206784, 2206848, 2206912, 2337793, 2337857, 2223632, 2337921, 1977409, 2337985, 372241, 2223696, 2632721, 2862611, 2223760, 372305, 2632785, 2721300, 2993172, 2862675, 2223824, 372369, 2632849, 2721364, 2993236, 2862739, 2870291, 372433, 2632913, 2721428, 2993300, 503317, 2870355, 2862803, 1977473, 2721492, 2993364, 503381, 2870419, 1977537, 2991639, 503445, 2870483, 2362898, 3253782, 634392, 503509, 3264002, 2755603, 3253846, 765444, 3264066, 2755667, 3384857, 634456, 896538, 765508, 3264130, 1027611, 2755731, 2991703, 896602, 765572, 3264194, 1027675, 2755795, 634520, 3384921, 896666, 765636, 642075, 3017752, 2991767, 896730, 1027739, 642139, 2362962, 634584, 3253910, 642203, 3017816, 3384985, 1027803, 642267, 2363026, 2991831, 3394577, 3017880, 3253974, 3394641, 2363090, 3385049, 3394705, 3017944, 3394769, 1715740, 1690650, 1715804, 1952789, 1715868, 1690714, 1715932, 1952853, 1690778, 2065949, 1952917, 2066013, 1690842, 2066077, 1952981, 2066141],
    [2593793, 2436097, 2198528, 2198592, 2198656, 2198720, 2698768, 2593857, 2091539, 2460691, 2698832, 2593921, 2698896, 2593985, 2353686, 2698960, 2733585, 2353750, 2733649, 2436161, 3000855, 2733713, 2436225, 2615832, 2733777, 2436289, 495129, 2615896, 3353625, 2995732, 2615960, 2995796, 2690578, 495193, 757274, 2616024, 3353689, 2995860, 757338, 3000919, 2995924, 2690642, 495257, 757402, 3000983, 3353753, 758800, 2461267, 757466, 2091091, 2690706, 3388949, 495321, 1019400, 3001047, 3353817, 758864, 1019464, 2461331, 2091155, 2690770, 3389013, 1150473, 1019528, 3917850, 758928, 1248795, 1150537, 1019592, 2461395, 2091219, 3389077, 1248859, 1150601, 3917914, 758992, 1248923, 1150665, 1674762, 3917978, 3389141, 1248987, 1674826, 3918042, 1781278, 1674890, 2353814, 1781342, 1674954, 2353878, 1821213, 1781406, 1952284, 1781470, 1821277, 1952348, 1821341, 1952412, 1821405, 1952476],
    [2343936, 2509825, 1698816, 1698880, 1698944, 1699008, 1829889, 1829953, 1830017, 2475535, 2509889, 1830081, 2591248, 2475599, 2509953, 2591312, 2475663, 2510017, 2591376, 2772498, 2475727, 388610, 2591440, 2772562, 2344000, 388674, 764436, 2772626, 2344064, 388738, 764500, 2772690, 2344128, 895511, 3042324, 3130901, 764564, 3042388, 3130965, 895575, 3042452, 3131029, 1149464, 3566616, 3131093, 895639, 3567192, 2745360, 1149016, 3567256, 2745424, 895703, 3567320, 2745488, 3508740, 1043973, 3043028, 2745552, 3508804, 1044037, 1723921, 3508868, 1044101, 1723985, 3508932, 1044165, 1724049, 1944089, 1724113, 1944153, 1732115, 1149080, 1994262, 1944217, 1732179, 1149144, 1994326, 388802, 764116, 1732243, 1944281, 1994390, 1732307, 1994454],
    [2321408, 2216961, 2083840, 2083904, 2083968, 2084032, 2453004, 2217025, 2723341, 2346511, 2453068, 2487311, 2723405, 2477584, 2346575, 2453132, 2487375, 2723469, 2477648, 2346639, 2453196, 2487439, 2723533, 2477712, 2346703, 2487503, 2583553, 3386897, 2477776, 3001875, 2610192, 2321472, 3247630, 3001939, 2610256, 2583617, 3386961, 3002003, 2610320, 2321536, 3247694, 3002067, 2610384, 2583681, 3387025, 2321600, 2217089, 3247758, 2583745, 2217153, 3387089, 3011603, 3108355, 3247822, 511512, 3011667, 3108419, 1289749, 3011731, 3108483, 1289813, 3011795, 3108547, 904729, 1035782, 1289877, 3362322, 904793, 1035846, 1289941, 3624468, 904857, 1035910, 1543703, 3755032, 904921, 1035974, 1682966, 511576, 3362386, 1297928, 1813529, 511640, 3624532, 1297992, 1543767, 511704, 3755096, 1298056, 1683030, 3362450, 1298120, 1813593, 3624596, 1543831, 3755160, 1683094, 3362514, 1813657, 3624660, 1543895, 3755224, 1683158, 1813721],
    [2379776, 2265089, 1978369, 1978433, 1978497, 1978561, 2109440, 2109504, 2099724, 2109568, 2379840, 2265153, 2109632, 2503184, 2099788, 2379904, 2265217, 2503248, 2238993, 2379968, 2265281, 2503312, 2239057, 422415, 2527244, 2239121, 2527308, 807438, 2239185, 2527884, 553490, 2099340, 2527948, 946709, 2099404, 3052045, 422479, 2623504, 3297795, 3052109, 2623568, 3052173, 946773, 2623632, 3052237, 807502, 2503376, 2623696, 692755, 553554, 2894356, 422543, 692819, 2894420, 692883, 946837, 2894484, 692947, 807566, 2894548, 3297859, 1216527, 3297923, 1347605, 3148311, 3289111, 3297987, 1216591, 3148375, 3289175, 1323529, 1724950, 1347669, 3148439, 3289239, 1323593, 1725014, 1216655, 3148503, 3289303, 1323657, 1725078, 1347733, 1323721, 1217231, 553618, 1725142, 1348309, 422095, 946389, 807630, 553682],
    [2504704, 2388993, 1576961, 1577025, 1577089, 1577153, 1708032, 1708096, 1708160, 2636303, 2389057, 1708224, 2593296, 2504768, 2389121, 2593360, 2636367, 2389185, 2593424, 3036160, 2504832, 2593488, 3036224, 2636431, 3379732, 3036288, 2504896, 3379796, 266755, 3036352, 2636495, 3379860, 266819, 3029525, 3044355, 3379924, 266883, 3029589, 3044419, 1020435, 266947, 3029653, 3044483, 1151510, 3291158, 3044547, 1151574, 3291222, 3307026, 3641879, 3291798, 3307090, 3641943, 791047, 922136, 3291862, 3307154, 3772440, 1053192, 922200, 3029717, 3307218, 3772504, 791111, 922264, 2497041, 1725460, 3772568, 1053256, 922328, 2497105, 1471511, 3642007, 791175, 2497169, 1725524, 3772632, 1053320, 2497233, 1471575, 3642071, 791239, 1725588, 1020499, 1053384, 1471639, 1151126, 1725652, 1020563, 1471703, 1151190, 1020627, 2069017, 2069081, 2069145, 2069209],
    [2516992, 2412544, 2125825, 2125889, 2125953, 2126017, 2412608, 289296, 2110993, 2519570, 2412672, 289360, 2111057, 2650643, 2519634, 2412736, 289424, 291331, 2111121, 2650707, 2519698, 2912788, 2805761, 289488, 2111185, 2650771, 2519762, 2912852, 2805825, 3033107, 2766357, 2650835, 2912916, 2805889, 3033171, 2766421, 2912980, 2805953, 3033235, 2766485, 684567, 815640, 3076119, 3033299, 2766549, 684631, 3076183, 3164178, 2757652, 684695, 3076247, 3164242, 2757716, 1110553, 3164306, 2757780, 684759, 3076311, 3164370, 1208840, 2757844, 815704, 1503250, 2517056, 291395, 3552790, 815768, 1503314, 2517120, 1208904, 3552854, 815832, 1503378, 2517184, 1339913, 3552918, 1503442, 1206289, 1339977, 3552982, 1206353, 1495579, 291459, 3683352, 1206417, 1110617, 1340041, 3683416, 1206481, 1110681, 1208968, 3683480, 1110745, 291523, 3683544, 1495643, 1340105, 1455642, 1495707, 1209032, 1455706, 1495771, 1455770, 1455834],
    [1961985, 2117633, 2117697, 2117761, 2117825, 2248704, 2248768, 2232848, 2248832, 1962049, 2248896, 283153, 2232912, 1962113, 2652691, 283217, 2232976, 1962177, 2652755, 2233040, 2871313, 545301, 2652819, 274453, 2871377, 676376, 3037719, 536600, 2617344, 676440, 2652883, 938521, 528916, 2617408, 676504, 3037783, 283281, 536664, 2871441, 676568, 3037847, 283345, 528980, 2871505, 545365, 3168794, 3027464, 2617472, 545429, 3168858, 938585, 3027528, 2617536, 545493, 3027592, 3011094, 938649, 3027656, 3142162, 938713, 274517, 3011158, 3168922, 274581, 3142226, 3562011, 536728, 3011222, 3562075, 529044, 3142290, 3562139, 274645, 3011286, 3037911, 1593884, 1454108, 3142354, 3562203, 1593948, 1454172, 3403801, 3168986, 1594012, 1454236, 3403865, 1735197, 1594076, 536792, 3403929, 1735261, 529108, 3403993, 1735325, 1856015, 1454300, 1735389, 1856079, 1856143, 1856207],
    [1878016, 1904640, 2142208, 2142272, 2142336, 2142400, 2166785, 559632, 446993, 2043920, 559696, 447057, 307730, 1904704, 2271250, 447121, 307794, 2166849, 2271314, 447185, 307858, 2043984, 2271378, 3068435, 307922, 1904768, 2271442, 709140, 2166913, 559760, 3199509, 2044048, 559824, 3199573, 1878080, 1904832, 3199637, 700931, 1878144, 2166977, 3199701, 700995, 832024, 2044112, 3049496, 3068499, 701059, 832088, 3346946, 3049560, 3068563, 832152, 856599, 3049624, 3068627, 1225221, 832216, 987155, 3049688, 1634838, 1225285, 1618457, 856663, 3442713, 709204, 1225349, 1618521, 987219, 3442777, 1634902, 1880583, 1618585, 1225413, 856727, 3442841, 3731976, 1880647, 1618649, 987283, 3442905, 3732040, 1880711, 1878208, 3347010, 3732104, 1880775, 1353729, 3347074, 3732168, 701123, 1353793, 3347138, 1896986, 856791, 1353857, 1897050, 987347, 1353921, 1897114, 709268, 1634966, 1897178, 709332, 1635030],
    [2101248, 2398208, 2134017, 2134081, 2134145, 2134209, 2101312, 2398272, 2422290, 2101376, 2398336, 2422354, 2626067, 2923028, 2422418, 2626131, 2923092, 2422482, 406037, 2923156, 406101, 2923220, 718358, 2398400, 406165, 710167, 3447299, 406229, 718422, 3447363, 2626195, 561688, 718486, 2799640, 2101440, 561752, 718550, 2799704, 2626259, 561816, 2799768, 3158545, 561880, 2799832, 3158609, 3339784, 3062279, 3158673, 3339848, 823818, 3062343, 3158737, 3339912, 823882, 3062407, 3019280, 3339976, 823946, 3062471, 3019344, 3577872, 3019408, 3577936, 3019472, 1716761, 3578000, 1716825, 3578064, 824010, 1716889, 3447427, 1716953, 3447491, 2020890, 710231, 2020954, 710295, 2021018, 710359, 2021082],
    [2584577, 2158593, 2158657, 2158721, 2158785, 2289664, 2289728, 2405904, 2410512, 2289792, 2584641, 2289856, 2790930, 2411088, 2584705, 2790994, 2411152, 2584769, 324099, 586242, 2405456, 2411216, 2839059, 324163, 2791058, 3590147, 2839123, 324227, 3590211, 2405520, 2839187, 324291, 2791122, 3590275, 2839251, 717335, 3590339, 2405584, 3371026, 833044, 3852311, 3502613, 979480, 3183640, 3467793, 3371090, 979544, 3183704, 3467857, 3502677, 979608, 3183768, 3467921, 3371154, 979672, 3183832, 3467985, 3502741, 717399, 833108, 3852375, 3371218, 717463, 833172, 3852439, 3502805, 717527, 833236, 3852503, 3756553, 2012694, 3756617, 1624601, 2012758, 3756681, 2012822, 3756745, 1765900, 1624665, 2012886, 1658905, 586306, 1763866, 1667089, 586370, 1763930, 1658969, 586434, 1624729, 1667153, 1763994, 1659033, 1624793, 1667217, 1765964, 1764058, 1659097, 1766028, 1667281, 1766092],
    [2414592, 2387969, 2150401, 2150465, 2150529, 2150593, 2535952, 2414656, 2388033, 2536016, 2642449, 2414720, 2536080, 2642513, 2414784, 2536144, 3078161, 2642577, 578067, 2929155, 3078225, 2642641, 569363, 3078289, 3166740, 2929219, 3078353, 2388097, 2929283, 842258, 2388161, 840213, 2929347, 842322, 971286, 1102360, 3322374, 842386, 971350, 578131, 3322438, 842450, 3166804, 840277, 3322502, 3734039, 3166868, 578195, 1364488, 3322566, 3864600, 3166932, 840341, 1486869, 3734103, 971414, 578259, 1102424, 1749014, 3864664, 971478, 840405, 1102488, 569427, 3734167, 1331737, 1102552, 1486933, 3864728, 1462810, 1749078, 3734231, 1462874, 1757723, 2011163, 3864792, 1331801, 1364552, 569491, 1890844, 1462938, 1757787, 2011227, 1364616, 1890908, 1331865, 1364680, 1486997, 1890972, 1463002, 1757851, 2011291, 1891036, 1749142, 1331929, 1757915, 569555, 1487061, 2011355, 1749206],
    [2426880, 2461696, 1650689, 1650753, 1650817, 1650881, 2461760, 2689548, 2576910, 2426944, 2461824, 2707981, 2461888, 2689612, 348688, 2427008, 3117068, 2708045, 2689676, 3248129, 2576974, 2830867, 2427072, 3117132, 348752, 2830931, 2689740, 3248193, 2708109, 2830995, 3117196, 1116687, 2577038, 2831059, 3248257, 862227, 3093014, 348816, 3117260, 993302, 3093078, 2708173, 3248321, 1378839, 3093142, 471556, 2577102, 1421845, 993366, 3093206, 602629, 348880, 1421909, 1378903, 471620, 3363345, 1421973, 1509913, 602693, 3494424, 733702, 1422037, 1116751, 471684, 3363409, 864775, 1675794, 862291, 602757, 3494488, 733766, 993430, 1946138, 995848, 471748, 3363473, 864839, 1126922, 1675858, 1378967, 995912, 602821, 3494552, 733830, 1126986, 1946202, 1116815, 995976, 3363537, 864903, 1127050, 1675922, 862355, 996040, 3494616, 1127114, 1509977, 1946266, 1929748, 1675986, 1510041, 2060306, 993494, 1946330, 1929812, 733894, 1510105, 2060370, 864967, 1379031, 1929876, 1116879, 2060434, 862419, 1929940, 2060498],
    [2061312, 2439169, 2273281, 1642496, 1642560, 1642624, 1642688, 2061376, 2570764, 2273345, 2036237, 2570828, 2273409, 2454541, 2036301, 2439233, 2798094, 2454605, 2036365, 2429455, 2061440, 2570892, 2798158, 2036429, 2439297, 2798222, 2454669, 2691603, 2061504, 2570956, 2798286, 2822676, 2429519, 2691667, 735252, 2273473, 2454733, 2822740, 2691731, 2847763, 735316, 430093, 2822804, 2691795, 2978831, 735380, 430157, 2822868, 2429583, 2847827, 735444, 430221, 463362, 963096, 2978895, 2439361, 2847891, 963160, 3086865, 2429647, 963224, 2978959, 3086929, 2847955, 963288, 3086993, 2979023, 954903, 3087057, 1136150, 1645074, 954967, 1136214, 1776153, 955031, 1136278, 1645138, 955095, 1136342, 1776217, 430285, 463426, 1479184, 1645202, 463490, 1776281, 2003477, 463554, 1511946, 1479248, 1645266, 1512010, 1776345, 2003541, 1512074, 1479312, 2045967, 1512138, 2046031, 2003605, 1479376, 2046095, 2046159, 2003669],
    [2478080, 2181121, 2191361, 2191425, 2191489, 2191553, 2322432, 2322496, 2322560, 2181185, 2740752, 2322624, 2692626, 356370, 2181249, 2740816, 2692690, 356434, 2181313, 2740880, 619027, 463891, 2740944, 750100, 734228, 2478144, 881154, 865282, 739861, 2478208, 750164, 734292, 3369494, 2478272, 619091, 463955, 3369558, 357010, 3133969, 881218, 2692242, 3369622, 357074, 3134033, 750228, 2692306, 3369686, 1143300, 3134097, 619155, 3741189, 739925, 1143364, 3134161, 881282, 3741253, 739989, 3527191, 750292, 3741317, 740053, 3527255, 619219, 3741381, 1405464, 1143428, 3527319, 881346, 1250328, 1405528, 1143492, 1395225, 1250392, 1405592, 3527383, 1250456, 1405656, 1561114, 1657371, 1250520, 1536522, 1692188, 1665565, 1512452, 1536586, 1395289, 1692252, 1512516, 1536650, 1561178, 1657435, 865346, 1536714, 1692316, 1665629, 734356, 1395353, 1561242, 1798670, 1512580, 1692380, 1657499, 1798734, 464019, 1561306, 1665693, 1798798, 865410, 1395417, 1798862, 734420, 1657563, 1512644, 1665757, 464083, 865474],
    [489472, 2183169, 2183233, 2183297, 2183361, 2314240, 2314304, 1913360, 2314368, 620545, 2314432, 315922, 1913424, 2587153, 2552340, 1913488, 2587217, 2675221, 1913552, 489536, 2675285, 2699795, 620609, 2970134, 2675349, 2699859, 2587281, 2970198, 2813974, 2699923, 489600, 2970262, 2675413, 2699987, 620673, 2970326, 479767, 2552404, 339991, 2587345, 872984, 479831, 2814038, 1004057, 593945, 489664, 2552468, 725530, 620737, 873048, 479895, 2814102, 1135131, 594521, 1003609, 2552532, 725594, 873112, 2814166, 1004185, 594073, 479959, 3469336, 725658, 873176, 3469400, 1004249, 594137, 3469464, 1135195, 725722, 3469528, 340055, 315986, 1135259, 340119, 316050, 340183, 316114, 1135323, 1519643, 2019868, 1519707, 2019932, 1519771, 2019996, 1519835, 2020060],
    [1970176, 2347009, 2207744, 2207808, 2207872, 2207936, 2338817, 2338881, 2599440, 2338945, 2494480, 2347073, 2339009, 2861585, 2495056, 2347137, 2598992, 2495120, 2347201, 2994707, 2852883, 389650, 2495184, 2994771, 2852947, 389714, 2756625, 2994835, 2853011, 389778, 1970240, 2994899, 2853075, 389842, 2757201, 3123734, 1970304, 2748432, 3123798, 2748496, 2757265, 2861137, 1970368, 2748560, 2599056, 2748624, 2757329, 897543, 3123862, 930327, 905239, 1159688, 2861201, 1061400, 1167384, 1159752, 2599120, 930391, 905303, 1683978, 3123926, 1061464, 1167448, 1684042, 2861265, 930455, 905367, 1684106, 1804820, 1061528, 1167512, 1684170, 1681945, 930519, 905431, 2075163, 1061592, 1167576, 1804884, 1307157, 1314834, 1682009, 1438236, 1847834, 2075227, 1307221, 1314898, 897607, 1804948, 1438300, 1847898, 1159816, 1682073, 1307285, 1314962, 897671, 2075291, 1438364, 1847962, 1159880, 1805012, 1307349, 1315026, 897735, 1682137, 1438428, 1848026, 2075355],
    [366593, 1963009, 2199552, 2199616, 2199680, 2199744, 2330625, 2330689, 2330753, 2356752, 366657, 2330817, 2356816, 366721, 2175508, 2986515, 364564, 1963073, 366785, 2437653, 2986579, 495637, 2209808, 2356880, 2437717, 2986643, 495701, 2209872, 1963137, 2437781, 2986707, 495765, 2603523, 2356944, 332310, 496341, 2603587, 1963201, 2953751, 889368, 2603651, 2618387, 2953815, 889432, 2209936, 2618451, 2953879, 365140, 2603715, 2618515, 2953943, 889496, 2210000, 2618579, 3355140, 365204, 2865176, 2880535, 3355204, 889560, 2865240, 2880599, 3355268, 1282570, 365268, 2865304, 2880663, 2437333, 1282634, 2865368, 2880727, 3355332, 1282698, 1546769, 1177106, 2175060, 1282762, 1546833, 1177170, 2175124, 1546897, 1177234, 2175188, 1546961, 1177298, 332374, 332438, 332502],
    [2213888, 1699840, 1699904, 1699968, 1700032, 1830913, 1830977, 2471439, 1831041, 2213952, 1831105, 414225, 2093584, 2471503, 2476049, 2781714, 2987540, 2476625, 3174420, 2987604, 2476689, 3174484, 2987668, 2476753, 3174548, 2987732, 2214016, 3174612, 2471567, 2214080, 2781778, 2471631, 3262480, 2781842, 3642386, 2746901, 2781906, 3642450, 2746965, 1069590, 2093648, 3642514, 3262544, 520709, 413777, 2093712, 3642578, 3262608, 1069654, 2093776, 3257875, 3262672, 1200667, 651782, 3257939, 2747029, 1200731, 782856, 3258003, 2747093, 413841, 651846, 3258067, 4049433, 1200795, 782920, 1553943, 4049497, 1069718, 651910, 1554007, 4049561, 520773, 413905, 782984, 1554071, 4049625, 520837, 1200859, 651974, 1554135, 520901, 1069782, 783048, 1947160, 1994775, 2078234, 1994839, 1947224, 1994903, 2078298, 1994967, 1947288, 1569293, 1987100, 2078362, 1569357, 1987164, 1947352, 1569421, 1987228, 2078426, 1569485, 1987292],
    [2453504, 2469889, 2095105, 2084864, 2084928, 2084992, 2085056, 2601484, 2715660, 2095169, 2609678, 2601548, 2715724, 2095233, 2609742, 2601612, 2715788, 2095297, 2609806, 2601676, 2715852, 2619920, 2609870, 2453568, 3125773, 2619984, 381457, 2453632, 3125837, 2620048, 2453696, 3125901, 2620112, 610835, 3013122, 3125965, 610899, 2469953, 1047058, 3265044, 3013186, 3633166, 2470017, 643605, 3265108, 3764245, 2470081, 1047122, 643669, 3265172, 1290257, 610963, 3013250, 643733, 3265236, 611027, 1047186, 643797, 1552918, 1036310, 3764309, 3013314, 1815063, 1298455, 3633230, 1047250, 1552982, 1036374, 3764373, 3405844, 1815127, 1298519, 381521, 3405908, 3633294, 2077208, 1429528, 1036950, 3764437, 3405972, 381585, 1290321, 1299095, 3406036, 3633358, 2077272, 1429592, 1037014, 1825295, 381649, 1290385, 1299159, 1825359, 1552534, 2052633, 1430168, 1825423, 2076824, 2052697, 1825487, 1814679, 2052761, 1430232, 1290449, 2052825, 2076888, 1552598, 1814743],
    [2397184, 2239489, 1979392, 1979456, 1979520, 1979584, 2381324, 2239553, 2659340, 275982, 2774541, 2239617, 2659916, 276046, 2774605, 2239681, 2659980, 2774669, 2660044, 2231823, 2774733, 2397248, 407056, 2380876, 2397312, 407120, 2380940, 2397376, 2231887, 2381004, 693249, 405010, 276110, 947729, 693313, 545806, 693377, 2231951, 538131, 676880, 693441, 405074, 669204, 538195, 807955, 2887189, 1095190, 407184, 939028, 2887253, 1095254, 538259, 947793, 2887317, 1095318, 276174, 545870, 669268, 2887381, 1095382, 407248, 676944, 669332, 2232015, 1611288, 538323, 808019, 1453591, 1611352, 800260, 939092, 1453655, 669396, 1611416, 800324, 947857, 1453719, 1742361, 800388, 545934, 1453783, 1742425, 800452, 677008, 405138, 1193479, 1742489, 808083, 405202, 1324553, 1611480, 939156, 1193543, 1586699, 1742553, 947921, 1324617, 1586763, 545998, 1193607, 1586827, 677072, 1324681, 1586891, 808147, 1193671, 939220, 1324745],
    [1577985, 1578049, 1578113, 1578177, 1709056, 1709120, 2511375, 1709184, 1709248, 2511439, 2511503, 2375184, 2602513, 2511567, 1711121, 2602577, 3305489, 1711185, 2602641, 2233876, 3035156, 1711249, 2602705, 2233940, 3035220, 1711313, 3380757, 267285, 2364950, 2234004, 3035284, 2375248, 3511318, 267861, 3305553, 2375312, 3773975, 267925, 2365014, 2234068, 3035348, 2375376, 3511382, 267989, 3305617, 3380309, 2365078, 3305681, 3774039, 3568146, 3511446, 2365142, 3568210, 3380373, 3568274, 2629147, 3774103, 3151386, 3568338, 3511510, 2898970, 3151450, 3699219, 2899034, 3380437, 3151514, 3699283, 2899098, 3774167, 3151578, 3699347, 1676824, 2899162, 3699411, 2629211, 1938972, 1864217, 2629275, 1676888, 1864281, 2629339, 1939036, 1864345, 1676952, 1864409, 1939100, 1677016, 1939164],
    [281600, 316417, 1839105, 2126849, 2126913, 2126977, 2127041, 2257920, 2257984, 2258048, 281664, 456208, 2363408, 2258112, 281728, 1839169, 456272, 281792, 2363472, 456336, 579093, 290321, 1839233, 2911766, 579157, 2363536, 2911830, 579221, 1839297, 2911894, 579285, 2364112, 2911958, 667669, 455888, 3200531, 3436055, 799250, 3200595, 3436119, 667733, 3200659, 3436183, 799314, 3200723, 3436247, 667797, 683540, 799378, 316481, 2888217, 316545, 945168, 2888281, 290385, 316609, 1340938, 2888345, 1635864, 683604, 1341002, 2888409, 1766400, 945232, 1341066, 1635928, 667861, 290449, 1341130, 1585690, 1766464, 683668, 1585754, 1635992, 945296, 1766528, 290513, 799442, 1585818, 1636056, 683732, 1766592, 945360, 1585882],
    [2094080, 1997825, 2118657, 2118721, 2118785, 2118849, 2249728, 2249792, 2249856, 2225680, 1997889, 2249920, 2242065, 2225744, 1997953, 2242129, 2643475, 2225808, 1998017, 2242193, 2905620, 2784256, 2225872, 2242257, 2905684, 2784320, 2094144, 2897426, 2905748, 2784384, 2094208, 3028483, 2905812, 2784448, 2094272, 2897490, 2741268, 3046417, 3028547, 2643539, 2741332, 3046481, 2897554, 2741396, 3046545, 3028611, 2643603, 2741460, 3046609, 2897618, 2514453, 2749459, 3028675, 2643667, 2514517, 2749523, 3421698, 1070600, 2514581, 2749587, 3421762, 1201673, 2514645, 2749651, 3421826, 1070664, 3266070, 3421890, 1201737, 3266134, 3282436, 1070728, 3266198, 3282500, 1201801, 3266262, 3282564, 1070792, 1570327, 3282628, 1857036, 1201865, 1570391, 1447448, 1570455, 1447512, 1857100, 1570519, 1447576, 1857164, 1447640, 1717785, 1857228, 1717849, 1717913, 1717977],
    [297984, 340993, 2143232, 2143296, 2143360, 2143424, 2545168, 298048, 341057, 308754, 2545232, 298112, 2823697, 439828, 447508, 298176, 2823761, 439892, 447572, 2919957, 2823825, 439956, 447636, 2920021, 2823889, 440020, 447700, 3320833, 3216899, 570884, 308818, 2545296, 2920085, 3216963, 308882, 2545360, 3320897, 3217027, 308946, 3069442, 2920149, 3217091, 964101, 3069506, 3749399, 3320961, 964165, 3069570, 3749463, 3321025, 964229, 3069634, 3583512, 3749527, 964293, 1496598, 3583576, 341121, 1758226, 3583640, 3749591, 1504793, 3583704, 341185, 1488393, 1504857, 4133888, 3845651, 1496662, 4133952, 3845715, 1758290, 4134016, 3845779, 1504921, 4134080, 3845843, 1496726, 1905685, 2010129, 1758354, 1905749, 2010193, 570948, 1504985, 1905813, 2010257, 571012, 1496790, 1905877, 2010321, 571076, 1758418, 1488457, 1488521, 1488585],
    [2281473, 2135040, 2135104, 2135168, 2135232, 2266113, 2266177, 2266241, 2281537, 2266305, 300561, 2543633, 2268690, 1971218, 300625, 2543697, 2922003, 300689, 2543761, 2922067, 300753, 2543825, 2922131, 2268754, 1971282, 2281601, 2922195, 2281665, 3159573, 2661397, 3207187, 2661973, 1971858, 1233430, 3159125, 2268306, 1233494, 2662037, 1971922, 824838, 1233558, 3159189, 2268370, 1233622, 3159765, 2661589, 3207251, 3315225, 3290137, 835096, 3207315, 3315289, 3290201, 835160, 3207379, 3315353, 3290265, 835224, 824902, 3330576, 3315417, 3290329, 835288, 824966, 3600916, 1480218, 661001, 1489946, 825030, 3330640, 1480282, 791558, 1490010, 3600980, 1480346, 931341, 1490074, 3330704, 1480410, 661065, 1490138, 3601044, 791622, 1752590, 3330768, 931405, 1752654, 3601108, 661129, 2028055, 791686, 1752718, 2028119, 931469, 2028183, 661193, 1752782, 2028247, 791750, 931533],
    [349184, 1895425, 2159616, 2159680, 2159744, 2159808, 2667024, 349248, 1895489, 325122, 2667088, 2184721, 2812945, 2667152, 2184785, 2813009, 2667216, 1895553, 2184849, 2658834, 2577923, 2813073, 587268, 2920981, 2935812, 2577987, 587332, 2658898, 2935876, 2578051, 587396, 2921045, 2935940, 2578115, 587460, 2658962, 2936004, 2184913, 2921109, 2971156, 1895617, 849432, 2659026, 3101720, 2813137, 849496, 2921173, 3101784, 3066896, 849560, 1356310, 3101848, 3066960, 849624, 1356374, 3101912, 3067024, 325186, 1356438, 3067088, 2971220, 3470873, 3444761, 325250, 3460627, 2971284, 3470937, 3444825, 325314, 3460691, 2971348, 3471001, 3444889, 1266707, 3460755, 3471065, 3444953, 1266771, 3460819, 1356502, 1266835, 1502229, 1741335, 349312, 1502293, 1741399, 1266899, 1502357, 1741463, 349376, 1502421, 1741527, 1537025, 1537089, 1537153, 1537217],
    [2151424, 2151488, 2151552, 2151616, 2282497, 2282561, 2528784, 2415632, 2520080, 2282625, 2282689, 2651665, 2528848, 2415696, 2676227, 2651729, 2416272, 3052547, 2807315, 2651793, 2416336, 3053123, 2675779, 2807379, 588817, 2651857, 2528400, 2676355, 2807443, 720405, 3052675, 2913299, 2807507, 588881, 2520144, 2528464, 3192338, 720469, 2913363, 3192402, 588945, 2520208, 2676419, 720533, 3052739, 2913427, 3192466, 589009, 2520272, 1103367, 3298311, 3192530, 720597, 1234455, 1103431, 1225751, 3298375, 1365512, 1103495, 3298439, 1218068, 1627672, 1103559, 1367577, 1750040, 3298503, 1234519, 1367641, 1225815, 2913491, 1365576, 1244698, 3429384, 1881113, 1627736, 1244762, 3429448, 1750104, 1234583, 1367705, 1225879, 1603094, 1365640, 1244826, 3429512, 1881177, 1627800, 1367769, 1750168, 1603158, 1234647, 1244890, 1225943, 1603222, 1365704, 3429576, 1881241, 1627864, 1750232, 1603286, 1881305, 1218132, 1218196, 1218260],
    [2462720, 2176000, 2176064, 2176128, 2176192, 2307073, 2307137, 2192912, 2307201, 2462784, 2307265, 331282, 2569234, 2192976, 2856465, 331346, 2569298, 2193040, 2856529, 2700819, 472596, 331410, 2569362, 2193104, 603669, 2462848, 2700883, 472660, 331474, 2569426, 742420, 603733, 2856593, 2700947, 3222547, 603797, 742484, 2462912, 2701011, 3222611, 603861, 1012757, 2856657, 3222675, 1012821, 1160193, 3616280, 1012885, 1160257, 3616344, 1012949, 1160321, 472724, 3616408, 742548, 1160385, 472788, 3616472, 742612, 3126290, 996892, 3214875, 1004572, 3126354, 996956, 3214939, 1127966, 3363870, 3126418, 997020, 3215003, 1128030, 3363934, 3126482, 997084, 3215067, 1128094, 3363998, 1021465, 1652233, 3222739, 1004636, 1685018, 1652297, 1379862, 1783327, 3364574, 1127646, 1021529, 1652361, 1510935, 1783391, 1397791, 1685082, 1652425, 1642013, 1783455, 1397855, 1021593, 1379926, 1783519, 1004700, 1685146, 1510999, 1397919, 1021657, 1642077, 1004764, 1685210, 1379990, 1397983, 1511063, 1642141, 1380054, 1511127, 1642205],
    [1915905, 2167808, 2167872, 2167936, 2168000, 2298881, 2298945, 2299009, 2178576, 2299073, 487938, 332802, 2178640, 2668051, 488002, 332866, 1915969, 2668115, 2178704, 2954773, 562708, 1916033, 2954837, 2668179, 1012246, 3085847, 726038, 2178768, 2929687, 3109400, 3085911, 857112, 1916097, 2929751, 3109464, 3085975, 857176, 2956818, 2929815, 1012310, 3086039, 726102, 2956882, 2929879, 3109528, 857240, 2956946, 2954901, 2668243, 1012374, 726166, 2957010, 3322902, 1274396, 988188, 857816, 3358225, 3322966, 3109080, 988764, 726742, 3358289, 3323030, 1273948, 988828, 3358353, 3323094, 1266185, 1119241, 333442, 3358417, 2954965, 3454491, 1266249, 1119305, 988892, 1391637, 1381898, 3454555, 1527818, 333506, 1391701, 3454619, 1266313, 1119369, 1391765, 1381962, 3454683, 1527882, 1391829, 562772, 1274012, 1119945, 1644061, 1785369, 1382026, 562836, 1921053, 1644125, 1785433, 562900, 1921117, 1644189, 1785497, 1382090, 2004506, 1921181, 1644253, 1785561, 2004570, 1921245, 2004634, 1527946, 2004698, 487554, 1265865, 1011926, 1528010, 1274076, 487618],
    [390144, 1668097, 1668161, 1668225, 1668289, 1799168, 1799232, 1799296, 390208, 1799360, 2298382, 488962, 2323470, 390272, 2298446, 489026, 2323534, 620036, 390336, 2306576, 750608, 2324110, 620100, 513548, 2706961, 2306640, 750672, 620164, 513612, 2297998, 2838034, 751248, 2585618, 620228, 513676, 882181, 2707025, 2306192, 2586194, 513740, 882245, 2969107, 2586258, 652813, 2969171, 2586322, 652877, 2969235, 3215893, 652941, 2969299, 2306768, 750800, 653005, 2707089, 3215957, 906767, 882309, 2707153, 3216021, 2324174, 1299457, 882373, 3239444, 2298062, 906831, 3239508, 3216085, 1299521, 1118744, 3239572, 906895, 1118808, 3239636, 1299585, 1118872, 2837586, 1144328, 906959, 1118936, 2837650, 1144392, 1299649, 1258009, 2837714, 1275401, 1144456, 1823762, 1258073, 1920535, 1275465, 1144520, 1823826, 1258137, 1920599, 1275529, 1823890, 1258201, 1920663, 489090, 1823954, 1920727, 1275593, 2059798, 489154, 2059862, 2059926, 2059990],
    [621568, 1659904, 1659968, 1660032, 1660096, 1790977, 1791041, 1791105, 753164, 1791169, 2561550, 480770, 753228, 2053648, 2684433, 2561614, 753292, 2053712, 2684497, 2561678, 753356, 2053776, 2684561, 2561742, 613392, 2053840, 3356175, 613456, 2938387, 3347973, 480834, 613520, 2938451, 3479058, 480898, 613584, 873991, 2938515, 3356239, 480962, 621632, 874055, 2938579, 3348037, 621696, 874119, 3077652, 3479122, 621760, 874183, 1111575, 3356303, 2972673, 3208728, 3348101, 2972737, 3077716, 3479186, 2972801, 1111639, 1390106, 2972865, 3208792, 3356367, 3243545, 3077780, 1390170, 3243609, 1111703, 3348165, 3243673, 3208856, 1390234, 1531405, 3077844, 3479250, 3243737, 1111767, 1390298, 1531469, 3208920, 2037269, 1793564, 2684625, 2045462, 1793628, 2029083, 2037333, 1793692, 2029147, 2045526, 1793756, 2029211, 2037397, 1529355, 1531533, 2029275, 2045590, 1529419, 1531597, 2037461, 1529483, 2045654, 1529547],
    [1840128, 2208768, 2208832, 2208896, 2208960, 2339841, 2339905, 2348560, 2339969, 1840192, 2340033, 374290, 2479635, 504851, 2503698, 374354, 2479699, 504915, 2503762, 3124756, 636437, 2479763, 504979, 2102801, 3124820, 767510, 636501, 2479827, 505043, 2102865, 3116054, 767574, 374418, 2348624, 2503826, 3124884, 767638, 636565, 2348688, 1840256, 3124948, 767702, 374482, 2348752, 2503890, 3378712, 1029144, 636629, 644117, 2496023, 3116118, 644181, 2496087, 3378776, 1029208, 1291803, 644245, 2102929, 3116182, 1291867, 644309, 2496151, 3378840, 1029272, 1291931, 1168411, 1840320, 3116246, 1291995, 3134981, 2102993, 3378904, 1029336, 1561622, 2496215, 3780124, 3135045, 529409, 3780188, 1692690, 529473, 3780252, 3135109, 529537, 4042266, 1168475, 529601, 4042330, 3135173, 1053716, 3780316, 1561686, 1316381, 4042394, 1692754, 1053780, 4042458, 1168539, 1316445, 3903001, 1561750, 1053844, 3903065, 1692818, 1316509, 3903129, 1168603, 1053908, 3903193, 1561814, 1316573, 1692882],
    [2202625, 2215937, 2200576, 2200640, 2200704, 2200768, 2331649, 2331713, 2331777, 2224656, 2202689, 2331841, 2224720, 2202753, 2831890, 2224784, 2202817, 2831954, 2224848, 2857984, 595475, 2858048, 2486801, 366086, 497172, 595539, 2858112, 2486865, 497236, 3487253, 2858176, 2486929, 497300, 595603, 2735124, 2486993, 497364, 2832018, 2735188, 2216001, 366150, 628232, 3618326, 2735252, 2216065, 628296, 3618390, 2735316, 2216129, 366214, 628360, 3618454, 2866182, 3657736, 628424, 3618518, 2866246, 3657800, 366278, 2832082, 2866310, 3657864, 3487317, 2866374, 3657928, 3487381, 3273241, 1285136, 3487445, 3789316, 1416209, 1152522, 1914392, 3273305, 1285200, 1152586, 1283595, 1914456, 3789380, 1416273, 1152650, 1283659, 1914520, 3273369, 1285264, 1152714, 1283723, 1914584, 3789444, 1416337, 1283787, 595667, 3273433, 1285328, 3789508, 1416401, 1954327, 1954391, 1954455, 1954519],
    [291840, 2214912, 1700865, 1700929, 1700993, 1701057, 1831936, 1832000, 1832064, 291904, 2214976, 1832128, 2855440, 291968, 2215040, 2855504, 292032, 2215104, 504338, 2485777, 554511, 504402, 2747393, 554575, 504466, 521731, 2747457, 554639, 504530, 521795, 2747521, 554703, 635411, 521859, 3175427, 2485841, 635475, 521923, 3175491, 2485905, 635539, 3175555, 2485969, 635603, 3175619, 3272213, 783894, 3510788, 1078289, 2747585, 783958, 3510852, 773652, 1209345, 784022, 2855568, 914950, 773716, 1078353, 784086, 3510916, 1046025, 773780, 1209409, 2855632, 915014, 773844, 1078417, 3510980, 1046089, 1209473, 3272277, 1937943, 915078, 1078481, 3272341, 1938007, 1046153, 1209537, 3272405, 1938071, 915142, 1734146, 1437208, 1046217, 1437272, 1864726, 1938135, 1734210, 1437336, 1437400, 1864790, 1734274, 1864854, 1734338, 1864918],
    [1922048, 1309697, 2085889, 2085953, 2086017, 2086081, 1922112, 1309761, 2725378, 1922176, 1309825, 2725442, 2315792, 1309889, 898578, 2096128, 2315856, 2725506, 2096192, 2315920, 2725570, 2096256, 2315984, 3249678, 2709009, 2096320, 898642, 2709073, 2219532, 3249742, 2709137, 2219596, 898706, 775699, 2709201, 2219660, 3249806, 775763, 1922240, 2219724, 898770, 775827, 3372051, 2752013, 3249870, 775891, 3503631, 2752077, 3905028, 1037845, 3372115, 2752141, 3905092, 1037909, 3503695, 2752205, 3905156, 1037973, 3372179, 3905220, 1038037, 3503759, 1414678, 3014152, 3372243, 1545233, 3014216, 3503823, 3014280, 1807892, 3765269, 1414742, 3014344, 3765333, 1545297, 1955339, 3765397, 1807956, 1955403, 3765461, 1414806, 1955467, 1545361, 1955531, 1808020, 1414870, 1545425, 1808084],
    [432128, 2381824, 1980416, 1980480, 1980544, 1980608, 2111489, 2111553, 2372108, 2111617, 2381888, 309260, 2111681, 276994, 2372172, 2381952, 309324, 408067, 2634255, 2382016, 571407, 2634319, 686605, 571471, 2634383, 309900, 686669, 2634447, 686733, 571535, 2371724, 309964, 686797, 2371788, 948225, 571599, 408131, 1088004, 948289, 659984, 277058, 948353, 1218573, 660048, 408195, 1088068, 948417, 660112, 277122, 1202693, 432192, 660176, 408259, 1202757, 1218637, 277186, 1088132, 1333777, 432256, 1464846, 1333841, 1218701, 1088196, 1202821, 1184274, 1743379, 1464910, 1184338, 1202885, 1743443, 1184402, 1718793, 1333905, 1743507, 1184466, 1718857, 1743571, 1464974, 1446420, 1849877, 1718921, 2005013, 1865749, 1446484, 1718985, 1333969, 432320, 1849941, 2005077, 1865813, 1446548, 1218765, 1465038, 1850005, 2005141, 1865877, 1446612, 2005717, 1865941, 1849557],
    [1939456, 1318913, 1579008, 1710081, 1579072, 1710145, 1579136, 1710209, 1579200, 1581583, 1939520, 1710273, 2653713, 1573395, 1939584, 2653777, 1704468, 1939648, 2653841, 1573459, 2464277, 2653905, 1704532, 2595346, 810500, 1573523, 2464341, 1072662, 1704596, 2595410, 1573587, 2464405, 1704660, 2595474, 2252311, 1581647, 2464469, 924184, 3177496, 2595538, 1318977, 924248, 3177560, 1581711, 924312, 3177624, 2996761, 1319041, 924376, 3177688, 2996825, 1581775, 2252375, 2996889, 1319105, 2252439, 2996953, 2761232, 1596939, 2761296, 2252503, 1055244, 2761360, 1597003, 1055308, 2761424, 1597067, 1055372, 1597131, 1055436, 1072726, 810564, 1072790, 810628, 1072854, 810692],
    [2291712, 2256896, 2127873, 2127937, 2128001, 2128065, 2256960, 449040, 293394, 2773010, 580113, 2113028, 293458, 424467, 555012, 2773074, 2291776, 2636819, 293522, 424531, 555588, 2773138, 449104, 2636883, 293586, 424595, 555652, 2773202, 580177, 2636947, 555716, 424659, 2291840, 2257024, 2637011, 817685, 2257088, 449168, 2112580, 1077265, 580241, 2112644, 817749, 2291904, 1077329, 2112708, 449232, 1077393, 2235413, 817813, 580305, 1077457, 2235477, 981527, 3428884, 2235541, 817877, 1243672, 3428948, 2235605, 1079817, 981591, 3429012, 1064473, 1079881, 1243736, 3429076, 1195546, 981655, 1470480, 1326614, 1759771, 1470544, 1064537, 1602076, 1759835, 1195610, 1079945, 1759899, 1733149, 1326678, 1602140, 1243800, 1064601, 1080009, 981719, 1733213, 1195674, 1473038, 1602204, 1759963, 1326742, 1473102, 1243864, 1470608, 1064665, 1473166, 1733277, 1195738, 1473230, 1602268, 1326806, 1470672, 1733341],
    [2119680, 2250753, 2119744, 2250817, 2119808, 2250881, 1972752, 2119872, 2250945, 285202, 1972816, 416273, 2357779, 2114050, 1972880, 2114114, 2357843, 1972944, 2638356, 2357907, 2897937, 2114178, 2742805, 2644485, 800786, 2768901, 3004951, 2644549, 2768965, 2882070, 932377, 2644613, 677913, 416337, 2769029, 3267098, 2898001, 2644677, 809499, 2769093, 3267162, 2898577, 940551, 415889, 3301383, 3267226, 1071644, 1194011, 940615, 285266, 3267290, 3301447, 1325084, 940679, 678489, 416465, 3301511, 3005015, 2898129, 940743, 809563, 3301575, 2742869, 800850, 2114242, 2882134, 931929, 285330, 3695128, 3005079, 1071708, 1194075, 678553, 3695192, 2742933, 1071772, 1325148, 809627, 3695256, 2882198, 1071836, 800914, 2357971, 3695320, 931993, 285394, 2638420, 3005143, 1194139, 678617, 2638484, 2742997, 1325212, 809691, 2638548, 2882262, 800978, 932057, 1194203, 1325276],
    [333824, 299008, 325632, 2144257, 2144321, 2144385, 2144449, 2275328, 2275392, 2275456, 325696, 465424, 2396176, 2275520, 325760, 465488, 2396240, 325824, 465552, 2396304, 2538004, 587777, 465616, 2396368, 2538068, 2789396, 727569, 587841, 2538132, 2789460, 727633, 587905, 2538196, 2789524, 727697, 587969, 2789588, 3201558, 727761, 989714, 3201622, 3183127, 1120792, 3201686, 3183191, 989778, 3201750, 3183255, 3332114, 1120856, 3183319, 3332178, 333888, 3314201, 989842, 3332242, 3314265, 3332818, 1120920, 3314329, 333952, 3463184, 3314393, 989394, 299072, 3463248, 1120984, 299136, 3463312, 334016, 299200, 3463376, 1767957, 1907227, 1610259, 2030106, 1907291, 1871873, 1768021, 1907355, 1610323, 2030170, 1907419, 1871937, 1768085, 1610387, 2030234, 1872001, 1768149, 1610451, 2030298, 1872065],
    [2373632, 2138112, 2136065, 2136129, 2136193, 2136257, 2267136, 2267200, 2267264, 2373696, 2138176, 2267328, 2767377, 2138240, 694786, 2767441, 2138304, 2547203, 694850, 2129922, 2767505, 2555410, 825860, 2373760, 2392068, 2555474, 825924, 2129986, 2767569, 2555538, 694914, 2373824, 2392132, 2547267, 956935, 825988, 2103827, 2130050, 2685959, 694978, 2103891, 2392196, 2817542, 956999, 826052, 2103955, 2130114, 2686023, 2104019, 2392260, 2547331, 957063, 2662928, 2686087, 2794004, 2547395, 957127, 2662992, 2686151, 2794068, 3079701, 2365974, 2663056, 3079765, 2366038, 2794132, 2817606, 2366102, 2663120, 3079829, 2366166, 2794196, 2817670, 3079893, 2817734, 2555602, 1874447, 1768983, 1874511, 1769047, 1874575, 1769111, 1874639, 1769175],
    [1883136, 2455553, 2160640, 2160704, 2160768, 2160832, 1883200, 2455617, 2423314, 1883264, 2455681, 455187, 457219, 2423378, 2407427, 2455745, 2683412, 2947588, 2423442, 2538500, 2718224, 455251, 2423506, 1883328, 2718288, 455315, 457283, 2407491, 2718352, 455379, 2947652, 2538564, 2718416, 2945557, 2800658, 3241984, 2945621, 457347, 2407555, 3242048, 2683476, 2947716, 1006104, 2538628, 2683540, 2800722, 1006168, 2683604, 457411, 1006232, 2407619, 3602952, 2945685, 2947780, 1006296, 2538692, 2945749, 2800786, 3242112, 3603016, 3338248, 2800850, 3242176, 3338312, 3063302, 1661457, 3603080, 3338376, 3063366, 1661521, 1626646, 1374746, 3063430, 1661585, 3603144, 3461146, 1374810, 3063494, 1661649, 3461210, 1374874, 3456537, 3233810, 3461274, 1374938, 3448343, 3233874, 3461338, 1899022, 3456601, 3233938, 3338440, 1899086, 3448407, 3234002, 1626710, 1899150, 3456665, 1626774, 1899214, 3448471, 1626838, 3456729, 3448535],
    [2154497, 2152449, 2152513, 2152577, 2152641, 2283520, 2283584, 2283648, 2154561, 2283712, 440849, 317457, 2277890, 2277954, 2783763, 2807827, 2278018, 3045908, 2938900, 702998, 318033, 2278082, 3045972, 2938964, 440401, 3070487, 711172, 2154625, 3438596, 2808403, 3184663, 3070551, 711236, 2154689, 3438660, 2939540, 3184727, 318097, 3070615, 711300, 3203072, 3438724, 440465, 3070679, 711364, 3203136, 3438788, 2808467, 3184791, 3203200, 2783315, 2939604, 3184855, 318161, 3203264, 3045524, 2808531, 440529, 3334167, 2783379, 1227288, 3334231, 3045588, 1366534, 1489435, 1497628, 3334295, 2783443, 1620506, 3334359, 3692550, 1366598, 1751068, 1497692, 3465744, 3824149, 1227352, 3465808, 3692614, 1366662, 1489499, 1497756, 3465872, 3824213, 1620570, 3465936, 3692678, 1366726, 1751132, 1497820, 1622557, 3824277, 703062, 1368594, 3692742, 1227416, 1622621, 3824341, 1489563, 1368658, 1997337, 1620634, 1622685, 1997401, 1751196, 1368722, 1997465, 703126, 1622749, 1997529, 1227480, 1368786, 1489627, 1620698, 1751260, 703190],
    [497664, 358400, 1781761, 2177024, 2177088, 2177152, 2177216, 1781825, 506384, 751632, 760337, 1781889, 752208, 760401, 1781953, 752272, 760465, 2560016, 752336, 358464, 760529, 2560080, 358528, 2726404, 2560144, 473605, 358592, 2726468, 2560208, 604691, 473669, 3084288, 2856979, 743425, 473733, 3084352, 2726532, 743489, 604755, 997909, 473797, 3084416, 2857043, 743553, 604819, 997973, 3084480, 2857107, 743617, 604883, 998037, 1267733, 3478019, 2726596, 1128982, 1145364, 3119126, 3478083, 998101, 1129046, 1407511, 3119190, 3478147, 1530392, 3478211, 2857171, 1249810, 1267797, 505936, 1249874, 1145428, 506000, 1129110, 1391116, 1249938, 1530456, 3119254, 1129174, 1522189, 1250002, 1407575, 3119318, 1391180, 1267861, 506064, 1522253, 1145492, 497728, 1391244, 1407639, 497792, 1522317, 1530520, 497856, 1391308, 1267925, 1522381, 1145556, 1530584, 1407703],
    [2301952, 2168833, 2168897, 2168961, 2169025, 2299904, 2299968, 2529808, 2300032, 2302016, 2300096, 2063890, 2431505, 2660369, 2302080, 2194963, 2431569, 2660433, 2302144, 596482, 2195027, 2431633, 2660497, 720915, 596546, 2063954, 2431697, 2660561, 729106, 596610, 2195091, 965140, 720979, 596674, 2064018, 2668546, 729170, 2195155, 965204, 721043, 2850309, 2668610, 1245717, 2850373, 965268, 860695, 2850437, 2668674, 860759, 2850501, 965332, 729234, 2064082, 2668738, 860823, 1006613, 2930711, 721107, 1408536, 2930775, 1384472, 1138201, 2930839, 1245781, 1006677, 2931415, 3473946, 1138265, 2529872, 3474010, 1408600, 2529936, 3474074, 1007253, 2530000, 3474138, 1138329, 2013718, 1384536, 1408664, 2013782, 1245333, 1007317, 2013846, 1384600, 1138393, 2013910, 1245397, 1408728, 729298, 1384664, 860375],
    [2169856, 1964033, 2193408, 2324481, 2193472, 2324545, 2193536, 2324609, 2193600, 2169920, 1964097, 2324673, 2169984, 1964161, 2170048, 1964225, 2978323, 2571794, 776720, 2978387, 605203, 776784, 2978451, 605267, 776848, 2978515, 605331, 776912, 3240468, 2571858, 1169937, 3101188, 2571922, 1170001, 3240532, 1014277, 2571986, 1170065, 3101252, 1014341, 605395, 1170129, 3240596, 1014405, 3218951, 3143680, 3101316, 1014469, 3219015, 3143744, 3240660, 3219079, 3143808, 3101380, 1276426, 3219143, 3143872, 3625493, 1276490, 1515031, 3887638, 1276554, 1515095, 3625557, 1276618, 1538572, 3349516, 3887702, 1538636, 3349580, 3625621, 1538700, 3349644, 3887766, 1931791, 1538764, 3349708, 3625685, 1931855, 3529240, 1515159, 3887830, 1931919, 3529304, 1515223, 1931983, 3529368, 3529432],
    [2048001, 2185217, 2185281, 2185345, 2185409, 2316288, 2316352, 2316416, 2449936, 2316480, 2677250, 342546, 2447362, 2450000, 342610, 2816517, 2572293, 342674, 2816581, 481811, 2572357, 342738, 2816645, 481875, 2572421, 2562580, 2816709, 612372, 2572485, 3340821, 2832403, 612948, 2447938, 2450064, 2676802, 2562132, 613012, 2448002, 481939, 2450128, 2676866, 2562196, 613076, 2448066, 3097105, 2676930, 2562260, 875032, 3097169, 1104406, 2955288, 875096, 482003, 2048065, 850455, 2955352, 3097233, 1104470, 3226116, 2048129, 850519, 2832467, 3097297, 1104534, 3226180, 2048193, 850583, 2955928, 874648, 3358739, 1104598, 2955992, 874712, 3490307, 850647, 2832531, 3358803, 1923609, 3340885, 3226244, 3490371, 1923673, 3340949, 2832595, 3358867, 1923737, 3341013, 3226308, 3490435, 2038298, 3358931, 1783833, 3490499, 2038362, 1794048, 1783897, 1794112, 1923801, 2038426, 1794176, 1783961, 1794240, 2038490, 1784025],
    [268289, 382977, 1685504, 1685568, 1685632, 1685696, 1816577, 1816641, 1816705, 399884, 645132, 1816769, 2724366, 375298, 530959, 2480653, 2724430, 375362, 531023, 645708, 2724494, 375426, 768517, 539153, 2611205, 2724558, 375490, 768581, 531087, 2611269, 627218, 768645, 531151, 2611333, 758291, 768709, 2611397, 399436, 627282, 268353, 383041, 766484, 400012, 2480717, 758355, 645260, 268417, 1028629, 400076, 383105, 766548, 268481, 2480781, 1028693, 539217, 645324, 627346, 539281, 383169, 1030664, 1544727, 539345, 2480845, 1544791, 3274754, 1587728, 1292809, 1030728, 758419, 3274818, 1587792, 1292873, 766612, 1423883, 3274882, 1587856, 1292937, 1030792, 1028757, 1423947, 3274946, 1587920, 1293001, 1544855, 1424011, 1956374, 1316864, 1030856, 627410, 1424075, 1570816, 1447949, 758483, 1956438, 1316928, 1544919, 1570880, 1448013, 766676, 1956502, 1316992, 1028821, 1570944, 1448077, 1956566, 1317056, 1571008, 1448141],
    [622592, 1677312, 1808385, 1677376, 1808449, 1677440, 1808513, 1572364, 1677504, 753676, 1808577, 1572428, 885261, 2202126, 629251, 1572492, 630785, 891396, 1825796, 2982415, 891460, 1825860, 2982479, 891524, 2693648, 1021968, 1825924, 2982543, 891588, 2693712, 1022032, 1825988, 2982607, 2202190, 2824723, 1572556, 1024014, 2202254, 2824787, 777230, 753740, 2202318, 2824851, 777294, 622656, 2693776, 1022096, 777358, 1147412, 2824915, 777422, 1147476, 2693840, 1022160, 908308, 885325, 1251861, 908372, 630849, 1382929, 908948, 1024078, 1415688, 1514002, 909012, 753804, 1260054, 622720, 1415752, 1251925, 629315, 1147028, 1382993, 629379, 885389, 1415816, 1514066, 630913, 1260118, 1024142, 1415880, 1251989, 629443, 753868, 1383057, 622784, 1514130, 1147092, 1260182, 885453, 1252053, 630977, 1383121, 1024206, 1514194, 1260246],
    [2390016, 637952, 1701889, 1701953, 1702017, 1702081, 1832960, 1833024, 1833088, 638016, 547343, 1833152, 391682, 547407, 2596368, 2226691, 522756, 547471, 2596432, 2226755, 653842, 547535, 2596496, 2226819, 522820, 2906641, 2596560, 3002899, 2750981, 2989061, 3307536, 3002963, 2751045, 2989125, 3569667, 3003027, 2751109, 2906705, 2989189, 3003091, 2751173, 2390080, 2989253, 774677, 391746, 915976, 891912, 3307600, 3396120, 653906, 916040, 891976, 3569731, 522884, 3396184, 916104, 2906769, 892040, 391810, 3396248, 916168, 892104, 2390144, 2226883, 653970, 3396312, 638080, 3307664, 1178137, 522948, 1045014, 638144, 3569795, 1178201, 391874, 1176084, 2906833, 1424388, 1178265, 654034, 774741, 2390208, 1555458, 1178329, 774805, 1686546, 3307728, 774869, 1424452, 3569859, 1045078, 1555522, 1857561, 1176148, 1686610, 1857625, 1045142, 1424516, 1857689, 1176212, 1555586, 1857753, 1823258, 1989143, 1686674, 1823322, 1989207, 1424580, 1823386, 1989271, 1555650, 1823450, 1989335, 1686738, 1045206, 1176276],
    [1564673, 2086912, 2086976, 2087040, 2087104, 2217985, 2218049, 1948172, 2218113, 1564737, 2218177, 2578959, 637454, 1564801, 2579023, 637518, 1564865, 2579087, 637582, 1827344, 2579151, 637646, 1827408, 907794, 2840594, 1038867, 1948236, 2088979, 2972165, 1038931, 1948300, 2089043, 907858, 2840658, 1038995, 1948364, 2089107, 2972229, 1039059, 2734605, 2089171, 907922, 2840722, 2734669, 1827472, 907986, 2840786, 1300999, 2734733, 2613255, 2972293, 2734797, 770577, 2972357, 1301063, 1153043, 2613319, 3103254, 1432087, 1161239, 1032725, 3103318, 1301127, 1153107, 1432151, 1827536, 3103382, 1432215, 1161303, 2613383, 3103446, 1301191, 1153171, 1432279, 2613447, 1669656, 1161367, 770641, 2054681, 1153235, 1032789, 2054745, 1161431, 770705, 2054809, 1554964, 1032853, 2054873, 1555028, 770769, 1669720, 1555092, 1032917, 1669784, 1555156, 1669848],
    [2128896, 277504, 277568, 277632, 277696, 408577, 408641, 408705, 2391561, 408769, 1588747, 2391625, 433676, 1850380, 1588811, 2391689, 1588875, 2391753, 1588939, 949770, 2670093, 671236, 949834, 2670157, 671300, 949898, 2670221, 671364, 949962, 2670285, 671428, 2128960, 2627086, 695823, 2129024, 695887, 2129088, 3020304, 1850956, 433228, 2645007, 1851020, 695951, 2645071, 2627150, 1851084, 1097234, 2645135, 2627214, 933383, 1097298, 2645711, 3020368, 933447, 1097362, 1342993, 2627278, 933511, 1359380, 1727499, 3020432, 433292, 1343057, 3020496, 695503, 1727563, 923155, 1613335, 1343121, 1185301, 1613399, 1727627, 923219, 933575, 1359444, 1343185, 1185365, 1613463, 1727691, 923283, 1359508, 1185429, 1613527, 923347, 1097426, 1185493, 1359572, 1848854, 433356, 1848918, 1848982, 1849046],
    [1186817, 1186881, 1186945, 1187009, 1317888, 1317952, 2521602, 1318016, 1318080, 2500099, 2521666, 2500163, 2521730, 2727439, 2500227, 269828, 2914308, 1031696, 2500291, 400913, 2521794, 663059, 2341905, 2631188, 269892, 3176467, 2727503, 2622994, 400977, 2914372, 2341969, 2631252, 269956, 2914436, 794118, 2727567, 2631316, 401041, 3701261, 2342033, 2631380, 270020, 2914500, 1031760, 663123, 2623058, 401105, 3176531, 2342097, 663187, 2623122, 3176595, 1031824, 663251, 2623186, 3176659, 1031888, 3701325, 2727631, 3701389, 3701453, 1595916, 3128854, 1726990, 3128918, 1210901, 3128982, 1595980, 3129046, 1727054, 1210965, 1596044, 1727118, 794182, 1211029, 794246, 1596108, 794310, 1727182, 1211093],
    [283648, 1841153, 293888, 293952, 294016, 294080, 424961, 425025, 2031118, 425089, 422926, 1841217, 425153, 2293263, 423502, 1841281, 2293327, 423566, 1841345, 2293391, 793091, 423630, 2293455, 670212, 685071, 2030670, 283712, 670276, 2030734, 670340, 685135, 2030798, 415248, 1063431, 1063495, 283776, 1080841, 2234377, 685199, 1080905, 2234441, 283840, 1113617, 1080969, 2234505, 415312, 1081033, 2234569, 685263, 3071508, 1332754, 793155, 3071572, 1332818, 793219, 3071636, 1332882, 1063559, 3071700, 1332946, 793283, 1506835, 1186325, 1474060, 1113681, 1186389, 415376, 1506899, 1186453, 1474124, 415440, 1113745, 1186517, 1474188, 1506963, 1988118, 1604630, 1063623, 1474252, 1996311, 1113809, 1735703, 670404, 1988182, 1507027, 1604694, 1996375, 1735767, 1988246, 1604758, 1996439, 1735831, 1988310, 1604822, 1996503, 1735895],
    [1440769, 1858560, 1858624, 1858688, 1858752, 1989633, 1989697, 1580546, 1989761, 1702914, 1989825, 2123267, 417296, 540174, 1703490, 1984015, 548370, 2244115, 1834513, 2384914, 548434, 540238, 1834577, 2384978, 548498, 2244179, 1834641, 2385042, 548562, 540302, 1834705, 2385106, 941575, 2244243, 2088470, 1984079, 941639, 540366, 1440833, 1984143, 941703, 2244307, 1703554, 1984207, 941767, 1580098, 1440897, 2123331, 417360, 1580162, 1703618, 2123395, 417424, 1580226, 1440961, 1465880, 2123459, 417488, 924696, 2088534, 1465944, 2770453, 924760, 2088598, 1466008, 2770517, 924824, 2088662, 1466072, 2770581, 2891289, 2882567, 2770645, 2891353, 2882631, 2901527, 2891417, 2882695, 2901591, 2891481, 2882759, 2901655, 924888, 3144720, 2901719, 1457684, 3144784, 1457748, 3144848, 1457812, 3144912, 1457876],
    [2274304, 1899520, 310272, 441345, 310336, 441409, 310400, 441473, 310464, 2274368, 450062, 441537, 2309648, 2274432, 450126, 2309712, 2274496, 450190, 2309776, 431105, 450254, 2309840, 581135, 431169, 728594, 581199, 431233, 867857, 581263, 431297, 728658, 581327, 701454, 728722, 704019, 1899584, 701518, 3096084, 704083, 1899648, 955925, 3096148, 1899712, 955989, 728786, 2809346, 701582, 3096212, 704147, 2939923, 956053, 1121814, 2809410, 1357335, 3096276, 966152, 2939987, 701646, 1121878, 966216, 2809474, 956117, 867921, 704211, 966280, 2940051, 1121942, 966344, 2809538, 867985, 2940115, 1873433, 1122006, 1621017, 1629720, 1873497, 868049, 1621081, 1629784, 1357399, 1629848, 1873561, 1777178, 1621145, 1629912, 1357463, 1873625, 1777242, 1621209, 1357527, 1777306, 1777370],
    [1874945, 1875009, 1875073, 1875137, 2006016, 2006080, 2006144, 2006208, 2663950, 1981454, 2554383, 2664014, 1981518, 2685457, 2664078, 1981582, 2685521, 2786834, 2554447, 3180051, 2685585, 3209744, 2664142, 1981646, 2554511, 2786898, 2685649, 3180115, 2554575, 2104853, 3311124, 2923541, 564758, 3471876, 2786962, 2767894, 564822, 3209808, 3180179, 2767958, 564886, 3471940, 2104917, 3311188, 2923605, 564950, 3209872, 2787026, 2768022, 3472004, 3180243, 2768086, 3209936, 2104981, 3311252, 1220105, 2923669, 3472068, 2105045, 3311316, 1220169, 2923733, 1476119, 1505816, 1220233, 3185687, 1476183, 1636889, 1220297, 3185751, 1482251, 1476247, 1505880, 3185815, 1482315, 1476311, 1636953, 3185879, 1482379, 1505944, 2008602, 1482443, 1637017, 1506008, 2008666, 1637081, 2008730, 2008794],
    [1932288, 2413569, 326657, 326721, 326785, 326849, 457728, 457792, 457856, 1932352, 2413633, 457920, 1932416, 2553359, 2791953, 2162194, 1932480, 2553423, 3054083, 2162258, 2317838, 2553487, 3054147, 2162322, 2317902, 2553551, 2424339, 3054211, 2162386, 2317966, 2413697, 3054275, 851460, 2318030, 2413761, 3315716, 851524, 2718739, 2946576, 3315780, 851588, 2710546, 2946640, 2424403, 3315844, 851652, 2718803, 2946704, 3315908, 2710610, 2946768, 2792017, 1242644, 2710674, 2792081, 1373201, 2710738, 2424467, 2792145, 1242708, 2718867, 1481237, 1373265, 2719443, 2424019, 1612311, 1242772, 1882646, 1373329, 1481301, 1242836, 1612375, 1373393, 1882710, 1889816, 1481365, 1889880, 1612439, 1889944, 1882774, 1890008, 1481429, 1612503, 1882838],
    [2417664, 2137089, 1891328, 1891392, 1891456, 1891520, 2022401, 2022465, 2260482, 2022529, 2417728, 2137153, 2022593, 318990, 2260546, 2541059, 2137217, 2260610, 2541123, 2137281, 2260674, 2541187, 2399232, 2915342, 2541251, 2399296, 2121234, 2803215, 2399360, 2417792, 2399424, 2803279, 2932241, 2803343, 2932305, 2121298, 2803407, 2932369, 319054, 2915406, 2417856, 2932433, 974343, 319118, 2915470, 3055125, 1230352, 974407, 319182, 2915534, 1230416, 1088527, 3309076, 1492502, 1088591, 3309140, 1492566, 1088655, 3309204, 1492630, 1088719, 3309268, 1351187, 1230480, 974471, 1498647, 2121362, 3316759, 1492694, 974535, 1498711, 2121426, 3316823, 1230544, 3055189, 1498775, 3316887, 3055253, 1498839, 3316951, 3055317, 1351251, 1760781, 1351315, 1760845, 1351379, 1760909, 1760973],
    [351232, 2429952, 343041, 343105, 343169, 343233, 474112, 474176, 474240, 2430016, 482830, 474304, 1949201, 2046993, 2430080, 482894, 1949265, 2047057, 2430144, 482958, 630288, 3094018, 483022, 630352, 3094082, 744975, 630416, 3094146, 351296, 630480, 3094210, 745039, 736773, 1949329, 2047121, 351360, 3609615, 1949393, 2047185, 3609679, 745103, 998918, 736837, 3120661, 2964501, 1130006, 351424, 3609743, 736901, 3120725, 2964565, 1130070, 745167, 3609807, 3120789, 2964629, 1130134, 2841622, 3871745, 3120853, 2964693, 1130198, 1259031, 2841686, 736965, 3251736, 1259095, 2841750, 3251800, 2841814, 3871809, 3251864, 1259159, 1269267, 3251928, 1539602, 3871873, 1259223, 1269331, 1539666, 3871937, 3513881, 1775124, 1269395, 3513945, 1775188, 1539730, 3514009, 1775252, 1269459, 3514073, 1775316, 1539794, 998982, 999046, 999110],
    [2014209, 1907712, 1907776, 1907840, 1907904, 2038785, 2038849, 2038913, 2276866, 2038977, 2688526, 882702, 2432014, 2276930, 591376, 350224, 2563088, 2014273, 466449, 350800, 2696209, 2563152, 2276994, 466513, 883278, 2696273, 2432078, 2014337, 2694674, 466577, 2709522, 2696337, 2563728, 2277058, 2694738, 466641, 2709586, 2696401, 2432654, 2014401, 590928, 350352, 2563792, 2792975, 2694802, 2709650, 2688078, 2432718, 2793039, 590992, 882830, 2793103, 2694866, 2709714, 2688142, 2793167, 1137175, 591056, 826901, 1399320, 2688206, 957972, 1399384, 3089942, 1228314, 1399448, 3090006, 1228378, 1399512, 3090070, 1228442, 1792539, 3090134, 1228506, 1508889, 1800217, 1646090, 826965, 1137239, 1639955, 1646154, 958036, 1792603, 1508953, 1646218, 958100, 1800281, 1640019, 1646282, 827029, 1137303, 1509017, 827093, 1792667, 1640083, 958164, 1800345, 1509081, 1137367, 1640147, 1792731, 350416, 1800409, 882894],
    [1178624, 1930241, 359424, 359488, 359552, 359616, 490497, 490561, 490625, 1178688, 1930305, 490689, 1178752, 1930369, 1015299, 1178816, 1930433, 1015363, 2446339, 1965582, 1015427, 2446403, 1965646, 1015491, 2446467, 1965710, 2963986, 2446531, 1965774, 3095044, 2840081, 2350607, 3095108, 2840145, 2350671, 3095172, 2840209, 2350735, 3095236, 2840273, 2350799, 2964050, 3233299, 2743810, 3217940, 3233363, 2874885, 3218004, 1277462, 3233427, 3005441, 3487766, 1277526, 3233491, 2743874, 3487830, 1277590, 3634704, 2874949, 3487894, 1277654, 3634768, 3005505, 3487958, 3634832, 2743938, 2964114, 2875013, 2964178, 3005569, 3634896, 3218068, 2744002, 3218132, 2875077, 1915413, 3005633, 1915477, 1801741, 1915541, 1801805, 1915605, 1801869, 1801933],
    [353280, 2153472, 2300929, 1924096, 2055169, 1924160, 2055233, 1924224, 2055297, 1924288, 345602, 2153536, 2300993, 2055361, 2442756, 335374, 2153600, 335438, 2153664, 746497, 2704902, 335502, 2704966, 335566, 2705030, 2301057, 2705094, 2301121, 876040, 2825733, 345666, 2825797, 1271314, 982547, 2825861, 3499540, 982611, 2442820, 2825925, 2948629, 3489297, 2442884, 2948693, 3489361, 2442948, 2948757, 3489425, 3499604, 2948821, 3489489, 1271378, 982675, 1261072, 3499668, 982739, 1523215, 3499732, 3202583, 1400344, 1653784, 353344, 3202647, 876104, 1400408, 1653848, 746561, 3202711, 1400472, 1261136, 1271442, 3202775, 876168, 1523279, 345730, 1637910, 876232, 1400536, 1653912, 353408, 1637974, 1261200, 746625, 1638038, 1523343, 1271506, 1638102, 1653976, 345794, 1261264, 353472, 1523407, 746689],
    [515072, 375808, 375872, 375936, 376000, 506881, 506945, 507009, 646670, 507073, 1719823, 769552, 646734, 1719887, 769616, 646798, 2506258, 769680, 900627, 646862, 1719951, 2864643, 769744, 900691, 2358288, 1720015, 3118596, 900755, 2358352, 802321, 3118660, 900819, 2358416, 3118724, 1842710, 1162262, 2358480, 3118788, 2506322, 1162838, 2612757, 2864707, 2506386, 1162902, 2612821, 2864771, 2506450, 1162966, 2612885, 2864835, 1842262, 2612949, 890388, 1842326, 1039379, 890452, 1842390, 1039443, 890516, 2498071, 1039507, 1422872, 2760198, 1039571, 1422936, 2498135, 1047567, 1423000, 2760262, 1047631, 1423064, 2498199, 1047695, 1816089, 2760326, 1047759, 1816153, 2498263, 515136, 2070042, 2760390, 1818124, 515200, 2070106, 802385, 1818188, 515264, 2070170, 802449, 1818252, 1816217, 802513, 1818316, 890580, 2070234, 1816281],
    [2327553, 1940480, 1940544, 1940608, 1940672, 2071553, 2071617, 514562, 2071681, 2327617, 2071745, 514626, 2327681, 514690, 2327745, 368142, 499215, 2488335, 493060, 2702864, 368206, 499279, 784398, 632326, 2702928, 499343, 2488399, 754690, 761351, 2702992, 499407, 784462, 885767, 859666, 2488463, 3122705, 2833939, 2488527, 1148419, 2834003, 368270, 784526, 3122769, 3227156, 368334, 784590, 493124, 3227220, 514754, 3122833, 761415, 3227284, 3397635, 885831, 3227348, 1023510, 3398211, 3122897, 761479, 3620373, 1154569, 3398275, 632390, 761543, 3620437, 1023574, 3398339, 754754, 3620501, 1154633, 1308694, 1147971, 3620565, 1023638, 1562633, 493188, 2834067, 1154697, 1308758, 885895, 2834131, 1547799, 1023702, 1693719, 632454, 2703056, 1547863, 1154761, 1693783, 754818, 859730, 1547927, 1562697, 1148035, 859794, 1547991, 1693847, 493252, 859858, 1308822, 885959, 1562761, 632518, 1693911, 754882, 1308886, 1148099, 1562825],
    [1866753, 392192, 392256, 392320, 392384, 523265, 523329, 523393, 2522633, 523457, 2079234, 1866817, 2079298, 382475, 654852, 2522697, 2079362, 382539, 654916, 1866881, 2079426, 382603, 654980, 2522761, 382667, 655044, 1866945, 2522825, 899598, 1203724, 899662, 2872847, 1203788, 899726, 3003921, 2489872, 1203852, 785925, 2988048, 3003985, 2489936, 1203916, 785989, 2988112, 3004049, 2490000, 2383373, 786053, 2988176, 3004113, 2490064, 2383437, 786117, 2988240, 1431060, 2383501, 1284627, 2872911, 916999, 2383565, 1284691, 2872975, 917063, 2776068, 1284755, 2873039, 917127, 2776132, 1284819, 1308181, 917191, 2776196, 899790, 1439254, 2776260, 1431124, 2907658, 1308245, 3038738, 1439318, 2907722, 1431188, 3038802, 1308309, 2907786, 1439382, 3038866, 1431252, 2907850, 1308373, 3038930, 1439446],
    [2333696, 1301505, 1301569, 1301633, 1301697, 384000, 384064, 384128, 2465282, 384192, 884233, 648714, 1564168, 2079752, 884297, 2352652, 1564232, 2079816, 884361, 2352716, 1564296, 2079880, 884425, 2483725, 1564360, 2079944, 1146383, 2483789, 2465346, 2999812, 2457105, 1956881, 2465410, 2483853, 2588176, 1957457, 2465474, 2483917, 2588240, 1957521, 2333760, 2999876, 2588304, 1957585, 2333824, 648778, 2588368, 2333888, 2456657, 2352780, 2997257, 2456721, 648842, 1293838, 2456785, 2352844, 2997321, 2981395, 648906, 1293902, 2981459, 2999940, 2997385, 1146447, 3000004, 1293966, 2981523, 1820181, 2997449, 1146511, 1820245, 1170951, 1294030, 1146575, 1820309, 1171015, 1678866, 2981587, 1820373, 1171079, 1678930, 1662486, 1951255, 1171143, 1678994, 1670676, 1951319, 1679058, 1662550, 1951383, 1809931, 1670740, 1951447, 1809995, 1662614, 1810059, 1670804, 1810123, 1662678, 1670868],
]
LEAVES = [
    [963, 964, 965],
    [963, 966, 967, 968],
    [964, 965, 968, 969, 971, 972],
    [962, 963, 964, 965, 967, 970, 971, 972, 973],
    [966, 968, 969, 971, 972, 973],
    [968, 969, 970, 971, 972, 973],
    [963, 964, 965, 966, 967, 969, 970, 971, 972, 973],
    [964, 965, 966, 967, 968, 970, 971, 972, 973],
    [963, 964, 965, 966, 967, 968, 969, 970, 971, 972, 973],
    [965, 966, 967, 968, 969, 970, 973],
    [962, 963, 964, 966, 967, 968, 969, 970, 971, 972, 973],
    [962, 963, 964, 966, 967, 968, 969, 970, 972, 973],
    [964, 965, 966, 968, 969, 970, 971, 972, 973],
    [964, 966, 967, 968, 969, 970, 972],
    [965, 966, 967, 968, 969, 970, 971],
    [962, 963, 966, 968],
    [962, 963, 964, 965, 967, 968, 970, 971],
    [965, 968, 970, 971, 972, 973, 974],
    [963, 965, 966, 970],
    [962, 963, 966, 967, 968, 969, 970, 971],
    [965, 966, 967, 969, 971, 972, 973, 974, 975],
    [962, 964, 965, 966, 967, 968, 969, 970, 971, 972, 973, 975],
    [964, 965, 966, 967, 968, 969, 970, 971, 973, 974, 975],
    [962, 966, 967, 969, 970, 971, 972, 973, 974, 975],
    [962, 965, 966, 967, 968, 969, 970, 971, 972, 973, 974, 975],
    [962, 965, 966, 968, 969, 972, 973, 974, 975],
    [962, 964, 966, 967, 968, 969, 970, 971, 972, 973, 974, 975],
    [962, 963, 964, 965, 966, 967, 968, 969, 970, 971, 972, 974],
    [963, 965, 966, 968, 969, 970, 972, 973, 974, 975],
    [964, 965, 966, 967, 968, 969, 970, 971, 973],
    [963, 964, 965, 966, 967, 968, 969, 970, 971, 972],
    [962, 967, 968, 970, 971],
    [963, 964, 965, 967, 969, 970, 971],
    [964, 965, 967, 969, 970, 971, 972, 973, 974],
    [962, 963, 965, 966, 967, 968, 971, 972, 974, 975],
    [964, 966, 967, 968, 969, 970, 971, 972, 973, 974, 975],
    [962, 963, 967, 968, 969, 971],
    [963, 964, 965, 967, 971],
    [964, 966, 967, 969, 971, 972, 973, 974, 975],
    [963, 964, 965, 967, 968, 969, 970, 971, 972, 973, 974, 975],
    [962, 964, 965, 967, 968, 969, 970, 971, 972, 973, 974, 975],
    [963, 965, 966, 967, 969, 970, 971, 973, 974],
    [962, 963, 964, 969, 970, 972, 973, 975],
    [964, 965, 966, 967, 968, 969, 970, 971, 972, 973, 974, 975],
    [963, 964, 965, 966, 967, 968, 969, 970, 972, 973, 975],
    [962, 963, 964, 965, 968, 969, 970, 971, 972, 973, 974, 975],
    [962, 963, 965, 966, 967, 968, 969, 970, 972, 973, 974],
    [962, 963, 965, 966, 968, 969, 970, 971],
    [967, 968, 969, 970, 971],
    [962, 963, 964, 965, 966, 967, 968, 969, 970, 972, 973, 974],
    [965, 966, 967, 968, 969, 970, 972, 975],
    [962, 963, 964, 965, 966, 967, 968, 969, 970, 971, 972, 973, 974, 975],
    [963, 964, 965, 966, 967, 970, 971, 972, 973, 974, 975],
    [962, 963, 964, 965, 966, 967, 969, 970, 971, 973, 974, 975],
    [962, 965, 967, 968, 969, 970, 971],
    [963, 965, 969, 971],
    [963, 965, 968, 969, 970, 971, 972, 973, 974, 975],
    [964, 965, 966, 967, 968, 969, 970, 971, 973, 974, 975],
    [963, 964, 965, 967, 968, 970, 972, 973, 975],
    [963, 964, 965, 967, 968, 969, 970, 971, 972, 973, 974, 975],
    [963, 965, 966, 967, 968, 969, 970, 971, 972, 973, 974, 975],
    [962, 963, 964, 965, 966, 967, 971, 972, 973, 974, 975],
    [963, 966, 967, 968, 969, 970, 971, 972, 973, 974],
    [962, 964, 965, 967, 969, 970, 971],
    [962, 964, 965, 966, 967, 968, 970, 971],
    [962, 964, 965, 966, 969, 970, 971, 972, 973, 974],
    [962, 964, 965, 966, 967, 970, 971, 972, 973, 974, 975],
    [962, 963, 964, 965, 966, 967, 969, 970, 971, 972, 973, 974],
    [964, 966, 969, 970, 971, 972, 973, 974, 975],
    [962, 964, 965, 966, 969, 971, 972, 973, 974, 975],
    [964, 965, 966, 967, 968, 970, 971, 973, 974, 975],
    [962, 964, 965, 967, 969, 970, 971, 972, 973, 974, 975],
    [962, 963, 969, 971],
    [963, 964, 965, 966, 967, 968, 969, 971],
    [963, 966, 967, 968, 969, 971, 972, 973, 975],
    [962, 963, 964, 965, 966, 967, 968, 969, 970, 971, 972, 973, 974, 975],
    [962, 963, 964, 965, 966, 969, 971, 972, 973, 974, 975],
    [962, 965, 966, 967, 968, 969, 971, 972, 973, 974, 975],
    [962, 963, 964, 967, 969, 970, 971, 972, 974],
    [963, 964, 965, 966, 967, 968, 969, 970, 971],
    [962, 963, 965, 966, 968, 970],
    [962, 963, 964, 965, 966, 967, 968, 969, 970, 971, 972, 973, 974],
    [962, 963, 964, 965, 966, 967, 968, 969, 971, 972, 973, 974, 975],
    [965, 966, 967, 970, 971, 973, 974, 975],
    [966, 967, 968, 970, 971, 972, 973, 974, 975],
    [962, 963, 964, 965, 967, 968, 970, 971, 972, 975],
    [965, 966, 967, 968, 969, 970, 971, 972, 973, 974, 975],
    [962, 964, 965, 966, 969, 970, 971, 972, 973, 974, 975],
    [962, 963, 964, 965, 966, 967, 968, 970, 971, 972, 973, 974, 975],
    [963, 964, 965, 966, 967, 968, 971, 972, 973, 974, 975],
    [963, 966, 967, 970, 971],
    [963, 964, 966, 968, 969, 970],
    [962, 963, 964, 966, 967, 968, 969, 970, 971, 972, 973, 974, 975],
    [962, 963, 965, 967, 969, 972, 973, 974, 975],
    [965, 967, 968, 970, 971, 972, 973, 974],
    [963, 965, 966, 967, 969, 970],
    [966, 967, 968, 970, 971],
    [962, 963, 965, 966, 967, 968, 969, 970, 973, 974],
    [962, 963, 965, 966, 967, 968, 970, 971, 972, 973, 975],
    [963, 964, 966, 968, 969, 970, 971, 972, 973, 974, 975],
    [962, 963, 964, 965, 966, 967, 968, 969, 970, 971, 972, 973, 974, 975],
    [965, 968, 969, 970, 971, 972, 973, 974],
    [962, 965, 967, 969, 970, 971, 972, 973, 975],
    [963, 965, 967, 968, 969, 970, 971, 972, 973, 974, 975],
    [962, 966, 967, 968, 969, 970, 971, 974, 975],
    [963, 964, 966, 967, 968, 969, 970, 971, 972, 973, 974, 975],
    [962, 963, 966, 968, 969, 971, 973, 974],
    [966, 967, 968, 969, 970, 971, 972, 973, 974, 975],
    [963, 964, 966, 967, 970],
    [962, 965, 966, 967, 969, 970, 971],
    [966, 967, 969, 970, 971, 972, 973, 974],
    [962, 963, 964, 966, 968, 969, 970, 971],
    [962, 963, 965, 966, 968],
    [965, 967, 968, 969, 970, 971],
    [962, 965, 966, 968, 970, 971, 973],
    [964, 965, 966, 968, 969, 970, 971, 972, 973],
    [963, 964, 965, 966, 967, 969, 970, 971, 972, 973],
    [962, 963, 965, 966, 967, 968, 970, 972, 973],
    [962, 965, 966, 967, 968, 969, 970, 971, 972, 973],
    [964, 965, 966, 968, 969, 970, 971, 972],
    [963, 964, 967, 968, 969, 970, 971, 972, 973],
    [963, 964, 965, 966, 967, 968, 969, 971, 972, 973],
    [966, 967, 968, 969, 970, 971, 972],
    [963, 967, 969, 970, 971, 972, 973],
    [962, 965, 967, 968, 969, 970, 971, 973],
    [965, 968, 970, 971, 972, 973],
    [963, 966, 968],
    [963, 965, 966],
]
ROLES = [
    [0, 0, 2, 1, 3, 3, 4, 5, 0, 0, 1, 2, 7, 6],
    [0, 2, 7, 8, 4, 5, 3, 6, 1, 1, 5, 4, 6, 3],
    [0, 5, 2, 7, 3, 6, 13, 10, 9, 9, 12, 11, 4, 8],
    [0, 5, 11, 3, 12, 10, 2, 7, 13, 13, 4, 8, 9, 6],
    [0, 5, 2, 9, 3, 7, 6, 10, 4, 4, 12, 11, 8, 13],
    [0, 7, 3, 13, 4, 9, 2, 12, 10, 10, 5, 6, 8, 11],
    [0, 12, 3, 10, 2, 5, 4, 8, 7, 7, 13, 9, 6, 11],
    [0, 9, 6, 5, 2, 8, 7, 12, 11, 11, 10, 4, 3, 13],
    [0, 10, 2, 12, 3, 13, 4, 11, 7, 7, 5, 8, 6, 9],
    [0, 12, 3, 13, 4, 11, 2, 8, 5, 5, 6, 9, 7, 10],
    [0, 8, 2, 11, 3, 12, 5, 9, 7, 7, 13, 10, 4, 6],
    [0, 11, 3, 7, 4, 5, 9, 8, 12, 12, 13, 6, 2, 10],
    [0, 10, 2, 13, 3, 11, 7, 12, 5, 5, 6, 4, 9, 8],
    [0, 13, 3, 12, 5, 11, 2, 8, 4, 4, 10, 7, 6, 9],
    [0, 5, 2, 10, 3, 8, 6, 4, 11, 11, 7, 9, 0, 5],
    [0, 7, 6, 6, 4, 3, 2, 2, 8, 8, 0, 7, 1, 5],
    [4, 4, 3, 5, 11, 11, 8, 9, 0, 2, 1, 7, 6, 10],
    [2, 3, 11, 8, 9, 10, 7, 5, 1, 4, 12, 13, 14, 6],
    [10, 6, 5, 8, 7, 11, 3, 4, 6, 10, 8, 5, 2, 9],
    [5, 9, 10, 3, 4, 6, 2, 8, 11, 7, 6, 4, 8, 2],
    [5, 13, 6, 8, 2, 14, 10, 12, 3, 11, 4, 7, 15, 9],
    [3, 6, 2, 11, 10, 14, 4, 13, 5, 7, 15, 8, 9, 12],
    [6, 15, 2, 8, 7, 10, 3, 12, 13, 14, 11, 4, 9, 5],
    [4, 8, 3, 15, 6, 13, 2, 5, 12, 14, 11, 9, 7, 10],
    [3, 7, 8, 9, 2, 10, 5, 6, 4, 13, 11, 15, 12, 14],
    [10, 11, 3, 14, 4, 7, 2, 8, 5, 9, 15, 12, 6, 13],
    [6, 7, 5, 10, 4, 9, 3, 15, 14, 12, 11, 13, 2, 8],
    [7, 13, 10, 11, 4, 15, 3, 12, 6, 9, 2, 14, 5, 8],
    [4, 10, 14, 11, 2, 9, 13, 12, 5, 3, 8, 6, 7, 15],
    [15, 13, 8, 5, 14, 12, 2, 7, 3, 4, 9, 11, 6, 10],
    [12, 9, 6, 10, 8, 11, 3, 2, 5, 14, 7, 13, 0, 4],
    [6, 9, 10, 10, 3, 2, 11, 11, 7, 8, 0, 5, 1, 4],
    [9, 9, 4, 3, 2, 2, 7, 8, 0, 5, 1, 10, 6, 11],
    [6, 2, 7, 11, 8, 9, 3, 13, 1, 4, 5, 14, 12, 10],
    [5, 12, 6, 13, 3, 7, 10, 9, 4, 11, 14, 15, 2, 8],
    [5, 14, 10, 15, 7, 6, 11, 12, 3, 13, 9, 8, 2, 4],
    [5, 3, 2, 11, 7, 4, 10, 9, 3, 5, 11, 2, 8, 6],
    [2, 10, 4, 8, 11, 9, 5, 7, 3, 6, 9, 11, 7, 5],
    [3, 12, 8, 6, 2, 7, 10, 5, 11, 4, 15, 9, 13, 14],
    [8, 6, 9, 4, 10, 5, 14, 13, 12, 3, 7, 11, 2, 15],
    [7, 11, 3, 15, 2, 5, 6, 14, 10, 13, 8, 9, 4, 12],
    [3, 15, 2, 14, 4, 12, 11, 8, 6, 9, 5, 7, 10, 13],
    [3, 5, 8, 14, 2, 11, 4, 6, 12, 13, 15, 10, 9, 7],
    [8, 15, 6, 7, 3, 5, 11, 13, 12, 14, 2, 4, 10, 9],
    [6, 15, 11, 7, 2, 10, 14, 5, 3, 12, 4, 13, 8, 9],
    [10, 7, 3, 8, 13, 6, 4, 9, 2, 11, 5, 12, 14, 15],
    [3, 7, 12, 8, 2, 9, 4, 11, 10, 13, 6, 14, 0, 5],
    [7, 4, 10, 10, 3, 8, 11, 11, 2, 6, 0, 9, 1, 5],
    [11, 11, 5, 6, 9, 9, 3, 10, 0, 2, 1, 8, 4, 7],
    [8, 10, 5, 9, 6, 11, 7, 2, 1, 12, 14, 4, 3, 13],
    [5, 9, 3, 14, 7, 12, 13, 11, 15, 6, 4, 8, 2, 10],
    [3, 14, 6, 5, 11, 8, 15, 12, 4, 9, 2, 13, 7, 10],
    [4, 12, 10, 13, 3, 14, 8, 9, 2, 5, 6, 11, 7, 15],
    [8, 12, 11, 4, 9, 10, 3, 5, 15, 2, 6, 13, 7, 14],
    [7, 10, 8, 9, 4, 5, 11, 2, 10, 7, 9, 8, 3, 6],
    [7, 8, 9, 3, 10, 2, 6, 11, 4, 5, 2, 10, 11, 6],
    [4, 11, 3, 14, 6, 8, 7, 5, 2, 9, 12, 10, 13, 15],
    [2, 12, 4, 9, 6, 3, 7, 8, 10, 11, 15, 14, 5, 13],
    [4, 8, 2, 9, 10, 7, 14, 11, 3, 15, 5, 6, 13, 12],
    [7, 9, 10, 3, 14, 12, 11, 4, 6, 8, 2, 5, 13, 15],
    [9, 11, 7, 8, 10, 5, 4, 12, 2, 14, 6, 15, 3, 13],
    [8, 9, 7, 6, 5, 10, 3, 13, 2, 11, 12, 15, 4, 14],
    [4, 12, 7, 9, 14, 6, 2, 5, 8, 3, 10, 13, 0, 11],
    [6, 8, 11, 11, 2, 7, 4, 4, 5, 9, 0, 3, 1, 10],
    [10, 10, 6, 8, 7, 7, 2, 9, 0, 5, 1, 3, 4, 11],
    [7, 8, 2, 11, 3, 10, 4, 14, 1, 13, 5, 12, 6, 9],
    [4, 12, 14, 9, 5, 15, 3, 8, 7, 11, 6, 13, 2, 10],
    [15, 10, 3, 6, 2, 9, 7, 13, 4, 14, 11, 12, 8, 5],
    [9, 12, 5, 3, 10, 15, 7, 6, 2, 11, 14, 8, 13, 4],
    [9, 5, 4, 15, 14, 10, 11, 13, 2, 3, 12, 7, 6, 8],
    [4, 13, 2, 12, 6, 7, 3, 10, 9, 15, 5, 14, 11, 8],
    [4, 13, 11, 7, 2, 8, 5, 6, 12, 14, 9, 15, 3, 10],
    [2, 9, 6, 11, 7, 10, 5, 8, 9, 2, 11, 6, 3, 4],
    [5, 10, 3, 2, 4, 7, 11, 9, 8, 6, 7, 4, 9, 11],
    [7, 3, 4, 14, 8, 13, 2, 10, 6, 15, 9, 11, 5, 12],
    [8, 13, 4, 14, 6, 11, 15, 5, 7, 9, 10, 3, 2, 12],
    [15, 6, 7, 10, 12, 13, 9, 8, 2, 4, 3, 5, 14, 11],
    [6, 12, 11, 9, 10, 8, 13, 15, 2, 14, 4, 5, 3, 7],
    [7, 2, 13, 5, 9, 10, 8, 6, 4, 12, 3, 11, 0, 14],
    [11, 3, 2, 2, 5, 4, 10, 10, 9, 6, 0, 7, 1, 8],
    [8, 8, 11, 7, 10, 10, 4, 9, 0, 5, 1, 6, 2, 3],
    [12, 9, 2, 4, 6, 10, 3, 5, 1, 7, 13, 14, 11, 8],
    [4, 6, 8, 10, 5, 7, 9, 14, 3, 11, 13, 12, 2, 15],
    [8, 10, 2, 13, 9, 12, 4, 14, 11, 7, 3, 6, 5, 15],
    [12, 15, 9, 4, 13, 7, 5, 6, 2, 14, 3, 11, 8, 10],
    [11, 4, 2, 9, 7, 6, 3, 13, 5, 14, 12, 15, 8, 10],
    [13, 9, 4, 10, 3, 12, 2, 8, 5, 11, 15, 6, 14, 7],
    [4, 8, 13, 15, 2, 7, 3, 11, 5, 12, 9, 6, 10, 14],
    [4, 13, 10, 8, 7, 5, 2, 9, 6, 14, 12, 11, 15, 3],
    [10, 9, 13, 7, 2, 12, 4, 3, 8, 14, 11, 6, 5, 15],
    [10, 7, 9, 8, 6, 5, 11, 3, 7, 10, 8, 9, 4, 2],
    [9, 8, 3, 4, 11, 2, 5, 10, 6, 7, 2, 11, 10, 5],
    [13, 12, 8, 2, 7, 10, 4, 9, 5, 6, 3, 15, 11, 14],
    [10, 6, 2, 9, 8, 11, 4, 5, 3, 15, 14, 12, 7, 13],
    [12, 8, 6, 14, 4, 11, 9, 3, 5, 10, 7, 13, 0, 2],
    [6, 11, 2, 2, 7, 3, 4, 4, 8, 9, 0, 10, 1, 5],
    [10, 10, 3, 2, 11, 11, 8, 9, 0, 4, 1, 5, 6, 7],
    [3, 2, 6, 9, 12, 13, 7, 10, 1, 14, 8, 11, 5, 4],
    [2, 6, 4, 14, 5, 8, 7, 9, 13, 15, 11, 10, 3, 12],
    [4, 11, 2, 15, 7, 8, 5, 14, 9, 13, 3, 10, 6, 12],
    [3, 8, 5, 7, 9, 15, 6, 14, 2, 10, 4, 13, 11, 12],
    [2, 7, 3, 11, 4, 15, 5, 13, 8, 6, 9, 10, 12, 14],
    [2, 8, 3, 10, 4, 11, 5, 14, 7, 15, 9, 13, 6, 12],
    [3, 6, 2, 7, 4, 14, 10, 15, 13, 9, 8, 11, 5, 12],
    [2, 10, 5, 12, 3, 11, 4, 13, 9, 14, 6, 7, 15, 8],
    [3, 10, 8, 13, 2, 11, 4, 7, 6, 15, 9, 5, 14, 12],
    [6, 14, 12, 10, 4, 9, 5, 15, 8, 11, 13, 7, 3, 2],
    [11, 9, 2, 8, 7, 14, 5, 12, 15, 10, 3, 13, 4, 6],
    [3, 7, 5, 11, 4, 2, 6, 9, 7, 3, 11, 5, 8, 10],
    [5, 10, 8, 7, 4, 9, 11, 6, 2, 3, 9, 4, 6, 11],
    [10, 7, 8, 9, 5, 13, 2, 4, 12, 6, 14, 11, 0, 3],
    [6, 7, 11, 11, 2, 3, 4, 4, 9, 5, 0, 8, 1, 10],
    [5, 5, 6, 2, 3, 3, 1, 4, 0, 7, 1, 4, 8, 8],
    [6, 4, 2, 7, 3, 5, 1, 10, 1, 10, 8, 11, 9, 9],
    [3, 11, 7, 12, 4, 6, 1, 9, 8, 13, 10, 5, 2, 2],
    [7, 11, 2, 12, 3, 8, 1, 13, 10, 9, 5, 4, 6, 6],
    [3, 6, 8, 9, 4, 7, 1, 11, 2, 5, 13, 12, 10, 10],
    [7, 9, 2, 12, 3, 11, 1, 13, 4, 5, 6, 8, 10, 10],
    [2, 11, 4, 13, 3, 10, 1, 7, 12, 5, 9, 6, 8, 8],
    [6, 13, 3, 12, 2, 7, 1, 9, 8, 10, 4, 11, 5, 5],
    [2, 9, 5, 6, 3, 10, 1, 12, 7, 13, 4, 8, 11, 11],
    [5, 7, 3, 12, 2, 10, 1, 4, 8, 6, 13, 9, 11, 11],
    [2, 10, 3, 13, 5, 12, 1, 6, 7, 9, 8, 4, 11, 11],
    [7, 13, 2, 12, 3, 8, 1, 6, 10, 11, 4, 5, 9, 9],
    [3, 11, 8, 12, 2, 7, 1, 5, 9, 4, 10, 6, 13, 13],
    [9, 13, 2, 4, 3, 7, 1, 6, 5, 8, 10, 11, 12, 12],
    [3, 6, 4, 5, 8, 7, 1, 2, 6, 3, 5, 4, 0, 0],
    [4, 5, 2, 2, 3, 0, 1, 1, 6, 7, 0, 3, 1, 1],
]


def fill_table(table, me, low, high):
    if high - low == 1:
        sends, leaves = SENDS[low], LEAVES[low]
        for place, word in enumerate([len(sends), len(leaves)] + sends + leaves):
            table[place] = jnp.int32(word)
        return
    middle = (low + high) // 2
    lax.cond(
        me < middle,
        lambda: fill_table(table, me, low, middle),
        lambda: fill_table(table, me, middle, high),
    )


def neighbours(col, row):
    x = lax.rem(col, 2) * 2 + lax.rem(row // 2, 2)
    y, z, core = col // 2, row // 4, lax.rem(row, 2)
    found = [(x, y, z, 1 - core)]
    for move in (1, 3):
        for other in range(2):
            found.append((lax.rem(x + move, 4), y, z, other))
            found.append((x, lax.rem(y + move, 4), z, other))
            found.append((x, y, lax.rem(z + move, 4), other))
    return [{"col": y * 2 + x // 2, "row": z * 4 + lax.rem(x, 2) * 2 + core} for x, y, z, core in found]


def spread_kernel(stored_ref, slots_ref, table, own_sem, send_sem, recv_sem):
    rows_per = stored_ref.shape[2] // CHUNKS
    col, row = lax.axis_index("col"), lax.axis_index("row")
    beside = neighbours(col, row)
    sibling = beside[0]

    barrier = pltpu.get_barrier_semaphore()
    for device in beside:
        pl.semaphore_signal(barrier, inc=1, device_id=device, device_id_type=MESH)
    own = [
        pltpu.make_async_copy(stored_ref.at[lane, 0], slots_ref.at[lane], own_sem.at[lane])
        for lane in range(2)
    ]
    for copy in own:
        copy.start()
    fill_table(table, col * lax.axis_size("row") + row, 0, len(SENDS))
    pl.semaphore_wait(barrier, len(beside))

    def hop(source, slot, chunk, place, device):
        return pltpu.make_async_remote_copy(
            src_ref=source,
            dst_ref=slots_ref.at[slot, pl.ds(chunk * rows_per, rows_per)],
            send_sem=send_sem.at[place],
            recv_sem=recv_sem.at[slot, chunk],
            device_id=device,
            device_id_type=MESH,
        )

    def arrival(slot, chunk):
        piece = slots_ref.at[slot, pl.ds(chunk * rows_per, rows_per)]
        hop(piece, slot, chunk, 0, sibling).wait_recv()

    sends = table[0]

    @pl.loop(0, sends)
    def _(place):
        word = table[2 + place]
        slot = word & 63
        chunk = (word >> 6) & 7
        device = {"col": (word >> 10) & 7, "row": (word >> 13) & 15}
        landing = word >> 17

        @pl.when(((word >> 9) & 1) == 1)
        def _():
            arrival(slot, chunk)

        @pl.when(slot < 2)
        def _():
            piece = stored_ref.at[slot, 0, pl.ds(chunk * rows_per, rows_per)]
            hop(piece, landing, chunk, place, device).start()

        @pl.when(slot >= 2)
        def _():
            piece = slots_ref.at[slot, pl.ds(chunk * rows_per, rows_per)]
            hop(piece, landing, chunk, place, device).start()

    @pl.loop(0, table[1])
    def _(place):
        word = table[2 + sends + place]
        for chunk in range(CHUNKS):
            @pl.when(((word >> (6 + chunk)) & 1) == 1)
            def _():
                arrival(word & 63, chunk)

    @pl.loop(0, sends)
    def _(place):
        hop(slots_ref.at[0, pl.ds(0, rows_per)], 0, 0, place, sibling).wait_send()

    for copy in own:
        copy.wait()


def spread(stored):
    most = max(len(sends) for sends in SENDS)
    return pl.pallas_call(
        spread_kernel,
        out_shape=jax.ShapeDtypeStruct((SLOTS,) + stored.shape[2:], jnp.float32),
        in_specs=[pl.BlockSpec(memory_space=pl.ANY)],
        out_specs=pl.BlockSpec(memory_space=pl.ANY),
        scratch_shapes=[
            pltpu.SMEM((2 + most + SLOTS,), jnp.int32),
            pltpu.SemaphoreType.DMA((2,)),
            pltpu.SemaphoreType.DMA((most,)),
            pltpu.SemaphoreType.DMA((SLOTS, CHUNKS)),
        ],
        compiler_params=pltpu.CompilerParams(collective_id=0, has_side_effects=True),
        name="spread",
    )(stored)


def split(value):
    high = value.astype(jnp.bfloat16)
    return high, (value - high.astype(jnp.float32)).astype(jnp.bfloat16)


def multiply_kernel(
    slots_ref, roles_ref, rows_ref, offs_ref, krow_ref, kcol_ref, kcnt_ref, out_ref,
    raw, left, right, done, pairs, pair_count, bucket, bucket_count, facts, in_sem, out_sem,
):
    grid = lax.axis_size("row")
    tile_j = lax.axis_index("row")
    col_id = lax.axis_index("col")
    me = col_id * grid + tile_j
    tiles, active, half = raw.shape[:3]
    block = raw.shape[-1]
    lanes, _, kept = krow_ref.shape
    slots = 2 * half
    steps = 2
    most = steps * slots * slots

    def load(place):
        return pltpu.make_async_copy(
            slots_ref.at[roles_ref[me, place]], raw.at[place], in_sem.at[place]
        )

    for place in range(tiles):
        load(place).start()

    first = rows_ref[0, 0]
    bits = [rows_ref[0, 1] ^ first, rows_ref[0, 2] ^ first, rows_ref[0, 4] ^ first]

    def rank(value):
        return sum(
            jnp.where((value & bit) != 0, jnp.int32(1 << place), jnp.int32(0))
            for place, bit in enumerate(bits)
        )

    def shifts(tile_x, tile_y):
        both = ((tile_x, tile_y), (tile_y, tile_x))
        return [rank(offs_ref[x, y, slot]) for x, y in both for slot in range(half)]

    tile_is = [col_id * lanes + lane for lane in range(lanes)]
    tile_ks = [lax.rem(tile_is[0] + tile_j + place, grid) for place in range(3)]
    right_moves = [shifts(tile_k, tile_j) for tile_k in tile_ks]

    for place in range(lanes * active):
        pair_count[place] = 0
    for lane in range(lanes):
        for step in range(steps):
            left_moves = shifts(tile_is[lane], tile_ks[lane + step])
            for slot in range(slots):
                move = left_moves[slot]
                turn = move if slot >= half else 0
                left_base = (2 * lane + step) * active * slots + slot
                for other in range(slots):
                    apart = move ^ right_moves[lane + step][other]
                    place = lane * active + apart
                    count = pair_count[place]
                    right_base = (lane + step) * active * slots + other
                    reach = move if other < half else apart
                    pairs[place * most + count] = (
                        turn | reach << 3 | left_base << 6 | right_base << 14
                    )
                    pair_count[place] = count + 1

    widest = 4
    room = 2 * lanes * kept
    for place in range(widest + 1):
        bucket_count[place] = 0
    for place in range(lanes * active):
        pair_count[place] = place << 3 | pair_count[place] << 7

    def put(size, word):
        filled = bucket_count[size]
        bucket[size * room + filled] = word
        bucket_count[size] = filled + 1

    for lane in range(lanes):
        count = kcnt_ref[lane, 0]
        together = 8

        @pl.loop(0, kept // together)
        def _(part):
            found = []
            for offset in range(together):
                item = part * together + offset
                row = rank(krow_ref[lane, 0, item])
                place = lane * active + (row ^ rank(kcol_ref[lane, 0, item]))
                found.append(jnp.where(item < count, pair_count[place] | row, 0))
            for offset in range(together):
                item = lane * kept + part * together + offset
                products = found[offset] >> 7
                facts[item] = found[offset] & 127
                begin = jnp.where(products > 0, ((products - 1) & 7) + 1, 0)
                put((begin + 1) >> 1, item | begin << 13)

                @pl.loop(0, (products - begin) >> 3)
                def _(more):
                    put(widest, item | (begin + 8 * more) << 7 | 1 << 12 | 8 << 13)

    left[4 * active * slots] = jnp.zeros((2 * block, block), jnp.bfloat16)

    for place in range(3):
        load(8 + 2 * place).wait()
        load(9 + 2 * place).wait()

        @pl.loop(0, active)
        def _(row):
            for slot in range(slots):
                value = raw[8 + 2 * place + slot // half, row, slot % half]
                high, low = split(value.T if slot >= half else value)
                into = (place * active + row) * slots + slot
                right[into, :, :block] = high
                right[into, :, block:] = low

    for place in range(4):
        load(2 * place).wait()
        load(2 * place + 1).wait()

        @pl.loop(0, active)
        def _(row):
            for slot in range(slots):
                value = raw[2 * place + slot // half, row, slot % half]
                high, low = split(value.T if slot >= half else value)
                into = (place * active + row) * slots + slot
                left[into, :block] = high
                left[into, block:] = low

    def gather(word, size):
        fact = facts[word & 127]
        row = fact & 7
        base = (fact >> 3) * most + ((word >> 7) & 31)
        products = word >> 13
        lefts, rights = [], []
        for place in range(2 * size):
            inside = place < products
            code = pairs[base + jnp.where(inside, place, 0)]
            source = ((code >> 6) & 255) + (row ^ (code & 7)) * slots
            lefts.append(left[jnp.where(inside, source, 4 * active * slots)])
            rights.append(right[(code >> 14) + (row ^ ((code >> 3) & 7)) * slots])
        total = jnp.dot(
            jnp.concatenate(lefts, 1), jnp.concatenate(rights, 0), preferred_element_type=jnp.float32
        )
        total = total[:block] + total[block:]
        return total[:, :block] + total[:, block:]

    def add(word, into, total):
        again = ((word >> 12) & 1) == 1

        @pl.when(again)
        def _():
            done[into] = done[into] + total

        @pl.when(jnp.logical_not(again))
        def _():
            done[into] = total

    @pl.loop(0, bucket_count[0])
    def _(place):
        done[bucket[place] & 127] = jnp.zeros((block, block), jnp.float32)

    for size in range(1, widest + 1):
        count = bucket_count[size]

        @pl.loop(0, (count + 1) >> 1)
        def _(place):
            start = size * room + 2 * place
            one = bucket[start]
            paired = 2 * place + 1 < count
            two = bucket[jnp.where(paired, start + 1, start)]
            total_one = gather(one, size)
            total_two = gather(two, size)
            if size < widest:
                done[one & 127] = total_one
                done[jnp.where(paired, two & 127, lanes * kept)] = total_two
            else:
                add(one, one & 127, total_one)
                add(jnp.where(paired, two, 0), jnp.where(paired, two & 127, lanes * kept), total_two)

    def store(lane):
        return pltpu.make_async_copy(
            done.at[pl.ds(lane * kept, kept)], out_ref.at[lane, 0], out_sem.at[lane]
        )

    for lane in range(lanes):
        store(lane).start()
    for lane in range(lanes):
        store(lane).wait()


def multiply(slots, roles, tile_rows, offsets, kept_rows, kept_cols, kept_count):
    block = slots.shape[-1]
    active, half = slots.shape[1:3]
    lanes, _, kept = kept_rows.shape
    tiles = roles.shape[-1]
    items = lanes * kept
    products = 2 * (2 * half) ** 2
    smem = pl.BlockSpec(memory_space=pltpu.SMEM)
    return pl.pallas_call(
        multiply_kernel,
        out_shape=jax.ShapeDtypeStruct((lanes, 1, kept, block, block), jnp.float32),
        in_specs=[pl.BlockSpec(memory_space=pl.ANY)] + [smem] * 6,
        out_specs=pl.BlockSpec(memory_space=pl.ANY),
        scratch_shapes=[
            pltpu.VMEM((tiles, active, half, block, block), jnp.float32),
            pltpu.VMEM((4 * active * 2 * half + 1, 2 * block, block), jnp.bfloat16),
            pltpu.VMEM((3 * active * 2 * half, block, 2 * block), jnp.bfloat16),
            pltpu.VMEM((items + 1, block, block), jnp.float32),
            pltpu.SMEM((lanes * active * products,), jnp.int32),
            pltpu.SMEM((lanes * active,), jnp.int32),
            pltpu.SMEM((10 * items,), jnp.int32),
            pltpu.SMEM((5,), jnp.int32),
            pltpu.SMEM((items,), jnp.int32),
            pltpu.SemaphoreType.DMA((tiles,)),
            pltpu.SemaphoreType.DMA((lanes,)),
        ],
        compiler_params=pltpu.CompilerParams(vmem_limit_bytes=56 << 20),
        name="multiply",
    )(slots, roles, tile_rows, offsets, kept_rows, kept_cols, kept_count)


def local(stored, tile_rows, offsets, kept_rows, kept_cols, kept_count):
    slots = spread(stored)
    roles = jnp.asarray(np.array(ROLES, np.int32))
    return multiply(slots, roles, tile_rows, offsets, kept_rows, kept_cols, kept_count)


def solution(mesh):
    in_specs = (
        P("col", "row", None, None, None, None),
        P(),
        P(),
        P("col", "row", None),
        P("col", "row", None),
        P("col", "row"),
    )
    out_specs = P("col", "row", None, None, None)
    return jax.shard_map(local, mesh=mesh, in_specs=in_specs, out_specs=out_specs, check_vma=False)
```

time: 771 us -> 133 us (0.17); the launches traced: 758 us -> 130 us
  waiting for transfers between devices: 337 us -> 0 us
  matrix products: 146 us -> 0 us
  local copies, waits for them, and re-layouts: 140 us -> 4.13 us
  Pallas kernels: 0 us -> 126 us
  blocking collectives: 63.6 us -> 0 us
  other arithmetic: 36.6 us -> 0 us
  starting transfers between devices: 28.2 us -> 0 us
    ppermute x5 -> x0, waiting for transfers between devices: 273 us -> none  [from_behind(): return lax.ppermute(value, axis, pairs)]
    dot_general x32 -> x0, matrix products: 146 us -> none  [the longest x16 102 us: lane_terms(): jnp.einsum('eij,ebjk->ebik', vals_a[:, slot], picked, precision=lax.Preci...]
    pallas_call x0 -> x2, Pallas kernels: none -> 126 us  [the longest x1 99 us: spread(): pl.pallas_call(spread_kernel, out_shape=jax.ShapeDtypeStruct((SLOTS,) + s...]
    gather x42 -> x0, local copies, waits for them, and re-layouts: 65.4 us -> none  [the longest x16 38.6 us: lane_terms(): picked = vals_b[position[:, slot]]]
    all_to_all x3 -> x0, waiting for transfers between devices: 64.1 us -> none  [the longest x1 43.9 us: local(): lax.all_to_all(spread, 'row', split_axis=1, concat_axis=1, tiled=True)]
    all_to_all x2 -> x0, blocking collectives: 63.6 us -> none  [the longest x1 33.1 us: local(): lax.all_to_all(routed, 'col', split_axis=1, concat_axis=0, tiled=True)]
    transpose x16 -> x0, local copies, waits for them, and re-layouts: 47.8 us -> none  [lane_terms(): jnp.einsum('eij,ebjk->ebik', vals_a[:, slot], picked, precision=lax.Preci...]
    all_to_all x3 -> x0, starting transfers between devices: 17.2 us -> none  [the longest x1 6.22 us: local(): lax.all_to_all(routed, 'col', split_axis=0, concat_axis=2, tiled=True)]
  transfers between devices with their start and end apart: 8 -> 0, of which waited for: 6 -> 0; matrix products, arithmetic and copies ran while one was open for 13% -> 0% of each run, Pallas kernels for 0% -> 0%
where the time goes in v3:
time: 133 us; the launch traced here: 130 us
  Pallas kernels  126 us (95%)
  local copies, waits for them, and re-layouts  4.13 us (3%)
    pallas_call x1, Pallas kernels, spread(): pl.pallas_call(spread_kernel, out_shape=jax.ShapeDtypeStruct((SLOTS,) + s...  99 us
    pallas_call x1, Pallas kernels, multiply(): pl.pallas_call(multiply_kernel, out_shape=jax.ShapeDtypeStruct((lanes, 1,...  26.9 us
    unnamed x3, local copies, waits for them, and re-layouts  4.13 us

profile of v3, /device:TPU:42, one launch (start us, length us, event | category | flops | bytes accessed | tf_op | source)
XLA Modules:
  0.0 130.0 jit_solution(7608576418290147695)
XLA Ops:
  0.0 1.3 copy.10.kcnt_ref
  1.3 1.3 %copy.8.rows_ref = s32[16,8]{1,0:T(8,128)} copy(s32[16,8]{0,1:T(8,128)} %param.8) | data formatting | bytes 1024 | tf_op args[1]
  2.6 1.5 %copy.9.offs_ref = s32[16,16,2]{2,1,0:T(8,128)} copy(s32[16,16,2]{1,2,0:T(2,128)} %param.9) | data formatting | bytes 4096 | tf_op args[2]
  4.1 99.0 %spread.1.slots_ref = f32[32,8,2,128,128]{4,3,2,1,0:T(8,128)} custom-call(f32[2,1,8,2,128,128]{5,4,3,2,1,0:T(8,128)} %stored_ref.1), custom_call_target="tpu_custom_call" | custom-call | tf_op jit(solution)/shard_map/spread/pallas_call | solution.py:504
  103.2 26.9 %multiply.1 = f32[2,1,32,128,128]{4,3,2,1,0:T(8,128)} custom-call(f32[32,8,2,128,128]{4,3,2,1,0:T(8,128)} %spread.1.slots_ref, s32[128,14]{1,0:T(8,128)} %constant.2.clone.roles_ref, s32[16,8]{1,0:T(8,128)} %copy.8.rows_ref, s32[16,16,2]{2,1,0:T(8,128)} %copy.9.offs_ref, s32[2,1,32]{2,1,0:T(1,128)} %krow_ref.1, s32[2,1,32]{2,1,0:T(1,128)} %kcol_ref.1, ...), custom_call_target="tpu_custom_call" | custom-call | tf_op jit(solution)/shard_map/multiply/pallas_call | solution.py:718

commit v4 on v0

v4 whole, which is shorter than its diff:
```python
import jax
import jax.numpy as jnp
from jax import lax
from jax.experimental import pallas as pl
from jax.experimental.pallas import tpu as pltpu
from jax.sharding import PartitionSpec as P

MESH = pl.DeviceIdType.MESH
CHUNKS = 4
SLOTS = 33
STEPS = [
    [118, 104, 12, 1851457, 9576512, 17965248, 26353664, 34742400, 42213441, 50601985, 58990785, 69222914, 75767937, 84286154, 93094408, 102113993, 1073746818, 1074811906, 111558857, 1075088323, 1074326531, 119675596, 128090827, 135668233, 1076690944, 1073824768, 145113097, 1074105345, 153631301, 160203400, 168435781, 177611401, 187056265, 1074651136, 1075979264, 1076258817, 195172940, 202146504, 211165769, 220610633, 227287558, 237142667, 245766734, 252322437, 261890575, 270287041, 277619334, 287848581, 295862859, 302654149, 312222351, 320618497, 327950918, 338180293, 346194443, 352985605, 362553935, 370950273, 1076540421, 378282694, 388511749, 395084360, 404497103, 413155394, 1077337094, 421665420, 430736016, 438321346, 446831116, 455901776, 463487106, 470161930, 481067536, 489439247, 495327818, 506233552, 514605135, 520493706, 529826449, 539771023, 547756686, 554869332, 564936911, 1075780548, 572922382, 581861971, 590364808, 597178898, 607027923, 615530568, 623254222, 632193555, 638861515, 647510674, 655655505, 664027275, 672676562, 680698516, 691028168, 697842258, 707691155, 714358859, 723270229, 731152913, 741359624, 748436181, 756195860, 764690443, 1075540935, 773601941, 781484753, 792224397, 798767637, 806527700, 817390157, 825244182, 834167309, 842021462, 850944717, 858798806, 867187350],
    [106, 92, 13, 1933440, 10249408, 17039553, 25427969, 33816641, 42205313, 50724992, 59113536, 67502080, 77620809, 85819456, 92668096, 102786697, 109806218, 117713611, 1073743810, 126353924, 1074020352, 136078336, 143360522, 151267851, 161507017, 168526538, 1073782785, 1075897345, 176433803, 186672649, 193692234, 203958924, 211575936, 220701261, 229124684, 236741696, 245998159, 254421518, 262824964, 271164047, 279587470, 285737668, 296379588, 304587405, 1076169669, 313141838, 1074354118, 1075161094, 321939150, 329884367, 338176716, 347104398, 354918925, 363473102, 372270158, 380215823, 388508172, 394789444, 405431364, 413639373, 420358800, 428343940, 438141120, 447374468, 1076482052, 1074932740, 454044306, 463306752, 472933390, 478423627, 489652233, 496125524, 504244816, 514818249, 521291476, 529410768, 539983945, 546457236, 554961489, 562954887, 573538441, 580273749, 588261906, 596509383, 605439701, 614179411, 621685264, 630063687, 638993941, 647733779, 655755798, 663618055, 672548501, 681288339, 1076775943, 689179281, 697452052, 706454227, 1074700232, 1075769352, 714091218, 722864790, 1077091267, 1075540995, 731253462, 739256914, 747899601, 756419158, 764676625],
    [142, 128, 11, 2368512, 8673408, 18636801, 27025537, 35414081, 43802817, 52322304, 60710976, 69099712, 77866048, 86399682, 94265472, 103047758, 111567428, 1073744322, 119953474, 127927364, 1074287555, 136864272, 1074823168, 142893777, 153507970, 161613009, 170181138, 176579206, 185098963, 193225233, 203839490, 211944465, 220512978, 226910726, 235430419, 243557009, 254564943, 262276241, 270844498, 277373587, 285499985, 296507919, 304219217, 312787602, 319316563, 329671172, 338451087, 346031108, 354706126, 363225796, 372005583, 379585732, 388260366, 396780164, 405952590, 414057491, 1073803268, 419848902, 430891732, 438592142, 445538951, 456284302, 463471748, 470180422, 481223188, 489185872, 495870535, 506615822, 514720851, 1076956166, 523166356, 531129040, 540170446, 548275411, 556720724, 564683408, 574118032, 581829779, 590397974, 596664342, 606348480, 616060944, 623952470, 630218838, 639902848, 649615440, 657506966, 663773334, 674781392, 680928327, 1074612165, 691061462, 697327830, 706094215, 714635398, 722526741, 731275928, 739661957, 747766936, 756081237, 764830296, 773216325, 781321304, 789635797, 798646986, 806249159, 815298630, 823665866, 831709783, 840589962, 848192007, 857089031, 865630214, 1074108423, 873652951, 882270936, 889477184, 898761944, 907207191, 916087370, 924211397, 932717642, 940761751, 949379608, 956586176, 965870616, 974185109, 983196170, 990140416, 999826442, 1075436554, 1075717067, 1075995659, 1076279240, 1008394777, 1016472775, 1024874501, 1033560793, 1041791174, 1050158218, 1077336012, 1058726489, 1075260365, 1067115161, 1076588489],
    [102, 88, 9, 1687681, 8790209, 17055936, 25444352, 33833024, 42221696, 50741249, 59129921, 67518593, 76030478, 85573697, 92684481, 103303760, 109707855, 119128257, 126501457, 136858128, 1073741824, 144293889, 152830547, 162024080, 168428175, 176677458, 187189968, 193594063, 201974292, 213019349, 218759695, 228975109, 238184981, 243802830, 254140997, 1073771458, 263350869, 270918341, 278659603, 1076927428, 288516757, 296084101, 303825619, 1075375109, 310895314, 320602771, 327672466, 336077390, 344605393, 353258072, 361243278, 369877590, 1076692931, 378159761, 386812632, 1074094022, 396894210, 403431958, 411978392, 422060098, 430818009, 436879889, 448285338, 455614658, 464372313, 473451098, 480780418, 487318166, 498617050, 503833106, 512630929, 523782682, 529408209, 539869849, 1075678152, 546195992, 554573905, 565035545, 571351057, 579592918, 587604033, 597017303, 604627604, 612769793, 1074385863, 1074932682, 622750299, 629547137, 638960151, 1076525001, 647916059, 654959188, 664693403, 672514647, 1077317579, 681470683, 688513748, 1074714573, 698239644, 706069143, 715016796, 723405532, 731793948, 1075258316, 1076061196],
    [110, 96, 3, 2275456, 10289153, 18931777, 27041984, 35430464, 43819008, 52207744, 60995584, 69263489, 77668930, 1073746754, 86161600, 94445570, 100983503, 1074809795, 109486725, 1074298880, 119715904, 128131205, 134537743, 143041093, 151435458, 161685573, 168092239, 176595461, 186851333, 193258127, 202021585, 210150085, 219191425, 228794565, 235586195, 1073797125, 245440706, 252363475, 260881108, 270606466, 277529171, 286046804, 294306323, 302684753, 313459221, 1075389380, 1075930116, 320117254, 330236501, 338346514, 1076211655, 344373314, 355402453, 363512402, 1076742022, 369664662, 379388033, 386710164, 397066962, 403219030, 412391494, 422511253, 430621330, 436773398, 446496833, 454334598, 464708302, 1074149321, 470328022, 479238145, 488440001, 498262542, 504406666, 513859777, 521583243, 1077310408, 530636801, 537311234, 546644567, 554343057, 565371470, 571810519, 580303563, 590537358, 1077056715, 596976151, 607437456, 613718214, 621847114, 630792792, 640991952, 647411723, 655399105, 666157584, 672473751, 682934864, 688560657, 697901720, 705733130, 714520651, 723173398, 731456024, 739031572, 748339350, 756622040, 764453578, 772192386, 781893718, 1075239946, 789616705, 798671062, 1075784653, 1076580300],
    [114, 100, 13, 1869888, 9568449, 17072193, 25460865, 33849537, 42237953, 50757760, 59146432, 67534848, 77367424, 85065729, 92700736, 103597711, 109609103, 119310528, 127008897, 137283152, 143556688, 1073741824, 152864768, 160563265, 170837520, 177111056, 186515982, 195209859, 204260943, 210272335, 220070542, 229026434, 237815503, 243826895, 253624910, 262318595, 269149713, 279609361, 286163600, 295568078, 304261827, 1073762435, 313443472, 321553105, 327713295, 337815619, 346038402, 355255311, 363496017, 370049744, 379723776, 388941008, 397322963, 403866258, 413147650, 421963778, 431277202, 437420754, 446963907, 456174164, 464831698, 472547985, 479363602, 488906883, 498117140, 506775122, 512917586, 522199618, 1074829826, 531671700, 540328978, 547365058, 556837588, 565503702, 573317830, 579527825, 590645781, 1075371972, 597827648, 605585993, 613082193, 624200277, 631513091, 1075644870, 641001110, 649366229, 657203206, 665233602, 674555414, 681713792, 690399298, 699721302, 707534918, 713745617, 724478611, 732045504, 739803785, 748471895, 758032979, 766255238, 773637783, 783583893, 790896707, 798803671, 808364563, 815301129, 823969303, 1074352075, 1074638791, 832078537, 1076746184, 1075184649, 1074164684, 1077060549, 1076028421, 1076308938, 1076590541],
    [118, 104, 11, 2401280, 10803264, 18669569, 27058305, 35446977, 43835457, 52355072, 60743744, 69132416, 77912256, 86419074, 94298304, 102711887, 111337551, 1073744578, 119855104, 128361666, 1074287555, 136266255, 144891919, 1074823168, 153409664, 161915906, 170345169, 178839761, 187081794, 195754193, 203375311, 212000975, 220505280, 227080784, 237847058, 245555855, 254059648, 260627150, 271401682, 279503505, 287614016, 296417425, 304955986, 310960773, 321446417, 329819269, 338360337, 346899090, 352903877, 363389521, 371762373, 380303441, 388448337, 394846789, 405316677, 411621902, 422002833, 428401157, 438871045, 445184528, 1073797125, 455557137, 461953614, 470713360, 480198799, 487621646, 498549268, 504029719, 512665110, 522936343, 529195671, 537953486, 549255897, 556490903, 1075382214, 562750167, 571385558, 582810137, 590045399, 596304471, 605587091, 615211095, 622364179, 633141913, 640639512, 646874192, 654899920, 665805400, 672040144, 683473497, 1074099143, 690971288, 697206416, 705230992, 716137176, 723027667, 731830938, 741819092, 747546262, 1077000132, 756996826, 766984788, 772712022, 1077275593, 782162458, 792150676, 798000206, 805886606, 815489557, 823166094, 832494170, 840655573, 1076502476, 848856659, 857432725, 1075728330, 865821269, 1074698189, 1075241931, 1076044811, 1076326344],
    [114, 100, 3, 2418688, 10510401, 17080449, 25477120, 33865856, 42254528, 50643008, 59162817, 67551361, 75939841, 86304896, 92963470, 102785025, 109494337, 119859264, 126517838, 136339585, 1073741824, 143294990, 153116865, 159959634, 168461006, 179366594, 187326658, 195356864, 204104194, 211984899, 221309506, 229269570, 237150915, 246475394, 254435458, 262316611, 1073764354, 1075360003, 269370000, 277127169, 288541205, 294535760, 302293185, 313707221, 321938006, 329425027, 338872981, 344236097, 355492566, 364038741, 369935063, 378454680, 386703951, 397469698, 405824150, 1076941764, 411877911, 420397592, 428647119, 439378454, 445432471, 453812879, 462578321, 470598231, 478978575, 487744017, 496421593, 504381972, 514760728, 521587225, 529687121, 539926680, 546226904, 554582736, 565092568, 1074858949, 571392600, 579748368, 590258264, 596951560, 605473369, 613433940, 622239895, 630506056, 638110354, 647127761, 655794263, 664060616, 671664658, 680542868, 689348631, 697877065, 705219282, 714097364, 722903255, 731431625, 739691161, 748331731, 756597257, 765258266, 773497427, 781763209, 790424218, 798663315, 1074353161, 806666888, 815589978, 823829011, 1075151880, 1074127814, 1075979270, 832367322, 1076260807, 1076803530, 1077341131, 1076568012, 1075793869],
    [86, 72, 1, 2064384, 10819648, 18686081, 27074561, 35463233, 43851969, 52762624, 61309570, 69288463, 1073744578, 77928576, 86474818, 1074287555, 94454351, 1074823168, 103094464, 111640770, 120144594, 128417794, 137444048, 145310354, 153059392, 162338881, 170476050, 178225344, 187504769, 195641938, 203391104, 212670657, 220283599, 229351950, 238107216, 245449359, 254640772, 263272976, 271794835, 279806660, 288438928, 1073797316, 296960723, 304945153, 313360388, 322126355, 330137668, 336542231, 347292243, 353180305, 363569806, 371811030, 378485335, 388588182, 395516565, 405512782, 413753878, 420289233, 430678734, 438919766, 445594263, 454115472, 462232081, 1075393479, 470892752, 479148759, 487669776, 496179925, 1076975558, 504447056, 512956949, 521626264, 529734229, 538403544, 546118225, 555180632, 1075160005, 1075962885, 563692116, 572080788, 580469460, 588857876, 1076240333, 1075736522, 1076803528, 1077333964, 597123608, 1074736073, 1076578251],
    [102, 88, 1, 2450624, 10823809, 18776257, 25493632, 33882112, 42270784, 50659520, 59179201, 67567617, 75956353, 86336576, 94709761, 102662145, 109510721, 119734863, 128279552, 136216641, 145304066, 153289423, 1073741824, 161834112, 169771137, 178858690, 186843663, 195461774, 204024450, 212689999, 220398223, 229016270, 237578818, 246244367, 1073764354, 252248771, 262570574, 271395011, 279798991, 285803075, 296124942, 304949315, 313353359, 319357571, 330262033, 338503811, 344523267, 355427921, 363669507, 1075351555, 371761732, 380700740, 388982481, 396927492, 405866500, 414148241, 422093444, 431032452, 438870724, 447809732, 1074841604, 454247956, 462848659, 473106960, 479815381, 488014355, 498272912, 504981013, 513180243, 523438672, 529745620, 538346195, 548604624, 554911380, 564472001, 571688532, 581249089, 1074339783, 1075673032, 588858902, 597494354, 1077261254, 605883026, 614024790, 622660306, 630784588, 639437330, 647579286, 656081485, 664364693, 672858637, 1077011402, 1075979274, 681116300, 1076260805, 689530453, 698024653, 1076793291, 706281996, 714688214, 723190413, 1074713613, 731448012, 1075260361, 1076577292],
    [110, 96, 7, 2447488, 10313793, 18702337, 27091073, 35479745, 43999360, 52387904, 60776640, 69556288, 77553664, 86333440, 1073746883, 1074809794, 1074298880, 94722240, 102621775, 109520400, 120150734, 127787535, 137045586, 145316366, 153207508, 159975121, 170482254, 178373268, 185140881, 195648142, 203538964, 210306577, 218587670, 228811415, 237730325, 245482068, 252249681, 260530902, 271284949, 278782671, 288040466, 294085206, 304308759, 313227925, 321643219, 329983634, 336028310, 346251991, 355170901, 363578009, 371926738, 378232985, 388194903, 395532308, 405521113, 411787481, 422773782, 429086804, 439083667, 445342233, 456328342, 462641300, 472629273, 478896729, 489882838, 496195796, 506192403, 515048534, 521624091, 530440847, 537339536, 546798300, 556515417, 563422744, 571964060, 581689939, 588850263, 598720597, 605381256, 613754584, 622295644, 632274965, 638935752, 647562778, 655850012, 1073795014, 665829525, 672489992, 681117402, 690995413, 697655880, 706283098, 1074599877, 1075140616, 713500240, 722950875, 731456535, 739727963, 748233879, 1075426247, 756505243, 765011159, 1077004234, 773138008, 1074149316, 781526680, 1077306315, 1076012043, 790169242, 1076293580, 797386448, 1076833225, 1076584397],
    [98, 84, 11, 2312320, 8724481, 17121280, 25509952, 34029569, 42418241, 50806913, 59195585, 67453120, 77809856, 84222145, 92618880, 102975552, 109387905, 1073741824, 119752704, 126165057, 134685390, 143222977, 151462478, 160000129, 168346128, 176900815, 185016974, 193677839, 201794062, 210289296, 218702415, 227108929, 235455056, 243867663, 252397647, 260645519, 269699794, 277422287, 286476818, 1073762243, 296428226, 303254098, 313205250, 320031378, 330482387, 1074569156, 336283791, 345055761, 355648019, 361326593, 370221713, 378356295, 387105492, 1075628997, 395387601, 406538773, 414368403, 420553297, 431704725, 437076615, 445825684, 453984790, 464330774, 473647829, 479019719, 489865811, 498813525, 504185351, 512934484, 523051606, 529481814, 1074332679, 538798615, 545833680, 555575895, 563266068, 573383318, 579813526, 589130391, 596959832, 606806658, 614296279, 622125720, 631972418, 1074090954, 1074900994, 638903000, 648880854, 655311062, 664068632, 672875021, 681263821, 1077009353, 1075456972, 689652365, 698040909, 1076524998, 1077318669, 1075241931, 1076044811, 1076326344],
    [106, 92, 9, 1310912, 10330305, 18849984, 27107457, 35627072, 43884609, 52404224, 60799490, 69181568, 77071042, 85827585, 92914318, 101163729, 111254019, 1073746306, 119013442, 1074809731, 127525584, 134718033, 1074298880, 144808131, 152576659, 161079952, 170107525, 178362435, 185049745, 194519635, 203547141, 212049925, 220305539, 226992657, 236462803, 244965968, 253993669, 262125762, 269197831, 278405651, 287432901, 295936581, 304068738, 311140935, 320340098, 1073796101, 328180308, 337764421, 344695495, 354400322, 362283010, 370795024, 378249863, 388741714, 395575296, 1075124231, 403677908, 413261957, 420717141, 430684882, 437518400, 445620884, 455721615, 462660309, 473143958, 479461504, 487563796, 497664591, 504603157, 515087062, 522453137, 531219151, 538157717, 548641302, 556007441, 564773391, 573807190, 581173329, 587842126, 598456850, 606339281, 613008078, 623622802, 631898183, 1075398601, 638173710, 1074110411, 648675463, 655343764, 665452743, 671998487, 682229767, 688898260, 699138261, 705553047, 715915285, 722330327, 732692629, 1075703752, 739107415, 749469781, 1076767684, 756006996, 1076523980, 764395540, 1077055437, 1074722762, 1077355462, 1076061190],
    [110, 96, 11, 1958913, 8759489, 17137665, 25526465, 33914945, 42303617, 50823168, 59211968, 69272270, 75989120, 84379854, 94233729, 101154880, 111608527, 117934734, 127788225, 1073741824, 136774223, 143100430, 152953921, 161939983, 170124480, 176654926, 187105935, 193693903, 203678784, 211877966, 220455936, 227256977, 1073765315, 237043726, 245621888, 252422673, 261325395, 270598286, 277734467, 285977169, 296166096, 302900227, 311527507, 321331856, 328051221, 336454787, 1075352517, 345211539, 354886224, 362136581, 370247827, 380183063, 386631759, 395953865, 404193994, 412320275, 421995024, 1074843591, 429508169, 437356563, 446136970, 455680727, 462283971, 471050776, 1074596169, 479691274, 487817939, 496181974, 505005193, 512993880, 521634378, 531178135, 537766549, 546686149, 1074353162, 556343895, 563463301, 571714264, 580067926, 588891145, 596486741, 605233814, 613264085, 622183493, 630522578, 638683347, 647430676, 655600280, 664502861, 672465490, 679848065, 689668621, 697762388, 705013825, 714834573, 722797074, 1075164104, 730564751, 740000461, 747840022, 755345409, 1077003277, 1074144194, 1075995650, 1076279243, 764740242, 1077338060, 772516561, 781648532, 789284879, 798425812, 1075784644, 1076588486],
    [98, 84, 10, 2589824, 9691137, 18079809, 26468545, 34857089, 43376832, 51765312, 60703426, 68542592, 78087232, 85319680, 95017612, 102646338, 1073744194, 111772812, 1074287555, 120183372, 1074823168, 127811586, 136938572, 142992004, 153737932, 161366146, 170493132, 178903564, 1073803264, 187270156, 195426894, 203678415, 210470477, 220592654, 228844047, 235636429, 244081233, 254925520, 262398607, 269190669, 277635793, 288479888, 295952975, 305235151, 311190033, 322034192, 327911053, 336355985, 347200080, 355566607, 363592274, 371688640, 380920468, 388758162, 397509711, 406086228, 414833301, 422020096, 431252180, 439999189, 447841423, 456417812, 464255698, 471434389, 478536260, 490330645, 496739926, 503702212, 514587154, 521766101, 528867844, 539359886, 547071702, 1076960260, 557439573, 563848854, 1075665861, 572914382, 580486229, 590766679, 597031507, 605791766, 615932439, 622197395, 630817813, 641098391, 1075419078, 646963723, 655751891, 666264279, 672129739, 680917523, 688906891, 1075179464, 697295435, 1076758471, 1074154507, 1074701257, 1076028425, 1076311047, 1077373898],
    [106, 92, 9, 2326721, 8765632, 17154112, 25542784, 33931264, 42451009, 50839553, 59228353, 69435457, 76005505, 86212737, 1073741824, 94601217, 101050891, 110068233, 1073768448, 117951180, 1076408321, 126845513, 134728332, 143376963, 152011465, 159990415, 168413710, 177177225, 185164304, 193448524, 204177994, 210233874, 218718928, 229343946, 235399762, 243884624, 254509578, 260565714, 271286922, 277439120, 288090772, 296206484, 302760643, 313630734, 321776341, 329761492, 336421523, 344703619, 355574350, 361587219, 371976404, 380092948, 386777669, 397517518, 403792598, 413919252, 422036052, 428720645, 437756433, 445866647, 455994005, 463045261, 470639315, 481028180, 488088273, 497936917, 504455766, 512606853, 521765581, 529001106, 538010262, 546030083, 556901006, 1076940803, 563307095, 570813131, 1074862018, 580362897, 590211669, 596853464, 605651469, 612756107, 622019224, 630047429, 639205965, 1075147781, 646433292, 654918351, 664248913, 672359127, 679864907, 688507086, 696861263, 1077251014, 1074383878, 705284238, 713638415, 722690583, 730449998, 739459672, 1074661319, 1074162695, 1076796356, 1075502084, 747463251, 756236824, 764502550, 1075782600, 1076061192],
    [122, 108, 13, 1449152, 10363968, 18752640, 27141312, 35529728, 44049473, 52438209, 60826753, 68959884, 77603841, 85870093, 92546702, 102514380, 111036045, 119291404, 127813197, 134751824, 144457292, 1073750016, 1075865601, 152979149, 162432721, 168436945, 177609792, 185222863, 195986961, 201991185, 211688528, 218907790, 229803668, 235546257, 245505732, 1076396484, 1073792004, 252593232, 263095441, 269100625, 278273152, 1074076613, 285886095, 296649809, 302523920, 312351760, 321537686, 330466900, 336078544, 345906384, 355092182, 364021460, 370157079, 377759310, 388111364, 397035030, 405964308, 411575952, 419702478, 429792400, 438978134, 447783959, 454043223, 462822400, 470435407, 481339095, 487597271, 495199758, 505552004, 512509134, 523282071, 529540247, 538060506, 547494980, 554451982, 565224535, 570957523, 579617870, 588547739, 596123219, 604653071, 613713499, 621289107, 1075406786, 630473946, 638879451, 646454803, 1076202438, 655246544, 664045083, 672022165, 680412304, 689604248, 697443866, 705699545, 714359834, 723420818, 730998362, 739911242, 747642457, 1074385859, 1074926595, 1075212231, 756302938, 765363730, 773465738, 781196953, 789464080, 798656088, 806495898, 815408650, 823017173, 831800474, 840861266, 848963274, 856571477, 1076796426, 865764888, 873348629, 1075761096, 1074738121, 882542296, 890248729, 899581650, 1077114827],
    [126, 112, 12, 2327553, 9962625, 18351169, 26739713, 35128513, 43648000, 52036672, 60973647, 68813952, 77825217, 85591232, 95170068, 100926994, 109855376, 117835283, 128156737, 137244309, 142870098, 151798288, 159909013, 170099841, 179187221, 185074709, 193618435, 201982979, 212567122, 1073750017, 221130325, 227017813, 235561539, 243926083, 254510098, 263073493, 268960981, 277504707, 285869251, 296584719, 304885332, 310773459, 319447683, 327812227, 338527311, 1075859459, 346828500, 353125072, 363693775, 371994260, 378290768, 388859535, 1074831301, 395052743, 404906191, 411961046, 420717776, 428213907, 438460559, 445515286, 454272144, 1075636166, 464142929, 473277975, 478809688, 487327367, 497180687, 504603664, 1076170692, 512765593, 522863121, 529401494, 538158160, 548029137, 556928602, 563586262, 1074617282, 570689234, 581583505, 587990599, 596250136, 607495895, 1075427272, 612632210, 622354643, 630195722, 640814618, 648774802, 655099399, 663896199, 674369178, 682329298, 1077264391, 689061959, 696913560, 708159127, 714629267, 722873947, 733324887, 738592339, 748183635, 755633880, 764282454, 773301334, 781190730, 790249482, 798371547, 806855830, 814745226, 823803978, 833752794, 840410134, 848445447, 857091739, 865076938, 874135754, 882257435, 1073875913, 1074414602, 890912906, 898641625, 1074173901, 907165895, 915418649, 924344339, 932195929, 1075245003, 1076833228, 1076589518],
    [118, 104, 9, 2409600, 8944769, 18375680, 26764416, 35153088, 43541568, 52061377, 60449857, 68838529, 77907136, 84573836, 94004225, 101082754, 111461376, 118128332, 127533571, 134637122, 143156227, 153404480, 160202382, 170157583, 176947215, 184968706, 193756750, 203712143, 210501775, 218686992, 227311310, 237266511, 244056143, 252241488, 260865550, 270821071, 277610703, 285795984, 294288908, 302802629, 310961872, 319454796, 328099462, 1073748932, 336512721, 344352450, 353131663, 1075343362, 363355794, 369911429, 380823060, 386686031, 395495061, 403996301, 412746435, 419980483, 431408854, 438853138, 446300803, 456320660, 461923459, 472407762, 481740374, 487095361, 495740485, 505020995, 515294870, 520643651, 531127890, 537814726, 1076928456, 1075639299, 548595412, 554204161, 562980358, 571482775, 582149716, 588539465, 596794899, 604923462, 613425687, 621987413, 630482633, 1077219334, 638344399, 646735365, 655368791, 666289686, 672425609, 1074874373, 1074375685, 680681171, 688923351, 697222737, 706111051, 714374669, 722388497, 731277003, 738753729, 747554449, 756442635, 764567123, 772982485, 781608587, 789872333, 1076743179, 1074669579, 798934616, 806643209, 814504975, 1076515849, 824100504, 1075218375, 1074192391, 831676051, 840877592, 1076036554, 1073964042, 848592461, 857655000, 865256981],
    [114, 100, 8, 2499585, 8774849, 18367616, 26756288, 35144704, 43533376, 52053121, 60441793, 68830209, 78259852, 84272129, 93996097, 103181839, 111814156, 117819021, 128591436, 134596109, 145256133, 151536837, 162145996, 168281681, 178810501, 185091205, 195437761, 201836241, 212364869, 218645573, 229246478, 235390609, 245788239, 252200453, 262801102, 268944913, 1073745925, 1074818053, 279342735, 286139584, 294504147, 304508623, 311420562, 321266817, 329804805, 336611016, 346441237, 355075662, 361612947, 1076662211, 370036246, 379995861, 386802816, 395167251, 403590742, 412108296, 422708816, 428721747, 437546644, 445662792, 455739022, 462546133, 471101012, 479323157, 487466048, 495865494, 504383112, 514213461, 521266261, 529802253, 1074582536, 1075128328, 538209812, 547767957, 554574848, 565167642, 571363030, 582092432, 590333594, 1076448196, 597053143, 607258320, 615499354, 622096084, 631645249, 640665306, 1074374599, 647646873, 655484053, 664020557, 1076216774, 672812633, 680519186, 689185933, 1073881033, 1075736585, 697978393, 707921424, 713410253, 722882135, 730851026, 739517645, 748047895, 756418200, 763741261, 1077058498, 1075508226, 773476057, 781583960, 789571154, 1077348299, 798379671, 806749912, 814081089, 1074226122, 823526936, 830858369],
    [122, 108, 5, 302272, 10527744, 18916544, 27305024, 35693696, 44213313, 52602049, 61392400, 69379201, 75799616, 86156289, 94971394, 103335568, 111582865, 120137346, 126133780, 136890064, 143042133, 153525841, 162080322, 168076948, 178832976, 184985301, 195469009, 204023490, 210282134, 221300291, 226928277, 237411857, 1073745922, 246228691, 252225110, 262988886, 268871189, 279624725, 288171539, 294168086, 302835410, 311082711, 321726035, 330359956, 336248343, 346891923, 352626388, 363906691, 371899477, 380282458, 389359128, 394831574, 405857492, 411745943, 1074809796, 422225562, 431433350, 439149782, 445300311, 1074310085, 455780058, 464987718, 470066772, 481347267, 489340117, 497722906, 506930694, 514901507, 523549701, 1076412934, 1073815555, 532096198, 537716370, 548977731, 557131480, 565240916, 573226133, 582297240, 590144662, 599047237, 607463000, 613213778, 624213125, 632751322, 638379538, 649640963, 655795850, 666305562, 674292756, 683195587, 689350218, 699860058, 707585046, 716487877, 722904778, 733414554, 741917717, 750304387, 756459018, 765265497, 775472277, 780442752, 1075923978, 1074633675, 790431257, 800638037, 807050305, 1075441607, 815597273, 825803989, 830774272, 840763033, 849274459, 857381889, 866051611, 874159297, 882828955, 890936449, 1076770766, 899606235, 1077307336, 1076273097, 1075759053, 1074213836, 1077106639],
    [106, 92, 13, 2015297, 10224769, 18908160, 27296896, 35685568, 44074048, 52593857, 60982337, 69370881, 77464768, 85901313, 94536833, 103452178, 111330000, 117843473, 128749203, 134620753, 144621761, 153915091, 159786705, 169787521, 179080723, 186827408, 193341073, 204246611, 210273989, 220381712, 228459648, 237670098, 243828293, 253936208, 262013952, 1073750979, 271224466, 277382661, 287179840, 296542277, 304778834, 310937221, 321708229, 328991809, 1075855365, 338485381, 345769153, 353152597, 363865171, 372039685, 1073781700, 378318485, 387712001, 395095765, 406062288, 1075366850, 411872789, 420528662, 430973971, 439922200, 445440663, 456139923, 465088216, 470606423, 481305811, 490253976, 495903449, 506865236, 515419736, 521307656, 529580630, 538347145, 548808404, 557493385, 563528410, 571901449, 582222864, 591047689, 596566681, 605455945, 615777360, 624602185, 629990103, 639010505, 649471636, 1074335753, 658156745, 663914120, 672187094, 682886288, 689079880, 697229913, 1074874315, 708191764, 714523290, 1074113478, 1076481994, 722264599, 730784281, 1074667463, 739689050, 1075734476, 747800264, 756466202, 1076270088, 1075245006, 764461718, 1076835277, 1077114831],
    [106, 92, 9, 2153536, 10970304, 18907265, 27321408, 35709952, 44098688, 52487360, 61006977, 69395649, 77784065, 86467584, 94559952, 102793217, 111338561, 119725584, 127959233, 137061905, 145286869, 153280144, 161513537, 170616529, 178841109, 187204116, 195223120, 204170833, 212395605, 220758740, 229336721, 237436503, 245950101, 254313044, 262882516, 270990871, 279478932, 288048276, 296418902, 304825428, 313196246, 319849048, 329991188, 338362006, 346488471, 355681429, 361948871, 370180760, 380304918, 389235733, 396846144, 405208791, 1073755075, 413195456, 422790229, 428901080, 438789248, 446749824, 1076911042, 454066712, 463526912, 473122005, 481642066, 487644755, 498419218, 504683544, 515196626, 521460952, 531973778, 538500634, 546365139, 555706009, 1075361738, 1077200840, 563142291, 572483289, 1074072517, 580181144, 589260377, 1074348998, 596829767, 605594140, 614262413, 621862419, 631203353, 1073845188, 638772743, 647537308, 656205325, 664329946, 673138395, 1074916300, 1076506571, 680715911, 689480284, 698148429, 706272922, 715081371, 1076780039, 723034844, 731702989, 739564632, 748635675, 1075743757, 756604506, 765412955, 1074717646, 1076041679, 1075275721],
    [122, 108, 9, 295937, 8676545, 18924736, 27313216, 35701760, 44090496, 52610113, 60998785, 69387265, 75908624, 84182145, 94553281, 100986578, 109733585, 117736513, 128380610, 134899345, 142902465, 153546370, 159696387, 168469696, 176842321, 185003732, 193250947, 202024000, 210396689, 218558036, 226805315, 235578368, 245916739, 252112532, 260490901, 269132928, 279471107, 285787734, 296414294, 302434005, 311199376, 321414275, 327861958, 338095618, 344376853, 353142352, 363750598, 369936024, 380824728, 386696208, 397567493, 1073749956, 405589141, 411485781, 419841744, 428639440, 437044952, 447933656, 453395600, 464299539, 1075599490, 470861337, 478725846, 489352406, 495240899, 505963715, 514631379, 1075351555, 522644546, 528893008, 539797139, 548195413, 553935873, 564962899, 571524761, 579520134, 590138389, 598631558, 605332633, 613205592, 624094296, 629433409, 638886937, 646497942, 657124502, 664446682, 674391685, 680576729, 688571974, 699190485, 705995993, 716334661, 1074850759, 722519641, 730514950, 738520658, 749626438, 756852247, 1076428806, 764200472, 775089176, 783180806, 790406807, 797492758, 808119318, 813982849, 823436377, 1073838024, 830795282, 840607322, 850552517, 1077256197, 1075956682, 856092180, 865773082, 872738450, 882681559, 1074409419, 1076786124, 1077057481, 891070039, 899327642, 1075234766, 1074204621, 1074751439],
    [118, 104, 11, 1916097, 10560512, 18949184, 27337856, 35726528, 44246145, 52634689, 61023425, 69024769, 77800449, 86449730, 92882640, 103227074, 109659664, 120004098, 128820754, 134825616, 145170050, 153986706, 1073745922, 162088467, 168371219, 176891605, 186465345, 195929682, 202597972, 210445845, 220019841, 229607108, 235881493, 244000405, 254746115, 263038674, 269436117, 277554773, 288300675, 296715780, 1074807427, 305219077, 313465923, 321881732, 329860819, 336143571, 1073787012, 347020483, 355435588, 363415187, 369697939, 378355345, 1076945797, 389104773, 395413015, 403646038, 414399511, 422659269, 428811990, 437075665, 445875737, 456213573, 462366358, 471015128, 479430297, 487810772, 495920662, 504569432, 512984793, 522798675, 529081427, 540229207, 546407511, 555173078, 562904657, 571704921, 580085268, 588719706, 598949591, 605127895, 1075911622, 612976208, 622274074, 630398488, 641574619, 647710426, 655828186, 666058391, 675128859, 680477845, 689383066, 698033675, 705510929, 717071963, 722945174, 731588299, 739450520, 750626459, 756499542, 765142603, 772899991, 1075406793, 781665302, 790439567, 1076207559, 1075702728, 798189204, 807216847, 1076500429, 815481882, 823993935, 1075201998, 1074182090, 832259226, 840640139, 1077333003, 848249941, 857548303, 1074726927, 865813594, 1074491340],
    [118, 104, 10, 1916928, 10781888, 19344577, 27821584, 36383760, 43860096, 52496066, 61550160, 69764752, 77414592, 86181587, 94438914, 103492752, 110968896, 120358017, 128255508, 136513043, 144770690, 153824976, 162218004, 170689601, 178587284, 186844755, 195102274, 204161172, 212632577, 220671041, 1073747970, 228918868, 237274112, 246104148, 254225409, 262473428, 270730899, 279479504, 288047316, 296168577, 304907457, 312828630, 319368786, 329548864, 337994262, 344534738, 353175238, 363365456, 371548758, 378088978, 1075334085, 386729606, 396657792, 405103254, 411643538, 420283910, 428944921, 438788290, 448168979, 456593051, 463953922, 473334995, 481758811, 490112147, 498680516, 506924571, 514285698, 523666515, 532090587, 538093201, 549012100, 554632776, 563258897, 573005890, 580062876, 1074302919, 588056134, 596813393, 607732292, 613748378, 1074585668, 1075908614, 621979345, 632897540, 638783004, 647048793, 656320085, 665935955, 672958103, 682713107, 689245914, 697239048, 706651861, 716267667, 722669276, 730793608, 739323545, 748455447, 758210771, 1074880459, 764348104, 773621335, 781664792, 789909018, 1075680264, 798787287, 806830744, 815074906, 823209689, 832480917, 840385112, 849258005, 857162456, 865275484, 1075177420, 1076234189, 1074163663, 1076803529, 1077330894, 1073951690, 1077111747],
    [110, 96, 5, 2344000, 10706113, 18965504, 27354304, 35742848, 44131392, 52651073, 61039617, 69428353, 77841600, 85818896, 94594241, 103088850, 111764690, 119784448, 127762000, 136643218, 145319058, 153339008, 161316496, 170197522, 178873362, 185296515, 194870992, 203810513, 212140626, 220816466, 227370693, 237337797, 245753425, 254607891, 260924997, 270892101, 279307793, 288162451, 294479365, 304307201, 312862353, 321716819, 328033925, 338290389, 346389509, 1073743877, 355271379, 363456149, 371416193, 378348052, 388621909, 397246102, 1074295746, 405890583, 413787669, 421747777, 428802584, 439576217, 447577814, 455861401, 462234324, 472999575, 481519129, 487286339, 497384581, 506192921, 512565908, 520840899, 531463702, 537854616, 548136537, 556885719, 565404761, 571172355, 582057171, 588186328, 1076926467, 598572630, 604963416, 615245529, 623994455, 632513753, 640777299, 647358042, 657415191, 1075367880, 663560788, 672523802, 682581079, 689301210, 699497491, 706078362, 1074605001, 716135575, 723198555, 1076450244, 733052051, 739975707, 749690071, 756753115, 765164564, 1074902982, 773530267, 781941844, 790330580, 1077272526, 1075709899, 798719124, 1074163658, 1076798412, 1076029391, 1076298695, 1073960909],
    [106, 92, 12, 328769, 8709249, 17132737, 27346048, 35734528, 44123328, 52511808, 61031425, 69420225, 77808769, 86601424, 92595393, 100992193, 111363137, 120155728, 126281233, 134546433, 145321616, 151447185, 159712385, 168232016, 176647701, 185001553, 195653136, 201786512, 210035713, 218563600, 226979413, 237954646, 243729616, 252145301, 263120406, 271787538, 277311189, 288286422, 296953554, 303001299, 313452182, 1073742790, 322119314, 328298007, 335864897, 345075287, 352773841, 363791882, 372450898, 378629847, 387245200, 1073762186, 395396747, 403795607, 412542612, 423175833, 428951243, 437576784, 444951681, 456730137, 462777408, 471254552, 481231946, 487671371, 495283201, 504809176, 515450457, 1074566085, 521225739, 529493523, 538371668, 548340938, 1074840587, 555017232, 562392129, 574170841, 580217856, 588695128, 598672522, 1074072516, 605383872, 613869268, 622265882, 630156947, 638903504, 647431898, 656230031, 663711315, 672581272, 680986202, 689784527, 698287232, 706047104, 714532372, 723338831, 731841728, 740115983, 748618816, 1074353167, 1075158989, 1075702722, 756483738, 1076508616, 765395968, 1077306316, 1076013001, 1076293582, 1076829123, 1075540935],
    [118, 104, 5, 2630657, 10593344, 18982080, 27370496, 35759232, 44278913, 52667457, 60810960, 69444801, 78128257, 86221825, 92644881, 102753872, 109553234, 120071361, 128040579, 134588113, 144696848, 153724035, 162014273, 169983555, 176531025, 186640016, 195667011, 201959060, 212207251, 220315331, 226862737, 237749330, 245998787, 252290644, 262538835, 269198933, 277595345, 285845204, 294397076, 302753301, 311149649, 319399444, 327951444, 1073750980, 336567877, 344958486, 353092753, 361506004, 370122437, 378512982, 386647057, 395060244, 404864515, 412067542, 420463638, 430547971, 1075855363, 439328471, 445621910, 454280340, 462530264, 472882711, 479708181, 1073779650, 1074851141, 489660055, 496084504, 504611924, 514197203, 523476551, 529900615, 538166292, 548642439, 555066503, 564905682, 571582040, 579314898, 589694483, 598974151, 605398215, 615237138, 621257746, 632528391, 638952455, 648791698, 654812306, 663856792, 1076698054, 1075398663, 674209367, 681158283, 688899158, 697277573, 705406613, 714589333, 723101387, 730831877, 738961109, 747619478, 756655627, 1074378697, 764918872, 773432907, 781173974, 1077267467, 790084632, 798213332, 806861976, 815252565, 823639256, 832029909, 1074670541, 1076523980, 840705561, 1077059530, 1075759048, 849094297, 857482841, 1074210766, 865871577, 1076320207],
    [114, 100, 13, 2329665, 8725697, 18973888, 27362304, 35750976, 44139648, 53325520, 59057153, 68674066, 75858962, 86879888, 92611713, 102490643, 109675539, 120434256, 126166081, 136045267, 143230163, 153988624, 162202832, 169599635, 176784531, 187368464, 195267777, 203801109, 210077266, 218728019, 229311632, 237210753, 1073748930, 245744213, 254477392, 262376449, 270910101, 277186194, 288730708, 294463185, 1075339204, 304464597, 313896660, 319628945, 329900695, 339062420, 344794641, 355066583, 361072338, 372616724, 380438104, 388620823, 395151049, 403803862, 413992664, 1075612615, 422175319, 428705417, 437358102, 447547032, 1074328518, 456122502, 462917201, 472712728, 479715538, 487425545, 496471057, 504440411, 514842694, 520980041, 529343569, 538414225, 1076957193, 548397062, 555058891, 563187350, 571680412, 580378770, 588745937, 596969053, 1074873290, 1073849283, 1075963848, 605544530, 613518934, 622134941, 630972499, 638658075, 649060550, 655435419, 1076236229, 664257049, 672902878, 680601307, 1074677708, 689423065, 697665099, 706457118, 714286684, 722977433, 731219595, 740011614, 747963933, 1074180045, 756531801, 764773899, 773566110, 781518557, 1076810763, 789701210, 798172892, 806478362, 814949916, 823255706, 1075260366, 831644378, 1076590543],
    [94, 80, 7, 1432576, 10380289, 18972865, 26862592, 35251328, 43640000, 52028480, 60548225, 68936705, 77325377, 85318784, 94470273, 102516367, 110879937, 119635969, 127682127, 136183314, 144039104, 153190465, 161236687, 168420994, 177593408, 186402319, 193569300, 201975298, 1073754112, 211803792, 220095553, 229212739, 236969552, 245261441, 252813909, 262038721, 270401170, 279544515, 287301328, 295978643, 304710275, 313288209, 320732882, 1076913219, 329875459, 1076148164, 338454097, 345898578, 353739462, 363087379, 371580566, 1077203909, 378905222, 388253395, 396746454, 404070918, 413951633, 421912086, 429236806, 438584915, 447077974, 1074867206, 455894737, 463461904, 472794245, 479306453, 489571333, 496083477, 504620567, 514737221, 521773079, 529786519, 539903173, 546939031, 554952279, 1076716492, 563716183, 571729623, 1075948490, 579969685, 587834004, 1076478919, 1073876941, 597270743, 604628674, 1074681801, 612999892, 621388372, 629794370, 1075218379, 1074190338, 639100430, 1075514312, 647489230, 655877710, 664266382, 1074486286],
    [114, 100, 5, 2466817, 8873153, 18859137, 27247617, 35636417, 44024897, 52544640, 60933120, 69321792, 76113420, 84379276, 94487744, 101156428, 109528717, 119918287, 126567631, 134710988, 145083983, 151733327, 161850433, 1073752064, 170249743, 1076391937, 177055310, 185287695, 193578704, 203804303, 210453647, 220570753, 227133008, 237883090, 244164302, 253060304, 260687376, 271437394, 277316620, 286614544, 294241936, 304991762, 312845505, 320169104, 330157714, 336438926, 345334864, 355585748, 361875079, 369993230, 377964109, 389140116, 395281472, 403130061, 414305876, 420447360, 428295693, 439471636, 445613248, 453469313, 1076932549, 462278294, 471582408, 478766284, 487556096, 496094741, 505136648, 512320588, 521634949, 1076683718, 529788567, 538691144, 545875084, 555189445, 563343063, 571966469, 580609667, 588369621, 597132357, 605775427, 1075918403, 613674519, 622700049, 631072339, 638701141, 647865937, 656106499, 663604822, 672908936, 681404115, 689931395, 1077241801, 1076200456, 697421461, 705807879, 714974929, 723215555, 1074121674, 1074400266, 731735571, 740262979, 747892311, 756139719, 763847681, 773817539, 781045462, 790472337, 798844563, 806211094, 814859847, 822568001, 832537603, 1074680772, 1074954247, 1073929154, 1075518466, 1075795915],
    [102, 88, 11, 1048576, 10266689, 18753536, 27142272, 35530816, 43919552, 51774156, 60598273, 69888578, 76546176, 85764289, 95054530, 101712064, 110930049, 120482510, 127271564, 136743567, 1073750016, 1075865601, 145385986, 152437324, 161909263, 1076400386, 1074844674, 170551426, 176695955, 185991692, 195603085, 204368462, 210250451, 219152448, 229157453, 237922958, 243804691, 254323213, 262144147, 271477262, 277359187, 287738447, 295698515, 305285840, 312904399, 320864275, 330451472, 338209485, 346030291, 355617360, 361507479, 372419222, 379715735, 1075125188, 389171856, 396886081, 403720786, 411839063, 421658711, 1075399619, 431254040, 1074374597, 438968977, 447916566, 456419928, 464134865, 473082454, 479480405, 487336663, 497689169, 506637014, 513034773, 521415175, 531103873, 1076216774, 1073873926, 540306072, 546712072, 556409361, 563366549, 571747015, 579611159, 589430807, 599026392, 605432392, 614989825, 621824722, 630598344, 639762647, 647252693, 655764104, 665321665, 1074154504, 672156178, 680798855, 688933522, 697576007, 1074699271, 706497108, 1075770313, 714885780, 723274452, 731662868, 1077098443, 1077374922],
    [114, 100, 6, 362689, 9963712, 18352256, 26740736, 35129408, 43649089, 52037761, 60830223, 68815041, 75860033, 85592065, 94384847, 101025921, 111282704, 119550607, 126191617, 136448656, 144716367, 154249231, 1073750017, 161614416, 170684113, 178794512, 187803855, 195168976, 204238481, 210111043, 220737744, 229746767, 235425298, 243796613, 254292112, 263301263, 271347217, 277350981, 285479572, 296716355, 304901713, 310905541, 319033940, 328173568, 336202261, 344477330, 352717443, 363343952, 372213891, 1075868612, 378145429, 389180549, 394791429, 403671232, 1076924421, 411699797, 419974738, 428214787, 439322627, 444863188, 453529298, 461769411, 472877251, 1074839555, 478808789, 489843717, 495717015, 506955927, 511971860, 523398213, 529271383, 540510295, 546452056, 556952773, 562825751, 574064663, 580006424, 588533395, 596380375, 607619287, 613560984, 622087699, 630163584, 1073817538, 638726872, 647253587, 655329344, 664015513, 672419539, 681420880, 689181273, 699420246, 706586768, 1076194246, 714347033, 724586134, 731752464, 739513049, 749751830, 756918480, 1076475847, 766529238, 773818517, 1077266379, 782134874, 790595669, 1074143180, 798912026, 807373013, 1075728333, 1074698186, 815689434, 824150037, 1075235785, 832466586, 1074474952, 1076845518],
    [106, 92, 9, 540736, 10512385, 18901185, 27289729, 35678273, 44198016, 52586560, 60975296, 69354192, 77752320, 86650385, 94519824, 103427793, 111297168, 120515156, 128593553, 136462928, 145680916, 153759313, 159924224, 170846868, 178917011, 185090240, 1073755074, 196012756, 204082771, 210256000, 221170197, 226897108, 237519570, 246336085, 252062868, 262685202, 1076904900, 271501973, 277228564, 287851154, 1073779651, 296667861, 304746003, 313016914, 322226903, 329912019, 1074848709, 338576089, 347392663, 353119830, 363741721, 372558423, 378416153, 388907609, 1075907526, 397855450, 403451606, 414073497, 420768328, 431278615, 436612180, 445931537, 456575578, 462302297, 471097489, 481741466, 487460444, 496263377, 504785482, 515295770, 521022617, 529941016, 538339850, 546891859, 554569436, 563372113, 572057619, 579742937, 588661464, 1074360263, 597060234, 605735451, 613166742, 622215832, 630901403, 638455324, 647654028, 655770200, 664038088, 672721043, 680398492, 689596940, 697723594, 706398811, 713829910, 723151564, 1076737995, 1077271562, 731146760, 739829971, 748317260, 1075710988, 756312712, 765119195, 1074681801, 1075222536, 1075496909, 1074211790, 1076586447],
    [134, 120, 11, 1960129, 10504385, 18892865, 27281409, 35670145, 44189696, 52578432, 60828176, 69355584, 77457537, 86132928, 92555923, 102771344, 109464210, 119916690, 128733780, 136595540, 142887443, 153102928, 159795730, 170248210, 179196501, 186927636, 193219155, 203434704, 210258646, 220973270, 229528277, 237259412, 243550931, 254027795, 260590166, 271304790, 277498583, 288116756, 295979732, 304761346, 312748115, 319310486, 330025110, 338579989, 346704450, 354691219, 361122386, 371574866, 380390105, 388780180, 397036162, 405022931, 411585046, 422299670, 428493399, 439243413, 447498777, 455756482, 464267394, 470174418, 480626898, 1073754114, 487213719, 497832148, 506219097, 512510532, 522987522, 531875908, 1076913091, 537545239, 548303576, 556550809, 562842116, 573319234, 581560849, 590246552, 596396676, 606873794, 615762052, 623800856, 629951172, 640690265, 649316548, 1075871748, 657355352, 665856025, 674482180, 682913795, 691021977, 699001425, 708341975, 716187865, 724167313, 733507735, 739387542, 1073798087, 748546049, 1075384265, 758411395, 764545108, 773711937, 783577155, 789719254, 799664849, 809005079, 814876884, 823388352, 1074618312, 834170967, 840706258, 848554048, 1075686342, 859074755, 865216534, 873719808, 882528794, 890374292, 898885760, 907694810, 915539988, 924313749, 932860570, 940714070, 949479509, 958026330, 1076480972, 966535314, 1074403275, 974645269, 983312402, 991422677, 1075201997, 1000089682, 1074172874, 1074984901, 1077356495, 1076326350],
    [134, 120, 5, 2007168, 10946625, 18393217, 26781889, 35170369, 43558913, 52078720, 60467264, 68856000, 77636172, 86444161, 94021632, 103205379, 109357570, 119579148, 128387073, 137161294, 144613440, 153684559, 161925763, 169779392, 176753361, 185256594, 195076748, 204016335, 210422482, 220110848, 227084817, 235588178, 245408460, 254347791, 260753938, 270836372, 277416593, 287754819, 296002260, 302582353, 1073743363, 1074028547, 312920259, 321167892, 329845391, 335981061, 345033235, 354722388, 363268289, 369535557, 378587731, 386573005, 395258518, 403221190, 411478661, 420530835, 428515917, 437463768, 445164166, 453421765, 464317070, 470721040, 479144534, 1075884037, 487639763, 495886928, 504310294, 512272966, 523037390, 529834517, 538389015, 545827334, 556591630, 562995856, 571943639, 1076943878, 582543876, 588939457, 597232154, 1075643268, 1073832964, 607709252, 613329480, 622493697, 630401560, 1076213703, 641263748, 646228610, 655008269, 664341210, 674818244, 680700553, 689218197, 697510552, 706529945, 713992904, 722774602, 731545729, 739715671, 748603931, 755935880, 764717706, 772711120, 781781594, 790416089, 797223618, 806791883, 815047381, 823601815, 832490203, 839821832, 848603658, 857374785, 865282648, 1077270536, 874302041, 881109570, 890677835, 898278029, 907610778, 1075447810, 1074424834, 916376219, 923970057, 932620811, 940876373, 948906710, 958319195, 965913289, 974563979, 1076792331, 1074718731, 983353881, 991078985, 999598794, 1076563977, 1075008522],
    [106, 92, 8, 264257, 9996352, 18385024, 26773696, 35162112, 43681793, 52070529, 60994188, 68847809, 75761857, 85624897, 94276174, 102937292, 109316225, 119573007, 127830542, 136491596, 142870529, 153127631, 161385166, 170045964, 176564288, 186681999, 194939534, 204124238, 210380943, 220236367, 229174929, 235188752, 243935311, 254332563, 260485714, 269101263, 279768724, 285651474, 294004864, 304777749, 313323092, 319206034, 327821327, 338332309, 346877460, 352760530, 361113600, 371886677, 380169809, 386183824, 394668224, 405441237, 413724369, 422621782, 430844557, 439152340, 447787542, 456010317, 464047635, 473084569, 481176077, 487492229, 497610257, 503624272, 514730701, 1073745859, 521046725, 529460951, 540062358, 546179093, 554601029, 565228246, 571475980, 579766789, 590524953, 1074550724, 1075095556, 596510933, 1076414469, 607302233, 613419084, 624079577, 630196428, 640208595, 648720590, 655362188, 665374291, 673886222, 680396949, 688844439, 699052174, 705562709, 714010199, 721728208, 733262424, 1074339784, 1075671048, 739175959, 750039704, 1076990919, 1074912198, 1075457031, 1076786182, 758428184, 1077314498, 766816984, 1073924043, 1074210761, 1076323274],
    [130, 116, 8, 1884160, 10545153, 18933889, 27322433, 35711169, 44230784, 52619456, 61007872, 69255696, 77785152, 84315714, 92596290, 103211537, 109481666, 117762242, 127976016, 137030163, 144490688, 154308308, 159836372, 169656384, 176769621, 187361939, 196251284, 201779348, 212254867, 221203030, 229805652, 235333716, 245940869, 254757398, 263360020, 268888084, 277146242, 1073743811, 287883973, 296700566, 305696324, 310700546, 321438277, 1074022402, 330255062, 335973378, 344648217, 354992645, 1074308101, 363939865, 371911251, 378440729, 386591449, 397197847, 405883097, 413854419, 420383961, 428534425, 438755985, 447826073, 454093320, 462326937, 470477401, 481084119, 489769049, 496036424, 504532679, 514253393, 1076150727, 523848344, 529590920, 538356872, 547799123, 557402648, 563522568, 572964883, 582568664, 588311240, 596544601, 606126800, 1073813512, 616122968, 622127819, 630361159, 640082641, 1075401673, 647973530, 655682059, 663915527, 672590540, 681624208, 1074894794, 689916442, 698264779, 706144780, 715571411, 723470938, 731024519, 739699340, 749519511, 757025498, 764734027, 773762123, 781642316, 791462487, 1075170316, 797526549, 809012868, 815579264, 822692565, 834178564, 840360594, 847858325, 859344580, 865526290, 1074671620, 874474203, 882174603, 889621634, 899080786, 1077042187, 908028507, 916368523, 924246738, 933194395, 941009992, 949971483, 958311435, 1075754957, 1077341126, 966175944, 1076572111, 1076847566],
    [118, 104, 6, 2386049, 10809537, 18925568, 27445377, 35834049, 44091520, 52480192, 60999681, 69118480, 77645888, 86272001, 94695489, 102942785, 111061712, 120351441, 128249985, 136227472, 145517137, 153415681, 159828499, 169781840, 179071633, 187486804, 193382995, 204130902, 212371601, 221041172, 228878401, 237816407, 243714707, 254314577, 262957585, 271372948, 279759383, 285657811, 296257745, 304927444, 312764609, 321702551, 329811985, 336261271, 344483904, 355257047, 361400339, 369815767, 378038272, 1073755075, 386845337, 394954835, 403370007, 411592832, 1076904898, 420399833, 428509331, 436924503, 445147328, 453954073, 462063827, 473223254, 479357461, 487508569, 495626393, 504165016, 512912085, 521325210, 529180889, 537719320, 546466453, 1073778629, 555010715, 563268186, 571123801, 579793618, 588409429, 598395542, 605342299, 613599962, 621455385, 632606870, 638896667, 647154202, 655140954, 663548632, 1074586567, 673893078, 680839899, 688695450, 1075909576, 699715798, 707447318, 714123355, 724881430, 731408924, 739027162, 747565650, 756574812, 764454939, 772600408, 781740700, 789620891, 797897234, 807168669, 814786779, 823063186, 1074874315, 832072412, 839690266, 849111645, 857500381, 1074113485, 865888797, 1076484042, 1075186636, 1074425801, 1076797390, 1075767238, 1076312004, 1077369807],
    [102, 88, 13, 2328577, 10428481, 18950336, 27338880, 35727360, 44116032, 52775504, 60760257, 69568592, 78080657, 85925889, 94734864, 103246545, 111091841, 119900880, 128412241, 137035840, 145066640, 153578001, 162201728, 170494547, 176630468, 186992656, 195756224, 204049043, 212158608, 220921856, 229214739, 235350532, 245713104, 253987009, 260768402, 269437524, 279152705, 285934162, 1073748931, 294070916, 302991892, 312707201, 319619797, 327625284, 338905622, 344785557, 355837956, 1075334148, 363932248, 370100948, 380995672, 386597586, 397486616, 406014614, 413764307, 420421782, 1074561989, 431041176, 439568982, 448104600, 453976150, 1073796034, 464595672, 473123542, 481659096, 487530710, 495930004, 506824728, 512557589, 522013335, 529473558, 540387396, 546925146, 554500693, 565553348, 1074858954, 572222169, 580330203, 590719108, 597510679, 605784601, 613884507, 622553689, 630950105, 639050267, 1074359238, 647842519, 656116377, 663421458, 1076474823, 672754330, 681281625, 1077004235, 689382043, 698050713, 706562647, 1074144206, 714697434, 1075996616, 723085850, 1076273103, 731605017, 1075763148, 1075261385, 1076852685],
    [118, 104, 13, 296960, 10301569, 18942017, 27330689, 35719169, 44107969, 52627648, 61016064, 69693136, 77793408, 84445392, 94187521, 102959168, 109382289, 120024656, 127742145, 136358033, 142936785, 153579024, 161296449, 169912529, 176491025, 187133584, 195498000, 203466769, 210176578, 218852884, 229052560, 237283394, 243730946, 252407444, 262867541, 270995664, 279226370, 285674114, 294350420, 304810645, 312938576, 321169538, 327617218, 336293588, 346753749, 355283667, 363112642, 1073745922, 369822359, 380595798, 388696597, 397191319, 405615123, 411765335, 422538902, 430745687, 439169619, 445319703, 456093206, 464300055, 472724115, 478874327, 489647830, 495784466, 506243287, 1074808771, 512035409, 523332821, 529339026, 539011153, 546638344, 556887125, 562595856, 573911048, 580192840, 590441493, 596150416, 607465544, 613747400, 624127122, 629704784, 641020104, 647301768, 657550485, 666185864, 672172115, 1074036744, 682847250, 688162944, 1073793988, 697912856, 705857665, 713888466, 724790482, 730892499, 739054162, 749956178, 756058259, 1074338757, 765397516, 773410456, 780437696, 790563532, 798576344, 806389779, 815353432, 822380608, 832506508, 840075265, 849283660, 856852673, 1075401740, 1075162059, 865241153, 1076486089, 1075717066, 1075998669, 1076802510, 1077077958, 1076301767, 1074755535],
    [126, 112, 9, 2189505, 10577985, 18966657, 27486208, 35875008, 44132353, 53030416, 61040768, 69429312, 77589137, 84371601, 94973520, 103105106, 111143633, 117926097, 128528016, 136405523, 144697937, 151480401, 162082512, 169863697, 176646161, 185274068, 195125907, 204458709, 210439828, 1073744834, 220291667, 229337686, 237365334, 243994132, 252406340, 262488594, 271280662, 279308310, 285937236, 296043154, 304835286, 312862934, 319499863, 329597650, 338676245, 344665623, 353200711, 363842197, 369831575, 378366471, 389007957, 395274953, 403386071, 414149144, 420168217, 428959769, 439052950, 447080598, 453995017, 464849944, 472869592, 1074283459, 479029959, 487547482, 496224778, 504326729, 515181784, 521365594, 531589784, 1073779654, 538012313, 547447507, 554559497, 563047049, 573901976, 580086426, 590309976, 1074842633, 596732505, 607898203, 613376154, 622029530, 632622168, 1074605000, 1076458437, 638675673, 646930650, 655222857, 663972378, 672738972, 680356487, 691784219, 697262106, 706293276, 1076992007, 716950235, 722157785, 731450909, 738934873, 747760139, 756624988, 767281819, 772489369, 781782685, 789922319, 798214858, 806948445, 1075435403, 815088207, 823257227, 832114397, 840254159, 848546378, 1075197199, 857288412, 1077298442, 864774660, 873808015, 881715401, 889940676, 898877578, 1074180044, 906717828, 915531979, 1076812804, 1075782605, 1076062158, 923658377, 932309067],
    [106, 92, 9, 313408, 10834112, 18958337, 27347137, 35735617, 44124289, 52898512, 61165568, 67422400, 75844162, 86452880, 92623441, 103344194, 111626770, 117787138, 128395792, 134566609, 145287170, 151341698, 161950288, 168120977, 178841730, 187124370, 193284802, 201675281, 212396226, 1073741826, 220678738, 227093204, 235358420, 243583104, 254103680, 1073769411, 260647444, 268912660, 277828179, 285526016, 294202004, 302467220, 313714833, 321212480, 328141333, 336415382, 344937107, 355657937, 361695829, 369969750, 378491603, 389212177, 394995862, 403524310, 412045843, 422766673, 428804821, 436685396, 448063617, 456486994, 462105110, 470632470, 481617985, 490041490, 497502930, 504826391, 515172545, 523595794, 532105816, 538381015, 548726785, 557150418, 562636884, 574058584, 1076398023, 582437400, 588712535, 599224344, 1074066372, 607603416, 613099734, 624390360, 1076967368, 1077243849, 629876822, 639070209, 1076728774, 649546392, 655297173, 666333336, 672598679, 681013441, 689401985, 698165849, 706179137, 1074912202, 714943129, 723331801, 1075454923, 731720217, 1075990478, 740223514, 748612186, 1074698181, 757000858, 1075235788, 765389530, 1074470861, 1075800015],
    [106, 92, 11, 2082880, 10356865, 18982976, 27371712, 35760128, 44148864, 52668481, 61057153, 69567120, 77834241, 85969024, 94242817, 103000257, 111782417, 119644866, 128174274, 136579089, 145599058, 153199170, 161622723, 170117186, 179153426, 186753666, 195177091, 203409408, 212708050, 220307970, 228731395, 237225986, 1073745922, 246262418, 254124755, 262285891, 270518464, 1074817027, 279282256, 287557762, 295569473, 304448208, 313641042, 320735425, 329613840, 338806994, 346819224, 355707032, 363700950, 371829457, 380749842, 1076396996, 388237521, 397650456, 405643798, 413772369, 420456967, 431081618, 438569041, 447982168, 455451283, 464104081, 470542868, 480512145, 489925336, 497918550, 504343239, 512486036, 522979352, 530948691, 538298967, 548145240, 556638870, 563464919, 573311192, 579594964, 589668883, 598878874, 605407895, 615656026, 621537876, 632433178, 638962199, 649210586, 655338119, 664259221, 672803545, 680503879, 689424981, 1073799115, 1075644423, 1074362314, 697969241, 706079259, 1077252041, 1074653128, 714746521, 722856667, 731523609, 739633819, 748145365, 1076238285, 756533781, 1075207118, 1075491782, 764799579, 1077069775, 1074209733, 1076064204],
    [110, 96, 13, 2304129, 8761537, 18738369, 27363457, 35751937, 44140609, 52529345, 61453008, 69069953, 77801665, 86880913, 94578689, 102624257, 112046801, 119401537, 126167637, 136572096, 145601041, 151333397, 161737856, 168110741, 179671635, 185174552, 195292160, 201665237, 213226003, 218729176, 229583504, 235400914, 246780627, 252283480, 263137872, 271167632, 279178304, 285837976, 296692240, 304984657, 310898194, 321857744, 327675538, 339055251, 346664976, 354625601, 361229906, 370379270, 380219472, 387000320, 394907289, 403777600, 412324564, 422440474, 428943552, 436850201, 445878804, 454109312, 462016217, 471044692, 481626200, 487821972, 496487637, 504859210, 515180568, 521769686, 530042005, 538151558, 546802314, 557123800, 563712662, 571984981, 580356618, 590678168, 597267030, 606989914, 613648966, 622299850, 629518401, 639306331, 648933082, 1073746954, 655592134, 663072897, 672868887, 682487450, 1075069958, 689801806, 697930262, 706202645, 714812055, 1074037703, 723356302, 730451545, 738570241, 748358171, 1073799113, 756910606, 765143639, 773688014, 781920983, 1075646478, 790301403, 798689947, 1074879432, 1075422146, 1075966915, 1077021643, 1074423749, 1076277199, 1076809676, 1074736068, 1076590541],
    [102, 88, 8, 1697857, 10086529, 18475201, 26863617, 35383424, 43771968, 52160512, 60549312, 69618255, 75861071, 85836304, 94784143, 101026959, 111002192, 120295058, 128051921, 137390804, 144695955, 153849362, 161606225, 1073754112, 170945172, 178503761, 187535061, 195291734, 204499540, 212058321, 218860630, 228715025, 237234902, 246442516, 254001169, 260803798, 270789270, 279333391, 285969558, 295944849, 304212113, 312732182, 321276623, 327912470, 336227031, 346787410, 353266392, 363564754, 370043416, 378777178, 386820760, 396214992, 403942938, 411986520, 421380752, 429108954, 436890135, 447865372, 454274714, 462416458, 470960795, 481419932, 489524821, 495971018, 504777309, 514974428, 523079317, 529680987, 539856405, 546302602, 555108893, 565677265, 572515027, 580274909, 590843025, 596634122, 1076908994, 1074830279, 1075371018, 605178395, 615637596, 1075646405, 624397393, 1074611142, 630606493, 639623763, 649563153, 654994007, 664789523, 1073842120, 673165017, 680676059, 689942105, 1074129859, 696937111, 706719257, 1076497356, 715107993, 721784015, 1074423757, 1076279241, 1077342155, 730172431, 1076828100, 1075274702],
    [106, 92, 13, 354368, 10856641, 17131520, 28027468, 36295309, 42322638, 50686080, 61581836, 69849677, 75877006, 84240576, 95136396, 103404045, 111766221, 120302284, 1073752064, 128569549, 1076391937, 136931341, 145074241, 154260047, 162097293, 170240129, 179425999, 187017217, 195913857, 204591759, 212961421, 221079617, 229757455, 238127117, 246245569, 252432978, 262760525, 271681613, 277596675, 285987538, 296847565, 304965633, 311151171, 319541778, 328313038, 339036755, 344705731, 353225236, 364202643, 370510417, 378522117, 387033230, 397757139, 403819222, 411816594, 420465285, 431311379, 437619345, 445999760, 454396433, 462277204, 471312468, 479685141, 487705238, 495831700, 504351429, 513386646, 521497296, 528861710, 538282705, 546794069, 554813974, 1076930500, 562416206, 571460165, 580495382, 588606032, 596363907, 1076154373, 604883668, 1074856963, 613918932, 622160400, 630835913, 638691406, 647457429, 655477334, 1074091975, 664523287, 672778825, 681158742, 689400533, 698077847, 706333193, 714582036, 723243735, 731499145, 739354638, 1075150857, 748409431, 1073865666, 756525204, 765044950, 1075973066, 1074416650, 1074699211, 1075502091, 1075785670, 1076852680],
    [126, 112, 9, 2395137, 10626049, 18754624, 27143360, 35531776, 43920512, 52440257, 60828801, 69619340, 77605889, 86123585, 94932684, 102771777, 111554126, 119950860, 128066753, 136875148, 145116364, 153232513, 159690321, 170282572, 178521744, 184856081, 1073750016, 1075865601, 195710669, 203687504, 210022033, 220876301, 228853456, 235187921, 245771790, 254430797, 260320916, 271320212, 279481356, 287715022, 296373901, 302264020, 313263316, 321424460, 327691862, 338448015, 344206868, 355206164, 363105473, 371601038, 378162772, 386149460, 397149268, 405048385, 411578070, 422866435, 430966483, 440044558, 445132438, 456420995, 463768705, 472122896, 478686742, 489975491, 498075283, 507153550, 515141187, 523634200, 529837655, 1076400131, 1074844675, 537545876, 548800152, 555003607, 564940367, 574262478, 582354520, 588394073, 598494927, 607816782, 615909080, 1075126212, 1075672002, 622079494, 632049167, 639274645, 649070163, 655502873, 664022726, 672681049, 681217557, 691013139, 697446041, 705965702, 714624153, 722732626, 731164311, 739520070, 748440726, 756287122, 764718615, 1076992006, 773336776, 780815380, 789841426, 798658261, 806891144, 815549526, 823396050, 832212565, 1075441605, 840445512, 849103894, 856829657, 865611272, 874007769, 1076759560, 882650827, 1074689991, 891047126, 899427851, 906644692, 1077314505, 1073923081, 916205131, 924339225, 932982411, 1074202635, 1074489290],
    [114, 100, 7, 1576065, 9964737, 18353153, 26872896, 35261632, 43519041, 53063247, 61368399, 68816000, 77204480, 86259408, 94244498, 103311887, 109554834, 119541393, 128202384, 136318481, 145255055, 153718420, 161746453, 170538518, 178261585, 187198159, 195661396, 1073750017, 203689685, 212088336, 220204753, 229215956, 235300945, 245632661, 254031440, 262541016, 271158804, 277244049, 287575637, 296891541, 305376472, 310798545, 322319897, 329886927, 335964177, 347485849, 355486231, 363441295, 372651609, 380218383, 389302938, 397817561, 405147160, 414428184, 422857434, 1075858370, 430585430, 438701720, 447982744, 456411674, 464139926, 472256088, 481537112, 489966170, 495455877, 506083030, 515263059, 521506001, 529010245, 1074305988, 540161045, 547229266, 557206227, 562539602, 570953413, 582104277, 589172434, 599149075, 604482770, 612896261, 624047189, 1075368965, 631115282, 641092243, 646425618, 1075128259, 657476183, 664637148, 674253527, 681414300, 691030679, 698191452, 706579996, 714623643, 723269277, 731221137, 739789339, 1076188106, 748434973, 1074899911, 756386833, 764955355, 773600861, 781552721, 790121051, 798766813, 807028756, 815417492, 1076481993, 1074661324, 1074165702, 823806036, 1077325771, 832194772, 1076818893, 1077085134, 1073962952],
    [114, 100, 3, 1837056, 8668288, 18672705, 27290688, 35679360, 44067840, 52456640, 60976129, 69364929, 77753409, 84165696, 94111936, 102551184, 111307905, 117720064, 127666240, 136105552, 142896660, 152832128, 161271504, 169886740, 176451156, 187042451, 194825744, 203441236, 210005652, 220596947, 228388033, 236995732, 243560148, 254151187, 261942273, 270550228, 279998165, 285492416, 296094291, 303885441, 313552405, 321842389, 328230609, 338167809, 347106901, 355396693, 363333697, 371738116, 1073749955, 380661397, 388892821, 397339797, 403727889, 414116885, 420505169, 430442689, 437284358, 447613013, 453824018, 464012932, 470838918, 479358536, 489687559, 496002705, 504155858, 512782022, 523242055, 529321618, 539510340, 1075606466, 546336326, 556665045, 562875986, 573064900, 1076928516, 1075894278, 581437569, 588407888, 598739591, 605185040, 615385109, 621962448, 632475274, 638742152, 649071303, 655516816, 1075393543, 666029578, 672672470, 682806858, 689073672, 697838166, 707972810, 714615446, 1077241866, 722914839, 732972632, 740060248, 748169750, 756469335, 766527128, 773614744, 781635223, 791692824, 798780440, 806514376, 815189719, 825247448, 832335064, 1076463624, 1074386893, 1075195851, 1076777934, 1074955205, 1073932233, 1076299724, 1074221007],
    [106, 92, 1, 2223104, 10628225, 18893953, 27282625, 35671041, 44059713, 52579328, 60968064, 69752400, 77745344, 86109248, 94514177, 102911040, 111695568, 119663744, 128068673, 136869586, 144829632, 153234625, 160069139, 170929360, 178646673, 184962563, 195581584, 203812433, 213003267, 218517123, 229135888, 237366993, 246557827, 252071491, 262698514, 270921233, 280112195, 1073755074, 285626051, 296253074, 304606936, 313666755, 1076909059, 319452755, 329772568, 338701328, 344618643, 354938456, 363867280, 369784531, 380104344, 389033040, 396916306, 403303506, 414190609, 422868633, 428469458, 439356561, 446199381, 453635090, 464522321, 471365269, 479325337, 489688273, 498365977, 506998484, 512879641, 1075090376, 1074850756, 523531865, 532164244, 538045529, 1076432839, 548697817, 557330004, 563211481, 572028437, 582495764, 587852946, 597579351, 607792790, 613936858, 622745239, 632958486, 639102554, 1074622410, 647910935, 658124374, 664268442, 672691925, 683290326, 689434138, 698242775, 706088146, 1076731852, 714476562, 1075694533, 722865234, 1074407373, 731795023, 1076249545, 1073914830, 739642514, 1076026315, 748572175, 1075525574, 756960975, 765349519, 1077363727],
    [126, 112, 0, 427072, 10816705, 18918528, 27307200, 35695616, 44084288, 52759617, 61507152, 69258769, 77925505, 86673104, 94424721, 103329492, 111479809, 120227472, 127979089, 137014805, 145272468, 153947217, 162170384, 169922257, 179113169, 185238657, 195481175, 204278929, 210404417, 1073750978, 218672857, 229420570, 235458072, 246459995, 252085376, 262999057, 269004441, 279367383, 288295957, 294290625, 302558809, 313175765, 321695386, 327732888, 338210324, 347147476, 353010689, 361279001, 371895957, 380415578, 388419223, 396930644, 403080384, 414256212, 420130396, 430616149, 436923417, 445023232, 456199188, 461950680, 472952539, 481234069, 489596563, 1075860422, 497470999, 504278557, 514895387, 523177045, 531539539, 1074829253, 539799258, 545836632, 556838555, 565251220, 573744346, 580038344, 587918553, 596553373, 607063253, 615818267, 621981192, 629861529, 639053334, 649241626, 655535688, 663415897, 672607830, 682927323, 689090184, 697355293, 706260684, 713993949, 722939542, 733127834, 1075103752, 739298461, 747548253, 1074344903, 756494038, 766420691, 772852957, 781757964, 791979099, 798821906, 1076973508, 806669404, 815312460, 823987858, 833791066, 839961693, 848866956, 859088027, 865930834, 1074633740, 1075701705, 874319570, 883861011, 1076243402, 1076517835, 890556060, 898280604, 907333148, 915057692, 1075492813, 924110556, 931835100, 1077342147, 1076824015, 1074217934],
    [130, 116, 11, 2536640, 10759297, 18910273, 27298817, 35818496, 44076161, 52595904, 60984448, 69372992, 78130832, 86422528, 94407873, 103213586, 109349906, 119967441, 128462416, 136754304, 145156690, 151293010, 161910353, 170405584, 178697280, 187099794, 193236114, 203853329, 212348432, 221026004, 229042898, 235179218, 245796497, 254840386, 262672019, 271357588, 277408258, 288394242, 294162115, 305042965, 313003731, 319604931, 330337922, 338169363, 347387543, 352905282, 361402009, 372281026, 378310234, 388501075, 1073747970, 394848450, 403475994, 411438097, 422483669, 428664922, 436899353, 445419226, 453381265, 464295444, 470738969, 478842457, 1075339204, 487362202, 495324369, 506771159, 512551130, 520785625, 528878673, 540325399, 546236569, 556018753, 565491287, 571402329, 581184705, 590124628, 596568281, 606350337, 615421525, 1075622854, 621996618, 630623306, 638324246, 648976021, 655551178, 664177866, 671649347, 680267478, 689223195, 697092611, 705203203, 713821846, 722777755, 730646595, 738758275, 747376214, 1076937673, 756725340, 1073808387, 764209178, 772935384, 1074088903, 781497947, 792390301, 798231637, 807056924, 817555997, 823561866, 831786197, 840611548, 851110493, 857116170, 865209944, 1074370508, 874165916, 1075171338, 884665053, 890375704, 898938587, 907208714, 915541656, 1074935758, 1077306312, 923986058, 932449429, 1076013005, 940361859, 949226517, 957147290, 1076285381, 965273730, 1074736079, 1076588491],
    [122, 108, 10, 2540608, 10570753, 18410688, 26799232, 35187712, 43576384, 52880908, 60902465, 69658252, 77679809, 86280847, 94563982, 103083151, 111601356, 119622785, 128223951, 136506958, 145026255, 153701376, 161932876, 170166863, 178450126, 186969167, 195644544, 203867328, 212109839, 220392974, 228912143, 237421696, 245976256, 254454288, 262587392, 271273490, 279620240, 286189265, 296439442, 302575108, 313174608, 319874765, 329993810, 338340560, 345040525, 355159762, 361295492, 369920723, 378621461, 386852497, 395086483, 403787477, 412018193, 422899350, 431130774, 437568719, 445730453, 453570244, 462195283, 470609414, 479511631, 487673429, 495749651, 504164038, 514411584, 521201165, 529067588, 537718406, 546620431, 555183246, 1073745924, 565348950, 573893718, 579661382, 588729876, 596567633, 1074812934, 607291926, 615836694, 622118031, 630680654, 641108631, 647457806, 656074328, 666274519, 1075353541, 672616084, 680584781, 691440151, 699723478, 706397849, 715083480, 724732118, 731049673, 739952153, 748637848, 758549079, 764603913, 773506649, 782192152, 789769801, 798445268, 807061209, 1075102664, 1073816584, 815066635, 823324297, 831999572, 840623320, 848621131, 1076196361, 857173198, 865789080, 873787019, 1077261251, 882566168, 891243608, 898952907, 1077004299, 1074408459, 1076780994, 1075742666, 1074188231, 1074733066, 1076062215],
    [126, 112, 13, 2387136, 10661057, 19199169, 26790912, 35179648, 43568320, 51956800, 61107328, 69381185, 77919361, 85642831, 94661632, 102935553, 111473729, 119721488, 128250881, 136490113, 143027216, 151310018, 161664656, 168228430, 176581776, 184987341, 195219024, 204901964, 210433617, 218524752, 228773584, 235861715, 246721615, 252079312, 260492995, 270192143, 279211072, 285931025, 297053199, 302435907, 312135375, 319450642, 327611918, 338996431, 344379011, 354078351, 361393810, 369555150, 380939407, 389451468, 394983057, 403459608, 412145239, 423005708, 428625560, 439783052, 445052558, 453791448, 462081541, 473345686, 479254039, 487345752, 496563867, 504516249, 515288598, 521729563, 529951823, 537308749, 546895579, 555380309, 562474509, 571133637, 1073752004, 580449883, 588672015, 596029069, 604688005, 613338823, 622515732, 630877909, 641117782, 1076122566, 1074834438, 646630981, 656070356, 666283734, 671772370, 1076682757, 681236052, 689598101, 698125906, 705746583, 714902674, 722889935, 730123842, 739956372, 747785945, 756977178, 764046418, 772470481, 782143194, 790261269, 797898259, 807308890, 814665351, 822398466, 831575767, 840731858, 848718991, 856608327, 1075912648, 1075671048, 864472579, 873614937, 881784403, 891195034, 1076988931, 1074645961, 897896066, 907169305, 915338899, 924617746, 1074402306, 1075210242, 932105735, 1076528135, 1074185162, 1073945547, 1075541003],
    [110, 96, 13, 2600064, 10562560, 18951296, 27339968, 35728448, 44248257, 52636737, 61286096, 69414017, 78359760, 86191105, 94588561, 103228944, 111914000, 119754321, 128394832, 137080464, 144920081, 153552403, 162245712, 170086097, 178726032, 187149376, 193408596, 201804884, 212805333, 220703936, 229582421, 237480960, 246359573, 254774998, 1073750980, 262604499, 271552022, 277564951, 286075927, 296158867, 305106518, 1075867589, 311250648, 319761624, 330245781, 338661014, 1076663234, 347033305, 353316440, 363922434, 1074842563, 370380434, 380587545, 386870808, 397477058, 403934930, 414142105, 420294295, 431031362, 437489234, 447696473, 453848663, 463930963, 471043602, 478891159, 487534232, 498140290, 504991323, 512446167, 520957143, 531957342, 538676890, 546131096, 557123102, 563711707, 1074335686, 571296792, 582289118, 589008474, 597388956, 607454878, 614043163, 621227668, 629623956, 639305437, 647728858, 656109276, 664743438, 672859741, 681283098, 1074618312, 688606295, 698297998, 706414237, 714706587, 721890836, 730287124, 740240974, 748357149, 756772380, 765406926, 1075688396, 1077008398, 772222676, 780618964, 1075456973, 1076511687, 789400664, 1073911754, 798715484, 1075234761, 1074210763, 1076328399],
    [122, 108, 9, 2165953, 10554433, 18943105, 27331585, 35851392, 44240064, 52866576, 61158416, 69560336, 77794368, 86182912, 95111891, 103198416, 111744657, 119975568, 128280720, 136910353, 143068802, 153529936, 161835088, 170464849, 176754262, 185011906, 195759831, 204770321, 212408017, 221071446, 227085846, 237702743, 245707920, 254717058, 263014422, 269029078, 279645719, 287650896, 297045137, 304957654, 310972054, 321588887, 329992723, 338900119, 347376721, 355158675, 363148496, 372157634, 377949698, 388713043, 397620439, 405711874, 414387928, 419892802, 431174743, 439266370, 447563926, 1073741826, 456330776, 464729111, 472213712, 481594577, 489885336, 498166357, 507057235, 512790226, 523439704, 1073767364, 529338057, 540611603, 546344466, 555174104, 1075879877, 562892361, 573663765, 582554835, 588287570, 596446857, 607218389, 616109203, 621842066, 630001161, 641537556, 647671444, 655837208, 1075633095, 1075381257, 663817739, 674327189, 683480788, 689745625, 1074089926, 697372235, 706391636, 717034580, 722946136, 730926731, 742200468, 748334292, 756500632, 764481227, 773657621, 782020121, 791898180, 1074631691, 798823637, 807186073, 817064068, 823989397, 832351833, 842229956, 849155157, 857386004, 867395588, 875915289, 884303961, 1075172303, 1074933708, 892692633, 1076775875, 901081305, 1074441160, 1076557773, 1077359566, 1077110730],
    [114, 100, 13, 2092160, 10831041, 18967616, 27356288, 35744768, 44133568, 52653121, 61041857, 69430273, 77589504, 86328449, 94596225, 101051920, 111494145, 117829200, 128271425, 136791056, 142995152, 151383696, 161957008, 168390354, 179007059, 186641600, 195511376, 201944722, 212561555, 220195904, 229065936, 235499090, 246115859, 254406225, 263013523, 1073755074, 269053458, 279775765, 288059091, 294480917, 305088017, 313126545, 321850070, 328035989, 338291729, 346899667, 355272853, 361590357, 372196497, 380235473, 388827221, 395144917, 403435156, 414008339, 422381781, 428601044, 439305425, 447678998, 455951443, 462286551, 472844950, 481248337, 487452183, 1076915140, 498010710, 506815570, 513134105, 1076400071, 1074589640, 523700937, 531981330, 537783895, 548866633, 555314698, 562818644, 573924498, 582421001, 588869194, 596373012, 607478994, 614017049, 622423690, 632767560, 638963417, 647571673, 655978186, 666321928, 672517721, 1076693002, 683084425, 689794573, 699876552, 705556119, 1074357257, 715091470, 723069593, 731737805, 741819528, 748014745, 757034574, 765012057, 773680717, 782200462, 790571544, 798846605, 1076201413, 1074124813, 807366350, 815737560, 1075452942, 1075733452, 824126040, 1076008907, 832514712, 1075233731, 1073943494, 1075017679],
    [106, 92, 2, 2436288, 10415169, 18961601, 27184784, 35990592, 44127297, 52350672, 60904449, 67440338, 75845332, 86978259, 94293584, 102847617, 109399636, 119764052, 128921171, 136236560, 142954132, 153318548, 162475539, 169798657, 178877955, 187641491, 194964673, 201674260, 212694533, 220130433, 226823762, 237860485, 246476305, 251989650, 263026245, 271642257, 277155346, 1073754052, 288192197, 296037504, 305196753, 1076649989, 1075879811, 310988375, 321483971, 329591808, 338751057, 344542871, 353324552, 364309655, 371815555, 378744534, 386485783, 395267656, 406252567, 413758531, 420687446, 1075636166, 428429015, 437210824, 448195799, 455308308, 462630550, 470765192, 481750103, 488862932, 496184854, 1076167688, 504321104, 514772096, 521080533, 529617920, 539937984, 547040792, 556715008, 563172480, 571412117, 579818640, 590269504, 597372568, 605892121, 613372944, 621989077, 1074099138, 630150352, 638766613, 646909525, 656223961, 663835840, 672320597, 1076986828, 681389657, 689001536, 697486485, 705629205, 714533906, 1073860551, 722922578, 731590360, 1074670538, 739699858, 748367448, 1076515790, 1074960335, 756887193, 764865746, 1075239883, 1075525577, 1077365709],
    [126, 112, 12, 1838144, 10595329, 18984065, 27372737, 35761217, 44281024, 52669568, 61058112, 69340752, 77835264, 86232657, 92646481, 102895120, 111283856, 120049347, 128689668, 134851588, 144838352, 151760532, 159894676, 170632772, 176794692, 186387456, 193834645, 202092116, 210226260, 220964484, 227126404, 236719296, 244166165, 252423892, 262655555, 271296196, 277196497, 285846724, 296488530, 1073750339, 1075857412, 303017686, 311143956, 319278292, 327528081, 337382528, 347186757, 352832532, 361082385, 371986130, 380741317, 388222097, 397151890, 405907077, 413650051, 422317586, 431072773, 438815747, 447614017, 1074308101, 453881429, 465020487, 472108241, 481168577, 487435989, 498706072, 505662481, 513126025, 523644041, 532391514, 537915031, 546680521, 557198537, 565814808, 571469527, 580234825, 590752841, 1076151238, 599500442, 605023831, 613789193, 624307209, 1073813513, 632792583, 638578199, 648940673, 655339094, 666347143, 672779349, 682494977, 688893590, 699901639, 706195150, 714722325, 1075407879, 722472665, 1076734923, 730836502, 741975640, 748138126, 756665557, 764415641, 1076484040, 775661082, 781692494, 790219925, 797970009, 809215706, 815246862, 823906003, 831524377, 1075186702, 842639064, 849071699, 1074689997, 859014683, 865979414, 1077315532, 875792027, 882756694, 1074189258, 892569179, 899534038, 909346523, 916311190, 924569107, 932957843, 1074995151, 1075803074],
    [114, 100, 11, 373825, 10587201, 18975937, 27364481, 35752961, 44157456, 50705537, 59059858, 69323344, 78362321, 84225746, 94736085, 103402198, 109546710, 120305169, 128421507, 136908372, 145067541, 153733782, 159878294, 170767381, 178622101, 187288150, 193432662, 204321941, 212176469, 220842518, 226987030, 237876309, 245885655, 252032193, 260386322, 271051415, 279819477, 1073742788, 286101209, 293940818, 304605719, 310752257, 1073761221, 322121416, 329771607, 338409105, 1074308034, 347287048, 355977347, 363574865, 372452936, 379701968, 389649408, 395152921, 406007432, 413256336, 423204032, 1075900424, 428707481, 439946393, 448383512, 456758336, 462261849, 473763401, 481938072, 1076961222, 490312832, 498929161, 507103960, 512726032, 522686019, 532483785, 540526659, 546280592, 556240579, 566038153, 574081219, 580097691, 1075667977, 1076204490, 589794819, 598281876, 607635459, 613651995, 1074911235, 624495833, 632932952, 638555216, 649661529, 657451539, 663983707, 673779220, 682617491, 1075449799, 689149659, 699993113, 707783379, 714052816, 724111060, 732949075, 1074677707, 740232732, 748538394, 757042895, 765398684, 773704346, 1074179020, 782208591, 790564444, 798870234, 1076557773, 807374351, 815730396, 824035930, 832540303, 1077351439, 1075277774],
    [86, 72, 4, 2598913, 10863617, 19156033, 26864704, 35253376, 43641856, 52030656, 61326991, 69487617, 78096577, 86492751, 94873665, 103042177, 111658511, 120039553, 128208065, 134720081, 145386577, 153601743, 1073754112, 160017106, 170247297, 179203795, 185436371, 195552788, 203801793, 212568789, 220578881, 229345813, 1076911042, 235695830, 246269584, 254511765, 263089747, 271435472, 279677525, 286027286, 296978947, 304989712, 1075348355, 311447127, 322144323, 330155600, 338325137, 347310275, 355364499, 364087427, 372141587, 380102292, 387295832, 397045457, 405268180, 412461720, 422211089, 430433876, 437627416, 445664919, 454404824, 464408089, 470263825, 479219223, 487041233, 497962585, 1073793991, 503949906, 1074335689, 514739865, 520980627, 1074618309, 531517145, 537757779, 546328279, 554534931, 1075681228, 562851478, 1075178443, 1076508616, 570927249, 579628630, 1077306308, 1076015050, 587836050, 596224530, 1076815814, 1076299726, 1074222029],
    [110, 96, 11, 2468992, 10605633, 19229889, 27249792, 35638464, 44026880, 52415552, 60935169, 69323969, 77712513, 86355136, 94727169, 102880449, 111266881, 118066704, 128177868, 136670337, 143232592, 153343564, 161836097, 168152578, 176787088, 187124812, 195155073, 1073752064, 201707074, 1076391937, 210341584, 220679820, 228840588, 235261634, 245845516, 254006284, 262515712, 268816002, 279399628, 287681600, 295818241, 1076924418, 303148750, 313347789, 321255107, 328314382, 338513549, 347067988, 355454036, 361868878, 372067853, 380622484, 389008532, 395423374, 405622349, 414176788, 422562836, 431197250, 439439061, 447731412, 456117460, 464751618, 472993365, 1074848195, 480637955, 487312964, 498306242, 506547733, 514192515, 520867524, 531860610, 540102293, 547746883, 554421764, 563432979, 574074511, 579849863, 588500616, 596987475, 607628815, 613404359, 622054920, 630541971, 641183439, 646958663, 655609416, 664096467, 674737743, 680513031, 689163976, 697937425, 706432530, 1075904519, 1073824776, 713805444, 723103377, 731598546, 1074105285, 1074383877, 1074664452, 739880529, 748375634, 756764306, 765308566, 773435089, 1075210182, 782085718, 1076272075, 1075502091, 1075787722, 790474262, 1077374921, 798863062],
    [102, 88, 9, 2510976, 10653889, 18755648, 27144320, 35532800, 43921600, 52842688, 60985409, 69208589, 78008384, 86413836, 94374605, 103174144, 111316993, 119540301, 128357004, 134640273, 1073750016, 1075865601, 144706189, 153260161, 159805969, 170273488, 178688588, 184971857, 195439248, 203854540, 210137809, 220605008, 229281805, 238310030, 245770768, 254709840, 263475918, 271190547, 280007298, 288641614, 296356563, 305173058, 313553476, 321522259, 327955141, 338595984, 347361806, 355076755, 361640518, 371888205, 380662468, 388665485, 397439492, 403452549, 414225090, 420377167, 430608589, 439382660, 1076400132, 1074844676, 448015062, 453784133, 1075129410, 464531670, 472944642, 479490706, 1076711363, 489957974, 495858182, 506474582, 514756816, 521040527, 531900950, 537801350, 548417558, 556699664, 563376850, 573844118, 579744454, 590360726, 597594836, 605319762, 613954056, 1074628614, 621556229, 631149076, 638874130, 647508552, 1074387973, 656314964, 663646735, 672674440, 681480852, 688812751, 697840328, 1075714056, 706499221, 1075463113, 1073906697, 1074198474, 714887893, 723276309, 731664981, 1077359559, 1077110731],
    [98, 84, 11, 2601025, 9965633, 18354369, 26742785, 35131521, 43651072, 52039808, 61094479, 68817088, 78098561, 85594176, 94649039, 103264449, 112088592, 119814671, 128430081, 137254608, 144980623, 154120335, 1073750017, 162420368, 170267218, 178927698, 187929105, 195974736, 204451919, 212760275, 220731924, 228987410, 238523093, 245897940, 252204753, 262542034, 272077333, 279452308, 286291605, 296096402, 305369297, 313145362, 322074308, 327553733, 336073302, 347312721, 355350614, 364017220, 369496581, 381128853, 1075866562, 388504148, 394810385, 403182294, 414167247, 422459606, 431126148, 436736534, 447976081, 456013846, 464680452, 470160005, 481275919, 1076402180, 489306258, 495998679, 503845526, 515347029, 523122838, 529028241, 537268805, 1075377091, 546680850, 1076954117, 556415186, 563115029, 571846738, 581858835, 588624018, 598636115, 605401298, 615413395, 622563928, 630216215, 1074096073, 639341208, 1076200391, 646468689, 656118296, 1073862598, 663778389, 672895704, 1075197896, 680547991, 688944341, 1077302220, 1074958283, 1074716621, 697325143, 1075776458, 1074491342],
    [114, 100, 5, 2517120, 10514625, 18903041, 27291713, 35680385, 44200000, 52588544, 61403664, 69365952, 78014464, 86143104, 94779027, 103313555, 111735376, 119957568, 128333523, 136868051, 145289936, 153512128, 161887827, 170422355, 178844304, 184838673, 195442195, 203976723, 210162262, 218393169, 229652056, 235434072, 246084114, 251947665, 263468631, 271381012, 277113553, 288896708, 294154968, 302436886, 313412245, 321926360, 327709336, 338490068, 346966741, 1073750979, 355480728, 361263640, 369545878, 380521045, 389035032, 397210196, 403466448, 414725700, 419877590, 428894938, 439891588, 447410834, 456018453, 1075859524, 465056772, 472707732, 479226522, 487223942, 495326939, 506131154, 512518160, 520778246, 528881307, 539685458, 546072656, 554332870, 562435611, 1074837445, 571535964, 579889690, 587887174, 595990107, 605057609, 613871763, 621832794, 1077200902, 1074344898, 632567319, 638611977, 647426131, 655124624, 666121879, 672166601, 680587932, 691287767, 697332361, 706146515, 1076972553, 716052121, 722530844, 1074627530, 732829209, 740225758, 1073858503, 749606489, 757002846, 1074143179, 766383833, 772862684, 781588125, 790032403, 1075731400, 798365213, 1075489740, 807334430, 815142493, 824111774, 1076553677, 831919837, 1076309966, 1076844495],
    [126, 112, 13, 1962113, 10506240, 18895040, 27283520, 35672192, 44191937, 52580353, 60822224, 69357697, 77459457, 86134849, 92558034, 102765136, 111538769, 120224404, 127931024, 136704529, 145390292, 153096720, 161870545, 170555988, 178926274, 186511425, 193352341, 204110356, 212480514, 220065985, 226906709, 235426518, 246035074, 254145169, 260461077, 1073754242, 268972246, 280481858, 285627093, 294146646, 302526550, 314036226, 1076913091, 321531970, 330813634, 336089750, 344469654, 355979394, 1075882948, 361255446, 369635350, 380629077, 389438167, 394940631, 405680338, 414183445, 422992535, 428494999, 439743059, 448158231, 453660695, 464400978, 470044754, 481686227, 487477913, 498489943, 503992407, 514732562, 520376338, 532017683, 540695046, 548287122, 554717767, 562319506, 571757083, 582479875, 588141273, 599546588, 605302811, 613700315, 623898837, 632969862, 638988441, 647385738, 657977475, 1076413381, 666524358, 672412315, 680546951, 689197211, 699396245, 705581593, 717249178, 722874393, 731271882, 739529307, 750252227, 758798918, 764817625, 773214794, 1073818630, 783676051, 789467737, 1076709320, 800872988, 806760537, 815157770, 825749571, 1074106313, 834427484, 1074648074, 840183899, 848318983, 857076376, 868244058, 873738459, 881873607, 890630744, 901536412, 1075187719, 907407896, 1074948043, 918575642, 924185304, 935353050, 1076273101, 1075764174, 1075514316, 1074493391],
    [114, 100, 0, 428032, 10293376, 18681920, 25593984, 33870545, 44347601, 52236480, 60984002, 67424849, 77901905, 85790720, 94538370, 101118483, 111751233, 119704066, 126145041, 136622097, 145437200, 153258562, 1073752066, 159838867, 168200256, 178860225, 187748948, 195342993, 201754816, 212414593, 218419345, 229323344, 237800068, 243724883, 254489296, 262965956, 269267653, 277279443, 288043664, 296650949, 302953174, 313578004, 321466369, 330336470, 1076381635, 338744020, 344920597, 355240516, 361542149, 372298388, 378483287, 388794884, 1074049028, 397865091, 403747464, 412267081, 420426391, 430868485, 437170774, 448196675, 454078984, 462598665, 470749781, 481331286, 487371333, 498528451, 504541897, 512692885, 523143237, 529445398, 540471299, 546484873, 556828694, 1076939785, 562868869, 574157325, 579801813, 590252165, 1074600965, 596554390, 607711821, 615549078, 624489165, 630141655, 638879824, 1075668938, 649654925, 655307287, 664045712, 1076210701, 672977496, 680571464, 689746639, 697731265, 706531992, 714126024, 723300879, 731154448, 1076754380, 1077286920, 740086488, 748466767, 756451393, 765252120, 773632655, 781617153, 1075464207, 790549202, 798394497, 1074435019, 807326226, 815040720, 1074976710, 824103506, 1075258318, 832492178, 1076052935],
    [98, 84, 10, 2553024, 10227777, 19175617, 27299841, 35688513, 44077249, 52465793, 61273088, 69507073, 77336577, 86438976, 94672961, 102502529, 111998609, 119812160, 128227457, 137164497, 145406674, 152834241, 162330193, 170143744, 178960978, 187495953, 195309760, 204126738, 212086912, 220656768, 229423827, 238089813, 246069906, 254554704, 262803990, 271751682, 280294979, 288683523, 296532499, 304886480, 313849475, 321698451, 330052112, 338301526, 347403971, 355252819, 1073753091, 362083991, 372415106, 380383888, 387224152, 395638295, 405410454, 414750808, 420778520, 429192791, 439916568, 447484115, 454595225, 462747351, 473086105, 481038419, 489855554, 497815571, 504664728, 515414168, 522981523, 1076643785, 529830616, 1074042822, 540580056, 546443924, 555258393, 1075114951, 565360665, 571609684, 580424281, 590526553, 596775636, 605590233, 615692505, 621941268, 632354517, 640291542, 649131541, 1076958152, 657520277, 1074880460, 666016450, 1075676110, 1073865730, 673109594, 1076236234, 1074689999, 1077322701, 681498266, 1076022212, 689886746, 1074469829, 1075538891, 698275546],
    [114, 100, 10, 2158592, 10547264, 18936000, 27324544, 35844225, 44232897, 52742672, 61296656, 69907472, 77787201, 86175745, 94685776, 103239760, 111851216, 120239760, 128405712, 136891090, 142930626, 153793616, 161960080, 170445458, 176484930, 185160211, 195611218, 204650070, 210326227, 220776978, 226816514, 238065219, 243880531, 254068880, 263370262, 269046419, 280020994, 285799000, 296924822, 304400592, 313479256, 319091330, 330479318, 338741378, 347165204, 1073747970, 355505667, 363907138, 372593286, 380671619, 389073090, 397759174, 403239448, 414758615, 423029393, 430919704, 436794072, 447780547, 456583761, 464867846, 1075339398, 1075885059, 470348440, 481867287, 490138129, 498028696, 507033175, 515304145, 523587654, 532199063, 538495705, 548360408, 1077203909, 555136597, 563278346, 572049945, 582046420, 588575305, 1074857927, 597079701, 605221578, 613993113, 623989396, 630518409, 1074086852, 1073846216, 639022613, 647164490, 655936089, 665932372, 672461321, 680965845, 689107594, 698052633, 706406487, 714404553, 1075169289, 1074400266, 723301914, 731607193, 739961047, 748467930, 756773081, 765126679, 773648974, 782022298, 790327385, 798681239, 1074688971, 807203470, 815576666, 1077061580, 823980750, 832369166, 1076288526, 1075785677, 1076849615],
    [110, 96, 9, 2553857, 10539008, 18927808, 27316352, 35704896, 44462608, 52885633, 61256337, 69628624, 78051521, 86422097, 94818836, 103182992, 111605825, 119976465, 128373332, 136737360, 145545232, 153531089, 161927892, 170685139, 179099792, 187093652, 196235779, 204265680, 212628051, 221042768, 227062293, 235458581, 246567555, 254859858, 260747798, 269144086, 279736979, 288553091, 296661637, 304902675, 313841684, 319476438, 330216133, 338842179, 1073746882, 347273283, 355381765, 364008131, 372439235, 1074812931, 378196566, 388936261, 395072151, 406116500, 1075359749, 412398233, 420401305, 428626455, 439409298, 445174421, 454087322, 462074070, 470733401, 478958295, 490002644, 495637142, 504418842, 512405590, 521065177, 529289815, 1076945860, 540072658, 545837781, 554750682, 563654874, 571396633, 580022939, 590665812, 596169301, 605082202, 613986394, 622228056, 632485891, 638890009, 647131739, 657512978, 663269461, 672297691, 681368092, 689483802, 697463323, 706533980, 713601173, 722891480, 731699932, 1075906505, 1074086858, 739815578, 748057240, 756865692, 1073848262, 764719193, 773222936, 781496537, 1075702727, 789098709, 1076498380, 797618326, 1074687944, 1076795342, 1075235787, 1074477005, 1077372879],
    [142, 128, 9, 2426880, 10842304, 19239105, 26816705, 35205121, 43593793, 51982465, 60502016, 68890816, 77279360, 86339584, 94701760, 103256780, 110833728, 119747214, 128667790, 136644736, 145199628, 153432721, 161690190, 170610766, 178587712, 187142732, 195375697, 203633358, 210055746, 220942542, 229085836, 237709378, 245707281, 253964814, 260387458, 271273998, 279652482, 287674369, 296039121, 302330562, 312832064, 321595586, 329617473, 335884802, 346386560, 355149826, 363171969, 1073745922, 369570371, 378245651, 386730573, 397234770, 403124739, 411930830, 420285069, 430789266, 436810436, 447689239, 454101015, 462394070, 472732370, 478622403, 489763545, 496175631, 504468053, 515330648, 520696324, 529634005, 537733337, 548229650, 554119811, 563188373, 574050968, 580200529, 1074820099, 587805252, 596455943, 607203993, 613495302, 621619353, 632771288, 638554710, 646525572, 657404503, 663827078, 671847123, 683102744, 689252497, 1077189636, 699478553, 706171476, 714183189, 722274829, 730673735, 741290647, 748139163, 756091031, 764891860, 772616839, 781693467, 790057620, 798304273, 1075630021, 1074604037, 806195342, 815223316, 822938317, 831337159, 841954007, 848007763, 857305744, 865142999, 1076447239, 1074375687, 873173651, 882471440, 890440271, 1076742089, 1074143241, 898708166, 909193817, 916026064, 923635726, 932383439, 940651078, 949465691, 957163609, 966742682, 1075991558, 1075223496, 974194775, 983519770, 990876182, 999133262, 1008685658, 1016408273, 1075508170, 1024963291, 1032661017, 1042240218, 1050243664, 1058212495, 1066373782, 1077085131, 1073964043],
    [126, 112, 13, 1799169, 10530945, 18419776, 26808512, 35196928, 43585664, 52771532, 60862465, 68908097, 77533903, 86325836, 94442126, 102855822, 111194177, 119476879, 128793104, 136385038, 144748737, 153441296, 161551054, 170736336, 178353166, 187216589, 195105358, 204290704, 212382285, 220550288, 229184084, 237845072, 245936781, 254104656, 262869525, 270875276, 279491085, 287659216, 296293076, 304429580, 312414799, 320959694, 327979730, 1073752002, 338236052, 347019791, 354357263, 363820180, 369922706, 380310101, 388962511, 397374548, 403477074, 413864661, 422516815, 428773911, 439317716, 445321797, 456071311, 464196245, 473265301, 479236761, 489230868, 498146003, 506426388, 512791065, 523311699, 1076120515, 531985493, 538350296, 545985029, 556866195, 563155527, 572617806, 580293272, 587928261, 598809107, 605098631, 1074304964, 1075111940, 614109722, 624260309, 629871237, 638925006, 647664218, 657814549, 1076429829, 664476369, 672830170, 681276545, 689256526, 697995930, 706442433, 714412617, 722811022, 731076246, 739283545, 747966985, 756890203, 1074086854, 764630742, 772838105, 781259463, 789910217, 798693969, 806573654, 814650007, 823202311, 832387611, 840128022, 848728664, 1073844231, 1074913226, 1075719175, 1076785162, 857553563, 1077060552, 865505816, 873796233, 882580113, 890016274, 1076022281, 899496667, 906924759, 915748878, 923701847, 1074731979, 1075541003, 932911633],
    [126, 112, 5, 2347136, 10579969, 18968705, 27357377, 35745857, 44265536, 52654272, 61042688, 69455872, 77820032, 84219602, 94980817, 101019858, 111636689, 119787712, 128923155, 136923793, 142963218, 153579665, 161730624, 171120194, 178866769, 187134033, 193426069, 204460688, 212809427, 220809745, 229077009, 235369045, 246403664, 255006338, 260534997, 271569616, 277574148, 288306835, 294089237, 305123856, 1073754690, 311128772, 322114562, 327512722, 336187411, 344945350, 353071684, 363804243, 370242119, 378130515, 386626180, 397612226, 403786326, 411398738, 420073683, 1076905988, 428151954, 437340822, 445739655, 453628051, 461706258, 471157272, 479294151, 487322260, 1074299845, 495260754, 504449750, 512848391, 521130649, 1073798151, 529732804, 538003990, 546427546, 555037703, 563694171, 571208276, 580195461, 588860123, 596628185, 605492373, 614156892, 621925082, 630527173, 639191579, 647328331, 655348249, 663950468, 672877276, 680882891, 688902745, 697766933, 706038488, 714437259, 722203156, 1075647432, 730821126, 739710165, 747981464, 756380171, 764539543, 1074878475, 772764230, 781390916, 789924440, 798085722, 806318726, 815076357, 823872028, 831640090, 1075416070, 1074644940, 840250439, 848906907, 856814295, 865408069, 874203804, 881979991, 890704981, 898757143, 1074146249, 907219972, 915141332, 924136583, 1076520910, 1076277199, 932525255, 1076819907, 1077355466, 1076058061],
    [106, 92, 3, 2551873, 8747137, 18960384, 27349056, 35737792, 44126336, 52507152, 59078721, 69660801, 78205650, 86061776, 92887761, 103215105, 111759890, 119616144, 126442129, 136769729, 144781904, 153801364, 159996433, 170578516, 176773713, 185012821, 193679445, 204132884, 210073601, 218567189, 227233813, 237687508, 243628225, 252252886, 260788949, 271143506, 279900224, 286226560, 1073744835, 294064341, 303125079, 313086610, 319780864, 330232000, 336138774, 347009024, 353335360, 361173653, 369840277, 380563584, 386889920, 1074283461, 1073783750, 1075899330, 394859094, 405860358, 414407187, 420024982, 431026310, 439573075, 448205402, 456192198, 464739027, 1076434888, 473371290, 481357894, 489904787, 498536986, 504451735, 515201234, 521326675, 532091610, 538006231, 548755602, 554881171, 563294811, 572084315, 582309970, 588435475, 596849179, 605638683, 613503511, 624252946, 630378707, 638792411, 647581915, 655938201, 664500888, 672608407, 681104089, 689666584, 697774295, 706302619, 714658393, 723221208, 1075139530, 731066523, 739824153, 748386904, 756494423, 1074890695, 764882967, 1074131915, 1077030861, 1076779983, 1075492804, 1077338060, 1075783630, 1076318153],
    [114, 100, 12, 2216064, 10358785, 18985025, 27373697, 35762177, 44150977, 52670464, 61059264, 69447744, 77713600, 85856449, 94613632, 102879232, 111022209, 120031955, 128045120, 136187969, 145730070, 153997909, 162009617, 170896086, 179163861, 187175569, 196061846, 203952849, 212595216, 221227606, 229503703, 237507153, 246254296, 252326610, 262926928, 271419928, 277492242, 288092880, 296192659, 305001111, 311038168, 321751640, 327807507, 336335443, 346523731, 355324437, 361378450, 1073753027, 372083352, 378138707, 386535576, 397912604, 405664343, 411710034, 422021139, 428847817, 439210645, 445255768, 1076388802, 456632988, 462402057, 470552595, 481030800, 490187484, 495956553, 506327575, 512495763, 523741788, 529511049, 537661651, 545910995, 1075874825, 1074582472, 555461211, 562688147, 571084824, 580487828, 588763154, 597307933, 606054937, 613929106, 622473949, 630958747, 639480397, 647483602, 656028317, 1074858955, 664775321, 673034893, 681037906, 689582685, 1074360266, 1076725701, 698331854, 706317012, 714977805, 723374810, 1074128836, 1076238284, 731886094, 740272729, 748532429, 756929050, 1075206157, 765440654, 773425748, 782095002, 790606414, 798993113, 807260762, 1075485710, 1075758022, 815507995, 823757332, 1073952711, 832285403, 1077375951],
    [114, 100, 6, 2044096, 8755265, 18740353, 27365377, 35754113, 44142785, 52531265, 61051072, 69439552, 77828096, 85930112, 92781136, 102626305, 111382656, 117772883, 126335504, 136180929, 145592853, 151360212, 159715987, 168278736, 178123841, 187536085, 193434262, 201659091, 210221712, 220845714, 229479061, 235377366, 245610710, 253883392, 260379155, 271422037, 277320214, 287553558, 295826496, 304033856, 312719510, 320811008, 329897554, 338278612, 347017745, 355063506, 361076737, 372445377, 380229138, 386241172, 396998804, 404878528, 414396565, 419926614, 430159958, 438432896, 447950869, 453351553, 464720001, 472380437, 481923608, 486904340, 497661972, 506401361, 514323605, 520458836, 531216468, 539751448, 548605953, 1073749957, 557421208, 565121681, 570792129, 581432405, 590975704, 597007057, 606598357, 615723221, 624530008, 630560913, 640414872, 649277525, 655856138, 665696776, 674173137, 682357976, 689410634, 699871301, 706058257, 715912280, 1075595207, 722965130, 732805704, 741544001, 1074048964, 748131018, 757971592, 766980101, 1076674570, 774748872, 783757445, 1073817608, 792146117, 798333009, 806818519, 815206935, 1076454338, 823595671, 1075951558, 1077269454, 1074934729, 831984215, 1077045187, 1076267980, 1074452431, 1075253195, 1074748365],
    [118, 104, 10, 2470912, 10768384, 18477057, 26865729, 35254465, 43643009, 52162688, 60551360, 68939776, 78139919, 86619151, 94105664, 102757008, 111694415, 120174223, 128436882, 136442002, 144700112, 151491792, 162025615, 169865744, 176657552, 186929344, 195938901, 203420240, 1073754112, 212448335, 220746447, 229493461, 235270742, 243766352, 254038080, 263047829, 268825302, 279203968, 287945935, 296602133, 305549912, 310875152, 322327256, 330413588, 336194074, 344453636, 355881624, 363968148, 372623963, 378008132, 389435928, 397522644, 406178331, 411562692, 422688340, 431771734, 439732955, 445117060, 456937686, 463844480, 1076910018, 473287323, 1075087364, 478540310, 490491926, 497398848, 503966298, 515273233, 522564800, 532050641, 540391059, 545909402, 554037910, 1074329541, 565989526, 573945363, 579463898, 590770833, 599111251, 606587602, 614592722, 624325201, 632665811, 638957271, 647524560, 1077224387, 656919122, 664924242, 673027676, 681078928, 1075933127, 690473490, 698478610, 1076728777, 705688075, 714454551, 723284633, 1074913222, 731630109, 739242635, 748525276, 756576272, 765184669, 772797131, 782079644, 790393433, 798739165, 806351435, 815633948, 823947993, 1075708874, 1073895435, 1075488712, 832293469, 840283735, 849113625, 857061015, 865628240, 1076285388, 1074726861, 1074228174],
    [130, 116, 11, 2314432, 10858625, 18862273, 27250689, 35639361, 44028033, 52646016, 61583884, 69718670, 77811776, 86749900, 94370447, 103272974, 111366144, 120304268, 128055889, 137065042, 145470028, 1073752064, 153221777, 1076391937, 162230802, 170242113, 178518739, 187396818, 195408065, 203684371, 212324942, 221212750, 228962305, 236976719, 243651092, 254268110, 263442965, 269201428, 280064021, 287308303, 293982868, 302502614, 311144596, 321614482, 329251535, 335925844, 347329109, 355692758, 361476180, 371325649, 380883669, 389132813, 397504725, 403034836, 412080784, 419943062, 431190166, 436973780, 446822929, 453890564, 464630413, 473002069, 481810436, 489796301, 498036878, 1076921283, 505674323, 512610884, 523350605, 531591374, 538170072, 548919364, 555078234, 562549334, 573796438, 580104337, 589560467, 597021402, 605270097, 615477262, 624163417, 630575642, 640930453, 647606362, 657551509, 663999000, 1073800130, 674495193, 679989782, 691236886, 698069016, 705942168, 716438041, 722326212, 731099153, 740119127, 747885144, 758634692, 764269188, 773566552, 782070299, 1075909636, 792189060, 798601434, 807228055, 817101465, 823775814, 832155674, 840790747, 848288336, 857330182, 865456794, 873705681, 882725399, 890231504, 899273414, 907653274, 916288091, 923785744, 932827782, 941338840, 949834455, 1075135494, 1074107335, 958115992, 966619803, 1074915272, 1076246473, 1077300165, 1074433029, 1074715594, 1075518474, 1075802059],
    [126, 112, 12, 2397376, 10368193, 18756609, 27145281, 35533953, 44053696, 52442176, 61232780, 69219456, 78157324, 85996544, 92550798, 103569101, 111711372, 117716494, 128734797, 136877644, 142882382, 153900557, 162043596, 1073750016, 168038031, 1075865601, 176436942, 187455117, 195335168, 201592527, 212497614, 220501056, 226758223, 237909649, 246051854, 254055552, 263466129, 268842515, 279852753, 287995022, 294556673, 305409233, 310785619, 321795601, 329937998, 336499777, 347352081, 352728723, 363738705, 371610700, 378442881, 389295185, 394802836, 405165260, 411997377, 420097680, 428357332, 438719500, 445813905, 453652048, 461780691, 470701586, 479368273, 487206608, 495466068, 503985813, 512644754, 521311249, 529149456, 537802370, 545928917, 554587730, 563516950, 570691087, 579745346, 587871829, 596530898, 605460182, 612906516, 621426197, 630477845, 639276739, 646854338, 655373892, 664425683, 672831107, 680408578, 689059397, 697710214, 706368531, 714774019, 1076403202, 722613893, 731264582, 740054228, 748328515, 1075637251, 756168389, 764819142, 773608468, 781620886, 789722629, 798373382, 807163028, 815175254, 1076692997, 1074351110, 823146180, 831804629, 840078545, 848965271, 856700548, 865358997, 874130967, 881866244, 891049044, 1074632708, 899296855, 907301973, 916074199, 1075439559, 924472467, 932861011, 1076237257, 1074942985, 1075217354, 1073923082, 1074214856, 1077375947],
    [98, 84, 12, 1578113, 9966593, 18355393, 26743873, 35263680, 43652096, 52926159, 60429440, 68817984, 78271184, 86480527, 95048336, 102776465, 111646287, 119412371, 128610449, 136330833, 145200655, 1073750017, 152966867, 162164817, 169885201, 179147923, 186521171, 195719185, 203439825, 212702291, 1075858370, 220075539, 229273809, 237868051, 245907095, 254431824, 263296600, 270933657, 280515154, 288199891, 296492634, 305680914, 311539227, 321404631, 329929232, 336705179, 346570327, 356012690, 361870939, 371736087, 381178578, 387036891, 397570710, 405902872, 1074302915, 411857429, 422680216, 431125206, 439457496, 447094297, 453800597, 465024145, 472260313, 478966485, 490190033, 1074585540, 497426009, 1075649477, 506622486, 515355729, 520909397, 532132881, 1075402695, 539762202, 548565590, 555063006, 564928154, 572019229, 580228766, 590094042, 597185181, 605394462, 1075151817, 1073858507, 613962333, 622835356, 630739677, 639612636, 647909972, 1074145222, 655726174, 1076253640, 664687124, 673166876, 1074966478, 681464468, 689944156, 1076819914, 698241748, 1077357516, 1076589517],
    [94, 80, 1, 281664, 8705217, 18904192, 27292672, 35681472, 44069952, 52589697, 60978369, 69341840, 77755393, 84202625, 94916112, 102921281, 111284240, 117756993, 128470608, 136450768, 142922753, 153635984, 161615952, 168482518, 178801872, 184824022, 193648214, 201879249, 209989718, 218813974, 227044945, 235287187, 243979926, 252210705, 260321302, 268717056, 279761936, 285487254, 294546965, 304927888, 310660288, 321705168, 328101525, 338482256, 344339027, 355923543, 360991872, 1073742787, 369504979, 381089303, 386821717, 394670611, 406255319, 411594385, 420902407, 428880536, 439407680, 445542101, 454456967, 462435032, 473364119, 479751890, 488011335, 495850009, 506516672, 513177287, 521155096, 531682432, 1073760263, 538472082, 547124876, 556848128, 563637778, 572315220, 579875416, 589092500, 597192274, 605869588, 1074307014, 1075640261, 613290649, 622622220, 631035604, 1077219273, 638456537, 647788108, 1074621380, 655233625, 664565452, 1076467724, 1075439567, 1076244427, 1076778958, 1075229634, 1077076936, 1076040650, 1075005389],
    [106, 92, 12, 1997952, 10482880, 18896001, 27284481, 35673153, 44061889, 52581504, 60970048, 69351056, 77747392, 85980160, 94272704, 102913024, 111294032, 119438400, 127923328, 136992338, 144848400, 152992768, 161863363, 170014416, 178640387, 186932948, 195171972, 203806339, 212237829, 220337860, 228972099, 1073748164, 1075341315, 237655570, 245502980, 254014546, 262700757, 268850389, 279057476, 287568914, 296254997, 302404629, 313153170, 322582097, 329512082, 1076399042, 338198165, 344347797, 356136465, 362804288, 371752533, 377902165, 389691089, 397530838, 405175877, 414856849, 422696470, 430341765, 437016201, 447484930, 456250966, 1074327045, 463895749, 472536786, 481039554, 487347785, 497284306, 506224282, 514593858, 523359894, 530865812, 537679561, 548148354, 555079257, 564420116, 571627021, 579475027, 588633625, 598498842, 605181645, 613029523, 622188249, 632053338, 638195411, 647354009, 1076691915, 656694868, 663901837, 671749651, 682385114, 688674313, 697308887, 1073828873, 705844813, 714085911, 1075151885, 722605592, 730994392, 739251799, 1074128844, 1076246471, 747771544, 1077302222, 756160088, 1074963400, 764417687, 1076027338, 1075777487, 1074754502],
    [122, 108, 13, 2403328, 10949824, 18920577, 27309249, 35697729, 44086273, 52892672, 61123648, 67557074, 75805906, 86289536, 95098385, 101242388, 109491220, 119844032, 129046099, 134796948, 143045780, 154046032, 162600595, 168351316, 176600148, 187600592, 196155091, 201905876, 210154708, 221165270, 227063509, 238202003, 246748373, 1073750978, 252360195, 262853845, 268744210, 279885462, 285783573, 296652432, 305468437, 310826002, 319075922, 327726741, 338865683, 347411605, 352769106, 361019026, 369669717, 380808275, 389354581, 394712210, 403486406, 412005895, 422646803, 431140051, 439014485, 445429318, 453948999, 464424464, 472585937, 478852803, 489346197, 495892103, 506377750, 514266240, 521186961, 529184387, 539677717, 546223815, 1075867588, 557519952, 563129937, 1076664327, 571929622, 579646982, 591074320, 596937729, 605214423, 613715073, 623580305, 1075375045, 630642392, 640595542, 648746065, 655920857, 664204374, 674960528, 680823873, 689100375, 698815552, 706252313, 713733699, 722924694, 731428557, 742069456, 748195417, 1076431875, 756471448, 764982925, 773534785, 781749913, 1074623434, 790033622, 797750918, 806925837, 815477889, 823430337, 1076996044, 1076217800, 1074137094, 831706775, 840480333, 849032385, 856730833, 1074420749, 865261079, 874198017, 881896465, 890689112, 1075741643, 899077656, 1073927113, 1074993103, 1075279822],
    [114, 100, 11, 2281473, 10523840, 18912384, 27300864, 35689536, 44209153, 52597953, 60986497, 69390465, 77763649, 86154833, 94910164, 103191633, 109352466, 120115218, 128491219, 136853012, 145135249, 151295570, 162058322, 170434067, 178796116, 187078353, 193238674, 204001426, 212377235, 220206741, 229021201, 235181778, 245944530, 254320211, 262149717, 270716993, 278927061, 287480977, 295882945, 1073748931, 302552665, 312481301, 321035281, 330486288, 337812689, 346568340, 355652176, 361272857, 369933401, 380818128, 1075334082, 1074308036, 386438809, 395099289, 405983888, 411604697, 420265177, 431157910, 437042201, 447935062, 453785096, 462339800, 473101014, 1075893191, 478951048, 489854684, 495894104, 506655254, 515650780, 521059864, 529846811, 540816924, 548574236, 554614424, 563648157, 571790043, 579614280, 590517852, 596950749, 605590749, 613732955, 1074863624, 624702556, 632460956, 639024841, 647534109, 655676059, 666645660, 672448093, 681088093, 1075660741, 689631767, 697177675, 706001949, 714789594, 722343435, 731299337, 739963479, 1074103238, 747509451, 756465289, 765121114, 1073859851, 1074665420, 772551880, 781499549, 790295255, 797840523, 806796873, 815452698, 1075209225, 1076278221, 823849623, 1077082058, 832230042, 1077357518, 1076588495],
    [118, 104, 1, 357569, 10153153, 18936896, 27325632, 35714048, 44102784, 52489744, 59077761, 69505746, 75822786, 86044304, 94590146, 103322323, 111736019, 117765762, 127987280, 136533122, 145422019, 153653843, 162067539, 168097346, 178319056, 186864706, 195596947, 204010643, 210040322, 220515844, 228807682, 1073747970, 237539859, 245953555, 252245701, 262886595, 270847620, 279753222, 286061574, 294188613, 302740672, 312790596, 319460052, 327742981, 336294976, 346345156, 1075335172, 355242709, 361559622, 369686149, 380292101, 386626688, 1074825221, 397080067, 405581894, 411891398, 420673046, 430623941, 439448598, 447411779, 453677588, 462616214, 472566917, 481391766, 489354883, 497857158, 504165510, 512947926, 522898501, 531723478, 1074315267, 1073814534, 539791957, 546502230, 556889174, 563801153, 571118164, 581653571, 588966913, 598512149, 606819331, 614132865, 1075664839, 621449876, 631985283, 638643219, 648843925, 656209496, 665898072, 671446081, 681873938, 688616448, 697363603, 707039890, 714929880, 724618456, 730166273, 740594258, 748484248, 758172824, 764507665, 1075154890, 774680774, 782038552, 791727128, 798062225, 807318167, 814839505, 823192659, 832483927, 840005201, 848358611, 1074656204, 857649687, 1077029837, 866038487, 1076519881, 1076017102, 1077340107, 1076309960, 1076840399],
    [110, 96, 7, 1899521, 10662977, 19158209, 27317248, 35705984, 44094528, 52483264, 61002817, 69391361, 77780097, 86179408, 94663760, 102937729, 111334593, 119733904, 128349713, 136492225, 144899600, 153515729, 161657857, 170065616, 178681425, 184981015, 195624467, 203715600, 212907670, 220790483, 229406420, 1073746882, 238073558, 245956179, 254047376, 263239254, 270335105, 279738004, 288405014, 296287891, 304510609, 310810327, 320666817, 330069524, 1074807748, 335976087, 344905241, 354221121, 363624020, 370193433, 378459801, 386858522, 396653776, 403747993, 412014169, 422597785, 428801626, 1073780678, 437302361, 445568729, 456152281, 462356186, 1075108809, 1075392451, 470988508, 481219804, 487521946, 498226709, 504411353, 513070732, 523260953, 529858130, 537302615, 546625036, 555024082, 564417665, 572298907, 580179660, 588578322, 597971969, 1076716490, 605853403, 613733964, 623924313, 630521490, 1075938316, 638760476, 648991772, 656071708, 665080897, 672315036, 682546332, 689626268, 699553429, 706655832, 716101212, 723180636, 733107925, 1074121678, 739423324, 748346588, 758273621, 1074407371, 1076261832, 765236763, 773764824, 1077055437, 1074719695, 1076574149, 782153240, 790541976, 798791259, 1077370823],
    [138, 124, 11, 2462912, 10564673, 18953409, 27341953, 35730433, 44250240, 52638720, 61027520, 69834256, 77804608, 86445585, 92755667, 103233106, 109393107, 120166096, 128789586, 134698515, 145176082, 151335955, 162109008, 168244930, 179121170, 187512468, 193549845, 203896530, 210318357, 220829328, 229453010, 237843988, 245839506, 254121088, 260789849, 269169753, 279784594, 288175700, 296064000, 304549585, 313341652, 321229888, 327898777, 336278681, 346492561, 355701777, 363933402, 372225044, 378230297, 386610201, 397487642, 406033553, 1073747907, 412169925, 422653594, 431199441, 437335685, 445339353, 456207962, 462107865, 472888468, 478623362, 489098833, 495539925, 503919829, 515085393, 520566274, 529870487, 537351827, 545600659, 556774612, 562509378, 574295560, 580073052, 590435420, 598717524, 1075082182, 1076927490, 607850120, 613627420, 623989788, 632534619, 641404616, 647182044, 657544412, 663303829, 674477595, 683347528, 689125020, 699487388, 705246805, 716420827, 1075630088, 1074857927, 722931286, 731330078, 738808981, 749975195, 756747291, 764884702, 772363349, 780482131, 790082753, 798045765, 806817494, 815216222, 823481374, 1074089924, 832025729, 839988741, 849022107, 857159326, 865424542, 873968705, 1074628613, 882576603, 890590302, 899134465, 907742299, 915756254, 924817112, 932523543, 941061725, 949982872, 1074392012, 957689431, 966227485, 975148568, 1076501455, 1075471310, 982978070, 991393501, 1000314456, 1076003789, 1073932234, 1008144022, 1016559261, 1076312011, 1024798423, 1032279123, 1077374921],
    [126, 112, 12, 2667713, 10556480, 18945024, 27333760, 35722432, 44241921, 52630593, 60898896, 69407937, 78164993, 86185089, 94453392, 103330881, 109531842, 119619280, 128759379, 137172500, 143086082, 153173520, 162313747, 168391172, 179256849, 187479763, 193819224, 201790552, 212811345, 221034131, 227373784, 235345112, 246365905, 254325889, 260928024, 268899352, 279920273, 286037717, 294196935, 302871192, 310842520, 319495826, 327980629, 336402073, 345198791, 355931802, 361438802, 372683930, 378761369, 389486106, 394993362, 406238234, 411899609, 420827675, 428807195, 436936210, 445421077, 453842521, 462647513, 473372250, 479010454, 490124378, 1073745861, 495523335, 504174105, 512970759, 523704026, 529473175, 540456154, 545878724, 554637019, 563027671, 574273180, 580211355, 588190875, 596581911, 1074550723, 607827676, 615323284, 622154331, 630133851, 638393878, 649770524, 657266260, 664490697, 672480340, 683325020, 688461383, 699209428, 705262148, 714423508, 722245269, 1075093961, 1075894532, 730404487, 739987465, 747977876, 756979357, 1075381255, 763843138, 772611670, 782145053, 1074088194, 789794951, 798955085, 806166230, 815699549, 823357465, 832509581, 840252436, 1074365384, 849254109, 1073864651, 856903751, 866064077, 873406039, 881422468, 891229709, 1075712013, 899371081, 1074948044, 906449026, 915632217, 924143835, 932925577, 1076279246, 1077342159, 1076833226, 1076589510],
    [126, 112, 9, 390209, 10056768, 18445440, 26833920, 35222720, 42333377, 52761102, 60650510, 69170703, 75986640, 84276353, 94704206, 102593614, 111113935, 117929552, 126219265, 136786000, 145051345, 152925838, 161445455, 168261136, 178771468, 187117584, 195382929, 203257550, 211777167, 218592912, 229103244, 235501060, 245838032, 254103121, 262633107, 269481024, 279253134, 287657489, 296187603, 303035520, 312807630, 321744532, 329766604, 338759759, 346910292, 353367040, 363278480, 372076244, 378533056, 389091471, 397241876, 405263948, 414257359, 422016531, 429084373, 438957072, 447811599, 454258198, 464122960, 473239763, 480736851, 489901591, 1073743813, 1074028549, 497677456, 503936708, 515182739, 523456151, 531231952, 538136149, 548737043, 554948109, 563301909, 573902931, 580114061, 588591640, 598953687, 604862023, 613676690, 622146264, 632507991, 638547464, 647230994, 655700632, 663965333, 672102024, 680777293, 688486020, 698175001, 706032216, 713913991, 722728530, 1075886022, 730428996, 740118105, 747468295, 756250249, 764663501, 1077202948, 1074863042, 773158410, 782061209, 789411527, 798193353, 806614738, 1075408903, 815101578, 824004313, 831485640, 840136265, 848819406, 857044554, 865300118, 873428552, 882079241, 890762382, 1076988937, 1074650120, 1075718153, 898987722, 907243094, 915928142, 1076515850, 924020438, 932705294, 1075219403, 1074457611, 1076822979, 1073964035],
    [114, 100, 0, 2186240, 10679296, 18437185, 26825857, 35214529, 43602945, 52122624, 60511424, 68899904, 77561484, 86176960, 94065792, 101013186, 111115788, 119731264, 128661007, 134567554, 144670412, 154072590, 162215631, 169836108, 179238478, 185415312, 195526221, 204404366, 212547151, 220691981, 229570254, 1073749955, 1075605507, 235878098, 245560448, 254237825, 262878863, 269547028, 279403585, 285939411, 294475461, 305329686, 312958145, 319493779, 328029765, 338884246, 346512385, 353187344, 361584261, 372438614, 379673664, 386872850, 397235736, 405993174, 413228160, 420549656, 430790296, 439940825, 446782656, 454104216, 464344792, 470873812, 479419925, 487658712, 497899096, 505083537, 512974485, 521213016, 529593940, 538271259, 546256466, 555415249, 563437211, 571422354, 582546969, 588471893, 596317779, 604329538, 616101529, 622026453, 629872147, 638408197, 649655897, 656899725, 1076922373, 664614490, 671438338, 680588948, 690454221, 1074319362, 1074867202, 698300119, 706410065, 714432091, 723334874, 1076717508, 731575825, 739598043, 748500634, 1076203462, 757020183, 1074650056, 1075459080, 764229200, 1077303239, 1075226631, 1076545481, 773281355, 782186071, 1074209738, 790058507, 798832154, 806835915, 815740567, 823613067, 831338192, 1076051979],
    [118, 104, 7, 1840256, 10597504, 18986176, 27374592, 35763264, 44283073, 52671617, 61060161, 68948992, 77837313, 84399826, 92779730, 102503488, 112176851, 118216212, 127669440, 137473621, 143382228, 153892050, 162508435, 168547924, 178525904, 187674195, 193713812, 203691536, 212839955, 220976642, 226997906, 237778066, 246525589, 252425815, 262919874, 268940818, 279720978, 288468693, 294368919, 302503058, 310883922, 321664082, 330411541, 336312023, 344445970, 353220121, 363075152, 370128602, 1073755075, 378506840, 386643479, 395170841, 405018256, 412071578, 422677655, 428725913, 437105817, 447354513, 454014490, 464882755, 470669017, 479048921, 489297617, 495957594, 506563607, 515233308, 522851921, 1076912514, 531991683, 537777753, 546157657, 556406289, 563056152, 573953628, 579343425, 1075874756, 588222104, 599119516, 604771477, 613387992, 624285404, 629937237, 640781399, 648795202, 655103189, 666209283, 673961090, 680268821, 691375299, 698209370, 705172673, 716278999, 723375322, 1074325446, 730338433, 1076167624, 741977622, 747099218, 756659790, 1073838021, 763892737, 775532182, 782095514, 789845595, 1077249993, 800697942, 807261210, 815380174, 823400155, 1074129863, 834252502, 840545934, 848565915, 1076501452, 857323022, 865343003, 1075465230, 1074704330, 1076810703, 1074993099, 1075273677],
    [110, 96, 11, 638017, 10589376, 18977856, 27366528, 35755008, 44274817, 52663489, 61198992, 69440577, 76135617, 86217729, 94975506, 103019074, 111132305, 120526356, 128184962, 136298193, 145692308, 151361237, 162001109, 169852433, 176526869, 187166741, 195018321, 204075542, 210353281, 221189716, 229241494, 235518977, 246018646, 254516352, 263132884, 270791362, 279682240, 287961814, 296459264, 1073744835, 305739288, 312734210, 321625152, 1074290690, 327783944, 339293848, 344299157, 354939029, 361995408, 1075884997, 369727112, 381236952, 386242133, 396882005, 403938832, 411670088, 423179864, 431222792, 437493456, 445224648, 455685778, 1076940743, 464777416, 471047760, 1074593800, 480851538, 489943112, 496352787, 1073830854, 506017490, 514183376, 521518739, 530134682, 540274824, 546684627, 555300378, 564514896, 571850323, 580466266, 589680656, 598719572, 605754971, 613282391, 623885524, 630920859, 639211211, 646836759, 656119498, 665828500, 672863771, 681154187, 688779991, 699382804, 706295514, 714708555, 722334359, 731616778, 739972827, 748262923, 756544025, 1075417099, 764932761, 773321305, 781948490, 790098649, 1074915268, 1076234188, 798725770, 1074162637, 1076532234, 1075240911, 1075787721, 1077374926],
    [118, 104, 11, 291840, 10218624, 18478273, 26866753, 35255425, 43643905, 52163712, 60552192, 68940992, 77327360, 84440655, 94106688, 103518800, 110881856, 117995151, 128684752, 136047808, 143160847, 154112721, 162122753, 168326863, 176682501, 187797509, 1073754112, 193229888, 204197586, 210237125, 221352133, 227276307, 235796116, 243561664, 254529042, 1076911042, 260568645, 271683653, 277608083, 285504640, 296472210, 302511749, 313496209, 321942675, 330026578, 1075349509, 338661905, 344847956, 355200148, 363885587, 371954192, 378271443, 386791124, 397143252, 405828819, 414290053, 420345364, 430697556, 437417622, 447713873, 455863316, 462583382, 472617616, 478934611, 489714771, 497667201, 507220614, 514444481, 521303766, 532386310, 539610177, 546993689, 554807834, 565431322, 572159705, 582718150, 588797057, 597028504, 1074319494, 605139546, 613545481, 624151642, 630879897, 638694042, 647100041, 657706138, 663909910, 1074870212, 1077242823, 672248538, 682872026, 689600089, 700158022, 706237441, 714468952, 1076467658, 723358423, 730986057, 739791937, 748023320, 1075176392, 756912663, 764957889, 773189336, 782078615, 789706441, 798913668, 1075977225, 807244375, 815690756, 1075725251, 824152597, 832468036, 1073909708, 840929941, 849245380, 1074710478, 857707221, 1074210765, 866095701, 1076326347],
    [102, 88, 9, 2053120, 9698369, 18863297, 27251777, 35640449, 44028929, 52934348, 60773568, 68418689, 75880002, 86742082, 94109325, 102716480, 109434562, 120296642, 127663821, 136270976, 142988930, 153851010, 161961615, 169606669, 1073752064, 176543234, 1076391937, 187405314, 195516111, 203161165, 1076924418, 212833870, 220952067, 227802113, 237999758, 246118083, 252968129, 263165646, 271283779, 279182528, 288331278, 1074839811, 296449155, 304348288, 1073821636, 314021511, 321345039, 329514048, 339187207, 347305682, 355204290, 364353223, 371676751, 379845632, 1077240774, 1075939463, 1074383879, 388478476, 397147138, 406287891, 412079123, 423072839, 430701698, 1074666437, 1075469317, 439842451, 445633683, 455587468, 464256066, 473134610, 479319573, 489141836, 497941525, 506689170, 512742995, 521246225, 531854930, 537908947, 546412177, 556662421, 565670995, 571593877, 579966673, 590216917, 599225555, 605673097, 613520977, 621925589, 632159829, 639227401, 647468692, 655479893, 664516112, 672781897, 681023060, 689411604, 697947849, 706459216, 1075746760, 1075233801, 714847888, 723236560, 731354836, 1074212811, 1076848586],
    [114, 100, 13, 292864, 8689728, 18757696, 27146240, 35535040, 43923584, 52443137, 60831873, 69220417, 75790528, 84195980, 94386369, 100940290, 109344832, 117750476, 128070159, 134494786, 142899328, 151304716, 161747664, 168081996, 178936461, 1073750016, 1075865601, 185088721, 195441347, 204102221, 210418319, 220345039, 229267981, 235583695, 243808849, 253898895, 262822605, 269138511, 279064655, 288381009, 294303759, 303208643, 313546961, 1076408261, 319846593, 328636493, 335821506, 345029268, 353400897, 361249425, 372267153, 378968269, 386415121, 396628496, 402930306, 414210065, 420911245, 1076677634, 430183056, 437303892, 445675649, 455348816, 462985811, 470841345, 480653827, 488019981, 498366990, 1074603395, 505819203, 512801492, 523532878, 530985091, 538483219, 548698766, 1076196294, 554701334, 562337792, 573864654, 579867222, 588921544, 597457093, 605592275, 1076988868, 613421718, 622475912, 631011397, 637835456, 646976214, 656030216, 664565893, 672701075, 1074387911, 680923799, 689584712, 697473027, 706508805, 1075452936, 714879637, 722516500, 731798034, 739644119, 746887296, 756964050, 765211349, 772970563, 782129746, 790377045, 798136451, 807295634, 1075729354, 1074959370, 815141463, 823931413, 1075233737, 1073939465, 831918615, 1074231243],
    [94, 80, 11, 1866816, 10328256, 18096257, 26744896, 35133568, 43522240, 51910656, 60430337, 68819009, 77207745, 85752832, 94214272, 101982209, 110762113, 119379968, 127696064, 135536833, 144545856, 152861824, 160702529, 168303107, 177873487, 187144913, 1073750017, 193469059, 203301458, 212703891, 218652244, 228467346, 237476497, 245873237, 253371023, 261258902, 270410450, 279419409, 285761172, 295313935, 304978451, 311590614, 319298115, 329130514, 338532947, 344481300, 354034383, 363305553, 370310678, 378411592, 388479509, 396763856, 403865174, 413532759, 422419155, 428367572, 437131912, 1075865540, 447095440, 1076135874, 455475927, 463864343, 472365717, 480649808, 489030295, 1074056133, 497531605, 506363404, 512236227, 522592784, 1074331651, 529406472, 539917964, 546183880, 1073827848, 556695244, 565083724, 1074902028, 572030542, 1077270477, 1075190730, 1075475401, 580419278, 1077055435, 1074719687, 588807822, 1076568006, 597196302, 1075801102, 605707800, 613816344, 622485080, 630593624, 639262424, 647370968, 656039576, 664148120],
    [118, 104, 11, 2422912, 10776768, 18905089, 27424832, 35813504, 44201984, 52590784, 60848257, 69236929, 75788816, 86571600, 94402625, 103086272, 109343440, 119684819, 126253267, 136640576, 142897232, 153239123, 159807571, 170194944, 179327569, 186793619, 193362067, 204011536, 210006672, 220610260, 227310229, 235305491, 246436561, 254343376, 262290451, 269253205, 279990929, 287897744, 296369237, 302807573, 313545233, 319477905, 329661972, 336362197, 347755090, 353032273, 363478165, 370047576, 381309458, 386586641, 397286488, 403602136, 414864018, 420141265, 430841048, 440029906, 447102548, 455372864, 464395928, 470710424, 482015963, 488927232, 497950232, 504264728, 515570331, 522481792, 530988692, 540736027, 546460247, 1073746884, 556416021, 565901915, 571626007, 1074807747, 581582037, 588700189, 596792023, 1073781702, 1075369925, 604642966, 613997278, 621957783, 629808854, 639031965, 647655962, 654974550, 664197853, 672821850, 680140310, 689896096, 698249759, 1075127240, 1075922887, 705969817, 714529373, 723153626, 1074105289, 731135577, 739826206, 748581599, 756432540, 764992094, 773485210, 781598428, 790559328, 798913119, 1074388941, 1075711946, 806764124, 815323806, 824079007, 1074685902, 1076278210, 831798809, 840890912, 1077082059, 848576217, 857668320, 1077357519, 1076588492, 865484316],
    [130, 116, 11, 2119681, 10508353, 18897089, 27285633, 35805312, 44193792, 52304400, 60971200, 69589585, 77748288, 86262274, 94656514, 102636176, 109468243, 119921361, 128205506, 136599746, 144579152, 151411411, 161864337, 170148418, 178542658, 186522320, 193485332, 203807249, 212091522, 220485762, 227162323, 235428436, 1073743874, 246178386, 254794245, 262945412, 271344274, 279960133, 288111172, 1074293699, 296509970, 305388246, 313277124, 321675986, 330054148, 1076408324, 338584279, 344611480, 353122456, 1076943814, 363749975, 369515027, 378157075, 389178056, 397400773, 403462344, 411711571, 420109016, 431120968, 439343749, 445405256, 454309908, 462051928, 1075388421, 471063129, 481190551, 487479385, 496384089, 503864020, 515103254, 523133463, 529029780, 538196116, 548657814, 556950152, 562845832, 571095699, 579229843, 588143129, 1075929031, 598989398, 607281672, 613177352, 621558296, 629823512, 1075679240, 640828053, 649845274, 655382554, 664025300, 672291339, 682771157, 691788378, 697325658, 706099865, 714365581, 722360473, 733102677, 742120090, 747657370, 755775576, 764566155, 1074919369, 775045653, 784063194, 789600474, 798374617, 806509259, 814635225, 823672841, 831772697, 840587982, 848574548, 856840779, 1077280779, 865616073, 873715929, 882530894, 890648601, 898914829, 907559049, 915658905, 924473998, 931936472, 940858061, 949502025, 958028302, 966023757, 1073890317, 1074172942, 1075242954, 1076301775, 1074753484],
    [106, 92, 10, 333952, 8714432, 17076417, 27310272, 35698752, 44087296, 52476032, 59045888, 67408001, 75963088, 86555346, 94968018, 100989056, 109350913, 120109586, 128522258, 134543424, 142905409, 153664082, 162076754, 168202835, 179231312, 187218578, 195631250, 204397200, 210277013, 218534547, 226957456, 237951184, 1073750979, 243866257, 254728720, 260608725, 1075858372, 271768086, 277254675, 285677648, 296934038, 302420691, 310843408, 322099798, 327752273, 336106069, 347265750, 352918225, 361271829, 1074305991, 369695249, 378329153, 387093079, 395106433, 403643028, 412258839, 420272129, 428808724, 437424855, 445438145, 453974612, 462590615, 470866522, 479140564, 488026843, 496171548, 503650304, 513577088, 521599513, 530004568, 538619920, 1075368907, 546363930, 555520000, 562370752, 571669148, 580336152, 588951760, 596835036, 604313664, 613855835, 622639822, 630651481, 639056536, 647671888, 1074866122, 656194190, 664205977, 672611032, 681349312, 689748558, 1076191181, 697359066, 706130459, 1075689420, 714914318, 722524826, 731558032, 1077267470, 1074671557, 739441244, 748458048, 756462235, 764869337, 1076773826, 1073918918, 1077069769, 1074206671, 1075276744],
    [106, 92, 2, 1867840, 10524865, 18913281, 27302017, 35690561, 44210240, 52598912, 60963536, 69376192, 77365376, 86153216, 94699153, 101095569, 111155922, 119308480, 128490131, 136642065, 143038481, 153499795, 159947394, 169639936, 178821715, 186973905, 193370321, 203569808, 210279106, 220496066, 229153491, 237305425, 243701841, 254163155, 260610562, 270827522, 279484947, 285776450, 295844368, 304382018, 1073741826, 313187973, 319723653, 329660435, 337936514, 346742469, 353278149, 363214931, 371630291, 380436182, 389060822, 396507728, 403610181, 413573267, 422239301, 428775941, 438739027, 1073762309, 446700050, 455793669, 463904787, 472710678, 480254610, 489723926, 497721345, 506265238, 513808978, 523278486, 531407572, 539819606, 548149783, 556832854, 564830401, 573315671, 581607489, 590093015, 598516372, 606870167, 615293460, 1074837449, 623778456, 630644377, 640459348, 648944344, 657490517, 664443532, 674110040, 682270849, 689609292, 699275800, 707822229, 1077202890, 714775052, 722918937, 732987925, 739941068, 748084825, 758153941, 1074598924, 764862169, 1075136462, 1074112459, 1076228040, 1076769743, 1077042119, 1075489734, 1076551629, 1075782595, 1076054980],
    [122, 108, 13, 2324480, 10549377, 18937857, 27326657, 35846208, 44103745, 52623488, 61133520, 69254352, 77789184, 86341840, 94566592, 102809168, 111465104, 119896144, 128241744, 136363152, 145062032, 153403027, 161796624, 170096832, 178568915, 187618001, 195393552, 204405270, 212783761, 220773975, 226949207, 237205632, 246348438, 254726673, 262717079, 268892311, 279148608, 1073742786, 288291542, 296669777, 304660183, 310835415, 321870484, 330234454, 338214423, 344773269, 352778263, 363813396, 369818245, 380812374, 386716373, 395115096, 405756628, 1073763267, 411761221, 422755542, 428659285, 439310932, 445315589, 456309782, 462213653, 472873046, 478870213, 489864342, 498397332, 506427414, 1074825221, 512686662, 523681306, 531951636, 539981974, 546241158, 557497432, 565506260, 573536470, 579664536, 591051928, 599060564, 604961286, 613767377, 621738694, 630641362, 639942227, 647321681, 1074321414, 655162072, 664335003, 674676378, 680876177, 689361426, 699842138, 706041873, 714799627, 723055195, 731954192, 739990233, 1075382215, 747436568, 756470354, 767212568, 773544601, 781908619, 790428174, 798413458, 807714323, 815487577, 823851723, 832371278, 840495643, 851098840, 857430553, 1074091977, 865925838, 874050267, 884391642, 890960459, 899480206, 1075153931, 1074650126, 1075720138, 1076782024, 1076016068, 1077078991, 1076570060, 1076328397],
    [126, 112, 9, 2152641, 10541185, 18929665, 27318337, 35838016, 44226688, 52869776, 61003968, 69392384, 77914705, 86530129, 92592786, 103201360, 111598099, 117891091, 128473809, 134666836, 145144528, 153541267, 159834259, 170416657, 176478930, 187087376, 195484371, 201777363, 212359825, 218421842, 227064018, 237427283, 243720275, 254572755, 1073744834, 260364818, 269261525, 279861846, 288022530, 294050324, 302561362, 313416342, 321577154, 327604948, 336509140, 346970838, 355131522, 361159316, 369924757, 380525078, 388685890, 395090453, 405856919, 414472728, 1074289603, 420395092, 431022615, 439638616, 445823706, 456579611, 464437275, 472676371, 479377946, 490134171, 497991835, 506230931, 512932506, 523688667, 1075348421, 531546331, 539785299, 546486874, 557242971, 565100635, 571767452, 579787485, 588560605, 598794967, 607410904, 613341853, 622114973, 630381278, 640737879, 649353880, 655284765, 664057885, 672324126, 1073796039, 681894033, 691951838, 697227869, 706000989, 715448337, 725506078, 731559966, 739433118, 749002961, 759060638, 765114526, 775217347, 781482524, 790280414, 798153310, 1074869190, 808771587, 817780830, 1076978632, 822655122, 833937539, 840202844, 1075948484, 848214164, 859103299, 865368796, 873379860, 882434777, 890943582, 1076479949, 1074141134, 899211929, 906795605, 915989017, 923318290, 1075214282, 932766297, 1077317577, 1074720716, 1076830155, 1075800015],
    [118, 104, 1, 497664, 8878144, 18550785, 27343040, 35731456, 44120128, 52508800, 61028481, 69417153, 77805633, 84375744, 92912272, 102961296, 111360001, 120011346, 126318720, 134855248, 144904272, 153565714, 159873024, 170236611, 178459152, 184891923, 193411796, 203897490, 210483921, 218855504, 228790992, 235485909, 243743252, 254229202, 262904021, 270209089, 277575696, 285817429, 294074964, 304846933, 312152193, 319518864, 327760533, 336018068, 346886163, 355178645, 361461968, 369441491, 380467218, 388829395, 396728963, 403389060, 414021778, 422680708, 429592769, 436812309, 447576274, 453718614, 464230421, 470104723, 481130578, 489492627, 497392195, 1073745987, 503659091, 512440900, 523343940, 531435603, 538007745, 545995460, 554381846, 565287108, 571562113, 579549700, 587936470, 598841348, 605116481, 1074808836, 613628551, 621490838, 631609347, 638670849, 647182855, 655560914, 666327124, 671725584, 680737351, 1074302917, 689115218, 699881684, 705411665, 714291911, 722669714, 733436052, 738966033, 1074583559, 747835410, 758601748, 764131985, 773675607, 780777680, 790452759, 797415616, 807230103, 814192768, 824007383, 830969920, 1075381186, 840923736, 1073832905, 849312280, 1075950542, 1077013446, 857701080, 1076508619, 866089624, 1077305295, 1075746760, 1075242957, 1076309964, 1076840394],
    [102, 88, 8, 2031616, 10795200, 18946049, 27334785, 35723329, 44112065, 52631616, 61020160, 69408896, 78027280, 85917760, 94574784, 103193168, 111083712, 119766738, 128359120, 136249472, 144932434, 153682452, 161913488, 168648214, 178593872, 187603665, 195657303, 203759824, 212769361, 220823063, 228925456, 237935121, 245989079, 254091408, 263101073, 1073752003, 271154839, 277553878, 287619072, 295927442, 302719574, 312785024, 321093138, 1076124612, 330367642, 337950784, 344808662, 355383318, 363922010, 369826502, 378363542, 1075350466, 388937814, 397476570, 403380870, 412450521, 422492374, 431030810, 436935174, 446004889, 456046742, 464061012, 1074316229, 470489670, 479026262, 1073808390, 489732755, 497615508, 504725017, 514898643, 522781396, 529890905, 540064339, 546374363, 556841491, 563282002, 1074090953, 572299992, 579928667, 589077144, 596705947, 1074896840, 1075705799, 605854296, 613097622, 622795276, 631020056, 638263318, 647928533, 655556754, 664738380, 673094165, 680722450, 689904268, 1077293003, 698260053, 705757723, 715070156, 1076777996, 723425941, 731054290, 1075220429, 1074721742, 1077095375, 1076585418],
    [106, 92, 8, 382976, 10582080, 18970816, 27359232, 35747968, 44252816, 50714688, 61436562, 69418704, 75880576, 86602322, 94584400, 101046464, 111768082, 120135364, 126474897, 136934098, 145301124, 151640657, 162362068, 170466820, 178780161, 185422547, 195632708, 201972241, 1073754116, 212693524, 220413456, 229112001, 1076908995, 237859412, 246488661, 252304081, 263025300, 271654613, 279443585, 1074824130, 288576152, 296820373, 303135239, 312997953, 322130520, 330374677, 336689735, 346945680, 355684888, 364239511, 372448968, 380850904, 387152072, 397794007, 406003336, 414798422, 420706440, 431348311, 439557704, 448352982, 454260808, 464386064, 473112072, 481907350, 487815176, 497940688, 1073797128, 1075391433, 1076451269, 504577625, 515461654, 521501386, 532011543, 537743891, 546520729, 555055690, 565049424, 571298387, 580075033, 588610186, 597285014, 604852883, 613629657, 622164490, 630839318, 1075152906, 1074382790, 639311578, 647983771, 656243278, 664393942, 672865818, 681538075, 689797646, 697399943, 706336854, 714808986, 723481179, 731740814, 739974746, 748647131, 756906702, 764508871, 1074142222, 1075734477, 1076268039, 1074722764, 1077358543, 1076847563],
    [114, 100, 3, 352257, 10573953, 18962497, 27351041, 35739841, 44259392, 52648128, 61036544, 67461313, 77813888, 86448657, 92624913, 102974019, 111876818, 117922002, 128139971, 137042514, 143087698, 153305731, 162331204, 170597010, 176642194, 186860035, 1073743875, 195885700, 203889361, 210065617, 220944965, 229589634, 237828804, 246626882, 252140050, 262887941, 269179475, 280051781, 288160260, 296425490, 302340753, 313219717, 319511187, 330252802, 1074293764, 338753541, 346495121, 352672337, 363551429, 369973972, 380584642, 1076664325, 1075376130, 389085253, 396826705, 403528212, 414138434, 423033366, 431175874, 439435397, 448199318, 456341634, 464863815, 473365206, 481507330, 490029767, 1076963655, 498530902, 504445011, 512449235, 523583495, 531691717, 537999571, 548487173, 556857477, 563550743, 571169299, 581788176, 588315221, 597105367, 607207621, 613735000, 621885459, 630020692, 640508496, 1076450249, 647035413, 655440019, 666189959, 672201429, 680991383, 688741012, 699228816, 705755797, 714815636, 721772673, 731175640, 739981332, 746938433, 1074889674, 756341272, 765147220, 774726352, 1073870795, 781507224, 790043223, 798580928, 807090388, 815357952, 1077290956, 1076256717, 823746688, 1075746766, 1075234760, 832135232, 1074209743, 1076056006],
    [114, 100, 9, 268289, 8902785, 18462721, 26851393, 35371200, 43759616, 52017281, 60536960, 68794561, 78108672, 84154433, 94091328, 103387854, 109427266, 117848589, 128703052, 136942222, 145217600, 151403149, 162107918, 168434192, 176674881, 187273806, 193600208, 204200588, 210219730, 218765904, 229366476, 235508435, 243931792, 254532108, 1073745860, 1074554884, 260682390, 268843597, 277338113, 285840019, 293869761, 302504129, 311276245, 321378496, 328219217, 336171539, 344308226, 354932864, 360978561, 369603218, 378550929, 389020303, 394900054, 405412505, 414185999, 419934802, 428194434, 438967001, 447740623, 453620438, 464132633, 472906319, 479312520, 487953112, 497687129, 504625869, 1076403143, 512867016, 521507352, 528857794, 538179597, 545667277, 1075368962, 555072137, 562672150, 571734093, 579877393, 588364360, 596488853, 605288589, 613432017, 622181065, 630559384, 638720128, 647748247, 655735369, 664113752, 672405644, 681302743, 689289737, 696881747, 706214612, 714217664, 1075130377, 1076983755, 1077251014, 1074392070, 722582024, 730706453, 739514572, 748411479, 1076763656, 1075729349, 755872341, 764934676, 773068812, 780644882, 789846092, 798743063, 1074955203, 1073924042, 1074208778, 1076061187, 806877844, 814880832, 823654996, 831657984],
    [122, 108, 12, 1178816, 8757377, 18454529, 26843329, 35231809, 43620481, 52140032, 60528704, 68917440, 76676096, 84509260, 94083200, 101548685, 110230592, 120273423, 128162512, 134847043, 143366788, 152173696, 160006860, 170866755, 178494032, 185178627, 193698372, 201949836, 210492624, 221198339, 228825744, 235510467, 244416640, 252435600, 263141571, 270768656, 277715653, 285842051, 294378512, 302882832, 1073742851, 313473155, 319135809, 327933008, 338377423, 345342546, 353361486, 363543183, 370245696, 378658450, 388708943, 395287047, 404872199, 414162951, 420297425, 428990162, 437616850, 445463185, 454007495, 463592647, 472883399, 479017489, 487432400, 495967758, 504183377, 512727687, 522312839, 531603591, 537991765, 546282055, 555867207, 565157959, 1074024455, 1074834439, 571808404, 579707024, 588242638, 597236307, 605126656, 613408398, 622402067, 630692361, 638294532, 647093778, 654680257, 1076683714, 664083156, 672635465, 680368709, 688751181, 697424978, 706288275, 714578633, 722311685, 730955968, 739850774, 748133001, 755866245, 763986444, 1075904517, 1073825801, 772872853, 780901060, 789938322, 1074373636, 798571094, 1076219850, 805675009, 815348374, 1074665416, 1075210248, 822968845, 832125654, 840269842, 1076534219, 1075508235, 848370389, 856523469, 1077354438, 1075802118, 865409620, 873308240, 881924629, 890837715, 898963988],
    [130, 116, 8, 2521152, 9157760, 18479233, 26867905, 35256385, 43644929, 52164672, 60553216, 68941952, 78018752, 84655296, 94107840, 101055185, 111016450, 117963395, 126196738, 136870415, 145478226, 151386641, 161348162, 168426003, 176528450, 187202127, 195810002, 201718417, 211679874, 218888789, 227048084, 235248770, 246141586, 252050001, 1073754112, 262011586, 269089363, 277379668, 285580482, 1076903938, 296473106, 302906006, 311425668, 319289923, 327711444, 336436356, 344849110, 353368644, 361495189, 369654292, 378379332, 389403159, 395180630, 403438293, 411810816, 422606993, 431346263, 437123606, 445381141, 454031876, 462265348, 472283136, 481940184, 487062019, 495696960, 506493137, 515494552, 520616643, 529529540, 537763012, 548436049, 1073776644, 1074321411, 557437464, 562690771, 571841619, 581466831, 590991960, 596245139, 605142101, 615021199, 624030425, 631666816, 638827651, 649450135, 655727827, 665876497, 674616023, 682343963, 689338896, 699527705, 705805525, 714766486, 1075386309, 724693657, 732675675, 739670672, 1075138502, 749859417, 756447952, 764656643, 775672349, 781613648, 789691413, 800838237, 806468757, 815429654, 826004125, 831888531, 840595670, 1074634698, 1075696584, 851170013, 858504923, 865761366, 873722394, 882801180, 892059291, 898888410, 907967068, 915651651, 1074931660, 924054170, 933133020, 940940307, 1076262857, 949219930, 958298780, 965983427, 1077324750, 1076555725, 1076824007, 1074226123],
    [110, 96, 8, 1818624, 10336321, 18864193, 27252865, 35641345, 44161216, 52549632, 60807361, 69326976, 77316224, 86096588, 94492736, 102481984, 111262284, 119259328, 128039564, 136428044, 144687297, 151878287, 1073752064, 1076391937, 161856013, 169852929, 178747984, 187021901, 195018881, 1076934594, 203913872, 212187789, 220184641, 229210833, 235911699, 245987857, 254130893, 261052946, 271049364, 277600404, 286243539, 1077211078, 294607442, 1076698053, 1075403781, 304996872, 311285768, 320714753, 328038927, 338158100, 344709140, 353352339, 1075680195, 363297488, 1074906055, 372105928, 378394824, 386906707, 395147983, 405267156, 411818196, 420600470, 429766849, 1073875908, 1074416644, 438794768, 447603272, 453892168, 463321217, 473004629, 480764500, 487315540, 496220686, 506034769, 514712200, 521001096, 529775182, 540113557, 1074693128, 546423320, 555080393, 563206678, 571718350, 581532305, 588497495, 597023241, 605149910, 613661326, 623999701, 630440663, 638966345, 647477270, 657553941, 663863896, 672520841, 680647254, 689420438, 697260690, 1074189321, 705937943, 714586326, 723475033, 730972824, 739752022, 747592402, 756138712, 765418009, 773046935, 782195353, 790584025, 1075259338, 797801039, 1076323275],
    [106, 92, 13, 2260032, 8666113, 17054785, 25443521, 33832065, 42351744, 50740288, 59129024, 69369024, 75906048, 86146176, 92708364, 102923264, 109485708, 1073747969, 118390473, 1075339264, 1075881985, 126262988, 135167625, 143040076, 153490958, 160333321, 170268238, 177110601, 185114191, 195434126, 204111562, 212342416, 220888714, 229686930, 237508304, 246054410, 1076416450, 252616339, 262543054, 271220298, 280018450, 287839824, 294542987, 305184466, 310646421, 319839761, 330350162, 335812181, 345407053, 353418776, 363337232, 370040331, 378584664, 386143957, 395337361, 403750552, 411309589, 420372043, 1074598851, 1074877443, 429143639, 437305048, 445267652, 454458893, 462995030, 471348761, 478821956, 488013517, 495492815, 505034260, 512376452, 521166417, 529284741, 537828947, 546846361, 554319364, 562978507, 1075160068, 571227845, 580138519, 588160531, 596655815, 605453965, 613170757, 622378518, 630732505, 638598791, 646995665, 655113733, 664024791, 672710294, 680541703, 1076222981, 1075719173, 689487574, 697972308, 705707591, 1076774919, 714356375, 721985167, 730767059, 739915476, 747150863, 756561497, 1074430918, 1073923078, 765081236, 1074213832, 1077113864],
    [110, 96, 13, 2390209, 9575552, 17964032, 26352704, 34741440, 43261057, 51649729, 60669442, 68426753, 77887489, 85204033, 93855244, 102612674, 1073746306, 111442049, 1074809795, 119152270, 127777858, 135798412, 144996417, 152706766, 1074305025, 161332354, 169352908, 176846860, 1075372033, 187172496, 194649614, 203792079, 211295820, 218789964, 229115472, 236592718, 245734991, 251928132, 263092292, 271058448, 277094084, 287678095, 296646852, 304613072, 310648324, 321494739, 330201092, 338437841, 344202884, 355367044, 361864852, 371992081, 1075905540, 380116565, 386276886, 394950860, 405257301, 414065686, 420116620, 430546451, 439494290, 447225493, 456292941, 463977621, 472655505, 478551766, 487749710, 496082644, 506734168, 512106134, 523401741, 529636884, 539894998, 546469902, 556375635, 565454360, 570826326, 580024526, 588357204, 599008920, 607287949, 615392406, 623484563, 630356110, 640558166, 648527381, 656940053, 666008269, 673982033, 682082005, 690494677, 697850521, 708060888, 714889815, 724706898, 731404825, 1074089925, 741484242, 748444375, 757440015, 765221527, 1074632646, 773610007, 783427090, 790125145, 1075168200, 798513881, 1073884103, 1076518857, 1075749897, 1076293578, 1076835275, 1077113867],
    [98, 84, 1, 283712, 10229888, 17071232, 25459904, 33848320, 42236992, 50756609, 59145345, 69140174, 75922625, 85727232, 92697806, 101088321, 111083150, 119281856, 126252558, 136248910, 144447552, 151417998, 1073747969, 161414158, 168195150, 178526273, 186914817, 193754831, 202407569, 209998976, 220469377, 1075332034, 227213010, 235828880, 245635265, 252739153, 260723793, 269228226, 277771792, 286005378, 294533827, 302806671, 1073777091, 311326416, 319961797, 328007316, 336336962, 345274067, 353253507, 361526863, 370179793, 378164433, 387070597, 1074319557, 395116052, 403734033, 411718673, 420624453, 428670676, 1074865092, 437000194, 445937235, 454221462, 462837269, 470693891, 479002196, 488003285, 495983319, 504036882, 511988928, 521149079, 529202834, 537547921, 546314775, 554884630, 563500693, 571480663, 579534418, 588396549, 596932115, 605748760, 613316176, 621688899, 1075931079, 630382294, 638998101, 647691992, 654595072, 1076212680, 1077015560, 1077286858, 664469144, 672429715, 681246296, 688682511, 1075212230, 697491030, 1076800457, 1076547531, 1074733004, 1075791821],
    [118, 104, 13, 1588225, 9829569, 18635968, 27024448, 35412992, 43801728, 52321281, 60709953, 69098689, 77070018, 85474433, 94264449, 102917713, 109337681, 1073744322, 119012418, 127417537, 1074287555, 136472273, 142892241, 152566786, 160971841, 170026641, 176446609, 1074829313, 186121346, 193478224, 203580945, 210000913, 220225158, 228588739, 235421392, 245786311, 252075207, 262168134, 270531651, 277364240, 287459023, 294018695, 304111302, 312474627, 319307408, 329671815, 335961607, 346054150, 354688134, 362150913, 1075371014, 371614727, 377904711, 388242438, 396360835, 1075642375, 405169223, 411721429, 421796934, 430440146, 1073834949, 439109332, 445275797, 455351494, 463994514, 472663700, 478830101, 489692691, 497548818, 506218068, 512384597, 523378254, 531103314, 540304405, 548413011, 555089025, 565470357, 1076470729, 573578899, 580254785, 590636117, 598735941, 607133395, 1075957704, 615802069, 623901701, 632430094, 640435732, 649067653, 657596110, 664946255, 674233541, 682761870, 690112015, 697048790, 705977879, 715277967, 722615319, 730603094, 739532439, 747380374, 756309719, 764558551, 773086807, 1074669515, 1076260804, 781335639, 789995084, 798514765, 806100502, 815161036, 823680717, 831667351, 840326796, 848846349, 857103884, 865623693, 1076790284, 1074189325, 1075262410, 1077113866],
    [98, 84, 9, 2405376, 8707200, 17087553, 25476225, 33864897, 42253313, 50773184, 59161728, 67550272, 75815936, 86291520, 92716032, 103068800, 109502095, 117775952, 128234688, 134536384, 145309265, 151568019, 1073747969, 159833615, 170563278, 176627282, 185122387, 193256512, 204117518, 210181778, 218676947, 226942543, 237672078, 243875477, 252231187, 260497103, 271226446, 277429973, 288152787, 294294593, 1075336131, 304692881, 313318419, 319460353, 329858577, 338484307, 345019927, 355024593, 363650195, 370185815, 377822928, 386457236, 394957953, 402988560, 411735233, 420404430, 428285458, 437556953, 445177556, 454106648, 462618326, 470849239, 479272600, 487888473, 495901774, 1074831302, 504438488, 1075632072, 513054233, 521338390, 528817808, 538099274, 546608793, 555286106, 563158616, 571653770, 1075120069, 580058774, 588289687, 596196949, 605208266, 613613142, 621223634, 630373898, 1074089929, 638508174, 1074628618, 646504020, 654892564, 664337946, 671694357, 681115290, 1074381771, 1073886156, 1077048332, 689503962, 1077322690, 697228302, 1076031431, 1076833229, 1076586436],
    [134, 120, 10, 1875073, 10263553, 18652225, 27171840, 35560640, 43949120, 52856386, 60726400, 68984001, 78174735, 86023758, 94799490, 1073746498, 102645456, 1074809795, 111729295, 119840337, 128353474, 136199760, 145414225, 153394833, 1074305025, 161907714, 169754256, 178968721, 186949329, 196117582, 203701906, 212507794, 220911825, 228892177, 236986003, 246062802, 254335567, 263226894, 270572558, 278929107, 287890127, 297043540, 304913941, 312516302, 1075372996, 320872019, 329963537, 338986644, 344628886, 354459278, 363740310, 372570821, 380929748, 388250834, 397736453, 406095380, 413965909, 420257350, 430980697, 439393369, 445685400, 456456837, 464553166, 470589062, 480255507, 489725657, 498399813, 506496142, 1075913733, 512794136, 523255321, 531667993, 537697990, 548993176, 554477079, 564960981, 571514584, 581975705, 590388377, 596418054, 607713496, 613197527, 1076188166, 621453014, 630234712, 640564438, 649656344, 655402523, 663395926, 672308744, 682507350, 691314269, 699988056, 705472151, 715955861, 722116118, 731029064, 741227542, 750034589, 756589725, 764737557, 772972168, 783301849, 791322194, 798532701, 806943386, 1075163079, 814915272, 824458322, 832231964, 839952027, 1076741128, 849009372, 856729179, 866008592, 874052122, 881632855, 1074136009, 892640797, 899195933, 907343957, 916733458, 925539346, 932772442, 941139677, 951360733, 957675669, 965781211, 974452949, 1073893322, 983104218, 1074700235, 1075770316, 1077097484, 991615644, 1000004188, 1077373901],
    [98, 84, 10, 2448513, 10802369, 17103936, 25492672, 33881088, 42269824, 50789441, 59178113, 67566785, 77945921, 86431438, 92732417, 103455362, 111213698, 119635471, 128374350, 137009666, 144768002, 153190095, 161928846, 170695250, 176750211, 1073747969, 186744399, 195483150, 204118722, 211877058, 218945043, 228687503, 237804050, 243858947, 254334676, 262495425, 271358610, 278986306, 286053971, 296049665, 1075331074, 304781378, 310967875, 319608531, 329866243, 338467538, 344522435, 355171989, 363386388, 1073776643, 372546128, 378328723, 388726485, 397842627, 405363843, 413718164, 423008387, 430669397, 438883924, 448174083, 455835157, 463787073, 473339971, 480861379, 488952833, 498375376, 506027075, 514118785, 523541136, 530109520, 539713233, 548706832, 555275280, 564878865, 572045975, 581656145, 589231761, 1074319302, 597211735, 605607056, 615210129, 622377495, 631174353, 639154903, 1074601925, 647550160, 656325334, 664728593, 673102358, 681505873, 689879638, 698268310, 1075664845, 1075163076, 1076753352, 1077031944, 1077299147, 1074177994, 1076286407, 1074996172, 1076063177],
    [98, 84, 7, 2417856, 10271809, 18668737, 27057153, 35445889, 43834433, 52354176, 60742848, 69131264, 77774402, 86689474, 94297152, 1073744194, 103465986, 111328386, 119832208, 1074287555, 128245329, 137020482, 144882882, 153386512, 161799825, 1074829313, 170048514, 178963586, 186965521, 195749009, 203209729, 212106960, 220520145, 229303505, 236764353, 246080529, 253541505, 262438480, 271498964, 280151759, 288276052, 296412241, 305053204, 313706127, 1075364804, 321830548, 330483215, 338861778, 347260495, 355098135, 363781143, 372416082, 379905152, 388652631, 397335639, 403365510, 411885063, 422747666, 430236736, 438984407, 447667415, 453828167, 464690834, 472179712, 478994119, 488162838, 496278607, 506093207, 514776215, 520805894, 529325703, 538502862, 546610319, 1073808391, 554360518, 563668494, 571776207, 580437590, 588553231, 596303430, 605593237, 613992150, 1074091014, 622370325, 630777486, 1075164106, 1077015562, 639147733, 647546518, 1077284808, 1074685897, 655924821, 664331854, 672841427, 1076276165, 681229843, 689618579, 1076555723, 698007123, 1076831180, 1076060109],
    [102, 88, 1, 351296, 10818624, 17120321, 25640064, 34028608, 42417344, 50805760, 59063425, 67452097, 77927424, 84639438, 92617729, 103093440, 109805070, 119870592, 126574287, 135118481, 1073747969, 145831507, 151346176, 160144914, 170997459, 176905871, 185310802, 195903188, 204551699, 210468494, 220699860, 229457556, 238106259, 244022862, 254254228, 263011860, 268786816, 280310913, 287808532, 296566356, 305476609, 311123471, 321363028, 330774039, 336289359, 344833617, 352672960, 364196929, 372350552, 378625236, 389362881, 397516504, 406271703, 412179604, 1075334084, 422682264, 431437463, 437345300, 1074308037, 447847960, 456603223, 462511188, 470523602, 481123397, 490419733, 498441945, 506289349, 515585685, 523607705, 531454981, 540751573, 548773465, 556620933, 565917269, 573939225, 1075893186, 580458128, 588734166, 596491985, 1074866120, 605623888, 613899862, 621518482, 630789840, 639065750, 646823441, 1076184003, 655955472, 664231446, 1073848267, 1075702726, 672882394, 681262298, 1076498380, 1074681801, 689659546, 698039450, 1075228615, 706436634, 714816538, 1076818893, 1077097485, 723213914, 731593818, 1077364682],
    [122, 108, 10, 2014209, 10822721, 18685120, 27073664, 35462208, 43850752, 52370433, 60759105, 69147777, 77511809, 86320321, 94313665, 103242446, 111221966, 119454785, 128263297, 1073744835, 136519313, 1074287554, 145038863, 151616080, 161553934, 170206209, 178175169, 186851025, 195370575, 201947792, 1074829313, 212403794, 220642449, 228793937, 235502288, 245958354, 254196945, 260667920, 271656467, 279362641, 288169495, 296573007, 304922261, 311100439, 321723991, 330127375, 337714766, 344654935, 355376143, 363667159, 369696389, 380721285, 388046478, 394986711, 405707855, 413998743, 421731857, 431053381, 436804677, 445318295, 455523345, 461970949, 472995845, 480839314, 487136965, 498161861, 506005010, 1075363845, 514760399, 522525903, 531454159, 540091987, 548191957, 556080783, 565008527, 573646483, 581746261, 589781006, 598812371, 606912021, 614946894, 621872336, 632200335, 640112782, 647169558, 655793689, 664369748, 672335574, 681138327, 689348185, 697369680, 706158153, 714701524, 722535568, 731455115, 739712649, 748255764, 756457177, 764610134, 773398219, 781655561, 790190295, 798164630, 806952459, 815210185, 823753364, 831954585, 839975952, 1073812489, 848895563, 857299031, 866068056, 1075135499, 1074111430, 874076183, 882845400, 1075957706, 1074672588, 1077048332, 891233816, 1077323716, 899622552, 1076289485, 1075785671, 1076849608],
    [102, 88, 5, 1301632, 10310657, 17136640, 25525440, 33913920, 42302592, 50822209, 59210945, 67599489, 77419585, 85589582, 92765185, 103365136, 109673488, 119362689, 127532686, 136139969, 144309774, 1073747969, 153450193, 161087182, 169729615, 178869906, 186506895, 195647058, 203283983, 1075344323, 1076933635, 212424402, 220593362, 229980819, 237590034, 244415635, 253615823, 262501905, 271923795, 277970003, 286514368, 1077201860, 296056465, 305478355, 311524563, 321256530, 330643987, 336690195, 347035156, 354811026, 1074336709, 363412048, 372201108, 378109008, 387177472, 1074873282, 396719697, 405355152, 411663504, 421919762, 430521040, 436829392, 445897792, 456604360, 464475860, 472505474, 481769992, 489641556, 497802372, 1073848712, 506681045, 515323976, 521633290, 1075964870, 531356868, 540235285, 548878472, 555187850, 564780034, 573789781, 580721366, 1076502471, 590208069, 598955669, 605887062, 615111746, 1075736521, 622664342, 632019972, 639441430, 648928389, 656358039, 664239690, 673832130, 681523927, 689405642, 699128900, 1076792330, 1074718667, 706689623, 716037317, 723466775, 732814341, 1076299724, 1074223053],
    [110, 96, 9, 353408, 10312705, 18701377, 27090113, 35478657, 43998400, 52386880, 60767746, 69164032, 75850816, 85941376, 94322242, 1073744642, 101008514, 1074287555, 111599118, 117923471, 128400527, 134831813, 142951490, 153672901, 159866383, 1074829313, 170343439, 176774661, 185558145, 195485262, 201809615, 212286671, 219244166, 229039822, 235363919, 245840975, 252003330, 262724613, 269172368, 277694151, 287760014, 294215301, 302726736, 310723778, 321444997, 327769669, 336281104, 344802887, 1075367239, 1074593797, 354999365, 361447120, 370238982, 380567058, 387923138, 395798165, 1073831558, 403660489, 414121554, 421477506, 429352661, 437214857, 447676114, 456212052, 461726720, 1075688392, 1077015560, 470875798, 481378004, 488072789, 498007698, 506543636, 513238549, 521207510, 531709588, 538265239, 1077291972, 546373142, 554647057, 563176518, 571432521, 580320984, 588586582, 596985367, 604986889, 613875288, 622411347, 630015111, 1076515849, 638647382, 646921937, 1075225546, 655320129, 664354323, 672482903, 680984088, 689520275, 697123847, 706297555, 713385152, 1076031436, 722927256, 731192534, 739337414, 747585169, 756369111, 764746902, 772760577, 1076824011, 781523990, 789537985, 797916753, 1074227149],
    [102, 88, 13, 1719360, 8903808, 17153024, 25541696, 33930432, 42318976, 50838529, 59227265, 67615937, 77216768, 84540942, 92781633, 102382784, 109706894, 119159936, 126484174, 1073747969, 136060418, 143261262, 152821457, 161226306, 169598545, 178003586, 185186002, 194780866, 202235535, 1075340290, 210351698, 219012687, 229391888, 1076145091, 238393043, 245096081, 254418566, 1076417476, 261078599, 271947411, 279576213, 287972934, 294633159, 305501715, 313130709, 321666768, 330667603, 338296341, 346832528, 353081047, 363462229, 371859142, 1074867270, 378377748, 388488841, 397164112, 403412631, 413654537, 422190086, 428578327, 439500377, 447209161, 454276760, 464666265, 472374857, 1076715529, 479041108, 489832153, 496754193, 1075939275, 1074124744, 504207060, 514997785, 521002703, 529372820, 537796310, 546168335, 554679943, 562796119, 570940416, 579739286, 588234247, 596227730, 605667021, 612883520, 621682198, 1075190791, 1075728332, 631092890, 639221261, 646438080, 655236694, 663992024, 672775821, 1074693061, 681424410, 689552973, 1073924109, 696890898, 706590426, 714323544, 1074475978, 1077113866, 722712088, 731756122],
    [126, 112, 11, 2458689, 10737857, 18717696, 27106368, 35495104, 43883648, 52403393, 60791937, 69180481, 78095874, 86235137, 94346241, 103104068, 111385668, 1073744770, 120038594, 128178305, 1074287555, 136658628, 144940228, 153592962, 161732673, 168271503, 1074829313, 178758722, 187553923, 195772048, 201825999, 210345553, 221226065, 229497027, 237706321, 243768847, 252288657, 263169169, 271439939, 279649425, 285711951, 294231569, 305112081, 313382915, 321592337, 329490052, 336174801, 346683524, 355443921, 363150468, 371432964, 378664975, 389260814, 1075372036, 396704772, 405642834, 413792260, 422815310, 430644433, 439197394, 445774031, 456369806, 464207568, 472751634, 480901316, 489924302, 1075908549, 497761872, 506306194, 512882767, 522552513, 531316240, 538418836, 548010052, 556106753, 563584596, 571603087, 581272705, 588750356, 598865938, 605783107, 613916372, 624031890, 630948995, 638664213, 647601674, 657586258, 664503491, 672611990, 681156234, 689800261, 699529426, 706166486, 714710730, 722982996, 731743237, 739720726, 748265034, 756930634, 765297797, 1074611210, 773275222, 782096586, 790332419, 800399063, 1074108359, 806869012, 815769299, 1075180488, 1077031944, 825564823, 832428170, 840934931, 850730519, 1077307334, 857593866, 866100819, 875896407, 882366612, 891126981, 1076273099, 1075758028, 898711189, 907532500, 916432531, 923876949, 932265685, 1073949645, 1076588489],
    [118, 104, 9, 2070592, 10517697, 17169409, 25558081, 33946817, 42466432, 50855104, 59243520, 67632192, 77568128, 86015105, 92667009, 101308041, 1073749954, 111122432, 119569473, 127899840, 136346625, 143259212, 1075599361, 153247370, 162110027, 168425100, 1075359744, 1076950016, 178887307, 187063436, 193590796, 202112709, 211967562, 218756812, 227392205, 237108814, 244055685, 254172172, 1077218244, 1074359300, 263050318, 271554638, 279051918, 285998597, 296115404, 304993422, 313498126, 319684230, 329382926, 336330309, 346848320, 1076726789, 1074653189, 355324942, 363829390, 370015814, 378535495, 388791488, 396990987, 405657294, 413269198, 422345856, 428463817, 439326926, 446848714, 456381968, 464100043, 472014346, 481547984, 487692945, 497441868, 503961097, 512753159, 521247441, 531397632, 538155667, 548656784, 556686532, 563190353, 571070025, 581852292, 588487379, 598988368, 605028039, 615406596, 622041683, 630707861, 638582407, 648961092, 1076499463, 655596051, 664524436, 674258578, 680630801, 689690132, 697171654, 707812882, 1075201992, 1074176008, 713931405, 722982613, 730725894, 741367378, 1076023302, 747485709, 756799060, 766533330, 772651597, 781579862, 790265423, 798357142, 807042767, 1074987971, 1073964035, 815519444, 823819791, 832034389, 840597135, 848688854, 857077270, 865588757],
    [114, 100, 9, 2202753, 8772608, 17161280, 25550016, 33938560, 44145729, 51215945, 59238090, 68672585, 77700097, 1073744835, 1074285571, 1074566082, 1074850818, 84770441, 95012356, 101309444, 110747212, 119004297, 128171084, 1076696064, 135233165, 144828107, 151641732, 1075140609, 161078924, 1075420161, 170114188, 1075701760, 177176269, 186771019, 193584836, 1076506625, 203021836, 1077048321, 212057100, 219119117, 228713995, 235527748, 244965068, 254000332, 1077313540, 262268555, 269450829, 279026881, 285992655, 294485513, 303553545, 312851520, 319546959, 328040137, 337108169, 346406080, 353101327, 361987793, 371571712, 1073924037, 378005002, 387153553, 396737664, 405765780, 411821711, 421780628, 430554253, 439320276, 447604371, 455335124, 464108621, 472874516, 481289938, 488889364, 497662989, 506429012, 514844306, 522443860, 531217613, 538148433, 545777290, 556646094, 563314193, 570943050, 581811854, 588873301, 598730258, 606977550, 614039061, 623494340, 632143438, 639205077, 648930899, 656121552, 1074209735, 664370837, 673825924, 681287184, 689528534, 698991684, 706453136, 714694230, 724559442, 731618896, 1076062150, 739859990, 749594323, 756792840, 765025942, 774759955, 781958792, 790480407, 798735944, 807257815, 815513288, 824034903, 832423575],
]


def fill_table(table, me, low, high):
    if high - low == 1:
        for place, word in enumerate(STEPS[low]):
            table[place] = jnp.int32(word)
        return
    middle = (low + high) // 2
    lax.cond(
        me < middle,
        lambda: fill_table(table, me, low, middle),
        lambda: fill_table(table, me, middle, high),
    )


def neighbours(col, row):
    x = lax.rem(col, 2) * 2 + lax.rem(row // 2, 2)
    y, z, core = col // 2, row // 4, lax.rem(row, 2)
    found = [(x, y, z, 1 - core)]
    for move in (1, 3):
        for other in range(2):
            found.append((lax.rem(x + move, 4), y, z, other))
            found.append((x, lax.rem(y + move, 4), z, other))
            found.append((x, y, lax.rem(z + move, 4), other))
    return [{"col": y * 2 + x // 2, "row": z * 4 + lax.rem(x, 2) * 2 + core} for x, y, z, core in found]


def split(value):
    high = value.astype(jnp.bfloat16)
    return high, (value - high.astype(jnp.float32)).astype(jnp.bfloat16)


def spread_kernel(
    stored_ref, slots_ref, halves_ref,
    table, tile_even, tile_odd, halves_even, halves_odd, load_sem, store_sem, send_sem, recv_sem,
):
    active, half, block = stored_ref.shape[2:5]
    rows_per = active // CHUNKS
    col, row = lax.axis_index("col"), lax.axis_index("row")
    beside = neighbours(col, row)
    sibling = beside[0]
    tiles = halves_ref.shape[0]

    barrier = pltpu.get_barrier_semaphore()
    for device in beside:
        pl.semaphore_signal(barrier, inc=1, device_id=device, device_id_type=MESH)
    fill_table(table, col * lax.axis_size("row") + row, 0, len(STEPS))
    pl.semaphore_wait(barrier, len(beside))

    def hop(source, slot, chunk, place, device):
        return pltpu.make_async_remote_copy(
            src_ref=source,
            dst_ref=slots_ref.at[slot, pl.ds(chunk * rows_per, rows_per)],
            send_sem=send_sem.at[place],
            recv_sem=recv_sem.at[slot, chunk],
            device_id=device,
            device_id_type=MESH,
        )

    def arrival(slot, chunk):
        piece = slots_ref.at[slot, pl.ds(chunk * rows_per, rows_per)]
        hop(piece, slot, chunk, 0, sibling).wait_recv()

    tile = (tile_even, tile_odd)
    halves = (halves_even, halves_odd)

    def load(source, turn):
        return pltpu.make_async_copy(source, tile[turn], load_sem.at[turn])

    def store(turn, role):
        return pltpu.make_async_copy(halves[turn], halves_ref.at[role], store_sem.at[turn])

    def prepare(turn, order, role):
        load(slots_ref.at[0], turn).wait()

        @pl.when(order >= 2)
        def _():
            store(turn, 0).wait()

        for mirrored in range(2):
            @pl.when((role & 1) == mirrored)
            def _():
                @pl.loop(0, active)
                def _(line):
                    for slot in range(half):
                        value = tile[turn][line, slot]
                        high, low = split(value.T if mirrored else value)
                        halves[turn][line * half + slot, :block] = high
                        halves[turn][line * half + slot, block:] = low

        store(turn, role).start()

    steps = table[0]
    sends = table[1]

    @pl.loop(0, steps)
    def _(step):
        word = table[3 + step]
        slot = word & 63

        @pl.when((word >> 30) == 0)
        def _():
            chunk = (word >> 6) & 7
            device = {"col": (word >> 10) & 7, "row": (word >> 13) & 15}
            landing = (word >> 17) & 63
            place = (word >> 23) & 127

            @pl.when(((word >> 9) & 1) == 1)
            def _():
                arrival(slot, chunk)

            @pl.when(slot < 2)
            def _():
                piece = stored_ref.at[slot, 0, pl.ds(chunk * rows_per, rows_per)]
                hop(piece, landing, chunk, place, device).start()

            @pl.when(slot >= 2)
            def _():
                piece = slots_ref.at[slot, pl.ds(chunk * rows_per, rows_per)]
                hop(piece, landing, chunk, place, device).start()

        @pl.when((word >> 30) != 0)
        def _():
            order = (word >> 14) & 15
            for chunk in range(CHUNKS):
                @pl.when(((word >> (6 + chunk)) & 1) == 1)
                def _():
                    arrival(slot, chunk)

            for turn in range(2):
                @pl.when((order & 1) == turn)
                def _():
                    @pl.when(slot < 2)
                    def _():
                        load(stored_ref.at[slot, 0], turn).start()

                    @pl.when(slot >= 2)
                    def _():
                        load(slots_ref.at[slot], turn).start()

                    @pl.when(order >= 1)
                    def _():
                        prepare(1 - turn, order - 1, (word >> 18) & 15)

    prepare((tiles - 1) % 2, tiles - 1, table[2])

    @pl.loop(0, sends)
    def _(place):
        hop(slots_ref.at[0, pl.ds(0, rows_per)], 0, 0, place, sibling).wait_send()

    for turn in range(2):
        store(turn, 0).wait()


def spread(stored):
    most = max(entry[1] for entry in STEPS)
    active, half, block = stored.shape[2:5]
    return pl.pallas_call(
        spread_kernel,
        out_shape=(
            jax.ShapeDtypeStruct((SLOTS,) + stored.shape[2:], jnp.float32),
            jax.ShapeDtypeStruct((14, active * half, 2 * block, block), jnp.bfloat16),
        ),
        in_specs=[pl.BlockSpec(memory_space=pl.ANY)],
        out_specs=(pl.BlockSpec(memory_space=pl.ANY),) * 2,
        scratch_shapes=[
            pltpu.SMEM((max(len(entry) for entry in STEPS),), jnp.int32),
            pltpu.VMEM((active, half, block, block), jnp.float32),
            pltpu.VMEM((active, half, block, block), jnp.float32),
            pltpu.VMEM((active * half, 2 * block, block), jnp.bfloat16),
            pltpu.VMEM((active * half, 2 * block, block), jnp.bfloat16),
            pltpu.SemaphoreType.DMA((2,)),
            pltpu.SemaphoreType.DMA((2,)),
            pltpu.SemaphoreType.DMA((most,)),
            pltpu.SemaphoreType.DMA((SLOTS, CHUNKS)),
        ],
        compiler_params=pltpu.CompilerParams(
            collective_id=0, has_side_effects=True, vmem_limit_bytes=24 << 20
        ),
        name="spread",
    )(stored)[1]


def multiply_kernel(
    halves_ref, rows_ref, offs_ref, krow_ref, kcol_ref, kcnt_ref, out_ref,
    blocks, done, pairs, pair_count, bucket, bucket_count, facts, in_sem, out_sem,
):
    grid = lax.axis_size("row")
    tile_j = lax.axis_index("row")
    col_id = lax.axis_index("col")
    tiles, each = halves_ref.shape[:2]
    half = offs_ref.shape[-1]
    active = each // half
    block = halves_ref.shape[-1]
    lanes, _, kept = krow_ref.shape
    slots = 2 * half
    steps = 2
    most = steps * slots * slots

    def load(place):
        return pltpu.make_async_copy(
            halves_ref.at[place], blocks.at[pl.ds(place * each, each)], in_sem.at[place]
        )

    for place in range(tiles):
        load(place).start()

    first = rows_ref[0, 0]
    bits = [rows_ref[0, 1] ^ first, rows_ref[0, 2] ^ first, rows_ref[0, 4] ^ first]

    def rank(value):
        return sum(
            jnp.where((value & bit) != 0, jnp.int32(1 << place), jnp.int32(0))
            for place, bit in enumerate(bits)
        )

    def shifts(tile_x, tile_y):
        both = ((tile_x, tile_y), (tile_y, tile_x))
        return [rank(offs_ref[x, y, slot]) for x, y in both for slot in range(half)]

    tile_is = [col_id * lanes + lane for lane in range(lanes)]
    tile_ks = [lax.rem(tile_is[0] + tile_j + place, grid) for place in range(3)]
    right_moves = [shifts(tile_k, tile_j) for tile_k in tile_ks]

    for place in range(lanes * active):
        pair_count[place] = 0
    for lane in range(lanes):
        for step in range(steps):
            left_moves = shifts(tile_is[lane], tile_ks[lane + step])
            for slot in range(slots):
                move = left_moves[slot]
                turn = move if slot >= half else 0
                left_base = (2 * (2 * lane + step) + slot // half) * each + slot % half
                for other in range(slots):
                    apart = move ^ right_moves[lane + step][other]
                    place = lane * active + apart
                    count = pair_count[place]
                    right_base = (8 + 2 * (lane + step) + other // half) * each + other % half
                    reach = move if other < half else apart
                    pairs[place * most + count] = (
                        turn | reach << 3 | left_base << 6 | right_base << 14
                    )
                    pair_count[place] = count + 1

    widest = 4
    room = 2 * lanes * kept
    for place in range(widest + 1):
        bucket_count[place] = 0
    for place in range(lanes * active):
        pair_count[place] = place << 3 | pair_count[place] << 7

    def put(size, word):
        filled = bucket_count[size]
        bucket[size * room + filled] = word
        bucket_count[size] = filled + 1

    for lane in range(lanes):
        count = kcnt_ref[lane, 0]
        together = 8

        @pl.loop(0, kept // together)
        def _(part):
            found = []
            for offset in range(together):
                item = part * together + offset
                row = rank(krow_ref[lane, 0, item])
                place = lane * active + (row ^ rank(kcol_ref[lane, 0, item]))
                found.append(jnp.where(item < count, pair_count[place] | row, 0))
            for offset in range(together):
                item = lane * kept + part * together + offset
                products = found[offset] >> 7
                facts[item] = found[offset] & 127
                begin = jnp.where(products > 0, ((products - 1) & 7) + 1, 0)
                put((begin + 1) >> 1, item | begin << 13)

                @pl.loop(0, (products - begin) >> 3)
                def _(more):
                    put(widest, item | (begin + 8 * more) << 7 | 1 << 12 | 8 << 13)

    blocks[tiles * each] = jnp.zeros((2 * block, block), jnp.bfloat16)
    for place in range(tiles):
        load(place).wait()

    def gather(word, size):
        fact = facts[word & 127]
        row = fact & 7
        base = (fact >> 3) * most + ((word >> 7) & 31)
        products = word >> 13
        ones, twos = [], []
        for place in range(2 * size):
            inside = place < products
            code = pairs[base + jnp.where(inside, place, 0)]
            source = ((code >> 6) & 255) + (row ^ (code & 7)) * half
            ones.append(blocks[jnp.where(inside, source, tiles * each)])
            other = blocks[(code >> 14) + (row ^ ((code >> 3) & 7)) * half]
            twos.append(jnp.concatenate([other[:block], other[block:]], 1))
        total = jnp.dot(
            jnp.concatenate(ones, 1), jnp.concatenate(twos, 0), preferred_element_type=jnp.float32
        )
        total = total[:block] + total[block:]
        return total[:, :block] + total[:, block:]

    def add(word, into, total):
        again = ((word >> 12) & 1) == 1

        @pl.when(again)
        def _():
            done[into] = done[into] + total

        @pl.when(jnp.logical_not(again))
        def _():
            done[into] = total

    @pl.loop(0, bucket_count[0])
    def _(place):
        done[bucket[place] & 127] = jnp.zeros((block, block), jnp.float32)

    for size in range(1, widest + 1):
        count = bucket_count[size]

        @pl.loop(0, (count + 1) >> 1)
        def _(place):
            start = size * room + 2 * place
            one = bucket[start]
            paired = 2 * place + 1 < count
            two = bucket[jnp.where(paired, start + 1, start)]
            total_one = gather(one, size)
            total_two = gather(two, size)
            if size < widest:
                done[one & 127] = total_one
                done[jnp.where(paired, two & 127, lanes * kept)] = total_two
            else:
                add(one, one & 127, total_one)
                add(jnp.where(paired, two, 0), jnp.where(paired, two & 127, lanes * kept), total_two)

    def store(lane):
        return pltpu.make_async_copy(
            done.at[pl.ds(lane * kept, kept)], out_ref.at[lane, 0], out_sem.at[lane]
        )

    for lane in range(lanes):
        store(lane).start()
    for lane in range(lanes):
        store(lane).wait()


def multiply(halves, tile_rows, offsets, kept_rows, kept_cols, kept_count):
    block = halves.shape[-1]
    half = offsets.shape[-1]
    tiles, each = halves.shape[:2]
    active = each // half
    lanes, _, kept = kept_rows.shape
    items = lanes * kept
    products = 2 * (2 * half) ** 2
    smem = pl.BlockSpec(memory_space=pltpu.SMEM)
    return pl.pallas_call(
        multiply_kernel,
        out_shape=jax.ShapeDtypeStruct((lanes, 1, kept, block, block), jnp.float32),
        in_specs=[pl.BlockSpec(memory_space=pl.ANY)] + [smem] * 5,
        out_specs=pl.BlockSpec(memory_space=pl.ANY),
        scratch_shapes=[
            pltpu.VMEM((tiles * each + 1, 2 * block, block), jnp.bfloat16),
            pltpu.VMEM((items + 1, block, block), jnp.float32),
            pltpu.SMEM((lanes * active * products,), jnp.int32),
            pltpu.SMEM((lanes * active,), jnp.int32),
            pltpu.SMEM((10 * items,), jnp.int32),
            pltpu.SMEM((5,), jnp.int32),
            pltpu.SMEM((items,), jnp.int32),
            pltpu.SemaphoreType.DMA((tiles,)),
            pltpu.SemaphoreType.DMA((lanes,)),
        ],
        compiler_params=pltpu.CompilerParams(vmem_limit_bytes=32 << 20),
        name="multiply",
    )(halves, tile_rows, offsets, kept_rows, kept_cols, kept_count)


def local(stored, tile_rows, offsets, kept_rows, kept_cols, kept_count):
    halves = spread(stored)
    return multiply(halves, tile_rows, offsets, kept_rows, kept_cols, kept_count)


def solution(mesh):
    in_specs = (
        P("col", "row", None, None, None, None),
        P(),
        P(),
        P("col", "row", None),
        P("col", "row", None),
        P("col", "row"),
    )
    out_specs = P("col", "row", None, None, None)
    return jax.shard_map(local, mesh=mesh, in_specs=in_specs, out_specs=out_specs, check_vma=False)
```

time: 771 us -> 138 us (0.18)
  the two profiles are of different devices: /device:TPU:42 before, /device:TPU:5 now
where the time goes in v4:
time: 138 us
  Pallas kernels  122 us (88%)
  local copies, waits for them, and re-layouts  15.7 us (11%)
    pallas_call x1, Pallas kernels, spread(): pl.pallas_call(spread_kernel, out_shape=(jax.ShapeDtypeStruct((SLOTS,) +...  104 us
    pallas_call x1, Pallas kernels, multiply(): pl.pallas_call(multiply_kernel, out_shape=jax.ShapeDtypeStruct((lanes, 1,...  18.2 us
    unnamed x13, local copies, waits for them, and re-layouts  15.7 us

profile of v4, /device:TPU:5, one launch (start us, length us, event | category | flops | bytes accessed | tf_op | source)
XLA Modules:
  0.0 137.8 jit_solution(5288847993269531685)
XLA Ops:
  0.0 0.0 copy-start.2
  0.0 1.6 %copy-done.2 = f32[2,1,8,2,128,128]{5,4,3,2,1,0:T(8,128)S(1)} copy-done((f32[2,1,8,2,128,128]{5,4,3,2,1,0:T(8,128)S(1)}, f32[2,1,8,2,128,128]{5,4,3,2,1,0:T(8,128)}, u32[]{:S(2)}) %copy-start.2) | copy-done | bytes 2097176
  1.6 103.9 %spread.1 = (f32[33,8,2,128,128]{4,3,2,1,0:T(8,128)}, bf16[14,16,256,128]{3,2,1,0:T(8,128)(2,1)S(1)}) custom-call(f32[2,1,8,2,128,128]{5,4,3,2,1,0:T(8,128)S(1)} %copy-done.2), custom_call_target="tpu_custom_call" | custom-call | tf_op jit(solution)/shard_map/spread/pallas_call | solution.py:298
  105.5 0.0 copy-start
  105.5 5.2 %copy-done = bf16[14,16,256,128]{3,2,1,0:T(8,128)(2,1)} copy-done((bf16[14,16,256,128]{3,2,1,0:T(8,128)(2,1)}, bf16[14,16,256,128]{3,2,1,0:T(8,128)(2,1)S(1)}, u32[]{:S(2)}) %copy-start) | copy-done | bytes 14680088
  110.7 0.9 copy.8.offs_ref
  111.6 0.8 copy.7.rows_ref
  112.4 0.7 copy.9.kcnt_ref
  113.1 0.0 copy-start.1
  113.1 5.2 %copy-done.1 = bf16[14,16,256,128]{3,2,1,0:T(8,128)(2,1)S(1)} copy-done((bf16[14,16,256,128]{3,2,1,0:T(8,128)(2,1)S(1)}, bf16[14,16,256,128]{3,2,1,0:T(8,128)(2,1)}, u32[]{:S(2)}) %copy-start.1) | copy-done | bytes 14680088
  118.3 0.0 copy-start.3
  118.3 0.7 copy-done.3
  119.0 0.0 copy-start.4
  119.0 0.7 copy-done.4
  119.6 18.2 %multiply.1 = f32[2,1,32,128,128]{4,3,2,1,0:T(8,128)} custom-call(bf16[14,16,256,128]{3,2,1,0:T(8,128)(2,1)S(1)} %copy-done.1, s32[16,8]{1,0:T(8,128)S(1)} %copy.7.rows_ref, s32[16,16,2]{2,1,0:T(8,128)S(1)} %copy.8.offs_ref, s32[2,1,32]{2,1,0:T(1,128)S(1)} %copy-done.3, s32[2,1,32]{2,1,0:T(1,128)S(1)} %copy-done.4, s32[2,1]{1,0:T(2,128)S(1)} %copy.9.kcnt_ref), custom_call_target="tpu_custom_call" | custom-call | tf_op jit(solution)/shard_map/multiply/pallas_call | solution.py:496
Async XLA Ops:
  0.0 1.6 %copy-start.2 = (f32[2,1,8,2,128,128]{5,4,3,2,1,0:T(8,128)S(1)}, f32[2,1,8,2,128,128]{5,4,3,2,1,0:T(8,128)}, u32[]{:S(2)}) copy-start(f32[2,1,8,2,128,128]{5,4,3,2,1,0:T(8,128)} %stored_ref.1) | copy-start | bytes 6291460
  105.5 5.2 %copy-start = (bf16[14,16,256,128]{3,2,1,0:T(8,128)(2,1)}, bf16[14,16,256,128]{3,2,1,0:T(8,128)(2,1)S(1)}, u32[]{:S(2)}) copy-start(bf16[14,16,256,128]{3,2,1,0:T(8,128)(2,1)S(1)} %get-tuple-element.6.halves_ref) | copy-start | bytes 44040196
  113.1 5.2 %copy-start.1 = (bf16[14,16,256,128]{3,2,1,0:T(8,128)(2,1)S(1)}, bf16[14,16,256,128]{3,2,1,0:T(8,128)(2,1)}, u32[]{:S(2)}) copy-start(bf16[14,16,256,128]{3,2,1,0:T(8,128)(2,1)} %copy-done) | copy-start | bytes 44040196
  118.3 0.7 copy-start.3
  119.0 0.7 copy-start.4

commit v5 on v4

v5 whole, which is shorter than its diff:
```python
import jax
import jax.numpy as jnp
from jax import lax
from jax.experimental import pallas as pl
from jax.experimental.pallas import tpu as pltpu
from jax.sharding import PartitionSpec as P

MESH = pl.DeviceIdType.MESH
CHUNKS = 4
SLOTS = 33
STEPS = [
    [118, 104, 12, 1851393, 9576640, 17965056, 26353792, 34742336, 42213377, 50602177, 58990721, 69223106, 75767873, 84286154, 92963528, 102113929, 1073746370, 1074811906, 111558793, 1075088323, 1074326531, 119675597, 128090700, 135799499, 1076690944, 1073824768, 144720002, 1074105345, 151394826, 161645260, 169353739, 178929675, 1074651136, 1075979264, 1076258817, 187185861, 193626760, 201990341, 211165705, 220217346, 227287750, 237116045, 245531276, 252322373, 261628491, 269369484, 277619270, 287848517, 295862796, 302653957, 311829193, 321273865, 327950854, 338180101, 346718927, 352985733, 362291851, 371867787, 1076540421, 378282630, 388511877, 397050511, 404103753, 413548617, 1077337094, 419830410, 429670465, 438835728, 445284872, 455491785, 462062152, 472390288, 479084620, 488774221, 496779457, 505944784, 512664211, 521027596, 530070033, 539656783, 548552840, 554048074, 565215829, 572276865, 581048845, 588161747, 598360139, 605567569, 615547605, 624050184, 1075780548, 631773776, 640320015, 648036418, 656161490, 663659091, 674652814, 681065105, 691045013, 699547848, 707803732, 716210709, 724189387, 731396817, 739156499, 750150222, 1075540935, 756824722, 765100566, 772686028, 781990418, 790266518, 800211016, 808467092, 815432278, 825647822, 832322130, 840598230, 850813454, 858798804, 867187220],
    [106, 92, 13, 1860608, 10321984, 17039553, 25428033, 33816705, 42205185, 50725056, 59113536, 67502080, 77430912, 85746816, 92668032, 102917769, 110985216, 117713547, 1073743810, 126354052, 1074020352, 136078528, 143622794, 153365196, 159908420, 170288332, 178627213, 1073782785, 1075897345, 186919436, 194798656, 202342986, 209988107, 220358153, 229343817, 237906574, 245785612, 254517904, 262416972, 270689993, 279290445, 288238286, 296117900, 304849616, 1076169669, 313403918, 319291908, 1074354118, 1075161094, 330006537, 338715652, 346958414, 354575433, 363569680, 371468428, 380658756, 388735568, 394537675, 405824644, 412058122, 420358739, 430335052, 438673933, 445655700, 454313685, 462389962, 470682198, 480084160, 487867989, 495856339, 503841476, 514556041, 523265220, 1076482052, 1074932740, 529664658, 538199573, 547726029, 554576403, 562954823, 573276361, 580273873, 588384786, 596509383, 605308565, 614179535, 621816404, 630063751, 638994065, 647733775, 655239827, 663618055, 672548369, 681288335, 1076775943, 688925204, 698065487, 1074700232, 1075769352, 705563286, 714491473, 722340374, 1077091267, 1075540995, 730868436, 739379922, 746859083, 756157010, 764283606],
    [142, 128, 10, 2368576, 8673472, 18636929, 27025601, 35545280, 43802689, 52191233, 60710912, 69099584, 77865984, 86399554, 94265472, 103047694, 111567364, 1073744706, 119953538, 127796228, 1074287555, 136864464, 1074823168, 142893649, 153508034, 161481809, 170050130, 176579270, 185098899, 193225361, 203839490, 211944595, 218522246, 229139088, 235168273, 246176399, 253756433, 260629012, 269246997, 277111505, 288249870, 295699665, 304267794, 313025040, 321282628, 330062543, 337642641, 346211026, 353264263, 361783944, 371467456, 380786704, 388948566, 394813971, 405168772, 412115464, 422729872, 430048275, 439140373, 445407893, 455500484, 464672976, 471729348, 1073803268, 481083541, 487088723, 497834511, 505545811, 512123462, 523166422, 530866766, 539908174, 547226756, 554066438, 565109398, 570974931, 581720655, 589432019, 1076956166, 598663702, 604922439, 613442120, 621041792, 631112772, 639812242, 648307406, 656680064, 665737422, 672195096, 680419847, 688939720, 696539136, 706356232, 1074616328, 714138328, 722756249, 730093632, 739509401, 747692696, 757359246, 766400654, 773596295, 780722900, 789340757, 798631112, 806771333, 1075414725, 816627797, 823419417, 832337926, 840172569, 847831636, 858284624, 867326032, 874259527, 881910360, 890905672, 899446918, 907469463, 915694297, 924612806, 932447449, 1074132937, 941023959, 948724437, 958014600, 966154437, 1077289930, 1075995658, 976011477, 982931461, 991699975, 998826644, 1007575751, 1016887366, 1025254599, 1076272135, 1033298519, 1041523289, 1050040389, 1058276441, 1075763149, 1066852887, 1075261387, 1076849612],
    [102, 88, 9, 401537, 10076353, 17055808, 25444544, 33832960, 42221696, 50741249, 59129985, 67518529, 76030606, 85573697, 92684481, 103303888, 109584974, 119128193, 126501457, 136858128, 1073741824, 143262415, 152682497, 162024080, 168428111, 176677588, 187189840, 193593871, 201974290, 213019158, 218759823, 227271381, 237914711, 245883589, 253755923, 1073771458, 263350998, 268968462, 279437957, 287826437, 295699027, 305293910, 312476307, 321635032, 327828177, 336612057, 346030803, 355189400, 364014230, 371859458, 380355160, 1076928457, 386943577, 394912338, 405414082, 414075543, 422191170, 428982810, 1075627971, 1074076612, 439241239, 445129422, 455598661, 1075407877, 462045713, 472795863, 478798546, 489300098, 495995545, 504242257, 512483861, 1076728776, 520766097, 529549849, 537796817, 548127256, 554295954, 562962577, 571351057, 579592853, 587603969, 596370005, 605702811, 612885140, 621158593, 631139036, 637935681, 647086682, 656304732, 663216660, 673081884, 680641242, 1074908102, 1074408395, 1076525005, 689859228, 696771156, 706366043, 714195610, 1077319623, 723143387, 1075236810, 731531803, 1074734028, 1076061196],
    [110, 96, 10, 2275328, 10543105, 18677761, 27041856, 35430592, 43819008, 52207744, 60995648, 69263489, 77669058, 1073746370, 86161600, 94445570, 100983311, 1074809795, 1074298880, 111327360, 119611522, 126149327, 134912001, 144777282, 151315023, 161284161, 168343682, 176734739, 185115335, 195371207, 201900627, 210680340, 220004481, 226812559, 235838149, 243835463, 252229634, 262479943, 269009619, 277389959, 285784130, 296034439, 302563987, 1073800132, 1075913732, 311075541, 320921665, 329056449, 336894609, 1076195270, 344629909, 353015937, 363921943, 372294226, 378053127, 388030657, 396697607, 403618452, 1076729863, 411998725, 422642263, 431014418, 437172820, 445850198, 456180370, 1075430789, 1074149321, 462723665, 472957650, 479404566, 489997008, 496286283, 504013397, 514917015, 523551312, 529840779, 540082903, 546609873, 556982862, 1077302859, 563552856, 571390676, 582271504, 588718808, 596949003, 607314574, 613065237, 622107153, 632480462, 638788246, 647280843, 657646094, 664216216, 1075229640, 674546320, 680433733, 689381912, 696948929, 706396309, 714285782, 722114625, 731562005, 739942925, 1077071820, 747157698, 756728021, 765108877, 772708485, 781893717, 790274637, 798663373, 1074732045, 1075801034],
    [114, 100, 5, 1869888, 9568385, 17072193, 25460929, 33849473, 42237953, 50757632, 59146304, 67534976, 76939982, 85755904, 92700864, 103597583, 109608975, 118882830, 127699072, 137283088, 143425552, 1073741824, 152864960, 160563201, 170837712, 176980176, 185991758, 195471874, 204392080, 210534544, 219283649, 229026370, 237815503, 243826895, 253100686, 262843076, 271369807, 277381199, 286392385, 296135298, 304924303, 310935695, 321135171, 330213969, 338609744, 344752208, 354820676, 363505732, 370075156, 380534804, 387089043, 396763332, 405973650, 414246549, 422478420, 429032019, 438837250, 447916754, 456442963, 462586387, 472391810, 481471058, 489998035, 496140499, 506208320, 1073762628, 1074829826, 515025426, 523551763, 530850499, 540445206, 548464341, 556016259, 1075365955, 563643015, 573220868, 579789908, 590250644, 598089732, 606775428, 613344980, 623804628, 631513091, 640067778, 649381011, 656941122, 664306375, 674147025, 680453268, 690364548, 699828822, 706660055, 715923648, 724994710, 733013525, 741089408, 1074342854, 748192327, 758032913, 765380183, 1076453317, 774643712, 783198865, 790546071, 799547586, 808880854, 816899669, 823689735, 832488983, 1075676167, 1074130888, 1076770761, 1077310412, 1077060555, 1076028427, 1076301770, 1074747341],
    [118, 104, 5, 2401280, 10803264, 18669697, 27058369, 35446785, 43966592, 52355136, 60743680, 69001281, 77912064, 86419074, 94298304, 102711951, 111337615, 1073744578, 119855232, 128230528, 1074287555, 136266447, 144892111, 1074823168, 153409728, 161915970, 170345104, 178970768, 187081730, 196016272, 203375183, 212000847, 220636354, 227072590, 238109265, 245555727, 254059712, 260627086, 270483471, 277537284, 288023248, 296395780, 305068240, 312950992, 319480388, 329966160, 338338884, 347011152, 355549713, 363111488, 372570708, 380715729, 386589380, 397074960, 405447876, 414119952, 422002704, 428532356, 439002244, 445709011, 1073797124, 455827990, 462456339, 470874771, 1075394501, 481903125, 487651347, 495888087, 507069141, 512665175, 522666064, 529326809, 537953427, 548364505, 554492441, 562996887, 573530137, 579926611, 1077233607, 588285011, 599063252, 607208081, 613212761, 622232654, 631036506, 641286805, 647399118, 657416281, 663279822, 672827026, 682320534, 691337748, 697098905, 706381522, 1074114505, 716136601, 724892308, 731285006, 741040726, 747165710, 1076751307, 756057299, 765254170, 775504469, 781878802, 1076507592, 790420122, 798712344, 1077043148, 806266391, 815586010, 823878232, 831947918, 841704150, 848987730, 857432792, 1075749834, 1076028426, 865821336, 1076301766, 1074747341],
    [114, 100, 7, 2418752, 8691777, 18899137, 25477184, 33865856, 42254336, 50643136, 59162817, 67551233, 75939905, 86304896, 92577793, 102785025, 109494401, 117875407, 128248000, 136339585, 1073741824, 143041103, 153116737, 160090771, 168723150, 179069442, 187222740, 193241217, 204235458, 210422355, 219169424, 227443278, 238479554, 244335120, 252609166, 262720148, 269271556, 280422978, 288120898, 296264195, 305588866, 313680598, 321430083, 1073764354, 329574400, 336495118, 346841218, 353288791, 1075360515, 361808472, 369402049, 381085698, 389177942, 394699407, 403718736, 411749075, 1076941765, 420528856, 428253711, 439509526, 445563607, 453691923, 462439120, 472424579, 479117975, 489841302, 497590467, 504283671, 512901845, 523149528, 529580696, 538600017, 548315288, 555270664, 563233365, 573481048, 580436680, 589875732, 596787861, 605201106, 613991048, 623430228, 630874833, 638886039, 646759108, 656067161, 663896597, 672309778, 681233049, 689594897, 697606167, 705479236, 1074858950, 714787545, 722518552, 731538065, 741253144, 748208712, 756730393, 1074353160, 764584530, 1075163079, 773777946, 781361810, 790555226, 798269655, 807332506, 815046743, 1076754378, 822919812, 832498394, 1077281796, 1074160585, 1076012041, 1076292556, 1076563915, 1074749389],
    [86, 72, 13, 2430976, 10453056, 18686017, 27074561, 35463361, 43851905, 52762816, 61309442, 69288655, 1073744770, 77928576, 86474882, 1074287555, 94454287, 1074823168, 103094336, 111640642, 120144530, 128417986, 137443920, 145310290, 153059328, 162469953, 169951887, 178225280, 187775696, 195641874, 203391168, 212801537, 220283471, 229483022, 238107152, 246759955, 254648974, 263273104, 271925843, 279814734, 288299201, 297091795, 305076353, 313491972, 322257555, 330146510, 336534225, 346907284, 355435204, 362093142, 372072980, 380600900, 387258902, 1073797380, 396968658, 405766276, 412432920, 422404820, 428808785, 1075389381, 1075930117, 437338320, 445585937, 455959124, 462756566, 470892624, 479541912, 1076212678, 488063637, 496319192, 504446992, 512694929, 521626327, 529873496, 538395157, 546642582, 555180631, 1077008327, 563569303, 571555984, 1075195849, 580338261, 588734999, 1076776906, 1074700236, 1075759051, 1074211784, 597115605, 1076590541],
    [102, 88, 10, 2450560, 10387457, 19212353, 25493568, 33882112, 42270848, 50659520, 59179137, 67567809, 75956289, 86336512, 94709889, 102662337, 109510657, 119734863, 128279616, 136216641, 145304258, 153289231, 1073741824, 161907214, 170469890, 179135503, 186843791, 195461710, 204024450, 212690063, 220398287, 228491393, 237578818, 246244559, 1073764354, 254478992, 262570702, 271410255, 277414532, 287663296, 296125070, 304424961, 310969028, 321168003, 330524370, 338634948, 344523268, 355411972, 363111107, 372467282, 380831939, 388276803, 397633170, 405997635, 413442563, 422774787, 1075349507, 429294291, 436798020, 447686724, 1074319364, 454459987, 462636628, 472852612, 481519122, 488014483, 498272387, 504791571, 513631766, 521470537, 531302992, 538527317, 548080144, 555024905, 563693077, 573246160, 1074869189, 580470485, 589637825, 597517974, 605882897, 1076983752, 614024853, 622660177, 1077256135, 630784652, 639460950, 647826129, 655950412, 663963348, 672991889, 680854153, 689129108, 697893580, 706569942, 1075700683, 1075979275, 714294804, 722797257, 731447820, 1076252618, 1074693129, 1074189324, 1075261382, 1076849613],
    [110, 96, 7, 2447488, 10313793, 18702337, 27222080, 35610624, 43868289, 52388032, 60776576, 69556416, 77422785, 86333440, 1073744835, 1074287554, 1074823168, 94722112, 102621839, 109520592, 120412686, 127787727, 137307794, 145578574, 153477779, 160106193, 170744526, 178766484, 185271825, 195519127, 204298894, 212320852, 218572432, 226976344, 237730453, 245875220, 252380817, 262896213, 270393871, 277546577, 288061973, 295559759, 305079826, 311255578, 319250968, 328423444, 338543194, 347023058, 353198170, 361194200, 371679767, 378755220, 388874970, 395141338, 405743186, 412449371, 422429338, 428695706, 439551192, 447445717, 455467731, 464716824, 472343127, 479549980, 489537562, 498271320, 504715996, 514187859, 521348825, 531063511, 538139348, 547864788, 554116688, 563444443, 572908051, 580215496, 588711510, 596858964, 607109333, 615712408, 621240472, 630553243, 640663637, 647431830, 655712840, 1073795015, 664107547, 674218005, 679945744, 689265308, 699383957, 706552983, 714433032, 722929366, 731063961, 1074599878, 739596892, 748496087, 1075147716, 756229721, 1076987850, 765273175, 773153416, 1074124808, 781649430, 1075454924, 1075995660, 790438935, 798172697, 1076279237, 1077342155, 1076833225, 1076584397],
    [98, 84, 13, 2312384, 8724673, 17121281, 25641152, 34029632, 42418176, 50675777, 59195520, 67453057, 77809664, 84221953, 92618945, 102975552, 109387905, 118047312, 1073741824, 128141440, 134553665, 143073935, 151603919, 159982222, 168388673, 176866001, 185158159, 193536718, 203997778, 210313742, 218720385, 227197457, 235489871, 243736783, 252363345, 260513871, 269568724, 277291023, 285829121, 294306449, 302588494, 311511700, 321462352, 328288788, 336152719, 346890754, 353724949, 361832979, 370590358, 1073761222, 378104001, 386998931, 396935890, 405611138, 412174932, 420430409, 429310486, 437330515, 445596297, 456870615, 462865110, 470885075, 479150793, 490424855, 497598994, 504316425, 514376338, 523051586, 1074299913, 529973846, 539566800, 545865936, 1074061253, 1075646403, 557533783, 563405528, 573121168, 579420304, 588606101, 596959896, 607865495, 613736984, 623715010, 1074622466, 630549077, 638902872, 648618512, 654917648, 664486413, 1076998087, 672875085, 680880853, 1076745162, 1074932684, 689652429, 1076517828, 1075487691, 1076028427, 698040973, 1076302861, 1075279816],
    [106, 92, 13, 1310912, 10330177, 18849856, 27107457, 35627200, 43884545, 52273345, 60799618, 69181440, 77202114, 85958784, 92914254, 101163537, 111254211, 1073746114, 118751232, 1074809283, 128041551, 134718033, 1074298880, 144808003, 152699010, 161473168, 168403653, 178362499, 186393235, 195027472, 203661959, 211793922, 218735109, 228336147, 236970704, 243901061, 253737026, 261890771, 270525008, 279159367, 287414275, 294232645, 303300736, 1073797125, 311403028, 321511495, 329234626, 337388115, 346145423, 352821969, 363575826, 370802754, 378512020, 388620423, 394764945, 405518930, 413270097, 420455124, 430031375, 437494358, 447462034, 455213073, 463585999, 471048726, 481016530, 488898693, 495567502, 504603350, 515086871, 522715222, 529121806, 538157718, 546570304, 554672724, 565418711, 573170183, 581148679, 588906498, 596501013, 607361623, 614727749, 624138903, 631890631, 639869127, 648544278, 1075385351, 654951118, 665059525, 671998613, 681705617, 689291284, 698613765, 705553109, 715260113, 1075136457, 722845844, 732430550, 1074111432, 1075962888, 739622996, 749207702, 755884629, 764788948, 1076243398, 1076523980, 1077059531, 1075761101, 1074737092, 1076852682],
    [110, 96, 11, 370753, 10347585, 17137793, 25526465, 33914881, 42303553, 50823360, 59211904, 69272142, 75988992, 84379726, 94233729, 101154880, 111608335, 117934734, 127788225, 1073741824, 136774287, 143100622, 152953857, 161546446, 170124352, 176654862, 187105999, 193694287, 203678848, 210993810, 220266510, 228844544, 235251713, 245432462, 252414159, 262399168, 270991439, 277857796, 285977233, 1073763204, 296166032, 303023300, 311274132, 320045650, 329720528, 336570902, 344974851, 354886160, 361736854, 370140739, 1074830083, 380052048, 387434057, 395291222, 405479960, 411797519, 420463748, 429359626, 439034456, 445622998, 454026371, 462619347, 470132929, 479192259, 1075366729, 1074335687, 487817746, 497754840, 504349764, 512600596, 522920600, 530039945, 537766612, 546505299, 555205833, 562801361, 571933205, 579569807, 588760073, 596869842, 605758039, 614303762, 622297802, 630923991, 639469650, 647463498, 656114381, 663945747, 671853137, 681280013, 689373909, 698189970, 1074623432, 1077000140, 706445965, 714277523, 721791105, 731349642, 740000333, 748094037, 755870292, 1077269514, 1075184653, 764871317, 772516369, 1074159563, 1075749826, 1076028418, 781918743, 790464722, 1076308933, 1076588486, 798696087],
    [98, 84, 10, 2589760, 9691329, 18079745, 26599552, 34988096, 43245633, 51765248, 60703234, 68411521, 78087360, 85319872, 95148748, 102646338, 1073744642, 111641728, 1074287555, 120314444, 1074823168, 127811714, 134973005, 142991940, 153868940, 161211022, 169754818, 179012748, 187423244, 194765326, 1073803264, 204366416, 212304896, 220592783, 227247821, 237369871, 245097038, 254903438, 261251793, 271317650, 280069198, 286417425, 297130643, 303817422, 313230540, 319971921, 330685011, 338396236, 345137809, 355203666, 363955214, 372138640, 380369426, 388727820, 397304336, 406182419, 411797133, 422470352, 431610454, 439452878, 444981892, 456776406, 462128653, 470147588, 481942166, 488220245, 497810130, 505119830, 515496470, 521896982, 530971215, 538551957, 545645252, 557177555, 563717845, 1076960260, 571865748, 580617366, 590897879, 598080207, 605783254, 616063575, 1075665861, 622197332, 630826517, 641229335, 646963915, 655751892, 666395287, 1075419078, 1075176391, 1075979271, 672129547, 680917524, 1076260809, 688906891, 1076791242, 1074197514, 697295435, 1077349387, 1074752456],
    [106, 92, 9, 2326529, 8765440, 17154176, 25542848, 33931328, 42450945, 50839617, 59228289, 69435457, 76005569, 84640457, 1073741824, 93028873, 101051083, 109806217, 1073768448, 1076408321, 118194761, 126470798, 136945806, 143248078, 151732944, 160154116, 170098881, 178907794, 185164433, 193839813, 203653249, 210618895, 221086282, 227011283, 235627092, 246006293, 254640650, 263055381, 269443670, 279806666, 285731475, 294347412, 304972426, 311020046, 319775446, 329884238, 336062995, 346669653, 353059408, 363438094, 372107349, 380224149, 387015191, 395035204, 405381326, 414050453, 420438678, 429499021, 438954706, 445342228, 455721685, 463045196, 472770773, 479412888, 487310020, 496599564, 506063442, 512451284, 520995333, 530162381, 537389651, 545874513, 555328077, 564783634, 571687448, 579584644, 1076942786, 588882445, 595978763, 1075122180, 605119191, 613270149, 622428812, 629533323, 638673559, 646824517, 655983308, 663603855, 1074885637, 671703569, 680381007, 688874006, 696895566, 705905368, 1077251014, 1074383878, 713419339, 722158096, 730712783, 738812625, 1074666435, 1075469315, 747324048, 1075742663, 1074195463, 756236888, 764502615, 1076831176, 1076061192],
    [122, 108, 13, 1449152, 10363968, 18752704, 27272257, 35529728, 44049409, 52307072, 60826817, 68959820, 77603969, 85870285, 94125580, 102647373, 110902924, 119424525, 126363151, 136068812, 1073750016, 144590477, 1075865601, 154043984, 160179280, 169221184, 176965134, 187213457, 193864849, 203300421, 210519694, 221414996, 227288592, 236329984, 244204559, 254706704, 260843216, 269493909, 279321615, 286278805, 1076403142, 296649936, 302786192, 311827584, 321406487, 330204304, 336076499, 344737358, 355632660, 361637393, 369761814, 380126807, 388539409, 394798799, 404104857, 413539535, 420627609, 431130260, 437134929, 445654613, 454958597, 464012951, 472425553, 478684815, 487991001, 497425551, 504382549, 514369233, 521020625, 530456261, 538068185, 548570836, 554182223, 563619465, 572922959, 579618510, 588416667, 596254422, 604914831, 613713426, 621690394, 1075374018, 631785175, 638748379, 647374361, 656285317, 1076166661, 1073824773, 663635151, 672302683, 680535573, 688799450, 697320469, 705857051, 714090197, 721952339, 730875093, 1074114504, 740198104, 748168905, 755908186, 1076745155, 1074926595, 764560409, 773752472, 780672659, 789464143, 798918168, 806888969, 814358166, 1075203012, 823281241, 832472664, 840311897, 848832073, 856170003, 1074437129, 865371794, 873348762, 1075761095, 882149074, 889855574, 898926162, 1074738122, 1077114827],
    [126, 112, 12, 2327681, 9962561, 18351105, 26739841, 35259584, 43648128, 51905729, 60973647, 68813824, 78218959, 85591104, 95170132, 100927058, 109855440, 117835283, 128550415, 137113108, 142870034, 151798416, 159909378, 170099777, 179187285, 185205845, 195576337, 202114627, 212436047, 1073750017, 220999380, 227411525, 235561667, 244057283, 253985985, 262942356, 268961410, 277504643, 286000259, 296584210, 302515906, 311058947, 319554563, 328205910, 338265743, 1075859459, 344327827, 354960081, 363037697, 369757911, 379740367, 388858962, 394528466, 403456592, 412091926, 422413522, 1074831302, 430845461, 436864021, 445399568, 456632025, 462171672, 472400465, 481797657, 487219267, 495988314, 504734806, 512362197, 522346511, 531508437, 538289174, 547898001, 556928539, 563586192, 570820179, 581066895, 588000920, 599238297, 1075636169, 1076180935, 604243602, 613965843, 621416087, 630195926, 640517266, 1077235652, 646579861, 655909011, 665726101, 672507094, 680935554, 691146395, 697803856, 705562309, 714621125, 724700891, 730859158, 739615894, 746981075, 756564037, 766643803, 773301264, 781738195, 789327448, 798467280, 1074633672, 805832258, 815153218, 822742615, 1075429378, 831391365, 840450181, 848047832, 859285081, 864945669, 873873602, 881864410, 1073873925, 890650626, 898641562, 1074154443, 1074436044, 1075245005, 907558917, 915418650, 924344403, 931794455, 1076833230, 1076589514],
    [118, 104, 9, 2409664, 8944705, 18375680, 26764480, 35284033, 43541568, 51930240, 60449985, 68838529, 77907072, 84573708, 94004225, 101082754, 111461440, 118128332, 127664707, 134637122, 143156291, 153380559, 161793024, 168722126, 176947407, 186934863, 193887886, 202113103, 210298448, 220489231, 227442254, 235667471, 243852816, 254043791, 260734540, 269222031, 277399249, 286156294, 294289036, 302573200, 311322246, 319577167, 327739088, 335963650, 346578450, 1073748933, 352896529, 362545795, 369648771, 378562184, 386432001, 396100291, 403752659, 411591875, 420380174, 429654531, 436757507, 448185941, 453928518, 462183631, 1075344387, 470181570, 481740501, 487882253, 1077194754, 496551508, 505962194, 515172055, 520649921, 1076944836, 532071957, 537945672, 547905106, 557115031, 563373770, 573070994, 579871320, 590792341, 596928074, 604923590, 613703318, 1075644422, 1074359302, 621814296, 630244883, 638877261, 646980248, 657778263, 664036874, 672423638, 680534744, 689489620, 697722571, 705977942, 713606737, 722757258, 730883592, 738753665, 1076728842, 747161233, 756442763, 764438216, 773095053, 1075171336, 781239891, 789997067, 797727887, 806929940, 815029782, 823551563, 1074923463, 1074159623, 833938967, 839670799, 1076005899, 1074718731, 848873108, 856981197, 1076560841, 1073964041, 865126035],
    [114, 100, 1, 2499585, 8774785, 18367616, 26756096, 35144768, 43533504, 52052993, 60441665, 68830401, 75768832, 84272193, 93996161, 103181903, 111814220, 117819021, 126494285, 134595661, 145387205, 151537222, 160056517, 168043648, 176670224, 187330117, 193610821, 201598144, 210224784, 220622479, 227165701, 237380737, 243779280, 254438405, 262932113, 269215378, 277368532, 285886085, 296486417, 302769682, 1073745925, 1074818053, 313158789, 321529356, 328451606, 336088660, 344475270, 355206865, 361219664, 369643028, 380896910, 389006935, 396783119, 403195590, 413943320, 422192844, 428197389, 438726351, 447481425, 453764690, 1076661188, 462974549, 470304262, 481052248, 489038913, 498058903, 1074319299, 1074598918, 1075144710, 503860884, 514606744, 523503118, 529917080, 538472149, 546694232, 556410508, 563498521, 573834958, 580110038, 588926682, 596256461, 605275734, 613969557, 623658712, 630580440, 640033985, 1076462535, 647384665, 657720910, 665830935, 672812698, 679748672, 689161878, 697978458, 705307789, 716162775, 1073864649, 1075720201, 723144218, 731243544, 738862093, 1077044170, 748187157, 756418131, 763741389, 1076013000, 773213849, 781584083, 789309138, 1076288450, 1075524610, 798379737, 806749843, 814081217, 1077364683, 823526931, 830858241],
    [122, 108, 5, 302144, 10527744, 18916416, 27305152, 35693696, 44213313, 52601985, 61392400, 69379265, 75799680, 86156289, 94971522, 103335632, 111582865, 120137282, 126133972, 136890000, 145137169, 153953875, 159688340, 170444368, 176727637, 187080273, 195897043, 201631252, 212526292, 220904963, 229189122, 235185748, 246080596, 254721540, 263005843, 269002453, 280151684, 285916759, 296560147, 305316868, 313179779, 321693400, 330638982, 336111125, 346743828, 355908629, 1073746434, 363406530, 370206226, 378191383, 389490326, 395093595, 405988443, 411746007, 1074809797, 422913606, 428926610, 438738641, 447522456, 456467974, 461940373, 470869714, 480952003, 489465432, 498411206, 504145563, 515040411, 520797847, 531408408, 1074298886, 1073801347, 540485206, 546088667, 556983515, 565623893, 574039766, 579921490, 590789845, 599065816, 604808731, 615696068, 623819972, 632759830, 640869403, 649510037, 655926921, 666174616, 674416196, 682540100, 1076436996, 691340312, 699065492, 707705988, 714647241, 724894808, 733529301, 740998211, 1075928007, 748201545, 756876889, 767083669, 773495873, 781755913, 790431449, 800638037, 807050241, 1075416073, 815597081, 825803797, 830774272, 840763033, 849274522, 855940288, 1074655176, 866051802, 874159297, 882828890, 890936449, 1076758479, 899606042, 1074161611, 1076273100, 1075770317, 1077098446, 1077368778],
    [106, 92, 3, 1836032, 10403969, 18908160, 27296832, 35685504, 44074176, 52593857, 60982337, 69370881, 77333632, 85901505, 94536833, 103583250, 111198864, 117843537, 129011347, 134620881, 144621633, 153915026, 160073411, 168175249, 178176001, 187731539, 193627715, 203473616, 210118161, 221285907, 228639312, 237634689, 246853189, 252609605, 263071443, 271376579, 1073744834, 280407749, 285902467, 294552773, 304136720, 312214592, 321687250, 330311189, 338485315, 347114707, 353011203, 363988112, 372039683, 1074282499, 380407378, 388817027, 397018177, 406367892, 414319824, 420659864, 429043414, 439363221, 445956631, 456699412, 463209664, 471122647, 1073783748, 479374934, 489563283, 495903385, 507031124, 514728979, 521069145, 532197076, 540148752, 546488856, 557231749, 562988165, 573178881, 580043480, 1075895238, 588426774, 598344897, 605209176, 615951877, 621708293, 632301141, 638509593, 647530126, 1075384325, 655535766, 665723987, 672326362, 682632917, 688841433, 1074883528, 699532368, 705880602, 1076463564, 1074128842, 714392215, 723027470, 731046554, 739557975, 748193486, 756212314, 764970574, 1076240327, 1075736521, 1076794382, 1075246029, 1077098447, 1077366731],
    [106, 92, 5, 2581696, 10542272, 18907329, 27321344, 35710016, 44098688, 52618305, 61006977, 69264576, 77784065, 86467584, 94559760, 102793281, 111338689, 119725648, 127959169, 137062097, 145286677, 153148480, 161513473, 170616337, 178841173, 187204116, 195643092, 203611856, 212395733, 220758676, 229196948, 237567511, 245950101, 254313044, 262751316, 270720656, 279478484, 288056913, 296287895, 304694292, 312531968, 319481540, 328237721, 338493014, 347292885, 353403417, 363554449, 372047510, 380173911, 389235861, 394978820, 406144722, 413990614, 422012032, 430767638, 438894295, 447955989, 1073748930, 454485707, 463527040, 473121877, 1075344325, 481642130, 487907027, 497509440, 504814617, 515196498, 521461331, 529564377, 540362258, 546889242, 1076923335, 555277978, 564094488, 571507289, 580314635, 588700761, 597648984, 1074320329, 605609562, 614426264, 622371548, 630513171, 639452891, 1074856899, 646637124, 655925916, 664200843, 672718554, 681395739, 688580228, 697868892, 706010771, 714950235, 1073830916, 1075686350, 1076490186, 723034652, 731307225, 740255448, 748084377, 756893339, 1076765647, 1076000710, 764864075, 1077315533, 1074194380, 1076300811, 1074747336],
    [122, 108, 9, 287745, 8684673, 18924608, 27313152, 35832961, 44090496, 52610241, 60867776, 69387265, 75908688, 84182081, 94553153, 100986450, 109487296, 118122193, 128380418, 134652992, 143287889, 153546370, 159696387, 168453649, 176456705, 187100738, 193758864, 204104707, 210169556, 218416707, 226927744, 235562641, 243713749, 254471381, 260342977, 271213635, 1073748482, 277268053, 288025685, 294012048, 302425088, 312929474, 319473239, 327567056, 338732691, 346868823, 352732688, 361530448, 369542677, 380300309, 386582039, 395084816, 402940993, 1075339204, 412009992, 422366231, 428131971, 437028048, 447899143, 454215257, 464841817, 470468247, 478463683, 489317507, 498116307, 1075613699, 504284808, 514641623, 520799447, 531260611, 540059219, 546227912, 556584087, 565470408, 573613587, 580044441, 590671001, 599024648, 605202006, 614123226, 621987545, 632614105, 640967816, 647406810, 655279688, 663023122, 672835224, 682780231, 1074839560, 689620634, 696708756, 708076616, 714253974, 1073818569, 722650649, 733277209, 739419862, 749889223, 755297938, 764847258, 775054983, 1076453383, 781895258, 788973205, 799730837, 805594241, 815178842, 822537812, 830760129, 840607256, 1075949516, 1076753357, 847572690, 857384664, 1077021642, 864480788, 873637398, 1074419653, 882550360, 1075220430, 890676762, 899335194, 1074722758, 1077348299, 1074227151],
    [118, 104, 11, 1916097, 10560576, 18949312, 27337728, 35726464, 44246017, 52634753, 61023297, 69024833, 77800641, 86449730, 92882640, 103227010, 109659664, 119356545, 128951954, 137053779, 143205459, 153951875, 162506322, 170608275, 176759955, 185280021, 194853889, 201934480, 210446037, 220667394, 229869253, 238110340, 244000341, 254222018, 263423493, 1073745922, 271271443, 277423123, 285943445, 294338129, 305112594, 313607748, 321723971, 330532485, 338773508, 347291159, 355698245, 361841877, 1074819077, 369835729, 378504215, 388712147, 394863827, 403777240, 413998595, 422553298, 429352596, 437331544, 445333137, 454518292, 464330435, 471041753, 1076920323, 1073799684, 481379524, 487663128, 496180758, 504595993, 1075911622, 513229848, 523452055, 529499287, 538395736, 548617943, 554927705, 563168277, 571678294, 582854362, 588334229, 597108315, 604716561, 613385431, 622290516, 630662811, 640892503, 649963162, 655845076, 663824024, 672868045, 680730262, 691906074, 697779352, 706422413, 714284758, 725460570, 731333848, 739976781, 747865753, 756491803, 765412379, 773793359, 781157463, 1075410887, 790578267, 798959247, 1077254088, 807355547, 815474189, 1075169230, 823600859, 1074143180, 1075726349, 1074441162, 832521435, 840902351, 1076553673, 848381013, 857679375, 1076300815, 864634448, 1074753483],
    [118, 104, 12, 2393088, 10305664, 19344577, 27821776, 36383952, 43859968, 52496066, 61550160, 69764752, 77414592, 86181459, 94438914, 103319056, 110968896, 117911058, 128255636, 136513043, 144770626, 153650256, 162218132, 170339329, 178587220, 186713730, 193635921, 203776066, 210185874, 1073747970, 220938324, 227190481, 235351762, 245565075, 254487696, 262440064, 271147734, 279250452, 287508179, 296435732, 304557121, 313820371, 321596432, 330728513, 338256534, 344786630, 355763219, 363422230, 369569362, 1075334085, 378340998, 388269248, 396831873, 406274628, 413468372, 420283974, 431689370, 439042260, 448169089, 454241813, 464946369, 472211650, 482020954, 488932416, 497640022, 1074307908, 504169990, 515575322, 523666433, 532103364, 1075892230, 540741338, 545957521, 556097538, 564486274, 573867091, 579931739, 587900433, 599212164, 605621916, 613625557, 624198803, 632766468, 639403673, 649158867, 655953436, 664340172, 673097367, 682713235, 689508060, 698263127, 707878931, 714149403, 723060300, 731817495, 741433427, 747704027, 1074859976, 1074621379, 756614796, 764620373, 773621337, 781795864, 789786261, 798787097, 806961752, 815334924, 824092375, 832127640, 840502876, 1076466700, 849118937, 857293528, 865144475, 1075168205, 1073881035, 1075736519, 1076803530, 1077331919, 1074210766, 1076327369],
    [110, 96, 4, 2343936, 10706049, 18965504, 27354176, 35742912, 44131456, 52651009, 61039681, 69428417, 77841536, 85949968, 94594177, 103088786, 111764626, 119784640, 127893200, 136643154, 145318994, 153338944, 161447568, 170459795, 176907779, 186613328, 195421713, 203751954, 212427794, 218982085, 229080261, 237364945, 245957331, 252536325, 262792916, 270752833, 277553749, 288319062, 294479429, 304735892, 312695809, 319496853, 328033925, 338290260, 346914391, 1073743877, 354639041, 363193937, 369951384, 1074295746, 380233236, 388463621, 396952083, 406152921, 413525649, 422411927, 428671576, 438920914, 447183941, 455992537, 463798482, 473261721, 478897795, 489520855, 497935513, 504168984, 514811542, 520840899, 529786586, 539458693, 545989333, 554395203, 565140566, 573112915, 1076926467, 581821977, 590308886, 599090201, 607222867, 613098005, 623765081, 632252118, 641033305, 649026582, 655164120, 664004250, 674070039, 682720275, 689170010, 697901723, 707747030, 714335770, 723067483, 733052115, 741301398, 748233435, 758217875, 1075375052, 1076432842, 765164565, 1074624454, 773399067, 781941909, 1077249995, 790330453, 798719189, 1074127817, 1075978189, 1075734478, 1076277191, 1076811727, 1075250120, 1073959876],
    [106, 92, 11, 320513, 8717377, 17132673, 27345920, 35734656, 44123328, 52511808, 61031553, 69420097, 77808833, 86601232, 92595329, 100992129, 111363073, 120268434, 128544400, 134669841, 145321552, 151454864, 159704129, 170600018, 176647893, 185001553, 193424917, 201655297, 210035905, 220819152, 226821313, 237823638, 246097426, 252013633, 262989526, 268895312, 277179393, 288155222, 294088277, 304932374, 313460233, 1073742790, 321595090, 328298201, 335996561, 344392720, 353594368, 361162449, 369585813, 378848855, 389621466, 1073762185, 395407001, 404022416, 411501776, 420799696, 428174529, 439953050, 445990538, 454127193, 462734999, 472843401, 479545034, 488337107, 496559764, 506397897, 1074566085, 513099338, 521366592, 529843735, 540616218, 546401817, 555017296, 565782106, 571698304, 580445908, 590283849, 597388883, 605750464, 614000212, 622554771, 630916224, 639165972, 647317002, 656098831, 664497683, 672457744, 681247808, 1074840586, 689653327, 697527488, 706004695, 715064920, 723207823, 1074079691, 731842200, 739968000, 1076191181, 748619480, 1075688386, 757007896, 1077005252, 1074408392, 765150927, 1076519886, 1076007951, 1075239875, 1075525575, 1077374924],
    [118, 104, 9, 2630721, 10593408, 18981888, 27370688, 35759168, 44278977, 52667521, 60810960, 69444673, 78128129, 86221825, 92645009, 102753808, 109553170, 120071361, 128171715, 134850260, 144696912, 153724099, 162014337, 170114691, 176793108, 186640016, 195667075, 203818643, 210607685, 218474065, 229360658, 237373139, 245612035, 252290644, 260818001, 271164419, 277718677, 287704659, 293971665, 302761169, 312870419, 319659717, 328181270, 336315537, 345121941, 353484440, 361342612, 370263124, 378643608, 387196503, 397516505, 403023377, 411812881, 420587096, 429008597, 439459353, 445621846, 454149268, 462267605, 470951509, 480493123, 487565014, 496354389, 506045507, 512599125, 1073741827, 523345561, 529638936, 538559510, 546448917, 557030918, 563323910, 571589652, 579707925, 1073763266, 1074832324, 590585542, 596878534, 606848722, 612869330, 622077463, 632528518, 638821510, 648791634, 654812242, 663856856, 674471494, 680764486, 690734738, 696755346, 1075890182, 1074343237, 707894873, 714843723, 722846741, 730700805, 739223190, 748274838, 756786891, 764525592, 773564043, 781829334, 789691480, 798729739, 806470868, 1076710411, 814857432, 823510229, 831364229, 840549462, 1074634696, 848675989, 1075704781, 1077025738, 1075468239, 1075230665, 1077331911, 856958679, 1074211790, 865347223, 1076586444],
    [114, 100, 10, 2329665, 8725697, 18973888, 27362368, 35750912, 44139648, 53325328, 59057153, 68674258, 75859154, 86879952, 92611649, 102359571, 109675539, 120434320, 126166145, 135914067, 143230035, 153814032, 162377296, 170123909, 176785043, 187368656, 195267777, 203801237, 212534352, 220433409, 228966997, 237700240, 246656724, 254534168, 260908753, 270765185, 279298773, 288599700, 294463121, 1073754821, 304464405, 310740562, 322154004, 328017489, 1076906948, 337109074, 344295058, 353472017, 363923161, 1074305986, 371974744, 378768919, 389088857, 397140632, 403015186, 411666131, 422817364, 428680209, 437772306, 445877847, 456197657, 464249560, 470910538, 479432407, 487523994, 1075371974, 496623827, 504464906, 512855121, 521078362, 530833413, 538281611, 546409617, 554632730, 1075652552, 564387909, 571707031, 580200156, 1076184009, 1073849283, 588898451, 596741329, 605628125, 613933202, 621905610, 632358553, 1075957703, 639885509, 647333451, 656125662, 664348253, 672645846, 680625802, 689514141, 1074661325, 1074156554, 697811478, 706053643, 714845854, 722405082, 730981019, 739608267, 748400158, 756622877, 1075220491, 764920470, 773566046, 781526556, 1074982860, 790086230, 798303900, 806478363, 815081052, 1076836302, 823255643, 831644379, 1077373903],
    [94, 80, 7, 1432640, 10380353, 18972737, 26862784, 35251264, 43639808, 52028544, 60548097, 68936833, 77325505, 85318784, 94470273, 102516431, 110879809, 119266896, 128024577, 136070799, 144432656, 153190593, 161236559, 168420994, 177987216, 186541185, 193700436, 201975362, 1073754112, 212362961, 220593682, 229212675, 237528657, 244702400, 252813845, 262424083, 270786262, 279544451, 287860241, 295033856, 304710339, 312231439, 321117846, 1076918212, 329147393, 338034322, 344695316, 354313409, 363200082, 370516489, 379864787, 388366034, 1077187525, 1074848899, 396984387, 403826263, 413689489, 421781014, 429367383, 436856322, 446973523, 455335510, 462135956, 471588560, 480528019, 488088215, 496100503, 506479685, 512860885, 523256837, 529637973, 540034181, 1076177863, 546677449, 556811461, 563454537, 571581077, 1076454347, 580362775, 588375063, 597009033, 1075938248, 1073867785, 605528791, 613541079, 621519572, 1076758476, 629794498, 1074155469, 1074698186, 1075238914, 639100494, 1075514310, 647489038, 655877774, 664266446, 1074486286],
    [114, 100, 5, 484353, 10855617, 18859201, 27247617, 35636353, 44024897, 52544704, 60933248, 69321792, 76113612, 84378828, 94487552, 101156492, 109528589, 119918287, 126592654, 134956239, 145083919, 151733263, 159876620, 1073752064, 170249807, 1076391937, 176924238, 185287759, 193578640, 203804303, 210478798, 218842255, 227132944, 237882898, 244033038, 252929040, 260687440, 271437522, 279290945, 286483536, 294242000, 305254100, 311281285, 321234049, 328426704, 338808468, 344835589, 352814668, 361981072, 372362836, 377964173, 388342785, 397266514, 403538944, 411518669, 422694420, 428704960, 436684365, 447598226, 453870720, 463038035, 470666966, 479053381, 487425088, 496723651, 504745687, 512189505, 521635398, 529387158, 538691210, 546924243, 555189958, 1076929479, 562941462, 572245578, 579298433, 588744326, 596495958, 604595212, 613910022, 1075899398, 622325397, 631211523, 639329923, 1076704387, 647491285, 656131786, 663315532, 673154243, 680906391, 689660995, 698319939, 706072151, 714826755, 723485827, 1077234633, 1074367497, 731237911, 740271697, 748250643, 756794890, 765437457, 772367500, 1074653128, 1076233226, 781708885, 790603473, 797402305, 806874645, 814597829, 824157841, 832136851, 1074156484, 1074954245, 1073929154, 1075518466, 1075795915],
    [102, 88, 11, 1048768, 10266689, 18753536, 27142272, 35530944, 43919424, 51905100, 60598273, 69888514, 77071052, 85764225, 95054466, 101712000, 111577679, 120482510, 127402636, 136743567, 1073750016, 1075865601, 145386178, 152568332, 161261761, 1076400258, 1074844674, 170551362, 176696019, 187214349, 194904275, 204491472, 210250387, 220768845, 228458643, 237922894, 245934797, 253895313, 263211536, 269101718, 277872640, 288402071, 296766032, 302656022, 311427136, 321293007, 330197646, 336079379, 346169873, 354847247, 363751950, 371589249, 380152461, 389040784, 394799699, 405842455, 413007955, 422865496, 431008471, 438444753, 1075121092, 448031256, 1074358211, 456174167, 463864001, 473197272, 481034262, 1076206534, 487869077, 496893971, 504646357, 513157640, 522584129, 1075430341, 1073873925, 531917464, 538323656, 547749889, 555109010, 563489352, 571091670, 581697750, 588663506, 597305995, 604645974, 615252054, 622217746, 630860299, 639771217, 647383634, 656026315, 665583766, 672418325, 681192011, 1074154507, 689195605, 697707144, 1074699272, 706628308, 715016788, 723405332, 731794068, 1075770314, 1077098441, 1077374919],
    [114, 100, 9, 362561, 9963648, 18352192, 26740736, 35260481, 43518144, 52037633, 60830223, 68815041, 75860161, 85592193, 94384719, 101025793, 111282768, 119550607, 126191745, 136448528, 144716495, 154249423, 1073750017, 161614480, 170815057, 178925648, 187803663, 193333970, 204369553, 210242115, 220868624, 229746831, 235276818, 246173397, 252316374, 262811792, 271689807, 279055056, 285888212, 294128323, 304754896, 313493699, 321809937, 327682691, 335942295, 347048003, 352717394, 363753169, 369887750, 380864726, 386274007, 395333331, 403442310, 414156931, 419828247, 431255238, 436996294, 445753552, 453382743, 462442131, 470288899, 481265667, 1075855363, 486935186, 497831445, 503974550, 515082390, 1073787844, 521155096, 529157652, 537659974, 546801856, 1076940806, 554709720, 563105363, 571083350, 582191190, 588264024, 599026758, 604637718, 615745558, 622072410, 629821076, 639076416, 647238170, 657215061, 664242304, 672150168, 682912774, 689023120, 697569946, 708078726, 714188816, 722735834, 730877459, 739354704, 1074867141, 747261524, 756516864, 766267029, 773818386, 1076457415, 782134937, 790595730, 1076725709, 1074126798, 798912089, 807373010, 1075711945, 1074681803, 815689241, 824150098, 1075219402, 832466649, 1074460616, 1077353420, 1075537858],
    [106, 92, 9, 540672, 10512449, 18901185, 27420672, 35809344, 44198080, 52455425, 60844161, 69354064, 77752448, 86650385, 94519952, 103427793, 111297040, 120646356, 128454163, 136463056, 145811988, 153620179, 159924288, 170977940, 178925137, 187449938, 196004373, 204091025, 210256000, 221170389, 227159188, 235421888, 1073755074, 246475348, 252324884, 262947538, 271501909, 277614167, 288113298, 296667797, 304615059, 313278994, 1076908995, 322095641, 329780819, 338706968, 347392731, 353250904, 363872984, 1074824133, 372427353, 378154196, 389038168, 1073793988, 395758106, 403844694, 414204568, 1074340806, 422759129, 429010454, 437674001, 448055899, 453774871, 462839889, 473221787, 478940823, 487866972, 496528010, 506776091, 512495319, 521421532, 530082506, 538372243, 546451094, 555114641, 1075933128, 565365401, 571354136, 580141596, 588933771, 597084826, 604908760, 613696156, 622488267, 630646803, 638463128, 647785100, 655778001, 664431115, 672582234, 680668886, 689728076, 1076729799, 697985611, 706136794, 713698388, 723282444, 1075173387, 731408906, 739698771, 748186186, 756476115, 765225676, 1075452938, 1075727372, 1074706377, 1077331918, 1074211791, 1076586445],
    [134, 120, 9, 1960129, 10504321, 18892865, 27281601, 35670017, 44189696, 52578432, 60828240, 69355712, 77457473, 86132800, 92555795, 102771216, 109464274, 119916754, 128733716, 136595476, 142887571, 153102992, 159926978, 170125841, 179196437, 186927764, 195709635, 203827219, 210389654, 220457681, 229396628, 237259348, 246041091, 254421187, 260459154, 270911634, 277629655, 288116820, 295979732, 302271059, 312486608, 319310466, 330287234, 338580117, 344214227, 354822227, 361122386, 371574866, 380389913, 388911829, 397036099, 405416003, 411716182, 422955094, 430854741, 438979203, 447097043, 453659350, 464898262, 1073754115, 472664793, 481054932, 487344727, 495340050, 505817235, 514181138, 1076913092, 523399832, 529025602, 539633795, 548390978, 556550745, 565342936, 571099670, 581576707, 590727190, 596396695, 607547588, 612911618, 623912985, 631105537, 1075871746, 640436889, 646728215, 658010199, 665856217, 674220226, 683175959, 691021913, 698608273, 708341975, 716187801, 724945046, 733114904, 739518614, 749717506, 758673559, 764676244, 773712001, 783446616, 790112466, 799271505, 1073802181, 808873988, 815278226, 823519232, 834039940, 840173780, 1076435913, 848685120, 1075400648, 1074634694, 859205700, 865609810, 873851008, 882659866, 890513622, 899147925, 907825882, 915679254, 924182720, 932991642, 1075694538, 940845142, 949479637, 958157402, 1074409419, 966002708, 1076777933, 1074968519, 974645269, 983050258, 991422549, 999557204, 1077336012, 1075251150, 1074227151],
    [134, 120, 5, 2007040, 10946561, 18393089, 26781889, 35170369, 43559041, 52078720, 60467392, 68855808, 77636108, 86444225, 94021696, 103205571, 109357634, 119579340, 128387137, 137292292, 144745100, 153684559, 161925635, 169779392, 176753362, 185518675, 194945088, 201918994, 211077717, 220110976, 227084946, 236243477, 245408332, 254347919, 261016211, 270967441, 279513807, 286575317, 296133201, 302582354, 1073743235, 1074028547, 312920195, 321298961, 329845263, 335981125, 345295509, 354853585, 363268225, 369535685, 378456787, 387219649, 395258454, 403221126, 411478661, 420399635, 428647124, 437332695, 445032965, 455526467, 462201428, 471280345, 1075884037, 481225284, 487367188, 496052823, 1076937476, 1073816580, 507177678, 512795216, 521218711, 532343438, 538214465, 546253526, 557509198, 562342402, 571515536, 580454939, 590276804, 596683464, 604807828, 613362198, 621324998, 633006606, 637840002, 647012880, 655829593, 665774212, 672312009, 680569416, 689209345, 697248406, 1076197319, 705210950, 714918554, 722774730, 731292173, 739838555, 747153926, 756861530, 763669186, 1077255174, 773235341, 781658649, 1075693570, 1074408450, 790415898, 798140937, 806791883, 815178445, 823724699, 832490200, 840084105, 848734795, 856728272, 865151511, 874433048, 882158154, 890284680, 899064397, 907610843, 916245210, 924101258, 932620939, 940867713, 949430937, 958319192, 966044170, 974170632, 1076775944, 1074698250, 1075505160, 983485080, 991078985, 999729675, 1076563977, 1075008523],
    [106, 92, 8, 264193, 9996352, 18384896, 26773696, 35162240, 43681921, 52070465, 60994060, 68847809, 75761793, 85624833, 94276174, 102937292, 109316289, 119573199, 127830542, 136491660, 142870593, 152996494, 161657420, 168175680, 178817680, 186681935, 195735630, 204221133, 212389395, 221033170, 226896064, 237013647, 245943891, 253659854, 262844430, 268839040, 278956559, 288288276, 294302225, 302786575, 313454164, 319599190, 327952527, 338201168, 347008724, 353153750, 361507023, 371755536, 380825301, 386708118, 394668032, 405310160, 414379605, 422752920, 430713485, 438881939, 445428246, 453781583, 464449172, 473215705, 481045069, 487492101, 495906391, 506245714, 514599437, 1073745859, 520794769, 529532944, 537823813, 548581976, 554698960, 565374485, 571378373, 582267417, 588253264, 598929045, 606909074, 613812364, 623431379, 630098565, 638235345, 647366668, 1074546693, 655290071, 663401041, 672532684, 682275022, 689309772, 699183634, 705693840, 714010135, 1074304964, 1075111940, 724217998, 1076429762, 1073830854, 1075426310, 730787479, 741519896, 749908696, 1077272519, 1075720199, 758428249, 766816921, 1077040074, 1074965514, 1076807624, 1074210761, 1076323275],
    [130, 116, 8, 1884224, 10545345, 18933761, 27322433, 35711105, 44230848, 52619328, 61008000, 69526096, 77785088, 84315778, 92596354, 103080656, 110936192, 120384211, 128237779, 137531013, 142928386, 153535121, 162327059, 168726228, 179128532, 185133268, 195478033, 202041927, 212814549, 218934343, 229032657, 235727382, 246368789, 255495190, 262849098, 271534741, 280137285, 285797012, 296403466, 302705287, 311224918, 321734804, 330992726, 338608855, 344779414, 356158614, 363809365, 371901130, 380430995, 387091976, 1073743812, 397888152, 405717591, 412257928, 419752514, 431442520, 439009930, 1074029578, 445311687, 456298181, 461695682, 473385688, 481215127, 1076135938, 487254535, 495357122, 506939928, 514245201, 1074321415, 523037267, 529328854, 540184069, 547179033, 556056659, 1075392517, 565873878, 572344921, 580698304, 1076970120, 588418120, 597510873, 606388371, 1073845187, 613739020, 621186114, 631196379, 639951376, 1074911177, 647293580, 654740482, 664750747, 672972800, 680061460, 689236556, 697470152, 707610644, 715448976, 722004564, 731179724, 739150932, 749553748, 757383187, 1075186700, 765127245, 773762125, 782060185, 791593495, 798681741, 807316621, 815745563, 823714514, 832236237, 839691271, 849300059, 857268754, 865790477, 874425357, 882862746, 890823250, 1074682893, 898534548, 1075754955, 908028442, 915989138, 923577543, 933194330, 940354695, 949971674, 1077341126, 1076572110, 957254676, 966700237, 1076847567],
    [118, 104, 6, 2420737, 10774721, 18925633, 27314305, 35834048, 44222528, 52480193, 60868609, 69118672, 77777024, 84175040, 94695489, 102942720, 111315601, 120350865, 128250049, 134662803, 144616016, 153380993, 161804417, 168348372, 178424529, 184838272, 196006485, 201902740, 211724944, 218690130, 228878401, 237685464, 244369945, 253667856, 260763864, 271346257, 279628312, 286444186, 295864401, 302706712, 313288913, 321571480, 327731796, 337807889, 344649880, 354707457, 361941722, 369789012, 377776192, 388944405, 394709715, 403343572, 413952017, 422498965, 430623320, 436783636, 445041235, 453675156, 462090328, 470050816, 479251097, 487229460, 497996501, 504392406, 512403481, 520679954, 529558038, 537700435, 546239195, 554986007, 563137113, 571123801, 579793499, 588671708, 1073742786, 596691673, 604678361, 1073763269, 613347995, 622226012, 630376986, 637979155, 646883482, 655290907, 664037975, 1074836422, 1076946883, 674679517, 680708698, 688564377, 699715805, 705718870, 716622493, 722249747, 733270173, 739273366, 750176861, 755935322, 766824541, 773090007, 780970131, 789115602, 1076178887, 798386844, 808897053, 814524627, 825544733, 831810199, 839821530, 847835794, 1076711364, 1074628554, 857106972, 864987162, 1074129868, 1076500429, 1075214280, 1077316555, 1074454479, 1075782601, 1076059086],
    [102, 88, 9, 2039873, 10717377, 18950272, 27338752, 35727552, 44116032, 52775568, 60760065, 69568656, 78080657, 85926017, 94734864, 103246417, 111091905, 119900752, 128412177, 137166848, 145328723, 153438224, 162332800, 170494483, 176630468, 187132625, 195887168, 204843204, 210184708, 220547792, 229441728, 238397444, 243739268, 254101584, 260768402, 271952004, 277826132, 287672528, 294322706, 302992020, 313101011, 319750679, 327625284, 338905752, 344924312, 355838020, 1073748935, 1075334148, 363932377, 372460056, 379815937, 386867224, 397486681, 403794581, 414681177, 420151890, 431041049, 437209620, 447318675, 453706450, 462375636, 473401369, 479134359, 488327894, 497256577, 504701594, 1074566082, 514927257, 523455064, 532121753, 537862232, 547048086, 557287641, 563421914, 1074840515, 573786840, 581142593, 588194008, 596732437, 605784661, 613753370, 1073810376, 622684763, 630950613, 638517847, 1074360265, 647850523, 656115861, 663683799, 1076736970, 672877142, 681281557, 689793755, 697639514, 706431510, 1077011406, 714172501, 1075981253, 1076512715, 722561237, 1074175949, 731736731, 1075763148, 1075263439, 1077372870],
    [118, 104, 12, 297024, 10301505, 18942081, 27461632, 35719361, 44238912, 52496449, 60884993, 69693072, 77793408, 84445712, 94187521, 102959296, 109382161, 120024784, 126388432, 136909008, 142936657, 153578512, 162074768, 170043473, 176622293, 187395666, 195340501, 203239553, 210176597, 218852884, 228894805, 237974035, 243730965, 252407444, 263139923, 270706705, 277809732, 285961812, 296292368, 304916548, 311364292, 319516372, 329068737, 338471108, 344918660, 355167762, 363792918, 371790416, 380414084, 386861572, 397504214, 405735638, 414134931, 422356996, 1073745924, 428935750, 439578135, 446998549, 456339526, 462490118, 473132759, 478709904, 489893894, 1074809797, 1074300867, 496044678, 505900112, 514787926, 520652880, 531837062, 537201297, 548499094, 556730518, 565129939, 572696721, 579144401, 590573143, 596709394, 606251217, 615739031, 621875858, 629442560, 637995669, 649161814, 655429714, 665102485, 673934482, 679774336, 1074060226, 691221190, 697370822, 707882006, 714246337, 1075380230, 723340824, 731154643, 739969612, 747705042, 757820626, 763660480, 773523980, 782061272, 789743617, 798689996, 807226968, 814909569, 1073827783, 824004248, 831817811, 840206483, 849021580, 856983571, 1074631692, 865241153, 1075175368, 1075718093, 1076257737, 1076017103, 1077341131, 1076572110, 1076851658],
    [126, 112, 7, 2189377, 10709120, 18966721, 27486400, 35874816, 44263488, 53030544, 60909569, 69298305, 77589201, 84371665, 94973648, 103105170, 111143441, 117925905, 128527952, 136536787, 145476309, 151480913, 162082320, 169863825, 176646289, 185273876, 195256851, 203417681, 210439764, 220422739, 228934162, 238227158, 246245590, 254528021, 1073744834, 262365843, 269299415, 279702040, 288319512, 296043218, 302853655, 312820306, 319630999, 330033880, 338651352, 344681031, 353200840, 1074283461, 364056214, 372074646, 378268234, 386624135, 394989268, 403522201, 412207627, 420440217, 428698248, 436932244, 448514586, 453853721, 464480920, 470771737, 479423068, 487418376, 1073779651, 496447131, 506186389, 512974940, 521366172, 1074852804, 530001499, 539740757, 546529436, 554396167, 563309276, 571944667, 580083932, 590080152, 596339399, 605252124, 1076959239, 613232215, 622026780, 630450312, 638413384, 1075399688, 647441947, 655704590, 665578072, 674195544, 680487513, 689639133, 697647694, 705423882, 714804765, 725338778, 731202254, 739207897, 748382927, 1074637769, 1076483850, 755843289, 764529291, 773548687, 784058970, 789397593, 800263702, 808282134, 817613530, 825429590, 833448022, 1075185291, 840026187, 849022557, 857031310, 1074160582, 1076016142, 865331272, 874188445, 882600463, 890497032, 899377743, 1077342156, 1076832205, 1076321295, 906750154, 915663048, 923912395, 931915914],
    [106, 92, 9, 2445312, 8702080, 18958465, 27346945, 35735745, 44124225, 52898384, 59069073, 69658753, 75844162, 86452944, 92623377, 103475266, 111626962, 117787266, 128395792, 134566609, 142919680, 151472788, 161950352, 171108369, 179138770, 187124242, 193284802, 201664660, 210063953, 220915906, 229067346, 235620949, 244000853, 252662291, 262858882, 1073753027, 271010450, 277170690, 288024578, 296579218, 1076379650, 302721557, 311117845, 321212608, 329705665, 336276117, 344672405, 354766912, 363259969, 369830613, 378226901, 386880083, 397600913, 402991828, 411519188, 419743808, 430264448, 437586647, 445074004, 453298368, 464351314, 473254425, 478489108, 487016468, 495932115, 506652753, 513092248, 521097875, 531818705, 538249879, 548892697, 556197889, 562374740, 573403154, 580323990, 588869825, 1073787844, 596970007, 605646977, 1076941765, 1074868169, 613878486, 622424129, 1076709318, 632638105, 638913111, 649556121, 655978497, 666192473, 674721881, 1074116551, 682969817, 691499225, 697764374, 706538074, 1077271500, 714541654, 1075454923, 722807512, 731195992, 740092570, 747973144, 1075992525, 756869850, 1075224520, 765258266, 1075760078, 1074466762, 1074751439],
    [106, 92, 11, 2082816, 10356865, 18983104, 27371520, 35760256, 44148800, 52668545, 61057089, 69566992, 77834433, 85969088, 94242881, 103000065, 111782609, 119644738, 128174146, 136579281, 145468050, 153199298, 161622595, 170117314, 179022354, 186753538, 195177091, 203671554, 212576850, 220308098, 228731587, 237226114, 1073745922, 245867219, 253897219, 262129792, 1074817027, 271821461, 279282384, 287295552, 296618133, 304448080, 314034322, 320735425, 329613968, 339200018, 345901057, 355977298, 1076396996, 363831832, 372115989, 380872725, 388737746, 397920466, 405250643, 414059221, 422815957, 428731092, 439224917, 447981653, 454413015, 463735313, 472492049, 479062548, 489136787, 498346587, 504875670, 514826968, 521284250, 529656473, 540289563, 546941643, 555076183, 1073795015, 565158488, 572787345, 581544081, 588114516, 598712984, 607398555, 613542425, 623354387, 632564443, 639216203, 646834836, 656673361, 664382091, 673818705, 680905239, 1074602949, 689056282, 697682583, 1075929034, 705833690, 714205913, 722610778, 731368150, 739879435, 748145238, 1075682249, 1075431435, 1074403277, 756148825, 764922390, 1075213254, 1077065672, 1077331919, 1074210766, 1076326348],
    [110, 96, 11, 372737, 10692609, 18738305, 27363329, 35752001, 44140673, 52529345, 61452816, 69412929, 77458625, 86715088, 95269521, 102624257, 111880784, 120435409, 126348882, 137046032, 145338576, 152955969, 161868992, 168372822, 179540499, 185174744, 195670096, 201927382, 210235090, 218728984, 228977664, 237875793, 243870358, 252283544, 260647446, 271815379, 279703258, 285837912, 294463552, 304475200, 313758291, 319629312, 330150417, 338423450, 344795264, 355701395, 363589146, 370117127, 380220048, 388361344, 396568705, 403671687, 412324565, 421734593, 430698074, 437226055, 445876936, 456591448, 462656021, 470281746, 479562377, 489367696, 496472596, 503836306, 512723655, 523700440, 529765013, 538430614, 1073742855, 546121920, 555339289, 562409601, 571836937, 582420632, 588893849, 597136084, 605391433, 615974936, 622301844, 630705238, 639225561, 646295745, 656222871, 664111817, 671461441, 681036822, 689900059, 1074025481, 697535112, 706334297, 714576468, 723331671, 731089416, 739480149, 748145878, 757009115, 764643912, 773786267, 1075089416, 1074850756, 782051863, 1076435915, 790563419, 1075397580, 1073849282, 798829271, 1075961798, 1075711946, 1074685893, 1076267981, 1074459587, 1077098447, 1077374926],
    [102, 88, 13, 1697985, 10217600, 18475137, 26994752, 35383488, 43640833, 52029505, 60549120, 69618191, 75861007, 85967504, 94784207, 101027023, 111133200, 120164050, 128051793, 137390612, 144827091, 153848913, 161606353, 1073754112, 170945236, 178503889, 187403793, 195160081, 203811542, 212888212, 220446737, 227380438, 237103761, 245754454, 254831188, 262389841, 269323350, 279333519, 287555729, 294891096, 304474646, 312887887, 319654934, 329640598, 336480857, 347442778, 354542163, 361654997, 372608730, 378694299, 388599314, 395471387, 406162970, 412248795, 422699676, 429108888, 437250762, 445794845, 455066192, 462261398, 470706837, 480874130, 487483989, 498197212, 506826394, 512911963, 523362844, 529772056, 537913930, 546195993, 555729616, 564890769, 571361945, 581034515, 589925970, 1076908994, 596527833, 606200467, 613658328, 1074824131, 1073795015, 621955741, 632414812, 640388305, 646965770, 1074595781, 1074093001, 655256085, 664776343, 672131722, 1075420170, 680675933, 689942231, 697453277, 706719319, 1075701708, 715107863, 1076235213, 1074419652, 721783887, 730172559, 1075228619, 1076816838, 1076569038, 1076066248],
    [106, 92, 13, 354368, 10856641, 19518093, 25520256, 36022337, 42322638, 53072589, 61713036, 69822593, 75876942, 86626893, 92629184, 103656012, 112186063, 120285261, 128821964, 1073752064, 134728209, 1076391937, 145740303, 153847949, 159737856, 168282833, 178901517, 187394061, 195930636, 204460687, 212560013, 220571777, 229626447, 237725901, 245737473, 252430996, 262899725, 271149249, 279677133, 287926337, 294507029, 303024835, 313231437, 321480705, 330910291, 336693778, 344838869, 353356419, 364464787, 370248274, 378784454, 387295380, 398019283, 403032590, 412076547, 420980750, 431573523, 437504518, 445745874, 454519382, 461884049, 471574673, 479816336, 487312084, 496478286, 504850966, 512610965, 521644238, 530016982, 537250446, 546556486, 554420820, 563456084, 572091088, 579719765, 587713105, 596625987, 605792337, 614033936, 1076921347, 622449175, 630966794, 638306836, 647219846, 655730708, 664365648, 1074057222, 672909898, 681027726, 689400470, 697946775, 706464394, 714844369, 723112663, 730958482, 1074862023, 739889751, 748407498, 756394196, 1075134474, 765175825, 1073843144, 1074383880, 1074668482, 1075993547, 1075485707, 1075767236, 1076309961, 1076852677],
    [126, 112, 11, 2395137, 10626241, 18754560, 27143360, 35531904, 43920448, 52440065, 60828737, 69619404, 77606081, 86123521, 94932172, 102771841, 111554190, 120213005, 128066689, 136875596, 145116812, 153232449, 162041356, 170282060, 178521808, 184987346, 1073750016, 1075865601, 195440142, 204099213, 212076048, 218672785, 228994766, 237653581, 246975694, 254019152, 260320854, 270945292, 277229079, 288228375, 296258700, 304762573, 313525781, 321162369, 327429654, 338849411, 344338007, 355337303, 363105345, 372133391, 380634709, 388271297, 394669719, 405958339, 414057623, 423136398, 1076409282, 431124035, 439355093, 445165137, 456019535, 463734416, 470330897, 481185487, 487720595, 495365714, 506621443, 515245720, 520531602, 1076940803, 1074861059, 528887511, 538070039, 548275415, 554085906, 563359257, 572927566, 580406297, 590908494, 599131864, 604253910, 615403151, 622210695, 632851470, 641074776, 1075142596, 647376583, 656166102, 666240536, 671657681, 681331798, 689047251, 697994772, 705965721, 713305750, 1075689414, 722619543, 731549396, 741344917, 747908825, 756559498, 764955865, 772933139, 781880916, 789851737, 798371399, 806898841, 815279818, 823264851, 832212628, 840445514, 849104022, 857091591, 1077270535, 865611274, 873614423, 1075448842, 882650635, 890391767, 899427915, 907824150, 916205195, 924339289, 1074685896, 932982475, 1076265929, 1073923081, 1074202635, 1074491333],
    [114, 100, 0, 1576129, 10095616, 18484288, 26741825, 35130369, 43519105, 53063183, 61368335, 68816064, 77204608, 86259216, 94244370, 103394895, 111700623, 119541457, 128202320, 136318609, 145254479, 153587348, 161877525, 170538582, 178261521, 187198159, 195530324, 1073750017, 203820757, 212481558, 220204625, 229084692, 235432017, 245642960, 253627986, 260597777, 269462610, 279580184, 287979222, 296357464, 302540945, 311405586, 321261141, 329922198, 338275535, 344484049, 354815637, 364394010, 372616216, 380914387, 386403844, 397948634, 405409496, 414559448, 422988507, 430192272, 439725144, 448023187, 456799445, 464104591, 473188883, 481834586, 488509138, 495955154, 506874459, 512233156, 523908117, 532171351, 539463380, 548943514, 555191836, 565594779, 574239829, 580357788, 590760475, 596119108, 607794325, 614338194, 624446167, 630172818, 638062212, 1075858371, 1074304004, 647466716, 657738323, 666389015, 673025169, 682233496, 691554967, 699772056, 706229981, 714968081, 723012249, 731352668, 739789401, 1075108802, 748172893, 756911313, 764955161, 773338781, 781994004, 790465617, 1075384266, 798504477, 1074621383, 806898393, 1076466635, 1074919369, 815548628, 1077282764, 1074163654, 1076799429, 823937108, 832325780, 1076294605, 1077092296, 1075790798],
    [114, 100, 3, 279680, 10225856, 18672833, 27290688, 35810369, 44199041, 52587713, 60845184, 69233856, 77753345, 85723136, 92554304, 102682320, 111176704, 119277696, 126641745, 136236560, 142896724, 152832064, 161402512, 169886804, 178810389, 184839700, 195431123, 203222017, 211829780, 218394260, 228985491, 236776577, 245384340, 251948756, 262670465, 270454352, 278938836, 287862421, 296487061, 304934037, 310658048, 321416789, 330041365, 338488405, 344745617, 353005270, 363654165, 371591699, 379995350, 1073749955, 388525781, 397413060, 403465937, 414109381, 420769478, 428098752, 438700627, 446491713, 456133188, 464317653, 470574609, 481298948, 487509586, 497960648, 504655366, 514328577, 521299024, 529452562, 539494593, 546229970, 556680840, 562720278, 571764294, 581437505, 588172946, 598098966, 607128196, 613573840, 623824389, 1075606532, 631008778, 640420053, 647286488, 657344072, 664039046, 672951882, 682362965, 689071120, 1077188614, 1075377090, 699321989, 706506442, 714237072, 723266199, 730492502, 739560984, 748432087, 757482582, 765226634, 773597783, 1076955146, 781504152, 790374935, 799950344, 806669912, 1074356232, 816762437, 1075947525, 1076490189, 824592022, 831155350, 1076766663, 1076254667, 1075217353, 1073927118, 1074989004, 1074221007],
    [106, 92, 1, 2223232, 10628289, 18894017, 27413504, 35671105, 44059649, 52579392, 60836993, 69752400, 77745280, 86109248, 94514305, 102911168, 111695504, 119663808, 128068609, 136869522, 144829440, 153234497, 160069203, 170929680, 178515601, 184962627, 195589650, 204483664, 212069969, 218516995, 229135376, 237497876, 246688771, 252071619, 262690512, 270790161, 280243395, 1073755074, 285625987, 294286995, 304606868, 313535696, 1076909059, 321418834, 330837525, 337899217, 346584786, 354938452, 364129347, 370308694, 381169365, 388493012, 395204248, 403303506, 414461059, 420370008, 428469394, 439356561, 445281811, 456666773, 462417626, 470447827, 478800914, 489688273, 498365658, 506465361, 512880217, 521303574, 531631121, 538045977, 1075089350, 546469526, 556805264, 562687186, 1074588612, 573863514, 582627031, 588246106, 596530904, 607661653, 613543577, 1076433866, 621967062, 632958551, 638709465, 649360922, 658124439, 663743514, 674526874, 683290135, 688909466, 1074879435, 1075413966, 697194008, 706087954, 1073866701, 714476626, 722865298, 1076244428, 731795087, 1076782021, 739642578, 1076010953, 748572239, 1075771336, 756960783, 1077349319, 765349583, 1074480143],
    [126, 112, 12, 427009, 10816577, 18918400, 27307136, 35695680, 44084416, 52088464, 59278464, 69536897, 77254160, 86313985, 95061585, 103329492, 110808784, 120237589, 126387200, 136907792, 145665558, 153661012, 161795671, 170855446, 176587969, 187215380, 194694736, 203754689, 212502225, 221163158, 228904471, 237571280, 243696769, 252358297, 262844117, 269012121, 279514192, 287999505, 297053914, 302952156, 311086747, 321823957, 330632404, 338996762, 346599060, 354733719, 363766805, 372575380, 1073750978, 378580509, 389328474, 394980381, 405343376, 414360666, 420130393, 430878422, 439660186, 447393429, 455397079, 464456854, 472549009, 479243869, 487255133, 498011350, 503743553, 512798365, 523152982, 529444508, 537586845, 548736084, 556967066, 563392202, 571526300, 581897302, 590653011, 1075861448, 1075090372, 597077707, 605335178, 613076571, 623554133, 629703872, 641010708, 646622937, 655797771, 664055370, 671796763, 681258712, 691316243, 697740939, 705998346, 713608281, 723201688, 730367040, 1074846730, 738897433, 748072523, 755551257, 764743250, 775070746, 1075644427, 781233885, 789491292, 798018780, 807087704, 817145555, 1074355142, 823045660, 831573020, 840240786, 850568410, 1075417029, 856354013, 865807896, 875471957, 881512155, 892249237, 898960914, 1074655171, 906546393, 915738322, 926197395, 1076766665, 932236380, 1076259788, 1076541389, 1077331919, 1074201550, 1073968071],
    [130, 116, 10, 2536448, 10759169, 18910336, 27430017, 35818561, 44076032, 52595713, 60853312, 69373121, 78130832, 86422592, 94407872, 103344850, 109350098, 119967249, 128462416, 136754304, 145287826, 151293074, 162016784, 170308800, 176613974, 185109590, 195860180, 203697217, 210553538, 218795202, 229510675, 237803092, 245951058, 251956306, 262573713, 269258435, 279746068, 285609105, 294578371, 303074969, 313953924, 321785427, 330741272, 336652420, 344231442, 354848465, 363894295, 369495249, 380168210, 386436630, 397448855, 405671571, 414771931, 420515353, 430345809, 439129748, 444992593, 456714843, 463744193, 472946391, 478603286, 487624409, 495488726, 505949904, 515290840, 520546518, 529567321, 537431702, 545655825, 556832343, 563275801, 574000708, 581832403, 590788184, 596043926, 607555076, 614739073, 624342680, 630123075, 638356547, 646614594, 655232666, 664319516, 671926338, 680300163, 688787162, 698005085, 705620483, 713853955, 722112130, 730860567, 1073747914, 1075073027, 739948061, 747563139, 755666434, 1074827205, 764546581, 1074578379, 1073808386, 773371548, 783870619, 1074094024, 789712533, 798668445, 806414404, 817270468, 823004762, 1075678151, 1074386948, 832222941, 842590747, 848170522, 857257564, 864864258, 873467031, 1075459017, 882423516, 890431705, 898764373, 1077044173, 907077828, 915410007, 1076013006, 923854852, 932187351, 1076295628, 940361858, 949096149, 957540441, 965929113, 1077358534, 1076849615],
    [122, 108, 12, 2540544, 10570881, 18410624, 26799104, 35187776, 43576512, 52880908, 60902465, 69649536, 77679809, 86026893, 94564047, 103083600, 111627264, 119989900, 128616528, 136506895, 145026576, 153570368, 161932876, 170559504, 178450063, 186969744, 195487436, 203508737, 212502672, 220524240, 229033024, 237456576, 246057168, 254198976, 263016083, 270576205, 279113295, 286057998, 296570387, 304130573, 311215312, 319508117, 329296589, 336129669, 344674005, 353560273, 361532050, 369839637, 378725905, 389082710, 397445206, 403498574, 414010963, 422873816, 430394496, 437700311, 447802902, 456165398, 462210128, 470502997, 481593944, 487386695, 495764624, 506285779, 514911958, 523274454, 529329671, 538537039, 546498193, 556854934, 565217430, 571010629, 579661511, 588868815, 596829777, 604801746, 612953605, 621604487, 630811791, 639428313, 1073747975, 649366168, 656100884, 664192535, 671910482, 680718026, 689759897, 698305689, 705464850, 714821332, 722265742, 733252120, 739569291, 748252175, 756467351, 764603914, 773123659, 782034457, 790580249, 797503173, 806678027, 815588953, 824134873, 1075337158, 1075089413, 831712906, 840232651, 849038932, 856474640, 1074841540, 1074077700, 1075934219, 865267274, 874204820, 881649358, 1077248968, 1073865736, 1076234250, 1074424842, 1076797378, 890685015, 899632217, 1075761097, 1074735113, 1076589507],
    [126, 112, 13, 2386944, 10660865, 19199169, 26790912, 35179712, 43568256, 51956800, 61509132, 69495936, 77919297, 85773903, 94661824, 103085057, 111979599, 119721552, 128251009, 134638672, 142913229, 151309890, 161664528, 168359633, 178433153, 184970256, 195219152, 204115660, 210302481, 218524880, 228773520, 235468433, 245542081, 252079248, 261934607, 269416083, 279211072, 288140303, 294047427, 302970387, 311324306, 321039425, 328128150, 338333324, 344739540, 354209487, 361647829, 369686097, 380415183, 387763855, 395769486, 405580943, 412511439, 420269573, 428799571, 440053335, 445402644, 455773772, 462319314, 471266894, 478989893, 487904857, 495734356, 503623245, 512544389, 521860635, 532327959, 538340431, 547026651, 555380314, 562343565, 571657799, 579786454, 588009108, 595897869, 605345497, 614100634, 624602775, 630912603, 639266522, 649768663, 1073746886, 1074818054, 654626306, 664467099, 672959698, 680946703, 688311939, 697620121, 706514066, 714501263, 722652871, 731174425, 739929626, 748588696, 755289730, 764202693, 772689493, 781112854, 790531672, 1076666373, 797855381, 807177810, 815199758, 822529603, 831704583, 839798293, 848221782, 857640664, 1075898308, 1076174792, 1075671048, 864341698, 873647751, 881749074, 890697422, 899583512, 1076990978, 1075177474, 1076497354, 906415619, 1074414599, 915338963, 924618258, 932080658, 1074170883, 1074709449, 1073945547, 1075541003],
    [110, 96, 9, 2599936, 10562752, 18951232, 27339776, 35728512, 44248065, 52636865, 61285968, 69413953, 78359632, 86191233, 94588433, 103228944, 111914704, 119754449, 128386643, 134975122, 144920145, 153552531, 162245648, 170086033, 178726544, 185306706, 193416725, 201927701, 210447895, 220669136, 227249682, 235359829, 243870805, 254215699, 262909072, 269044759, 280176278, 285970130, 296701528, 304940674, 313626324, 319639258, 328150234, 338896406, 346532928, 353193626, 361704602, 371656403, 380087488, 1073750980, 389228246, 1075858371, 397512340, 1074303682, 405753368, 411774615, 422380738, 430419072, 436817047, 445329111, 455934978, 464621076, 472862360, 479145562, 489489474, 498175572, 504187994, 512437847, 1074851781, 521209564, 530157273, 539971288, 546254362, 554763804, 563842717, 572354139, 582420062, 588877465, 597520091, 607585950, 614174237, 621358741, 629623957, 639577674, 649274966, 656117341, 663301845, 671567061, 680592988, 689671901, 698183195, 706686602, 1076694982, 716637726, 722029783, 730924700, 740126363, 748629514, 1074618311, 756649497, 764234778, 773795530, 781815385, 1075681290, 792135390, 797527127, 1075440585, 1076507597, 1077035979, 1073907660, 1074190280, 1075263439, 1077372878],
    [122, 108, 12, 2165825, 10554369, 19074048, 27462720, 35720321, 44240064, 52866768, 61158608, 69560528, 77663425, 86183040, 95111891, 103101968, 111586960, 119974928, 128280592, 136656016, 143068738, 153529936, 161835088, 170989265, 176623106, 187502230, 195389584, 204516354, 212932113, 218697367, 229445334, 237718035, 246486609, 255102161, 260640279, 271388182, 280267793, 288429713, 296830999, 305204824, 313996502, 322210897, 330394243, 336137943, 346371152, 355765393, 363940055, 369561282, 378080855, 389493910, 397454530, 404047960, 411504258, 422799893, 431559891, 439397506, 1073741826, 447811096, 456988372, 464563266, 472991895, 1073767107, 481365656, 487394952, 498669203, 506153107, 513183442, 520949256, 531319379, 540874260, 546737682, 556863192, 562892360, 574428820, 580292242, 588597464, 599331923, 605458002, 613763096, 623709782, 632763478, 639151769, 649152599, 1075875781, 655298253, 666069653, 674706454, 681356308, 1074584519, 688852621, 700257876, 706260505, 714426520, 1075388358, 724789845, 733549587, 740076692, 747572813, 1075670987, 756880469, 766733013, 773369433, 780996296, 1076724744, 790434837, 798797012, 808806489, 1074121668, 814681613, 823989397, 832351316, 842098883, 1074402317, 849155285, 857255641, 867264579, 875915417, 884041731, 1075205071, 1074968522, 892692697, 1077341129, 901081113, 1076570060, 1076327374],
    [114, 100, 13, 2092224, 10830977, 18967616, 27356160, 35744896, 44133568, 52653249, 61041729, 69430273, 77589568, 86328385, 94596225, 101052048, 111625360, 117829200, 128271361, 134606544, 145179856, 153972306, 162350673, 169864320, 176778900, 187297297, 196035666, 201944660, 212692690, 218492432, 229729364, 237832853, 245361664, 254231568, 263260822, 271412882, 277834902, 287960785, 296699026, 1073755074, 305203734, 313355794, 319777814, 329903761, 337986753, 346884821, 355069009, 363807954, 372050517, 380454033, 386657879, 397216277, 403566099, 413615184, 422906503, 428830294, 437120723, 447562769, 456198230, 464340177, 471059993, 481626823, 489636882, 495709719, 504721098, 1076916165, 514919126, 521629323, 529493206, 540107924, 546041495, 557124103, 565658757, 571723353, 580462681, 589262348, 599213125, 604761815, 1076669385, 612986580, 622405657, 630681163, 638447251, 649159892, 655960793, 664235531, 674710725, 680774873, 1076416456, 688483860, 698296920, 706702924, 713944659, 724657172, 733284935, 740257484, 1074594755, 1073832967, 750208005, 756272793, 765012121, 773811852, 781544970, 1076205580, 790571672, 798453451, 806710922, 1075431435, 815737368, 1074406350, 823488074, 832514776, 1075991494, 1074961418, 1075759044, 1074206669, 1075279823],
    [106, 92, 13, 2436096, 10572801, 18803777, 27315792, 35990592, 44127297, 52481552, 60904641, 67440274, 75845140, 86847123, 94424720, 102847617, 109399700, 120026260, 128790227, 136367824, 142954068, 153580628, 162344467, 169798657, 179009219, 186985664, 195620369, 204305925, 212397777, 218435090, 226840276, 237860485, 245296321, 251989586, 262632660, 270871680, 278850689, 288192197, 296799424, 302321362, 1073750149, 313226755, 321965120, 328281751, 336678600, 346911813, 355003985, 361836055, 370363929, 381086745, 388724291, 395390551, 403918553, 414641369, 422278787, 429207256, 1075862531, 437341832, 447181844, 455945811, 464055953, 470897792, 481348736, 487927448, 1075622850, 496193113, 504450632, 513617429, 523693145, 529749072, 538136217, 548859033, 554783936, 563547734, 1076946887, 571692240, 582011904, 588328663, 596725256, 605892245, 613635088, 622251670, 1076167688, 630412432, 639028310, 647433366, 655447040, 664194582, 672476760, 1074098116, 681389781, 689001536, 697749206, 706145426, 714419736, 1076727757, 1074650060, 722930710, 731311314, 1075450831, 1074949065, 1076530126, 739708118, 748088338, 1074447307, 756887125, 764865618, 1073944522, 1075279814],
    [126, 112, 12, 1838208, 10595457, 18984001, 27372737, 35892352, 44280832, 52669632, 60926977, 69340816, 77835328, 86232657, 92646481, 103025857, 110889984, 120049155, 128689796, 134720644, 144444608, 151629459, 159894675, 170632772, 176926341, 185052228, 195825234, 202223316, 210349651, 218614867, 229353156, 235384004, 246557829, 252292627, 262655619, 271550037, 277589573, 285715972, 293973713, 304877074, 1073750659, 1075857412, 312986691, 321627140, 327921157, 335916561, 347220997, 354667729, 364095174, 372386885, 379833361, 389260870, 395030213, 403025553, 413273680, 1074305029, 421776529, 431334999, 438439440, 447204547, 456369670, 463735873, 471182938, 478661651, 490055319, 497290369, 504737498, 512478806, 523208213, 530844673, 537767444, 546294996, 557164055, 563874880, 571846170, 579448531, 587713747, 599369435, 606867154, 613920267, 622063256, 633054922, 639766224, 647474827, 655085078, 666084998, 674376901, 1075373062, 680373908, 689171992, 699141778, 708552266, 714452634, 722972363, 731115096, 739511961, 1076172745, 750495370, 755748566, 764677849, 1075145672, 775268055, 781175956, 789843545, 800826890, 806202964, 815001304, 823397913, 1076462535, 1073867786, 1076758477, 834250267, 840412747, 848023190, 1074154507, 859416219, 865061908, 876193371, 882756698, 1074697166, 892307157, 898616404, 909084309, 1074984908, 916311066, 924699802, 933088474, 1077354447, 1075803074],
    [114, 100, 10, 373825, 10587329, 18975873, 27364417, 35752961, 44157584, 53056704, 59059794, 69323280, 78362193, 84225554, 94735957, 103402006, 109546518, 120305361, 128650772, 136679125, 145345238, 151489750, 159757505, 170593876, 176656022, 187287702, 195802769, 203787797, 212453974, 218598486, 226866177, 237496855, 246396117, 254643783, 260386514, 271829063, 279688721, 1073742787, 288198151, 293940882, 304451221, 312994391, 321893525, 330510024, 338937863, 347059221, 353340954, 364064328, 371714711, 377861249, 1073763269, 1074832322, 386895578, 397872346, 405269207, 414168149, 420449882, 431173256, 439995032, 447321088, 456338952, 463587920, 472487040, 1075900424, 481136327, 490146906, 498321607, 506041408, 515706441, 523881176, 529503963, 540872329, 549046808, 554931344, 1076956100, 564858516, 572639952, 580097104, 590188167, 598413012, 607373447, 613389915, 1074354183, 624364570, 632285715, 638555803, 649924105, 658098776, 1075417034, 663721499, 672108186, 683084954, 691006099, 697537552, 706678300, 716171987, 722703568, 733810377, 741337683, 1074651078, 1075717129, 748621468, 756927001, 1076250571, 765431439, 773704281, 782175964, 790597327, 798870233, 1074182093, 807341660, 815763023, 824035993, 1077342156, 832540175, 1076827151, 1075276750],
    [86, 72, 1, 2378753, 10863617, 19376193, 26864768, 35253440, 43641856, 52030528, 61327055, 69487745, 78096577, 86492815, 94873729, 103042241, 111658575, 120039425, 128207937, 134720081, 145517649, 153601551, 1073754112, 160017106, 170772176, 179334675, 185436179, 195552852, 204326544, 212699797, 220578945, 229477077, 235957782, 245744705, 254642773, 263220883, 270910657, 279808533, 1076911042, 288386643, 297110083, 304989712, 313290449, 322275971, 330155600, 338456081, 345221784, 355233425, 361343570, 372272851, 380102356, 389384707, 397430489, 403941912, 412372503, 422045204, 429107800, 437538391, 447211156, 456493763, 1075347459, 462704343, 471050968, 481316377, 487172626, 496258711, 1073805254, 503818257, 1077223364, 514870937, 520727186, 531648089, 537757907, 546336342, 554534995, 563113686, 1075667916, 571312275, 579890838, 1075948491, 1076490185, 1076759501, 1074423754, 587704465, 1076270021, 1074974664, 596093137, 1074730951, 1075267534],
    [110, 96, 11, 2468928, 10605633, 19229825, 27249664, 35638464, 44158017, 52415616, 60935297, 69192768, 77712577, 86234764, 94743552, 103115841, 111266817, 118066832, 128177740, 136670401, 143232592, 153439308, 161600641, 168152706, 176787152, 186898124, 195390465, 1073752064, 201707074, 1076391937, 210341392, 220548300, 228709377, 235261634, 245618188, 254127296, 262885005, 270879884, 279293056, 287429825, 296734228, 303148750, 313644052, 321211404, 327536130, 336703054, 346552003, 355159757, 1076924418, 363329091, 372476994, 380325453, 389009108, 395423374, 405918932, 413879821, 422563476, 428977678, 439473300, 447827670, 456117844, 464639060, 473411151, 481382038, 487181892, 498577103, 506547734, 512347780, 521621139, 532131343, 539489795, 546426567, 557026306, 565268054, 573044355, 579456516, 588860945, 598969474, 1074847747, 605507155, 616017551, 622579337, 630672915, 640912578, 646565572, 655969873, 664382997, 1075909636, 672910857, 680644167, 689811154, 697913041, 1075144645, 706465353, 714976850, 723078801, 731754130, 739725011, 1076206536, 1075436552, 747752967, 756657877, 1075710918, 1074416646, 765185737, 772918919, 781823637, 1074692105, 1073923079, 1074214858, 790212181, 798862866, 1077374923],
    [102, 88, 9, 2510912, 10653697, 18755776, 27144256, 35532928, 43921408, 52842688, 61116940, 69208717, 78008448, 86282892, 94374605, 103174144, 111317057, 119540237, 128094337, 134640145, 1073750016, 145238608, 1075865601, 153391820, 159806033, 170404560, 178426049, 184971921, 195693203, 203723340, 210137809, 220203597, 229412941, 238572238, 245901968, 254710288, 263737870, 271190739, 279744653, 288387650, 296356435, 302789317, 313561731, 322458254, 329910803, 336343621, 346984528, 355496642, 363341840, 372126358, 380670659, 389567054, 397551766, 403452421, 414069270, 422613507, 428765775, 439494678, 445395589, 1076407427, 456167491, 462320143, 1076676613, 472813712, 479359572, 487731784, 496382601, 506236941, 514880130, 523381334, 529937097, 539897942, 548180173, 556823042, 1074335746, 1074877442, 565324502, 571880009, 581841110, 590254288, 596800148, 605983250, 613577428, 622760530, 630354452, 638726792, 647926482, 655258255, 663892488, 1075154884, 672543241, 681464341, 689869458, 697447112, 1074643915, 1073873931, 1074158601, 1075746824, 1075509194, 705589967, 715018965, 723407445, 1077359558, 1077110727, 731796117],
    [98, 84, 11, 2601089, 9965569, 18354241, 26873984, 35262464, 43520193, 52039744, 61094607, 68817088, 78098497, 85463169, 94648911, 103264257, 112088592, 119814799, 128954895, 137254480, 145101457, 153368591, 161984705, 1073750017, 170808976, 178655953, 187316369, 196186642, 204109523, 212210257, 220870865, 230265556, 237917904, 245766741, 255431252, 262829587, 270932501, 279949519, 288519876, 293868118, 304487061, 313627282, 322074116, 327684741, 338041557, 346427921, 355446927, 361387730, 369365718, 380516438, 389124306, 1075866562, 397571716, 405420049, 414167119, 420902100, 428348101, 439236822, 448369172, 455767699, 464140369, 473010770, 1076402308, 481457220, 490312340, 496399508, 506346134, 512233989, 520360086, 530034705, 1075364806, 538334808, 548289046, 553914390, 563589265, 1073820611, 571896852, 580620823, 587879442, 597143761, 605443800, 614175447, 623539795, 629674565, 639086673, 1076970501, 647386648, 1074112456, 656118423, 664171604, 672895575, 680154194, 1076219847, 1074665419, 689329816, 1075205065, 1074968522, 1077338061, 696931474, 1075776460, 1074491342],
    [114, 100, 10, 2516992, 10514433, 19034176, 27291713, 35811456, 44199936, 52457665, 61403856, 69365952, 78014592, 86012033, 94778963, 103313491, 111735440, 117861073, 128333523, 136868051, 145289744, 151415313, 161887891, 170422419, 178844240, 187066432, 195442195, 203976723, 212660885, 220620992, 229783257, 235434201, 246477394, 252078673, 263468611, 268989081, 277664278, 285633169, 296891545, 302543449, 311218774, 322062868, 330445913, 338752146, 347228756, 355743235, 361263641, 372044309, 378169488, 389166105, 395104918, 403466972, 1073746691, 1074815940, 414463107, 420270806, 428501200, 436475547, 447541845, 456280788, 462189064, 473183427, 481096405, 487221264, 498874071, 506524178, 512518748, 520909448, 528750107, 540078802, 546073116, 554463816, 565982807, 571535379, 579496016, 591148567, 597095064, 607275668, 1075884994, 612636251, 622359179, 630911582, 638347932, 646738632, 654579419, 664466142, 1076938760, 675034775, 681079371, 689369816, 1074332615, 699274906, 1073838022, 705753171, 1077249989, 716051994, 723022347, 731312728, 741217882, 748188363, 756740638, 1074126794, 1075710987, 766383834, 773255704, 781588189, 789639379, 798365277, 806416531, 1074682825, 815142429, 823849630, 1075488718, 1076287436, 831919773, 1075261391, 1076849613],
    [126, 112, 13, 1961985, 10506432, 18894976, 27283520, 35803329, 44060672, 52580481, 60822032, 69357569, 77459521, 86134849, 92558034, 102765136, 111538833, 120224340, 127931088, 136704593, 145390292, 151409365, 162017986, 171037250, 178944660, 184963669, 193483350, 203960386, 211677313, 220887572, 228594320, 237891670, 243815062, 252195029, 263188995, 268849685, 277369366, 285749269, 296743491, 305551877, 313012866, 321909443, 1073750275, 1075867714, 327570069, 336089814, 344469653, 355586050, 361386647, 371732482, 380752002, 1076931524, 386412629, 397800083, 406608537, 411848857, 420369114, 430977234, 438694417, 448551641, 453791961, 462303383, 471724225, 482237147, 486822482, 498085970, 504255002, 514969794, 524311132, 529158679, 538071623, 548418194, 553930898, 564523729, 574642716, 580014599, 590361106, 596529818, 604262418, 615510147, 624974556, 630477385, 639119578, 649458387, 658266649, 663506969, 671765079, 680407127, 690876630, 699816517, 705581658, 714616922, 724430998, 733764185, 739004505, 747262679, 756306569, 764293335, 775287315, 1076413382, 784226843, 789861065, 797847575, 808316950, 1073819397, 817781403, 823415305, 832057498, 842396243, 1076717515, 851335771, 1076204553, 856838791, 865611802, 873853592, 884365509, 890630680, 1075169228, 901142661, 907170503, 915796696, 1074139080, 926964380, 1074679815, 1074962378, 932573784, 1075760077, 1074469838, 1075541967],
    [114, 100, 8, 1904640, 8816832, 17205248, 27070656, 33870353, 44347409, 52236416, 61115074, 67564050, 78196865, 86280706, 92730002, 102568000, 111446658, 117756497, 128233553, 134645888, 145305793, 1073752194, 154194516, 161788561, 170471425, 178554946, 184864913, 193366080, 204550672, 212914708, 220508881, 229191745, 237800003, 243708501, 252113618, 263270992, 271485013, 277139665, 286175750, 296825488, 304908803, 310817493, 319222354, 330379984, 338594005, 345027272, 355521236, 361566806, 372410568, 1076381636, 381087940, 387101193, 395121302, 405572227, 411480725, 423030916, 428946007, 439257237, 1074049539, 445690504, 456716876, 462598729, 470888983, 481069251, 490271244, 496153289, 506628232, 514904724, 521177281, 529576520, 540603020, 546386583, 556959816, 562893334, 574025796, 579777094, 588286017, 596685320, 604836566, 615968772, 624068616, 1076943880, 629584405, 639423192, 647049943, 655274694, 665749525, 672977432, 681357839, 689091209, 697731280, 1075643335, 1073826825, 708375244, 714912335, 722896976, 1074637836, 731697816, 739160710, 748466895, 756058241, 1076746246, 765252184, 773632655, 781617296, 1075447823, 790549075, 798001153, 1074423749, 807326419, 815171600, 824103443, 1076270029, 832492179, 1074984907, 1077352394, 1075274702],
    [98, 84, 10, 2552896, 10786881, 18616385, 27300033, 35688577, 44077057, 52465729, 61273088, 69507073, 77336769, 86126720, 94827648, 103061633, 111292608, 119993536, 128227521, 137295569, 144846912, 153795090, 162461329, 169611265, 179092115, 187627025, 195738194, 203165825, 212792913, 220904082, 229388880, 235573974, 246847702, 254867029, 262287360, 271644181, 279624402, 288109264, 296358423, 305699333, 311752408, 321654931, 330087123, 339146310, 346821139, 355252819, 364312262, 371856023, 380418067, 389478022, 395743897, 405977241, 413938320, 420804248, 430715408, 1073753158, 439809030, 447483987, 454874842, 464951894, 470454358, 481038547, 487913048, 498637445, 504763028, 513078808, 523418201, 529961049, 538317396, 547149338, 555094548, 565615254, 571117718, 1076647880, 580260564, 590912197, 1075098563, 598348375, 607689285, 615125719, 1076945925, 1076168649, 623965909, 1074088909, 632723990, 638226454, 1074369479, 649131669, 1074913226, 1075708878, 1073898443, 657635865, 664178713, 1076009922, 1075509199, 674413273, 680956121, 1077350340, 1074752460, 689755738, 698144410],
    [114, 100, 10, 2158784, 10547328, 18935872, 27455681, 35713024, 44232769, 52742736, 61296720, 69907536, 77787265, 86175745, 95073808, 103074512, 111628496, 120016912, 128240272, 137016528, 142930434, 153405456, 161960080, 170833492, 176902803, 188017297, 195999252, 204781143, 210457107, 221039122, 226816578, 235622995, 246737617, 254719700, 260895320, 271496852, 279759442, 288313432, 293925506, 302823001, 313313938, 322261525, 328004120, 338343056, 347129986, 355422232, 364164631, 372295746, 381243911, 386200258, 397719191, 405850306, 414798471, 1073747970, 422745734, 428561107, 439404546, 445444824, 456300230, 464308946, 472862936, 1075344582, 478983833, 490007057, 498684615, 1077190791, 504149721, 515172945, 523588245, 531797062, 538495510, 549015623, 1075893187, 554889738, 565491415, 572050070, 582308565, 588575241, 1074857924, 596439704, 605352521, 613201433, 622381654, 632246424, 1074086853, 1073846216, 638907017, 649237510, 655936214, 666194517, 672330314, 681490138, 689926230, 697886740, 706015945, 1075169289, 714273418, 723433050, 731869398, 739829844, 748483278, 756987546, 765423638, 773384404, 782037518, 789770954, 798930458, 807366806, 815327380, 1074400266, 1074685901, 823980686, 1076278219, 832369230, 1077074958, 1075785676, 1076849615],
    [110, 96, 9, 2553921, 10539072, 18927744, 27316224, 35705024, 44462800, 52885697, 61256401, 69890771, 78051457, 86422033, 94819028, 103445075, 111860304, 119976593, 128373396, 136736848, 145160193, 153530961, 161927700, 171201027, 178969232, 187093588, 195719699, 204667523, 210023062, 218550422, 227070487, 237400592, 246077456, 252227607, 260756056, 271217299, 279632080, 288404165, 297029763, 305191634, 313569797, 321286288, 330357394, 338735749, 344642200, 352899671, 364139203, 372300306, 378056791, 386322966, 395334165, 406247508, 412398234, 420532378, 431247939, 1073746882, 439547971, 1074812931, 1075359877, 447787077, 454054549, 464575058, 470069846, 478597206, 487117463, 495997525, 506910868, 512274583, 520540886, 529584666, 537948827, 548600003, 555003930, 562745880, 571527770, 579392215, 588673689, 598931459, 605728792, 613077720, 621859546, 630215381, 641128660, 646230038, 655782425, 666294292, 1076944839, 672837848, 680948313, 1075651526, 689887772, 698003544, 706114265, 715053660, 723169432, 730886683, 740219548, 1075921866, 747942106, 756052699, 764719194, 772829787, 782162652, 788836566, 1073842121, 1074122700, 1074670532, 797487319, 1076522955, 1076795342, 1075247055, 1077349320, 1074489293],
    [142, 128, 9, 2426944, 10842304, 19238977, 26816641, 35205121, 43593921, 52113536, 60502016, 68759617, 77279296, 86339648, 94701760, 103256780, 110833856, 119747086, 128667662, 136644736, 145199628, 153301710, 161821265, 170199040, 178614400, 187142796, 195506899, 203764369, 212021902, 220942542, 229085772, 235604493, 245838355, 254496910, 260900945, 270897153, 279130702, 288051278, 294455441, 304451713, 310850050, 321220608, 330115074, 338006209, 346501715, 352793282, 361468564, 372058306, 380719762, 386478723, 396702417, 403507409, 414667480, 420319766, 428552708, 437105367, 445844111, 456610328, 463942291, 470233666, 478909012, 489498690, 498160210, 504050244, 512176770, 523053186, 529502809, 540103378, 1073745922, 545862211, 556085777, 563187790, 574050968, 580069523, 587936452, 596587078, 605000409, 613624019, 623989266, 629879428, 638530182, 649409243, 655069716, 663947855, 674714200, 1074813956, 680725199, 689656533, 697144022, 705901064, 714822229, 722440857, 731064403, 739455624, 747737294, 756765205, 764086989, 1075613637, 1074587653, 773009992, 781038167, 789776911, 798708373, 807105104, 815474907, 822973014, 831468038, 839463427, 848269849, 857690714, 864750221, 1076430793, 1074094089, 873411270, 881406659, 892678747, 898339540, 907749467, 916411034, 1075939334, 1074392070, 1076769795, 924005064, 934621851, 941322960, 948810263, 958081179, 1077302280, 1075223495, 966742554, 973968022, 982190669, 993341979, 1000043024, 1007784078, 1016801307, 1024561166, 1033851610, 1041442835, 1050374800, 1057862295, 1066207249, 1075508170, 1077085131, 1073964043],
    [126, 112, 3, 1799169, 10530945, 18419712, 26808512, 35197056, 43585600, 52771468, 60862465, 68908097, 77533711, 86579215, 94442062, 102986830, 111194177, 119607822, 128268812, 136541198, 144748737, 154090000, 162050701, 170349584, 178983572, 187243151, 194973839, 203993805, 212293264, 220271246, 229587664, 237548109, 245847248, 254481108, 263141968, 270759054, 279491085, 288035348, 296695952, 305230868, 311202326, 322114072, 329595468, 336499282, 345732225, 355144276, 363403983, 371134671, 379654862, 388199630, 395219602, 406000216, 413481676, 422671508, 429167315, 436933190, 447814357, 456331928, 464876696, 471110227, 481497816, 487536654, 496538201, 506557524, 1073752003, 512430790, 522787407, 530518095, 538481177, 548762840, 554373766, 565254677, 572035737, 582055124, 588190280, 598809237, 606557264, 614109914, 1076123589, 1075095557, 621482502, 632363605, 638521864, 647722177, 655135318, 1076413446, 663697550, 672043538, 682980440, 689246730, 698030737, 708146200, 713855702, 722408072, 731585041, 739595799, 747541202, 755972302, 764973785, 773150359, 782187099, 789927639, 797741718, 806294216, 814692430, 1074070471, 823481943, 832213594, 1073826756, 1074368520, 1074916360, 1076763586, 1075475458, 840241802, 849296091, 1077322697, 857379482, 866073115, 873763347, 882184778, 1076027339, 1075785739, 891239067, 899322394, 907350730, 916134609, 924095123, 1077103626, 932911697],
    [126, 112, 8, 2347008, 10580097, 19099648, 27488448, 35745857, 44265536, 52654208, 60911617, 69980880, 77689025, 84219410, 94980625, 101019666, 111636497, 120312400, 128784002, 136923729, 145190993, 153342144, 162338306, 168260117, 179032592, 187504322, 195285120, 204682899, 210203349, 220450880, 227242629, 238237267, 243757717, 254530192, 1073754242, 260796933, 271389762, 279530193, 286224903, 296186065, 302477909, 311021651, 319517253, 330512083, 336415446, 344576531, 355677203, 361974424, 369455826, 378130643, 386208978, 395790874, 403010130, 413627025, 420213460, 428151890, 438913169, 445608519, 454152921, 461706898, 471419419, 478507154, 487453207, 496448583, 504187542, 513135260, 520843973, 530002951, 538528411, 546271943, 554562135, 1076905989, 563558023, 571689496, 579825799, 588116695, 1074306055, 596996811, 605230662, 613632600, 621539924, 630527109, 639060634, 647459533, 655094292, 664212629, 672352984, 681013837, 689295964, 697659979, 705894022, 714558170, 722956813, 730976857, 739578885, 747457046, 756511373, 764146324, 1075626566, 1073813517, 773157387, 781522117, 790055514, 797560979, 1075401668, 806827207, 814565974, 823251481, 831877771, 840242245, 848906971, 857068252, 1074891787, 865539093, 874072667, 881971865, 890704981, 898495127, 1074644940, 907482325, 915788316, 923997190, 1074147279, 932385990, 1076784072, 1076537289, 1076287438, 1075263427, 1077371850],
    [106, 92, 7, 489664, 10940609, 18960576, 27348992, 35737664, 44126336, 52507280, 59209728, 69660737, 78205650, 86061584, 92756689, 103215233, 111759954, 119616080, 128380929, 134969473, 143217173, 153170640, 162197568, 168261760, 176771669, 184889429, 195646098, 201808529, 212529152, 218976919, 229577430, 238211732, 244021441, 252531287, 260509847, 271766100, 277575745, 285807128, 296932052, 302741505, 313086482, 321852054, 330494534, 336026129, 1073744835, 344527448, 352811072, 363524224, 369561687, 380826246, 386357841, 394875541, 403247832, 414372372, 422795795, 428413592, 439546374, 448092242, 456069718, 464869394, 472576192, 1074291206, 1075882946, 478490773, 489877702, 498423954, 503656469, 512938003, 523459283, 1076413381, 530141723, 538259483, 546132503, 557144274, 563270227, 1073813447, 573510166, 582178899, 588436115, 596054039, 607344787, 613601491, 621630167, 629608663, 639292057, 647723546, 654922453, 663040213, 672846425, 681278106, 689525403, 697643163, 706400985, 714832474, 1075139531, 723178009, 1074892744, 1074656204, 731198043, 739998426, 748245083, 1077032900, 756363995, 765022427, 1077299146, 1074180047, 1076812750, 1075521481, 1076322253],
    [114, 100, 12, 2215936, 10358977, 18985089, 27504704, 35893376, 44282048, 52539393, 60928065, 69316801, 77713472, 85856385, 94613504, 102879424, 111415953, 120031955, 128045184, 136187969, 145730198, 151384595, 161353729, 170895894, 178909847, 186913297, 196061910, 203690577, 212595216, 221227606, 230019733, 237245137, 246917787, 252048019, 260715154, 271682074, 279573079, 285872339, 296192595, 302649427, 310767699, 322415323, 327545043, 336212690, 347581019, 355848917, 361369619, 371689619, 380236503, 386535571, 1073753027, 397511386, 403321362, 413921936, 423078427, 431346261, 437392026, 1076388802, 447842906, 455865040, 462557402, 473008282, 479572491, 490066453, 496111706, 505907219, 514585168, 521810653, 530156244, 539619863, 545927762, 555322004, 563458763, 572371469, 580374738, 588919389, 597264916, 605401739, 613928978, 621940762, 631089752, 639480525, 647483538, 656028189, 1075881924, 664644248, 673043161, 681194141, 1076155335, 689943054, 698198552, 706064971, 714977933, 723374745, 1074858956, 1074350021, 1074105355, 731886222, 740272796, 748532301, 756535378, 1074649033, 1075189773, 765440718, 773827164, 782094937, 1075476422, 790604508, 798872089, 1077325770, 807383630, 815368788, 1076812814, 1075774408, 824158748, 832416472, 1073968079],
    [114, 100, 3, 2043904, 8755329, 18740353, 27365441, 35754177, 44142721, 52662272, 60919809, 69439680, 77828160, 86184529, 92781200, 102626369, 111382656, 119739025, 126335504, 136180929, 145592981, 151360020, 161427584, 168278608, 178123777, 187535893, 193434262, 203551936, 210221776, 221065237, 229479125, 235377366, 245741588, 253883456, 260379155, 271422037, 277189332, 287815894, 293933779, 304994002, 314020504, 321370262, 329454289, 337769472, 344298068, 354793556, 362754240, 372102802, 377983574, 388479062, 394596947, 405657106, 414683864, 421902548, 430568664, 436540051, 448238168, 455283217, 463598720, 470128641, 478646806, 489142294, 496971840, 506320466, 514702023, 523702465, 531362965, 540512792, 545624724, 556120212, 565654216, 573174808, 580098193, 589952088, 598552661, 607597064, 612735169, 623637717, 629512257, 640414805, 648884437, 655987211, 666317384, 672372817, 682357781, 1073749256, 689541771, 699251207, 707392664, 715993237, 722704593, 733417537, 739873483, 749582983, 758583425, 1075605444, 766360135, 775368840, 1076668423, 781816395, 789813265, 800526337, 1076412427, 1073816514, 806818455, 1075934153, 815207127, 1076996035, 1076217802, 823595543, 1074149317, 1077302222, 831984215, 1074961357, 1075501007, 1075252172, 1074483142],
    [118, 104, 10, 2379840, 10859648, 18477249, 26865793, 35254337, 43773952, 52162624, 60420097, 68939968, 77877440, 86619727, 94105728, 102756880, 111785487, 120214159, 128436946, 136442066, 144699984, 151491664, 162156559, 169865936, 176657616, 186929152, 195939030, 203551314, 211808912, 1073754112, 218600592, 229265487, 237881942, 246265428, 254038144, 263309912, 271995415, 279819988, 288213526, 297161431, 304723663, 313379478, 319287962, 330715799, 336040976, 346540114, 352973380, 364270167, 371831951, 378137115, 386527748, 397260308, 406090449, 414304792, 420082372, 430289920, 438980815, 447859352, 455980692, 464810513, 470282970, 482103450, 490059411, 1076912066, 498365073, 505787456, 515657946, 522564800, 531090066, 539095186, 545780314, 557600858, 565556819, 1075615685, 573688536, 581038610, 590639697, 599111187, 606586898, 612889114, 624709658, 632665811, 638184027, 647468572, 656044048, 664390237, 672634460, 681210000, 689556189, 697561803, 706188956, 714764368, 1075110851, 723110557, 1075918790, 731116043, 740144725, 748450521, 756664861, 764670603, 772403844, 782087701, 790393433, 1077233668, 797567707, 807253717, 815427792, 824030869, 832336537, 1074365385, 1073861575, 840168011, 848795356, 857502233, 1074925517, 864676507, 1074681867, 1075490760, 1076807628, 1074210762, 1076325326],
    [130, 116, 13, 2314240, 10858689, 18862145, 27250881, 35639425, 44027905, 52645952, 61584012, 69718542, 78344206, 86749708, 94370319, 103273038, 111898702, 120304332, 128055889, 137327250, 145470028, 1073752064, 153090639, 1076391937, 162493010, 171029133, 178518611, 184930818, 195252416, 203796609, 212850690, 220713614, 227005076, 238252180, 245739521, 254016211, 263442965, 271692493, 280326165, 287570579, 296858189, 304304256, 312605201, 319148674, 330002574, 338014273, 347068546, 353096408, 361222740, 372469844, 378646744, 386912921, 396622355, 403034690, 414298637, 420704791, 430954562, 436982424, 444977858, 454144152, 462639702, 1076925442, 472897730, 478925336, 487838362, 496087064, 504590935, 512741977, 522320593, 528995028, 538161233, 548368914, 555743887, 562811480, 573035214, 582210197, 590573780, 596750424, 606206609, 614051994, 624259221, 631241423, 640930517, 649032402, 656126041, 666106395, 672378897, 682324174, 691272283, 697553626, 708039253, 714715354, 724922453, 1075110851, 733215387, 738710036, 749957140, 756265105, 766769883, 773042385, 783642837, 790485712, 798741128, 806605338, 815378458, 823358103, 1075907525, 1074351109, 832428560, 840684232, 849064089, 856904342, 865063449, 874371664, 882627080, 890491482, 899395609, 907235862, 915395289, 1074627524, 924703376, 932958792, 941338841, 949187287, 1073857544, 957984858, 965956310, 1074140105, 1074948038, 1076272074, 1075502090, 1075785675, 1076852679],
    [126, 112, 12, 2397312, 10368064, 18887681, 27276481, 35664961, 43922432, 52442241, 61232780, 69088448, 78156940, 85865600, 92550670, 103568973, 111711756, 117716686, 128734861, 136614976, 142882382, 153900749, 161780928, 1073750016, 168037967, 1075865601, 176436878, 187454989, 195597900, 201592527, 212612816, 221017166, 228889600, 238431440, 243676819, 254571726, 262706892, 268971538, 277362324, 288126094, 294425793, 302255631, 310916820, 321680398, 327980033, 335810191, 346830416, 352728595, 363222092, 369768085, 378311809, 389426256, 396776460, 403322453, 411866177, 419966674, 430716560, 438719692, 445265621, 454202576, 464923792, 472659472, 479221457, 487208469, 496145552, 506866704, 512112339, 521164305, 529020500, 538220246, 545795666, 554055251, 563369044, 571356803, 580556418, 587738770, 596661841, 604911107, 613717590, 621827729, 630076995, 638751760, 646985285, 656168019, 663238164, 672830978, 680670726, 689190535, 697586900, 705574595, 714380822, 722613958, 1076403203, 730871493, 739529748, 747803728, 756168262, 764687879, 773739605, 781882946, 789722758, 797980293, 807163027, 815437506, 1075637250, 1076692998, 823145989, 832328915, 840210070, 1074358212, 1076205573, 848965271, 856962759, 866014421, 874130967, 882128455, 891180181, 1075432455, 899296855, 907957269, 916074199, 924079252, 932992019, 1074664393, 1074942985, 1075217354, 1073923082, 1074214856, 1077375947],
    [98, 84, 12, 1578113, 9966785, 18355201, 26874944, 35132481, 43652288, 52974159, 60429440, 69703184, 77206528, 86528527, 94869200, 102776401, 111964241, 120034896, 127800915, 136330769, 145773074, 153589392, 1073750017, 161355475, 169885329, 179073169, 187929811, 194909843, 204238865, 213095507, 1075858370, 220872406, 228464147, 235565589, 246650003, 253771473, 262959313, 272078553, 279868059, 288592915, 296768210, 305632921, 313146966, 321409743, 330798681, 338711122, 345093852, 355090070, 363877010, 372741657, 380640989, 388919835, 395425308, 405421590, 1074307013, 411726421, 420591196, 430972445, 438850191, 448246801, 1075633091, 456269534, 464417371, 470922908, 481304157, 487223957, 498578577, 506470045, 514749147, 523744465, 531766814, 1075384260, 537555669, 548910161, 556932702, 1074616263, 563630612, 572241626, 580538903, 589010584, 1075161030, 598875806, 605704855, 614184602, 1076216777, 622350932, 630953496, 1073877960, 639128276, 647730776, 655905428, 664508120, 1074939850, 672813655, 681293338, 1074180044, 689590999, 698070618, 1076816843, 1076574157, 1077375950],
    [94, 80, 4, 281728, 8705153, 18904128, 27292864, 35681280, 44070016, 52589697, 60978241, 69341904, 77755585, 84202561, 94916176, 102921217, 111284752, 120081424, 128504848, 136450128, 145247888, 153670864, 161616016, 168482390, 178801872, 184823894, 193648278, 201879249, 210121363, 218814166, 227044945, 235155990, 243979286, 252210833, 260321430, 271504576, 277638677, 285487318, 296277072, 303197906, 313849431, 319048896, 327946968, 339015191, 344747669, 352727635, 361026561, 370306642, 1073742787, 378828422, 386282003, 394546240, 402969793, 411832856, 420245205, 430494864, 437941960, 445002451, 456455831, 462188117, 471496200, 479474201, 487880390, 497996928, 503868945, 512496216, 523564759, 528763904, 538605128, 546583257, 556717120, 563771016, 571633298, 580154886, 590271488, 1073760264, 597612116, 606000788, 613692057, 622778068, 630469209, 638875206, 647943700, 1074302924, 1074583558, 655102616, 663907858, 1075390407, 1076192203, 1075951556, 1077275589, 1076500431, 1075208137, 1075752909, 1076807626, 1074213826, 1077105614],
    [106, 92, 3, 2094144, 10386496, 18896065, 27284545, 35673217, 44061697, 52581568, 60970048, 69350992, 77747200, 85884032, 94368960, 102913152, 111293968, 119534720, 127827136, 136992338, 144848528, 152992768, 161994371, 169875140, 178771651, 186801812, 195966609, 203937347, 212500037, 220346064, 229103107, 1073748420, 1075341315, 237133332, 246044178, 254686801, 262403154, 271351382, 277238870, 287315012, 295957522, 304905942, 310793430, 321795601, 329249792, 338460310, 344347798, 355096210, 362812548, 371455122, 380272261, 386291222, 396366852, 406050327, 1076399042, 413957142, 422319298, 429250265, 438459988, 447370962, 456013521, 463729874, 472014548, 481039426, 487970457, 496129676, 506205314, 515102423, 522878469, 531371010, 538301977, 548044485, 554849804, 562828819, 571856473, 1074326533, 581852890, 588797454, 596383443, 604771923, 615765655, 622352078, 629937811, 1076691917, 640573018, 649320023, 655906382, 663754453, 672683662, 680662680, 1073824782, 688920149, 1074112457, 699293210, 705844812, 714086037, 1076220874, 1074935751, 724459162, 730994200, 1077306315, 1076010952, 739382872, 1075770310, 747787980, 756160216, 1077089292, 764417557, 1075269583],
    [122, 108, 13, 2403520, 10949824, 18920449, 27309185, 35697857, 44086337, 52892736, 61123712, 67557010, 75805842, 86937168, 94967505, 101242516, 109491348, 120001536, 128880144, 134796820, 143045652, 151565909, 161786944, 171119701, 178967637, 184858194, 193509077, 204648083, 213062869, 218552018, 226800850, 238073558, 245672960, 255267987, 260748803, 271242453, 277263956, 288405078, 296652432, 304682513, 310957140, 319075858, 330348054, 336115221, 347254291, 355669013, 1073750978, 361412227, 369546258, 377927380, 386446997, 397315792, 406000789, 413848725, 420394694, 431140563, 439817427, 445174996, 453948934, 465245200, 473083475, 478598226, 487503494, 498120342, 506009233, 513052375, 522900501, 529446470, 540480531, 546606743, 1075861510, 1075358661, 554882584, 565646419, 571772503, 579516099, 588838038, 599463120, 605326871, 613865177, 622114315, 633017424, 639143041, 647558166, 655799949, 665392721, 672836753, 681112790, 689223243, 700126352, 706251841, 714528345, 723981440, 731557073, 738899523, 747820696, 756332235, 764851725, 773665793, 781888593, 1076415491, 1074603975, 789763672, 798275211, 807220353, 815303873, 1076195268, 1076736972, 1077004299, 823580185, 832386113, 840608785, 1074399176, 1074156489, 848884822, 857126477, 865635329, 874329281, 882038488, 890681037, 1074961421, 899077785, 1075758026, 1073944527, 1075279822],
    [114, 100, 11, 2281665, 10523776, 18912320, 27300864, 35820737, 44209217, 52466880, 60986497, 69390465, 77763585, 86154961, 94910036, 103191761, 109352530, 120246354, 128491027, 136853012, 145135121, 151295698, 162320976, 170040977, 178796180, 187077777, 195875536, 203988627, 212080149, 220632657, 229569046, 237934167, 245931731, 254817367, 260347538, 271241362, 279877143, 287874643, 296760343, 302290450, 313184274, 319329882, 329520853, 337812497, 346214401, 355374807, 362978385, 372258007, 380564054, 1073744834, 388929175, 395099226, 405812375, 413847762, 1074289603, 1075356612, 420396761, 430184021, 438489153, 445562457, 455620308, 464310800, 470324762, 478985242, 488904341, 495883997, 506393238, 512267930, 520893960, 529317018, 537826909, 548197008, 1075893191, 554178118, 563264733, 573502166, 579614408, 588168729, 596955676, 604509830, 613596701, 621712413, 630772251, 638064326, 646889113, 655938203, 1074863496, 663499848, 672710217, 680433309, 689230428, 696817370, 705442952, 713866458, 722784924, 730338822, 739819209, 1075660741, 748212827, 1074105350, 756202653, 764728028, 1074643914, 772979805, 782168664, 1073887181, 790557208, 798539401, 807334552, 1077303243, 815316489, 1075229644, 824111832, 1077077001, 1076308943, 832099035, 1076588494],
    [118, 104, 1, 357376, 10153153, 18936960, 27325504, 35714240, 44102656, 50689216, 60878416, 69636818, 75822722, 86044176, 94590082, 103191058, 109377090, 119598800, 128144450, 136902275, 145265235, 153810003, 159839764, 169930384, 178877460, 187208403, 195753171, 201782996, 212554883, 220647044, 229151251, 237696019, 243988037, 254201348, 262763732, 271225429, 277673478, 285931141, 296406149, 302740545, 313063107, 321826822, 327874245, 338384067, 346737861, 355111637, 361559750, 369817093, 380292101, 386233472, 1073743877, 395350742, 403502726, 412284631, 419787840, 430362180, 438892035, 447656070, 453441108, 464212995, 471526465, 480940693, 489344069, 497644628, 504402582, 512554566, 522636996, 529233025, 1074286596, 1074830342, 539555395, 547787410, 553973250, 564876355, 572189825, 1075625987, 581472915, 590017683, 595916482, 606295234, 614132737, 1073813506, 621843030, 629601940, 640863447, 648639636, 656839250, 665015298, 672197779, 1075402696, 680563222, 689108631, 699583639, 705918609, 715821589, 722170881, 730917971, 741257286, 747828823, 758303831, 764114113, 774811846, 781383191, 791858199, 798193233, 807318104, 814970385, 823192787, 832483864, 840136401, 848358419, 1075154892, 857649816, 1074654154, 866038488, 1076507597, 1077049295, 1077322697, 1076029387, 1076309959, 1076840398],
    [110, 96, 7, 1899649, 10769601, 19051713, 27317248, 35705920, 44094656, 52483200, 61002945, 69391489, 77780033, 86275664, 94568080, 102937601, 111334401, 119733776, 128349713, 136492161, 144899792, 153515729, 161657921, 170327699, 178681425, 184981014, 195326992, 203619408, 213038807, 220659411, 229013137, 235312790, 245825043, 254703125, 263370391, 270990931, 279213200, 288536087, 296769236, 303889409, 313701975, 321147969, 329055297, 1073742789, 336639513, 345035801, 354710736, 362609857, 370194073, 378590361, 386989714, 397432340, 1073772484, 403085014, 412286555, 422475477, 428914393, 437310681, 447894553, 454229723, 1077188550, 462599900, 472962268, 479395483, 489707092, 496023129, 504419417, 515003609, 521329884, 1075106754, 529708636, 538498573, 548459612, 554892827, 564417665, 1074863043, 570857046, 580441805, 588438620, 598636181, 605861464, 613482066, 623801941, 631019098, 640832665, 647036626, 1075405770, 656184858, 664327757, 674387033, 680590866, 689739418, 697882253, 707843612, 714267676, 724588180, 1075940297, 1074381837, 731035292, 741397660, 747822236, 757355521, 764589084, 1074139080, 1074686927, 773625562, 1076537292, 1076294606, 782022360, 790410776, 798799512, 1077096395, 1076846535],
    [138, 124, 9, 2462848, 10564673, 18953217, 27341953, 35861632, 44250112, 52507841, 61027392, 69668433, 77960192, 86193344, 92755667, 103233042, 109393107, 120000145, 128816656, 134698579, 145176274, 151336019, 161943057, 170890961, 176633346, 185161428, 195507858, 201929940, 212806802, 221091472, 227227286, 235361811, 245839442, 251999251, 263138322, 271423184, 277558806, 288306904, 294343830, 305213017, 312841408, 319502038, 330249752, 336286934, 347024594, 355578904, 363804248, 369841174, 380578898, 388994065, 397358744, 403265044, 411644948, 421989585, 430806608, 436942422, 445338710, 456207897, 464630872, 472985241, 481539674, 487536263, 498667013, 505779264, 512177858, 523458268, 529609948, 540094169, 548517016, 1073747907, 554120770, 563042014, 571684062, 579417748, 590941893, 598709329, 604976711, 612841090, 624121500, 630273180, 639184535, 649311962, 1075076098, 654922900, 663959070, 672739031, 682866202, 688871070, 697513118, 708382277, 716149905, 724784732, 730936412, 739446426, 749843672, 755971591, 764367902, 772355668, 1075613636, 781388890, 791917722, 797914823, 806712861, 815599125, 823505985, 1074579463, 1074333640, 831878813, 840119902, 847591059, 859377285, 865448961, 1074089989, 1074901958, 875779612, 881931292, 890842711, 899003521, 906581076, 916262549, 924169409, 932140126, 940772570, 949982875, 957707997, 965938202, 975148571, 1077013453, 981947539, 991759957, 1000314587, 1076495308, 1073901514, 1076796367, 1075504078, 1008039517, 1016671767, 1025480283, 1033703125, 1076049867, 1077372873],
    [126, 112, 12, 2667585, 10556480, 19076161, 27464897, 35853313, 44111040, 52499584, 60898896, 69407873, 78164993, 86053888, 94453456, 103330945, 109531842, 120012433, 128759315, 137041556, 143086146, 153173520, 162313939, 168391364, 178732625, 187479699, 193417730, 201791062, 212286993, 221034067, 227088006, 235761750, 246748888, 253836944, 263763160, 269570182, 280303128, 285941394, 297317400, 302871190, 310842518, 321339089, 329823425, 336402139, 345075931, 355800664, 361438930, 372814936, 378368534, 386339862, 394993234, 1073745861, 406501082, 411899547, 420311766, 428283094, 436936210, 448443994, 453580358, 462516379, 473241240, 479141529, 490255512, 495523334, 504713820, 512824412, 521215639, 529962517, 537490052, 546381399, 557495834, 564860436, 571822748, 579933340, 588324375, 597071445, 1074550723, 605901448, 613488156, 621747737, 632993434, 638129862, 646541828, 655302361, 664180437, 1075086342, 673912404, 680334939, 689263324, 697373916, 706296916, 714512021, 724244180, 730666523, 739340315, 748240084, 756979421, 1074059396, 764506203, 773405844, 1075381191, 782145181, 789147716, 798955022, 806297177, 815699485, 1073831881, 1075677442, 824005128, 832509582, 840514580, 849253981, 1074389640, 856772678, 866063950, 873537239, 881938438, 891229902, 1075981259, 1076514830, 899502280, 907104454, 1074964428, 916279368, 923226242, 932532252, 1076293581, 1076836303, 1077375946],
    [126, 112, 11, 390209, 10056896, 18445376, 26833920, 35222656, 42333377, 52761102, 60650510, 69170831, 75986448, 84276353, 94704270, 102593678, 111113807, 117929552, 128308940, 137048784, 145313425, 151483600, 161445583, 170251788, 178867793, 186979022, 194868430, 203781714, 210204304, 218493953, 227112644, 237310542, 245199950, 254113426, 260961408, 269315604, 280039631, 287274511, 296088720, 305098262, 313593871, 321222354, 329635468, 338652822, 347148367, 353236032, 363818582, 372576338, 379967052, 386496004, 395267733, 405868687, 413529296, 420433621, 430649488, 437122240, 1073743813, 1074028549, 447958551, 455815184, 463860752, 1075886018, 470765077, 481628370, 487453696, 496324312, 506146896, 514160146, 522581072, 529364679, 540233303, 548737042, 554825235, 565145302, 573902994, 579991251, 587822724, 598298321, 605500057, 613381768, 622581389, 630027911, 640896727, 647443161, 655455817, 664524493, 673795601, 680997465, 688879304, 697431635, 705525255, 714034773, 722564809, 730986131, 741559959, 747730441, 756512266, 765187661, 773148184, 781285001, 790066826, 798742029, 1077205958, 806826521, 1075392521, 815091352, 823096840, 832009930, 840430734, 847869508, 857034328, 865039944, 873952842, 1076973572, 882373646, 890074695, 1074891786, 1074650120, 1075718154, 898461332, 1076515847, 907539662, 915238612, 924316750, 932015700, 1075217347, 1073931267, 1076300747, 1074490379],
    [114, 100, 0, 2290688, 10574912, 18437313, 26825793, 35214465, 43734080, 52122624, 60380161, 68900032, 77692620, 86176960, 94065792, 101012994, 111246860, 119731264, 128661135, 134567618, 145063437, 153941518, 162215503, 169967180, 178451584, 185415312, 195133068, 204273294, 212547279, 220812820, 229071937, 237827790, 1073749955, 1075605507, 243995668, 254237889, 262993486, 271267343, 279533268, 286324307, 295787648, 302716116, 311252549, 322106902, 329735297, 336533138, 347272854, 354507776, 361576016, 369448578, 378599059, 388333197, 395130384, 403002946, 414381782, 421616832, 1076922370, 428807762, 439940825, 447053389, 454374929, 464082516, 473101910, 480730113, 487265364, 495801989, 507049561, 512974551, 520959696, 530380437, 538140183, 546248210, 555546197, 563568283, 571414226, 581523092, 588314131, 596860503, 604705940, 614266581, 623214285, 630929112, 641267225, 647192215, 655701713, 663574021, 674821785, 681008859, 689395210, 698037912, 705517253, 714143443, 722951707, 731338378, 1074319365, 1074867205, 740243162, 748484117, 756506203, 765408794, 1076711368, 773142161, 1074633673, 1075442697, 782186074, 1077290948, 1076254663, 1075226631, 790058698, 1076545483, 798701144, 1074209734, 807089688, 815224394, 824129178, 1076051978, 831862353],
    [118, 104, 13, 1840128, 10597568, 18985984, 27505665, 35894401, 44151872, 52540544, 61060289, 68949184, 77837377, 84399762, 92779666, 102503488, 112176659, 117954066, 126333970, 136057984, 143242901, 154119891, 160159254, 170006160, 176797269, 187674195, 195679956, 202094295, 212211345, 221359768, 227268246, 237114896, 246394515, 254793410, 263599250, 271552131, 277599958, 285718226, 296097297, 305106499, 313513538, 321001040, 330411608, 338679426, 344700439, 354555600, 361739996, 372354776, 378524695, 389428242, 1073750082, 1075868227, 394901013, 405909016, 411817558, 421926609, 430935043, 437245143, 447092305, 454014620, 462010069, 473402581, 481285122, 487044690, 498480210, 504729307, 514446868, 523646162, 532262553, 537908823, 546026583, 554308673, 565816857, 573167252, 579736728, 588232220, 597003867, 606721620, 613029057, 622169755, 630183575, 638301335, 646845464, 655341148, 665816259, 673043676, 680137857, 1076923333, 689278491, 698209436, 1074325444, 705303553, 716672021, 721933394, 731493899, 739120344, 750226581, 756929564, 765048395, 772674648, 1076168647, 783780949, 790484060, 798602891, 806622938, 1074086856, 817475289, 822596818, 831788634, 1073851337, 842640985, 848565914, 1076485068, 856954394, 1075451850, 1075212237, 865711819, 1076797390, 1075760139, 1074729935, 1075017670],
    [110, 96, 13, 638081, 10589312, 18977856, 27497537, 35755200, 44274689, 52663489, 61199056, 69309440, 77962432, 86217857, 94975634, 103019074, 111263313, 120526420, 128307792, 136429265, 145692180, 151361109, 162000981, 169983505, 176527061, 187166933, 195402880, 203682498, 212180032, 218470037, 229109909, 235518977, 246756950, 254013954, 262258321, 271922902, 280097495, 285850689, 296687316, 302355989, 312995861, 319405249, 330429079, 338009088, 347018900, 355594775, 362004115, 372586006, 379843202, 387292688, 1073750018, 395024072, 405354002, 414315095, 422558804, 431306390, 438686352, 445890259, 1075868612, 1076923331, 453744136, 463025818, 472240144, 481279188, 487298632, 497628754, 506982408, 512998931, 522794706, 532148296, 539999380, 546018952, 555292187, 565702792, 573553684, 1074315272, 580466202, 590868680, 596885075, 1073814469, 605632218, 1075400647, 613544600, 622173392, 630789723, 639211082, 647099096, 655727760, 664344283, 672765450, 680653336, 689282128, 697898651, 706320010, 714207832, 723072602, 731485898, 739766937, 748525134, 1074630666, 756913678, 764932697, 773691086, 781709849, 1074915270, 790468238, 798487257, 1076244425, 1076777998, 1075218380, 1074195407, 1076568013, 1075804107],
    [118, 104, 11, 1829952, 8680640, 18478273, 26866817, 35255361, 43643905, 52163584, 60552320, 68940864, 77327488, 84440783, 94106816, 103518800, 110881984, 117995087, 128946833, 136047616, 143160847, 154112593, 162122817, 168326799, 179016336, 185202386, 1073754112, 193229888, 204197523, 210499077, 221614085, 227145234, 235172864, 246140627, 254776017, 263222482, 271306323, 277608069, 288068112, 294647510, 305165330, 313249299, 1076911042, 321884689, 330550996, 335836288, 344716997, 355177168, 361363090, 370144918, 380497110, 389051538, 395292884, 403699222, 414051478, 420238465, 431329477, 436860498, 447605782, 456160338, 464883845, 472501441, 479753877, 487323205, 498438213, 504362582, 514714710, 520901825, 1075349509, 532386311, 539610113, 546862613, 557552327, 564776065, 572290586, 579842580, 590597140, 596399105, 607883847, 614233818, 622194201, 630174356, 640928916, 647788122, 1074321354, 655340116, 664139405, 674483284, 681342618, 691769991, 697693901, 705451073, 714469081, 1075122183, 1074883531, 723358232, 731412053, 739634841, 1076470729, 748524184, 756971140, 764800601, 773690072, 781579853, 790525636, 1075957708, 798986967, 806745613, 815298261, 1074666509, 824021592, 832468484, 1075726286, 1074181252, 840929943, 849245252, 1077330883, 857707095, 866095639, 1073948614, 1076326344],
    [102, 88, 11, 2053248, 9698369, 18863233, 27251905, 35640385, 44028929, 52934348, 60773440, 68811904, 75880002, 86742670, 94240397, 102716608, 109434562, 120297038, 128276047, 136183373, 142988930, 154244226, 161830543, 169737741, 1073752064, 1076391937, 179409986, 186602496, 194247809, 203929228, 212162255, 219806720, 226874882, 238130178, 246380037, 254409794, 1076924418, 263558790, 270401229, 279934597, 288462018, 295304256, 304846350, 311688385, 1074853827, 321877701, 329758284, 336854017, 347305683, 353621716, 363566798, 370801856, 380859987, 389387846, 397016194, 1077222340, 1075403780, 405100047, 414553798, 422181890, 430929477, 437769877, 447198732, 1075675141, 456129748, 1073865671, 465007765, 471062036, 481662470, 489683988, 1075972102, 1074416646, 496227924, 504469137, 514849876, 523466259, 530175496, 538023633, 546821845, 556399810, 565409427, 572118728, 580228690, 588764757, 599225557, 605541909, 613783058, 624391189, 632290964, 638833812, 647075345, 657945685, 664393288, 672241233, 681170568, 689280722, 1074693128, 698332816, 706721360, 714446482, 1074190282, 723498704, 731887120, 1075259337, 1076326347],
    [114, 100, 13, 292928, 8689792, 18757633, 27146305, 35665920, 43923649, 52443328, 60831808, 69220480, 75790336, 84195852, 94255233, 100940482, 109361740, 120216205, 128201231, 134494786, 142916300, 153770573, 161886915, 168065216, 176470668, 1073750016, 1075865601, 185088721, 195310223, 202275009, 210418255, 220606979, 227440769, 235583503, 245895760, 252606529, 260749455, 268974737, 279195727, 285505664, 294304463, 304361679, 311466061, 321542861, 330848465, 335845376, 344234048, 355097101, 1076408261, 363213443, 372791441, 377788608, 388502032, 395745475, 406092366, 411963925, 421042836, 428767233, 437260886, 445135441, 454441546, 465066065, 470849741, 479072853, 487996106, 496540180, 506755790, 514331280, 521583315, 531921550, 1076677572, 539497168, 546740355, 557087246, 1074340995, 564539459, 570964497, 582506513, 588692115, 596644502, 605714629, 613980884, 621810198, 630880389, 638621709, 646976214, 656046149, 664189459, 1076196295, 672010965, 680934026, 689346627, 697989125, 706490903, 713308674, 722909779, 731798034, 739119765, 748042762, 756062349, 765352594, 1076993034, 773599959, 780417666, 790141524, 798907090, 1075698630, 1075448834, 807154327, 815175683, 824072786, 1074680776, 1074959368, 832320087, 1075233737, 1073939465, 1074231243],
    [94, 80, 11, 1939456, 10255552, 18096321, 26744832, 35264577, 43653121, 52041857, 60299328, 68688000, 77076672, 85752960, 94214336, 101982337, 110762177, 119153296, 127768640, 136084544, 144473088, 152934528, 160702529, 168303107, 178887377, 186524239, 1073750017, 193468995, 203432594, 212441681, 219816528, 229612179, 235560660, 245375698, 254392981, 261258966, 271170261, 278798991, 285892180, 294394566, 304095762, 313498131, 319446548, 327948806, 337650258, 347052627, 353001108, 362029057, 372218579, 378699414, 386669190, 395977232, 405379729, 412253782, 422183511, 430545425, 437419542, 447330837, 454959823, 461904515, 472515287, 480885333, 487070403, 496640720, 1075855363, 506363404, 513679887, 1073787847, 522846871, 531235351, 1076943813, 539917900, 1075390404, 546864846, 556695180, 563633752, 571873368, 1076191176, 1075686346, 581861068, 587995718, 1076491276, 1077283789, 1074417670, 597196430, 1074960331, 1075236809, 605584910, 1074726850, 613965464, 622205080, 630750798, 1074228238, 639131352, 647370968, 655908376, 664147992],
    [118, 104, 13, 2388160, 10811584, 18905280, 27424769, 35813569, 44070976, 52590721, 60848256, 69236736, 77920384, 84177616, 94533697, 100954704, 111737040, 119684691, 126253139, 136640512, 142897680, 153370260, 159939221, 168196755, 178583616, 187847377, 195181715, 201882197, 210139859, 221401745, 229177424, 237125139, 243693587, 254956113, 262732432, 271334485, 279509008, 285503632, 295976660, 305287697, 311220241, 321666197, 330977810, 336386193, 346308180, 356143826, 361552081, 371473940, 378043093, 386980379, 398086802, 405675740, 412252380, 423252562, 428660817, 438451411, 445151765, 455372864, 464272597, 470973084, 482146974, 488927360, 497949852, 507312862, 514093056, 1073747911, 522992661, 529988319, 538211032, 548281948, 554858588, 563665504, 571888282, 1075076038, 1075348419, 579739350, 588831264, 596931096, 1073796036, 605175511, 613997280, 622219866, 1074869186, 630341143, 641530398, 647262872, 657333788, 663910428, 672193115, 680940058, 1076978632, 688791126, 700250718, 706106074, 1075939269, 714489433, 722926111, 731804253, 739122710, 748092063, 756314712, 1074122698, 764288662, 773257823, 782135837, 789724759, 798022363, 807301789, 1074667469, 1075727305, 815152857, 823188123, 832467677, 1074442188, 840318617, 848878240, 857095705, 1076815822, 1076308943, 1076590539, 865222295],
    [130, 116, 3, 2119809, 10508481, 18896897, 27416576, 35805376, 44062785, 52943568, 60971136, 69081617, 77748288, 86262338, 94656578, 103275088, 109468179, 119413393, 128606866, 136600066, 145218064, 151411283, 161356369, 170549970, 176708244, 187161232, 194910929, 203702274, 210131667, 218773652, 228868802, 235657814, 245651650, 252336214, 262945478, 271467221, 280091144, 286022343, 296499782, 1073753027, 305160391, 313776791, 319576711, 327834326, 338442886, 347103367, 355719767, 361519687, 371997190, 1076391942, 380657735, 386652374, 396647042, 403593881, 412104857, 1076922370, 422863384, 428366356, 436877332, 446972034, 453925593, 462567638, 470538774, 481583704, 487217174, 495868441, 504379417, 515138264, 521034329, 529545305, 1074322372, 540793434, 548037138, 554719322, 562584276, 571095252, 581984775, 590469704, 596400135, 604396179, 614086803, 1075384327, 623788629, 632412872, 638081620, 646592596, 658234074, 666133144, 672159962, 680679946, 689584211, 700177050, 707420754, 714102938, 722754124, 731527379, 1074880776, 741229077, 750508570, 756045850, 764697292, 772945942, 1075951557, 783172245, 791927319, 797596310, 806509194, 814889110, 823803909, 833870551, 840587981, 848583180, 856701145, 1077272521, 865747077, 875681928, 882530957, 890526348, 899299347, 1075708940, 907690181, 915134614, 924473933, 932338378, 940718166, 1074161611, 949633093, 958028301, 965892682, 1076264970, 1073927181, 1075261390, 1076842447],
    [106, 92, 12, 334016, 8714432, 17076417, 27310272, 35698816, 44087360, 52475904, 59045952, 67407873, 75962960, 86555218, 95098962, 100989056, 109351041, 120109586, 128653330, 134516801, 145545936, 153664146, 162207890, 168097792, 176591445, 187218642, 195762386, 201888339, 212654608, 218665619, 229431376, 235346128, 1073750979, 243866321, 254597776, 260477461, 1075858372, 269032017, 277534849, 285643413, 294163155, 302700609, 310843536, 322099802, 327752209, 336106003, 344529553, 353032193, 361927192, 1074305990, 369809601, 377952272, 386306773, 395500246, 403905236, 412258904, 422763226, 429070932, 437424856, 1075364802, 445970972, 454471824, 462625300, 473094682, 479402644, 488157847, 496581209, 506649242, 513191952, 521329174, 530135769, 538742912, 546495126, 555301529, 563655191, 571800220, 580467225, 588419736, 597490267, 605851712, 612702336, 622770894, 630381142, 637868032, 647409872, 656325198, 664599195, 671422528, 681095895, 1073819594, 689879694, 697629404, 706130000, 1076715469, 714406492, 723292160, 731822606, 740096731, 748204631, 1075678222, 756873755, 765235392, 1074648008, 1074932677, 1076525004, 1077315531, 1074190287, 1075259335, 1076327369],
    [106, 92, 2, 1867840, 10524737, 18913473, 27301889, 35690625, 44210368, 52598848, 60963536, 69376000, 77365248, 86153344, 94699025, 101095441, 111155794, 119308480, 128490131, 136642129, 143038545, 153238096, 159947266, 170164226, 178821651, 186973905, 193370321, 203831443, 210278978, 220495938, 229153363, 237305489, 243701905, 253901328, 260610754, 270827714, 279485139, 285776514, 296106195, 304259155, 1073741826, 313196182, 322082966, 329660435, 336370245, 346202323, 355130885, 361535493, 371603539, 380404309, 388685445, 395090053, 404896400, 413835924, 422239941, 428644549, 438075520, 1073762309, 446700050, 455793733, 464297985, 1074830275, 472521239, 480542850, 489357014, 497818200, 506632406, 514499284, 522852951, 531299926, 540186710, 548176405, 556465686, 564140690, 573741078, 581083283, 588308121, 597695186, 606248979, 615258840, 623681601, 632035992, 640458881, 648813080, 657105428, 664443468, 673848023, 682394261, 688971353, 697997964, 707402391, 715956417, 1075378120, 1077226439, 723163852, 732602964, 741114581, 748329484, 1076450316, 1075161034, 1076219849, 1074671563, 1076786126, 1077053391, 1074192333, 756080153, 1075782596, 1076054982, 764468953],
    [122, 108, 9, 2324480, 10549377, 18937857, 27457664, 35715137, 44103873, 52623424, 61133328, 69254160, 77789376, 86210624, 94566400, 103338577, 111197776, 119896720, 128504337, 136363728, 145062096, 153402963, 162058961, 170227728, 179108437, 187224721, 195608278, 201783510, 212170832, 221035605, 228905040, 237205632, 246217365, 254328342, 262459536, 268892182, 280058580, 1073742786, 285669974, 296270934, 302961239, 313358485, 321714709, 329825942, 336515607, 344389782, 354646208, 361298438, 372030485, 378458775, 388823765, 394984069, 405887572, 1073763267, 411630214, 422362325, 431288980, 437189336, 445315653, 456218772, 461961926, 473480856, 480563408, 487520408, 498162196, 504560136, 515423768, 521065175, 529463320, 537590277, 548239573, 554236486, 564968597, 573894676, 579533509, 590182485, 1074825222, 1074321413, 597736592, 607449172, 615348245, 621738584, 632863832, 641003732, 647452817, 655806994, 666549915, 672618513, 681112282, 690273939, 697916121, 706277914, 716750040, 723081817, 731443866, 740605651, 748247705, 756470418, 767213083, 773281873, 781908495, 790024786, 799325715, 806967833, 814938696, 823851599, 832107098, 842710747, 848779473, 857406095, 865522386, 876265051, 1075389385, 1075926983, 1075164100, 1077004235, 1074147277, 882571983, 1076780047, 890436296, 1075751886, 1076557770, 898824840, 1077349384, 1074751436],
    [126, 112, 11, 2152449, 10672192, 19060928, 27449472, 35707009, 44226560, 52869776, 60872769, 69261505, 78045841, 86530193, 92592850, 103201296, 111598163, 120120002, 128473809, 134535826, 145144400, 153541331, 161931857, 170416209, 176610004, 187087568, 195484307, 201777299, 212359697, 218421778, 226932948, 237926547, 245949058, 251976274, 260880402, 270981651, 277274643, 288258131, 1073744066, 294050388, 302430292, 310829139, 321936085, 327604884, 335984788, 344383699, 355752664, 361159188, 369539092, 380691030, 389044757, 395483863, 405201105, 414210709, 1074289603, 420403802, 428652626, 439411414, 447765077, 454081115, 465197146, 472309777, 481614557, 487758359, 498254045, 506362067, 515168797, 521189915, 531808285, 539916307, 546355931, 556851862, 565467800, 1075348420, 1073796037, 573889117, 580311710, 588429470, 598917213, 605452956, 613866206, 621983966, 632576600, 640212994, 1074869191, 646756562, 657742360, 665378882, 674552477, 680573595, 1076980680, 691191965, 697727580, 705616602, 714782938, 725244122, 733274243, 739948634, 748059356, 758178326, 764860958, 772978718, 781613596, 791994563, 797891098, 807057434, 817518618, 825548803, 831445658, 840358494, 848476254, 859461786, 867491907, 874166426, 1076470726, 882565721, 890411607, 899342873, 906803346, 916120281, 1075963851, 1076240330, 1075730381, 923966103, 932897433, 1075220430, 1074722764, 1077348297, 1074229199],
    [118, 104, 5, 497664, 8747008, 18550785, 27343040, 35862721, 44251201, 52639745, 60897344, 69286016, 77674496, 84244672, 94048385, 101300752, 111360129, 120011282, 126449680, 134855376, 145166544, 153565906, 161847875, 170332176, 176781520, 184891923, 193411669, 203897490, 212668435, 218462336, 227261009, 235223635, 243743253, 254229074, 263000147, 268793920, 277592721, 285817494, 294075029, 304978070, 312939088, 319388304, 327760598, 336018133, 346921174, 354095297, 361330768, 369703446, 380598482, 388340419, 396038209, 403389124, 414152722, 422680772, 430379152, 436812374, 445332036, 453849687, 464623684, 470898689, 478493331, 489492627, 497392259, 504453185, 512440836, 523204690, 529347287, 540121092, 545995396, 554513047, 565287044, 571562177, 1073743876, 579156691, 590313618, 598544595, 606444035, 1074286595, 613628617, 621621783, 632772629, 640522326, 647182921, 655560850, 665688086, 672225409, 680737289, 689115154, 699881685, 705280144, 714291849, 722669650, 733436053, 738966033, 1074829321, 747835602, 758601813, 764132049, 773675732, 780777552, 790592024, 797415616, 1075365832, 807230036, 814192768, 824007316, 830969920, 1074080711, 1076449221, 840923800, 849173012, 1074627522, 1073865674, 857701080, 866089560, 1075984332, 1077305295, 1075753934, 1077077965, 1076309963, 1076844486],
    [102, 88, 12, 2406464, 10420416, 18946113, 27334657, 35723393, 44112065, 52631744, 61020224, 69408768, 78027472, 85917696, 94574720, 103193104, 111354064, 119766674, 128358992, 136249472, 145424980, 153524880, 161709586, 169803840, 179346001, 187268758, 195240080, 204511953, 212434454, 220405840, 229677713, 237600342, 245571600, 254843409, 1073752003, 261185047, 269296215, 279230464, 286350423, 296663571, 305070682, 313097942, 1076124612, 321960023, 330236634, 337870418, 346995283, 355140244, 361437830, 371424978, 378601554, 388282496, 395673305, 405471764, 413448384, 1075348421, 420839001, 1073793986, 431012567, 439288474, 445734103, 456178327, 464192212, 470489606, 479559193, 489732119, 495788247, 504044230, 512842903, 523156179, 531563034, 538279577, 548321939, 554508311, 1074336713, 563911384, 571539666, 580688472, 588972699, 597465752, 605749851, 613096006, 1074884556, 1076724742, 622762581, 630259858, 639572494, 647797272, 656081627, 664738510, 1074132938, 673094165, 680337559, 1077284808, 1074684871, 689904270, 698260181, 705757202, 1076010957, 715070030, 1075762190, 723425941, 731578907, 1075260363, 1076589519],
    [106, 92, 11, 383104, 10582208, 18970688, 27359360, 35747840, 44252816, 50714816, 61436562, 69418704, 76012241, 86602450, 94584400, 101046336, 111768082, 120266435, 126343697, 136933970, 144915984, 151377920, 162624022, 170860245, 176675473, 187519700, 195763843, 203945985, 212955734, 221191701, 229111873, 1073746884, 238244567, 246357653, 252172881, 263287510, 271523413, 277969543, 287832257, 296841878, 304815619, 312998017, 321737364, 328432136, 338893832, 347593432, 1074807746, 355685015, 361986632, 371924547, 380762128, 1073786883, 388846164, 397614152, 405928080, 412570323, 420707016, 431168712, 439867992, 447959575, 454114841, 465033752, 473125463, 479665818, 489814224, 496456275, 504855179, 515055240, 521369736, 531757136, 1076942856, 1075382214, 539841044, 546798091, 554778329, 565697176, 571953683, 579944025, 588765204, 597521051, 605109913, 613931156, 1074097097, 1076467653, 622285459, 631077582, 639049242, 647485524, 656241179, 664238667, 672603866, 680622663, 689428692, 698184411, 706574926, 714546778, 1075177420, 723350107, 731347659, 740129422, 747731463, 1076234251, 756120263, 1074416647, 765295118, 1074706381, 1077337102, 1075782602, 1076064207],
    [114, 100, 3, 352257, 10573953, 18962625, 27482304, 35870720, 44128321, 52648064, 60905473, 69296720, 77813824, 86448657, 92624913, 102973954, 111614545, 117790801, 128139970, 137173650, 145422852, 151607442, 162224132, 170738371, 179116754, 187366084, 193550546, 204167364, 212812421, 221313734, 229448210, 235493394, 245580418, 255015045, 260659794, 269179475, 279134786, 1073743874, 288168018, 296417924, 302340753, 313219204, 322126020, 329717905, 338360900, 346773572, 353196628, 363676291, 1074288644, 372456133, 378337941, 388973061, 1075359877, 397621253, 406518487, 411392721, 420305620, 431177860, 440072727, 447158481, 453859988, 464732228, 1076947139, 473118789, 481360518, 487283219, 498024517, 507181655, 512833684, 520446081, 529610964, 540080710, 548356293, 1076440134, 555293334, 565245958, 573390915, 582679191, 588847830, 596466196, 606945283, 614128216, 621885460, 629889747, 637886529, 646773269, 656095443, 664888016, 1076712393, 672848408, 681261075, 688609939, 698442384, 705493717, 714815635, 724779012, 731568856, 739842646, 746938561, 755825237, 764491860, 773939728, 1074902986, 781900440, 790313043, 798580928, 806951446, 815357952, 823746688, 1077272525, 1075718092, 1076249547, 832135232, 1073907656, 1074190286, 1075258319, 1076056007],
    [114, 100, 12, 2480128, 8657089, 18462913, 26982528, 35371072, 43628545, 52017281, 60537024, 68794433, 75765825, 86629004, 94091264, 103387662, 109427330, 117848589, 128571980, 136942286, 145086592, 151403085, 162107982, 168434384, 178903756, 187273870, 193600080, 201971841, 210219602, 218765968, 227137537, 235508436, 244071121, 254409231, 1073745861, 1074554885, 260674132, 270915648, 277625361, 285848215, 294263312, 304470208, 311278279, 319533782, 327800897, 336345745, 344437458, 355064332, 361765068, 369734231, 378673216, 386521281, 394900183, 403028482, 411449997, 422181455, 428718663, 436712082, 445004493, 455736015, 462787096, 472783385, 480901775, 487166484, 496236685, 504371340, 1076403144, 512471638, 523115225, 529791053, 538284632, 545635010, 556669529, 563345613, 571324935, 579449367, 587577922, 598612633, 605411989, 1075368962, 612995732, 621942912, 630577685, 639089163, 646689430, 655882771, 663754764, 671988359, 680891032, 1075125255, 689174541, 696522753, 1075661766, 1074375686, 705147410, 714603091, 722221649, 1076754378, 1077285828, 730575382, 739768979, 746854529, 756388568, 764418124, 773184213, 1074938819, 1073907657, 1074192393, 1076044803, 781712083, 789714944, 798472907, 806492352, 815127125, 823638667, 832027211, 1076326411],
    [122, 108, 3, 1178688, 8757441, 18454529, 26843265, 35362944, 43620417, 52009153, 60528640, 68917440, 76676096, 84508864, 94083136, 101842048, 109937164, 120273551, 128162512, 134846980, 143366787, 152173760, 160268876, 170735747, 178494096, 185178820, 193698307, 202474189, 210493006, 221067267, 228825680, 235641411, 244178000, 252551248, 263010371, 269195971, 277715525, 286622289, 294509712, 1073742851, 304822799, 312711696, 319658629, 327524481, 336452624, 346765903, 353361553, 361603088, 372062403, 378110080, 386916049, 397097679, 404062737, 411950288, 420297363, 428972551, 438950919, 447848455, 453843541, 462527047, 472505415, 481402951, 487660242, 495821008, 504094414, 513219284, 521247431, 531225799, 540123335, 546126355, 554801799, 564780167, 573677703, 1074024455, 1074834439, 579680979, 588350093, 596368910, 605100690, 613253836, 621534862, 630266450, 638950089, 647070285, 655350865, 664214164, 672504329, 680106628, 688905233, 696623169, 705763858, 714447497, 722311685, 730956301, 1076683714, 739064403, 747477701, 755597312, 1075904517, 765278742, 773167689, 780769860, 789938385, 1073825801, 1074373636, 798833366, 1076221894, 1075193862, 1076518856, 1075752968, 806191756, 815610518, 822452225, 832387670, 839753872, 1077074890, 1075524618, 848108053, 856260672, 864885461, 873824401, 882317908, 890706452, 898439829, 1077366731],
    [130, 116, 11, 2521088, 9157760, 18479105, 26867905, 35387584, 43644993, 52164672, 60553216, 68941952, 78018624, 84655296, 93976705, 101055057, 111016578, 117963282, 126196866, 136870543, 145609427, 151386641, 161348290, 168426132, 176528578, 187070656, 195940947, 202111702, 210369108, 219019971, 227310293, 235650048, 246272531, 252443158, 1073754112, 262011458, 268958354, 277641813, 285580354, 296604307, 302774934, 311032532, 319683075, 327973525, 336698371, 345111172, 354286082, 361527829, 369466370, 1076903938, 377879185, 387054084, 395180675, 403807363, 414349457, 423088664, 428588096, 438860303, 448000665, 453376721, 461896274, 470916291, 481458385, 490328730, 495450834, 504232515, 512859203, 523401233, 1073776643, 532271706, 538049092, 548126231, 556955729, 565441113, 571079188, 581680791, 589855439, 596636379, 605158084, 614046866, 623278208, 1074321412, 632934938, 640400983, 648575567, 655096406, 665566935, 672430608, 683397725, 689290244, 697858134, 708301400, 714587156, 723024086, 733467352, 739539600, 748141716, 1075386311, 758895325, 765041874, 773355542, 1075138502, 784061085, 790084692, 798521494, 1074631624, 809226781, 815037136, 823508036, 833876505, 840202832, 848673988, 859042521, 866024156, 873839748, 884593370, 891189916, 899259410, 1074913225, 1075718091, 909628056, 916355612, 924425298, 1076262853, 932180507, 941521500, 949468372, 957346459, 1077315534, 1074195404, 965735003, 1076569037, 1076064202],
    [110, 96, 8, 1818688, 10336321, 18864193, 27252929, 35772544, 44030081, 52549696, 60938240, 69195777, 77316224, 86096588, 94492864, 102873740, 111001729, 119650892, 127778817, 136559181, 144425152, 152009231, 1073752064, 1076391937, 161593868, 169721921, 178747984, 186890893, 194756608, 202340943, 210623047, 220445389, 228442305, 237599313, 246276167, 253999629, 261053074, 269343431, 279830727, 286243347, 296319697, 303020627, 311411220, 321485457, 328194582, 338681878, 345880769, 1076934594, 354908688, 361618055, 372105351, 378518227, 1077201859, 1074334723, 389118613, 1074611142, 395303510, 405790806, 412072595, 422672981, 429766657, 437502551, 1073847236, 1075436548, 447838741, 454154776, 463321217, 471057047, 1075712968, 480868881, 487709336, 496220878, 504349396, 514292432, 521132694, 531619990, 538163726, 1074950085, 546273935, 554687190, 563337865, 573563094, 580106894, 589789840, 596498951, 605149912, 613669449, 623763463, 630569112, 640776917, 1076790279, 647224009, 655481432, 663992910, 672121428, 681531929, 689289240, 697549527, 705649234, 714455128, 722453140, 731863641, 739621080, 747880983, 755980818, 764664329, 772758226, 1074189321, 782195353, 790584025, 1075259338, 797932239, 1076323275],
    [106, 92, 13, 2259968, 8666241, 17054913, 25443393, 33831937, 42351744, 50740224, 59129024, 69368960, 75906112, 86146240, 92708428, 101481993, 109485708, 1073747969, 120094218, 1075339264, 1075881985, 126262988, 136477760, 143040012, 153622158, 162037322, 170399438, 178814666, 187743888, 193756745, 204084881, 212369034, 220862033, 227319315, 235699913, 246027985, 252755541, 260865673, 271193617, 1076416450, 280018512, 285884100, 294543051, 304617038, 311451215, 319166100, 327982803, 336485963, 344331796, 355515920, 362184205, 369497684, 380681936, 387350157, 396891662, 403750549, 411844102, 420503247, 428218068, 437689880, 446070349, 454440470, 462855896, 470703627, 479606422, 487603911, 496025109, 504790733, 513160790, 521191125, 529555087, 538588759, 546741848, 554589835, 563885650, 572178137, 579616454, 587873860, 596663823, 1074598851, 1074877443, 605697559, 613432903, 622509657, 629948038, 639383186, 646749779, 655113798, 663371396, 672806551, 1075152902, 680541703, 689348248, 697710294, 705707655, 713858707, 722091524, 1074387975, 1075719175, 731526871, 1076782084, 739950233, 748435154, 1076265928, 1073923080, 756727321, 765212178, 1074213829, 1077113861],
    [110, 96, 11, 2390145, 9575488, 17964224, 26483841, 34741376, 43129856, 51649601, 60669570, 68426753, 77887681, 85204161, 93855308, 102612546, 1073746498, 111441985, 1074809795, 119152206, 127777986, 135798412, 143292494, 152706574, 1074305025, 161332226, 169352908, 179075661, 1075372033, 187172432, 194649742, 204054031, 211295756, 219183116, 229385809, 236592846, 246128274, 251928196, 262961869, 271058576, 277093892, 287940175, 296777732, 304612880, 310779604, 321494735, 327841934, 338437649, 346299990, 352591556, 363445334, 371488769, 380773588, 386276884, 397123282, 402923076, 414218308, 422716436, 1075905540, 430186134, 438942870, 447511053, 456402515, 464232018, 472938692, 480773840, 486940308, 497786386, 504002574, 515253784, 521641557, 529561676, 540157076, 546807509, 554727628, 564930257, 572792534, 581549270, 590379140, 599140056, 605527573, 613447820, 624305816, 631512598, 640269334, 646609102, 657204881, 665427599, 674003597, 683026008, 689413781, 697850585, 706239129, 716449427, 721821268, 731404889, 741483604, 748444375, 758392531, 765221399, 773347865, 783558163, 790387351, 1074086854, 798775895, 1073846216, 1075171269, 1074670535, 1076518858, 1075749898, 1076294603, 1077097483, 1077374921],
    [98, 84, 1, 1841152, 8672384, 17071296, 25459840, 33848320, 42236992, 50756609, 59145409, 69140110, 75922497, 85727296, 92697742, 101088385, 111083214, 119281792, 126252238, 136248846, 143029838, 153360577, 1073747969, 161414222, 169613504, 176583694, 186914817, 193754639, 203692161, 210531983, 218824337, 227573330, 235828880, 245635137, 252582402, 261125651, 1075331970, 269155857, 277756420, 286291539, 294682322, 302535890, 311311044, 319749652, 328088132, 336623315, 345013906, 352867474, 362035779, 1073778948, 369382400, 378804821, 1074848709, 386823696, 395582165, 1075907395, 403373649, 411325632, 420362372, 428539601, 437532803, 445413071, 453967572, 463099414, 470685890, 479133268, 487620114, 496653910, 504641731, 512687764, 520639506, 529406082, 538631895, 546985622, 554571842, 563805848, 571373264, 580131477, 588971608, 596538960, 605304835, 614129239, 622074389, 630224531, 639303192, 646739535, 1074358215, 656080600, 663245906, 1076212680, 1077015560, 672849431, 681203414, 689626775, 696538176, 1077291978, 1076516809, 1075228614, 1076813773, 1075777483, 1074743244],
    [118, 104, 1, 1588289, 9829569, 18635904, 27024448, 35413184, 43801600, 52321409, 60710081, 69098561, 77069954, 85474433, 94264321, 102786577, 109337617, 1073744578, 119012354, 127417537, 1074287555, 136341137, 142892177, 152566850, 160971777, 169895633, 176446673, 1074829313, 186121410, 193478288, 203572943, 210132486, 220225223, 228719683, 235421200, 245515791, 252206612, 262168199, 270539911, 278264897, 288121862, 293887569, 304111175, 311819393, 319307472, 329278545, 336092756, 346160323, 352861776, 363750484, 369647316, 380370629, 388636245, 1075374533, 397035094, 403070534, 413924421, 421534791, 430589654, 436756116, 447487630, 455998994, 464413844, 470179526, 480255175, 489553618, 497698454, 503733894, 513826311, 522198023, 531496594, 1076428806, 1073830919, 539641366, 548019861, 555875459, 564946118, 573316622, 581041155, 590111814, 598482510, 605420545, 1075684297, 614614607, 623639557, 632037070, 640574484, 648683029, 657325650, 663903767, 673997958, 682359941, 690626261, 1075957704, 699294932, 705969175, 715277967, 722476563, 731012695, 739523671, 1074669515, 747642515, 756440780, 764419667, 772955799, 1076260804, 781466775, 790257165, 797974227, 806510295, 815423117, 823409879, 831938188, 840589005, 848715276, 857366093, 1076794381, 1075246026, 1077097482, 865492556, 1077363724],
    [98, 84, 13, 2405440, 8707136, 17087553, 25476225, 33864897, 42253313, 50773184, 59161664, 67550208, 77903040, 84336271, 92716160, 101113359, 111842894, 117776080, 126147584, 137008846, 145309393, 151568019, 1073747969, 161789056, 168090752, 176627346, 185122323, 195343360, 201776847, 212418193, 218676819, 226942543, 237671950, 243736274, 251976896, 262837902, 268901970, 279764115, 285906049, 1075336131, 293936784, 304929875, 311071937, 321469969, 330095635, 336237569, 346635857, 352902740, 361403457, 369958486, 378574424, 386718798, 394731026, 403496078, 411901654, 420517592, 428392147, 439147731, 445464149, 454596313, 461954708, 470621718, 479762009, 487120404, 495787670, 504927897, 513080858, 520429072, 529569432, 538230474, 546897495, 553983568, 563648025, 571784778, 1074829252, 579395284, 1075103685, 588289560, 596967066, 604847765, 614006423, 622116490, 630521434, 638402261, 647560727, 1074077639, 655670794, 1075662792, 663542990, 1074628618, 671956501, 680320014, 1074381769, 689503959, 697630426, 1073882050, 1075998667, 1076799430, 1076292557, 1076573132, 1077113868],
    [134, 120, 13, 1874945, 10394752, 18652289, 27040961, 35560512, 43949056, 52856386, 60726464, 68983873, 78174799, 86023886, 94799554, 1073746242, 102645264, 1074809795, 111729167, 119840401, 128353282, 136199760, 145676433, 153394897, 1074305025, 162301134, 169754320, 178838223, 186949137, 195462274, 203832914, 212507730, 221174353, 228891729, 238061268, 245505683, 254728209, 262184590, 270671443, 279741582, 288136790, 296671441, 304127502, 312614611, 321684494, 329833103, 337681998, 344497816, 354557459, 363627598, 372701765, 378183385, 388906201, 397444756, 406386840, 411737753, 422485531, 428777030, 439369238, 447519766, 456164948, 464976389, 470851144, 481312470, 489462998, 498107924, 506919621, 512400921, 520658520, 531512345, 537962138, 548707996, 557381720, 562994694, 573455513, 579905242, 590650908, 596957719, 1075372996, 604937862, 613459482, 623918742, 632069270, 641137285, 1075913733, 646487576, 655664284, 664682128, 674822168, 682532443, 688430808, 697607772, 707804246, 716479580, 725154008, 732864219, 738893401, 747675272, 758004825, 765240989, 773118679, 781493276, 791035538, 799710354, 806942939, 816750235, 1076195271, 823174746, 833920732, 840227415, 848338440, 856990940, 866533074, 875207890, 881761990, 890828891, 1076728838, 898670280, 907847197, 916388437, 1075168264, 925253138, 933927954, 941554325, 949790429, 958331605, 1074139081, 1074676682, 966567517, 974445207, 983103643, 1073916875, 991492123, 1076551628, 1000274453, 1075786701, 1077113869],
    [98, 84, 1, 2448513, 10802369, 17104000, 25492480, 33881280, 42269760, 50789505, 59178177, 67566657, 77430351, 86299649, 92732417, 103455298, 111213634, 119373519, 128374350, 137140944, 143195779, 153443329, 161928910, 170826243, 176749571, 1073747969, 186482191, 195483150, 204118530, 211876866, 218945043, 228425359, 237673090, 245431426, 254596820, 262495297, 271358544, 277413571, 286054099, 296049857, 305437266, 310967875, 319608467, 329866243, 1075333123, 338598083, 346095298, 355032131, 363648532, 1074298882, 371890370, 380329681, 388814484, 397187600, 403494483, 414154389, 422877906, 430931669, 438621313, 447649923, 456097365, 463918734, 473209362, 481263125, 489477716, 498375314, 506027203, 514118721, 523147331, 530240528, 539713041, 548182672, 555406480, 564878993, 572045911, 580572368, 589913219, 597211799, 606821969, 614397137, 622377687, 631174225, 1073795015, 639416854, 647951377, 1074606020, 655931927, 1076715461, 664728721, 672971350, 681235536, 689748630, 698137302, 1075681225, 1075176396, 1075975110, 1074951114, 1077064714, 1077341133, 1076570059, 1076316104],
    [98, 84, 8, 2417728, 10271937, 18668545, 27188288, 35445953, 43834433, 52223105, 60742784, 69131264, 78300674, 86163074, 94297280, 1073744514, 103466050, 111328450, 119832144, 1074287555, 128245393, 136494082, 145409218, 153411089, 1074829313, 161659970, 170574978, 178577105, 187745807, 194821249, 203718160, 212911759, 219986945, 228884112, 237297233, 246342737, 253541441, 263503571, 271631951, 280280595, 288285713, 1075364804, 295993040, 305446483, 313575119, 322223763, 330228881, 338452183, 347004119, 355638994, 363783377, 369810951, 380804626, 388293760, 397581906, 405071040, 413949463, 422501399, 428793417, 439525010, 447013888, 455892567, 464444503, 470736585, 480036437, 487890127, 495902345, 505202389, 513055823, 523001495, 531553431, 1073818565, 537583303, 546750100, 555411086, 563011081, 571915860, 580576974, 1076446217, 587914823, 597353998, 605330575, 613080711, 622370326, 630908494, 1074107399, 639420053, 647273487, 1075171270, 655924950, 664585749, 1074672584, 1077048328, 672579284, 680967700, 689479318, 697867862, 1077321677, 1075769291, 1076832204, 1076323274],
    [102, 88, 3, 351232, 10818560, 17120385, 25509057, 34028672, 42286081, 50805952, 59194432, 67451969, 77927616, 84639438, 92748800, 103093376, 109805198, 119870528, 126574287, 134848081, 1073747969, 145569363, 151748110, 160284306, 168123520, 179385537, 185179793, 196034261, 204551169, 210460239, 221093077, 229455507, 235232448, 244170322, 252665045, 263271489, 271556311, 279920277, 288175635, 294354510, 304979093, 313341651, 319512207, 330276375, 338769025, 344677903, 355442327, 364459606, 369450048, 380608087, 388972053, 395271317, 406533720, 414030869, 423179926, 430792389, 1075339717, 439721497, 447692373, 1075872707, 456734230, 462380117, 472751189, 479157269, 490419928, 1073793988, 498441817, 507066070, 514677829, 523607769, 531454981, 540751384, 546520666, 554278609, 1074341830, 565009541, 574305944, 579714770, 588977872, 597253844, 605241050, 615882393, 1076188098, 622532176, 630808212, 638164497, 647697936, 656104666, 663961242, 671989266, 681252496, 689659034, 697515546, 706436186, 1074896842, 1075703751, 714824730, 1076758476, 1074157513, 723082772, 1075227592, 1076556747, 1077097483, 1077366733, 731471444],
    [122, 108, 11, 2014273, 10822721, 18684992, 27073728, 35462144, 43850880, 52370497, 60759041, 69147777, 77511681, 86320129, 94313665, 103242446, 111221966, 119454849, 128263297, 1073746882, 136519247, 1074809795, 145038993, 153704527, 161553998, 169786561, 178595009, 186850959, 195370705, 202210000, 1074305025, 212403858, 220642449, 228794063, 237575827, 245979343, 254090833, 260637843, 270974033, 279402574, 287383182, 296822293, 304528593, 310976196, 321461843, 330258628, 337976849, 344523859, 354860049, 363404819, 371808399, 379657742, 389201622, 394855443, 403250820, 411925136, 422755990, 431040085, 438786062, 445589144, 456170575, 464068307, 472864900, 481476118, 489760405, 495811152, 506005010, 514890959, 520976912, 529073363, 540056719, 545857028, 556750852, 564725330, 571645465, 579411524, 590305348, 598279890, 1075363844, 606558350, 615589589, 624082518, 631447055, 640243727, 647169623, 657497103, 664083976, 672758484, 680854544, 689657939, 697474713, 705635864, 714808906, 723089940, 731029209, 739444247, 747970248, 756644500, 764740688, 773529098, 781524552, 790321363, 798164695, 1073816517, 806690440, 815486995, 823303769, 831465176, 1075926024, 840530516, 848626896, 857415306, 1075158985, 865818771, 873792656, 882581194, 1075695564, 1074660362, 890439319, 1074161606, 898573912, 1076276167, 1076556747, 1077097483, 1077374925],
    [102, 88, 9, 1301504, 10310657, 17136704, 25525248, 33914048, 42302592, 50822337, 59210753, 67599425, 77419649, 85720590, 92765313, 103365200, 109673552, 119633553, 127663758, 136175183, 144528577, 1073747969, 152917057, 161218126, 170743314, 177995470, 187520658, 195558546, 203284111, 213203539, 221075026, 227769427, 237362690, 1075344323, 1076933635, 245462609, 255146707, 261323987, 271048388, 279016977, 287914640, 294222992, 303291520, 313998023, 321869332, 328433299, 337501711, 347166421, 355023376, 361331728, 371711556, 1077201220, 379680465, 389363859, 397139461, 1074336645, 405355216, 414144084, 420052176, 430440146, 1074873218, 439827079, 447567058, 455859397, 464861715, 471038995, 481025093, 488061527, 498030292, 504618176, 514938389, 523713031, 530963650, 1073848455, 540104341, 548878407, 555318923, 564518018, 572332630, 581916308, 1075964872, 588504128, 598824533, 605887190, 614325967, 622664214, 631766098, 1076506569, 639056599, 647593675, 656931858, 664222359, 672759307, 682351749, 689388055, 697925195, 1076780998, 707124290, 1075743755, 714939030, 724032644, 1074710474, 732421124, 1074206669, 1075275724],
    [110, 96, 9, 353409, 10312897, 18701313, 27089985, 35478657, 43998272, 52386944, 60767810, 69164032, 75843074, 85941440, 94322306, 1073744386, 101008514, 1074287555, 111599119, 117923536, 127876290, 134831813, 142951618, 153672901, 159866384, 1074829313, 170605584, 176774789, 185558598, 193814151, 203873999, 210321102, 219243520, 229039759, 235363920, 246103120, 252272133, 260916872, 271113221, 277307024, 285818510, 293946434, 304667781, 313605780, 319120449, 329702991, 338377872, 344286209, 355401427, 363937364, 370108038, 378338902, 386489925, 397491732, 403654293, 1075363845, 413719621, 420036110, 428958784, 439287315, 445201998, 454387351, 1073811144, 464453203, 472595664, 479553239, 487390934, 496974850, 504718935, 1074617926, 1075686340, 512581319, 523173523, 531709652, 537879558, 546111126, 555293846, 563037717, 1076491209, 1077031945, 571301383, 580320856, 588725778, 596731072, 605625430, 613237832, 621608470, 630668882, 638936599, 647429656, 655834834, 1077306314, 663569608, 672734422, 680346632, 689372888, 697900054, 705644245, 713907783, 723205841, 730162369, 1076007943, 739704472, 748371601, 756114560, 765148689, 772760774, 1075234764, 781663890, 789530197, 1074212811, 798703185, 1076848589],
    [102, 88, 13, 515072, 10108032, 17153024, 25672833, 34061313, 42449985, 50707648, 59096128, 67484800, 77216768, 84541006, 92781761, 102382656, 109706894, 119160000, 126483982, 1073747969, 136060546, 143261390, 153353938, 161226434, 169991825, 178798288, 185581126, 193836564, 203685522, 211557954, 218732181, 228851282, 237518352, 247043798, 254287368, 261217871, 1075340354, 269467334, 277722708, 287432209, 296230536, 302888660, 311549583, 321404560, 1076145091, 1076417477, 330929814, 337763921, 346562248, 352949973, 363068946, 371727944, 1074867208, 378115669, 388095697, 396106754, 403543576, 414047754, 420224531, 431592982, 439500313, 445767375, 454276634, 464666329, 470933007, 481924694, 489832089, 495443072, 503944725, 514997849, 520608832, 529372760, 537386176, 547896912, 1076709319, 554679814, 563590807, 571219667, 580105818, 588889613, 596385427, 1074108363, 605271706, 615374538, 622444109, 629939795, 1075171273, 638424728, 648928906, 1074660292, 655343238, 663598740, 674094666, 1073896454, 1075748874, 680769242, 689553101, 697808471, 706330253, 1076021261, 713922264, 1074475980, 1077113868, 722974423, 731362839],
    [126, 112, 13, 2458625, 10737729, 18717888, 27106368, 35495040, 44014657, 52272128, 60791809, 69180609, 78095874, 86235137, 94346369, 103104132, 111385732, 120038978, 128834243, 1073744642, 1074287043, 136814095, 145204354, 153999363, 159882832, 1074829313, 170368719, 179152462, 187553923, 195903185, 201826000, 210476562, 219150416, 229745682, 237846161, 243768848, 252681875, 263038478, 270784641, 280042514, 285974162, 294648016, 305243282, 313597074, 321758926, 329504961, 338509329, 346267140, 353083090, 363722756, 372090510, 379927556, 386375312, 395026002, 403699856, 414295122, 422648914, 430153284, 439220292, 447194306, 1075367877, 455425092, 463707844, 472358479, 481294415, 489792722, 1074601988, 497368260, 505912975, 514848911, 522552513, 531700946, 538156681, 548264003, 556106817, 565001809, 571448915, 581826692, 589661313, 596590229, 606992580, 614040581, 624238167, 630431433, 638580752, 647857347, 655703638, 663723731, 673031764, 682621135, 691347159, 697540105, 705666579, 714703941, 724563983, 731201046, 739891337, 748520579, 758455959, 765188179, 773695188, 783621655, 789814857, 798742675, 807240707, 1075921929, 815087254, 823777481, 832144581, 840253142, 848943177, 857581204, 1074110408, 865025621, 1075701702, 874240019, 882746900, 890191381, 1076238279, 899274761, 907904067, 1075212234, 915357397, 924571859, 932807813, 1076790220, 1073933261, 1076573131, 1077113867],
    [118, 104, 9, 2070720, 10517633, 17169600, 25558144, 33946688, 42466433, 50723840, 59243521, 67632193, 77568128, 86015169, 92798145, 101307913, 1073749954, 111122432, 119569409, 128424523, 136739904, 143128076, 1075599361, 153065536, 161512513, 168294028, 178257486, 1075359744, 1076950016, 186932810, 195795022, 204198990, 210501189, 220617740, 227014220, 235798086, 245783628, 1077218244, 1074359300, 252680911, 260568780, 269352582, 279207626, 287808139, 296474254, 304086158, 311295494, 321281228, 330012814, 336451090, 346316426, 353483408, 361879251, 370146888, 380263492, 386898511, 394909321, 403570374, 413818052, 1076726790, 1074653190, 422025931, 430691854, 437255816, 446692366, 455498892, 464230414, 473290260, 480672896, 489134603, 498456148, 504102597, 514227200, 521255440, 532010708, 539254282, 546281999, 554956501, 564559040, 571587152, 582342292, 588250824, 596377093, 607149713, 613915158, 621401801, 630193672, 638320261, 648699012, 1076498440, 1074942981, 655334031, 663606994, 674258513, 680639184, 688772754, 699030532, 1075218375, 1074192391, 705951317, 716201489, 1076036547, 1073964035, 724277966, 732681422, 740293838, 749756113, 755619401, 765099533, 773298902, 781448725, 790265485, 798464662, 806614677, 815431373, 823630422, 831379026, 840597069, 848418451, 856806931, 865195603],
    [114, 100, 8, 2202817, 8772800, 17161344, 25549824, 33938496, 44022784, 51215945, 59238090, 68672585, 77577408, 1073744834, 1074285570, 1074566083, 1074850819, 84901516, 95012420, 101309508, 110747149, 119913485, 1076696064, 126975630, 136439435, 143253124, 1075140609, 152690317, 1075420161, 161987726, 1075701760, 168918606, 178382347, 185196036, 1076506625, 1077048321, 195411085, 202472974, 211936843, 218750660, 228187725, 237083649, 1077313540, 245491403, 254508753, 262134993, 270130893, 278388361, 287685837, 294512208, 302873737, 312851533, 321504260, 330006161, 337632401, 346135681, 355058820, 363560529, 371186769, 379567168, 386787024, 395411150, 404733056, 411926217, 422307475, 429382857, 439205394, 445480457, 453502538, 462937097, 472366158, 1073924038, 479166156, 489678550, 497925714, 506166801, 512222858, 522181649, 530684993, 537886220, 546170512, 556252366, 563437271, 571336208, 581417998, 588742164, 596108810, 606977682, 613768791, 623634131, 632143570, 639074004, 649062038, 656121359, 1074210759, 1076323269, 664239700, 674227798, 681287247, 688881228, 699393558, 706461384, 714432151, 724157636, 731627016, 739597847, 749463123, 756784847, 764903060, 774628883, 781950607, 790480469, 798736008, 807257621, 815513160, 824034965, 832423637],
]


def fill_table(table, me, low, high):
    if high - low == 1:
        for place, word in enumerate(STEPS[low]):
            table[place] = jnp.int32(word)
        return
    middle = (low + high) // 2
    lax.cond(
        me < middle,
        lambda: fill_table(table, me, low, middle),
        lambda: fill_table(table, me, middle, high),
    )


def neighbours(col, row):
    x = lax.rem(col, 2) * 2 + lax.rem(row // 2, 2)
    y, z, core = col // 2, row // 4, lax.rem(row, 2)
    found = [(x, y, z, 1 - core)]
    for move in (1, 3):
        for other in range(2):
            found.append((lax.rem(x + move, 4), y, z, other))
            found.append((x, lax.rem(y + move, 4), z, other))
            found.append((x, y, lax.rem(z + move, 4), other))
    return [{"col": y * 2 + x // 2, "row": z * 4 + lax.rem(x, 2) * 2 + core} for x, y, z, core in found]


def split(value):
    high = value.astype(jnp.bfloat16)
    return high, (value - high.astype(jnp.float32)).astype(jnp.bfloat16)


def spread_kernel(
    stored_ref, slots_ref, halves_ref,
    table, tile_even, tile_odd, halves_even, halves_odd, load_sem, store_sem, send_sem, recv_sem,
):
    active, half, block = stored_ref.shape[2:5]
    rows_per = active // CHUNKS
    col, row = lax.axis_index("col"), lax.axis_index("row")
    beside = neighbours(col, row)
    sibling = beside[0]
    tiles = halves_ref.shape[0]

    barrier = pltpu.get_barrier_semaphore()
    for device in beside:
        pl.semaphore_signal(barrier, inc=1, device_id=device, device_id_type=MESH)
    fill_table(table, col * lax.axis_size("row") + row, 0, len(STEPS))
    pl.semaphore_wait(barrier, len(beside))

    def hop(source, slot, chunk, place, device):
        return pltpu.make_async_remote_copy(
            src_ref=source,
            dst_ref=slots_ref.at[slot, pl.ds(chunk * rows_per, rows_per)],
            send_sem=send_sem.at[place],
            recv_sem=recv_sem.at[slot, chunk],
            device_id=device,
            device_id_type=MESH,
        )

    def arrival(slot, chunk):
        piece = slots_ref.at[slot, pl.ds(chunk * rows_per, rows_per)]
        hop(piece, slot, chunk, 0, sibling).wait_recv()

    tile = (tile_even, tile_odd)
    halves = (halves_even, halves_odd)

    def load(source, turn):
        return pltpu.make_async_copy(source, tile[turn], load_sem.at[turn])

    def store(turn, role):
        return pltpu.make_async_copy(halves[turn], halves_ref.at[role], store_sem.at[turn])

    def prepare(turn, order, role):
        load(slots_ref.at[0], turn).wait()

        @pl.when(order >= 2)
        def _():
            store(turn, 0).wait()

        for mirrored in range(2):
            @pl.when((role & 1) == mirrored)
            def _():
                @pl.loop(0, active)
                def _(line):
                    for slot in range(half):
                        value = tile[turn][line, slot]
                        high, low = split(value.T if mirrored else value)
                        halves[turn][line * half + slot, :block] = high
                        halves[turn][line * half + slot, block:] = low

        store(turn, role).start()

    steps = table[0]
    sends = table[1]

    @pl.loop(0, steps)
    def _(step):
        word = table[3 + step]
        slot = word & 63

        @pl.when((word >> 30) == 0)
        def _():
            chunk = (word >> 6) & 7
            device = {"col": (word >> 10) & 7, "row": (word >> 13) & 15}
            landing = (word >> 17) & 63
            place = (word >> 23) & 127

            @pl.when(((word >> 9) & 1) == 1)
            def _():
                arrival(slot, chunk)

            @pl.when(slot < 2)
            def _():
                piece = stored_ref.at[slot, 0, pl.ds(chunk * rows_per, rows_per)]
                hop(piece, landing, chunk, place, device).start()

            @pl.when(slot >= 2)
            def _():
                piece = slots_ref.at[slot, pl.ds(chunk * rows_per, rows_per)]
                hop(piece, landing, chunk, place, device).start()

        @pl.when((word >> 30) != 0)
        def _():
            order = (word >> 14) & 15
            for chunk in range(CHUNKS):
                @pl.when(((word >> (6 + chunk)) & 1) == 1)
                def _():
                    arrival(slot, chunk)

            for turn in range(2):
                @pl.when((order & 1) == turn)
                def _():
                    @pl.when(slot < 2)
                    def _():
                        load(stored_ref.at[slot, 0], turn).start()

                    @pl.when(slot >= 2)
                    def _():
                        load(slots_ref.at[slot], turn).start()

                    @pl.when(order >= 1)
                    def _():
                        prepare(1 - turn, order - 1, (word >> 18) & 15)

    prepare((tiles - 1) % 2, tiles - 1, table[2])

    @pl.loop(0, sends)
    def _(place):
        hop(slots_ref.at[0, pl.ds(0, rows_per)], 0, 0, place, sibling).wait_send()

    for turn in range(2):
        store(turn, 0).wait()


def spread(stored):
    most = max(entry[1] for entry in STEPS)
    active, half, block = stored.shape[2:5]
    return pl.pallas_call(
        spread_kernel,
        out_shape=(
            jax.ShapeDtypeStruct((SLOTS,) + stored.shape[2:], jnp.float32),
            jax.ShapeDtypeStruct((14, active * half, 2 * block, block), jnp.bfloat16),
        ),
        in_specs=[pl.BlockSpec(memory_space=pl.ANY)],
        out_specs=(pl.BlockSpec(memory_space=pl.ANY),) * 2,
        scratch_shapes=[
            pltpu.SMEM((max(len(entry) for entry in STEPS),), jnp.int32),
            pltpu.VMEM((active, half, block, block), jnp.float32),
            pltpu.VMEM((active, half, block, block), jnp.float32),
            pltpu.VMEM((active * half, 2 * block, block), jnp.bfloat16),
            pltpu.VMEM((active * half, 2 * block, block), jnp.bfloat16),
            pltpu.SemaphoreType.DMA((2,)),
            pltpu.SemaphoreType.DMA((2,)),
            pltpu.SemaphoreType.DMA((most,)),
            pltpu.SemaphoreType.DMA((SLOTS, CHUNKS)),
        ],
        compiler_params=pltpu.CompilerParams(
            collective_id=0, has_side_effects=True, vmem_limit_bytes=60 << 20
        ),
        name="spread",
    )(stored)[1]


def multiply_kernel(
    halves_ref, rows_ref, offs_ref, krow_ref, kcol_ref, kcnt_ref, out_ref,
    blocks, done_first, done_second, pairs, pair_count, bucket, bucket_count, facts, in_sem, out_sem,
):
    grid = lax.axis_size("row")
    tile_j = lax.axis_index("row")
    col_id = lax.axis_index("col")
    tiles, each = halves_ref.shape[:2]
    half = offs_ref.shape[1]
    active = each // half
    block = halves_ref.shape[-1]
    lanes, _, kept = krow_ref.shape
    slots = 2 * half
    steps = 2
    most = steps * slots * slots

    def load(place):
        return pltpu.make_async_copy(
            halves_ref.at[place], blocks.at[pl.ds(place * each, each)], in_sem.at[place]
        )

    waves = ([0, 1, 2, 3, 8, 9, 10, 11], [4, 5, 6, 7, 12, 13])
    for wave in waves:
        for place in wave:
            load(place).start()

    first = rows_ref[0, 0]
    bits = [rows_ref[1, 0] ^ first, rows_ref[2, 0] ^ first, rows_ref[4, 0] ^ first]

    def rank(value):
        return sum(
            jnp.where((value & bit) != 0, jnp.int32(1 << place), jnp.int32(0))
            for place, bit in enumerate(bits)
        )

    def shifts(tile_x, tile_y):
        both = ((tile_x, tile_y), (tile_y, tile_x))
        return [rank(offs_ref[x, slot, y]) for x, y in both for slot in range(half)]

    tile_is = [col_id * lanes + lane for lane in range(lanes)]
    tile_ks = [lax.rem(tile_is[0] + tile_j + place, grid) for place in range(3)]
    right_moves = [shifts(tile_k, tile_j) for tile_k in tile_ks]

    for place in range(lanes * active):
        pair_count[place] = 0
    for lane in range(lanes):
        for step in range(steps):
            left_moves = shifts(tile_is[lane], tile_ks[lane + step])
            for slot in range(slots):
                move = left_moves[slot]
                turn = move if slot >= half else 0
                left_base = (2 * (2 * lane + step) + slot // half) * each + slot % half
                for other in range(slots):
                    apart = move ^ right_moves[lane + step][other]
                    place = lane * active + apart
                    count = pair_count[place]
                    right_base = (8 + 2 * (lane + step) + other // half) * each + other % half
                    reach = move if other < half else apart
                    pairs[place * most + count] = (
                        turn | reach << 3 | left_base << 6 | right_base << 14
                    )
                    pair_count[place] = count + 1

    widest = 4
    room = 2 * kept
    for place in range(lanes * (widest + 1)):
        bucket_count[place] = 0
    for place in range(lanes * active):
        pair_count[place] = place << 3 | pair_count[place] << 7

    def put(lane, size, word):
        place = lane * (widest + 1) + size
        filled = bucket_count[place]
        bucket[place * room + filled] = word
        bucket_count[place] = filled + 1

    for lane in range(lanes):
        count = kcnt_ref[0, lane]
        together = 8

        @pl.loop(0, kept // together)
        def _(part):
            found = []
            for offset in range(together):
                item = part * together + offset
                row = rank(krow_ref[lane, 0, item])
                place = lane * active + (row ^ rank(kcol_ref[lane, 0, item]))
                found.append(jnp.where(item < count, pair_count[place] | row, 0))
            for offset in range(together):
                item = lane * kept + part * together + offset
                products = found[offset] >> 7
                facts[item] = found[offset] & 127
                begin = jnp.where(products > 0, ((products - 1) & 7) + 1, 0)
                put(lane, (begin + 1) >> 1, item | begin << 13)

                @pl.loop(0, (products - begin) >> 3)
                def _(more):
                    put(lane, widest, item | (begin + 8 * more) << 7 | 1 << 12 | 8 << 13)

    blocks[tiles * each] = jnp.zeros((2 * block, block), jnp.bfloat16)
    def gather(word, size):
        fact = facts[word & 127]
        row = fact & 7
        base = (fact >> 3) * most + ((word >> 7) & 31)
        products = word >> 13
        ones, twos = [], []
        for place in range(2 * size):
            inside = place < products
            code = pairs[base + jnp.where(inside, place, 0)]
            source = ((code >> 6) & 255) + (row ^ (code & 7)) * half
            ones.append(blocks[jnp.where(inside, source, tiles * each)])
            other = blocks[(code >> 14) + (row ^ ((code >> 3) & 7)) * half]
            twos.append(jnp.concatenate([other[:block], other[block:]], 1))
        total = jnp.dot(
            jnp.concatenate(ones, 1), jnp.concatenate(twos, 0), preferred_element_type=jnp.float32
        )
        total = total[:block] + total[block:]
        return total[:, :block] + total[:, block:]

    done = (done_first, done_second)

    def add(lane, word, into, total):
        again = ((word >> 12) & 1) == 1

        @pl.when(again)
        def _():
            done[lane][into] = done[lane][into] + total

        @pl.when(jnp.logical_not(again))
        def _():
            done[lane][into] = total

    def store(lane):
        return pltpu.make_async_copy(
            done[lane].at[pl.ds(0, kept)], out_ref.at[lane, 0], out_sem.at[lane]
        )

    for lane in range(lanes):
        for place in waves[lane]:
            load(place).wait()
        head = lane * (widest + 1)

        @pl.loop(0, bucket_count[head])
        def _(place):
            done[lane][bucket[head * room + place] & (kept - 1)] = jnp.zeros((block, block), jnp.float32)

        for size in range(1, widest + 1):
            count = bucket_count[head + size]

            @pl.loop(0, (count + 1) >> 1)
            def _(place):
                start = (head + size) * room + 2 * place
                one = bucket[start]
                paired = 2 * place + 1 < count
                two = bucket[jnp.where(paired, start + 1, start)]
                total_one = gather(one, size)
                total_two = gather(two, size)
                into_one = one & (kept - 1)
                into_two = jnp.where(paired, two & (kept - 1), kept)
                if size < widest:
                    done[lane][into_one] = total_one
                    done[lane][into_two] = total_two
                else:
                    add(lane, one, into_one, total_one)
                    add(lane, jnp.where(paired, two, 0), into_two, total_two)

        store(lane).start()

    for lane in range(lanes):
        store(lane).wait()


def multiply(halves, tile_rows, offsets, kept_rows, kept_cols, kept_count):
    block = halves.shape[-1]
    half = offsets.shape[1]
    tiles, each = halves.shape[:2]
    active = each // half
    lanes, _, kept = kept_rows.shape
    items = lanes * kept
    products = 2 * (2 * half) ** 2
    smem = pl.BlockSpec(memory_space=pltpu.SMEM)
    return pl.pallas_call(
        multiply_kernel,
        out_shape=jax.ShapeDtypeStruct((lanes, 1, kept, block, block), jnp.float32),
        in_specs=[pl.BlockSpec(memory_space=pl.ANY)] + [smem] * 5,
        out_specs=pl.BlockSpec(memory_space=pl.ANY),
        scratch_shapes=[
            pltpu.VMEM((tiles * each + 1, 2 * block, block), jnp.bfloat16),
            pltpu.VMEM((kept + 1, block, block), jnp.float32),
            pltpu.VMEM((kept + 1, block, block), jnp.float32),
            pltpu.SMEM((lanes * active * products,), jnp.int32),
            pltpu.SMEM((lanes * active,), jnp.int32),
            pltpu.SMEM((10 * items,), jnp.int32),
            pltpu.SMEM((10,), jnp.int32),
            pltpu.SMEM((items,), jnp.int32),
            pltpu.SemaphoreType.DMA((tiles,)),
            pltpu.SemaphoreType.DMA((lanes,)),
        ],
        compiler_params=pltpu.CompilerParams(vmem_limit_bytes=60 << 20),
        name="multiply",
    )(halves, tile_rows, offsets, kept_rows, kept_cols, kept_count)


def local(stored, tile_rows, offsets, kept_rows, kept_cols, kept_count):
    halves = spread(stored)
    return multiply(
        halves, tile_rows.T, jnp.swapaxes(offsets, 1, 2), kept_rows, kept_cols, kept_count.T
    )


def solution(mesh):
    in_specs = (
        P("col", "row", None, None, None, None),
        P(),
        P(),
        P("col", "row", None),
        P("col", "row", None),
        P("col", "row"),
    )
    out_specs = P("col", "row", None, None, None)
    return jax.shard_map(local, mesh=mesh, in_specs=in_specs, out_specs=out_specs, check_vma=False)
```

time: 138 us -> 124 us (0.90)
  the two profiles are of different devices: /device:TPU:5 before, /device:TPU:29 now
where the time goes in v5:
time: 124 us; the launch traced here: 123 us
  Pallas kernels  123 us (99%)
    pallas_call x1, Pallas kernels, spread(): pl.pallas_call(spread_kernel, out_shape=(jax.ShapeDtypeStruct((SLOTS,) +...  107 us
    pallas_call x1, Pallas kernels, multiply(): pl.pallas_call(multiply_kernel, out_shape=jax.ShapeDtypeStruct((lanes, 1,...  16.3 us

profile of v5, /device:TPU:29, one launch (start us, length us, event | category | flops | bytes accessed | tf_op | source)
XLA Modules:
  0.0 123.1 jit_solution(1874971545719689570)
XLA Ops:
  0.0 106.8 %spread.1 = (f32[33,8,2,128,128]{4,3,2,1,0:T(8,128)}, bf16[14,16,256,128]{3,2,1,0:T(8,128)(2,1)}) custom-call(f32[2,1,8,2,128,128]{5,4,3,2,1,0:T(8,128)} %stored_ref.1), custom_call_target="tpu_custom_call" | custom-call | tf_op jit(solution)/shard_map/spread/pallas_call | solution.py:298
  106.8 16.3 %multiply.1 = f32[2,1,32,128,128]{4,3,2,1,0:T(8,128)} custom-call(bf16[14,16,256,128]{3,2,1,0:T(8,128)(2,1)} %get-tuple-element.6.halves_ref, s32[8,16]{1,0:T(8,128)} %bitcast.4, s32[16,2,16]{2,1,0:T(2,128)} %bitcast.3, s32[2,1,32]{2,1,0:T(1,128)} %krow_ref.1, s32[2,1,32]{2,1,0:T(1,128)} %kcol_ref.1, s32[1,2]{1,0:T(1,128)} %bitcast.5), custom_call_target="tpu_custom_call" | custom-call | tf_op jit(solution)/shard_map/multiply/pallas_call | solution.py:505

commit v6 on v5

v6 whole, which is shorter than its diff:
```python
import jax
import jax.numpy as jnp
from jax import lax
from jax.experimental import pallas as pl
from jax.experimental.pallas import tpu as pltpu
from jax.sharding import PartitionSpec as P

MESH = pl.DeviceIdType.MESH
CHUNKS = 4
SLOTS = 32
STEPS = [
    [118, 104, 12, 111, 88, 2242753, 9576576, 17965120, 26353856, 34742272, 42213505, 50601985, 60572290, 67379265, 77740033, 84156609, 92963464, 102113865, 111034441, 1073744578, 1074293762, 119683137, 1076663235, 1074844675, 126517960, 135668233, 1075118080, 144588809, 1073824768, 153237633, 1074105345, 160072264, 169222857, 178143433, 185211530, 1074651136, 1075979264, 1076258817, 193626632, 202777225, 212222152, 218766026, 228885069, 237387848, 245662221, 254165000, 262029449, 271596175, 279216781, 287719560, 296762063, 302949073, 312229954, 321927695, 330072786, 337780946, 345784322, 1076534212, 355482191, 363102925, 371335762, 379338946, 386537994, 397181010, 404890130, 1075503045, 414073484, 421796436, 430736018, 438444178, 445792846, 455350932, 464289810, 470688262, 479347214, 488127189, 496272019, 504513230, 512367178, 521052753, 531513868, 538458709, 546603731, 556679756, 564402900, 571384337, 580010638, 589568532, 596935251, 605037127, 615400140, 622344725, 630489619, 638591623, 647512592, 655899285, 663659153, 672014918, 681067088, 690625048, 697991894, 705569414, 714621584, 724179672, 731554327, 739123910, 748176080, 1075786758, 757733976, 765100630, 772809415, 781869707, 791288472, 798655126, 806363655, 815424011, 1077374983, 823829207, 832201291, 840606295, 848978635, 857383575, 865763862],
    [110, 96, 13, 109, 86, 2326721, 8650880, 17039424, 25427968, 33816768, 42336321, 50724993, 60712585, 67502081, 77824001, 84279489, 94267081, 102989953, 109587019, 1073743810, 117965316, 1074020352, 127821321, 136544321, 143141387, 153511437, 162234370, 1073782785, 1075897345, 170273422, 178677325, 187400322, 195439118, 203843213, 212566210, 220605006, 227148421, 237397709, 246514249, 254159566, 260571780, 270427209, 278921808, 288456713, 296364751, 302514884, 312755204, 321233092, 327811653, 338307663, 344457796, 354698308, 362807824, 371949634, 378143237, 1076170756, 1074883588, 388639247, 396362448, 405693648, 414285961, 420086469, 428354187, 439247952, 1076728837, 1075177477, 447062020, 455748239, 463471248, 472802320, 480879116, 487074507, 497304708, 506176138, 512756434, 522470596, 531341898, 537922066, 548299920, 1076502470, 1075736582, 556376780, 563087954, 571491985, 581673674, 588253842, 597051027, 606445636, 613689877, 621823697, 632389833, 638847574, 647382611, 656777348, 664021589, 672155153, 682336778, 689179286, 697714387, 707371660, 714344982, 722880019, 732537420, 739519189, 747652689, 756785812, 764684949, 773563092, 1077054407, 781454038, 790340180, 798728724, 1074450376, 1074731971, 1075540995],
    [134, 120, 11, 133, 110, 2259008, 10626112, 18636801, 27025473, 35414145, 43802817, 52322496, 60711040, 69099584, 77734912, 86399682, 94265344, 1073744322, 103176194, 109454915, 120087182, 1074287427, 1074823168, 128342146, 134620163, 142893647, 153507906, 160179279, 170181136, 176448015, 187324419, 193733647, 203735632, 210002639, 220362880, 227288271, 1073804228, 235463186, 243688147, 252207687, 262305984, 269354195, 1076955077, 279233168, 285631059, 294412820, 304764995, 311297107, 321700565, 330195157, 335962643, 346191872, 353240083, 363643413, 372138005, 377774735, 386687636, 397039747, 403448975, 411984470, 422363797, 430858389, 436626067, 447371459, 453903507, 1074100168, 464306773, 472801365, 480797262, 487350996, 498227342, 504497172, 514351630, 520905300, 531913425, 537273539, 547906254, 556947662, 562439299, 571523735, 581051520, 590633617, 596533910, 605315657, 612917895, 624056398, 630326356, 639943376, 647258633, 654860807, 1077254086, 664937664, 674519633, 680419862, 689201865, 696804039, 708100696, 716462609, 722601172, 730751702, 1075170311, 741655064, 749885454, 756155540, 766821080, 773224454, 781722825, 789865097, 800375448, 807172167, 815277193, 1074666505, 823182039, 832338119, 840574102, 848847372, 856736343, 865892487, 873997385, 882401868, 890290711, 899053702, 907682838, 915956364, 923329106, 933001223, 941106185, 949510860, 956883666, 966162502, 974791766, 1075730444, 982049426, 991328454, 999957718, 1075487691, 1076028427, 1076308938, 1076588493],
    [110, 96, 9, 109, 86, 401601, 8667264, 17055936, 25444416, 33832960, 42352769, 50741249, 59129921, 67641870, 75907265, 86526545, 92815888, 102375440, 109724306, 120343251, 126370384, 1073741824, 135929936, 143245972, 151667218, 162286163, 168313488, 177873040, 185221842, 195840659, 201867984, 211427536, 218776146, 229394963, 235414158, 245490326, 252723350, 260580046, 271739461, 279044694, 286277718, 294134350, 305293957, 312599254, 319832278, 329515733, 338848261, 346153494, 353386518, 363070037, 372402885, 380355287, 388235797, 1073765314, 1075360773, 396905105, 405398088, 413401749, 1077202883, 422070801, 430563848, 436994575, 447236817, 455729864, 463872649, 1074604998, 471223002, 480895624, 489038345, 1076456456, 496388634, 506446489, 514204361, 521685659, 531350167, 539370057, 1076736009, 546720410, 556515927, 562954322, 572017179, 581943897, 588120210, 1077004228, 597183067, 1074143175, 607109849, 613155407, 622750424, 632013335, 638321295, 647514843, 657441305, 663487183, 1075730378, 673082008, 680116948, 688783570, 697715290, 705282644, 713949202, 723413528, 730448404, 738598977, 1075219403, 748579416, 756531804, 763764865, 773308956, 780541953, 1074451404, 790086364, 798474908, 1074996173, 1076061197],
    [110, 96, 13, 109, 86, 1884160, 8820737, 18677953, 27041984, 35430400, 43950081, 52207744, 60596288, 69116097, 77504641, 84449472, 94159040, 102563841, 111059009, 1073744834, 119718082, 128516675, 136624836, 1074287427, 1074823168, 144883714, 153682051, 161790532, 170049666, 178061441, 186956420, 194822208, 204013763, 210549319, 220381250, 229179395, 235715271, 245153920, 253558849, 260880903, 1073792965, 271237711, 277658247, 288293585, 1074076614, 1075401735, 296403663, 304396804, 313205267, 1075159044, 1075962884, 319862915, 329958031, 338625169, 346735119, 353540229, 363790929, 371761685, 378050560, 386712208, 397345297, 405316309, 411473985, 420266512, 430645907, 438870677, 445028481, 453829198, 464200403, 472425045, 478995086, 488028758, 498401365, 504423060, 512923653, 522920531, 529588756, 538360342, 548732949, 554869386, 562469057, 571785879, 582287509, 588692182, 596951639, 607453397, 613589706, 621863636, 630241347, 639181458, 647412374, 655671831, 664347154, 672309834, 680040512, 689226455, 697901778, 705864202, 713595008, 722264590, 731456082, 1076239370, 739041998, 747804741, 1075737544, 1077055433, 756193477, 764199632, 772847619, 780976720, 1074720715, 789635668, 798013635, 1076833228, 1076590541],
    [94, 80, 3, 93, 70, 1179713, 8683584, 17072256, 25460736, 33849536, 42369153, 50757825, 59146305, 68288513, 75923457, 86280848, 93454529, 103058128, 1073741824, 110231681, 120121041, 128223760, 135037444, 144581326, 153782276, 162195026, 168592004, 178135630, 187336836, 195618449, 202146372, 211821135, 220891204, 229303826, 235700932, 245244430, 1073762308, 254445764, 262727185, 270541327, 279218768, 287893073, 295707343, 305048131, 313190098, 320742030, 1074826051, 330213571, 338355858, 346038927, 353534663, 363767811, 372164230, 379855557, 388933763, 397329926, 405021189, 1074327174, 414106694, 422742611, 430187077, 1076701445, 439272646, 447908563, 455352453, 463005204, 472951509, 480911874, 488171220, 498117205, 506208320, 1076452226, 513328790, 523405843, 531243074, 538083911, 546891348, 556837397, 564928640, 572049110, 582126227, 590094336, 596804103, 605603414, 615557781, 623517890, 630769174, 640295042, 647554708, 657203392, 663913095, 1075426250, 1077008329, 1075184647, 1074165707, 1077321676, 1075766216, 1076044808, 1076318157],
    [110, 96, 10, 109, 86, 1892544, 10280960, 18669696, 27058240, 35578049, 43966593, 52877890, 60907586, 69132289, 77520961, 86418958, 94822414, 102851074, 111598274, 1073746178, 1074809795, 119973582, 128377038, 1074298880, 136763394, 144793730, 153921233, 162062864, 170317954, 178348226, 187737104, 195617488, 204169745, 210303695, 221291728, 229335697, 235469455, 246195345, 254206542, 262889681, 271114832, 277666451, 288400464, 296444497, 303094484, 312910926, 321315470, 330260558, 1073798084, 336132687, 346858513, 355000976, 363815054, 370203156, 380675216, 388980942, 394852879, 405185678, 414146574, 420797077, 430744657, 437215890, 445700756, 453813847, 462643734, 471128597, 479241359, 487547474, 496302744, 504530585, 512975510, 521069192, 529849045, 538347224, 546530006, 554490579, 563250713, 571433490, 1075393479, 579918420, 588031511, 596599506, 1076975557, 605346389, 613582425, 622027350, 631167578, 638748377, 647944730, 655402191, 664074776, 671917719, 1075154889, 681499354, 688841416, 697345039, 1074655178, 705485395, 714007112, 722896024, 1076770763, 731183704, 739172872, 747676751, 1077304328, 756996762, 764192471, 772594195, 781616152, 1075742668, 1074193350, 1076044806, 789903576, 798393432, 1076325325],
    [126, 112, 7, 125, 102, 2418880, 8691777, 19030081, 25477185, 33865729, 42254465, 50643137, 59162624, 67551424, 75939968, 84320782, 94790350, 103082048, 109494336, 119956046, 128247936, 134783503, 144622290, 1073741824, 153510542, 161802240, 168338063, 178176658, 187064334, 193503823, 201648784, 210289282, 218669775, 229401233, 235203152, 243843778, 252092494, 262955601, 268757520, 277398018, 287752853, 294035598, 304898769, 311225044, 319341122, 329827030, 335978702, 346841617, 352643792, 1073762306, 1074836419, 362725970, 371769878, 379740289, 386179265, 398248599, 404668946, 411746840, 421683201, 431286296, 438992899, 447267414, 455237825, 464158915, 473745943, 480821910, 489971926, 497713283, 507300439, 514245333, 523526166, 531267651, 540854999, 545964760, 554615385, 562339841, 573989013, 582281432, 587907736, 596558489, 604283009, 615800982, 624224408, 631685653, 638501401, 649486357, 657236121, 663546388, 673628757, 680444633, 691429461, 699179097, 705489556, 713736792, 724852822, 733276248, 741122265, 1076948933, 747815561, 758538453, 766287897, 773507610, 781369929, 789996115, 798400722, 807062106, 814924297, 823550483, 832086168, 840616602, 848478921, 857105043, 865640664, 874171098, 1076691977, 882270931, 890675346, 898427476, 907583576, 915841106, 924229650, 1074092998, 1075419079, 932749336, 1075176395, 1075979275, 1076252612, 1074706381, 1077332936, 1074473930, 1076584396],
    [98, 84, 5, 97, 74, 2308224, 10305665, 18686081, 27074753, 35594304, 43851841, 52371648, 60628993, 69567106, 77537408, 86194240, 94191809, 102703104, 111510018, 1073744514, 119748608, 127746049, 1074287555, 1074823168, 136675394, 144914624, 152911937, 161948244, 170229954, 178993809, 185287377, 195502740, 204440210, 212550357, 220936401, 229605970, 237716053, 243874387, 254223060, 263160338, 271270549, 277813776, 287777300, 295805646, 302727761, 313210961, 320971278, 329990677, 336534096, 346137230, 353059345, 363542545, 372212434, 378092243, 386753239, 396468814, 403258003, 411918999, 422027476, 428556433, 437197456, 445850200, 455581780, 464861272, 470639191, 1073798086, 1075389384, 1075930120, 479404568, 489136276, 498415640, 504193559, 1076210628, 512959192, 522690580, 531970264, 538395353, 546513560, 557136024, 563560985, 1076479946, 571957839, 579418643, 588855834, 597254678, 604969680, 614032086, 622410458, 630669977, 1074147271, 639187546, 647586390, 1076781003, 655843983, 664353434, 672752278, 681009871, 689398287, 1075753925, 1077071820, 697778777, 1074739145, 1077368781],
    [110, 96, 13, 109, 86, 2557953, 10256577, 17105024, 25493696, 33882176, 42270720, 50790529, 59179073, 67567617, 78055553, 85753985, 92733633, 103507665, 111215312, 120138434, 128098512, 137062033, 145031811, 1073741824, 153551442, 161941697, 170172498, 179135619, 186712720, 195635778, 203595920, 212559441, 220529219, 229048850, 237439041, 245669906, 254633027, 262472195, 270598672, 279652480, 287481872, 296576003, 304153168, 313076354, 321036368, 329999889, 336396869, 346489554, 355149888, 363110610, 372335685, 380043922, 388573698, 396664978, 1073764354, 405628611, 413466819, 422085263, 430647296, 1075349507, 439445125, 445448325, 455813312, 463241281, 472999621, 479002821, 489194191, 498018894, 506553861, 512557061, 523184654, 530350081, 1074319365, 538535445, 547914319, 556739214, 563544648, 572090005, 581468687, 590293710, 597255893, 607455892, 615975443, 622265032, 630670998, 641141395, 1074868169, 647430792, 655976021, 666176212, 672613910, 682953236, 1076715466, 689784407, 699861715, 706150920, 714557142, 723059340, 733416019, 1075680264, 1075176388, 1075979268, 740116119, 748225036, 758450772, 764888662, 773391052, 782059031, 790168140, 1076249612, 798836439, 1074181063, 1077078982, 1076563917, 1074755531],
    [106, 92, 10, 105, 82, 1925248, 10313920, 18702336, 27091008, 35610817, 43999297, 52387841, 60776577, 69059214, 78055119, 84238543, 94593166, 1073744834, 1074287555, 102613710, 111370446, 1074823168, 119390734, 128779857, 136536078, 145318610, 152945230, 162465427, 170090574, 179010068, 186892498, 196019923, 201810629, 212564628, 220578384, 229574163, 235496149, 246119124, 255132885, 260661845, 271547095, 280298581, 285565455, 294216341, 304839252, 313853077, 319251013, 330267287, 338626131, 344547861, 355432983, 364184597, 369451663, 377971205, 388987479, 397215441, 405895189, 413385298, 422142034, 430376079, 1073805254, 439449813, 446939794, 455696530, 463930383, 470246021, 481392725, 488882706, 497639442, 1077221381, 505873999, 512057423, 523335829, 530956816, 1075409860, 539821585, 547734224, 557021782, 564987537, 1076987850, 572899984, 582187542, 1074126792, 588842585, 599095835, 607346715, 614139482, 624130774, 632513115, 639305370, 649427675, 657678555, 664471066, 674593435, 682844315, 689505945, 699628182, 706283033, 1075711943, 1074684873, 1076012041, 716535899, 723191514, 731871768, 739837657, 748649176, 1076287436, 757037656, 765426328, 1075261387, 1076849613],
    [110, 96, 10, 109, 86, 354304, 8724673, 17121472, 25641025, 33898624, 42418305, 50675712, 59195585, 67452992, 75965070, 84240576, 92749825, 101017728, 109387841, 117760657, 126436050, 1073741824, 134685262, 142960704, 151315153, 159851022, 170740240, 176480785, 187517520, 193273985, 201646673, 212683472, 218833487, 227205844, 237849232, 243605505, 252529301, 260514510, 269306581, 277553807, 286081622, 294208018, 302860821, 311108303, 319635990, 328026709, 336273935, 344801942, 353462337, 363922003, 1073761220, 370098821, 378356438, 387007174, 395921422, 405864979, 412435032, 420037266, 428950150, 436920916, 446253198, 456196819, 462766616, 470368850, 478864020, 487942743, 498139795, 504709848, 512836166, 520806932, 529623233, 539828370, 1074303939, 546652824, 554779142, 563440151, 573382866, 1074852802, 1076958214, 580470862, 590159890, 597248206, 607068246, 613859865, 622160599, 632234134, 1075146696, 638534341, 647414361, 655714967, 665657426, 1076727751, 672088645, 680968921, 689006721, 699343062, 1074651081, 705643013, 714523289, 722561025, 732897302, 1075708933, 739959386, 748363928, 756736666, 765141208, 773513946, 781918296, 1074165706, 1077322700, 1076028428, 790290970, 798695448, 1076304843, 1075538893],
    [106, 92, 3, 105, 82, 2070720, 10330113, 18718913, 27107393, 35627072, 44015616, 52404352, 60031618, 68796546, 77570240, 85956736, 94216321, 101032592, 110363330, 119522001, 1073744066, 127899648, 1074287555, 134718099, 1074823168, 144450194, 153076241, 161454144, 168272595, 178004498, 186630801, 195401872, 201826899, 211558994, 220185169, 228833812, 235381267, 245113554, 253616847, 262388308, 269066951, 278790291, 287171087, 296204942, 302359248, 312344787, 320725583, 329619664, 336175623, 345620482, 354287635, 363313678, 369730183, 379174978, 387842131, 396606164, 403546649, 411673159, 420741122, 429777551, 438811214, 445489753, 1073797127, 453354064, 463061186, 472383555, 480614480, 487432921, 495297040, 503964373, 514326659, 522557456, 529375897, 539623623, 546037785, 555989652, 563347522, 571073173, 581417678, 589955143, 596369561, 1075389381, 1075930117, 604627541, 614990019, 623378435, 629924057, 640286727, 646701145, 1076212681, 654959125, 665452679, 674234903, 680772118, 1077013446, 688906776, 699400919, 705684056, 716178007, 1076508616, 722461336, 732955287, 1077303243, 739492502, 1075224524, 747881174, 1075759050, 1074212804, 756269654, 764404440, 1076842445],
    [102, 88, 11, 101, 78, 2089985, 8759489, 18809025, 25526400, 33914880, 42303680, 50692160, 59211969, 67600513, 75989057, 86180558, 94364737, 101034113, 109543425, 117934735, 128123534, 136307905, 1073741824, 145425103, 151365697, 161473665, 170590799, 176932483, 185174158, 195756175, 201951438, 210757250, 218875459, 228786766, 235251713, 246088207, 252152015, 260818435, 1073760771, 269060622, 279117838, 286246596, 294094927, 304021569, 311420610, 319662800, 329187457, 336578052, 345237202, 353217040, 362741761, 369994384, 378521220, 387252881, 1074303108, 394889294, 403695170, 412418769, 420734482, 428714576, 437584465, 1074845762, 446005780, 1075388358, 454026242, 462750225, 471173140, 479691413, 1075672005, 487572548, 496216213, 504857173, 512476355, 521767507, 529892052, 538544851, 546800341, 554936533, 563340882, 572099219, 1076997065, 580487699, 588874443, 1076492232, 596895378, 605268053, 614040139, 622297621, 630433813, 639205899, 647332500, 655722644, 664371851, 672498260, 1077285899, 680888404, 689668749, 697665748, 706446029, 713525263, 723223117, 1075209162, 1076012042, 731611661, 1076285388, 1074725901, 1074229191],
    [90, 76, 9, 89, 66, 1302592, 9691264, 18079744, 26468544, 34988225, 43376705, 52790850, 60153985, 69458563, 76931073, 86345218, 94624323, 1073744642, 1074287171, 1074823168, 103122114, 111401155, 118243917, 126214863, 136676482, 144955395, 153239759, 159769103, 1073803264, 170624654, 176677508, 186793999, 193323663, 204178958, 211959951, 218489423, 229344846, 237125711, 246274769, 254510798, 262947408, 271812243, 279960276, 286016141, 295952596, 305366547, 313514580, 321938002, 329506900, 338921043, 347069076, 354672788, 364086995, 369902093, 378775052, 389011988, 397165200, 405004308, 412329612, 420233933, 430824017, 437495500, 447496720, 455989905, 462661196, 472662736, 481155601, 487958229, 498098706, 504756822, 513255063, 523264722, 529922582, 538289813, 548430482, 555088534, 563455573, 571975255, 580363991, 1076959175, 588643030, 597009941, 1075141574, 1075414981, 1074131973, 605529623, 612885188, 621273668, 1077291976, 629662212, 1076517892, 1075744714, 1074720713, 1076831179, 1076061195],
    [94, 80, 9, 93, 70, 2195585, 8765504, 17285249, 25673729, 33931456, 42319872, 50708608, 59228225, 69698185, 76005569, 86475465, 1073741824, 94863945, 103252489, 1073768448, 111921868, 1076408321, 118457034, 128698892, 136413377, 145476172, 152011274, 162253452, 170746447, 177177226, 1076943810, 1075387394, 185322190, 195912207, 202342986, 212593296, 221078159, 228687937, 237759056, 246244047, 253853697, 262925008, 269591051, 279702032, 286474834, 294879757, 302770772, 311517907, 320045645, 327936532, 336446148, 345072147, 353477195, 361491156, 370131461, 378626643, 387154573, 395045524, 403554948, 412443285, 420709069, 429247121, 437240453, 445735571, 454140619, 462146126, 470663748, 479412754, 487694987, 495700494, 504349381, 513106453, 521267734, 529515077, 538133138, 1075672069, 546433750, 554549764, 563299026, 1077252100, 571853329, 580215381, 588630609, 597017286, 605381333, 613141134, 622182918, 630319766, 638960262, 647096918, 655737414, 1074906118, 1074146310, 664128209, 1076778947, 1075219399, 1074449415, 1074734024, 1076061192],
    [110, 96, 13, 104, 81, 1448960, 10364032, 18752576, 27141312, 35529728, 44049537, 52438081, 60573324, 69215233, 76946496, 85992641, 92956238, 102112448, 111846991, 118122190, 127278208, 137012751, 143287822, 1073750016, 151395920, 1075865601, 162170385, 168436753, 176842382, 184950288, 195724945, 201991313, 211568204, 218504912, 229279441, 235545809, 245122572, 252059280, 262833745, 269100113, 277882387, 287065804, 295705619, 304785039, 311436883, 321275533, 329260115, 338339535, 344991379, 354830029, 362814611, 372418119, 378545875, 388384269, 396369107, 405972679, 413550157, 421797527, 431138311, 437143058, 1076408583, 447915143, 1076948934, 455613961, 462693385, 470697554, 1076693955, 1074355144, 479110804, 488906327, 495863506, 504399446, 514072087, 521029266, 1075417028, 529442516, 539238103, 546219604, 554976921, 564665929, 571745353, 580265113, 1074643909, 1073873925, 588285590, 596647514, 605308633, 613819609, 621840086, 630474265, 640163529, 647242953, 655762457, 1074161602, 663782934, 672417369, 682106505, 689185929, 697705561, 1076272137, 705603092, 714087962, 723158744, 730865370, 740067029, 747642522, 756844181, 1075762123, 1074992139, 1075279818, 765101656, 773621333, 782009877, 790267544, 798656024],
    [126, 112, 12, 125, 102, 369729, 9962624, 18351104, 26739776, 35128512, 43648193, 52036673, 61104783, 68813825, 75867137, 85591169, 92538449, 103047695, 109446658, 117810369, 126092817, 136602319, 143001282, 151364737, 159778370, 170156623, 178890450, 1073750017, 185075396, 193872464, 204056146, 212610630, 218760723, 227172935, 237241415, 245999250, 254553606, 260572804, 269116039, 279184519, 287942162, 294389460, 304885446, 312739335, 319447047, 330269711, 336332308, 344469141, 354682567, 361390279, 372606033, 1075863493, 378275476, 1075615751, 386412053, 395314761, 403726409, 414680643, 419966549, 428869129, 437280777, 447710351, 455880326, 461899332, 470835913, 479200457, 490178051, 495715924, 1075367880, 1074607110, 503852757, 512099970, 521167497, 529532041, 539985103, 1077231618, 1073844233, 548548247, 554305171, 562971280, 573539407, 582102615, 587728388, 596525584, 607618755, 1074906116, 615788054, 621413971, 630080208, 641173123, 1074144259, 649211607, 654575249, 664027268, 671745747, 682984465, 691154455, 697581764, 708150417, 716451414, 721684177, 731267219, 741704913, 750005974, 756432915, 765043924, 775302744, 781860994, 790209684, 800337558, 806764627, 815637584, 1076254666, 1075219403, 825634520, 831799300, 840803536, 850800152, 857358402, 865707092, 875966104, 882262227, 890872852, 898908228, 907912208, 916078786, 924689552, 1074457548, 932855810, 1076572110, 1076851661],
    [114, 100, 10, 107, 84, 285824, 9987265, 18375745, 26895488, 35284160, 43672576, 52061248, 60162764, 68707457, 76053569, 85484545, 92694146, 102105676, 109739597, 119694990, 126248642, 135660172, 143294093, 151807492, 160825868, 168451214, 176875087, 184968770, 193601678, 202014221, 210134530, 218389696, 1073754114, 227305028, 235437057, 1076911043, 243933774, 253912142, 260859588, 269384780, 1075350469, 1074326533, 277488142, 287466510, 296806032, 302668814, 311042766, 321021134, 327870159, 335830080, 1076692934, 1074094086, 344728211, 353035919, 361921683, 369894099, 378201615, 387341842, 395059731, 405858000, 412253203, 420225619, 431023632, 437419091, 445539847, 456189520, 462839378, 470705735, 479651537, 488005266, 495871687, 504817297, 512517764, 520379392, 1075944452, 529426055, 538625749, 545938510, 1075695623, 554854024, 563791509, 571762185, 579763212, 588670603, 597345813, 605316809, 613579987, 621962952, 630900309, 638871177, 646601934, 655779403, 664200721, 672425545, 680426700, 1074934793, 689071624, 697755217, 705592460, 1077298122, 1073914890, 714499787, 723314260, 730365121, 739665419, 748611222, 755530881, 1076286475, 764569160, 773645844, 780828365, 1075252232, 1074751496, 790554198, 798383826, 807331350, 815720150, 823977620, 832366292],
    [118, 104, 1, 115, 92, 271360, 8766528, 18367681, 26756097, 35144769, 43533441, 52053120, 60441600, 68830400, 75769024, 84403788, 93996096, 103050958, 109323328, 117958156, 128216718, 134629060, 142984384, 151529164, 160056901, 170421444, 176572036, 187049485, 193717840, 202000069, 212364420, 218514948, 227403409, 235415180, 244074003, 252331525, 262695940, 268846660, 279315475, 288081426, 1073745924, 1074818052, 294405715, 302663301, 313289861, 321258579, 330024530, 1076658181, 1073795011, 336348819, 346844165, 354813075, 363579090, 369903315, 380136516, 388367571, 397133458, 405564485, 411952721, 419963980, 430730437, 436479104, 445113484, 455372302, 462284305, 472262285, 480538190, 487072780, 495707792, 504262296, 514205261, 520873488, 529559252, 539371213, 546039504, 554978838, 565446159, 570803200, 580538069, 590612047, 596502225, 605703829, 615777999, 621274316, 1074599878, 1075144710, 630091480, 640943759, 646300800, 1076471751, 655257112, 664134861, 672531585, 681201173, 689300557, 697697281, 1076223944, 1075720200, 705719892, 714466317, 722863169, 731139734, 739632269, 748029121, 1077038026, 756051604, 765208279, 773317633, 781086296, 790374039, 798483585, 1074437058, 1075508226, 806637270, 815539799, 823649345, 1077355467, 831548948, 840705559, 848815297, 1076053961, 857362005, 865357398],
    [122, 108, 1, 121, 98, 302208, 10527744, 18916480, 27305024, 35693760, 44213377, 52602049, 60990465, 67411136, 77767745, 84198930, 94701122, 101236432, 109364882, 119867010, 128106001, 134530642, 145032898, 153271953, 159696594, 170198530, 178437713, 1073745922, 187491923, 193242195, 201762516, 210288144, 1074815939, 221447894, 229426179, 235447895, 243705364, 252231248, 263390742, 271508567, 277128851, 285648532, 295878353, 302843480, 313320595, 319334039, 327457792, 338888342, 347006103, 352888535, 361145940, 372022869, 378611225, 388949207, 394569427, 403226256, 1075872708, 412165721, 422372563, 428385815, 439131797, 445720217, 455927315, 461677587, 472686293, 1073802181, 479004184, 489612311, 497851925, 1076431814, 504170200, 514639043, 520395840, 531826262, 540066964, 548453588, 554772185, 564970627, 573750341, 580167240, 588580507, 598787092, 605464266, 613983836, 624082053, 630523611, 640730324, 647407242, 655926940, 665894036, 671942296, 682673236, 689350154, 697870044, 707968005, 714385032, 722798171, 732742723, 739681866, 748201500, 758299845, 764716744, 1074354186, 773129755, 782025884, 791723092, 798270984, 807191580, 1075416072, 816888852, 1074657225, 824100570, 832216257, 1077290956, 840746204, 1076256711, 848993281, 857523292, 865770561, 874432026, 882547841, 891209306, 899597978, 1075746766, 1075245003, 1076835279, 1077102541],
    [106, 92, 10, 105, 82, 1836096, 10519553, 18908289, 27427840, 35816512, 44074177, 52462657, 61006352, 69371072, 77333696, 86148224, 92702290, 102949520, 110887936, 117868242, 128115408, 136053888, 145403411, 151422610, 161669712, 168698945, 179080724, 184976914, 195747986, 202253441, 213036758, 218662615, 229433559, 235807745, 246722072, 252216855, 262987799, 269362369, 280276696, 285771351, 296804885, 303179345, 313699990, 319588037, 330096727, 336733713, 347385432, 352880279, 363651223, 370288337, 380284499, 386696837, 397074642, 403842705, 1073750979, 413961876, 420251205, 431022805, 439231621, 448048792, 453805573, 464577173, 472785989, 1075862468, 1075347461, 480947859, 489349138, 497951941, 1073793986, 506637910, 514515026, 523117573, 532327961, 540074581, 548537488, 554600071, 565882457, 571663002, 582091984, 590122708, 596828762, 607257616, 613320391, 623554259, 630383130, 640812112, 646874695, 657231444, 663937754, 672400467, 683323097, 689177747, 700100249, 706142811, 714343635, 1074336715, 1074876364, 724741654, 731308763, 739509267, 747537927, 756474395, 1074628554, 1074123783, 764863131, 1075191753, 1075734472, 1076277197, 1076818886, 1077098446, 1077373903],
    [110, 96, 9, 109, 86, 2581696, 10387521, 18932737, 27321537, 35841024, 44229760, 52487233, 60875905, 69393936, 77784256, 86467712, 94273729, 102949952, 111337104, 120022016, 127827969, 136502864, 145187904, 152993921, 159966722, 170321619, 178446032, 186991618, 195068498, 201909890, 212264467, 220782225, 228934786, 235578004, 243852866, 254207635, 262725137, 270877762, 278954514, 285796034, 296150611, 304668369, 311223939, 321209538, 329286354, 1073743874, 336389699, 346611281, 355288212, 362840722, 369944259, 378199058, 389243921, 395346454, 403498499, 411884566, 420127444, 430785748, 1074288643, 437313044, 445292564, 455951380, 462478548, 470458964, 481117268, 487644244, 498295889, 504553111, 515073233, 520805522, 531850385, 538107479, 1075348421, 548619283, 554730198, 562879702, 1073796038, 573785299, 580166296, 588577944, 1074862023, 598950995, 605061782, 613211286, 624116883, 1075145673, 630497816, 639297229, 647298072, 656369301, 664052440, 672851597, 680852696, 689923797, 1076474824, 697606744, 706405901, 714407000, 723478037, 730890838, 739960397, 747428950, 757032533, 1077009421, 1075720132, 764468372, 1076782028, 772463698, 1076017098, 781377047, 1077333963, 789241042, 798154455, 1074726862, 1074227151],
    [106, 92, 9, 105, 82, 296001, 8676481, 18664641, 27313153, 35701953, 44090497, 52479041, 60998848, 69387264, 77775936, 84436688, 94161921, 100959361, 111330432, 117991056, 127716481, 134513857, 143156752, 151290881, 161270849, 170829521, 176711248, 184872466, 195995153, 204105219, 210030291, 221161041, 229271107, 235195923, 1073744643, 243967168, 254568004, 260361875, 269141590, 1074283332, 279881361, 288681046, 296379523, 302687360, 313287812, 319082067, 327992919, 336241728, 346842116, 352644690, 361416342, 370067096, 378184704, 389344406, 397435991, 1073779654, 403490455, 414213271, 423003717, 428142290, 437044951, 447767767, 456558213, 461696658, 470468310, 481619158, 489448644, 498501317, 1074846789, 504022550, 512673496, 523562006, 531260611, 540443653, 546096663, 554616344, 565208087, 571647128, 579782232, 588399633, 597337748, 1075656649, 605472459, 613565649, 622503444, 1077238722, 630638219, 638731409, 647144472, 1075424202, 655508561, 664446548, 671376449, 681354773, 1076490184, 688153793, 698132117, 704930817, 714253528, 722912779, 1076762573, 731030616, 1075213255, 739690059, 748463701, 1077052427, 1074193356, 756721364, 765241045, 1076039631, 1074751438],
    [106, 92, 9, 103, 80, 2172032, 10560704, 18949120, 27337792, 35857473, 44246145, 52634817, 61023233, 67716688, 75834448, 84352721, 94873170, 101410515, 109651668, 119881219, 128427666, 136922820, 143072785, 153593554, 162219220, 168238673, 177030869, 187147794, 193799831, 203767363, 210585237, 221087447, 227353815, 235871832, 244262617, 252528213, 263029911, 269297175, 1073746882, 279264899, 286205465, 1074807299, 296437396, 304972823, 310977684, 321207491, 328304346, 338249220, 347020827, 352658960, 361703065, 1073781701, 370247322, 380323348, 386475028, 397352667, 402990736, 413746820, 420578906, 428680791, 439295579, 444933840, 454133274, 464078404, 472850075, 1075372036, 478757904, 489522263, 495527508, 504307416, 514540628, 523871449, 529473048, 540648601, 546653910, 554639000, 563029593, 574202969, 579561043, 588717660, 599368729, 605373974, 613883612, 622544089, 1075912647, 629612177, 638928534, 647568989, 1075662793, 655058451, 664346141, 1074628550, 1074121672, 672482902, 680992412, 688473232, 697900765, 1074403274, 705250512, 714546716, 1075213259, 1077065679, 723207193, 731455133, 739067413, 1077341134, 1076572109, 747333267, 1076848588, 756761753, 765150297],
    [118, 104, 3, 117, 94, 2393088, 10955841, 19607248, 27559040, 35734097, 42272466, 52627155, 61113408, 70069458, 77938899, 86705667, 94570003, 103493136, 111445184, 120143875, 128648835, 136513107, 142935698, 153519696, 162344082, 170475651, 178980547, 186844819, 193267282, 204375105, 212675666, 220807363, 227215045, 238093909, 246099024, 254183056, 263143621, 271255107, 280037077, 285541906, 296649857, 304950290, 1073743875, 313081923, 319489669, 330368533, 338373776, 346981569, 355418245, 361432581, 372311701, 380011728, 388443329, 397361157, 403375685, 414090241, 423046804, 1074286597, 430915653, 438731792, 448212692, 455426131, 463940609, 473203861, 479135240, 488980627, 498369557, 506932820, 512689736, 522534931, 529598025, 1074836422, 540312661, 548875796, 554632840, 1076943810, 564216337, 571672139, 581381249, 590644437, 597770961, 605095561, 1075389380, 613713105, 624504017, 631325329, 638649865, 647267473, 658058385, 666320917, 672335499, 680821777, 691612753, 697239240, 708264021, 1075929031, 714278411, 1075680264, 725167121, 731153489, 741818581, 747833035, 758451400, 1075168267, 1074149325, 766984341, 772867785, 783617096, 1077297161, 792027734, 800394376, 808805014, 817171464, 1073917898, 825582294, 833970710, 1076815820, 840647319, 849035799, 857424599, 1076308942, 865813079, 1076580303],
    [90, 76, 5, 89, 66, 2186304, 10347521, 18965504, 27354176, 35742848, 44131520, 52651009, 61039809, 69428289, 77683904, 86492816, 94594177, 102849664, 111658704, 118056515, 128435728, 136543299, 143222467, 152953921, 161709251, 168388099, 178119873, 186874883, 195633747, 202204243, 210331267, 220710480, 228818051, 1073747971, 235602644, 244147859, 252667525, 262626437, 270394497, 279519379, 286090771, 294610501, 304569413, 313073683, 319645395, 328164869, 338386514, 346628307, 354936470, 361719493, 371940882, 1075333125, 378479317, 388455621, 396879574, 403645077, 413884050, 422045206, 428941911, 439049938, 447211094, 456327896, 463952901, 473104920, 481263185, 487662295, 498040465, 504439447, 514817553, 523436632, 531359257, 539983569, 548602520, 556525273, 564222976, 571548183, 581690969, 587923988, 598468249, 604701332, 1074302920, 1074579399, 613360149, 621478484, 630137429, 1074080714, 1076454347, 1075945423, 1075704770, 1077023684, 1074948046, 1076279241, 1077330886, 1073950668, 1076844493],
    [110, 96, 8, 109, 86, 355328, 8709313, 19211457, 27345985, 35734657, 44123137, 52511937, 59172368, 67568656, 75852928, 86197971, 92726928, 101018816, 111486081, 119752339, 126281424, 134573120, 145040449, 153306643, 161958931, 168224336, 176620624, 186861139, 195513427, 201770641, 212149249, 220819094, 226952336, 235325009, 245845203, 252118224, 260490961, 1073746884, 271150678, 277267985, 288818193, 296316438, 305595601, 311486034, 321342611, 330761297, 336783060, 1074821062, 347041368, 355927185, 361948692, 1077183431, 371814102, 378741824, 387114580, 395265562, 405761688, 411362369, 420947543, 430927576, 437462144, 444916865, 456093208, 462627840, 471000724, 479282700, 488197721, 495248385, 504833687, 512837260, 521094746, 530140889, 537978386, 546776599, 554780364, 563695129, 571533010, 580331223, 588861081, 596845760, 605087378, 613369498, 622546064, 631055893, 638666316, 646923994, 656100368, 664741082, 1073792012, 673138319, 681266384, 689776213, 698304207, 706571457, 715072538, 1074076611, 723469839, 731737089, 740238426, 1075408845, 1076726730, 748635727, 756763728, 765273749, 1074385935, 1075194818, 773680193, 782051029, 1076514761, 790457473, 798958746, 1074705355, 1077075918, 1075783624, 1076323269],
    [110, 96, 13, 109, 86, 2204864, 10593280, 19113089, 27370560, 35759232, 44278849, 52553296, 61056193, 69444609, 75998865, 86107856, 94373458, 102743746, 109553233, 119662224, 127927826, 136297986, 143107793, 153216528, 161482450, 169852482, 176662033, 187286673, 195036818, 203669204, 212575748, 220841041, 1073746178, 229254805, 237616132, 246130372, 254395601, 262809109, 270515330, 279684676, 287949841, 296363605, 304725060, 313239172, 319931987, 1074806788, 329918165, 338279556, 344696343, 353616919, 361604696, 372115097, 380222660, 386901594, 395429395, 403547672, 413934616, 421772820, 428975707, 437372627, 445490840, 456001113, 464625302, 470525591, 479446167, 487433944, 497944089, 505659028, 512861723, 521651227, 531498713, 539213396, 546023127, 554943703, 564929752, 573677270, 579577431, 1073787848, 588498007, 598484056, 607231574, 613525211, 622314715, 632300616, 640785942, 647079579, 655869083, 665854984, 672114202, 681296922, 690758808, 697280154, 706462874, 1076948934, 716186824, 722446042, 731628762, 1076697034, 741352584, 748398283, 756532315, 1075136457, 765175307, 773571674, 781305491, 790341195, 1074113479, 1076487109, 1075980227, 798729867, 1076256716, 1075743755, 1074715597, 1075514318, 1074493391],
    [122, 108, 9, 121, 98, 2329601, 10552385, 18973760, 27362496, 35751040, 44139520, 50800144, 61049921, 68928066, 78087234, 84248274, 92743312, 102993089, 110747858, 120030722, 126191122, 134686416, 144936065, 152690706, 161973954, 168134226, 176524432, 185280209, 194633810, 203916930, 210077330, 218467344, 226960976, 1073747970, 236576914, 243633360, 252389009, 1075340227, 261865602, 268799056, 277554705, 287949525, 297119443, 302720593, 313115221, 322285203, 329319425, 338281109, 347450899, 354485377, 362528770, 372616787, 379651265, 388612629, 395152529, 404039319, 412860610, 420318289, 429467350, 439205891, 445875802, 454764249, 465153114, 1075884998, 472760387, 479430362, 488318617, 498707674, 506323483, 513115163, 520981713, 530130582, 539878043, 546669723, 554535953, 563815961, 1076939717, 573423747, 580093466, 588981849, 599370778, 1074342857, 606986843, 613778523, 622142999, 630959836, 1076453320, 640541403, 647333083, 655697495, 664514140, 674087107, 680756890, 689252055, 700034202, 705553108, 714704588, 723068502, 731622940, 1075679175, 739107348, 748258956, 756622870, 765177500, 772661908, 781944398, 790464015, 797827668, 807110350, 1074657226, 814867160, 823756364, 832407183, 1077293003, 840032856, 848922124, 857573071, 1076777996, 865198744, 874219022, 881975832, 890996366, 899515983, 1075218381, 1074184207, 1073942542, 1075013572],
    [86, 72, 9, 85, 62, 1432640, 10452993, 18638017, 26862656, 35382337, 43770881, 52028416, 60548225, 68805760, 77325505, 85581391, 94135425, 102727873, 110748864, 117827138, 127524495, 136078401, 144670849, 152690383, 161244161, 169836609, 177856015, 187197139, 193324738, 1073754112, 203974163, 211812050, 220751507, 228589138, 235643540, 245366290, 252420692, 262694483, 269608469, 278920850, 288587797, 294774357, 304340688, 313753685, 321406615, 328328917, 337894928, 347308245, 354960919, 361883285, 370531520, 380862613, 388515415, 397016593, 403415572, 413681367, 421781072, 428581588, 438558352, 445883030, 1076918212, 455736977, 462660118, 471194624, 479437398, 487971968, 495314434, 506068561, 1077183433, 1073802183, 512991958, 522845905, 1076437957, 530031308, 1075923910, 538419788, 545646210, 1074371523, 1075436546, 555196940, 563585676, 1075719180, 572105230, 1076778955, 580494030, 1075220426, 1074710477, 588882574, 1074205640, 597271118, 1075012622],
    [114, 100, 7, 113, 90, 484417, 10855617, 18859072, 27247744, 35636416, 44024832, 52544577, 60933249, 69321729, 75974221, 86352897, 94487745, 103271950, 109528781, 119907393, 128568912, 134727235, 143083021, 153461889, 162123472, 168281603, 176784908, 185026189, 1073752064, 193578577, 204066448, 1076391937, 210453648, 218728140, 229232144, 235619408, 243893836, 252177938, 260949638, 269173776, 277448332, 285732498, 296846927, 302728400, 312987342, 322012687, 328426577, 336064082, 347178639, 353723532, 361230034, 372344527, 378889292, 386516689, 396873294, 403555910, 414557265, 420701393, 1076930504, 428459665, 438816398, 446023369, 453494403, 462775308, 473277649, 478791185, 487583379, 495830534, 504587281, 515352068, 521137683, 529745620, 540518020, 546303699, 555075081, 563299988, 573940753, 579858003, 587686913, 599238212, 1076159431, 1075916741, 605242964, 616015556, 1076720644, 621659846, 632661137, 639460356, 1077248006, 647351829, 654821059, 663184577, 672629957, 1073860611, 680906453, 688350337, 697795589, 706072149, 714458697, 722822348, 731882496, 1074927554, 739626645, 748127301, 756900932, 764790409, 773825664, 781411473, 1075201033, 790602944, 798844036, 1074170826, 1074449418, 806569492, 815236229, 824157248, 832398532, 1074731979, 1075534859],
    [102, 88, 13, 101, 78, 1048704, 10766337, 18753536, 27142208, 35530880, 43919552, 52333132, 59769024, 69486785, 77499084, 84934720, 95054338, 102664716, 110100480, 117983950, 127830668, 136053453, 143149582, 1073750016, 1075865601, 153397970, 161219085, 168315470, 176827091, 186952338, 194773645, 201869966, 210381331, 220506706, 228328013, 237660866, 1076400067, 245672466, 253886657, 262826626, 271362769, 279052289, 287992386, 1074581506, 1074861058, 296528529, 304218177, 312756289, 321694289, 329533569, 338034899, 344861205, 352987795, 363637265, 371327105, 378686100, 386804437, 394930771, 405834447, 413532243, 420629204, 428747349, 439388815, 447086739, 454183444, 1075137476, 464554511, 472252435, 479349332, 487467669, 1074374597, 498109007, 506200277, 513042966, 521284296, 532056656, 539754581, 546597590, 554838536, 1076229062, 565611024, 573440198, 580413975, 588393032, 599165648, 606994438, 614222424, 621947528, 632720016, 1077025800, 640548934, 647776920, 657326214, 664300183, 1075731401, 673972245, 681077335, 1075479495, 1073923079, 690749589, 697854679, 706497240, 714369686, 723274264, 731146838, 1074212810, 1076852683],
    [118, 104, 11, 114, 91, 2240512, 8751105, 18352193, 26740865, 35129537, 43517953, 52037824, 60426304, 68814848, 77738176, 84248641, 93980800, 102903936, 109414593, 117836418, 128069696, 137070722, 145125059, 151390722, 162236418, 170406083, 1073750017, 179064466, 184945218, 195790914, 203960963, 210259537, 218499778, 229345474, 1075856386, 237515331, 243814033, 252020865, 260575763, 271339218, 280079055, 288109204, 296504850, 305244687, 313274900, 319311569, 327682630, 338799183, 1074042947, 344591061, 355218004, 363613778, 369625734, 380742287, 386533973, 397161172, 403197457, 411568646, 422807558, 428476949, 436736595, 447114243, 453511878, 464750790, 1075363846, 470291155, 480668803, 487459350, 498305158, 1073818565, 503974549, 514223171, 522727427, 529402518, 540248134, 546459223, 554177171, 563219144, 1076455364, 574064662, 582511816, 588122710, 599230614, 1076202439, 605179543, 613560856, 621939208, 632784982, 641231880, 647115480, 655493768, 664504848, 674786440, 680669784, 689048136, 698189888, 1074384904, 708340808, 714224280, 722340566, 1074927561, 733448406, 739397335, 748391120, 756174359, 765168208, 773606937, 782076032, 790384281, 798722704, 1075204043, 1074705357, 807161433, 815630528, 1077075918, 823938777, 1075787722, 832407552, 840927253, 1077374924, 849316053, 857704597, 866093141],
    [102, 88, 10, 101, 78, 2121728, 10512513, 18900993, 27289793, 35678273, 44197952, 52586624, 60558864, 69363712, 77619264, 86141120, 95087122, 102502032, 111173760, 120253138, 127667920, 136339648, 145803859, 152833616, 162160833, 170683094, 179358227, 184814806, 195715201, 204237398, 212912787, 218369110, 229130769, 1073746883, 237791894, 246467283, 251923606, 262824001, 271346198, 280545879, 285477910, 296239761, 1074815940, 305711639, 313003076, 321544193, 330877655, 338169028, 346571473, 1075872709, 356043415, 361369304, 371737169, 380299858, 386534936, 395468944, 405465746, 413666436, 420634640, 429058773, 437021321, 445255320, 454189264, 1073793990, 462744089, 470575817, 480775172, 487743568, 495872714, 504556053, 512518665, 520752728, 531644484, 537815690, 546499221, 554461769, 563490388, 1074337735, 573587460, 1075141641, 579758602, 588573401, 596905498, 607142084, 1075688386, 613313098, 622127705, 630599316, 640696452, 1077008394, 647653965, 655682201, 664153620, 1075460040, 672819853, 680716885, 689180250, 697985741, 705957594, 714762765, 722874068, 1077300237, 731123354, 1074694092, 1074194379, 1076309967, 1076849614],
    [118, 104, 6, 117, 94, 1960065, 10504193, 18892993, 27281473, 35670145, 44189760, 52578304, 60828304, 69355648, 77457473, 86132928, 92555859, 101067474, 109463762, 119663313, 126241298, 136587906, 144829009, 154038996, 162154708, 168184466, 176564370, 186509505, 195842581, 204098196, 210127442, 218507346, 228452353, 237924500, 246041172, 252332567, 262417090, 271566871, 1073754306, 279867924, 287983636, 294275799, 304359426, 313510103, 322204291, 327830103, 335947794, 347064407, 355758659, 361384599, 371468354, 380618903, 388780757, 395070149, 405407767, 414697669, 422335125, 428755482, 437012997, 447350999, 456640517, 464278101, 470567557, 480905303, 490195077, 1076912707, 495864474, 506753219, 512510533, 522201680, 532138053, 1075871749, 540307459, 548014231, 556657305, 562973274, 573468756, 579095059, 589310672, 598600409, 604916442, 615928534, 621038227, 631253520, 640543321, 649482774, 654592723, 665987219, 673311249, 683037334, 691152915, 699263513, 1073797062, 708473560, 716318931, 723643025, 733639256, 741484627, 1075123143, 747628544, 758805016, 765208666, 772794496, 1074883529, 783700566, 790374554, 797960384, 809136792, 815540442, 823126080, 832317466, 1076463565, 840427605, 1074121675, 848816277, 1074407374, 1076252620, 1074700232, 857204949, 865593365, 1075771332, 1077358543, 1076845514],
    [122, 108, 10, 114, 91, 557248, 10004609, 18393153, 26781697, 35170497, 43690176, 52078720, 60467200, 67665984, 77244480, 86559310, 92831872, 102673104, 111987333, 117877444, 126779983, 136227408, 145672388, 151431748, 160334543, 169781776, 179226692, 185500175, 194947728, 202050196, 210422418, 219054735, 229157397, 235448902, 246229013, 252365522, 260603904, 271100565, 279783573, 285919762, 294428752, 304654933, 313337941, 321440398, 327592580, 336371920, 346598101, 355281109, 363776132, 369926288, 378055302, 389220950, 394971730, 403480592, 414386710, 422365765, 428255748, 439255697, 1073746948, 445164230, 453708372, 464308933, 472810065, 478718470, 489884374, 497863173, 506364433, 1075082246, 1077182469, 1073800197, 512428564, 523159556, 531530449, 540215958, 546622104, 554740296, 563126924, 571943641, 580176600, 588294792, 596681420, 605497945, 613730904, 622232077, 1076168643, 1074094083, 630925978, 638896664, 647397965, 656091674, 665373390, 672180936, 681083009, 689646170, 698927630, 1075950537, 706118285, 714812122, 723184215, 731414593, 1077007303, 741935771, 748481235, 756580545, 767101659, 773646995, 781615821, 792267355, 798681623, 806398472, 1074929610, 815300609, 1075727298, 1074441218, 1076811784, 825821723, 832367187, 839950860, 1075515339, 1074751499, 848767513, 857532947, 865116748, 873933465, 882567831, 889916116, 899345111],
    [126, 112, 11, 123, 100, 2404416, 8652801, 18385089, 26904576, 35293312, 43550849, 51939393, 60459072, 68847808, 77901952, 84159116, 93882369, 103083534, 109349442, 117868558, 128233664, 134490636, 145010688, 151267916, 161909456, 168045260, 176599248, 187494033, 195463760, 203982993, 209979585, 218542160, 229437009, 237406736, 245925969, 251922561, 260485136, 271379985, 279480337, 288273043, 293865537, 304934609, 313034961, 319563840, 330216019, 336129621, 344729728, 355381971, 361295381, 369895424, 380547603, 386461333, 395061440, 403485266, 413567632, 420015829, 430713357, 437039634, 447490701, 453817042, 1073750979, 463793806, 470190222, 479210191, 487371410, 495880838, 506210893, 512791254, 1075858372, 522514126, 528910542, 537956950, 546318863, 554863303, 564457038, 570853454, 579899926, 588262031, 596806151, 605351640, 613321222, 621843094, 630205007, 638749319, 647294552, 655264326, 665594573, 671527056, 680692295, 1074301959, 691188311, 697838100, 1074585545, 1075654665, 705989194, 714403352, 722373318, 733131415, 739781204, 747932170, 1076978694, 755272386, 764840651, 773195927, 783594196, 1076206533, 1075442693, 789875338, 798289560, 805603970, 815172235, 825536532, 832055508, 840207050, 847546882, 857115211, 1077285898, 1075210250, 865470999, 875868244, 1076527106, 882280971, 890637015, 900903127, 1073923083, 907553428, 917811348, 1074205640, 1075014664, 926068759, 932579415],
    [130, 116, 10, 129, 106, 2156737, 10545217, 18933761, 27453568, 35711105, 44230720, 52749008, 61008064, 69396480, 77914768, 86461139, 92581442, 101114386, 111626835, 118001219, 126280338, 137161366, 143092245, 151555587, 159834834, 170846935, 179260121, 185002201, 193244802, 201777746, 212789847, 220678803, 227192474, 237298256, 243985029, 255150744, 260746842, 270852624, 277539525, 288705240, 294301210, 305053783, 311093765, 319769180, 327986181, 338608343, 344934940, 352882307, 361687710, 372294225, 377940569, 386878172, 397339287, 403737758, 414105751, 1073742339, 419883545, 428534341, 437209756, 445156547, 453962270, 464568977, 1073765381, 472705622, 478603929, 489637977, 496012318, 504293982, 515031190, 521202184, 1075614274, 531426006, 539969561, 546344030, 554625758, 565232337, 571533896, 581757462, 590301337, 596675806, 605088456, 615694358, 623831575, 631720467, 639142984, 647031432, 657375255, 1074843590, 1074603972, 1076185096, 664201866, 674581080, 681086088, 691191894, 697756362, 708135448, 714779850, 724746454, 1074370503, 731310666, 742083163, 748334154, 758170129, 764865034, 775637723, 781888522, 790282836, 1075173386, 800803355, 805612546, 815448724, 1075457993, 825969307, 830778562, 840614420, 847735381, 857246920, 865657373, 1076786125, 872901269, 881634501, 890823261, 1077065678, 898067157, 906800261, 915989149, 924355592, 932889300, 1077331915, 941272202, 949543645, 957131845, 965390042, 1074209740, 1076063183],
    [118, 104, 8, 117, 94, 2386113, 10537153, 18925569, 27314241, 35702913, 44222464, 52611200, 60852944, 69388352, 77883393, 86165696, 94696081, 103205586, 111184464, 117754451, 128215169, 136639185, 145148498, 153127440, 159828564, 170158145, 178582097, 187353621, 195480210, 203459216, 210160148, 221145617, 228913169, 237685461, 245811730, 252479572, 260360851, 271476945, 279761109, 288672386, 296396930, 302303763, 313419857, 321703957, 330615362, 338339906, 346974353, 353169944, 361548356, 372558338, 380282882, 386558144, 395113112, 403098260, 411863188, 420112384, 428929234, 437045892, 448056002, 455780546, 462055552, 470610648, 1073754114, 478595796, 487360724, 495609920, 504426642, 512674329, 520914964, 531908754, 537719384, 545573587, 554346579, 565463250, 571929114, 581618261, 587901075, 599017554, 1076910021, 606916693, 615172757, 621726425, 629983940, 638757081, 649349138, 1075095491, 657248405, 663538180, 672057945, 680699929, 688941783, 1076151300, 1074080711, 697758426, 705865817, 714500630, 722924186, 730778265, 739420313, 747661847, 1076446152, 756470299, 764061907, 772827799, 781636251, 789227539, 798386838, 806802011, 815164118, 823587418, 1073845195, 831941206, 1074917322, 839970898, 848325207, 1076759497, 857133787, 865136658, 1074417606, 1074700236, 1075764174, 1075525581, 1077371855],
    [106, 92, 5, 105, 82, 2468032, 10559681, 18950272, 27338944, 35727360, 44116032, 52799552, 61153872, 69421713, 78064147, 86607873, 94445697, 103507987, 111618707, 120162433, 128262672, 137062547, 144777217, 153716929, 161696273, 170339027, 178628608, 186720321, 195782867, 201796291, 212437057, 220537552, 1073746882, 228805329, 235350531, 245836371, 254126208, 262480528, 271280211, 277293699, 288327696, 294584916, 304302673, 310848067, 322013781, 328270418, 1074808835, 338659408, 345047762, 355436688, 361824914, 370109143, 380602576, 386990610, 395258457, 404179033, 414288597, 420414164, 1074305990, 428812825, 437733401, 447842837, 454370008, 465127640, 473008789, 479535640, 487533273, 496453849, 506833558, 512688660, 523848344, 531999446, 538255960, 546253465, 1075377092, 555174041, 565684230, 571809944, 582568024, 590850118, 596574868, 607733784, 616016006, 1076964296, 622684890, 632662550, 638544535, 649570502, 655321623, 666217046, 673147483, 681247388, 689793690, 1076453327, 1075687374, 698024668, 706702043, 714801756, 722430551, 1076742090, 1074149323, 731578908, 740256283, 1077307337, 748513882, 1076265927, 1073931212, 757033627, 765291034, 1076039629, 1074747333],
    [118, 104, 3, 117, 94, 305216, 10162305, 18941953, 27330625, 35719361, 44107905, 52627584, 61016064, 69404864, 76188304, 86061776, 94570560, 100993745, 111227408, 119580881, 126159441, 135991297, 144746577, 151482068, 159713809, 170592468, 178335888, 186689553, 195889794, 201656977, 212248706, 219877569, 229444162, 235368020, 246089812, 253833808, 262580290, 271387330, 279357634, 286986305, 296552962, 304967317, 312911874, 321729234, 1073743874, 328010436, 336031380, 346753172, 353011792, 363933892, 369953348, 380464725, 388016273, 397488196, 1074283459, 403507844, 411528724, 422250516, 428509392, 439431300, 445450756, 455962133, 462063632, 472985604, 1073778692, 481128149, 487368833, 497889874, 506678855, 512788562, 523055762, 531844615, 539832850, 546343058, 555175446, 563286739, 571254785, 582176455, 588452371, 596420673, 605507286, 613757527, 621840594, 630917835, 640896647, 1074846727, 647172691, 655141057, 664472139, 672616086, 680866519, 688171200, 698288781, 1075655625, 708398221, 714281619, 721725568, 1076981702, 731843085, 741952525, 747975191, 755279872, 765397581, 775507021, 781529751, 789612562, 798952141, 809061581, 1076728845, 1075181516, 1077291973, 815222358, 824135192, 1076517838, 1075487688, 832523864, 840912600, 1076029386, 849021451, 857689752, 865798795, 1076298763, 1074221007],
    [130, 116, 10, 129, 106, 2189313, 10709056, 19097792, 27486208, 35743937, 44263552, 52521025, 60909697, 69689872, 78078608, 86978193, 94988433, 103270994, 112027730, 120021584, 126168787, 137325204, 145187536, 153554453, 162490900, 170737684, 178874897, 187109013, 196045524, 204292308, 1073742787, 212806673, 221211220, 229458004, 237595345, 245829333, 254921432, 263012500, 271388374, 277441178, 288475672, 296829655, 302738054, 313092689, 321326677, 327772890, 338807384, 344678554, 353069766, 364210759, 372190289, 378137160, 386754632, 397500487, 403401222, 414542343, 422383190, 431082136, 439443463, 445344326, 456485575, 464465105, 1073765382, 472369874, 481126610, 489775303, 496200394, 1075614658, 506817159, 514657942, 521005643, 531718279, 538143306, 1074852871, 548212246, 556788379, 565264983, 571697802, 1077217225, 579153555, 588114443, 597125852, 607207959, 613640714, 621096531, 1074087946, 630442057, 640762519, 646262291, 655223499, 664234652, 671834330, 680996377, 688482906, 697166475, 707619474, 713777242, 1074369547, 722939481, 730425882, 740804754, 748120668, 755720218, 764882585, 1075180492, 774359570, 781675036, 791504914, 798572572, 807218781, 816835163, 823738524, 832384541, 842000923, 848904284, 857550557, 867166939, 873294344, 1077030853, 882458844, 891104925, 1076783053, 898230984, 906848456, 915877593, 923396744, 932014216, 1076268040, 940820489, 1074717646, 948561928, 1076042692, 957597833, 965986505, 1075538895],
    [106, 92, 9, 105, 82, 2445313, 10938433, 19212816, 27847249, 35999809, 42289810, 52767440, 61567490, 69790225, 75975315, 84224147, 94824577, 103108801, 109529683, 117778515, 128676482, 136767489, 145443349, 151472851, 159721683, 170619458, 179365909, 187386517, 1073752578, 193415699, 201664531, 212920469, 220549249, 227101187, 235481816, 246116546, 254339729, 262884053, 269036120, 280029397, 286085841, 296962649, 302590616, 311251089, 321448145, 330517145, 338381397, 344533528, 355526741, 361582673, 372460057, 377834066, 388311632, 395137041, 405203137, 414403289, 419777234, 430254736, 437307392, 447959040, 453331474, 464595546, 470861888, 481513536, 489761306, 496027840, 506679488, 1076385733, 514927322, 521193600, 531845248, 540093082, 546656852, 557247003, 563685465, 571822740, 582412955, 588851417, 596988436, 607578715, 1075086281, 614279378, 622154452, 632744667, 639445010, 647713366, 656198167, 664348825, 672879254, 681364119, 1073803204, 689514521, 698045142, 706530007, 714942546, 1076705227, 723210774, 731695703, 1077235658, 1074633676, 1075438541, 740108434, 747194947, 1075983304, 755583619, 763972291, 1077036998, 1074171907, 1074973639, 1074470863, 1075800014],
    [106, 92, 1, 105, 82, 1933312, 10733760, 18745537, 27371648, 35760128, 44148800, 52537536, 61057089, 69445825, 77834369, 85819520, 94619776, 102894160, 111388673, 120171218, 128174144, 136938001, 144967890, 153725522, 161728512, 170492625, 178522194, 187280018, 195930644, 204065346, 212435537, 220465298, 229222930, 237873812, 245203008, 252299925, 262408210, 271428308, 279055056, 285854229, 296321681, 303923392, 312609296, 319408725, 330148436, 337775248, 344574677, 354656790, 363448962, 371067009, 379822742, 1073746498, 389261847, 397002754, 404621377, 413377238, 422168770, 429787137, 438542934, 447982167, 456771796, 464259095, 473148055, 481937556, 489424983, 498313943, 507103252, 514590935, 1074807749, 523880532, 531368087, 1073785796, 540027416, 548530835, 556804824, 565307987, 1076416455, 1074601928, 573581912, 582085139, 1075673030, 590359192, 598862547, 605538905, 613821018, 622438925, 630704665, 638986970, 647998030, 655870681, 664152730, 672647833, 680929818, 1077254092, 689547981, 697690843, 706325069, 714467867, 723495566, 731245211, 739879565, 748022363, 1075179467, 1076762637, 1075475401, 757050062, 1077061578, 765438478, 1076283406, 1074471875, 1076053967],
    [110, 96, 13, 109, 86, 1961089, 8761537, 19081409, 27363392, 35752064, 44140736, 52529152, 61049025, 69437441, 77826113, 86618640, 94628880, 102967361, 111380609, 120304337, 128133121, 136178881, 144961168, 153858641, 161687681, 168233152, 179024529, 186510337, 195292752, 201787392, 212578833, 220836560, 228846800, 235341952, 246001744, 252119104, 262007873, 269420560, 279556240, 288091328, 1073750978, 296858322, 302975056, 313256960, 319523544, 330238168, 338801170, 346811520, 353077784, 363792408, 372355666, 380365888, 1075866564, 1076403141, 386894534, 395020888, 403802759, 414124120, 422687378, 428601044, 437225990, 445352600, 454134279, 464455832, 471175830, 478932628, 487557766, 496341590, 504098324, 513215063, 521243207, 529896150, 537652820, 546646613, 554666566, 563186375, 571838998, 580201109, 1075364870, 1074074631, 589009561, 596978197, 605146778, 614175321, 622660115, 630312666, 637907009, 647826003, 655871515, 663685328, 672895513, 681037403, 689672921, 698157779, 706203291, 713404545, 722930199, 730975770, 738570241, 748489363, 1075137475, 756535003, 764873431, 1074368456, 772918874, 781650583, 1074653129, 1076240330, 1075737547, 789916373, 797902992, 1077056460, 1074982862, 1076822991, 1073969101],
    [106, 92, 13, 105, 82, 1697920, 10086592, 18475072, 26863616, 35383361, 43772097, 53063375, 60549249, 68937729, 78146257, 86617679, 94923409, 103394831, 111700561, 120172175, 128477713, 1073754112, 137203346, 143157843, 153207380, 161867860, 170757714, 176548565, 187721941, 195543684, 201844868, 212700690, 218491413, 229664789, 237486596, 243787780, 254643922, 260434517, 1076908994, 271607893, 279429700, 285730884, 297111255, 302377621, 313550997, 321372868, 327674052, 339054167, 1074829316, 345000664, 354804310, 363195028, 372608535, 378554904, 388087956, 396749332, 406302352, 412109400, 421642964, 430303444, 439717527, 446808084, 454314716, 465022672, 471091868, 481026714, 490188304, 1075365830, 496257564, 505799190, 515354192, 521423452, 531358298, 538291867, 546327192, 556524058, 563457627, 570976979, 581296790, 588623387, 1074073543, 597453534, 606462678, 613789403, 622619294, 632021722, 639610397, 1074616264, 647784990, 655616587, 664637145, 1075151811, 672950878, 680782347, 689802777, 696805907, 705948363, 715107997, 721971859, 731114123, 740273885, 1073863691, 748523097, 1075710924, 1074424773, 757050973, 765300377, 1076536266, 1076029390, 1076309965, 1076852681],
    [110, 96, 11, 109, 86, 2451585, 10848449, 18860224, 27248640, 35637376, 44025920, 52914828, 61179969, 67488398, 78080588, 86345857, 92654158, 103246540, 111511553, 119796239, 126339792, 134719696, 145189388, 1073752064, 151505488, 1076391937, 159885392, 171010765, 176673489, 184928974, 193702030, 204565069, 210227857, 218483214, 227256334, 238119565, 244033742, 254896653, 262927059, 269199438, 279275585, 288092691, 296995476, 304441537, 311265428, 1076929474, 321647187, 329607169, 336702101, 344836245, 1075893187, 355201683, 362105024, 370256469, 378390613, 388231759, 397658644, 404047936, 412199637, 420333781, 430174927, 437602432, 445483028, 453888533, 464767700, 471156736, 479037652, 487574085, 498322004, 504482454, 513370706, 520980564, 529517061, 539226767, 546425558, 555313682, 563456150, 571460293, 579990167, 588368470, 597379736, 605399126, 613403269, 621267472, 1074856965, 630811346, 638035984, 647088662, 656099864, 664119318, 671599248, 681142930, 688367760, 697944583, 1074100166, 706431704, 714188821, 721932881, 731499143, 739986008, 748005590, 755487249, 765053639, 772928087, 781830727, 1077248007, 789705239, 1073862601, 798094039, 1075193800, 1076251594, 1074433034, 1074715595, 1075518475, 1075802052],
    [118, 104, 1, 117, 94, 2378752, 10660864, 18744908, 27544704, 35826880, 43910668, 52604032, 61361869, 69338638, 77769792, 86527501, 94504590, 103304845, 111979649, 1073750016, 1075865601, 119670478, 128470605, 137145537, 144836174, 151268881, 161762496, 170699841, 178128524, 184823505, 195316800, 204254209, 211683020, 218377873, 229805762, 238054540, 246023824, 254971522, 263220300, 269102610, 279709395, 286011011, 296914434, 305163276, 1076405378, 313536084, 319696597, 330040915, 338857026, 347106508, 355479252, 361639445, 371984019, 378162197, 387092111, 395194005, 405538323, 411840067, 419704401, 428494037, 439914181, 445263442, 455738896, 462433926, 470953494, 481857029, 487476305, 498085524, 503983826, 514851988, 521285206, 529542726, 538086991, 546327638, 554446339, 562966101, 573572308, 579612355, 588262918, 597183698, 607686277, 613560022, 1076156419, 623914516, 630468103, 640680980, 647114390, 655903762, 663916239, 671755922, 682231376, 689188551, 696929365, 708349509, 1075392517, 714354247, 724567124, 731024911, 739134673, 747908743, 757728976, 765242967, 772689041, 1076972551, 781201094, 790408919, 797854737, 1074634692, 1075693574, 807186071, 815287442, 823963159, 832064594, 1074411465, 839928982, 848317462, 1077302216, 1074959368, 856706262, 1075245002, 864701589, 1076822987, 1073955851],
    [106, 92, 10, 105, 82, 2469057, 9964609, 18353281, 26741953, 35130369, 43650176, 52038848, 60427328, 69577729, 77204480, 86395473, 94244560, 102764175, 111520897, 119949841, 127798800, 136318543, 145075265, 153499155, 161893009, 170626706, 1073750017, 178665043, 187058897, 195792594, 203830995, 210135183, 220958226, 229389908, 235300943, 245370383, 254512722, 262551187, 268855311, 278793872, 285839061, 296498708, 305424402, 312348240, 320868047, 327683779, 336170645, 346830548, 352741583, 361336405, 371996308, 380922002, 386502165, 397416022, 405948432, 412200148, 422581782, 431253586, 437365844, 447747734, 456419538, 462531732, 1075863490, 472913622, 481446032, 487697428, 1075621828, 498223312, 504598168, 515000400, 521505807, 1076681671, 1075385286, 529413658, 538593365, 545787459, 554929688, 1074876361, 563759253, 570953347, 580095704, 1074629573, 588925141, 596119043, 605392015, 613299802, 1074385923, 622479381, 630951639, 1075185610, 638465754, 647908057, 656117399, 1074152392, 664147547, 673073689, 681283159, 688797338, 698239641, 706448919, 714479323, 1073918924, 723405401, 731221199, 1077077963, 1076312013, 739644955, 747998287, 756422299, 764644952, 1077373902],
    [106, 92, 11, 105, 82, 1837120, 10406976, 17056896, 27290817, 35679297, 44067969, 52456449, 60738688, 67388608, 77334720, 85723136, 92816913, 103075472, 111070208, 117720128, 127666304, 136710868, 145411284, 151274496, 161876500, 170576916, 176703057, 1073755074, 184970883, 195743380, 201869009, 212347011, 218656406, 226913795, 237686356, 245901315, 253772950, 260468291, 270453952, 279455811, 287458884, 294022851, 304621763, 312790608, 321013380, 1076905987, 327708374, 338036884, 346344976, 354436310, 361262614, 371591252, 379899600, 387990550, 395053714, 404899524, 414239746, 419982934, 428608210, 438322262, 447794370, 1074309188, 453773842, 463619076, 472960066, 478965318, 487328338, 495470225, 506514562, 512519878, 521072213, 531630209, 537945232, 546074246, 556795969, 563110992, 571666067, 580021833, 588017158, 597061131, 607127553, 613442576, 621997587, 1076419590, 630615627, 638512661, 649070785, 655385808, 663907977, 672558795, 680455829, 689580759, 697724555, 706357783, 714272467, 1075648523, 723135127, 731049555, 739176149, 748300887, 756182729, 1075402695, 764571145, 1075153929, 1074643916, 1073874888, 1074160590, 1076007877, 1074984909, 1077356495, 1076326346],
    [102, 88, 11, 101, 78, 1977473, 10505409, 18893825, 27282561, 35671105, 44190720, 52579520, 61232848, 69356608, 77474881, 86133888, 94787088, 103296064, 109432401, 119953040, 128462016, 134598161, 145118800, 153627776, 159764113, 170554513, 178138113, 187297492, 195720209, 203959296, 212463252, 220886097, 228469953, 237628948, 244086418, 254151888, 263179926, 269252306, 279317584, 288345622, 296636056, 304772817, 312872080, 1073742787, 321515092, 330190424, 338711640, 346426384, 355454550, 363744792, 372266136, 378277525, 389009110, 397299416, 405820632, 411831893, 422702803, 1073767364, 430986264, 436997653, 447868435, 454448859, 462294033, 473034387, 478967378, 487460049, 498200147, 504911447, 512625745, 520473809, 529298962, 537791633, 546565852, 555112091, 562826965, 1075877830, 571862553, 580408855, 589049434, 596897308, 605574871, 613813913, 622063260, 630609499, 639381210, 1075106763, 1074859973, 647229020, 655775259, 664546842, 1074623436, 672525913, 681072279, 689310809, 1076993994, 697691865, 706490010, 1075702722, 714468505, 1076496329, 722865177, 1074154445, 731253977, 1074440135, 1076288463, 1075525576, 1077374926],
    [126, 112, 3, 125, 102, 2401344, 10685504, 18918465, 27307137, 35695809, 44084225, 52481680, 61017216, 69510336, 77901522, 86437523, 94676096, 102960320, 111455890, 119991827, 128230400, 136514560, 145157715, 153423572, 162039505, 170323667, 178589332, 187205137, 1073750978, 193375765, 203476688, 212143700, 220759697, 227061270, 237030928, 245698068, 252347585, 262196816, 269160087, 279479889, 285650645, 294178005, 302714583, 311067713, 1075856325, 319204949, 327732309, 338628313, 344622209, 352759445, 361286805, 372182681, 378176513, 386838170, 394841109, 406103575, 414256282, 1073779651, 421834322, 431148226, 439291481, 448046231, 453553814, 462597768, 471117449, 481479682, 488943122, 498011673, 506766551, 1074850758, 512667226, 523422850, 531932759, 540085338, 1076438980, 546483720, 1076196295, 555134493, 565365826, 571387418, 582518360, 590416922, 596815432, 605335113, 613338141, 621719258, 632850072, 640748762, 647147208, 655797981, 663669981, 671812631, 683181784, 1076993032, 689352349, 697224349, 705998537, 713755735, 725124632, 730377942, 739691734, 748359387, 758555730, 764849757, 772721757, 781495817, 790302299, 800498898, 805875286, 1075694538, 1074403337, 815189078, 825664530, 832507612, 1075464139, 840354838, 849022491, 859219090, 865520790, 874450588, 882804318, 891227676, 899581470, 1074182095, 908004956, 916358814, 924520091, 1077336014, 933136094, 1075261388, 1076842445],
    [142, 128, 7, 141, 118, 2370561, 10521728, 18910400, 27298816, 35687488, 44207169, 52595713, 60984449, 69479617, 77761729, 86423057, 94931985, 103033985, 111589073, 120098001, 128199745, 136754833, 145935059, 153652369, 159812819, 170536528, 178697809, 185125396, 195595345, 202017812, 212479696, 220902420, 227076695, 235703383, 246320790, 252350100, 262811280, 269011092, 279622804, 286035607, 296652502, 302681684, 313142800, 321565780, 327739543, 338595414, 344624852, 352718488, 361664026, 369674324, 380286164, 388926998, 394694227, 405679130, 411995866, 422622422, 431147091, 436637203, 447622362, 456176790, 464701459, 470585047, 478580371, 486936152, 495881818, 506508374, 515033235, 523119706, 1073748931, 531674134, 537454807, 546082327, 554044952, 563254869, 571009047, 582389339, 588549640, 595988184, 604933786, 613987993, 621332692, 630623772, 638881416, 648948890, 655529621, 663930888, 672567004, 680529618, 689485401, 697485896, 708218395, 714378312, 722603099, 731428569, 739428488, 750161627, 756715212, 764546267, 1075344327, 773232221, 781765212, 790006876, 798789278, 1076926409, 806358546, 815175197, 823315144, 834047643, 840207560, 848432155, 1075101704, 856856277, 866044108, 873893532, 882544140, 890375323, 898799125, 907986956, 915410514, 1073810379, 1074353098, 1074892740, 924227293, 932759772, 940576402, 949393053, 958327518, 966560990, 974698009, 983493150, 991726622, 1074653122, 1076241359, 1076000718, 1000270430, 1008503902, 1016645788, 1025150540, 1033816140, 1041927820, 1077314572, 1050200092, 1058982028, 1074196429, 1067378846, 1076833222, 1076584389],
    [122, 108, 11, 118, 95, 2409664, 10258497, 18410561, 26799297, 35187713, 43576449, 52096064, 60484608, 68873408, 77907072, 86149644, 94039168, 102977101, 111210063, 119850048, 128092812, 136531661, 144764559, 153667216, 161647308, 170085901, 178974354, 186958848, 194808001, 203640461, 211873295, 218678931, 228362241, 235630158, 246345429, 252233235, 261916801, 268782805, 279899669, 288419542, 294055618, 304253516, 311354900, 319114261, 330231445, 335998466, 346605264, 353062487, 363785813, 369553026, 380159504, 386617047, 396422863, 405325392, 411782807, 422480580, 428534980, 439021138, 445050434, 453560019, 1073754114, 462114327, 472812100, 478866500, 489352722, 498134614, 504685654, 512052309, 523143812, 529198212, 539684562, 546628822, 553995413, 565086724, 571141124, 582020758, 588179092, 1076908036, 596864018, 604941017, 615575062, 1074829253, 622126230, 630542040, 638495257, 647284433, 1075109827, 655707736, 663661209, 672457750, 680873624, 688826969, 697363974, 706004561, 714697871, 722774618, 730918598, 739174100, 748252239, 756328986, 764472902, 773113489, 780889806, 789883546, 798027398, 805881427, 1075655686, 814967890, 823438042, 831448660, 840527055, 848610833, 1077232583, 1073849351, 857304079, 865422872, 1076222921, 873688210, 1075449802, 1074685962, 1076529099, 1074187208, 1074470923, 1076063240, 881553038, 890465490, 898330126],
    [138, 124, 12, 130, 107, 2290752, 10783937, 18402432, 26790912, 35179712, 43568192, 52087873, 60476545, 69365324, 77253825, 86176768, 94669953, 102419457, 111308300, 119731392, 128364239, 136498705, 144862860, 153285760, 162049041, 170315411, 178441873, 184962195, 195612244, 203992209, 212530241, 220646931, 228773457, 235293715, 245944020, 254323793, 262861825, 270978643, 279105233, 285625427, 296275476, 302435842, 313044177, 321582273, 329699027, 335957203, 346748033, 354856527, 362966732, 369808919, 380022287, 389181005, 395105872, 405188239, 414346765, 420410969, 431263382, 436915780, 447901389, 453965529, 463768641, 470470148, 478596674, 489844365, 495908377, 505711617, 1073745859, 512413316, 522768020, 529288792, 537851545, 548703830, 554356420, 562482882, 571231960, 582145670, 590646806, 1074552836, 596037250, 604786328, 615700038, 624201430, 1075881925, 1076155394, 1075128322, 629952024, 640865798, 647540430, 655649940, 666031814, 675064980, 1076451334, 1075426310, 680578631, 689597457, 698021589, 708611730, 714264201, 723151953, 731575829, 739814926, 747949770, 756207113, 764701780, 772462295, 784109138, 789892682, 798019079, 806644756, 814536400, 826052114, 831573639, 840199380, 847959639, 859614420, 865390090, 1077267400, 873647817, 882535633, 889902743, 901557268, 907202121, 916090001, 924513877, 935111764, 940887690, 1074401289, 1074949129, 949014215, 1076790282, 958287386, 966456981, 974696014, 1074184199, 1073946571, 1075802123, 983453274, 990697104, 999861902, 1008619162, 1015862800, 1027378898, 1033785050],
    [122, 108, 10, 121, 98, 2599936, 10953921, 18951361, 27339905, 35728449, 44116993, 52896769, 61312592, 69674049, 78089936, 86451329, 94867088, 103108162, 111879232, 120032784, 128273922, 137045184, 145862339, 153439874, 159854290, 170599424, 179416579, 186994370, 193408658, 201928211, 212542592, 221359683, 1073750018, 229592660, 235613268, 243740242, 252259987, 263302787, 271394000, 1075855363, 277433554, 285683218, 296201280, 304948304, 310987922, 319630933, 328150661, 336146131, 346533056, 355279888, 361319442, 369962709, 378482373, 387133142, 397905489, 405611664, 411913430, 420818647, 428420691, 439848593, 448333446, 454118615, 462237205, 471150231, 480750720, 490406979, 496192533, 504573526, 515346129, 523830854, 531582676, 537603284, 546123413, 555036247, 565677585, 574292995, 581914260, 587934868, 596979223, 605236886, 616139987, 624494278, 1073777607, 632245780, 638266388, 647179798, 658082835, 666437126, 1074321352, 1075122182, 671960214, 683248787, 691733699, 697388183, 708414547, 716899459, 722685077, 730803717, 740230745, 748531288, 756108311, 764358213, 773785305, 782085656, 1074878469, 1075423177, 789400598, 1076223940, 798951065, 807374554, 814959701, 824116761, 832540250, 839732310, 849317530, 856247378, 866094618, 873680085, 882749080, 1075711950, 890326103, 899526360, 1074689999, 1077315531, 1074197453, 1077096396, 1076849610],
    [110, 96, 10, 109, 86, 2526336, 10826817, 18943041, 27331713, 35720385, 44108801, 52857856, 61158529, 69552723, 78023744, 86324225, 94980756, 103189696, 111490241, 120146452, 128792278, 137006610, 145312468, 154220245, 162573968, 170478164, 176754370, 187512470, 196128336, 204556501, 212678230, 220892882, 229722645, 238105621, 246058578, 254888533, 263009814, 271224466, 277957209, 288437909, 296791568, 1073744835, 305219733, 311365320, 321991765, 330346192, 337988307, 345050779, 356455635, 361803281, 372721819, 378605275, 386862600, 398398547, 403746449, 1074295748, 414672904, 420417160, 431953427, 440044564, 448227464, 454102619, 462360136, 471414359, 479243857, 1076920328, 490170440, 496045595, 504968919, 515542228, 1073798086, 523725000, 532616851, 540707988, 1075384266, 547702931, 1074619333, 554241666, 565917404, 571518673, 1075945417, 582436955, 587796034, 599471772, 607816788, 614811667, 621350402, 633026140, 639536794, 1075696642, 649545947, 658191900, 664702554, 674711579, 681381388, 689518103, 698256922, 1075188679, 705776153, 714935884, 723072663, 731811546, 739330777, 748490444, 756107929, 765267596, 1074938892, 773802712, 1074182093, 782191192, 1077342158, 790579864, 1076832203, 798968344, 1076325327],
    [118, 104, 9, 117, 94, 2450561, 10480769, 18967552, 27356224, 35744896, 44133568, 52423681, 61433552, 69201089, 78210640, 85978177, 94987792, 103113729, 111668432, 119891009, 128446096, 134810194, 143224339, 153611280, 162096272, 168364562, 176778835, 187000001, 195554384, 202058452, 212855827, 218696402, 227372738, 237987414, 244280406, 252276435, 263187667, 269683349, 277704194, 286355096, 296741971, 305203352, 313476677, 319909464, 327806609, 338757720, 347031237, 353464024, 361328275, 372239507, 380700888, 388974213, 395406872, 403304017, 414255128, 422528517, 428830358, 1073753093, 436858385, 445852247, 456090774, 462253634, 470773270, 478801617, 487131794, 498033686, 504196738, 1076650947, 512716502, 1075873794, 521268825, 529738455, 539976918, 546434585, 554904215, 563441163, 572081882, 580349516, 588458519, 1074326471, 596766425, 605775579, 613904076, 622004949, 630550219, 639329819, 647458316, 655043220, 663875225, 672884315, 681012876, 688597588, 1076435980, 697659019, 706438811, 713763348, 723373724, 731606670, 739853850, 747833941, 756928028, 765161166, 773794461, 782093916, 790326798, 798960157, 807259868, 815492686, 823739994, 1075664838, 1075157006, 831719957, 840265291, 1075430340, 1073887178, 1077300235, 849291997, 1074705357, 1077072841, 857680477, 865683098, 1074989000, 1074227151],
    [102, 88, 7, 101, 78, 357568, 10693824, 18803905, 27348161, 35736705, 44125249, 52513793, 59332112, 69397520, 77802624, 84498064, 94563472, 102968320, 109663824, 119729232, 126291666, 134829776, 144895184, 151457298, 159740992, 168234578, 178187329, 1073753026, 187266755, 193400466, 203353089, 210072576, 220408896, 228519041, 237719187, 243748500, 254506132, 263384130, 269291089, 279541315, 288550082, 294727381, 302468692, 313226324, 322104322, 328011409, 336023060, 346650243, 355658882, 361836053, 371946516, 378613397, 386722961, 395267671, 405370371, 412167765, 420277329, 1076387843, 1075875780, 428297940, 1074587592, 439055572, 445443601, 453840593, 462376599, 473396375, 479005713, 487386321, 495931095, 506950743, 512543762, 523439251, 531320531, 1076167622, 537873943, 1073835975, 548893719, 554486994, 565382355, 573263443, 582448343, 588041298, 598936659, 606817811, 612725888, 621595794, 632491027, 639071425, 647573016, 655848513, 664350296, 672625665, 681127640, 1076729803, 689403009, 697904792, 706686550, 715075222, 1075170252, 723463894, 1074402253, 731852310, 1074939850, 1074181070, 1077074889, 1075525583, 1077370821],
    [126, 112, 1, 125, 102, 2108609, 10595520, 18984064, 27372544, 35761216, 44280897, 52669441, 60943952, 69446785, 77605889, 86224065, 92646929, 102886928, 111553553, 120303187, 128052880, 134590033, 145108049, 153716436, 162376916, 170634963, 178384592, 184921809, 195439825, 204048020, 212708500, 220966547, 229362899, 235253393, 245771409, 254379540, 263040020, 268938901, 279694483, 288075283, 295709825, 304711252, 313371732, 319270613, 330026003, 337652801, 346924695, 352824853, 363580499, 371461650, 380610198, 386510360, 394767957, 405917378, 413797587, 422553110, 428453528, 1073750466, 436973252, 447859778, 455740435, 464758489, 470658778, 478916228, 489802882, 497683603, 503950936, 514696919, 520990298, 529247812, 540134402, 547622482, 554282712, 565028439, 571321882, 579579396, 587845211, 596618331, 606342866, 615753369, 1075861508, 621784731, 629787803, 640289875, 649307673, 1075353541, 655208090, 666094609, 674106456, 682468887, 1075114947, 688893659, 696896731, 707006098, 716416601, 722447899, 730450971, 741215448, 749709014, 758369425, 766381208, 774874710, 1076956103, 783535185, 791546904, 1074359238, 1076465608, 800312529, 807022236, 815385626, 823799388, 832293973, 840576540, 849071253, 857353948, 1074651083, 865848341, 874105946, 882869981, 890883226, 899647133, 1075722189, 907791573, 916424221, 1077309391, 924437722, 933201501, 1076794314, 1074971593, 1073948622, 1076316108],
    [114, 100, 13, 112, 89, 2436097, 10982529, 18975808, 27364480, 35752960, 44141760, 53030544, 61314113, 69200403, 77958163, 86584848, 94868481, 103362256, 111645889, 119794390, 128527952, 136951313, 144960150, 153859604, 161819841, 170773079, 178894545, 186985537, 1073750978, 195554008, 204060305, 212151425, 218599065, 229108248, 237702738, 246003281, 254274136, 262911700, 271257298, 277581530, 287828632, 297086105, 304854612, 310873625, 1075862467, 321228371, 327913114, 337635411, 346797716, 355143186, 363171539, 369856026, 379578579, 389360665, 397391381, 403410522, 414042647, 422252178, 430945941, 436702937, 1075360708, 445615816, 455985815, 464858329, 472888917, 478645849, 1076941765, 487558728, 497389203, 505407635, 515189849, 520983760, 529632905, 537890440, 548260567, 554538000, 563285723, 1074859974, 571575817, 579833352, 591251482, 596481168, 605228571, 613519049, 1074610184, 624806106, 630035536, 638783067, 647073353, 1073843143, 655855242, 1074381833, 666749082, 674215637, 680726171, 689409610, 700303450, 706186762, 715385430, 723201566, 731352778, 740551190, 748367518, 1074140170, 756795933, 765144798, 773704412, 781921886, 790350557, 1075210189, 798870108, 1076276171, 807127709, 815647260, 1076551628, 824035996, 1075785679, 1076852686, 832293469],
    [98, 84, 1, 97, 74, 2343936, 10898561, 18476224, 26864768, 35253248, 43641920, 52161729, 60550209, 68938881, 77973199, 86395969, 94104577, 103254736, 111527439, 119950529, 128420496, 136693327, 145116161, 153586192, 162156114, 170247823, 176549442, 187140688, 1073754112, 195710482, 203670656, 210103810, 218737364, 229265042, 237225152, 243658370, 252291732, 262819538, 270779456, 277457428, 288255572, 296732309, 302622804, 313420948, 321898005, 330198228, 338675285, 344959639, 355888856, 363841237, 370125335, 381054552, 388621392, 395544792, 406220440, 413787344, 420457047, 428732035, 439774744, 447341712, 454011607, 462286531, 472804372, 480896016, 490048068, 496389649, 506825348, 513166929, 521644569, 529395267, 538332881, 548768452, 555110033, 1076904004, 565544964, 570814146, 579726851, 1073780677, 1075104710, 1074337794, 589065939, 596871256, 1075403779, 605843091, 613919321, 622751446, 1075685319, 630696665, 639528534, 647473817, 656305686, 663980056, 1076230090, 672951891, 680757400, 1077284809, 689860246, 1074686923, 698117651, 1076536264, 1076031438, 1076827085, 1075005388],
    [118, 104, 3, 116, 93, 2321473, 10605697, 18861248, 27249792, 35638336, 44026880, 52784844, 60937281, 69832397, 77844111, 86339084, 94762127, 103386765, 111529552, 119787023, 128282188, 136705039, 145329677, 153472528, 161730255, 170225292, 178648271, 1073752064, 187272781, 195415696, 203673167, 1076391937, 212202575, 220425409, 229879441, 237358800, 246271699, 254268432, 262368257, 271683086, 279826067, 287823056, 296447168, 305237646, 313380371, 321377424, 329477249, 338931217, 346934867, 354931792, 363555840, 372346446, 380333184, 388093121, 397512398, 405498944, 413258753, 422817489, 430830675, 439447043, 447983185, 455996435, 464613059, 1076931971, 471051924, 481162387, 489778243, 496217620, 506328275, 514944131, 520867544, 529387143, 538160852, 546295321, 557141718, 562810392, 571330055, 580103764, 588238425, 599215826, 604753560, 1076681668, 1075387396, 1075667909, 613273287, 622309077, 632770066, 638307928, 646827591, 655993944, 663735961, 674713170, 1075937287, 681029141, 691490450, 697552585, 706317847, 714067673, 1073861570, 724913686, 1074927558, 731483799, 742083737, 747884041, 756526741, 1075210184, 767249433, 773049993, 781823192, 792022614, 798215753, 806858325, 1076265993, 817581273, 1074198475, 823766040, 834358361, 840543384, 850742934, 857312855, 1077349322, 1074482186, 865701591],
    [106, 92, 13, 105, 82, 2379776, 10653761, 18755585, 27144321, 35532865, 44052544, 52310209, 60829824, 69208780, 77606912, 86266048, 94539905, 102772928, 111424080, 119540364, 128208960, 136482817, 144978640, 153234001, 161763456, 170037441, 178532880, 186788497, 195465356, 201749140, 1073750016, 1075865601, 212087440, 220342993, 229019852, 235688654, 245508625, 254186060, 260469460, 270534732, 279351820, 285897362, 295700492, 305173133, 311185934, 321390800, 330338893, 336228946, 346556560, 355619332, 363893453, 372257302, 380110928, 389059085, 394686996, 405276688, 412250639, 420123283, 430844501, 436900563, 445018708, 456010453, 462582351, 470454867, 481176213, 489837124, 495620627, 1076406213, 506475158, 514721814, 523391684, 529699535, 539896341, 546722519, 554995860, 565195478, 573442262, 1076161796, 582111364, 588419151, 1076698051, 598608022, 605303369, 613831319, 621973519, 632304214, 640550998, 647246473, 655528591, 663384594, 1075409858, 672412169, 680824916, 688673422, 1076989895, 697578185, 705990676, 713839182, 1074645960, 1074402246, 1074942982, 1075223561, 722628751, 731156692, 739660311, 748048983, 755659474, 764571855, 1075758026, 1073939466, 1074231243],
    [110, 96, 7, 109, 86, 2504896, 10777601, 18354369, 26742849, 35131393, 43520129, 52039872, 60428416, 68816960, 78133775, 86275137, 93982720, 103256656, 111688271, 119829633, 128422416, 136722560, 144995521, 153588432, 162419712, 170276928, 1073750017, 178754192, 187585664, 195574415, 201953874, 212751424, 220740303, 229872149, 237385728, 246305984, 255038101, 260444866, 271465172, 279868610, 288592469, 296630868, 305297107, 313758421, 319164930, 330185364, 338588674, 345084566, 355612822, 364017171, 369726162, 378278553, 389167638, 397571667, 406163609, 411832921, 422722134, 431126163, 439980631, 445518343, 456276694, 462574677, 473535127, 479072839, 486937218, 497424977, 506360962, 515478231, 1075868614, 521146952, 530979473, 538072277, 548769881, 554701448, 562434626, 573454868, 581858370, 590975511, 1076924418, 596513415, 606477009, 613971031, 621908054, 630198984, 638325465, 648419857, 655914135, 666210521, 672010951, 680678421, 688493074, 1074840583, 697307656, 705434137, 714634263, 724930585, 1074069512, 1073834948, 731411671, 739348694, 747787413, 1076475849, 755602066, 1077270474, 1075187659, 764514326, 1074682821, 773820952, 1075488716, 1076284355, 782209688, 1074474958, 790598232, 798986968, 1076846541],
    [118, 104, 5, 117, 94, 2517056, 10801216, 18903105, 27291649, 35680385, 44069057, 52744192, 59009680, 69350993, 78017042, 86298816, 92564048, 102905489, 111702611, 119960274, 128610900, 136630400, 142895824, 151286339, 161625809, 170422931, 178680402, 187331284, 195743937, 201615888, 211957265, 220754451, 229012114, 237662740, 246075457, 254691411, 262813205, 271086291, 279605908, 288018433, 296634387, 304756373, 313184385, 321800403, 329922261, 336097815, 347009047, 355354771, 363476565, 369652311, 380563543, 389040338, 397022228, 403206871, 411988504, 1073746885, 422506711, 430983186, 1074820034, 438965332, 445837394, 456149138, 464131284, 470315671, 479097560, 489615511, 498092114, 504394312, 514462868, 1076921284, 521040472, 529855001, 539387904, 546337480, 557201110, 562983576, 571666642, 581331072, 587494083, 599144022, 605221010, 614885568, 621834760, 632698518, 638775314, 647129233, 655651529, 666252822, 672461401, 680683729, 1073800135, 689205769, 699937880, 706015961, 714237969, 725103768, 731435547, 739403857, 750269656, 756347545, 763654659, 775435288, 781767323, 788820611, 798373402, 806933211, 1075910659, 815150682, 1075398606, 823710299, 831550088, 840316570, 1074109448, 1075702726, 848589385, 857093850, 1076508618, 1077307340, 865366665, 1076267981, 1074449417, 1074737099, 1076844495],
    [114, 100, 11, 113, 90, 1962177, 10506241, 18894977, 27283521, 35672257, 44191808, 52580480, 60953168, 69357568, 77459457, 86134976, 92557905, 102896272, 111923281, 120093203, 126112401, 136450768, 145477777, 153647827, 161616400, 169734273, 176706070, 187202131, 193204820, 203288641, 210391704, 221141719, 226759188, 237367488, 243946200, 254311059, 260985561, 268840982, 279310400, 285889048, 296639127, 302273233, 310645460, 321638609, 327832152, 338582039, 344216081, 352989272, 363581457, 369644118, 380656282, 388903622, 396750976, 403198678, 414210650, 420368921, 430846534, 438693888, 445141654, 456012422, 464384725, 470700633, 481178118, 489681490, 1073756100, 1077178374, 498489947, 503722134, 514847378, 523655835, 528887894, 540013074, 1076927427, 1075367879, 548428314, 554586777, 562704408, 573567698, 582375963, 587870360, 598602389, 607148762, 612635284, 623768149, 630870604, 640571991, 647778908, 655765596, 666103897, 672813708, 683039451, 689721884, 697708572, 707654165, 714635997, 723276444, 731263132, 741601433, 748190301, 756830940, 764817628, 775155929, 781865484, 790133277, 797585624, 1074598850, 808710169, 814100694, 823687837, 1074883531, 1076467656, 832197324, 1075167244, 1073883086, 1076250570, 1074175951, 1075766213, 1076038601, 1074491341],
    [118, 104, 9, 117, 94, 1878016, 10293376, 18919616, 27308096, 35696768, 44085248, 50891472, 60764368, 67555921, 76057168, 85930064, 92721809, 100971154, 111096464, 119711890, 126276113, 134525522, 145297537, 153266258, 159830737, 168079890, 178065600, 186820626, 196006547, 201634514, 211759632, 220375250, 227201556, 237572161, 243828880, 254857813, 260616791, 271126721, 279742551, 288281171, 294171159, 304680961, 313296919, 321835731, 327856772, 337448960, 344492048, 355521045, 361411076, 369668823, 379392064, 388794583, 397464277, 403354180, 412919936, 422908610, 430887443, 436777623, 445452888, 455903383, 1073756099, 464573077, 470987397, 479007384, 488417472, 496562710, 504541893, 513323737, 520950488, 530360384, 537580180, 546484805, 555266713, 563417235, 573868185, 582415048, 588952199, 597209625, 605204997, 613748819, 624199705, 1077168133, 632746568, 638235332, 647541337, 655691987, 666142809, 1074301956, 674689544, 681226823, 691343938, 699697369, 708244104, 714781383, 722905281, 733287042, 1074588680, 739963610, 748335623, 756459649, 766841346, 1076697095, 1075404802, 773517850, 780997144, 790014017, 1075938249, 798552726, 806686739, 815179777, 823849562, 832107222, 1073869771, 1077023690, 839570004, 1074943949, 848884310, 1075224518, 1075768268, 856347348, 865792666, 1076561871, 1074227150],
    [94, 80, 7, 93, 70, 2398208, 10489920, 18911425, 27299841, 35688513, 44077185, 52729984, 60821696, 69531218, 77598720, 86284352, 94697106, 102764672, 111975059, 119862994, 128586260, 137140947, 145028626, 153752148, 162306579, 168047317, 179083859, 186947776, 195695252, 202045014, 1073750978, 213162499, 218378773, 227210966, 235311767, 246069399, 254546448, 260765334, 268866135, 279623767, 288502417, 294319638, 302420695, 313178327, 322056785, 327586327, 338343959, 346690260, 355661382, 363641543, 369373845, 380827142, 388807239, 397152912, 1075868612, 403477066, 414381766, 422361735, 428094037, 437031434, 447936134, 455916039, 464261840, 1076931591, 1076687878, 470586058, 481728720, 489829073, 498375363, 506204752, 1077216201, 515283088, 523383313, 1073825733, 1074113484, 530068120, 540318275, 546845208, 557095555, 1076487171, 563926617, 1076235208, 572011224, 582391824, 1074418637, 589092505, 597176920, 607557712, 614389466, 622777882, 629969546, 639555162, 1074959370, 647812825, 656332442, 1075239886, 664589849, 1075515343, 1074749387],
    [114, 100, 10, 113, 90, 2584641, 10547200, 18935872, 27324544, 35713216, 44232705, 52621441, 61126160, 69519376, 77787329, 86470657, 94564417, 103074448, 111458000, 120025281, 128234640, 136628432, 145191041, 151319107, 159969922, 170825426, 178571856, 187519699, 193262211, 204379730, 213305475, 221074067, 226816515, 237934226, 246859843, 254628371, 260371139, 272025795, 279229520, 288452690, 1073747971, 294318743, 305042962, 313968643, 322007058, 327988884, 339396759, 347435541, 353301080, 363893848, 372435473, 380727442, 386593367, 395097620, 406505559, 414011987, 420147927, 428652244, 440060119, 447836370, 453964312, 464557080, 473098961, 481653397, 487518936, 498111704, 506653265, 515207765, 520811031, 529315412, 540723223, 548762325, 554627736, 565220504, 573762193, 1075336136, 582570505, 1074829255, 589084246, 1075102660, 599347849, 1073821638, 605612697, 1077240457, 614250134, 624513097, 630639258, 639415830, 649679049, 655804954, 664581846, 672747674, 681110041, 688452290, 697913946, 706136154, 713617986, 723349713, 731441753, 738783746, 748515345, 1075939330, 1074388938, 756607705, 765292625, 773648911, 781634266, 790188250, 1075709901, 798814799, 1074164684, 1077063627, 806965274, 815592143, 824012945, 1076815822, 832369295, 1076300815, 1074752453],
    [114, 100, 9, 113, 90, 2414784, 10776705, 18927617, 27316417, 35704897, 44093569, 52974160, 61134912, 69775889, 78140112, 86300800, 94941777, 103305744, 111466496, 120107729, 128471696, 137165008, 143184595, 153662097, 162330704, 170160129, 179089987, 187496592, 195326017, 201904787, 212644547, 221050896, 228880577, 237810307, 244109845, 1073746882, 252631762, 263213588, 269013523, 279753219, 1074819075, 286186066, 294572694, 305181190, 311218773, 319740562, 330322644, 336646872, 347124358, 353161877, 361683474, 372265556, 378581139, 389478999, 397431444, 403755672, 414233286, 423033559, 428790294, 437309976, 446083094, 456718485, 462344918, 470864472, 481342022, 1076927494, 487903754, 498530967, 504287830, 512283219, 521187411, 529322709, 1075633093, 540473879, 546591321, 555135190, 1075384263, 565770325, 572019354, 579907795, 590936277, 597185050, 1074613193, 605859928, 613732938, 624490517, 630477337, 638627859, 647287498, 656202331, 664294106, 672575638, 681235164, 689756891, 697586393, 706523160, 714396298, 723178076, 731699867, 739529369, 1074369546, 748466328, 756732444, 765254171, 773345882, 782151708, 1075181515, 790287004, 1077281732, 798929052, 807186648, 815706332, 1073900488, 824094812, 831959126, 1076529102, 1074193356, 1076047823, 1076848589],
    [130, 116, 10, 125, 102, 2427008, 10850432, 18428033, 26816577, 35205121, 43593921, 52793344, 61409804, 69685902, 77924416, 86347968, 94982797, 103125056, 111741644, 120279696, 128256000, 137334849, 145314317, 153684620, 162500801, 168120980, 178991827, 187238988, 196186316, 204165648, 212546195, 220530880, 229740556, 237589197, 246100499, 254775297, 261163663, 271274576, 279654995, 288460876, 294717967, 305082966, 312955598, 321884289, 328018006, 338637462, 344273475, 352670420, 363958412, 369961110, 380580374, 386224660, 395686421, 403777747, 414134998, 420033029, 430395982, 437629589, 445720723, 453325443, 464868055, 471183957, 479529690, 486879747, 498422423, 504050246, 513127125, 521734681, 528822979, 539447822, 545993350, 555192913, 562899158, 1073755139, 571290183, 581521997, 587936454, 597537304, 605096527, 613233159, 621359685, 629494356, 638530186, 647049929, 656257688, 663816911, 671953543, 680080069, 691360343, 697250378, 705769993, 714576593, 722282518, 730411653, 741036752, 747582154, 756519441, 765004377, 1077172229, 772616903, 783634967, 789656137, 798462609, 806685274, 1075354631, 1075627976, 1074077704, 815493137, 823462554, 832418392, 840659025, 848376457, 857584344, 865150995, 1075934148, 1076990985, 874213521, 881537542, 890316883, 1075168194, 1073882114, 1076250630, 1074441222, 899379409, 906965514, 915737114, 1076809738, 924807826, 932776601, 1074991051, 1074751499, 941585106, 949553881, 958362130, 966750802],
    [118, 104, 13, 115, 92, 2061312, 10661889, 19216449, 26808384, 35196928, 43585664, 51974336, 60781632, 69679692, 77770881, 85922317, 94713857, 102936769, 111506445, 119476941, 128127695, 136647376, 145177228, 153793166, 161838285, 169808525, 178459215, 186978832, 195508940, 204124878, 212169869, 220140109, 228790927, 236942528, 245708929, 254456398, 262476432, 270874817, 279622158, 287667277, 296424084, 304051328, 311244948, 321040449, 329978580, 337842703, 346362448, 355300559, 361576660, 369660045, 380310100, 388985872, 395130964, 403214349, 413864468, 422540368, 428685332, 436768845, 445559512, 455963791, 463944204, 470356675, 481260688, 487502424, 498014866, 504279704, 514683919, 523180562, 531592400, 537834008, 548346578, 556627023, 562991767, 573512274, 580081366, 588847827, 596152525, 604574275, 613635606, 622533273, 630100567, 1073744834, 638801494, 647698969, 655266519, 663967382, 672733715, 680432151, 689377866, 697899667, 706384597, 713626243, 723196633, 731550229, 1074287556, 1074834436, 738791939, 748098250, 1076680646, 1075128326, 756619859, 765104789, 1076448259, 773624337, 781916761, 790041098, 798963919, 807047765, 1074634697, 1075703817, 1077027784, 815207050, 823956049, 832518159, 1075987397, 1073906698, 840733393, 849295439, 1074191307, 1075521479, 1076327435, 857510545, 866072719],
    [130, 116, 11, 129, 106, 2478080, 10569729, 18968705, 27357377, 35745793, 44134465, 52654080, 61042752, 69431488, 77678721, 86626960, 94597248, 103355922, 109408274, 119621697, 128570064, 136910418, 142962770, 153176257, 162124368, 168391315, 176624787, 187290128, 193688212, 204019410, 210071762, 220581952, 227232405, 235615380, 245747904, 255027799, 260796948, 269169684, 279302272, 288582295, 294613634, 302855298, 310735506, 322032209, 330525207, 338236562, 347198097, 355691223, 361460436, 369833172, 378630853, 389141009, 395528854, 406525638, 412185157, 422695633, 429083350, 436826835, 448468550, 456512152, 462385858, 471026198, 482022918, 490066648, 1073754374, 495940098, 504580694, 515576966, 521368089, 529625733, 540398168, 545878611, 554387989, 563287641, 571699289, 579957253, 590729752, 1076904900, 1073776645, 596331093, 605230105, 613642969, 1074317251, 622187226, 630396569, 638808217, 647352986, 656108059, 663319059, 1074078663, 672339161, 681013834, 689558044, 698051163, 705393236, 714544261, 722956938, 731501212, 739994331, 747598402, 756487365, 764899850, 1075927042, 773444188, 782060125, 788993107, 798454474, 806736474, 815491739, 1075418056, 1074912266, 823751371, 830936275, 839600853, 848941788, 857305739, 864892098, 873845274, 882723485, 890057730, 899500765, 907637323, 915870725, 924666397, 1075713997, 932803083, 940389442, 1075203083, 948646996, 1074702286, 957813829, 1076295628, 965153811, 1077357513, 1076588495],
    [102, 88, 9, 101, 78, 358593, 10571841, 18960513, 27348993, 35737793, 44257344, 52645888, 60633744, 69423232, 76249152, 86200512, 92590738, 102576848, 111639249, 119993044, 127742544, 136805009, 145281557, 152908304, 161970769, 170324628, 178860691, 187136529, 196039254, 204001941, 212415187, 218855552, 229593750, 237433364, 245969491, 252409856, 263148054, 271110741, 279523859, 285964480, 296702678, 302469847, 313585878, 319378008, 327618648, 335902721, 344936985, 1073755074, 354996949, 361320984, 369570007, 377845825, 389083286, 394990106, 403011713, 411521559, 422637590, 428954331, 436671128, 445206680, 453988953, 464580694, 470897243, 478613528, 487019159, 497480276, 503927512, 512168152, 521097881, 528962135, 540340377, 545730647, 557117465, 562762330, 1076913094, 571429593, 1075872712, 582283353, 587928282, 599060697, 605114907, 613094042, 1073802185, 621073106, 629616791, 1076431812, 637850194, 647058075, 654782487, 1074356165, 663015954, 672608475, 1075680199, 681366172, 689385563, 1074911179, 698143452, 706162715, 714920476, 722940059, 731697756, 1075185612, 1074158541, 1075492814, 1077342147, 1076826063, 1074751434],
    [122, 108, 0, 121, 98, 1970304, 10735681, 18985088, 27373760, 35762240, 44150784, 52670657, 61059137, 69708432, 77836289, 86380688, 94621825, 103002241, 111651536, 119787713, 128455313, 137079313, 145601107, 153490000, 161730561, 170896086, 179155475, 184939026, 195564241, 204310547, 212710099, 218493650, 228987088, 238004758, 246264467, 254153232, 262664272, 271419539, 277459524, 285602450, 295571648, 305113686, 310768210, 321392657, 1073753027, 330139859, 337514496, 346550480, 355305555, 362680384, 371716112, 380611222, 388493456, 396890705, 1076388802, 405252176, 412201608, 420205144, 428749335, 439068753, 445231812, 453915223, 462541463, 472623249, 479211608, 487314072, 496611978, 506177745, 512766104, 520868568, 1075873735, 530166346, 539469840, 546426967, 554578071, 563720906, 571968084, 579875032, 588369943, 597275146, 605522452, 613298903, 621924567, 1074060233, 1075383306, 630688468, 638595608, 646696984, 656124572, 663859784, 672395925, 681194139, 689809945, 697692762, 706359835, 714975897, 722055684, 731123794, 739635866, 1074620358, 748399196, 756281877, 765080155, 1076204491, 1074911181, 773696217, 1075196878, 781300424, 789844178, 798356186, 1077047237, 806849172, 814330500, 823390805, 831787154, 1076791300, 840674012, 848409096, 857076250, 865743579, 1074460620, 1077353480, 874359385, 882111189, 890507282, 899394076, 1075790799],
    [102, 88, 2, 101, 78, 366721, 10351809, 18976896, 27365568, 35754048, 44142592, 52662337, 61051073, 69439617, 77854352, 84252673, 94605313, 102873616, 111014977, 119747092, 128815827, 134582292, 144963152, 153204880, 161952469, 170758739, 176656597, 186759248, 195294928, 203895381, 212701715, 218599509, 228455425, 235247681, 245838485, 254644883, 260542613, 270908035, 279180304, 285545174, 294097429, 304199888, 312341633, 321720919, 327520980, 338016771, 346551507, 355275415, 361075284, 371571395, 380105747, 1073754243, 388829719, 394629780, 405271699, 411408577, 422384343, 428839640, 438679619, 447214675, 456340101, 462393880, 472627416, 481031319, 489894405, 495948376, 506181720, 514585687, 1076914821, 523448389, 529764874, 537891480, 548124824, 556528855, 565391557, 571708042, 581679128, 590083095, 598159381, 605262410, 613915281, 622196370, 631451732, 638816970, 647469649, 655750674, 1076400138, 665006228, 672635601, 680916690, 690172116, 697801233, 706082386, 1074841548, 713364118, 721752598, 730141270, 1074081734, 1076716482, 1075947470, 1076216772, 1073876937, 1074689991, 1077319624, 1075239885, 1075519439, 1075792843],
    [118, 104, 13, 117, 94, 2213888, 10088576, 18477248, 26865664, 35254336, 43774081, 52162561, 61191887, 68939841, 77711552, 85717185, 92688977, 102757072, 111523407, 119916625, 128741906, 137074324, 145083025, 154169492, 162240212, 170248913, 179335380, 1073754112, 187405908, 195414545, 204501524, 212571156, 220317824, 229666900, 236974672, 245741071, 253872192, 262959698, 270907023, 279571093, 288125650, 297113234, 305514704, 313290898, 320860688, 330667026, 339068944, 345002582, 355833042, 363457045, 370168534, 379581072, 389387346, 397789328, 403067089, 414430739, 422177493, 428888598, 436728389, 447985363, 455731797, 462025414, 470962907, 478933640, 489928339, 1076913092, 498452560, 504517147, 512225925, 523482707, 532400665, 538473048, 545780421, 555333336, 565955225, 572027544, 579596872, 588887128, 599509593, 604631622, 612782097, 621539848, 630830616, 641452761, 1075876809, 646574726, 654725265, 663483080, 672773272, 1074841538, 1074075656, 680129030, 689467416, 696775173, 706590295, 1075399686, 1074633733, 714101398, 723367575, 731009627, 740275866, 1075692487, 748187864, 757053018, 1073878987, 1075210188, 764564123, 773830362, 781709901, 1076277194, 790516380, 798865111, 1076816835, 806875789, 815682268, 824030743, 832041485, 840847964, 849327642, 857207501, 866013724, 1076561933, 1074493390],
    [122, 108, 13, 121, 98, 2453632, 10858497, 18872385, 27250880, 35639296, 44028032, 52416576, 61321932, 69824716, 77592705, 86495950, 94876236, 103379596, 111147009, 120050190, 128430604, 136933452, 144701633, 153710604, 161984652, 170392144, 1073752064, 1076391937, 178614464, 187675213, 195557904, 201708049, 212325006, 220557376, 229618317, 237501072, 245879374, 254111744, 263172621, 271055568, 279958099, 285954770, 296727245, 302774996, 311120466, 321780418, 329625793, 338557506, 347566286, 354791489, 361353941, 1076922690, 1074318338, 372232915, 381120590, 388345985, 395049492, 403296789, 414175763, 420720657, 428561042, 436992596, 445239893, 456118931, 462115346, 472774786, 478794389, 488092374, 495964374, 507080725, 512490132, 520475217, 529772625, 538169943, 549023893, 556660738, 562418385, 572239959, 580113047, 590608403, 599224334, 605794455, 613667351, 624521301, 632551571, 638824657, 647483928, 655610583, 666106067, 674721934, 679858833, 689680599, 697291414, 708407509, 716437587, 723497624, 731369624, 739234390, 748411407, 756527254, 765284953, 773313112, 781965903, 1074598853, 790081622, 797954582, 1074874308, 807131791, 1074108355, 815772376, 824005273, 832032984, 840686287, 849326104, 857559769, 865317009, 874336793, 882618391, 891269208, 899133462, 1075174346, 1075452938, 1075734472, 1076274121, 1076020171, 1073950663, 1076852678],
    [122, 108, 11, 121, 98, 2397248, 10628161, 18756672, 27145216, 35534016, 43922560, 52713100, 60959745, 69768332, 75773518, 86660685, 94514305, 103323212, 109327886, 120215245, 128068801, 136877772, 145381005, 153654796, 1073750016, 161615375, 1075865601, 170546701, 178558144, 186781391, 195318860, 203723904, 211947151, 218510865, 228873420, 237278208, 243674834, 252065425, 262427660, 269128705, 277231185, 285758478, 294294657, 302265998, 311326416, 319460417, 327693972, 336221201, 344626369, 354553423, 1076409282, 361379415, 369906775, 378574547, 388763157, 394933783, 403600976, 412128787, 422317653, 428095182, 437155472, 445953624, 455872213, 462042775, 470709776, 479507992, 489426581, 495597271, 504124439, 513062552, 520498770, 529020628, 537278161, 545805518, 554735251, 562441874, 570963540, 579614340, 589059156, 596948696, 604384786, 613168644, 622613716, 630757017, 639119062, 646460948, 655111876, 664556564, 672699929, 681061974, 688928453, 697054788, 705189006, 714643033, 723004950, 731133639, 1076942852, 738874449, 748197593, 756559510, 764425797, 773338697, 780948631, 789616211, 797980293, 806893193, 814371985, 823145989, 832058889, 1075387397, 839537873, 848574023, 857224905, 865883284, 873739783, 1075660809, 881611991, 890517127, 1074369480, 1074910216, 1075186695, 898126926, 1074689995, 1077323718, 1076282314, 1073939466, 1074229187],
    [102, 88, 11, 101, 78, 1578113, 9966593, 18355265, 26744001, 35263552, 43652224, 52843087, 60429312, 68818112, 78008975, 86488656, 93985872, 103174671, 111654608, 119151824, 128340687, 1073750017, 136820368, 144317584, 154300624, 161486355, 170374672, 177871888, 187584531, 195040851, 204094993, 212211284, 221139027, 229873173, 235148309, 245372627, 254426833, 262543060, 271470803, 280204949, 285480085, 296369745, 305295376, 314021527, 319035093, 329258643, 338312849, 346428948, 355356819, 364090581, 369366613, 380386516, 388765273, 397570128, 406426713, 413940756, 422998614, 431462103, 439106644, 448164502, 456627735, 464679056, 473405015, 481050260, 489034900, 498496022, 506696789, 1075858370, 514596571, 522983129, 532050646, 540644569, 548150875, 556537369, 565736018, 574198809, 1074302917, 581705371, 590091929, 599290386, 607753369, 1074584515, 615259675, 624456338, 630822492, 641233618, 647861848, 1075388356, 656175770, 664639192, 672952858, 681154076, 1075663814, 689730266, 697931484, 706507354, 714970648, 723359384, 1074894792, 1075181511, 731485852, 1077294027, 1077035980, 1073915849, 1076283338, 1074211789, 1076588494],
    [98, 84, 0, 97, 74, 281728, 8705025, 18616385, 27292865, 35812416, 44201152, 52589696, 60847105, 69235841, 77755392, 84167872, 94638608, 101119632, 111178817, 117722112, 127668417, 134674128, 142888000, 151451216, 161747152, 168351317, 176451153, 186912912, 195718742, 201905877, 211554305, 220884502, 227071637, 236720257, 246050518, 252237333, 262410320, 271216278, 277360661, 285668368, 296801811, 305425943, 311177938, 321967763, 330591959, 336343698, 347133523, 355757719, 361246805, 372299475, 380923479, 386675218, 394948308, 403452498, 411358273, 422449753, 428502548, 436524161, 1073755074, 447615705, 453275281, 461690049, 471103112, 481169945, 487912448, 495611476, 504657416, 514724505, 521598552, 530082832, 538211912, 545796245, 555021376, 563637392, 571930328, 579350741, 588803280, 596932296, 605353088, 613052052, 1076907016, 622130368, 630746192, 1074564042, 639382170, 647427736, 654601745, 1074322375, 664547866, 672593432, 679767761, 689713754, 1075389379, 698102490, 1075931083, 1076210633, 1076490188, 1076764621, 1075729349, 1074960334, 1075234758, 1074214863, 1077363652],
    [110, 96, 13, 109, 86, 2094144, 10386497, 18896001, 27284481, 35673281, 44061761, 52581504, 60969984, 69358656, 77608529, 86111952, 94272705, 102913216, 111163089, 119666256, 127827073, 136861203, 144717457, 153220752, 161381377, 170677844, 178271761, 187333696, 195163664, 204232212, 212350530, 220888064, 228586624, 1073744706, 237786836, 245904578, 254442624, 262141120, 1074293699, 271341204, 279852163, 287306752, 296385728, 304633427, 313013250, 321639572, 330202257, 338187923, 347223634, 355194068, 363756625, 1076403140, 372126915, 380533969, 388625427, 397292547, 405699601, 413791379, 422074067, 430847043, 439080020, 447110741, 1075377093, 455619714, 464245780, 472276693, 479090184, 489830098, 497442453, 506066131, 512644808, 523384338, 530996757, 540005910, 546592457, 556938898, 564786259, 571758217, 582096004, 590337686, 1076963271, 596923913, 607261700, 615503446, 622482955, 630085192, 640816196, 649058006, 656037451, 664032841, 674370756, 681047767, 1076195270, 1076723721, 689591947, 697194120, 1073858506, 705828440, 714602007, 1074139144, 722605720, 731379351, 739382808, 748156503, 756160216, 1074947020, 765081177, 773478091, 781858521, 1076007947, 790247065, 798635545, 1075236814, 1074733005, 1075804111],
    [110, 96, 2, 109, 86, 298176, 8729601, 18920512, 27309056, 35697856, 44086400, 52876880, 59018304, 67449985, 75806290, 86431376, 92572672, 103487121, 109491860, 117888148, 126127232, 137041489, 143046228, 151442516, 162442305, 170596049, 176600788, 184997076, 195996801, 204543555, 210155028, 218551316, 229674711, 238097923, 243840516, 251967186, 262592208, 271617623, 277165249, 285521554, 296146448, 305172119, 313595587, 1073750978, 319075858, 330224770, 338603201, 347149955, 1075865603, 353285637, 363779074, 372280855, 381097024, 386840197, 397333570, 405711873, 413865489, 420394565, 430888130, 439791192, 448205952, 453949125, 462739029, 473476627, 481900182, 1076402181, 488035410, 498642643, 507065878, 513070741, 523677208, 532231766, 538236629, 548843224, 557397718, 563532818, 574139987, 579155009, 588698834, 599174808, 607589568, 1075371974, 614266393, 624366592, 632860307, 1075648455, 639432281, 647828503, 656321553, 664598233, 672994519, 681487569, 688436868, 1075146698, 697750674, 706548823, 715041873, 721991236, 731707033, 740103319, 748596369, 755545796, 764728853, 1076726788, 1074656201, 1077023692, 1074938824, 1073919947, 773764623, 782153295, 1077331918, 1074210765, 790542031, 798930575, 1076316175],
    [114, 100, 0, 113, 90, 2281601, 10523712, 18912256, 27300992, 35689664, 44209281, 52597761, 60986433, 69390529, 77763777, 84186833, 94818513, 102931986, 111023122, 117741201, 128372881, 137008659, 144875218, 152966354, 159684113, 170315793, 178951891, 186818194, 194909330, 203608065, 212506259, 220917779, 229283411, 235181649, 245813329, 1073748931, 254817813, 262708245, 271249491, 279983765, 287874197, 296415379, 304651861, 312350290, 321048641, 1075334082, 330315477, 338205909, 344757894, 353554966, 363869269, 371366994, 378720854, 386274438, 395099863, 403478022, 412275350, 422745689, 431240281, 437042839, 445421254, 455798995, 1074303943, 464688857, 473183449, 479384278, 489854617, 498349209, 506778256, 515020313, 523514905, 529710669, 537695814, 548721168, 1074844678, 554997466, 562435270, 571915482, 582275664, 588551770, 1075127237, 596383241, 605469786, 616100564, 622106138, 630339272, 639024154, 649654868, 1075924873, 655660698, 1074639818, 663893512, 672578714, 683209236, 1077009800, 689058888, 697482893, 708375188, 1075720142, 713823433, 722255447, 733270736, 738989129, 747814605, 757002776, 763761734, 772980237, 1076774852, 782168792, 1074177037, 789722248, 797752855, 807334488, 814486665, 824111768, 1076292556, 1076574155, 830870534, 1077363663],
    [110, 96, 8, 109, 86, 349376, 10284225, 18936832, 27325504, 35714176, 44102848, 52867728, 59339841, 69004417, 75822594, 86422224, 94459473, 103345233, 111587856, 119625425, 128511185, 136753744, 145288721, 153179793, 162042386, 170708176, 178869891, 185136708, 195859029, 204393540, 212424259, 218691268, 229151442, 237948100, 245978819, 252245636, 262967829, 271502468, 279533059, 1073745923, 285799940, 296260242, 305056772, 312562705, 1074808836, 321688213, 330091600, 338515604, 344782360, 354980434, 363811864, 371780753, 378336920, 388797141, 397366424, 405589136, 411891288, 420786774, 430920792, 439143440, 445445848, 454341142, 464475352, 471657537, 478475842, 487895766, 497899092, 505211905, 515176089, 523538585, 528807554, 540331603, 548230868, 1074307017, 557119065, 565481561, 570750658, 582274579, 590173716, 1075632130, 599062041, 607424537, 1075386311, 613897875, 624217235, 632616665, 640979161, 1075136456, 647451731, 657772243, 664179351, 672617491, 680979477, 689345239, 696603776, 706145429, 714510935, 722949331, 731311317, 739676695, 746935360, 756477013, 764719766, 1074106316, 772371649, 1074643915, 780760065, 1073885125, 1076786125, 788878336, 1077061578, 797537409, 1076295622, 1077357519, 1076585422],
    [118, 104, 3, 117, 94, 2151552, 10540032, 18928704, 27317440, 35836929, 44225601, 52860432, 61135888, 69628944, 77780161, 86168705, 94926417, 103192272, 111467728, 120116867, 128480785, 136633936, 145527939, 153802387, 162035409, 170300496, 178577040, 187225795, 195745363, 201916049, 212366481, 221025859, 229168195, 237688339, 243858449, 254178384, 262575248, 271242963, 277413073, 287732880, 296522947, 305051282, 311229973, 321680595, 330217170, 336133201, 346846355, 354997763, 361561813, 371619024, 380408835, 1073742788, 1073764355, 386848471, 395359447, 403504789, 413955091, 420533912, 429053511, 437433496, 447894599, 453836373, 462345815, 1075356613, 470996679, 479245399, 489837767, 496031320, 504550919, 512930904, 523392007, 529849945, 537843351, 546494087, 556946567, 563786841, 1075900358, 1076696071, 571792921, 579917336, 588428312, 598504531, 605347545, 613340695, 621851671, 630617622, 638779034, 647026392, 655537368, 664172118, 1075139522, 672456345, 680572055, 689338006, 1074899912, 697499226, 706270860, 716461196, 723170457, 731053786, 739825164, 750015500, 758036050, 1076491209, 764608026, 773379660, 783569996, 790279385, 798545612, 808735948, 815445017, 1077019660, 1074154442, 825144850, 831944406, 840865300, 1074438094, 1075767243, 849253972, 857642708, 1076312013, 866031252, 1077366735],
    [130, 116, 13, 129, 106, 2462720, 10564800, 18953280, 27341824, 35730560, 44250177, 52638721, 60913360, 69416129, 77960256, 86193281, 92606034, 103232594, 111244816, 119903424, 126160402, 136786962, 144799376, 153982609, 162084371, 168244756, 176492178, 187118738, 195130960, 201930389, 212702801, 220804691, 226965076, 235212498, 245839058, 252531732, 260650581, 271423185, 279525011, 287903319, 294205141, 302863444, 313366033, 319239892, 330378323, 336688213, 346395776, 355675736, 361854165, 370259137, 380841496, 387019925, 395424769, 405875859, 411915476, 420590721, 428291732, 439561944, 445469844, 454145089, 464727704, 470759003, 479286363, 489796690, 1073747909, 496056029, 506007255, 512308757, 521237525, 531739666, 539571923, 546387549, 556338839, 563033755, 573789919, 580072671, 590460114, 1075078086, 596719133, 606670359, 613627487, 624120927, 632403090, 638662301, 649145555, 655570463, 666063903, 672110300, 681260617, 691088403, 697390235, 706459353, 714814985, 722800158, 731206749, 740013657, 748369545, 756485786, 764622495, 775115935, 781956761, 1075876807, 790312649, 798559894, 806303451, 815092957, 823105052, 1074846729, 1075646410, 1074617282, 831852254, 839857691, 848647325, 856659548, 865406622, 873551067, 881825436, 890834518, 898978845, 907785753, 916000470, 923882523, 1075413956, 1073859528, 1074408396, 932646426, 1076512717, 1074177998, 941035226, 949423706, 957943318, 966069854, 1076294607, 1077096395, 1076852675],
    [134, 120, 13, 133, 110, 1916097, 10556608, 18945024, 27333760, 35722304, 44241921, 52630721, 61019265, 69287632, 77796417, 84374018, 92607490, 102579201, 111720019, 117928578, 126162050, 136396304, 145274387, 153173648, 162338517, 168334868, 178076801, 187504213, 195606163, 202207958, 210441430, 220282448, 229160659, 237990616, 246748761, 252515544, 261962817, 271365209, 277705366, 288691737, 294327446, 304946834, 313308185, 319255234, 330634969, 336270934, 344265922, 355278546, 363640025, 372208152, 380966553, 386733080, 397221394, 405607957, 413971609, 420311574, 428545046, 439164498, 447551125, 456307798, 464482968, 470619288, 1073749955, 481509073, 489862358, 498037336, 504173656, 515063313, 523416726, 529363030, 540229201, 1075600324, 548582422, 555053724, 563025052, 573783697, 579933706, 590657242, 596857547, 605361355, 613357084, 622017557, 632600154, 638800459, 647304267, 655300188, 1075351496, 663960661, 674543130, 680882268, 689247883, 697243356, 705903765, 714151626, 724874906, 731074699, 739579403, 746919490, 756235477, 1074578443, 1074073602, 763926164, 773280477, 781784285, 790314519, 1074881481, 798037578, 805869140, 815223453, 823727261, 1075943373, 832257751, 839423700, 849301706, 857282141, 865812119, 1075170247, 873535114, 882677467, 890720349, 899225117, 1074407374, 907755095, 1076248586, 916231771, 924274717, 933008923, 941576266, 1073916876, 949786267, 957706268, 966742026, 973566018, 1076555718, 982732811, 1076835269, 991260892, 1000296586, 1077114831],
    [122, 108, 6, 121, 98, 390208, 10056705, 18445505, 26833985, 35222657, 43742336, 52131008, 60519488, 67499200, 77296640, 86053518, 92763842, 102986894, 109442048, 119607886, 126580228, 136541262, 142996608, 153432656, 160265296, 170096142, 176912004, 185063116, 195104782, 204033746, 210597584, 220689618, 227243588, 235394636, 245853841, 254096016, 260928656, 271021650, 277575364, 285726348, 1073754116, 294614534, 304959059, 312815824, 321353234, 327669260, 336557638, 347164308, 355406357, 361494157, 372330068, 380572373, 386659917, 397496020, 405239442, 411825677, 422661652, 430256656, 437089296, 445380301, 453998278, 464342675, 472846933, 479056897, 487552646, 497896979, 506401429, 514029262, 521393743, 1076909062, 530649294, 539840211, 546559503, 554635864, 564621009, 571331777, 579801624, 589786705, 596497473, 1075090375, 604967576, 614952465, 622057167, 630403801, 640240786, 647198409, 655217793, 663687896, 673795154, 680752649, 689165967, 697512473, 707349522, 714438283, 722695753, 731501778, 739455641, 748506775, 756381259, 764638857, 773444690, 1074842633, 1074604041, 781398617, 790449879, 798324235, 806999186, 1076453315, 815615511, 822572674, 832164882, 840781399, 848656075, 1075677195, 1074392075, 857697942, 864515650, 1076758474, 1074159626, 874475222, 1076003784, 1073931272, 882863702, 891252246, 898070018, 1076311042, 1077369797],
    [118, 104, 11, 117, 94, 2317377, 10048576, 18437248, 26825920, 35214336, 43734209, 52122753, 60511233, 67862220, 77288513, 86447630, 92755650, 101416524, 111105744, 120125073, 128390734, 134960708, 143219920, 153048592, 162068049, 170333838, 176914060, 186603152, 195622417, 204420623, 210468364, 220157520, 229430995, 238229138, 243883088, 254596691, 263395026, 268916290, 277437456, 1073745861, 288151059, 296695375, 302603408, 311383624, 321844948, 330503762, 336025090, 346250433, 353326792, 363804367, 372307605, 378633408, 386881160, 398005958, 405730900, 412187648, 422639189, 430380750, 438524929, 1074551238, 1075360774, 447674004, 456078991, 463690881, 472970773, 479540760, 487685184, 1077208007, 495932936, 506394132, 515053074, 521239680, 1075913736, 531691221, 540611654, 548503129, 555038424, 564721361, 573668889, 580449947, 590943238, 598834905, 605615643, 613758552, 622288461, 630781531, 641275014, 649166489, 655947483, 664090264, 671569538, 681008653, 1076188162, 1075161090, 689911382, 699192979, 706305756, 1076479945, 715060762, 723457687, 731471388, 740226778, 748623383, 756637340, 765392538, 773797526, 781803100, 1074136010, 1073897419, 1075752971, 790558298, 798955095, 806049476, 815226509, 824121047, 831215108, 840392397, 849294870, 857683670, 864769668, 1077070787, 1074466820, 1075014660],
    [126, 112, 0, 125, 102, 1840192, 10597568, 18985984, 27374720, 35763264, 44282881, 52671617, 61069008, 69448897, 77337600, 86225985, 92648978, 103143059, 109556883, 119813138, 126203474, 136697427, 143111251, 153367634, 162508372, 168146642, 178640403, 185054227, 195310802, 204451540, 210351765, 219002518, 228972243, 235386067, 245503505, 254774421, 260683477, 269334102, 279172688, 287446673, 296726036, 302626389, 311277270, 321115664, 329389649, 338669204, 344569365, 353220118, 363058832, 370939008, 380866263, 386905303, 394638994, 403297366, 413414546, 422546645, 428848663, 436851862, 447616600, 456100949, 462665370, 470406358, 481170968, 1073753027, 489918103, 495957143, 504608282, 512349206, 521934016, 531860503, 538162906, 546296914, 556668568, 565152789, 571717210, 579851410, 590223064, 1076386757, 598969943, 605008983, 613799002, 1075351490, 622991057, 633056795, 638964890, 646452353, 658222747, 665966278, 671618049, 683388507, 691131910, 696784065, 708554459, 716297862, 721949761, 733851164, 741463622, 747640477, 1074585606, 759017116, 765187157, 773067860, 784183004, 789959706, 797972189, 1075907528, 809348700, 815518933, 823399636, 1074356169, 834375385, 840684693, 848303645, 1075680199, 859541145, 865457370, 873469533, 884706841, 891016213, 898897044, 909872729, 915395602, 924062740, 1074911178, 1075185614, 932173010, 1074164683, 1077065676, 1077342159, 1076832196, 1076315085],
    [114, 100, 9, 113, 90, 2202817, 10604737, 18977984, 27366400, 35755136, 44143680, 52663297, 61052097, 69440641, 77722128, 86088833, 94606401, 102888016, 111254529, 120272594, 128053968, 136420417, 145438290, 153219728, 162241728, 168367699, 179018752, 186765377, 193304197, 201922259, 210212372, 220576788, 229241553, 1073750979, 235476627, 246127744, 254407249, 263534101, 268932820, 279297236, 287428609, 296433170, 302487188, 312851604, 321516049, 1075863492, 1075616710, 329987730, 336303816, 344430164, 354794580, 362926209, 1075366850, 369464837, 381105878, 386635272, 397261829, 405402257, 414529237, 420189832, 430816389, 439865480, 444962501, 456472149, 462132808, 472620096, 481808584, 1074335752, 486905413, 498415253, 506313925, 515362824, 1074873349, 523712086, 531479621, 540528712, 1074106313, 548877974, 1074656199, 556921367, 563453137, 574043670, 580361296, 590991494, 597505561, 605132299, 615641751, 622173265, 631060121, 638817996, 647075467, 657584727, 664116369, 673003097, 680760908, 689018571, 697801936, 708431878, 714946265, 722703884, 730961483, 741470935, 748002321, 1077018635, 755570195, 764647052, 773299216, 783929542, 1073894412, 790076560, 800706630, 807260760, 815649304, 1075228621, 824038040, 832426712, 1076819914, 1077357518, 1076586447],
    [110, 96, 0, 109, 86, 291840, 10603712, 18478273, 26866689, 35255425, 43643969, 52163648, 60552192, 68940928, 75789440, 86101120, 94106816, 103518864, 111266816, 117732416, 128684624, 136432704, 142898368, 151499410, 161868801, 168326735, 176665170, 1073754112, 187034817, 193492495, 201830930, 210237123, 220589121, 227047055, 235385554, 243791427, 254143617, 260601551, 269201939, 277345923, 1076918210, 288388163, 296611409, 302642900, 311145171, 319288835, 330331139, 338554385, 344585748, 1077189635, 353088147, 363885699, 372109009, 378140308, 386642515, 397440195, 405663377, 413897424, 419942037, 428897281, 436860500, 448238212, 453496533, 462451905, 473404100, 479065606, 487748817, 498331158, 1075630276, 1074865093, 506957892, 512882249, 521303185, 531885654, 540512260, 546436617, 554159701, 563246097, 573280784, 579729094, 588280897, 598994582, 604894790, 612879893, 621966417, 1075932104, 631083736, 638711497, 647001217, 657714902, 664637976, 672003718, 681045655, 689599572, 1076467718, 698192536, 705820297, 714600151, 723154068, 1075431433, 731746904, 740062338, 748154455, 756542999, 765097172, 773616834, 782005250, 1074409420, 790393922, 1076776910, 798651412, 1074694090, 1074194379, 1076303821, 1075266503],
    [102, 88, 9, 101, 78, 1922176, 9698369, 18863105, 27251905, 35640449, 44028993, 52253760, 60030081, 69834306, 77419520, 85195777, 95000258, 102979217, 110361793, 118208146, 128407120, 136175308, 1073752064, 145331714, 1076391937, 153573008, 161340940, 1076922626, 1074318338, 170497154, 178738704, 186506828, 196056782, 203904720, 211672716, 221222414, 228808273, 237370496, 244037138, 253974225, 262536192, 271554190, 277599955, 287528465, 296090688, 1074599875, 302757586, 311154195, 321256640, 329077952, 336311890, 344708755, 355563023, 363331277, 372217422, 378263123, 389248083, 396885517, 1075141573, 1075420165, 406557893, 412210837, 1075705796, 422802451, 430440013, 440112261, 445765205, 456226511, 463994509, 473666629, 479319765, 489911507, 498832389, 504485397, 514946639, 521508374, 531496586, 540243091, 546804817, 556662282, 565278351, 573439690, 580621972, 590968021, 597005910, 606993994, 616133653, 1077285830, 1074946058, 622302353, 631101131, 641299605, 1076003784, 647468049, 656266763, 666465365, 672503510, 681432715, 689280662, 698209867, 1073923083, 706188497, 1074212809, 714839572, 723228244, 731616980, 1076848583],
    [114, 100, 1, 113, 90, 2381824, 8689792, 18757824, 27146368, 35534912, 43923456, 52443137, 60831873, 69220545, 77879360, 84580876, 94386241, 103166541, 109328962, 119822464, 126270093, 136720909, 143014595, 153376960, 159824589, 170275021, 176847564, 185252367, 1073750016, 195702799, 1075865601, 202012684, 210418319, 220868751, 227179148, 235584079, 246034511, 252098637, 260733516, 271200975, 1076406212, 277264397, 286160961, 296104077, 302938113, 311081167, 319427280, 327432706, 336492673, 344627404, 352981648, 361118339, 370448388, 378435777, 386536016, 395614276, 403724933, 411701776, 420780228, 428890821, 436484738, 445290636, 454187662, 1076164552, 462445061, 470063296, 479607378, 488151122, 496392785, 504773266, 512915602, 521968211, 529666644, 537279043, 546871442, 554851022, 563221140, 572275273, 1077226629, 579885125, 587503680, 596775444, 604387843, 613833425, 622631635, 1076714439, 630330068, 638991058, 1075415043, 646200002, 655923410, 663910610, 672545298, 1074383874, 1074672582, 681089042, 689076306, 698104329, 706517523, 714234382, 722770052, 731273873, 739643925, 748436169, 755669068, 764566094, 773198549, 781990537, 789994001, 797218816, 1077042185, 806752853, 814905362, 823958163, 831918741, 1075745739, 1074975755, 1075250122, 1073955850],
    [90, 76, 7, 89, 66, 1939520, 9707521, 18356289, 26744833, 35264576, 43522241, 51910785, 60430528, 68818944, 77079247, 85825536, 93984896, 103186129, 110625491, 119380096, 128351761, 135922196, 144545984, 153517649, 161088084, 170105554, 1073750017, 178683537, 186122899, 195533397, 202900051, 212048530, 219045462, 228197012, 237476565, 244342406, 253362900, 262642325, 269359623, 278397459, 287808021, 295853783, 303571471, 312711698, 319822488, 1075868612, 330464408, 337125967, 346266194, 353376984, 364018904, 370417793, 378542616, 389184536, 397261465, 403577479, 412360769, 420485720, 431127640, 439204377, 445915329, 455237207, 464370265, 470686407, 479732367, 488791703, 497924825, 505946768, 512646806, 522724048, 1076934342, 530079436, 539501136, 547511831, 554572359, 564666896, 1077202951, 572022348, 579886278, 1074856899, 588144150, 1073825730, 1074113481, 597188108, 1076488139, 1076239306, 605576844, 1075473420, 613440582, 1076792261, 621698774, 1074450376, 630217734, 1074730958, 1075273677],
    [118, 104, 8, 117, 94, 2291712, 10645568, 18905281, 27293825, 35682369, 44070913, 52588672, 59169488, 67402258, 78270482, 84335120, 94387780, 100956754, 109476563, 117995588, 128602194, 134666896, 144981203, 151288466, 159939268, 168196627, 178933906, 185260561, 195312659, 201620178, 210270724, 218528403, 229265618, 235592273, 245644435, 252213892, 260471379, 270692544, 277535377, 1073743876, 287587411, 294418965, 304246784, 312670272, 320879620, 329447616, 336359632, 346045572, 354613376, 361525840, 371211460, 378305109, 386324560, 395079824, 404888597, 411753169, 420245520, 430054485, 437025429, 445446679, 456413908, 1074295747, 463609557, 470579413, 479263320, 489968148, 497163413, 504396424, 512555735, 523522708, 1076927430, 529415766, 537950920, 546110103, 557077076, 563232474, 572185179, 580284433, 588529305, 596670984, 605739675, 613838993, 622083673, 630258200, 639004881, 1075365829, 647249625, 656044637, 664459803, 1074070466, 1073829834, 672022230, 681210589, 688978648, 697581081, 705722952, 713882199, 723415580, 1075158024, 731004442, 739932878, 748346075, 756445265, 1075696583, 764559002, 773487118, 781253272, 790524572, 798113370, 807041678, 815428125, 823017110, 832207438, 840856284, 1074924558, 848182806, 1074689997, 857633372, 865759901, 1077324745, 1076555723, 1076832207, 1076323276],
    [114, 100, 8, 113, 90, 2119809, 10508481, 19027968, 27416704, 35674113, 44062785, 52304592, 60971072, 69359808, 75782674, 85858832, 92691025, 102777346, 111024784, 119798355, 127943234, 136190544, 144964307, 153371156, 162281553, 170514965, 178274946, 187194053, 193607698, 204200598, 1073744386, 212484293, 220748293, 229374679, 1074283460, 1073785795, 237649925, 244333208, 254302853, 260463249, 269113496, 279697942, 287981701, 296499345, 304634437, 310794961, 319052498, 330029654, 1076418565, 338313285, 346831057, 353131079, 361650778, 371841685, 380788807, 387201690, 395074055, 403593370, 411458065, 422304470, 431120391, 439105553, 445405831, 453925594, 464116437, 473063559, 479475930, 487348935, 495213202, 506714715, 1075384327, 515006663, 521418842, 531880603, 1074885574, 538984642, 546322968, 554326040, 564918935, 571759196, 582509273, 588920924, 596269784, 606861911, 613702172, 624452249, 630863900, 638212696, 648280723, 655645404, 666395225, 671758930, 679762002, 690608725, 697588380, 708338201, 714750108, 723778067, 732185236, 739260504, 749984475, 757350996, 764688922, 772691994, 783538715, 790905556, 797587666, 808188439, 1076991944, 814364818, 823146712, 832190684, 1075169229, 1074145228, 1076260814, 1076793295, 1074716617, 1075787723, 1077371850],
    [106, 92, 11, 105, 82, 325632, 8722496, 17076416, 27310145, 35698689, 44087425, 52476097, 60995712, 69384256, 77772992, 84211904, 94671504, 101128912, 111327232, 117897345, 126294544, 136614480, 142932032, 153391120, 159848592, 170310292, 176617473, 185014352, 195334352, 203864660, 212504660, 218831441, 226949185, 237419028, 243595392, 252385809, 263098967, 270973652, 277551761, 285669569, 296653335, 304779284, 313580054, 319494865, 328276690, 338746006, 346985175, 355111124, 361962072, 372300502, 380688982, 386209984, 397316759, 1073744838, 405442708, 414374418, 420551250, 1074289607, 428152832, 439670928, 447910617, 456317138, 461707392, 473076377, 479402520, 490002448, 498242073, 1075351496, 506648658, 512826002, 523407961, 529602578, 540203154, 545558592, 554900184, 562335872, 573888592, 580721371, 587501568, 599054544, 605747930, 613620376, 622366785, 1074588611, 631175893, 639441563, 647532545, 656341653, 664309953, 672856730, 681480915, 689773083, 698022490, 706646675, 1076434892, 714938971, 723188250, 731418753, 1075143620, 740227669, 748589651, 1075939274, 1074132941, 757004821, 765366803, 1077288911, 1075729349, 1074964425, 1076294603, 1077085122, 1073967054],
    [98, 84, 7, 97, 74, 2138240, 10762432, 18913409, 27302081, 35690561, 44079105, 52598784, 60987584, 69376064, 77871168, 86024384, 94541952, 103430737, 111190016, 119578688, 128202880, 136764930, 143432323, 153368576, 161915472, 170327762, 176986819, 186810563, 195705553, 203882066, 210672133, 220871313, 229015557, 237436562, 244226693, 254425617, 262570117, 271121990, 277912199, 286169669, 295705299, 304251011, 313195655, 319855303, 327981635, 337648275, 346193987, 355138759, 361536003, 371202643, 379748355, 1073741827, 1073768262, 388561926, 395221701, 404757011, 413565125, 1076137989, 421977666, 428907079, 439001812, 447143618, 455516880, 463920770, 470850055, 1074841602, 480673861, 1074332679, 489356359, 497721940, 506133511, 514333271, 1074092996, 522625552, 531562005, 539499159, 548053524, 556727957, 564664855, 572957328, 581500102, 589830871, 598385300, 607059541, 615054470, 623836885, 631701010, 639539919, 1075425227, 647691990, 656317007, 1076754378, 664469078, 673094159, 681246230, 689871503, 1077285903, 698023574, 1075211214, 1076536264, 1076032460, 1077088201, 1074749389],
    [118, 104, 13, 117, 94, 1883136, 10844225, 18937920, 27326464, 35715264, 44103808, 52214912, 61175809, 69532370, 77642962, 86341761, 92729939, 103348931, 111475282, 119848131, 128284865, 136901140, 145291779, 153418386, 161790979, 170490384, 176616147, 187234947, 195361298, 203734147, 212433616, 218559123, 227211781, 237812741, 245987984, 252113427, 260766277, 271367237, 279542352, 288158357, 294320773, 304921733, 313358464, 321450708, 329301138, 338524224, 346616404, 354466898, 361716248, 1073748932, 371782292, 379632658, 386882200, 397605385, 405598741, 413727299, 420436696, 430226499, 1075332034, 1073778691, 439548553, 447541973, 453704389, 462379608, 472693957, 1074841605, 1074344903, 481491529, 489484885, 496811200, 504715985, 515043401, 521337498, 530365504, 539850944, 548589722, 556710983, 565016576, 573763593, 580057626, 590265543, 596990481, 607320777, 615698458, 623819783, 630545041, 1076970505, 640872649, 648985735, 655710801, 1074108363, 666038409, 672332378, 1075171276, 682933785, 691099730, 699584602, 705886938, 1074668488, 716480214, 724654226, 733139162, 740096590, 1075997642, 750042777, 758208530, 765383191, 773651150, 783597273, 791763154, 798937687, 807205518, 817143318, 1076539341, 824103639, 832371214, 842309270, 1076812814, 849269399, 859086422, 867483225, 1075783631, 1076328390],
    [130, 116, 10, 129, 106, 2154625, 10541121, 18929665, 27318465, 35707009, 44226624, 52615168, 61003968, 69263425, 77781120, 84195857, 92592145, 102810114, 111198914, 120224275, 128636947, 134789844, 143186563, 153149441, 162297987, 170580563, 176732692, 186696258, 195721299, 204135059, 210287252, 221043414, 227072515, 237035713, 246183939, 254466771, 263231702, 271374934, 277404227, 288284800, 296515651, 305060439, 313563222, 321706646, 329302658, 1073743874, 338327699, 347117718, 352639569, 363649558, 369679043, 380559360, 1074286595, 388790467, 397335255, 402962513, 411359953, 422502464, 430602451, 439278231, 444905681, 453302929, 464445632, 473331799, 481221143, 486848657, 498262102, 506886295, 514889750, 523427990, 532052183, 537442900, 546757211, 1074836420, 556982294, 1076937669, 565606423, 572054151, 580041241, 588700379, 598925526, 607672917, 613997255, 622377498, 632611344, 641358407, 647551047, 655932058, 664197787, 674554576, 683301063, 689617051, 697752091, 708108880, 716724757, 723048967, 731429594, 741663376, 1073808391, 750279381, 756857368, 764985948, 775445141, 782023320, 789897746, 800741383, 806533785, 815317660, 1074093001, 825907335, 832223451, 840229458, 1075417030, 849246749, 857520728, 865395346, 874412765, 882686680, 890815004, 1074655180, 1076766664, 899578461, 907197017, 915981020, 1076254670, 924744349, 932886555, 940892882, 1075230667, 1077338061, 949533274, 957528793, 1075782607, 966441051, 1076063178],
    [114, 100, 12, 113, 90, 489472, 8886464, 18558977, 27342976, 35731520, 44120064, 52508864, 60502209, 67615312, 76118672, 84646417, 94056577, 101284560, 109812305, 119222337, 126450192, 134978193, 143226960, 153555152, 159873216, 168532689, 178720912, 185038912, 195795524, 203886608, 1073746883, 210188869, 218593408, 229349892, 237441104, 244005396, 252131845, 1074813700, 263262403, 271423508, 277567617, 285686405, 296947904, 304847044, 311121921, 319503060, 328153749, 336018117, 347279488, 355309780, 361453633, 1075349509, 369834644, 380702787, 388733060, 395008193, 403389012, 412039701, 420575827, 431034371, 439195732, 445725334, 453982933, 462641365, 472881302, 481497088, 487668310, 496195733, 506662976, 514693268, 521091669, 530020887, 539990102, 548475011, 554766866, 563575511, 570931408, 1074316226, 579932882, 588741207, 596097168, 605371084, 613487186, 622295703, 629651472, 638663382, 647445133, 655430290, 663967829, 674207958, 1073819592, 680606230, 689388045, 698309336, 707762198, 714422796, 722565779, 730306624, 739588748, 748640920, 755472512, 1076718535, 1076475849, 764885709, 773806616, 780638208, 789920332, 798063123, 1077267468, 806828621, 814840531, 1074661322, 1074158605, 824138328, 1075749835, 831739925, 1076029390, 1076303814, 1075278799],
    [106, 92, 3, 105, 82, 2302144, 10557505, 18946177, 27334849, 35723265, 44243072, 52631552, 61250192, 69408832, 77799552, 86186176, 94338642, 103094929, 111712401, 119742528, 128024147, 136649297, 145266769, 153296896, 159980098, 169836050, 178592273, 187209745, 195887700, 201923074, 211910291, 220535505, 229152977, 235479058, 243866242, 253853395, 261012117, 269025491, 277420738, 287276690, 294566613, 302588050, 1073745922, 312442578, 321435650, 327745683, 338263686, 346601666, 353567319, 363429574, 370063957, 378348118, 388595270, 396933250, 403243091, 1074807747, 413761030, 420395541, 428679702, 1073785862, 438402579, 447264834, 1076681669, 453574675, 462249047, 472823894, 481100500, 487415511, 497990294, 504561879, 512982681, 523155478, 1075388359, 529080530, 538140186, 548322006, 556597780, 563306202, 572955216, 581763732, 588471962, 598121168, 605495449, 613637722, 623286800, 629743698, 1075667908, 638811737, 647936728, 1075940296, 655827033, 663576087, 673102424, 680337622, 689143513, 698268184, 706159129, 713907863, 723434136, 731054103, 1074392009, 739474457, 747446422, 1076496330, 1074165708, 756220055, 1077319627, 764879065, 1075246030, 1077094351, 1076318157],
    [102, 88, 5, 101, 78, 2169856, 10352641, 18970688, 27359424, 35878913, 44267649, 52525056, 60913792, 69433537, 77667392, 85850177, 94599233, 102833344, 111016065, 119610496, 126474896, 137196115, 145178130, 152959169, 162362003, 168377491, 176806416, 187527699, 193543187, 201972432, 212693715, 218709203, 227138128, 238252564, 245841618, 252828241, 263279300, 1073755075, 271007314, 277994129, 288445060, 294615685, 304561810, 311548625, 1076908228, 322138708, 328169989, 336149587, 345102865, 355553348, 361724485, 372317703, 380762112, 389247636, 395279045, 405872263, 414316608, 1074829317, 422662148, 431038151, 439482496, 447967956, 454261448, 464592455, 473036992, 1075375111, 481776149, 487815816, 496335562, 506666186, 515330645, 521370184, 529866455, 540496597, 546535944, 555032215, 1076694024, 565924438, 571832842, 582163466, 1074611142, 590828181, 597391884, 605387402, 615718026, 624644758, 630553162, 640883786, 1073842186, 649810454, 656112268, 666229336, 672472663, 683365078, 689666764, 699783832, 706027031, 714832460, 724949528, 1074387980, 733338328, 1075722178, 1077299149, 1074179022, 1076553679, 1076306891, 1076058057],
    [118, 104, 11, 117, 94, 2048193, 10574017, 18962561, 27351041, 35739713, 44259456, 52648000, 61036736, 69558992, 77813760, 86563331, 92617298, 103110659, 111362641, 117783058, 128645764, 136790148, 142949010, 153811652, 159865555, 170344644, 176503506, 187365892, 193419923, 203898884, 212408852, 220920388, 227104788, 235362899, 245841988, 1073747972, 254752851, 262724291, 269048532, 279271619, 285694483, 295649281, 304683220, 313055811, 319380116, 329603139, 337994256, 346626196, 354998915, 361323092, 371546243, 379798225, 1075333123, 388569172, 395500053, 403528342, 413089921, 1074310085, 422385814, 429054613, 437082710, 446906897, 455940182, 462608981, 472212112, 1076426694, 481245395, 487520919, 497377872, 1077228482, 506673282, 512686807, 522141761, 1076974535, 531839170, 537852503, 547570321, 557004802, 563272405, 573784147, 581769942, 588077270, 596572695, 607469637, 615324182, 621631510, 633010776, 641024005, 649279554, 658176728, 664492633, 1074890697, 674578565, 682571795, 691731096, 698047001, 708001939, 1074128843, 716126355, 725285400, 733298885, 739981337, 748378841, 758333459, 1076233162, 765147353, 775110867, 782179034, 790323392, 798956186, 807099033, 1073895373, 815489024, 823867545, 832266368, 840899162, 849043520, 1075224526, 1075761096, 857676314, 865810521, 1074734031, 1076064204],
    [122, 108, 9, 117, 94, 268353, 8771649, 18462848, 26851328, 35240000, 43628736, 52148353, 60536897, 68925633, 75897548, 84269057, 94091265, 103387726, 109427330, 117971663, 126212225, 136942094, 142981634, 151526031, 161864205, 170496654, 176929285, 185080335, 195549189, 204051150, 210483781, 218634831, 229103685, 235639505, 244038277, 252459666, 262658181, 269324883, 277199426, 285981381, 296212677, 302922256, 1073743877, 1074293765, 311136913, 319805964, 327424001, 336433875, 344971852, 352721548, 1076665286, 361607701, 369900242, 377870529, 1075365831, 1074077703, 386904598, 396745293, 403585680, 411931283, 419805890, 430962690, 436476033, 1075926018, 445627080, 454013654, 463854221, 470694608, 479181320, 487567958, 495729234, 505797325, 512735880, 521255561, 529379989, 537672210, 546298060, 554809929, 562934357, 570824780, 579852428, 588878423, 598735042, 604912208, 613530121, 622432919, 630569611, 640678018, 646322188, 655342152, 663458385, 672512587, 682620994, 688134337, 1075158024, 697143827, 706067147, 714602496, 722737280, 730970825, 739095253, 748009995, 756931092, 764680256, 1075696580, 1074933769, 1077038091, 1074702347, 772510225, 781711488, 789846208, 798593559, 807262932, 815142989, 1076557770, 823759575, 832428628, 840308941, 848278166, 857594516, 865474701, 1077347267, 1073964035, 873986240, 882251789, 890509312, 899151936],
    [110, 96, 13, 107, 84, 622720, 10066112, 18585793, 26843200, 35362945, 43620352, 52140097, 60292748, 68786304, 76251660, 85694465, 93847116, 101548621, 111254030, 118069827, 127400972, 135102989, 143497732, 153557520, 160405520, 169597956, 179143247, 185440836, 195500688, 202348688, 211541060, 221086223, 227383940, 237443664, 244291664, 253484164, 263029455, 270637646, 277682705, 286785228, 296583823, 302881476, 313203346, 320593092, 327909580, 1073745924, 1074818052, 1076659141, 337746574, 346495696, 353343696, 361487438, 369852492, 379689678, 388700690, 395041998, 403538637, 413866706, 420207758, 428843022, 437590675, 445373454, 454132244, 464198226, 470802068, 478773248, 1073800130, 487922195, 495967252, 504070284, 512965270, 521133780, 529506510, 538384981, 546299476, 555065537, 563452489, 571685462, 579961044, 588585683, 596220611, 605126804, 1075912646, 1075671046, 613784265, 622017238, 629774979, 638419597, 647338505, 655825557, 663329283, 1076991943, 1075177479, 672112718, 1076503555, 680991253, 689012820, 697670281, 705903126, 713654336, 1076252616, 1074694090, 1074186249, 722803283, 731226241, 739711701, 747208896, 755833425, 764780545, 772610769, 781557825, 1074469835, 1075541003, 789387921, 797941902],
    [130, 116, 11, 129, 106, 2390016, 9026688, 18479105, 26867841, 35256513, 43644993, 52164800, 60553344, 68941888, 76135616, 84433487, 94107648, 101055042, 109599439, 120036880, 128055875, 134609410, 143153679, 153591376, 161610243, 168163970, 176708239, 187145872, 195164803, 201849362, 1073754112, 212204164, 221010513, 229481604, 237883923, 245866192, 254834819, 263049811, 270924292, 279214272, 288201732, 296604307, 304478916, 313367748, 322205776, 330551957, 338033220, 346922052, 355760272, 1076908036, 363713235, 370014727, 378534472, 386899016, 397703376, 1074825157, 406049301, 411957831, 420477576, 428842120, 438597760, 1074063302, 444988098, 456381013, 462420680, 472668817, 479173832, 1076172802, 487062098, 495833814, 504363528, 512728072, 523270147, 1075398664, 530709187, 540267221, 545897536, 556824771, 1074377731, 563214936, 570948242, 579728084, 587840512, 598767683, 605158104, 612891346, 621802073, 631535680, 638958674, 647101080, 655227591, 663605846, 673995281, 681032903, 1077268425, 689043992, 697170567, 705548950, 715938513, 722844818, 1074660298, 1073896455, 730714646, 739884034, 750024720, 756019865, 764787922, 773609688, 781054548, 789953554, 798775320, 806220436, 815250439, 823941272, 831517401, 840416327, 849107032, 857461338, 866015831, 874101826, 882627226, 891181719, 899267714, 1075746765, 907792922, 916347415, 924433602, 932958938, 941513431, 949468295, 1075241932, 1076046798, 957346329, 965603860, 1076588491],
    [110, 96, 3, 109, 86, 1564673, 10475648, 18864192, 27252928, 35641344, 44161089, 52549825, 60668428, 69326977, 77062337, 86104065, 94853711, 101300750, 110616705, 120019599, 126466638, 135782465, 145185295, 151632526, 161210960, 1073752064, 170351311, 1076391937, 178109004, 186376720, 195779140, 202103379, 210352846, 220192851, 227400404, 237852884, 244046355, 253606540, 262135827, 269343316, 279795796, 285989523, 295549644, 304078995, 311286292, 321738772, 327932627, 338279117, 346022099, 353229460, 363681940, 370399941, 380221965, 387703440, 397105796, 405387917, 413655237, 422271684, 430553677, 436978385, 447437316, 454285829, 462657683, 472375301, 1076925378, 1074848772, 481254102, 487840325, 496212051, 504748568, 514318405, 1076167623, 523197078, 529914456, 538163288, 547087056, 556751446, 563337861, 571709459, 580246168, 589815941, 1073824773, 598694422, 605412056, 613660888, 621920917, 1074109379, 1075436547, 630807065, 638826520, 646693457, 656243415, 663984339, 671859345, 1075720136, 1076778950, 681138841, 689158296, 697418453, 706304729, 714586770, 722190865, 731470425, 739752466, 747749973, 756906583, 764918482, 773683863, 781304341, 790084178, 798849559, 1075230666, 1077339081, 1076038603, 1074482187],
    [106, 92, 2, 102, 79, 2129088, 8666305, 17054785, 25443457, 33831937, 42351680, 50740224, 59128960, 69500425, 75906240, 85474827, 94666313, 101097036, 110902348, 119029323, 128220873, 135806667, 1073747969, 144998025, 1075339264, 153796173, 1075881985, 160972427, 168591050, 178962125, 186914510, 193609283, 202145290, 212516493, 218775043, 227311178, 237682189, 243941059, 252477066, 260718211, 270564416, 279451279, 1076419587, 1075653635, 285908496, 295730304, 302685776, 312507392, 1076711362, 320617996, 327588876, 338189968, 1074631621, 1074910213, 346297998, 354172620, 361406160, 371743760, 379852366, 387726988, 1075184580, 1073890308, 394697868, 405298256, 413669071, 419863756, 430464208, 438834767, 445816340, 454327889, 463738382, 470826631, 479510098, 487882449, 497554959, 504380999, 513326806, 521436689, 529143511, 537935367, 546881110, 555375691, 562960085, 571489991, 580173330, 588545681, 1074177031, 596252247, 605339346, 614095883, 621418135, 630767126, 639261835, 646583831, 655933078, 664427723, 672011861, 680697556, 688789013, 697474708, 705566357, 714251860, 1076294600, 1077097480, 723269203, 731168402, 740046547, 1077365702, 747281552, 756823571, 765212307],
    [94, 80, 9, 92, 69, 1186817, 9575617, 17964161, 26352705, 34872512, 43260992, 52700866, 60038144, 68426880, 78019139, 86255170, 1073746242, 94796483, 1074809155, 103031810, 111779343, 119961603, 126099140, 1074305025, 136586370, 1075372033, 143638096, 154040516, 159653380, 168304273, 178792146, 187276943, 195459203, 201989779, 210247377, 220734994, 229096595, 238188753, 243932755, 254289554, 262650963, 271743121, 277093956, 287835669, 296646724, 304594451, 311041043, 321390293, 330201092, 336576016, 344202884, 353115654, 1075905540, 363341394, 1074091973, 372144260, 380092115, 386538707, 394796561, 405276245, 414349329, 420462224, 428351057, 438830741, 447903825, 456113878, 465074765, 472890902, 481851917, 489668182, 498629325, 504348368, 515406477, 523222678, 529824468, 539598543, 546855566, 556375631, 563763788, 571767380, 1075154888, 580541068, 588929548, 1074654154, 597318348, 604773958, 613964302, 621551302, 630741582, 1076507593, 1077048329, 638328454, 1077325771, 647264788, 1076805638, 655653524, 1073946567, 1075799047, 664296142],
    [110, 96, 10, 109, 86, 283776, 10229953, 17071168, 25459712, 33848512, 42237056, 50756673, 59145409, 69140110, 75922561, 84309134, 94115905, 101088257, 111345231, 117864014, 127670401, 136511119, 143029774, 152836097, 1073747969, 161676815, 168565443, 176584398, 186580046, 193477188, 202011727, 212008655, 218387520, 227031748, 236911630, 243808900, 252343311, 1075335236, 262077646, 268850704, 277362692, 286407174, 294286543, 303070921, 312613065, 319452303, 328236553, 337778697, 344216576, 1074826118, 353435345, 361791113, 371333257, 377771200, 386956873, 396499017, 1074322441, 405724820, 412112530, 420624518, 1075642819, 430890516, 437278226, 445790278, 456056404, 462444114, 470554755, 481222356, 486954576, 1073825738, 496114261, 504430225, 512775890, 520886339, 529989331, 537286288, 546733782, 554440707, 1074115522, 1077015554, 563642060, 572413526, 580320915, 588676182, 596785350, 605967574, 613875283, 621943317, 630750796, 638647889, 646338256, 656047639, 664695831, 672202257, 680663765, 1077292997, 689372691, 697440917, 706248204, 715028183, 723156183, 1076783053, 731414156, 740185622, 748059670, 1076268044, 756971159, 765099159, 773740182, 781614230, 1074717639, 790525527, 798653527, 1076041672, 1075276747],
    [106, 92, 7, 105, 82, 1440769, 10247296, 18635968, 27024384, 35413056, 43932673, 52321345, 60300866, 69098689, 77200450, 85875841, 94398019, 101080784, 109592270, 1073744706, 118881409, 127813199, 1074287427, 134766098, 143146510, 152829457, 161768466, 168320594, 1074829313, 178667156, 186384017, 195322962, 201875154, 212221524, 219938385, 228877522, 235429522, 243809870, 253492945, 262431890, 269246150, 279330324, 286915778, 295585487, 302800390, 310918798, 320470146, 329139855, 336354886, 346439380, 354024450, 362694159, 369909382, 379067394, 388488726, 1075363846, 396387459, 403070544, 412622018, 422043222, 429941763, 436625040, 446176386, 454425665, 462708377, 471884995, 478567952, 489037464, 497540758, 504651481, 514475733, 522591960, 529923265, 1073813448, 538205721, 548029973, 554572953, 564649686, 571760217, 581584469, 588127321, 598473926, 606750357, 613293081, 623639622, 632047191, 638459097, 648805382, 657213079, 665198168, 673971334, 682378775, 690363928, 699399184, 707544791, 714489491, 724565200, 731266579, 741342352, 1075143626, 1075947465, 748043987, 758119504, 764821075, 1076229063, 1077031943, 1077299148, 1074180036, 1076816837, 1076563915, 1074749389],
    [106, 92, 9, 105, 82, 1899648, 10663104, 17087680, 25607297, 33995777, 42253440, 50641920, 59030592, 67550273, 77771904, 84336206, 92716225, 102973072, 111326208, 117890574, 128138832, 134648897, 143056526, 153304592, 1073747969, 159814657, 168222414, 178470608, 186823744, 193519311, 202063377, 211614720, 218535105, 227221202, 236780608, 243700865, 252395153, 260628047, 269136974, 277561041, 285793935, 294302926, 305217044, 310959631, 319723221, 330382996, 337444032, 344888917, 1075336132, 355548756, 361414230, 371907670, 378188814, 389103316, 397204994, 403609237, 412163795, 420134550, 429307479, 439016598, 445718099, 453689046, 464313986, 471250455, 479272595, 487243286, 496025287, 506125334, 512406670, 521215507, 529579655, 539811394, 546215445, 1074824131, 1073799682, 554384977, 563133959, 573365442, 579542674, 588299847, 598400214, 1075906567, 604708434, 613998296, 1074352072, 622499353, 629874194, 639286297, 647552536, 656053913, 664452249, 672718424, 680965847, 689643226, 697884312, 706385497, 714783833, 1074634700, 1075697606, 722908823, 1075185610, 731551449, 739974682, 748338393, 756752026, 765140570, 1074163657, 1076800461, 1076556747, 1077097483, 1077372869],
    [102, 88, 11, 101, 78, 1875137, 10263617, 18652289, 27040769, 35560448, 43949248, 52337728, 60726400, 69772814, 77478926, 86440463, 1073744834, 1074287555, 94938766, 102644878, 111606351, 119283408, 128383631, 136617168, 1074829313, 145524434, 153549519, 162301458, 170409556, 179239507, 185113684, 196147729, 204506709, 212352660, 218668180, 229410450, 237959891, 245906964, 252222484, 263357974, 271514259, 280135254, 288291347, 296238804, 302554324, 313850436, 322078358, 328998544, 337943696, 347142737, 354164304, 363890197, 371498064, 380959364, 387718672, 397444821, 405052432, 1075372612, 414513156, 422348370, 431028945, 439518934, 447806097, 455648974, 463355086, 470851143, 481622212, 489203278, 496909390, 504405639, 1075914693, 513211096, 523273877, 529571527, 540057175, 546866263, 555285081, 563125767, 573611735, 580427467, 1076184071, 588809751, 597228185, 607165463, 1074103240, 613981771, 622364311, 630651544, 640720023, 647536139, 655918295, 664336921, 672702091, 681114329, 689874458, 1073861643, 697760344, 706651802, 714537496, 723429082, 1075196876, 1077048332, 1077321673, 1075761101, 1074736070, 731817562, 1076588490],
    [98, 84, 10, 97, 74, 1932352, 10802369, 17103873, 25492545, 33881217, 42269889, 50789440, 59178176, 67566720, 77429888, 86299649, 92732416, 102595584, 111605391, 120232465, 127991314, 136150208, 145159759, 154049091, 161545938, 1073747969, 170221070, 178714127, 187603459, 195100242, 203775694, 212268751, 220528147, 229546627, 237043346, 245718670, 254071937, 1075335683, 263100611, 269156036, 279273038, 287626305, 296917188, 304700562, 313325072, 321559121, 330005523, 338491024, 346725009, 353041988, 363420882, 372045392, 380803140, 386596484, 396975122, 405599952, 414357636, 420150788, 428930580, 438918226, 1074825220, 447911940, 454226961, 464223827, 472185939, 480942801, 487781521, 497778387, 505740499, 1074316226, 513063509, 521205396, 531332755, 539294867, 546740758, 554759764, 563780247, 571537108, 580295318, 588444753, 596949653, 605222097, 613726741, 1073815495, 622515800, 630627030, 1075664842, 639293080, 647281365, 656070168, 664443479, 672847576, 681220631, 689609431, 1075152843, 1074128838, 1076241356, 697735766, 1075998664, 1076802501, 1077081093, 1077350349, 1074752457],
    [102, 88, 1, 101, 78, 2417664, 10525825, 18668608, 27057280, 35445760, 43834560, 52354241, 60742657, 69369346, 77519937, 86303936, 94411841, 102685825, 109371022, 119701122, 1073746562, 128370371, 136354817, 1074809283, 144866370, 153535491, 161520833, 1074305025, 170032322, 178701443, 187219537, 195853454, 203867203, 212385425, 220225042, 229295759, 237551121, 246072911, 254188672, 262962702, 268753934, 279241792, 287882961, 296517198, 302308430, 313181711, 321297600, 329959119, 338074688, 347111061, 354851840, 363127936, 372276949, 378461895, 1075375044, 388931156, 395363856, 403627591, 413957838, 419749070, 430874132, 437307024, 1076429765, 446717522, 454215318, 462331087, 1073836998, 1076999174, 471883474, 479381206, 487496847, 497049234, 504546902, 512662543, 523271765, 529712662, 537828431, 546233991, 556826133, 563519059, 571524816, 579788295, 588701207, 1077269511, 598907927, 605079120, 613867159, 624073879, 632200916, 639032919, 649239639, 657366676, 664198871, 1075191753, 674405591, 1075734474, 680959507, 1076274120, 689626829, 697736915, 1076031435, 706403917, 1076826060, 714514067, 723181069, 731569805, 1074742285],
    [110, 96, 9, 109, 86, 2430016, 8739968, 17120385, 25509057, 33897537, 42286081, 50805824, 59194560, 67583104, 77927424, 84369102, 92748800, 102612561, 111098961, 119870592, 126312014, 136167121, 144653521, 153425088, 159866382, 169721489, 178207889, 1073747969, 185032334, 196023887, 201956944, 213071428, 218455232, 227122896, 238237188, 244014159, 252288528, 263403204, 269180623, 277454480, 1075336130, 288568964, 294346383, 1074823172, 303939089, 312425489, 319512079, 330241039, 336412358, 347053589, 355286037, 361709206, 369449984, 380572879, 388996757, 397229205, 403652310, 411393088, 422515855, 430939733, 439172181, 445595158, 455957718, 465376257, 472882901, 481115349, 487538262, 497900630, 507319425, 515087896, 521615063, 531455126, 540253848, 546780759, 556620822, 563166920, 573808344, 580335255, 588209811, 596721224, 607362648, 613889559, 622296722, 630275720, 641048281, 646930003, 658314433, 663830024, 672628434, 683480129, 1073800135, 1075906568, 689641172, 697794130, 708156953, 714806932, 722427603, 733322905, 739972692, 748125714, 1074359235, 1076469705, 758488665, 765138452, 772759059, 1075703749, 781008390, 789397126, 797785670, 1076769738, 1077048330, 1077316614, 1074714571, 1075251148, 1074227149],
    [118, 104, 3, 117, 94, 2014209, 10296512, 18684928, 27073600, 35462272, 43981825, 52370625, 60759105, 69123137, 77536385, 86574798, 93157582, 103095502, 1073746882, 111066241, 1074809795, 118032080, 126179536, 136781008, 144620737, 151330449, 160266766, 170468497, 178592782, 1074305025, 187087938, 193273425, 201677328, 212411473, 220666896, 229031106, 237575698, 243605009, 254367762, 262743057, 270999184, 279362690, 285548241, 293951632, 304686289, 312811150, 321305602, 329843854, 336427150, 346496592, 355114703, 363404882, 371808338, 378078224, 388308558, 397057615, 405341198, 411924558, 422223375, 430513810, 438917266, 445187216, 455777935, 464068306, 472471762, 478741584, 487366356, 496065237, 506004558, 512532052, 1075371972, 521230997, 531572310, 537837146, 1075651527, 546396757, 556738198, 563003034, 571562517, 581904086, 588168922, 597260825, 607069718, 613334554, 622287448, 630654547, 638787081, 647274007, 656235227, 664209043, 672341577, 680304148, 689789531, 698156697, 705896073, 1075921864, 714382935, 1073850309, 722950680, 731711065, 739450569, 747937431, 1076220937, 756505240, 764872211, 772578964, 780490832, 790038227, 798269143, 807230107, 815597273, 824007195, 832373785, 1075194829, 840530137, 1076523978, 1077064714, 1077331910, 848779992, 1074212811, 857307289, 865695833, 1076842444],
    [98, 84, 5, 97, 74, 1178752, 10318849, 17136640, 25525312, 33914048, 42302592, 50822337, 59210881, 67599361, 76676288, 85816385, 92765249, 103365201, 109673553, 118619200, 127759489, 135233219, 145052867, 152173568, 160398915, 1073747969, 170218563, 178249422, 187513540, 193953283, 203772931, 211803662, 219119235, 229332498, 237240015, 1075333123, 246109906, 253746830, 263010884, 270881923, 279182991, 288438931, 296441426, 304078414, 313342468, 321125903, 329086145, 1074310404, 338507908, 344555217, 355161746, 363069007, 1076679621, 371800273, 380720661, 388619397, 397490771, 405886549, 413785285, 1074856898, 422656723, 428441105, 439441045, 447470721, 455686161, 461995665, 473265744, 481025025, 489240721, 498431632, 506191041, 514931219, 523327189, 531225605, 540089044, 548763344, 556653698, 565254740, 573430786, 582032020, 590208194, 599094800, 607197716, 615242817, 622672470, 631888965, 1073834953, 639449622, 648928322, 1076463562, 656227030, 664501964, 673004182, 681278988, 1074126792, 1075718087, 689667724, 1076257734, 698056268, 1076005900, 1074721739, 1077097483, 1077368781],
    [106, 92, 3, 105, 82, 353344, 10542208, 19078209, 27089921, 35609600, 43867329, 52255873, 60775552, 69033025, 77552832, 84231682, 94428352, 102964417, 111107136, 1073744770, 117793792, 127982656, 136518785, 1074287555, 143203918, 151340162, 161537024, 1074829313, 170346054, 176758286, 187123334, 193535694, 203900422, 210312846, 220677830, 228793345, 1075371014, 1075643335, 1073835973, 237706245, 243614786, 254483589, 261187090, 269418195, 279649349, 286745601, 294583891, 304815301, 313878037, 321715860, 330645073, 338773704, 346881748, 355810961, 363939336, 372047444, 380976849, 386229376, 397213204, 406142481, 414541397, 420413075, 429211215, 439436872, 1076736964, 1077015556, 445578771, 454376975, 464602760, 1077291016, 472964695, 479288906, 487939672, 496451088, 506816149, 514907799, 521494040, 530136088, 540370645, 548462103, 554786506, 563437272, 571817679, 579954386, 590405335, 596729482, 605633624, 613508690, 622394902, 630546072, 639057552, 647455937, 655949398, 664223312, 671442112, 681115286, 689004042, 697646735, 704988354, 1076515850, 1075226571, 714669782, 722943696, 731341889, 739851480, 748119169, 756628632, 764503698, 1076290505, 1076037581, 1074221004],
    [110, 96, 13, 109, 86, 515200, 8764480, 17153024, 25541760, 33930432, 42449985, 50838529, 59227329, 67755726, 76004481, 85606095, 93044432, 101309966, 110771727, 118210192, 126475854, 136461970, 143375888, 1073747969, 151895571, 160030350, 170016466, 176930384, 185450067, 195165200, 201954836, 211435087, 219004563, 228719696, 237876931, 244989583, 252821142, 262274256, 271685188, 278797462, 286113491, 295828624, 305239748, 311180817, 319929878, 329637589, 338793988, 1075331523, 346177042, 353484502, 363191829, 1073784068, 372348036, 379731538, 387038806, 396746389, 405648387, 413015062, 1076155330, 420338771, 430814275, 438181078, 445504531, 455980163, 463346774, 470670547, 478779028, 489299479, 497409621, 504739480, 1074868167, 514465431, 521141455, 530036249, 539892935, 546307215, 555202201, 564797143, 571472975, 580368089, 590224455, 1076715461, 596638735, 605533785, 615390343, 1075677129, 621665427, 629774036, 640556039, 646438080, 655734488, 1074124742, 665460311, 672906892, 679992320, 689288728, 1075186632, 697056849, 706461388, 713546816, 723490330, 1074424778, 730611409, 740015628, 748656282, 755777169, 765181516, 773822042, 1076530188, 1074717643, 781563480, 790599386, 797546068, 1076048845, 1077113869],
    [122, 108, 10, 121, 98, 2327681, 10329280, 18717760, 27106432, 35494912, 44014785, 52403201, 59234882, 69180481, 77825089, 85957761, 92789250, 1073744642, 102991041, 1074287555, 109566082, 119768065, 126197326, 1074829313, 134871118, 143099588, 153697999, 159751886, 168271568, 178911440, 185304258, 195640847, 201694862, 210214480, 220854352, 227124806, 235642439, 1075372997, 245972559, 252157456, 262797328, 269321287, 277683921, 285712016, 296351888, 303006723, 313212434, 319420558, 330409619, 1075912518, 338640404, 344586446, 355575379, 363544274, 369466894, 378379861, 386529294, 397518355, 403414535, 413875858, 419944642, 428573826, 1075668936, 439041618, 445488661, 456251459, 464627411, 470523527, 481771030, 487694025, 498194627, 503948486, 512990935, 523714198, 529636937, 540137603, 546145415, 554933783, 565132884, 573691907, 579699719, 588488279, 599211734, 605288533, 612861444, 621518535, 1076202884, 632766038, 638426837, 647485641, 1074648071, 655197383, 663985815, 674184852, 680631945, 689559703, 697009218, 707346063, 713924245, 722983049, 730825795, 741293780, 747740681, 756283605, 764380291, 1075183625, 772611601, 781834327, 789021764, 797777553, 807000279, 814712003, 1073902538, 1077064714, 822943313, 831780885, 839615490, 848943127, 856130692, 865589321, 873047046, 1077331917, 882112661, 889824390, 899143689, 1074212812, 1076849611],
    [106, 92, 9, 101, 78, 1866945, 8780864, 17169536, 25558016, 33946816, 42466305, 50854977, 59243649, 68975617, 76020929, 85965378, 94928521, 102742530, 109434507, 1073749762, 118095556, 128482889, 136296642, 142989003, 151649796, 1075599361, 161250369, 169851010, 176543307, 185204292, 1075359744, 1076950016, 195591689, 201709067, 212441806, 218758788, 228457678, 236747905, 1077217284, 1074359300, 246011599, 254384654, 262011918, 271089353, 279565839, 287939150, 295566414, 303193804, 313105038, 321509007, 329120910, 336748044, 344832720, 353525388, 361496133, 370252498, 380229199, 387079756, 395050693, 403806738, 414045715, 421813901, 428605061, 437361298, 447600211, 455368205, 462159365, 470661776, 479196820, 487456326, 497311309, 1076726789, 1074653189, 504216080, 514709139, 521010694, 531258436, 537770576, 546567829, 554565318, 564420301, 571578962, 581818067, 590110410, 596899349, 606887498, 1076496327, 1074159623, 613414420, 623533060, 630707862, 640572945, 647484950, 657087684, 663746260, 672005766, 682253444, 1076007880, 1074975750, 689174101, 699293393, 705951445, 715939338, 722982486, 732847761, 1075250115, 1073964035, 739759830, 749493898, 756020820, 766402129],
    [114, 100, 8, 100, 77, 2333696, 9690113, 18078913, 26467457, 34856001, 42327104, 50715776, 59104256, 69574274, 75881664, 84770377, 92923402, 102227592, 1073744578, 1074285570, 111516866, 1074566083, 1074850819, 118324873, 128181836, 135782088, 144817352, 1076696064, 151879177, 160032394, 169336392, 1075140609, 1075420161, 178371656, 1075701760, 185433801, 195421709, 202890760, 1076506625, 1077048321, 211926024, 220587661, 228703368, 237880836, 245726736, 253877264, 262511618, 1077314436, 270919245, 279412431, 287432272, 296066114, 304473805, 312966735, 320986832, 330021961, 337897164, 346390160, 354540688, 363044032, 371451532, 380075535, 388742153, 396852879, 405005836, 412335825, 421887056, 430818436, 437501521, 447053008, 453633610, 463707264, 472743444, 481150020, 488873024, 1073924037, 496336466, 503965386, 514571465, 523075220, 531481796, 538164881, 546668242, 555337429, 563207879, 573291657, 580222610, 588891733, 596762247, 605273617, 615349844, 622446101, 630316615, 639213198, 648904404, 656000661, 663870983, 672767694, 1074209799, 680885778, 689817111, 697933326, 706313939, 714983127, 723099214, 1076323270, 731479571, 740148887, 748396043, 756645523, 765314647, 773561931, 781934102, 790339211, 798711382, 807116491, 815488726, 823754323, 832265878],
]


def fill_table(table, me, low, high):
    if high - low == 1:
        for place, word in enumerate(STEPS[low]):
            table[place] = jnp.int32(word)
        return
    middle = (low + high) // 2
    lax.cond(
        me < middle,
        lambda: fill_table(table, me, low, middle),
        lambda: fill_table(table, me, middle, high),
    )


def neighbours(col, row):
    x = lax.rem(col, 2) * 2 + lax.rem(row // 2, 2)
    y, z, core = col // 2, row // 4, lax.rem(row, 2)
    found = [(x, y, z, 1 - core)]
    for move in (1, 3):
        for other in range(2):
            found.append((lax.rem(x + move, 4), y, z, other))
            found.append((x, lax.rem(y + move, 4), z, other))
            found.append((x, y, lax.rem(z + move, 4), other))
    return [{"col": y * 2 + x // 2, "row": z * 4 + lax.rem(x, 2) * 2 + core} for x, y, z, core in found]


def split(value):
    high = value.astype(jnp.bfloat16)
    return high, (value - high.astype(jnp.float32)).astype(jnp.bfloat16)


def spread_kernel(
    stored_ref, slots_ref, halves_ref,
    table, tile_even, tile_odd, halves_even, halves_odd, load_sem, store_sem, send_sem, recv_sem,
):
    active, half, block = stored_ref.shape[2:5]
    rows_per = active // CHUNKS
    col, row = lax.axis_index("col"), lax.axis_index("row")
    beside = neighbours(col, row)
    sibling = beside[0]
    tiles = halves_ref.shape[0]

    barrier = pltpu.get_barrier_semaphore()
    for device in beside:
        pl.semaphore_signal(barrier, inc=1, device_id=device, device_id_type=MESH)
    fill_table(table, col * lax.axis_size("row") + row, 0, len(STEPS))
    pl.semaphore_wait(barrier, len(beside))

    def hop(source, slot, chunk, place, device):
        return pltpu.make_async_remote_copy(
            src_ref=source,
            dst_ref=slots_ref.at[slot, pl.ds(chunk * rows_per, rows_per)],
            send_sem=send_sem.at[place],
            recv_sem=recv_sem.at[slot, chunk],
            device_id=device,
            device_id_type=MESH,
        )

    def arrival(slot, chunk):
        piece = slots_ref.at[slot, pl.ds(chunk * rows_per, rows_per)]
        hop(piece, slot, chunk, 0, sibling).wait_recv()

    tile = (tile_even, tile_odd)
    halves = (halves_even, halves_odd)

    def load(source, turn):
        return pltpu.make_async_copy(source, tile[turn], load_sem.at[turn])

    def store(turn, role):
        return pltpu.make_async_copy(halves[turn], halves_ref.at[role], store_sem.at[turn])

    def prepare(turn, order, role):
        load(slots_ref.at[0], turn).wait()

        @pl.when(order >= 2)
        def _():
            store(turn, 0).wait()

        for mirrored in range(2):
            @pl.when((role & 1) == mirrored)
            def _():
                @pl.loop(0, active)
                def _(line):
                    for slot in range(half):
                        value = tile[turn][line, slot]
                        high, low = split(value.T if mirrored else value)
                        halves[turn][line * half + slot, :block] = high
                        halves[turn][line * half + slot, block:] = low

        store(turn, role).start()

    steps = table[0]
    sends = table[1]

    def act(step):
        word = table[5 + step]
        slot = word & 63

        @pl.when((word >> 30) == 0)
        def _():
            chunk = (word >> 6) & 7
            device = {"col": (word >> 10) & 7, "row": (word >> 13) & 15}
            landing = (word >> 17) & 63
            place = (word >> 23) & 127

            @pl.when(((word >> 9) & 1) == 1)
            def _():
                arrival(slot, chunk)

            @pl.when(slot < 2)
            def _():
                piece = stored_ref.at[slot, 0, pl.ds(chunk * rows_per, rows_per)]
                hop(piece, landing, chunk, place, device).start()

            @pl.when(slot >= 2)
            def _():
                piece = slots_ref.at[slot, pl.ds(chunk * rows_per, rows_per)]
                hop(piece, landing, chunk, place, device).start()

        @pl.when((word >> 30) != 0)
        def _():
            order = (word >> 14) & 15
            for chunk in range(CHUNKS):
                @pl.when(((word >> (6 + chunk)) & 1) == 1)
                def _():
                    arrival(slot, chunk)

            for turn in range(2):
                @pl.when((order & 1) == turn)
                def _():
                    @pl.when(slot < 2)
                    def _():
                        load(stored_ref.at[slot, 0], turn).start()

                    @pl.when(slot >= 2)
                    def _():
                        load(slots_ref.at[slot], turn).start()

                    @pl.when(order >= 1)
                    def _():
                        prepare(1 - turn, order - 1, (word >> 18) & 15)

    def sent(place):
        hop(slots_ref.at[0, pl.ds(0, rows_per)], 0, 0, place, sibling).wait_send()

    pl.loop(0, table[3])(act)
    pl.loop(0, table[4])(sent)
    pl.loop(table[3], steps)(act)
    prepare((tiles - 1) % 2, tiles - 1, table[2])
    pl.loop(table[4], sends)(sent)

    for turn in range(2):
        store(turn, 0).wait()


def spread(stored):
    most = max(entry[1] for entry in STEPS)
    active, half, block = stored.shape[2:5]
    return pl.pallas_call(
        spread_kernel,
        out_shape=(
            jax.ShapeDtypeStruct((SLOTS,) + stored.shape[2:], jnp.float32),
            jax.ShapeDtypeStruct((14, active * half, 2 * block, block), jnp.bfloat16),
        ),
        in_specs=[pl.BlockSpec(memory_space=pl.ANY)],
        out_specs=(pl.BlockSpec(memory_space=pl.ANY),) * 2,
        scratch_shapes=[
            pltpu.SMEM((max(len(entry) for entry in STEPS),), jnp.int32),
            pltpu.VMEM((active, half, block, block), jnp.float32),
            pltpu.VMEM((active, half, block, block), jnp.float32),
            pltpu.VMEM((active * half, 2 * block, block), jnp.bfloat16),
            pltpu.VMEM((active * half, 2 * block, block), jnp.bfloat16),
            pltpu.SemaphoreType.DMA((2,)),
            pltpu.SemaphoreType.DMA((2,)),
            pltpu.SemaphoreType.DMA((most,)),
            pltpu.SemaphoreType.DMA((SLOTS, CHUNKS)),
        ],
        compiler_params=pltpu.CompilerParams(
            collective_id=0, has_side_effects=True, vmem_limit_bytes=60 << 20
        ),
        name="spread",
    )(stored)[1]


def multiply_kernel(
    halves_ref, rows_ref, offs_ref, krow_ref, kcol_ref, kcnt_ref, out_ref,
    blocks, done_first, done_second, pairs, pair_count, bucket, bucket_count, facts, in_sem, out_sem,
):
    grid = lax.axis_size("row")
    tile_j = lax.axis_index("row")
    col_id = lax.axis_index("col")
    tiles, each = halves_ref.shape[:2]
    half = offs_ref.shape[1]
    active = each // half
    block = halves_ref.shape[-1]
    lanes, _, kept = krow_ref.shape
    slots = 2 * half
    steps = 2
    most = steps * slots * slots

    def load(place):
        return pltpu.make_async_copy(
            halves_ref.at[place], blocks.at[pl.ds(place * each, each)], in_sem.at[place]
        )

    waves = ([0, 1, 2, 3, 8, 9, 10, 11], [4, 5, 6, 7, 12, 13])
    for wave in waves:
        for place in wave:
            load(place).start()

    first = rows_ref[0, 0]
    bits = [rows_ref[1, 0] ^ first, rows_ref[2, 0] ^ first, rows_ref[4, 0] ^ first]

    def rank(value):
        return sum(
            jnp.where((value & bit) != 0, jnp.int32(1 << place), jnp.int32(0))
            for place, bit in enumerate(bits)
        )

    def shifts(tile_x, tile_y):
        both = ((tile_x, tile_y), (tile_y, tile_x))
        return [rank(offs_ref[x, slot, y]) for x, y in both for slot in range(half)]

    tile_is = [col_id * lanes + lane for lane in range(lanes)]
    tile_ks = [lax.rem(tile_is[0] + tile_j + place, grid) for place in range(3)]
    right_moves = [shifts(tile_k, tile_j) for tile_k in tile_ks]

    for place in range(lanes * active):
        pair_count[place] = 0
    for lane in range(lanes):
        for step in range(steps):
            left_moves = shifts(tile_is[lane], tile_ks[lane + step])
            for slot in range(slots):
                move = left_moves[slot]
                turn = move if slot >= half else 0
                left_base = (2 * (2 * lane + step) + slot // half) * each + slot % half
                for other in range(slots):
                    apart = move ^ right_moves[lane + step][other]
                    place = lane * active + apart
                    count = pair_count[place]
                    right_base = (8 + 2 * (lane + step) + other // half) * each + other % half
                    reach = move if other < half else apart
                    pairs[place * most + count] = (
                        turn | reach << 3 | left_base << 6 | right_base << 14
                    )
                    pair_count[place] = count + 1

    widest = 4
    room = 2 * kept
    for place in range(lanes * (widest + 1)):
        bucket_count[place] = 0
    for place in range(lanes * active):
        pair_count[place] = place << 3 | pair_count[place] << 7

    def put(lane, size, word):
        place = lane * (widest + 1) + size
        filled = bucket_count[place]
        bucket[place * room + filled] = word
        bucket_count[place] = filled + 1

    for lane in range(lanes):
        count = kcnt_ref[0, lane]
        together = 8

        @pl.loop(0, kept // together)
        def _(part):
            found = []
            for offset in range(together):
                item = part * together + offset
                row = rank(krow_ref[lane, 0, item])
                place = lane * active + (row ^ rank(kcol_ref[lane, 0, item]))
                found.append(jnp.where(item < count, pair_count[place] | row, 0))
            for offset in range(together):
                item = lane * kept + part * together + offset
                products = found[offset] >> 7
                facts[item] = found[offset] & 127
                begin = jnp.where(products > 0, ((products - 1) & 7) + 1, 0)
                put(lane, (begin + 1) >> 1, item | begin << 13)

                @pl.loop(0, (products - begin) >> 3)
                def _(more):
                    put(lane, widest, item | (begin + 8 * more) << 7 | 1 << 12 | 8 << 13)

    blocks[tiles * each] = jnp.zeros((2 * block, block), jnp.bfloat16)
    def gather(word, size):
        fact = facts[word & 127]
        row = fact & 7
        base = (fact >> 3) * most + ((word >> 7) & 31)
        products = word >> 13
        ones, twos = [], []
        for place in range(2 * size):
            inside = place < products
            code = pairs[base + jnp.where(inside, place, 0)]
            source = ((code >> 6) & 255) + (row ^ (code & 7)) * half
            ones.append(blocks[jnp.where(inside, source, tiles * each)])
            other = blocks[(code >> 14) + (row ^ ((code >> 3) & 7)) * half]
            twos.append(jnp.concatenate([other[:block], other[block:]], 1))
        total = jnp.dot(
            jnp.concatenate(ones, 1), jnp.concatenate(twos, 0), preferred_element_type=jnp.float32
        )
        total = total[:block] + total[block:]
        return total[:, :block] + total[:, block:]

    done = (done_first, done_second)

    def add(lane, word, into, total):
        again = ((word >> 12) & 1) == 1

        @pl.when(again)
        def _():
            done[lane][into] = done[lane][into] + total

        @pl.when(jnp.logical_not(again))
        def _():
            done[lane][into] = total

    def store(lane):
        return pltpu.make_async_copy(
            done[lane].at[pl.ds(0, kept)], out_ref.at[lane, 0], out_sem.at[lane]
        )

    for lane in range(lanes):
        for place in waves[lane]:
            load(place).wait()
        head = lane * (widest + 1)

        @pl.loop(0, bucket_count[head])
        def _(place):
            done[lane][bucket[head * room + place] & (kept - 1)] = jnp.zeros((block, block), jnp.float32)

        for size in range(1, widest + 1):
            count = bucket_count[head + size]

            @pl.loop(0, (count + 1) >> 1)
            def _(place):
                start = (head + size) * room + 2 * place
                one = bucket[start]
                paired = 2 * place + 1 < count
                two = bucket[jnp.where(paired, start + 1, start)]
                total_one = gather(one, size)
                total_two = gather(two, size)
                into_one = one & (kept - 1)
                into_two = jnp.where(paired, two & (kept - 1), kept)
                if size < widest:
                    done[lane][into_one] = total_one
                    done[lane][into_two] = total_two
                else:
                    add(lane, one, into_one, total_one)
                    add(lane, jnp.where(paired, two, 0), into_two, total_two)

        store(lane).start()

    for lane in range(lanes):
        store(lane).wait()


def multiply(halves, tile_rows, offsets, kept_rows, kept_cols, kept_count):
    block = halves.shape[-1]
    half = offsets.shape[1]
    tiles, each = halves.shape[:2]
    active = each // half
    lanes, _, kept = kept_rows.shape
    items = lanes * kept
    products = 2 * (2 * half) ** 2
    smem = pl.BlockSpec(memory_space=pltpu.SMEM)
    return pl.pallas_call(
        multiply_kernel,
        out_shape=jax.ShapeDtypeStruct((lanes, 1, kept, block, block), jnp.float32),
        in_specs=[pl.BlockSpec(memory_space=pl.ANY)] + [smem] * 5,
        out_specs=pl.BlockSpec(memory_space=pl.ANY),
        scratch_shapes=[
            pltpu.VMEM((tiles * each + 1, 2 * block, block), jnp.bfloat16),
            pltpu.VMEM((kept + 1, block, block), jnp.float32),
            pltpu.VMEM((kept + 1, block, block), jnp.float32),
            pltpu.SMEM((lanes * active * products,), jnp.int32),
            pltpu.SMEM((lanes * active,), jnp.int32),
            pltpu.SMEM((10 * items,), jnp.int32),
            pltpu.SMEM((10,), jnp.int32),
            pltpu.SMEM((items,), jnp.int32),
            pltpu.SemaphoreType.DMA((tiles,)),
            pltpu.SemaphoreType.DMA((lanes,)),
        ],
        compiler_params=pltpu.CompilerParams(vmem_limit_bytes=60 << 20),
        name="multiply",
    )(halves, tile_rows, offsets, kept_rows, kept_cols, kept_count)


def local(stored, tile_rows, offsets, kept_rows, kept_cols, kept_count):
    halves = spread(stored)
    return multiply(
        halves, tile_rows.T, jnp.swapaxes(offsets, 1, 2), kept_rows, kept_cols, kept_count.T
    )


def solution(mesh):
    in_specs = (
        P("col", "row", None, None, None, None),
        P(),
        P(),
        P("col", "row", None),
        P("col", "row", None),
        P("col", "row"),
    )
    out_specs = P("col", "row", None, None, None)
    return jax.shard_map(local, mesh=mesh, in_specs=in_specs, out_specs=out_specs, check_vma=False)
```

time: 124 us -> 121 us (0.976)
  the two profiles are of different devices: /device:TPU:29 before, /device:TPU:36 now
where the time goes in v6:
time: 121 us
  Pallas kernels  121 us (100%)
    pallas_call x1, Pallas kernels, spread(): pl.pallas_call(spread_kernel, out_shape=(jax.ShapeDtypeStruct((SLOTS,) +...  105 us
    pallas_call x1, Pallas kernels, multiply(): pl.pallas_call(multiply_kernel, out_shape=jax.ShapeDtypeStruct((lanes, 1,...  16 us

profile of v6, /device:TPU:36, one launch (start us, length us, event | category | flops | bytes accessed | tf_op | source)
XLA Modules:
  0.0 120.9 jit_solution(6223422815708257483)
XLA Ops:
  0.0 104.9 %spread.1 = (f32[32,8,2,128,128]{4,3,2,1,0:T(8,128)}, bf16[14,16,256,128]{3,2,1,0:T(8,128)(2,1)}) custom-call(f32[2,1,8,2,128,128]{5,4,3,2,1,0:T(8,128)} %stored_ref.1), custom_call_target="tpu_custom_call" | custom-call | tf_op jit(solution)/shard_map/spread/pallas_call | solution.py:300
  104.9 16.0 %multiply.1 = f32[2,1,32,128,128]{4,3,2,1,0:T(8,128)} custom-call(bf16[14,16,256,128]{3,2,1,0:T(8,128)(2,1)} %get-tuple-element.6.halves_ref, s32[8,16]{1,0:T(8,128)} %bitcast.4, s32[16,2,16]{2,1,0:T(2,128)} %bitcast.3, s32[2,1,32]{2,1,0:T(1,128)} %krow_ref.1, s32[2,1,32]{2,1,0:T(1,128)} %kcol_ref.1, s32[1,2]{1,0:T(1,128)} %bitcast.5), custom_call_target="tpu_custom_call" | custom-call | tf_op jit(solution)/shard_map/multiply/pallas_call | solution.py:507
